TPU v7x, 32 devices: a whole 2x2x4 slice. The times are simulated.
32 devices in a mesh: segment: 4 (over z), seq: 4 (over y, core), dp: 2 (over x).
Axes of the slice: x: 2, y: 2, z: 4, core: 2. Of those that a mesh axis runs over, the one named last changes fastest.
Arguments:
- clean: bfloat16 [2, 512, 64], P('dp', 'seq'), may hold values from -16 to 16
- noise: bfloat16 [2, 512, 128], P('dp', 'seq'), may hold values from -24 to 24
- timesteps: int32 [2, 2], replicated, may hold values from 20 to 979
- text_vec: float32 [2, 256], P('dp'), may hold values from -6 to 6
- w_embed: bfloat16 [4, 64, 3072], P('segment'), may hold values from -0.75 to 0.75
- w_time: bfloat16 [4, 256, 3072], P('segment'), may hold values from -0.375 to 0.375
- w_mod: bfloat16 [4, 3072, 15360], P('segment', None, 'seq'), may hold values from -0.109375 to 0.109375
- w_qkv: bfloat16 [4, 3072, 4, 3, 128], P('segment', None, 'seq'), may hold values from -0.109375 to 0.109375
- w_out: bfloat16 [4, 4, 128, 3072], P('segment', 'seq'), may hold values from -0.25 to 0.25
- qk_gain: float32 [4, 2, 128], P('segment'), may hold values from 1.5 to 2.5
- w_final: bfloat16 [4, 3072, 64], P('segment'), may hold values from -0.109375 to 0.109375
Outputs:
- sample_grad: float32 [2, 512, 64], P('dp', 'seq')
- final_grads: float32 [4, 3072, 64], P('segment')
All inputs are finite; a program needn't handle non-finite values. Where the computation divides by a largest or mean magnitude, that divisor is 1e-20 or more.
Results may differ from a plain program's by a relative error of at most 0.025.
Values may be sent and summed in bfloat16 or wider, within the bound.
No kernel may reach another device: no remote copies, remote signals or barrier semaphores. Data moves between devices by JAX's collectives and lax.ppermute only.
A program may use at most 192 MiB of HBM per device.

v0:
```python
import math

import jax
import jax.numpy as jnp
from jax import lax
from jax.sharding import PartitionSpec as P

SHIFT = 7.0
EPS = 1e-06
ADV_WEIGHT = 3.0


def from_root(value, axis, source):
    kept = jnp.where(lax.axis_index(axis) == source, value, 0).astype(value.dtype)
    return lax.psum(kept, axis)


def noise_level(step):
    fraction = step.astype(jnp.float32) / 1000.0
    return SHIFT * fraction / (1.0 + (SHIFT - 1.0) * fraction)


def time_features(step, feature_count):
    half_width = feature_count // 2
    frequency = jnp.exp(-math.log(10000.0) * jnp.arange(half_width, dtype=jnp.float32) / half_width)
    angles = step.astype(jnp.float32) * frequency
    return jnp.concatenate([jnp.cos(angles), jnp.sin(angles)])


def condition(step, text_row, time_w, mod_w):
    features = (time_features(step, text_row.shape[0]) + text_row).astype(jnp.bfloat16)
    hidden = jax.nn.silu(jnp.dot(features, time_w, preferred_element_type=jnp.float32)).astype(
        jnp.bfloat16
    )
    return jnp.dot(hidden, mod_w, preferred_element_type=jnp.float32)


def normalize(values):
    row_mean = jnp.mean(values, axis=-1, keepdims=True)
    centered = values - row_mean
    inverse = lax.rsqrt(jnp.mean(centered * centered, axis=-1, keepdims=True) + EPS)
    return (centered * inverse, inverse)


def normalize_back(gradient, normed, inverse):
    return inverse * (
        gradient
        - jnp.mean(gradient, axis=-1, keepdims=True)
        - normed * jnp.mean(gradient * normed, axis=-1, keepdims=True)
    )


def rms_scale(values, gain_vec):
    inverse = lax.rsqrt(jnp.mean(values * values, axis=-1, keepdims=True) + EPS)
    unit_vec = values * inverse
    return (unit_vec * gain_vec, unit_vec, inverse)


def rms_back(gradient, unit_vec, inverse, gain_vec):
    scaled = gradient * gain_vec
    return inverse * (scaled - unit_vec * jnp.mean(scaled * unit_vec, axis=-1, keepdims=True))


def head_front(normed_in, head_w, gains):
    head_width = head_w.shape[-1]
    flat_w = head_w.reshape(head_w.shape[0], 3 * head_width)
    projected = jnp.dot(normed_in, flat_w, preferred_element_type=jnp.float32)
    queries, q_unit, q_inverse = rms_scale(projected[:, :head_width], gains[0])
    key_vecs, k_unit, k_inverse = rms_scale(projected[:, head_width : 2 * head_width], gains[1])
    query_b = queries.astype(jnp.bfloat16)
    key_b = key_vecs.astype(jnp.bfloat16)
    value_b = projected[:, 2 * head_width :].astype(jnp.bfloat16)
    scores = jnp.dot(query_b, key_b.T, preferred_element_type=jnp.float32) / math.sqrt(head_width)
    weights = jnp.exp(scores)
    soft_max = weights / jnp.sum(weights, axis=-1, keepdims=True)
    head_out = jnp.dot(
        soft_max.astype(jnp.bfloat16), value_b, preferred_element_type=jnp.float32
    ).astype(jnp.bfloat16)
    return (head_out, (q_unit, q_inverse, k_unit, k_inverse, query_b, key_b, value_b, soft_max))


def head_back(grad_out, stored, gains):
    q_unit, q_inverse, k_unit, k_inverse, query_b, key_b, value_b, soft_max = stored
    head_width = query_b.shape[-1]
    grad_soft = jnp.dot(grad_out, value_b.T, preferred_element_type=jnp.float32)
    grad_value = jnp.dot(
        soft_max.astype(jnp.bfloat16).T, grad_out, preferred_element_type=jnp.float32
    )
    grad_scores = soft_max * (grad_soft - jnp.sum(soft_max * grad_soft, axis=-1, keepdims=True))
    grad_scores_b = (grad_scores / math.sqrt(head_width)).astype(jnp.bfloat16)
    grad_query = jnp.dot(grad_scores_b, key_b, preferred_element_type=jnp.float32)
    grad_key = jnp.dot(grad_scores_b.T, query_b, preferred_element_type=jnp.float32)
    grad_q = rms_back(grad_query, q_unit, q_inverse, gains[0])
    grad_k = rms_back(grad_key, k_unit, k_inverse, gains[1])
    return jnp.concatenate([grad_q, grad_k, grad_value], axis=1).astype(jnp.bfloat16)


def guarded(active, func, operand):
    return lax.cond(active, func, lambda item: jax.tree.map(jnp.zeros_like, func(item)), operand)


def shards(
    clean, noise, timesteps, text_vec, w_embed, w_time, w_mod, w_qkv, w_out, qk_gain, w_final
):
    section = lax.axis_index("segment")
    batch_idx = lax.axis_index("dp")
    tok_rows = clean.shape[1]
    latent_width = clean.shape[2]
    model_width = w_embed.shape[2]
    seq_devices = lax.axis_size("seq")
    full_rows = tok_rows * seq_devices
    head_width = w_qkv.shape[4]
    head_total = w_qkv.shape[2] * seq_devices
    group_count = max(
        [
            count
            for count in range(1, seq_devices + 1)
            if seq_devices % count == 0 and count * tok_rows <= max(512, tok_rows)
        ]
    )
    block_rows = group_count * tok_rows
    block_total = full_rows // block_rows
    embed_w = w_embed[0]
    embed_f32 = embed_w.astype(jnp.float32)
    head_w = w_qkv[0, :, 0]
    flat_head_w = head_w.reshape(model_width, 3 * head_width)
    gains = qk_gain[0]
    final_w = w_final[0]
    step_pair = lax.dynamic_index_in_dim(timesteps, batch_idx, 0, keepdims=False)
    sigma_student = noise_level(step_pair[0])
    sigma_critic = noise_level(step_pair[1])
    own_step = jnp.where(section == 0, step_pair[0], step_pair[1])
    mod_piece = condition(own_step, text_vec[0], w_time[0], w_mod[0])
    modulation = lax.all_gather(mod_piece, "seq", axis=0, tiled=True)
    shift_in, scale_in, gate_vec, shift_out, scale_out = [
        modulation[slot * model_width : (slot + 1) * model_width] for slot in range(5)
    ]
    gathered_rows = lax.all_gather(w_out[0], "seq", axis=0, tiled=True)

    def input_rows(latent_block):
        embedded = jnp.dot(latent_block, embed_w, preferred_element_type=jnp.float32)
        normed, inverse = normalize(embedded)
        return (normed, inverse)

    def modulated_rows(latent_block):
        normed, _ = input_rows(latent_block)
        return (normed * (1.0 + scale_in) + shift_in).astype(jnp.bfloat16)

    def forward(latent_local, active):
        latent_all = lax.all_gather(latent_local, "seq", axis=0, tiled=True)

        def front(latent_rows):
            blocks = latent_rows.reshape(block_total, block_rows, latent_width)
            normed_in = lax.map(modulated_rows, blocks).reshape(full_rows, model_width)
            return head_front(normed_in, head_w, gains)

        head_out, stored = guarded(active, front, latent_all)
        own_rows = jnp.dot(latent_local, embed_w, preferred_element_type=jnp.float32)
        local_heads = lax.all_to_all(head_out, "seq", split_axis=0, concat_axis=1, tiled=True)

        def project(mixed):
            stacked = mixed.reshape(tok_rows, head_total, head_width)
            per_head = jnp.einsum(
                "thk,hkd->htd", stacked, gathered_rows, preferred_element_type=jnp.float32
            )
            return jnp.sum(
                lax.optimization_barrier(per_head.astype(jnp.bfloat16)).astype(jnp.float32), axis=0
            )

        attended = guarded(active, project, local_heads)
        residual = own_rows + gate_vec * attended
        normed_out, inverse_out = normalize(residual)
        final_in = (normed_out * (1.0 + scale_out) + shift_out).astype(jnp.bfloat16)
        result = jnp.dot(final_in, final_w, preferred_element_type=jnp.float32)
        return (result, final_in, (latent_all, stored, normed_out, inverse_out))

    noisy_student = (
        (1.0 - sigma_student) * clean[0].astype(jnp.float32)
        + sigma_student * noise[0, :, :latent_width].astype(jnp.float32)
    ).astype(jnp.bfloat16)
    velocity, student_in, _ = forward(noisy_student, section == 0)
    sample = noisy_student.astype(jnp.float32) - sigma_student * velocity
    sample = from_root(sample.astype(jnp.bfloat16), "segment", 0).astype(sample.dtype)
    second_noise = noise[0, :, latent_width:].astype(jnp.float32)
    noisy_critic = ((1.0 - sigma_critic) * sample + sigma_critic * second_noise).astype(
        jnp.bfloat16
    )
    critic_out, critic_in, cache = forward(noisy_critic, section >= 1)
    latent_all, stored, normed_out, inverse_out = cache
    is_judge = section == 3
    grad_logit = -jax.nn.sigmoid(-critic_out)
    grad_final = jnp.dot(
        grad_logit.astype(jnp.bfloat16), final_w.T, preferred_element_type=jnp.float32
    )
    grad_residual = normalize_back(grad_final * (1.0 + scale_out), normed_out, inverse_out)
    grad_attended = (gate_vec * grad_residual).astype(jnp.bfloat16)

    def spread_heads(grad_rows):
        per_head = jnp.einsum(
            "td,hkd->thk", grad_rows, gathered_rows, preferred_element_type=jnp.float32
        )
        return per_head.astype(jnp.bfloat16).reshape(tok_rows, head_total * head_width)

    grad_local = guarded(is_judge, spread_heads, grad_attended)
    grad_head = lax.all_to_all(grad_local, "seq", split_axis=1, concat_axis=0, tiled=True)
    grad_proj = guarded(is_judge, lambda grad_in: head_back(grad_in, stored, gains), grad_head)

    def latent_rows(first_row, row_count):

        def through(pieces):
            proj_rows, latent_block = pieces
            normed_rows, inverse_rows = input_rows(latent_block)
            grad_normed = jnp.dot(proj_rows, flat_head_w.T, preferred_element_type=jnp.float32)
            grad_embedded = normalize_back(
                grad_normed * (1.0 + scale_in), normed_rows, inverse_rows
            )
            return jnp.dot(grad_embedded, embed_f32.T, precision=lax.Precision.HIGHEST)

        pieces = tuple((source for source in (grad_proj, latent_all)))
        return guarded(is_judge, through, pieces)

    grad_latent = lax.psum_scatter(
        latent_rows(jnp.int32(0), tok_rows * lax.axis_size("seq")).astype(jnp.bfloat16),
        "seq",
        scatter_dimension=0,
        tiled=True,
    ).astype(jnp.float32)
    grad_latent = grad_latent + jnp.dot(grad_residual, embed_f32.T, precision=lax.Precision.HIGHEST)
    adverse = (1.0 - sigma_critic) * grad_latent
    real_part = jnp.where(section == 1, sigma_critic * critic_out, 0.0)
    fake_part = jnp.where(section == 2, sigma_critic * critic_out, 0.0)
    judge_part = jnp.where(is_judge, adverse, 0.0)
    real_term, fake_term, adverse_term = (
        lax.psum(real_part.astype(jnp.bfloat16), "segment").astype(jnp.float32),
        lax.psum(fake_part.astype(jnp.bfloat16), "segment").astype(jnp.float32),
        lax.psum(judge_part.astype(jnp.bfloat16), "segment").astype(jnp.float32),
    )
    error_local = jnp.sum(jnp.abs(sample - noisy_critic.astype(jnp.float32) + real_term))
    error_total = lax.psum(error_local, "seq")
    spread = error_total / (full_rows * latent_width) + EPS
    sample_grad = (real_term - fake_term) / spread + ADV_WEIGHT * adverse_term
    target = jnp.where(
        section == 0,
        -sigma_student * sample_grad,
        jnp.where(
            section == 2,
            2.0 * (critic_out - (second_noise - sample)),
            jnp.where(is_judge, jax.nn.sigmoid(critic_out), 0.0),
        ),
    )
    final_rows = jnp.where(section == 0, student_in, critic_in)
    term = jnp.einsum(
        "td,tc->dc", final_rows, target.astype(jnp.bfloat16), preferred_element_type=jnp.float32
    )
    total = lax.psum(term.astype(jnp.bfloat16), ("seq", "dp")).astype(jnp.float32)
    final_grads = total / full_rows
    return (sample_grad[None], final_grads[None])


def solution(mesh):
    placed = (
        P("dp", "seq", None),
        P("dp", "seq", None),
        P(),
        P("dp", None),
        P("segment", None, None),
        P("segment", None, None),
        P("segment", None, "seq"),
        P("segment", None, "seq", None, None),
        P("segment", "seq", None, None),
        P("segment", None, None),
        P("segment", None, None),
    )
    return jax.shard_map(
        shards,
        mesh=mesh,
        in_specs=placed,
        out_specs=(P("dp", "seq", None), P("segment", None, None)),
        check_vma=False,
    )
```

profile of v0, /device:TPU:0, one launch (start us, length us, event | category | flops | bytes accessed | tf_op | source)
XLA Modules:
  0.0 274.7 jit_solution(8759388569653749423)
XLA Ops:
  7.2 0.7 all-gather.5.cloned.1.call-update
  7.9 0.7 constant_dynamic-slice_fusion
  8.6 0.6 fusion.98
  11.1 1.0 fusion.37
  12.2 0.9 fusion.97
  13.2 10.6 %fusion.34 = f32[1,1,3840]{2,1,0:T(1,128)S(1)} fusion(bf16[3072,1]{0,1:T(2,128)(2,1)S(1)} %reshape.223, bf16[1,3072,3840]{2,1,0:T(8,128)(2,1)} %param.31), kind=kOutput, calls=%fused_computation.97 | convolution fusion | flops 23592960 | bytes 23614464 | tf_op jit(solution)/shard_map/dot_general | solution.py:35
  23.8 6.7 %all-gather.2 = f32[4,1,3840]{2,1,0:T(1,128)S(1)} all-gather(f32[1,1,3840]{2,1,0:T(1,128)S(1)} %fusion.34), channel_id=1, replica_groups=mesh['segment'=4,'seq'=4,'dp'=2] {'seq'}, dimensions={0}, use_global_device_ids=true | all-gather | bytes 76800 | tf_op jit(solution)/shard_map/all_gather | solution.py:134
  30.4 6.0 %all-gather = bf16[1,512,64]{1,2,0:T(8,128)(2,1)S(1)} all-gather(bf16[1,128,64]{1,2,0:T(8,128)(2,1)S(1)} %add_convert_fusion.6), channel_id=2, replica_groups=mesh['segment'=4,'seq'=4,'dp'=2] {'seq'}, dimensions={1}, use_global_device_ids=true | all-gather | bytes 81920 | tf_op jit(solution)/shard_map/all_gather | solution.py:150
  36.4 0.6 fusion.96
  37.1 9.9 %conditional.7 = (bf16[512,128]{1,0:T(8,128)(2,1)}) conditional(s32[]{:T(128)} %convert_element_type.187, () %tuple.57, (bf16[512,64]{0,1:T(8,128)(2,1)S(1)}, bf16[64,3072]{1,0:T(8,128)(2,1)S(1)}, f32[3072]{0:T(1024)}, f32[3072]{0:T(1024)}, bf16[1,3072,1,3,128]{4,1,3,2,0:T(8,128)(2,1)S(1)}, /*index=5*/f32[2,128]{1,0:T(2,128)S(1)}) %tuple.157), branch_computations={%region_0.1_spmd, %region_1.7_spmd} | conditional | flops 1559433216 | bytes 40133668 | solution.py:99
  37.1 0.7 broadcast_add_fusion
  37.8 2.4 copy.53
  40.2 1.1 fusion.91
  41.3 0.8 multiply_reduce_fusion
  42.1 0.9 copy-done.13
  43.0 2.4 fusion
  46.0 1.0 convolution_convert_fusion
  47.0 3.3 %all-to-all-start = ((bf16[4,128,128]{2,1,0:T(8,128)(2,1)}), bf16[4,128,128]{2,1,0:T(8,128)(2,1)S(1)}, u32[]{:S(2)}, u32[]{:S(2)}) async-start(bf16[4,128,128]{2,1,0:T(8,128)(2,1)} %bitcast.26), calls=%async_computation | async-start | bytes 262144 | tf_op jit(solution)/shard_map/all_to_all | solution.py:159
  51.0 3.9 %all-to-all-done = bf16[4,128,128]{2,1,0:T(8,128)(2,1)S(1)} async-done(((bf16[4,128,128]{2,1,0:T(8,128)(2,1)}), bf16[4,128,128]{2,1,0:T(8,128)(2,1)S(1)}, u32[]{:S(2)}, u32[]{:S(2)}) %all-to-all-start) | async-done | bytes 131104 | tf_op jit(solution)/shard_map/all_to_all | solution.py:159
  54.9 3.4 %conditional.8 = (f32[128,3072]{1,0:T(8,128)S(1)}) conditional(s32[]{:T(128)} %convert_element_type.187, () %tuple.56, (bf16[128,4,128]{2,0,1:T(8,128)(2,1)S(1)}, bf16[4,128,3072]{2,1,0:T(8,128)(2,1)}) %tuple.152), branch_computations={%region_7.8_spmd, %region_8.10_spmd} | conditional | flops 406978560 | bytes 11141128 | solution.py:99
  54.9 2.9 %convolution_convert_fusion.1 = bf16[4,128,3072]{2,1,0:T(8,128)(2,1)S(1)} fusion(bf16[128,4,128]{2,0,1:T(8,128)(2,1)S(1)} %get-tuple-element.132, bf16[4,128,3072]{2,1,0:T(8,128)(2,1)} %get-tuple-element.133), kind=kOutput, calls=%fused_computation.28 | convolution fusion | flops 404226048 | bytes 6422528 | tf_op jit(solution)/shard_map/cond/branch_1_fun/thk,hkd->htd/dot_general | solution.py:163
  57.7 0.6 convert_reduce_fusion
  58.3 0.5 fusion.99
  59.5 0.9 copy-done.7
  60.8 15.5 %psum.42 = bf16[128,64]{0,1:T(8,128)(2,1)S(1)} all-reduce(bf16[128,64]{0,1:T(8,128)(2,1)S(1)} %fusion.44), channel_id=1, replica_groups=mesh['segment'=4,'seq'=4,'dp'=2] {'segment'}, use_global_device_ids=true, to_apply=%region_12.13 | all-reduce | flops 8192 | bytes 32768 | tf_op jit(solution)/shard_map/psum | solution.py:15
  76.4 5.7 %all_gather.15 = bf16[512,64]{0,1:T(8,128)(2,1)} all-gather(bf16[128,64]{0,1:T(8,128)(2,1)S(1)} %fusion.56), channel_id=1, replica_groups=mesh['segment'=4,'seq'=4,'dp'=2] {'seq'}, dimensions={0}, use_global_device_ids=true | all-gather | bytes 81920 | tf_op jit(solution)/shard_map/all_gather | solution.py:150
  82.1 5.8 %conditional.9 = (bf16[512,128]{1,0:T(8,128)(2,1)S(1)}, f32[512,128]{0,1:T(8,128)}, f32[512,1]{0,1:T(1,128)}, f32[512,128]{0,1:T(8,128)}, f32[512,1]{0,1:T(1,128...) conditional(s32[]{:T(128)} %convert_element_type.194, () %tuple.61, ...), branch_computations={%region_13.14_spmd, %region_14.20_spmd} | conditional | flops 1559433216 | bytes 43594936 | solution.py:99
  82.1 0.6 broadcast.304.clone
  82.7 0.6 broadcast.304
  83.3 0.7 broadcast.302.clone2.1
  83.9 0.7 broadcast.302.clone2
  84.6 0.7 broadcast.302.clone
  85.3 0.7 broadcast.303.clone
  86.0 0.8 broadcast.303
  86.8 1.1 broadcast.305
  87.9 0.7 copy-done.15
  88.5 3.9 %all-to-all-start.1 = ((bf16[4,128,128]{2,1,0:T(8,128)(2,1)}), bf16[4,128,128]{2,1,0:T(8,128)(2,1)}, u32[]{:S(2)}, u32[]{:S(2)}) async-start(bf16[4,128,128]{2,1,0:T(8,128)(2,1)} %bitcast.134), calls=%async_computation.1 | async-start | bytes 262144 | tf_op jit(solution)/shard_map/all_to_all | solution.py:159
  92.5 4.7 %all-to-all-done.1 = bf16[4,128,128]{2,1,0:T(8,128)(2,1)} async-done(((bf16[4,128,128]{2,1,0:T(8,128)(2,1)}), bf16[4,128,128]{2,1,0:T(8,128)(2,1)}, u32[]{:S(2)}, u32[]{:S(2)}) %all-to-all-start.1) | async-done | bytes 131104 | tf_op jit(solution)/shard_map/all_to_all | solution.py:159
  97.2 1.3 conditional.10
  97.2 1.3 broadcast.311
  98.5 1.9 fusion.100
  100.8 1.2 add_convert_fusion.4
  102.0 2.1 select_convert_fusion
  104.1 0.7 fusion.90
  104.8 2.0 multiply_convert_fusion.9
  106.8 0.7 conditional.11
  106.8 0.7 broadcast.312
  107.5 3.3 %all-to-all-start.2 = ((bf16[128,4,128]{0,2,1:T(8,128)(2,1)}), bf16[128,4,128]{0,2,1:T(8,128)(2,1)S(1)}, u32[]{:S(2)}, u32[]{:S(2)}) async-start(bf16[128,4,128]{0,2,1:T(8,128)(2,1)} %bitcast.33), calls=%async_computation.2 | async-start | bytes 262144 | tf_op jit(solution)/shard_map/all_to_all | solution.py:205
  110.9 4.5 %all-to-all-done.2 = bf16[128,4,128]{0,2,1:T(8,128)(2,1)S(1)} async-done(((bf16[128,4,128]{0,2,1:T(8,128)(2,1)}), bf16[128,4,128]{0,2,1:T(8,128)(2,1)S(1)}, u32[]{:S(2)}, u32[]{:S(2)}) %all-to-all-start.2) | async-done | bytes 131104 | tf_op jit(solution)/shard_map/all_to_all | solution.py:205
  115.4 0.7 copy-done.11
  116.2 1.0 copy-done.4
  117.2 0.6 conditional.13
  117.2 0.6 broadcast.316
  117.8 1.7 copy.71
  119.6 60.8 %reduce-scatter.4.cloned.1.call-done = bf16[128,64]{1,0:T(8,128)(2,1)} async-done(((bf16[512,64]{1,0:T(8,128)(2,1)}), bf16[128,64]{1,0:T(8,128)(2,1)}) %reduce-scatter.4.cloned.1.call-update) | async-done | bytes 16400
  180.4 0.8 copy.72
  181.2 2.5 fusion.43
  183.7 19.9 %all-reduce = (bf16[128,64]{0,1:T(8,128)(2,1)S(1)}, bf16[128,64]{0,1:T(8,128)(2,1)S(1)}, bf16[128,64]{0,1:T(8,128)(2,1)S(1)}) all-reduce(bf16[128,64]{0,1:T(8,128)(2,1)S(1)} %fusion.43, bf16[128,64]{0,1:T(8,128)(2,1)} %get-tuple-element.343, ...), channel_id=1, replica_groups=mesh['segment'=4,'seq'=4,'dp'=2] {'segment'}, use_global_device_ids=true, to_apply=%region_45.46 | all-reduce | flops 24576 | bytes 98304 | tf_op jit(solution)/shard_map/psum | solution.py:236
  203.6 1.3 fusion.54
  205.0 6.6 %psum.45 = f32[]{:T(128)} all-reduce(f32[]{:T(128)} %fusion.54), channel_id=1, replica_groups=mesh['segment'=4,'seq'=4,'dp'=2] {'seq'}, use_global_device_ids=true, to_apply=%region_28.29 | all-reduce | flops 1 | bytes 8 | tf_op jit(solution)/shard_map/psum | solution.py:239
  212.1 1.9 convolution_convert_fusion.6
  214.0 0.6 fusion.89
  214.6 51.6 %all-reduce.3.cloned.1.call-done = bf16[3072,64]{0,1:T(8,128)(2,1)} async-done(((bf16[3072,64]{0,1:T(8,128)(2,1)}), bf16[3072,64]{0,1:T(8,128)(2,1)}) %all-reduce.3.cloned.1.call-update) | async-done | bytes 393232 | tf_op jit(solution)/shard_map/psum | solution.py:255
  266.2 1.9 multiply_bitcast_fusion
  (75 shorter events, 2.5 us)
Async XLA Ops:
  7.2 3.9 %copy-start = (bf16[1,256,3072]{2,1,0:T(8,128)(2,1)S(1)}, bf16[1,256,3072]{2,1,0:T(8,128)(2,1)}, u32[]{:S(2)}) copy-start(bf16[1,256,3072]{2,1,0:T(8,128)(2,1)} %param.30) | copy-start | bytes 4718596
  7.2 47.7 %all-gather.5.cloned.1.call-start = ((), (), s32[]{:S(2)}) async-start(), calls=%async_computation.5 | async-start | bytes 3932160 | tf_op jit(solution)/shard_map/all_gather | solution.py:138
  13.2 17.3 %copy-start.26 = (bf16[1,128,64]{1,2,0:T(8,128)(2,1)S(1)}, bf16[1,128,64]{1,2,0:T(8,128)(2,1)}, u32[]{:S(2)}) copy-start(bf16[1,128,64]{1,2,0:T(8,128)(2,1)} %param.25) | copy-start | bytes 49156
  13.2 23.9 %copy-start.3 = (bf16[1,3072,1,3,128]{4,1,3,2,0:T(8,128)(2,1)S(1)}, bf16[1,3072,1,3,128]{4,1,3,2,0:T(8,128)(2,1)}, u32[]{:S(2)}) copy-start(bf16[1,3072,1,3,128]{4,1,3,2,0:T(8,128)(2,1)} %param.32) | copy-start | bytes 7077892
  13.2 23.9 %copy-start.5 = (bf16[1,64,3072]{2,1,0:T(8,128)(2,1)S(1)}, bf16[1,64,3072]{2,1,0:T(8,128)(2,1)}, u32[]{:S(2)}) copy-start(bf16[1,64,3072]{2,1,0:T(8,128)(2,1)} %param.29) | copy-start | bytes 1179652
  13.2 23.9 %copy-start.28 = (f32[1,2,128]{2,1,0:T(2,128)S(1)}, f32[1,2,128]{2,1,0:T(2,128)}, u32[]{:S(2)}) copy-start(f32[1,2,128]{2,1,0:T(2,128)} %param.34) | copy-start | bytes 3076
  37.0 21.3 %copy-start.18 = (f32[3072]{0:T(1024)}, f32[3072]{0:T(1024)S(1)}, u32[]{:S(2)}) copy-start(f32[3072]{0:T(1024)S(1)} %get-tuple-element.341) | copy-start | bytes 36868
  37.0 22.1 %copy-start.20 = (f32[3072]{0:T(1024)}, f32[3072]{0:T(1024)S(1)}, u32[]{:S(2)}) copy-start(f32[3072]{0:T(1024)S(1)} %get-tuple-element.338) | copy-start | bytes 36868
  37.0 22.1 %copy-start.24 = (f32[3072]{0:T(1024)}, f32[3072]{0:T(1024)S(1)}, u32[]{:S(2)}) copy-start(f32[3072]{0:T(1024)S(1)} %get-tuple-element.337) | copy-start | bytes 36868
  41.3 1.7 copy-start.13
  47.0 7.9 %all-to-all-start = ((bf16[4,128,128]{2,1,0:T(8,128)(2,1)}), bf16[4,128,128]{2,1,0:T(8,128)(2,1)S(1)}, u32[]{:S(2)}, u32[]{:S(2)}) async-start(bf16[4,128,128]{2,1,0:T(8,128)(2,1)} %bitcast.26), calls=%async_computation | async-start | bytes 262144 | tf_op jit(solution)/shard_map/all_to_all | solution.py:159
  51.0 25.4 %copy-start.23 = (bf16[1,128,64]{1,2,0:T(8,128)(2,1)}, bf16[1,128,64]{1,2,0:T(8,128)(2,1)S(1)}, u32[]{:S(2)}) copy-start(bf16[1,128,64]{1,2,0:T(8,128)(2,1)S(1)} %copy.74) | copy-start | bytes 49156
  58.3 2.1 copy-start.9
  59.5 0.9 copy-start.7
  76.4 5.7 %copy-start.17 = (bf16[128,64]{0,1:T(8,128)(2,1)}, bf16[128,64]{0,1:T(8,128)(2,1)S(1)}, u32[]{:S(2)}) copy-start(bf16[128,64]{0,1:T(8,128)(2,1)S(1)} %psum.42) | copy-start | bytes 49156
  82.1 15.0 %copy-start.2 = (bf16[4,1,128,3072]{3,2,1,0:T(8,128)(2,1)S(1)}, bf16[4,1,128,3072]{3,2,1,0:T(8,128)(2,1)}, u32[]{:S(2)}) copy-start(bf16[4,1,128,3072]{3,2,1,0:T(8,128)(2,1)} %all-gather.5.cloned.1.call-done) | copy-start | bytes 9437188
  87.9 0.7 copy-start.15
  88.5 8.6 %all-to-all-start.1 = ((bf16[4,128,128]{2,1,0:T(8,128)(2,1)}), bf16[4,128,128]{2,1,0:T(8,128)(2,1)}, u32[]{:S(2)}, u32[]{:S(2)}) async-start(bf16[4,128,128]{2,1,0:T(8,128)(2,1)} %bitcast.134), calls=%async_computation.1 | async-start | bytes 262144 | tf_op jit(solution)/shard_map/all_to_all | solution.py:159
  98.5 2.3 copy-start.21
  98.5 2.3 copy-start.25
  98.5 3.5 %copy-start.10 = (bf16[1,3072,64]{1,2,0:T(8,128)(2,1)S(1)}, bf16[1,3072,64]{1,2,0:T(8,128)(2,1)}, u32[]{:S(2)}) copy-start(bf16[1,3072,64]{1,2,0:T(8,128)(2,1)} %param.35) | copy-start | bytes 1179652
  100.8 4.0 %copy-start.19 = (f32[3072]{0:T(1024)S(1)}, f32[3072]{0:T(1024)}, u32[]{:S(2)}) copy-start(f32[3072]{0:T(1024)} %copy-done.18) | copy-start | bytes 36868
  104.1 0.7 copy-start.16
  107.5 7.9 %all-to-all-start.2 = ((bf16[128,4,128]{0,2,1:T(8,128)(2,1)}), bf16[128,4,128]{0,2,1:T(8,128)(2,1)S(1)}, u32[]{:S(2)}, u32[]{:S(2)}) async-start(bf16[128,4,128]{0,2,1:T(8,128)(2,1)} %bitcast.33), calls=%async_computation.2 | async-start | bytes 262144 | tf_op jit(solution)/shard_map/all_to_all | solution.py:205
  110.8 69.6 %reduce-scatter.4.cloned.1.call-start = ((), (), s32[]{:S(2)}) async-start(), calls=%async_computation.6 | async-start | bytes 163840
  115.4 1.8 copy-start.4
  115.4 0.7 copy-start.11
  117.2 94.9 %copy-start.8 = (bf16[128,3072]{1,0:T(8,128)(2,1)S(1)}, bf16[128,3072]{1,0:T(8,128)(2,1)}, u32[]{:S(2)}) copy-start(bf16[128,3072]{1,0:T(8,128)(2,1)} %copy-done.7) | copy-start | bytes 2359300
  117.8 150.3 %copy-start.1 = (bf16[1,256,3072]{2,1,0:T(8,128)(2,1)S(1)}, bf16[1,256,3072]{2,1,0:T(8,128)(2,1)}, u32[]{:S(2)}) copy-start(bf16[1,256,3072]{2,1,0:T(8,128)(2,1)} %param.30) | copy-start | bytes 4718596
  119.6 146.6 %all-reduce.3.cloned.1.call-start = ((), (), s32[]{:S(2)}) async-start(), calls=%async_computation.4 | async-start | bytes 786432 | tf_op jit(solution)/shard_map/psum | solution.py:255
Sparse Core Ops, SparseCore 0:
  9.5 31.9 all-gather.4
  119.7 60.6 reduce-scatter.3
  214.1 52.0 all-reduce.2
where the time goes:
time: 276 us; the launch traced here: 275 us
  waiting for transfers between devices  126 us (46%)
  blocking collectives  60.4 us (22%)
  matrix products  29.3 us (11%)
  local copies, waits for them, and re-layouts  20 us (7%)
  between operations  17.2 us (6%)
  other arithmetic  10.9 us (4%)
  starting transfers between devices  10.7 us (4%)
    unnamed x4, waiting for transfers between devices  61.5 us
    psum x1, waiting for transfers between devices, shards(): lax.psum(term.astype(jnp.bfloat16), ('seq', 'dp')).astype(jnp.float32)  51.6 us
    psum x1, blocking collectives, shards(): lax.psum(judge_part.astype(jnp.bfloat16), 'segment').astype(jnp.float32)  19.9 us
    psum x1, blocking collectives, from_root(): return lax.psum(kept, axis)  15.5 us
    all_gather x2, blocking collectives, forward(): latent_all = lax.all_gather(latent_local, 'seq', axis=0, tiled=True)  11.7 us
    another operation x14, local copies, waits for them, and re-layouts  10.8 us
    dot_general x1, matrix products, condition(): return jnp.dot(hidden, mod_w, preferred_element_type=jnp.float32)  10.6 us
    all_to_all x2, waiting for transfers between devices, forward(): lax.all_to_all(head_out, 'seq', split_axis=0, concat_axis=1, tiled=True)  8.52 us
  transfers between devices with their start and end apart: 6, of which 5 were waited for; matrix products, arithmetic and copies ran while one was open for 9% of the time, Pallas kernels for 0%

commit v1 on v0

v1 whole, which is shorter than its diff:
```python
import math

import jax
import jax.numpy as jnp
from jax import lax
from jax.sharding import PartitionSpec as P

SHIFT = 7.0
EPS = 1e-06
ADV_WEIGHT = 3.0


def halves(values):
    top = lax.reduce_precision(values, 8, 7)
    return (top.astype(jnp.bfloat16), (values - top).astype(jnp.bfloat16))


def swaps(count, offset):
    return [(place, place ^ offset) for place in range(count)]


def gather_near(value, axis, count):
    return [value] + [
        lax.ppermute(value, axis, swaps(count, offset)) for offset in range(1, count)
    ]


def scatter_near(blocks, axis, count):
    return [blocks[0]] + [
        lax.ppermute(blocks[offset], axis, swaps(count, offset)) for offset in range(1, count)
    ]


def gather_doubling(value, axis, count):
    held = {0: value}
    bit = count // 2
    while bit:
        offsets = sorted(held)
        joined = jnp.concatenate([held[offset] for offset in offsets], axis=0)
        moved = lax.ppermute(joined, axis, swaps(count, bit))
        rows = value.shape[0]
        for place, offset in enumerate(offsets):
            held[offset | bit] = moved[place * rows : (place + 1) * rows]
        bit //= 2
    return [held[offset] for offset in range(count)]


def in_order(pieces, own_place):
    ordered = list(pieces)
    bit = 1
    while bit < len(ordered):
        flipped = (own_place & bit) != 0
        ordered = [
            jnp.where(flipped, ordered[place ^ bit], ordered[place])
            for place in range(len(ordered))
        ]
        bit *= 2
    return ordered


def dot32(left, right):
    return jnp.dot(left, right, preferred_element_type=jnp.float32)


def dot32_t(left, right):
    return lax.dot_general(
        left, right, (((1,), (1,)), ((), ())), preferred_element_type=jnp.float32
    )


def noise_level(step):
    fraction = step.astype(jnp.float32) / 1000.0
    return SHIFT * fraction / (1.0 + (SHIFT - 1.0) * fraction)


def time_features(step, feature_count):
    half_width = feature_count // 2
    frequency = jnp.exp(-math.log(10000.0) * jnp.arange(half_width, dtype=jnp.float32) / half_width)
    angles = step.astype(jnp.float32) * frequency
    return jnp.concatenate([jnp.cos(angles), jnp.sin(angles)])


def condition(step, text_row, time_w, mod_w):
    features = (time_features(step, text_row.shape[0]) + text_row).astype(jnp.bfloat16)
    hidden = jax.nn.silu(jnp.dot(features, time_w, preferred_element_type=jnp.float32)).astype(
        jnp.bfloat16
    )
    return jnp.dot(hidden, mod_w, preferred_element_type=jnp.float32)


def normalize(values):
    row_mean = jnp.mean(values, axis=-1, keepdims=True)
    centered = values - row_mean
    inverse = lax.rsqrt(jnp.mean(centered * centered, axis=-1, keepdims=True) + EPS)
    return (centered * inverse, inverse)


def normalize_back(gradient, normed, inverse):
    return inverse * (
        gradient
        - jnp.mean(gradient, axis=-1, keepdims=True)
        - normed * jnp.mean(gradient * normed, axis=-1, keepdims=True)
    )


def rms_scale(values, gain_vec):
    inverse = lax.rsqrt(jnp.mean(values * values, axis=-1, keepdims=True) + EPS)
    unit_vec = values * inverse
    return (unit_vec * gain_vec, unit_vec, inverse)


def rms_back(gradient, unit_vec, inverse, gain_vec):
    scaled = gradient * gain_vec
    return inverse * (scaled - unit_vec * jnp.mean(scaled * unit_vec, axis=-1, keepdims=True))


def attend(projected, gains):
    head_width = projected.shape[1] // 3
    queries, q_unit, q_inverse = rms_scale(projected[:, :head_width], gains[0])
    key_vecs, k_unit, k_inverse = rms_scale(projected[:, head_width : 2 * head_width], gains[1])
    query_b = queries.astype(jnp.bfloat16)
    key_b = key_vecs.astype(jnp.bfloat16)
    value_b = projected[:, 2 * head_width :].astype(jnp.bfloat16)
    scores = dot32_t(query_b, key_b) / math.sqrt(head_width)
    weights = jnp.exp(scores)
    soft_max = weights / jnp.sum(weights, axis=-1, keepdims=True)
    head_out = dot32(soft_max.astype(jnp.bfloat16), value_b).astype(jnp.bfloat16)
    return (head_out, (q_unit, q_inverse, k_unit, k_inverse, query_b, key_b, value_b, soft_max))


def attend_back(grad_out, stored, gains):
    q_unit, q_inverse, k_unit, k_inverse, query_b, key_b, value_b, soft_max = stored
    head_width = query_b.shape[-1]
    grad_soft = dot32_t(grad_out, value_b)
    grad_value = dot32(soft_max.astype(jnp.bfloat16).T, grad_out)
    grad_scores = soft_max * (grad_soft - jnp.sum(soft_max * grad_soft, axis=-1, keepdims=True))
    grad_scores_b = (grad_scores / math.sqrt(head_width)).astype(jnp.bfloat16)
    grad_query = dot32(grad_scores_b, key_b)
    grad_key = dot32(grad_scores_b.T, query_b)
    grad_q = rms_back(grad_query, q_unit, q_inverse, gains[0])
    grad_k = rms_back(grad_key, k_unit, k_inverse, gains[1])
    return jnp.concatenate([grad_q, grad_k, grad_value], axis=1).astype(jnp.bfloat16)


def shards(
    clean, noise, timesteps, text_vec, w_embed, w_time, w_mod, w_qkv, w_out, qk_gain, w_final
):
    section = lax.axis_index("segment")
    sections = lax.axis_size("segment")
    batch_idx = lax.axis_index("dp")
    seq_place = lax.axis_index("seq")
    tok_rows = clean.shape[1]
    latent_width = clean.shape[2]
    model_width = w_embed.shape[2]
    seq_devices = lax.axis_size("seq")
    full_rows = tok_rows * seq_devices
    head_width = w_qkv.shape[4]
    embed_w = w_embed[0]
    embed_f32 = embed_w.astype(jnp.float32)
    flat_head_w = w_qkv[0, :, 0].reshape(model_width, 3 * head_width)
    gains = qk_gain[0]
    final_w = w_final[0]
    step_pair = lax.dynamic_index_in_dim(timesteps, batch_idx, 0, keepdims=False)
    sigma_student = noise_level(step_pair[0])
    sigma_critic = noise_level(step_pair[1])
    own_step = jnp.where(section == 0, step_pair[0], step_pair[1])
    noisy_student = (
        (1.0 - sigma_student) * clean[0].astype(jnp.float32)
        + sigma_student * noise[0, :, :latent_width].astype(jnp.float32)
    ).astype(jnp.bfloat16)
    second_noise = noise[0, :, latent_width:].astype(jnp.float32)
    all_heads_w = jnp.concatenate(
        gather_doubling(w_out[0, 0], "seq", seq_devices), axis=0
    )
    student_rows = jnp.concatenate(gather_near(noisy_student, "seq", seq_devices), axis=0)

    mod_piece = condition(own_step, text_vec[0], w_time[0], w_mod[0])
    mod_parts = gather_near(mod_piece.reshape(1, -1), "seq", seq_devices)
    modulation = jnp.concatenate(in_order(mod_parts, seq_place), axis=1)
    shift_in, scale_in, gate_vec, shift_out, scale_out = [
        modulation[:, slot * model_width : (slot + 1) * model_width] for slot in range(5)
    ]

    centred_w = embed_f32 - jnp.mean(embed_f32, axis=1, keepdims=True)
    centred_top, _ = halves(centred_w)
    in_rows = jnp.concatenate([centred_w * (1.0 + scale_in), shift_in], axis=0)
    in_top, in_low = halves(in_rows)
    short = dot32(in_top, flat_head_w) + dot32(in_low, flat_head_w)
    short_w, short_shift = short[:latent_width], short[latent_width:]
    short_top, short_low = halves(short_w)
    gram = jnp.dot(centred_w, centred_w.T, precision=lax.Precision.HIGHEST)

    def forward(latent_rows, latent_local):
        centred = dot32(latent_rows, centred_top)
        inverse = lax.rsqrt(jnp.mean(centred * centred, axis=-1, keepdims=True) + EPS)
        projected = (
            inverse * (dot32(latent_rows, short_top) + dot32(latent_rows, short_low)) + short_shift
        )
        head_out, stored = attend(projected, gains)
        blocks = [
            head_out[place * tok_rows : (place + 1) * tok_rows] for place in range(seq_devices)
        ]
        mixed = jnp.concatenate(scatter_near(blocks, "seq", seq_devices), axis=1)
        residual = dot32(latent_local, embed_w) + gate_vec * dot32(mixed, all_heads_w)
        normed_out, inverse_out = normalize(residual)
        final_in = (normed_out * (1.0 + scale_out) + shift_out).astype(jnp.bfloat16)
        result = dot32(final_in, final_w)
        return (result, final_in, (inverse, stored, normed_out, inverse_out))

    velocity, student_in, _ = forward(student_rows, noisy_student)
    own_sample = noisy_student.astype(jnp.float32) - sigma_student * velocity
    own_critic = (1.0 - sigma_critic) * own_sample + sigma_critic * second_noise
    pair = jnp.concatenate([own_critic, own_sample], axis=1).astype(jnp.bfloat16)
    arrived = [
        lax.ppermute(pair, "segment", [(0, place)]) for place in range(sections - 1, 0, -1)
    ]
    pair = jnp.where(section == 0, pair, sum(arrived[1:], arrived[0]))
    noisy_critic = pair[:, :latent_width]
    sample = pair[:, latent_width:].astype(jnp.float32)
    critic_rows = jnp.concatenate(gather_near(noisy_critic, "seq", seq_devices), axis=0)
    critic_out, critic_in, cache = forward(critic_rows, noisy_critic)
    inverse, stored, normed_out, inverse_out = cache

    is_judge = section == 3
    grad_logit = -jax.nn.sigmoid(-critic_out)
    grad_final = dot32_t(grad_logit.astype(jnp.bfloat16), final_w)
    grad_residual = normalize_back(grad_final * (1.0 + scale_out), normed_out, inverse_out)
    grad_attended = (gate_vec * grad_residual).astype(jnp.bfloat16)
    grad_heads = dot32_t(grad_attended, all_heads_w).astype(jnp.bfloat16)
    grad_blocks = [
        grad_heads[:, place * head_width : (place + 1) * head_width]
        for place in range(seq_devices)
    ]
    grad_head = jnp.concatenate(scatter_near(grad_blocks, "seq", seq_devices), axis=0)
    grad_proj = attend_back(grad_head, stored, gains)
    through = dot32_t(grad_proj, short_top) + dot32_t(grad_proj, short_low)
    critic_f32 = critic_rows.astype(jnp.float32)
    along = jnp.sum(through * critic_f32, axis=-1, keepdims=True) / model_width
    spanned = jnp.dot(critic_f32, gram, precision=lax.Precision.HIGHEST)
    grad_rows = inverse * (through - spanned * (inverse * inverse * along))

    noisy_critic_f32 = noisy_critic.astype(jnp.float32)
    scaled_out = sigma_critic * critic_out
    error_local = jnp.sum(jnp.abs(sample - noisy_critic_f32 + scaled_out))
    error_top, error_low = halves(error_local / (tok_rows * latent_width))
    error_row = jnp.concatenate(
        [jnp.full((8, latent_width), error_top), jnp.full((8, latent_width), error_low)], axis=0
    )
    grad_parts = scatter_near(
        [
            jnp.concatenate(
                [
                    grad_rows[place * tok_rows : (place + 1) * tok_rows].astype(jnp.bfloat16),
                    error_row,
                ],
                axis=0,
            )
            for place in range(seq_devices)
        ],
        "seq",
        seq_devices,
    )
    grad_total = sum([part.astype(jnp.float32) for part in grad_parts[1:]], grad_parts[0].astype(jnp.float32))
    error_mean = (grad_total[tok_rows : tok_rows + 1] + grad_total[tok_rows + 8 : tok_rows + 9])[
        :, :1
    ] / seq_devices
    direct = jnp.dot(grad_residual, embed_f32.T, precision=lax.Precision.HIGHEST)
    adverse = (1.0 - sigma_critic) * (grad_total[:tok_rows] + direct)
    term_rows = jnp.where(is_judge, adverse, scaled_out)
    spread_top, spread_low = halves(error_mean + EPS)
    payload = jnp.concatenate(
        [
            term_rows.astype(jnp.bfloat16),
            jnp.broadcast_to(spread_top, (8, latent_width)),
            jnp.broadcast_to(spread_low, (8, latent_width)),
        ],
        axis=0,
    )
    received = [payload] + [
        lax.ppermute(
            payload, "segment", [(place, (place + offset) % sections) for place in range(sections)]
        )
        for offset in range(1, sections)
    ]

    def payload_of(source):
        chosen = received[0]
        for offset in range(1, sections):
            chosen = jnp.where((section - offset) % sections == source, received[offset], chosen)
        return chosen.astype(jnp.float32)

    real_rows, fake_rows, adverse_rows = [payload_of(source) for source in (1, 2, 3)]
    spread = (real_rows[tok_rows : tok_rows + 1] + real_rows[tok_rows + 8 : tok_rows + 9])[:, :1]
    sample_grad = (real_rows[:tok_rows] - fake_rows[:tok_rows]) / spread + ADV_WEIGHT * adverse_rows[
        :tok_rows
    ]
    target = jnp.where(
        section == 0,
        -sigma_student * sample_grad,
        jnp.where(
            section == 2,
            2.0 * (critic_out - (second_noise - sample)),
            jnp.where(is_judge, jax.nn.sigmoid(critic_out), 0.0),
        ),
    )
    final_rows = jnp.where(section == 0, student_in, critic_in)
    term = lax.dot_general(
        final_rows,
        target.astype(jnp.bfloat16),
        (((0,), (0,)), ((), ())),
        preferred_element_type=jnp.float32,
    ).astype(jnp.bfloat16)
    share_count = seq_devices * lax.axis_size("dp")
    share = model_width // share_count
    exchanged = lax.all_to_all(
        term.reshape(share_count, share, latent_width),
        ("seq", "dp"),
        split_axis=0,
        concat_axis=0,
        tiled=True,
    )
    own_total = jnp.sum(exchanged.astype(jnp.float32), axis=0).astype(jnp.bfloat16)
    total = lax.all_to_all(
        jnp.broadcast_to(own_total[None], (share_count, share, latent_width)),
        ("seq", "dp"),
        split_axis=0,
        concat_axis=0,
        tiled=True,
    )
    final_grads = total.astype(jnp.float32).reshape(model_width, latent_width) / full_rows
    return (sample_grad[None], final_grads[None])


def solution(mesh):
    placed = (
        P("dp", "seq", None),
        P("dp", "seq", None),
        P(),
        P("dp", None),
        P("segment", None, None),
        P("segment", None, None),
        P("segment", None, "seq"),
        P("segment", None, "seq", None, None),
        P("segment", "seq", None, None),
        P("segment", None, None),
        P("segment", None, None),
    )
    return jax.shard_map(
        shards,
        mesh=mesh,
        in_specs=placed,
        out_specs=(P("dp", "seq", None), P("segment", None, None)),
        check_vma=False,
    )
```

time: 276 us -> 150 us (0.54)
  waiting for transfers between devices: 126 us -> 26.3 us
  blocking collectives: 60.4 us -> 21 us
  starting transfers between devices: 10.7 us -> 29.8 us
  matrix products: 29.3 us -> 36.4 us
  between operations: 17.2 us -> 11.1 us
  other arithmetic: 10.9 us -> 7.27 us
  local copies, waits for them, and re-layouts: 20 us -> 16.7 us
    unnamed x4 -> x0, waiting for transfers between devices: 61.5 us -> none
    psum x1 -> x0, waiting for transfers between devices: 51.6 us -> none  [shards(): lax.psum(term.astype(jnp.bfloat16), ('seq', 'dp')).astype(jnp.float32)]
    psum x3 -> x0, blocking collectives: 42 us -> none  [the longest x1 19.9 us: shards(): lax.psum(judge_part.astype(jnp.bfloat16), 'segment').astype(jnp.float32)]
    ppermute x0 -> x29, starting transfers between devices: none -> 29.8 us  [the longest x12 7.84 us: scatter_near(): lax.ppermute(blocks[offset], axis, swaps(count, offset))]
    ppermute x0 -> x29, waiting for transfers between devices: none -> 26.3 us  [the longest x2 10.1 us: gather_doubling(): moved = lax.ppermute(joined, axis, swaps(count, bit))]
    all_to_all x0 -> x2, blocking collectives: none -> 21 us  [the longest x1 10.7 us: shards(): lax.all_to_all(term.reshape(share_count, share, latent_width), ('seq', 'd...]
    all_gather x3 -> x0, blocking collectives: 18.3 us -> none  [the longest x2 11.7 us: forward(): latent_all = lax.all_gather(latent_local, 'seq', axis=0, tiled=True)]
    all_to_all x3 -> x0, waiting for transfers between devices: 13 us -> none  [the longest x2 8.52 us: forward(): lax.all_to_all(head_out, 'seq', split_axis=0, concat_axis=1, tiled=True)]
  transfers between devices with their start and end apart: 6 -> 29, of which waited for: 5 -> 13; matrix products, arithmetic and copies ran while one was open for 9% -> 14% of each run, Pallas kernels for 0% -> 0%
where the time goes in v1:
time: 150 us; the launch traced here: 149 us
  matrix products  36.4 us (24%)
  starting transfers between devices  29.8 us (20%)
  waiting for transfers between devices  26.3 us (18%)
  blocking collectives  21 us (14%)
  local copies, waits for them, and re-layouts  16.7 us (11%)
  between operations  11.1 us (7%)
  other arithmetic  7.27 us (5%)
    dot_general x19, matrix products, dot32(): return jnp.dot(left, right, preferred_element_type=jnp.float32)  15.2 us
    all_to_all x1, blocking collectives, shards(): lax.all_to_all(term.reshape(share_count, share, latent_width), ('seq', 'd...  10.7 us
    all_to_all x1, blocking collectives, shards(): lax.all_to_all(jnp.broadcast_to(own_total[None], (share_count, share, lat...  10.3 us
    ppermute x2, waiting for transfers between devices, gather_doubling(): moved = lax.ppermute(joined, axis, swaps(count, bit))  10.1 us
    dot_general x1, matrix products, condition(): return jnp.dot(hidden, mod_w, preferred_element_type=jnp.float32)  10 us
    ppermute x12, waiting for transfers between devices, scatter_near(): lax.ppermute(blocks[offset], axis, swaps(count, offset))  9.04 us
    unnamed x93, local copies, waits for them, and re-layouts  9 us
    ppermute x12, starting transfers between devices, scatter_near(): lax.ppermute(blocks[offset], axis, swaps(count, offset))  7.84 us
  transfers between devices with their start and end apart: 29, of which 13 were waited for; matrix products, arithmetic and copies ran while one was open for 14% of the time, Pallas kernels for 0%

profile of v1, /device:TPU:0, one launch (start us, length us, event | category | flops | bytes accessed | tf_op | source)
XLA Modules:
  0.0 148.6 jit_solution(48981583097579858)
XLA Ops:
  0.6 0.8 constant_dynamic-slice_fusion
  3.4 1.0 fusion.3
  4.5 10.0 %fusion = f32[1,3840]{1,0:T(1,128)} fusion(bf16[3072,1]{0,1:T(2,128)(2,1)S(1)} %reshape.186, bf16[1,3072,3840]{2,1,0:T(8,128)(2,1)} %param.17), kind=kOutput, calls=%fused_computation | convolution fusion | flops 23592960 | bytes 23614464 | tf_op jit(solution)/shard_map/dot_general | solution.py:88
  15.0 2.6 %collective-permute-start.1 = (f32[1,3840]{1,0:T(1,128)}, f32[1,3840]{1,0:T(1,128)}, u32[]{:S(2)}, u32[]{:S(2)}) collective-permute-start(f32[1,3840]{1,0:T(1,128)} %fusion), channel_id=1, source_target_pairs={{0,6},{2,4},{4,2},{6,0},{1,7},{3,5},{5,3},{7,1},{8,14},{10,12},{12... | collective-permute-start | bytes 46088 | tf_op jit(solution)/shard_map/ppermute | solution.py:24
  18.2 0.7 fusion.125
  19.1 1.4 collective-permute-start.5
  20.5 0.8 collective-permute-start.4
  21.8 1.3 slice_bitcast_fusion.1
  24.3 1.4 copy.28
  25.8 4.3 %copy.23 = bf16[1,3072,1,3,128]{1,4,3,2,0:T(8,128)(2,1)} copy(bf16[1,3072,1,3,128]{4,1,3,2,0:T(8,128)(2,1)} %param.18) | data formatting | bytes 4718592 | tf_op args[7]
  30.1 1.7 %collective-permute-start.9 = (bf16[128,3072]{1,0:T(8,128)(2,1)}, bf16[128,3072]{1,0:T(8,128)(2,1)S(1)}, u32[]{:S(2)}, u32[]{:S(2)}) collective-permute-start(bf16[128,3072]{1,0:T(8,128)(2,1)} %bitcast.87), channel_id=1, source_target_pairs={{0,4},{2,6},{4,0},{6,2},{1,5},{3,7},{5,1},{7,3},{8,12},{10,14},{12... | collective-permute-start | bytes 2359304 | tf_op jit(solution)/shard_map/ppermute | solution.py:40
  31.8 0.8 broadcast_select_fusion.5
  32.7 0.8 fusion.15
  33.5 2.7 %fusion.27 = f32[65,384]{1,0:T(8,128)S(1)} fusion(bf16[3072,384]{0,1:T(8,128)(2,1)} %bitcast.83, f32[1,3072]{1,0:T(1,128)S(1)} %get-tuple-element.45, f32[64,3072]{1,0:T(8,128)S(1)} %fusion.15), kind=kOutput, calls=%fused_computation.67 | convolution fusion | flops 153953280 | bytes 3257856 | tf_op jit(solution)/shard_map/dot_general | solution.py:62
  36.2 0.9 convolution_add_fusion.4
  37.1 1.9 %multiply_reduce_fusion.1 = f32[512]{0:T(512)S(1)} fusion(bf16[1,64,3072]{2,1,0:T(8,128)(2,1)S(1)} %copy-done.2, f32[64]{0:T(128)S(1)} %copy-done.43, bf16[128,64]{0,1:T(8,128)(2,1)} %collective-permute-done.5, bf16[128,64]{0,1:T(8,128)(2,1)} %collective-permute-done.4, bf16[128,64]{0,1:T(8,128)(2,1)S(1)} %collective-permute-done.3, ...), kind=kOutput, calls=%fused_computation.3 | convolution fusion | flops 205520384 | bytes 461056 | tf_op jit(solution)/shard_map/dot_general | solution.py:62
  39.0 1.1 fusion.115
  40.1 10.1 %collective-permute-done.9 = bf16[128,3072]{1,0:T(8,128)(2,1)S(1)} collective-permute-done((bf16[128,3072]{1,0:T(8,128)(2,1)}, bf16[128,3072]{1,0:T(8,128)(2,1)S(1)}, u32[]{:S(2)}, u32[]{:S(2)}) %collective-permute-start.9) | collective-permute-done | bytes 786464 | tf_op jit(solution)/shard_map/ppermute | solution.py:40
  50.4 1.1 fusion.10
  52.3 1.5 %collective-permute-start.8 = (bf16[128,128]{0,1:T(8,128)(2,1)S(1)}, bf16[128,128]{0,1:T(8,128)(2,1)S(1)}, u32[]{:S(2)}, u32[]{:S(2)}) collective-permute-start(bf16[128,128]{0,1:T(8,128)(2,1)S(1)} %get-tuple-element.23), channel_id=1, source_target_pairs={{0,6},{2,4},{4,2},{6,0},{1,7},{3,5},{5,3},{7,1},{8,14},{10,12},{12... | collective-permute-start | bytes 98312 | tf_op jit(solution)/shard_map/ppermute | solution.py:30
  53.8 0.7 collective-permute-start.7
  54.6 1.1 collective-permute-done.8
  55.7 2.0 %collective-permute-done.7 = bf16[128,128]{0,1:T(8,128)(2,1)S(1)} collective-permute-done((bf16[128,128]{0,1:T(8,128)(2,1)S(1)}, bf16[128,128]{0,1:T(8,128)(2,1)S(1)}, u32[]{:S(2)}, u32[]{:S(2)}) %collective-permute-start.7) | collective-permute-done | bytes 32800 | tf_op jit(solution)/shard_map/ppermute | solution.py:30
  57.8 0.7 fusion.128
  59.2 0.6 copy-done.8
  60.2 3.5 %collective-permute-start.13 = (bf16[128,128]{0,1:T(8,128)(2,1)S(1)}, bf16[128,128]{0,1:T(8,128)(2,1)S(1)}, u32[]{:S(2)}, u32[]{:S(2)}) collective-permute-start(bf16[128,128]{0,1:T(8,128)(2,1)S(1)} %pad_maximum_fusion.9), channel_id=1, source_target_pairs={{0,8},{1,9},{2,10},{3,11},{4,12},{5,13},{6,14},{7,15}} | collective-permute-start | bytes 98312 | tf_op jit(solution)/shard_map/ppermute | solution.py:215
  63.7 2.7 %collective-permute-start.11 = (bf16[128,128]{0,1:T(8,128)(2,1)S(1)}, bf16[128,128]{0,1:T(8,128)(2,1)S(1)}, u32[]{:S(2)}, u32[]{:S(2)}) collective-permute-start(bf16[128,128]{0,1:T(8,128)(2,1)S(1)} %pad_maximum_fusion.9), channel_id=1, source_target_pairs={{0,24},{1,25},{2,26},{3,27},{4,28},{5,29},{6,30},{7,31}} | collective-permute-start | bytes 98312 | tf_op jit(solution)/shard_map/ppermute | solution.py:215
  66.4 1.5 collective-permute-start.12
  68.0 1.3 collective-permute-done.12
  69.4 0.8 collective-permute-start.15
  70.2 1.1 collective-permute-start.14
  71.3 1.3 collective-permute-done.16
  72.6 0.7 collective-permute-done.15
  73.2 1.1 multiply_reduce_fusion
  77.4 0.7 collective-permute-start.18
  78.1 0.7 collective-permute-start.17
  78.8 1.6 %collective-permute-done.19 = bf16[128,128]{0,1:T(8,128)(2,1)S(1)} collective-permute-done((bf16[128,128]{0,1:T(8,128)(2,1)S(1)}, bf16[128,128]{0,1:T(8,128)(2,1)S(1)}, u32[]{:S(2)}, u32[]{:S(2)}) %collective-permute-start.19) | collective-permute-done | bytes 32800 | tf_op jit(solution)/shard_map/ppermute | solution.py:30
  80.4 1.0 collective-permute-done.18
  83.1 1.0 fusion.65
  84.2 0.6 fusion.117
  85.4 1.2 convolution_convert_fusion.4
  86.6 0.7 fusion.119
  87.3 0.7 collective-permute-start.22
  88.3 0.8 collective-permute-start.20
  89.1 1.5 %fusion.19 = f32[64,64]{1,0:T(8,128)} fusion(bf16[1,64,3072]{2,1,0:T(8,128)(2,1)S(1)} %copy-done.2, f32[64]{0:T(128)S(1)} %copy-done.43), kind=kOutput, calls=%fused_computation.58 | convolution fusion | flops 151388160 | bytes 409856 | tf_op jit(solution)/shard_map/dot_general | solution.py:191
  93.3 1.7 %multiply_reduce_fusion.5 = (f32[512]{0:T(512)S(1)}, f32[512,512]{0,1:T(8,128)S(1)}) fusion(f32[512,512]{0,1:T(8,128)} %copy-done.6, f32[512]{0:T(512)} %copy-done.35, f32[512,384]{0,1:T(8,128)S(1)} %fusion.8, bf16[128,128]{1,0:T(8,128)(2,1)} %collective-permute-done.22, bf16[128,128]{1,0:T(8,128)(2,1)} %collective-permute-done.21, ...), kind=kOutput, calls=%fused_computation.49 | convolution fusion | flops 68419072 | bytes 2363392 | tf_op jit(solution)/shard_map/dot_general | solution.py:66
  96.8 1.1 convolution_convert_fusion.3
  99.0 0.6 fusion.124
  99.6 0.6 maximum_maximum_fusion
  100.3 1.0 collective-permute-start.25
  101.2 0.7 collective-permute-start.24
  102.1 2.0 %collective-permute-done.25 = bf16[144,64]{0,1:T(8,128)(2,1)} collective-permute-done((bf16[144,64]{0,1:T(8,128)(2,1)}, bf16[144,64]{0,1:T(8,128)(2,1)}, u32[]{:S(2)}, u32[]{:S(2)}) %collective-permute-start.25) | collective-permute-done | bytes 18464 | tf_op jit(solution)/shard_map/ppermute | solution.py:30
  104.1 1.4 collective-permute-done.24
  105.5 0.8 convert_add_fusion
  110.0 2.5 %fusion.77 = bf16[128,64]{0,1:T(8,128)(2,1)S(1)} fusion(f32[144,64]{0,1:T(8,128)S(1)} %convert_add_fusion, f32[128,64]{0,1:T(8,128)} %copy-done.12, f32[]{:T(128)S(6)} %div.124, f32[]{:T(128)S(6)} %sub.110, pred[]{:T(512)S(6)} %eq.50, f32[128,3072]{1,0:T(8,128)} %copy-done.5, bf16[1,64,3072]{2,1,0:T(8,128)(2,1)S(1)} %copy-done.2), kind=kOutput, calls=%fused_computation.145 | convolution fusion | flops 302030848 | bytes 2048009 | tf_op jit(solution)/shard_map/dot_general | solution.py:267
  113.1 2.9 %collective-permute-start.26 = (bf16[144,64]{0,1:T(8,128)(2,1)S(1)}, bf16[144,64]{0,1:T(8,128)(2,1)S(1)}, u32[]{:S(2)}, u32[]{:S(2)}) collective-permute-start(bf16[144,64]{0,1:T(8,128)(2,1)S(1)} %maximum_maximum_fusion.3), channel_id=1, source_target_pairs={{0,24},{8,0},{16,8},{24,16},{1,25},{9,1},{17,9},{25,17},{2,26},{10... | collective-permute-start | bytes 55304 | tf_op jit(solution)/shard_map/ppermute | solution.py:280
  116.4 1.9 %collective-permute-start.28 = (bf16[144,64]{0,1:T(8,128)(2,1)S(1)}, bf16[144,64]{0,1:T(8,128)(2,1)S(1)}, u32[]{:S(2)}, u32[]{:S(2)}) collective-permute-start(bf16[144,64]{0,1:T(8,128)(2,1)S(1)} %maximum_maximum_fusion.3), channel_id=1, source_target_pairs={{0,8},{8,16},{16,24},{24,0},{1,9},{9,17},{17,25},{25,1},{2,10},{10... | collective-permute-start | bytes 55304 | tf_op jit(solution)/shard_map/ppermute | solution.py:280
  118.4 2.4 %collective-permute-done.27 = bf16[144,64]{0,1:T(8,128)(2,1)S(1)} collective-permute-done((bf16[144,64]{0,1:T(8,128)(2,1)S(1)}, bf16[144,64]{0,1:T(8,128)(2,1)S(1)}, u32[]{:S(2)}, u32[]{:S(2)}) %collective-permute-start.27) | collective-permute-done | bytes 18464 | tf_op jit(solution)/shard_map/ppermute | solution.py:280
  120.8 1.4 collective-permute-done.28
  122.1 0.7 select_convert_fusion
  124.8 1.1 convolution_convert_fusion
  126.0 10.7 %all_to_all.10 = bf16[8,384,64]{1,2,0:T(8,128)(2,1)S(1)} all-to-all(bf16[8,384,64]{1,2,0:T(8,128)(2,1)S(1)} %bitcast.85), channel_id=1, replica_groups=mesh['segment'=4,'seq'=4,'dp'=2] {'seq','dp'}, dimensions={0} | all-to-all | bytes 786432 | tf_op jit(solution)/shard_map/all_to_all | solution.py:315
  136.7 10.3 %all_to_all.11 = bf16[8,384,64]{1,2,0:T(8,128)(2,1)S(1)} all-to-all(bf16[8,384,64]{1,2,0:T(8,128)(2,1)S(1)} %broadcast_in_dim.27), channel_id=1, replica_groups=mesh['segment'=4,'seq'=4,'dp'=2] {'seq','dp'}, dimensions={0} | all-to-all | bytes 786432 | tf_op jit(solution)/shard_map/all_to_all | solution.py:323
  147.6 1.0 div.162
  (189 shorter events, 16.3 us)
Async XLA Ops:
  0.6 2.8 %copy-start = (bf16[1,256,3072]{2,1,0:T(8,128)(2,1)S(1)}, bf16[1,256,3072]{2,1,0:T(8,128)(2,1)}, u32[]{:S(2)}) copy-start(bf16[1,256,3072]{2,1,0:T(8,128)(2,1)} %param.16) | copy-start | bytes 4718596
  4.4 13.8 %copy-start.18 = (bf16[1,128,128]{2,1,0:T(8,128)(2,1)S(1)}, bf16[1,128,128]{2,1,0:T(8,128)(2,1)}, u32[]{:S(2)}) copy-start(bf16[1,128,128]{2,1,0:T(8,128)(2,1)} %param.12) | copy-start | bytes 98308
  4.4 14.7 %copy-start.30 = (bf16[1,128,64]{1,2,0:T(8,128)(2,1)S(1)}, bf16[1,128,64]{1,2,0:T(8,128)(2,1)}, u32[]{:S(2)}) copy-start(bf16[1,128,64]{1,2,0:T(8,128)(2,1)} %param.11) | copy-start | bytes 49156
  4.4 16.8 %copy-start.2 = (bf16[1,64,3072]{2,1,0:T(8,128)(2,1)S(1)}, bf16[1,64,3072]{2,1,0:T(8,128)(2,1)}, u32[]{:S(2)}) copy-start(bf16[1,64,3072]{2,1,0:T(8,128)(2,1)} %param.15) | copy-start | bytes 1179652
  14.5 15.6 %collective-permute-start.2 = (f32[1,3840]{1,0:T(1,128)}, f32[1,3840]{1,0:T(1,128)}, u32[]{:S(2)}, u32[]{:S(2)}) collective-permute-start(f32[1,3840]{1,0:T(1,128)} %fusion), channel_id=1, source_target_pairs={{0,2},{2,0},{4,6},{6,4},{1,3},{3,1},{5,7},{7,5},{8,10},{10,8},{12,... | collective-permute-start | bytes 46088 | tf_op jit(solution)/shard_map/ppermute | solution.py:24
  15.0 15.1 %collective-permute-start.1 = (f32[1,3840]{1,0:T(1,128)}, f32[1,3840]{1,0:T(1,128)}, u32[]{:S(2)}, u32[]{:S(2)}) collective-permute-start(f32[1,3840]{1,0:T(1,128)} %fusion), channel_id=1, source_target_pairs={{0,6},{2,4},{4,2},{6,0},{1,7},{3,5},{5,3},{7,1},{8,14},{10,12},{12... | collective-permute-start | bytes 46088 | tf_op jit(solution)/shard_map/ppermute | solution.py:24
  17.6 14.3 %collective-permute-start = (f32[1,3840]{1,0:T(1,128)}, f32[1,3840]{1,0:T(1,128)}, u32[]{:S(2)}, u32[]{:S(2)}) collective-permute-start(f32[1,3840]{1,0:T(1,128)} %fusion), channel_id=1, source_target_pairs={{0,4},{2,6},{4,0},{6,2},{1,5},{3,7},{5,1},{7,3},{8,12},{10,14},{12... | collective-permute-start | bytes 46088 | tf_op jit(solution)/shard_map/ppermute | solution.py:24
  19.1 17.9 %collective-permute-start.5 = (bf16[128,64]{0,1:T(8,128)(2,1)S(1)}, bf16[128,64]{0,1:T(8,128)(2,1)}, u32[]{:S(2)}, u32[]{:S(2)}) collective-permute-start(bf16[128,64]{0,1:T(8,128)(2,1)S(1)} %fusion.78), channel_id=1, source_target_pairs={{0,6},{2,4},{4,2},{6,0},{1,7},{3,5},{5,3},{7,1},{8,14},{10,12},{12... | collective-permute-start | bytes 49160 | tf_op jit(solution)/shard_map/ppermute | solution.py:24
  20.5 16.5 %collective-permute-start.4 = (bf16[128,64]{0,1:T(8,128)(2,1)S(1)}, bf16[128,64]{0,1:T(8,128)(2,1)}, u32[]{:S(2)}, u32[]{:S(2)}) collective-permute-start(bf16[128,64]{0,1:T(8,128)(2,1)S(1)} %fusion.78), channel_id=1, source_target_pairs={{0,4},{2,6},{4,0},{6,2},{1,5},{3,7},{5,1},{7,3},{8,12},{10,14},{12... | collective-permute-start | bytes 49160 | tf_op jit(solution)/shard_map/ppermute | solution.py:24
  30.1 7.0 %collective-permute-start.3 = (bf16[128,64]{0,1:T(8,128)(2,1)S(1)}, bf16[128,64]{0,1:T(8,128)(2,1)S(1)}, u32[]{:S(2)}, u32[]{:S(2)}) collective-permute-start(bf16[128,64]{0,1:T(8,128)(2,1)S(1)} %fusion.78), channel_id=1, source_target_pairs={{0,2},{2,0},{4,6},{6,4},{1,3},{3,1},{5,7},{7,5},{8,10},{10,8},{12,... | collective-permute-start | bytes 49160 | tf_op jit(solution)/shard_map/ppermute | solution.py:24
  30.1 20.1 %collective-permute-start.9 = (bf16[128,3072]{1,0:T(8,128)(2,1)}, bf16[128,3072]{1,0:T(8,128)(2,1)S(1)}, u32[]{:S(2)}, u32[]{:S(2)}) collective-permute-start(bf16[128,3072]{1,0:T(8,128)(2,1)} %bitcast.87), channel_id=1, source_target_pairs={{0,4},{2,6},{4,0},{6,2},{1,5},{3,7},{5,1},{7,3},{8,12},{10,14},{12... | collective-permute-start | bytes 2359304 | tf_op jit(solution)/shard_map/ppermute | solution.py:40
  33.5 2.7 %copy-start.1 = (bf16[1,3072,1,3,128]{1,4,3,2,0:T(8,128)(2,1)S(1)}, bf16[1,3072,1,3,128]{1,4,3,2,0:T(8,128)(2,1)}, u32[]{:S(2)}) copy-start(bf16[1,3072,1,3,128]{1,4,3,2,0:T(8,128)(2,1)} %copy.23) | copy-start | bytes 7077892
  36.2 0.9 copy-start.43
  37.0 37.7 %copy-start.9 = (f32[65,384]{1,0:T(8,128)}, f32[65,384]{1,0:T(8,128)S(1)}, u32[]{:S(2)}) copy-start(f32[65,384]{1,0:T(8,128)S(1)} %convolution_add_fusion.4) | copy-start | bytes 299524
  37.1 13.2 %copy-start.11 = (bf16[1,1,128,3072]{3,2,1,0:T(8,128)(2,1)S(1)}, bf16[1,1,128,3072]{3,2,1,0:T(8,128)(2,1)}, u32[]{:S(2)}) copy-start(bf16[1,1,128,3072]{3,2,1,0:T(8,128)(2,1)} %param.19) | copy-start | bytes 2359300
  50.3 1.3 copy-start.31
  50.4 1.3 copy-start.33
  50.4 4.2 %collective-permute-start.10 = (bf16[256,3072]{1,0:T(8,128)(2,1)S(1)}, bf16[256,3072]{1,0:T(8,128)(2,1)S(1)}, u32[]{:S(2)}, u32[]{:S(2)}) collective-permute-start(bf16[256,3072]{1,0:T(8,128)(2,1)S(1)} %pad_maximum_fusion.1), channel_id=1, source_target_pairs={{0,2},{2,0},{4,6},{6,4},{1,3},{3,1},{5,7},{7,5},{8,10},{10,8},{12,... | collective-permute-start | bytes 4718600 | tf_op jit(solution)/shard_map/ppermute | solution.py:40
  52.3 3.4 %collective-permute-start.8 = (bf16[128,128]{0,1:T(8,128)(2,1)S(1)}, bf16[128,128]{0,1:T(8,128)(2,1)S(1)}, u32[]{:S(2)}, u32[]{:S(2)}) collective-permute-start(bf16[128,128]{0,1:T(8,128)(2,1)S(1)} %get-tuple-element.23), channel_id=1, source_target_pairs={{0,6},{2,4},{4,2},{6,0},{1,7},{3,5},{5,3},{7,1},{8,14},{10,12},{12... | collective-permute-start | bytes 98312 | tf_op jit(solution)/shard_map/ppermute | solution.py:30
  53.8 3.9 %collective-permute-start.7 = (bf16[128,128]{0,1:T(8,128)(2,1)S(1)}, bf16[128,128]{0,1:T(8,128)(2,1)S(1)}, u32[]{:S(2)}, u32[]{:S(2)}) collective-permute-start(bf16[128,128]{0,1:T(8,128)(2,1)S(1)} %get-tuple-element.24), channel_id=1, source_target_pairs={{0,4},{2,6},{4,0},{6,2},{1,5},{3,7},{5,1},{7,3},{8,12},{10,14},{12... | collective-permute-start | bytes 98312 | tf_op jit(solution)/shard_map/ppermute | solution.py:30
  54.5 3.2 %collective-permute-start.6 = (bf16[128,128]{0,1:T(8,128)(2,1)S(1)}, bf16[128,128]{0,1:T(8,128)(2,1)S(1)}, u32[]{:S(2)}, u32[]{:S(2)}) collective-permute-start(bf16[128,128]{0,1:T(8,128)(2,1)S(1)} %get-tuple-element.25), channel_id=1, source_target_pairs={{0,2},{2,0},{4,6},{6,4},{1,3},{3,1},{5,7},{7,5},{8,10},{10,8},{12,... | collective-permute-start | bytes 98312 | tf_op jit(solution)/shard_map/ppermute | solution.py:30
  58.8 1.0 copy-start.8
  58.8 1.0 copy-start.14
  60.2 7.7 %collective-permute-start.13 = (bf16[128,128]{0,1:T(8,128)(2,1)S(1)}, bf16[128,128]{0,1:T(8,128)(2,1)S(1)}, u32[]{:S(2)}, u32[]{:S(2)}) collective-permute-start(bf16[128,128]{0,1:T(8,128)(2,1)S(1)} %pad_maximum_fusion.9), channel_id=1, source_target_pairs={{0,8},{1,9},{2,10},{3,11},{4,12},{5,13},{6,14},{7,15}} | collective-permute-start | bytes 98312 | tf_op jit(solution)/shard_map/ppermute | solution.py:215
  63.7 4.3 %collective-permute-start.11 = (bf16[128,128]{0,1:T(8,128)(2,1)S(1)}, bf16[128,128]{0,1:T(8,128)(2,1)S(1)}, u32[]{:S(2)}, u32[]{:S(2)}) collective-permute-start(bf16[128,128]{0,1:T(8,128)(2,1)S(1)} %pad_maximum_fusion.9), channel_id=1, source_target_pairs={{0,24},{1,25},{2,26},{3,27},{4,28},{5,29},{6,30},{7,31}} | collective-permute-start | bytes 98312 | tf_op jit(solution)/shard_map/ppermute | solution.py:215
  66.4 2.9 %collective-permute-start.12 = (bf16[128,128]{0,1:T(8,128)(2,1)S(1)}, bf16[128,128]{0,1:T(8,128)(2,1)S(1)}, u32[]{:S(2)}, u32[]{:S(2)}) collective-permute-start(bf16[128,128]{0,1:T(8,128)(2,1)S(1)} %pad_maximum_fusion.9), channel_id=1, source_target_pairs={{0,16},{1,17},{2,18},{3,19},{4,20},{5,21},{6,22},{7,23}} | collective-permute-start | bytes 98312 | tf_op jit(solution)/shard_map/ppermute | solution.py:215
  69.3 13.8 %copy-start.13 = (bf16[128,128]{0,1:T(8,128)(2,1)}, bf16[128,128]{0,1:T(8,128)(2,1)S(1)}, u32[]{:S(2)}) copy-start(bf16[128,128]{0,1:T(8,128)(2,1)S(1)} %add_select_fusion) | copy-start | bytes 98308
  69.3 3.2 %collective-permute-start.16 = (bf16[128,64]{0,1:T(8,128)(2,1)S(1)}, bf16[128,64]{0,1:T(8,128)(2,1)S(1)}, u32[]{:S(2)}, u32[]{:S(2)}) collective-permute-start(bf16[128,64]{0,1:T(8,128)(2,1)S(1)} %slice.236), channel_id=1, source_target_pairs={{0,6},{2,4},{4,2},{6,0},{1,7},{3,5},{5,3},{7,1},{8,14},{10,12},{12... | collective-permute-start | bytes 49160 | tf_op jit(solution)/shard_map/ppermute | solution.py:24
  69.4 3.8 %collective-permute-start.15 = (bf16[128,64]{0,1:T(8,128)(2,1)S(1)}, bf16[128,64]{0,1:T(8,128)(2,1)S(1)}, u32[]{:S(2)}, u32[]{:S(2)}) collective-permute-start(bf16[128,64]{0,1:T(8,128)(2,1)S(1)} %slice.236), channel_id=1, source_target_pairs={{0,4},{2,6},{4,0},{6,2},{1,5},{3,7},{5,1},{7,3},{8,12},{10,14},{12... | collective-permute-start | bytes 49160 | tf_op jit(solution)/shard_map/ppermute | solution.py:24
  70.2 3.1 %collective-permute-start.14 = (bf16[128,64]{0,1:T(8,128)(2,1)S(1)}, bf16[128,64]{0,1:T(8,128)(2,1)S(1)}, u32[]{:S(2)}, u32[]{:S(2)}) collective-permute-start(bf16[128,64]{0,1:T(8,128)(2,1)S(1)} %slice.236), channel_id=1, source_target_pairs={{0,2},{2,0},{4,6},{6,4},{1,3},{3,1},{5,7},{7,5},{8,10},{10,8},{12,... | collective-permute-start | bytes 49160 | tf_op jit(solution)/shard_map/ppermute | solution.py:24
  72.6 2.1 %copy-start.19 = (bf16[128,64]{0,1:T(8,128)(2,1)}, bf16[128,64]{0,1:T(8,128)(2,1)S(1)}, u32[]{:S(2)}) copy-start(bf16[128,64]{0,1:T(8,128)(2,1)S(1)} %collective-permute-done.16) | copy-start | bytes 49156
  73.2 1.5 %copy-start.21 = (bf16[128,64]{0,1:T(8,128)(2,1)}, bf16[128,64]{0,1:T(8,128)(2,1)S(1)}, u32[]{:S(2)}) copy-start(bf16[128,64]{0,1:T(8,128)(2,1)S(1)} %collective-permute-done.15) | copy-start | bytes 49156
  73.2 1.5 %copy-start.23 = (bf16[128,64]{0,1:T(8,128)(2,1)}, bf16[128,64]{0,1:T(8,128)(2,1)S(1)}, u32[]{:S(2)}) copy-start(bf16[128,64]{0,1:T(8,128)(2,1)S(1)} %collective-permute-done.14) | copy-start | bytes 49156
  74.4 1.0 copy-start.37
  75.8 1.0 copy-start.6
  75.8 1.0 copy-start.35
  76.9 3.5 %collective-permute-start.19 = (bf16[128,128]{0,1:T(8,128)(2,1)S(1)}, bf16[128,128]{0,1:T(8,128)(2,1)S(1)}, u32[]{:S(2)}, u32[]{:S(2)}) collective-permute-start(bf16[128,128]{0,1:T(8,128)(2,1)S(1)} %get-tuple-element.19), channel_id=1, source_target_pairs={{0,6},{2,4},{4,2},{6,0},{1,7},{3,5},{5,3},{7,1},{8,14},{10,12},{12... | collective-permute-start | bytes 98312 | tf_op jit(solution)/shard_map/ppermute | solution.py:30
  77.4 3.9 %collective-permute-start.18 = (bf16[128,128]{0,1:T(8,128)(2,1)S(1)}, bf16[128,128]{0,1:T(8,128)(2,1)S(1)}, u32[]{:S(2)}, u32[]{:S(2)}) collective-permute-start(bf16[128,128]{0,1:T(8,128)(2,1)S(1)} %get-tuple-element.20), channel_id=1, source_target_pairs={{0,4},{2,6},{4,0},{6,2},{1,5},{3,7},{5,1},{7,3},{8,12},{10,14},{12... | collective-permute-start | bytes 98312 | tf_op jit(solution)/shard_map/ppermute | solution.py:30
  78.1 3.2 %collective-permute-start.17 = (bf16[128,128]{0,1:T(8,128)(2,1)S(1)}, bf16[128,128]{0,1:T(8,128)(2,1)S(1)}, u32[]{:S(2)}, u32[]{:S(2)}) collective-permute-start(bf16[128,128]{0,1:T(8,128)(2,1)S(1)} %get-tuple-element.21), channel_id=1, source_target_pairs={{0,2},{2,0},{4,6},{6,4},{1,3},{3,1},{5,7},{7,5},{8,10},{10,8},{12,... | collective-permute-start | bytes 98312 | tf_op jit(solution)/shard_map/ppermute | solution.py:30
  83.1 1.7 %copy-start.3 = (bf16[128,3072]{1,0:T(8,128)(2,1)}, bf16[128,3072]{1,0:T(8,128)(2,1)S(1)}, u32[]{:S(2)}) copy-start(bf16[128,3072]{1,0:T(8,128)(2,1)S(1)} %add_convert_fusion) | copy-start | bytes 2359300
  85.4 1.2 copy-start.5
  87.3 5.9 %collective-permute-start.22 = (bf16[128,128]{1,0:T(8,128)(2,1)}, bf16[128,128]{1,0:T(8,128)(2,1)}, u32[]{:S(2)}, u32[]{:S(2)}) collective-permute-start(bf16[128,128]{1,0:T(8,128)(2,1)} %get-tuple-element.15), channel_id=1, source_target_pairs={{0,6},{2,4},{4,2},{6,0},{1,7},{3,5},{5,3},{7,1},{8,14},{10,12},{12... | collective-permute-start | bytes 98312 | tf_op jit(solution)/shard_map/ppermute | solution.py:30
  88.0 5.3 %collective-permute-start.21 = (bf16[128,128]{1,0:T(8,128)(2,1)}, bf16[128,128]{1,0:T(8,128)(2,1)}, u32[]{:S(2)}, u32[]{:S(2)}) collective-permute-start(bf16[128,128]{1,0:T(8,128)(2,1)} %get-tuple-element.16), channel_id=1, source_target_pairs={{0,4},{2,6},{4,0},{6,2},{1,5},{3,7},{5,1},{7,3},{8,12},{10,14},{12... | collective-permute-start | bytes 98312 | tf_op jit(solution)/shard_map/ppermute | solution.py:30
  88.3 4.9 %collective-permute-start.20 = (bf16[128,128]{1,0:T(8,128)(2,1)}, bf16[128,128]{1,0:T(8,128)(2,1)}, u32[]{:S(2)}, u32[]{:S(2)}) collective-permute-start(bf16[128,128]{1,0:T(8,128)(2,1)} %get-tuple-element.17), channel_id=1, source_target_pairs={{0,2},{2,0},{4,6},{6,4},{1,3},{3,1},{5,7},{7,5},{8,10},{10,8},{12,... | collective-permute-start | bytes 98312 | tf_op jit(solution)/shard_map/ppermute | solution.py:30
  93.2 6.4 %copy-start.41 = (bf16[144]{0:T(256)(128)(2,1)}, bf16[144]{0:T(256)(128)(2,1)S(1)}, u32[]{:S(2)}) copy-start(bf16[144]{0:T(256)(128)(2,1)S(1)} %pad.14.clone) | copy-start | bytes 868
  93.2 6.4 %copy-start.42 = (bf16[144]{0:T(256)(128)(2,1)}, bf16[144]{0:T(256)(128)(2,1)S(1)}, u32[]{:S(2)}) copy-start(bf16[144]{0:T(256)(128)(2,1)S(1)} %pad.13.clone) | copy-start | bytes 868
  93.2 1.8 %copy-start.7 = (f32[512,512]{0,1:T(8,128)S(1)}, f32[512,512]{0,1:T(8,128)}, u32[]{:S(2)}) copy-start(f32[512,512]{0,1:T(8,128)} %copy-done.6) | copy-start | bytes 3145732
  93.3 1.8 %copy-start.36 = (f32[512]{0:T(512)S(1)}, f32[512]{0:T(512)}, u32[]{:S(2)}) copy-start(f32[512]{0:T(512)} %copy-done.35) | copy-start | bytes 6148
  95.1 0.9 copy-start.28
  96.0 0.8 copy-start.29
  96.8 1.2 copy-start.10
  96.8 1.4 copy-start.20
  96.8 1.4 copy-start.22
  96.8 1.4 copy-start.24
  98.0 0.8 copy-start.44
  99.0 25.8 %copy-start.4 = (bf16[128,3072]{1,0:T(8,128)(2,1)S(1)}, bf16[128,3072]{1,0:T(8,128)(2,1)}, u32[]{:S(2)}) copy-start(bf16[128,3072]{1,0:T(8,128)(2,1)} %copy-done.3) | copy-start | bytes 2359300
  99.0 25.8 %copy-start.15 = (bf16[1,128,64]{1,2,0:T(8,128)(2,1)S(1)}, bf16[1,128,64]{1,2,0:T(8,128)(2,1)}, u32[]{:S(2)}) copy-start(bf16[1,128,64]{1,2,0:T(8,128)(2,1)} %copy.28) | copy-start | bytes 49156
  100.3 3.8 %collective-permute-start.25 = (bf16[144,64]{0,1:T(8,128)(2,1)}, bf16[144,64]{0,1:T(8,128)(2,1)}, u32[]{:S(2)}, u32[]{:S(2)}) collective-permute-start(bf16[144,64]{0,1:T(8,128)(2,1)} %get-tuple-element.49), channel_id=1, source_target_pairs={{0,6},{2,4},{4,2},{6,0},{1,7},{3,5},{5,3},{7,1},{8,14},{10,12},{12... | collective-permute-start | bytes 55304 | tf_op jit(solution)/shard_map/ppermute | solution.py:30
  101.2 4.2 %collective-permute-start.24 = (bf16[144,64]{0,1:T(8,128)(2,1)}, bf16[144,64]{0,1:T(8,128)(2,1)}, u32[]{:S(2)}, u32[]{:S(2)}) collective-permute-start(bf16[144,64]{0,1:T(8,128)(2,1)} %get-tuple-element.48), channel_id=1, source_target_pairs={{0,4},{2,6},{4,0},{6,2},{1,5},{3,7},{5,1},{7,3},{8,12},{10,14},{12... | collective-permute-start | bytes 55304 | tf_op jit(solution)/shard_map/ppermute | solution.py:30
  101.9 3.6 %collective-permute-start.23 = (bf16[144,64]{0,1:T(8,128)(2,1)}, bf16[144,64]{0,1:T(8,128)(2,1)}, u32[]{:S(2)}, u32[]{:S(2)}) collective-permute-start(bf16[144,64]{0,1:T(8,128)(2,1)} %get-tuple-element.47), channel_id=1, source_target_pairs={{0,2},{2,0},{4,6},{6,4},{1,3},{3,1},{5,7},{7,5},{8,10},{10,8},{12,... | collective-permute-start | bytes 55304 | tf_op jit(solution)/shard_map/ppermute | solution.py:30
  113.1 5.3 %collective-permute-start.26 = (bf16[144,64]{0,1:T(8,128)(2,1)S(1)}, bf16[144,64]{0,1:T(8,128)(2,1)S(1)}, u32[]{:S(2)}, u32[]{:S(2)}) collective-permute-start(bf16[144,64]{0,1:T(8,128)(2,1)S(1)} %maximum_maximum_fusion.3), channel_id=1, source_target_pairs={{0,24},{8,0},{16,8},{24,16},{1,25},{9,1},{17,9},{25,17},{2,26},{10... | collective-permute-start | bytes 55304 | tf_op jit(solution)/shard_map/ppermute | solution.py:280
  116.0 4.8 %collective-permute-start.27 = (bf16[144,64]{0,1:T(8,128)(2,1)S(1)}, bf16[144,64]{0,1:T(8,128)(2,1)S(1)}, u32[]{:S(2)}, u32[]{:S(2)}) collective-permute-start(bf16[144,64]{0,1:T(8,128)(2,1)S(1)} %maximum_maximum_fusion.3), channel_id=1, source_target_pairs={{0,16},{8,24},{16,0},{24,8},{1,17},{9,25},{17,1},{25,9},{2,18},{10... | collective-permute-start | bytes 55304 | tf_op jit(solution)/shard_map/ppermute | solution.py:280
  116.4 5.7 %collective-permute-start.28 = (bf16[144,64]{0,1:T(8,128)(2,1)S(1)}, bf16[144,64]{0,1:T(8,128)(2,1)S(1)}, u32[]{:S(2)}, u32[]{:S(2)}) collective-permute-start(bf16[144,64]{0,1:T(8,128)(2,1)S(1)} %maximum_maximum_fusion.3), channel_id=1, source_target_pairs={{0,8},{8,16},{16,24},{24,0},{1,9},{9,17},{17,25},{25,1},{2,10},{10... | collective-permute-start | bytes 55304 | tf_op jit(solution)/shard_map/ppermute | solution.py:280
  124.8 1.2 copy-start.17
  (10 other events, 6.4 us)

commit v2 on v1

v2 whole, which is shorter than its diff:
```python
import functools
import math

import jax
import jax.numpy as jnp
from jax import lax
from jax.experimental import pallas as pl
from jax.experimental.pallas import tpu as pltpu
from jax.sharding import PartitionSpec as P

SHIFT = 7.0
EPS = 1e-06
ADV_WEIGHT = 3.0
TILE = 512
STREAMS = 6
VMEM = pl.BlockSpec(memory_space=pltpu.VMEM)
SMEM = pl.BlockSpec(memory_space=pltpu.SMEM)
ANY = pl.BlockSpec(memory_space=pl.ANY)


def halves(values):
    top = values.astype(jnp.bfloat16)
    return (top, (values - top.astype(jnp.float32)).astype(jnp.bfloat16))


def split_halves(values):
    top = lax.reduce_precision(values, 8, 7)
    return (top.astype(jnp.bfloat16), (values - top).astype(jnp.bfloat16))


def swaps(count, offset):
    return [(place, place ^ offset) for place in range(count)]


def gather_near(value, axis, count):
    return [value] + [
        lax.ppermute(value, axis, swaps(count, offset)) for offset in range(1, count)
    ]


def scatter_near(blocks, axis, count):
    return [blocks[0]] + [
        lax.ppermute(blocks[offset], axis, swaps(count, offset)) for offset in range(1, count)
    ]


def gather_doubling(value, axis, count):
    held = {0: value}
    bit = count // 2
    while bit:
        offsets = sorted(held)
        joined = jnp.concatenate([held[offset] for offset in offsets], axis=0)
        moved = lax.ppermute(joined, axis, swaps(count, bit))
        rows = value.shape[0]
        for place, offset in enumerate(offsets):
            held[offset | bit] = moved[place * rows : (place + 1) * rows]
        bit //= 2
    return [held[offset] for offset in range(count)]


def in_order(pieces, own_place):
    ordered = list(pieces)
    bit = 1
    while bit < len(ordered):
        flipped = (own_place & bit) != 0
        ordered = [
            jnp.where(flipped, ordered[place ^ bit], ordered[place])
            for place in range(len(ordered))
        ]
        bit *= 2
    return ordered


def dot32(left, right):
    return jnp.dot(left, right, preferred_element_type=jnp.float32)


def dot32_t(left, right):
    return lax.dot_general(
        left, right, (((1,), (1,)), ((), ())), preferred_element_type=jnp.float32
    )


def dot32_first(left, right):
    return lax.dot_general(
        left, right, (((0,), (0,)), ((), ())), preferred_element_type=jnp.float32
    )


def steps_of(times_ref):
    place = lax.axis_index("dp")
    return (times_ref[place, 0], times_ref[place, 1])


def noise_level(step):
    fraction = jnp.full((1, 1), step, jnp.int32).astype(jnp.float32) / 1000.0
    return SHIFT * fraction / (1.0 + (SHIFT - 1.0) * fraction)


def slot_of(mod_ref, slot, width, first, size):
    return mod_ref[:, slot * width + first : slot * width + first + size]


def lane_sum(values):
    total = values[:, :128]
    for first in range(128, values.shape[1], 128):
        total = total + values[:, first : first + 128]
    return total


def run(kernel, outputs, operands, specs, flops, scratch=(), **params):
    in_bytes = sum(operand.size * operand.dtype.itemsize for operand in operands)
    out_bytes = sum(output.size * output.dtype.itemsize for output in outputs)
    return pl.pallas_call(
        kernel,
        out_shape=outputs,
        in_specs=specs,
        out_specs=[VMEM] * len(outputs),
        scratch_shapes=list(scratch),
        compiler_params=pltpu.CompilerParams(**params),
        cost_estimate=pl.CostEstimate(
            flops=flops, bytes_accessed=in_bytes + out_bytes, transcendentals=0
        ),
    )(*operands)


def array(shape, dtype):
    return jax.ShapeDtypeStruct(shape, dtype)


def condition_kernel(times, text, time_w, mod_w, mod_out, held, arrivals):
    model_width = mod_w.shape[1]
    rows = model_width // STREAMS
    copies = [
        pltpu.make_async_copy(
            mod_w.at[0, pl.ds(part * rows, rows)], held.at[pl.ds(part * rows, rows)], arrivals.at[part]
        )
        for part in range(STREAMS)
    ]
    for copy in copies:
        copy.start()
    student_step, critic_step = steps_of(times)
    step = jnp.where(lax.axis_index("segment") == 0, student_step, critic_step)
    half = text.shape[1] // 2
    places = lax.broadcasted_iota(jnp.int32, (1, half), 1).astype(jnp.float32)
    frequency = jnp.exp(-math.log(10000.0) * places / half)
    angles = jnp.full((1, half), step, jnp.int32).astype(jnp.float32) * frequency
    features = jnp.concatenate([jnp.cos(angles), jnp.sin(angles)], axis=1) + text[...]
    features = jnp.broadcast_to(features, (8, 2 * half)).astype(jnp.bfloat16)
    hidden = dot32(features, time_w[0])
    hidden = (hidden / (1.0 + jnp.exp(-hidden))).astype(jnp.bfloat16)
    total = None
    for part in range(STREAMS):
        copies[part].wait()
        piece = dot32(
            hidden[:, part * rows : (part + 1) * rows], held[part * rows : (part + 1) * rows]
        )
        total = piece if total is None else total + piece
    mod_out[...] = total[:1]


def rms_scale(values, gain_vec):
    inverse = lax.rsqrt(jnp.mean(values * values, axis=-1, keepdims=True) + EPS)
    unit_vec = values * inverse
    return (unit_vec * gain_vec, unit_vec, inverse)


def rms_back(gradient, unit_vec, inverse, gain_vec):
    scaled = gradient * gain_vec
    return inverse * (scaled - unit_vec * jnp.mean(scaled * unit_vec, axis=-1, keepdims=True))


def centred(embed_ref):
    values = embed_ref[0].astype(jnp.float32)
    return values - jnp.mean(values, axis=1, keepdims=True)


def front(rows, central, short, gains, head_outs, proj_ref, inverse_ref, key_ref, value_ref):
    latent_width = central.shape[0]
    model_width = central.shape[1]
    count = len(rows)
    head_width = gains.shape[2]
    short_top, short_low = halves(short[:latent_width])
    short_shift = short[latent_width : latent_width + 1]
    scale = 1.0 / math.sqrt(head_width)
    size = rows[0].shape[0]
    for place in range(count):
        block = rows[place][...]
        squares = None
        for first in range(0, model_width, TILE):
            piece = dot32(block, central[:, first : first + TILE])
            piece = lane_sum(piece * piece)
            squares = piece if squares is None else squares + piece
        inverse = lax.rsqrt(jnp.sum(squares, axis=1, keepdims=True) / model_width + EPS)
        projected = inverse * (dot32(block, short_top) + dot32(block, short_low)) + short_shift
        low = place * size
        proj_ref[low : low + size] = projected
        inverse_ref[low : low + size] = jnp.broadcast_to(inverse, (size, 128))
        keys, _, _ = rms_scale(projected[:, head_width : 2 * head_width], gains[0, 1:2])
        key_ref[low : low + size] = keys.astype(jnp.bfloat16)
        value_ref[low : low + size] = projected[:, 2 * head_width :].astype(jnp.bfloat16)
    for place in range(count):
        low = place * size
        queries, _, _ = rms_scale(proj_ref[low : low + size, :head_width], gains[0, :1])
        scores = dot32_t(queries.astype(jnp.bfloat16), key_ref[...]) * scale
        weights = jnp.exp(scores)
        soft_max = weights * (1.0 / jnp.sum(weights, axis=-1, keepdims=True))
        head_outs[place][...] = dot32(soft_max.astype(jnp.bfloat16), value_ref[...]).astype(
            jnp.bfloat16
        )


def student_front_kernel(count, mod, embed_w, head_w, gains, *refs):
    rows = refs[:count]
    head_outs = refs[count : 2 * count]
    short_ref, proj_ref, inverse_ref, key_ref, value_ref = refs[2 * count :]
    model_width = embed_w.shape[2]
    central = centred(embed_w)
    scale_in = slot_of(mod, 1, model_width, 0, model_width)
    shift_in = slot_of(mod, 0, model_width, 0, model_width)
    in_rows = jnp.concatenate(
        [central * (1.0 + scale_in), jnp.broadcast_to(shift_in, (16, model_width))], axis=0
    )
    in_top, in_low = halves(in_rows)
    both = dot32(jnp.concatenate([in_top, in_low], axis=0), head_w[...])
    short = both[: in_rows.shape[0]] + both[in_rows.shape[0] :]
    short_ref[...] = short

    @pl.when(lax.axis_index("segment") == 0)
    def _():
        front(
            rows,
            central.astype(jnp.bfloat16),
            short,
            gains,
            head_outs,
            proj_ref,
            inverse_ref,
            key_ref,
            value_ref,
        )


def critic_front_kernel(count, short_in, embed_w, gains, *refs):
    rows = refs[:count]
    head_outs = refs[count : 2 * count]
    proj_ref, inverse_ref, key_ref, value_ref = refs[2 * count :]

    @pl.when(lax.axis_index("segment") != 0)
    def _():
        front(
            rows,
            centred(embed_w).astype(jnp.bfloat16),
            short_in[...],
            gains,
            head_outs,
            proj_ref,
            inverse_ref,
            key_ref,
            value_ref,
        )


def tail(mod, latent, embed_w, final_w, mixed, heads_w, final_in_ref, work):
    model_width = embed_w.shape[2]
    block = latent[...]
    sums = None
    for first in range(0, model_width, TILE):
        span = slice(first, first + TILE)
        attended = None
        for piece, rows_w in zip(mixed, heads_w):
            product = dot32(piece[...], rows_w[:, span])
            attended = product if attended is None else attended + product
        residual = (
            dot32(block, embed_w[0, :, span]) + slot_of(mod, 2, model_width, first, TILE) * attended
        )
        work[:, span] = residual
        part = lane_sum(residual)
        sums = part if sums is None else sums + part
    row_mean = jnp.sum(sums, axis=1, keepdims=True) / model_width
    sums = None
    for first in range(0, model_width, TILE):
        span = slice(first, first + TILE)
        middle = work[:, span] - row_mean
        work[:, span] = middle
        part = lane_sum(middle * middle)
        sums = part if sums is None else sums + part
    inverse = lax.rsqrt(jnp.sum(sums, axis=1, keepdims=True) / model_width + EPS)
    result = None
    for first in range(0, model_width, TILE):
        span = slice(first, first + TILE)
        normed = work[:, span] * inverse
        work[:, span] = normed
        final_in = (
            normed * (1.0 + slot_of(mod, 4, model_width, first, TILE))
            + slot_of(mod, 3, model_width, first, TILE)
        ).astype(jnp.bfloat16)
        final_in_ref[:, span] = final_in
        product = dot32(final_in, final_w[0, span])
        result = product if result is None else result + product
    return (result, inverse)


def student_tail_kernel(count, times, mod, latent, noise, embed_w, final_w, *refs):
    mixed = refs[:count]
    heads_w = refs[count : 2 * count]
    pair_ref, final_in_ref, work = refs[2 * count :]
    latent_width = latent.shape[1]

    @pl.when(lax.axis_index("segment") == 0)
    def _():
        student_step, critic_step = steps_of(times)
        sigma_student, sigma_critic = noise_level(student_step), noise_level(critic_step)
        velocity, _ = tail(mod, latent, embed_w, final_w, mixed, heads_w, final_in_ref, work)
        sample = latent[...].astype(jnp.float32) - sigma_student * velocity
        second = noise[0, :, latent_width:].astype(jnp.float32)
        critic = (1.0 - sigma_critic) * sample + sigma_critic * second
        pair_ref[...] = jnp.concatenate([critic, sample], axis=1).astype(jnp.bfloat16)


def critic_tail_kernel(count, times, mod, pair, noise, embed_w, final_w, *refs):
    mixed = refs[:count]
    heads_w = refs[count : 2 * count]
    grads = refs[2 * count : 3 * count]
    final_in_ref, term_ref, target_ref, error_ref, direct_ref, latent, work, other = refs[
        3 * count :
    ]
    model_width = embed_w.shape[2]
    latent_width = latent.shape[1]
    section = lax.axis_index("segment")

    @pl.when(section != 0)
    def _():
        _, critic_step = steps_of(times)
        sigma_critic = noise_level(critic_step)
        both = pair[...].astype(jnp.float32)
        sample = both[:, latent_width:]
        latent[...] = pair[:, :latent_width]
        result, inverse = tail(mod, latent, embed_w, final_w, mixed, heads_w, final_in_ref, work)
        scaled = sigma_critic * result
        term_ref[...] = scaled
        second = noise[0, :, latent_width:].astype(jnp.float32)
        target_ref[...] = jnp.where(
            section == 2,
            2.0 * (result - (second - sample)),
            jnp.where(section == 3, 1.0 / (1.0 + jnp.exp(-result)), 0.0),
        )
        gaps = jnp.abs(sample - both[:, :latent_width] + scaled)
        error = jnp.sum(jnp.sum(gaps, axis=1, keepdims=True), axis=0, keepdims=True)
        error = error / (gaps.shape[0] * latent_width)
        error_top, error_low = halves(jnp.broadcast_to(error, (16, latent_width)))
        error_ref[:16] = error_top
        error_ref[16:] = error_low

        @pl.when(section == 3)
        def _():
            grad_logit = (-1.0 / (1.0 + jnp.exp(result))).astype(jnp.bfloat16)
            plain, along = None, None
            for first in range(0, model_width, TILE):
                span = slice(first, first + TILE)
                gradient = dot32_t(grad_logit, final_w[0, span]) * (
                    1.0 + slot_of(mod, 4, model_width, first, TILE)
                )
                other[:, span] = gradient
                part = lane_sum(gradient)
                plain = part if plain is None else plain + part
                part = lane_sum(gradient * work[:, span])
                along = part if along is None else along + part
            plain = jnp.sum(plain, axis=1, keepdims=True) / model_width
            along = jnp.sum(along, axis=1, keepdims=True) / model_width
            direct = None
            totals = [None] * count
            for first in range(0, model_width, TILE):
                span = slice(first, first + TILE)
                grad_residual = inverse * (other[:, span] - plain - work[:, span] * along)
                top, low = halves(grad_residual)
                product = dot32_t(top, embed_w[0, :, span]) + dot32_t(low, embed_w[0, :, span])
                direct = product if direct is None else direct + product
                grad_attended = (slot_of(mod, 2, model_width, first, TILE) * grad_residual).astype(
                    jnp.bfloat16
                )
                for place in range(count):
                    product = dot32_t(grad_attended, heads_w[place][:, span])
                    held = totals[place]
                    totals[place] = product if held is None else held + product
            direct_ref[...] = direct
            for place in range(count):
                grads[place][...] = totals[place].astype(jnp.bfloat16)


def judge_back_kernel(count, short_in, embed_w, gains, proj_ref, inverse_ref, key_ref, value_ref, error, *refs):
    rows = refs[:count]
    grads = refs[count : 2 * count]
    outs = refs[2 * count : 3 * count]
    grad_key_ref, grad_value_ref, grad_query_ref = refs[3 * count :]
    section = lax.axis_index("segment")
    latent_width = rows[0].shape[1]
    model_width = embed_w.shape[2]
    head_width = gains.shape[2]
    scale = 1.0 / math.sqrt(head_width)
    size = rows[0].shape[0]
    for place in range(count):
        outs[place][size:] = error[...]

    @pl.when(section == 3)
    def _():
        for place in range(count):
            low = place * size
            span = slice(low, low + size)
            queries, _, _ = rms_scale(proj_ref[span, :head_width], gains[0, :1])
            query_b = queries.astype(jnp.bfloat16)
            weights = jnp.exp(dot32_t(query_b, key_ref[...]) * scale)
            soft_max = weights * (1.0 / jnp.sum(weights, axis=-1, keepdims=True))
            grad_out = grads[place][...]
            grad_soft = dot32_t(grad_out, value_ref[...])
            grad_value = dot32_first(soft_max.astype(jnp.bfloat16), grad_out)
            grad_scores = soft_max * (
                grad_soft - jnp.sum(soft_max * grad_soft, axis=-1, keepdims=True)
            )
            grad_scores_b = (grad_scores * scale).astype(jnp.bfloat16)
            grad_query_ref[span] = dot32(grad_scores_b, key_ref[...])
            grad_key = dot32_first(grad_scores_b, query_b)
            if place == 0:
                grad_value_ref[...] = grad_value
                grad_key_ref[...] = grad_key
            else:
                grad_value_ref[...] += grad_value
                grad_key_ref[...] += grad_key
        central = centred(embed_w)
        central_top, central_low = halves(central)
        gram = (
            dot32_t(central_top, central_top)
            + dot32_t(central_top, central_low)
            + dot32_t(central_low, central_top)
        )
        gram_top, gram_low = halves(gram)
        short_top, short_low = halves(short_in[:latent_width])
        for place in range(count):
            low = place * size
            span = slice(low, low + size)
            projected = proj_ref[span]
            _, q_unit, q_inverse = rms_scale(projected[:, :head_width], gains[0, :1])
            _, k_unit, k_inverse = rms_scale(
                projected[:, head_width : 2 * head_width], gains[0, 1:2]
            )
            grad_q = rms_back(grad_query_ref[span], q_unit, q_inverse, gains[0, :1])
            grad_k = rms_back(grad_key_ref[span], k_unit, k_inverse, gains[0, 1:2])
            grad_proj = jnp.concatenate([grad_q, grad_k, grad_value_ref[span]], axis=1).astype(
                jnp.bfloat16
            )
            through = dot32_t(grad_proj, short_top) + dot32_t(grad_proj, short_low)
            block = rows[place][...]
            along = jnp.sum(through * block.astype(jnp.float32), axis=1, keepdims=True) / model_width
            spanned = dot32(block, gram_top) + dot32(block, gram_low)
            inverse = inverse_ref[span, :1]
            outs[place][:size] = (
                inverse * (through - spanned * (inverse * inverse * along))
            ).astype(jnp.bfloat16)


def merge_kernel(count, times, direct, term, *refs):
    parts = refs[:count]
    payload_ref = refs[count]
    section = lax.axis_index("segment")
    rows = direct.shape[0]
    total = parts[0][...].astype(jnp.float32)
    for part in parts[1:]:
        total = total + part[...].astype(jnp.float32)
    _, critic_step = steps_of(times)
    sigma_critic = noise_level(critic_step)
    adverse = (1.0 - sigma_critic) * (total[:rows] + direct[...])
    spread = (total[rows : rows + 16] + total[rows + 16 :]) / count + EPS
    spread_top, spread_low = halves(spread)
    payload_ref[:rows] = jnp.where(section == 3, adverse, term[...]).astype(jnp.bfloat16)
    payload_ref[rows : rows + 16] = spread_top
    payload_ref[rows + 16 :] = spread_low


def finish_kernel(sections, times, target_in, student_in, critic_in, *refs):
    received = refs[:sections]
    grad_ref, term_ref = refs[sections:]
    section = lax.axis_index("segment")
    rows = target_in.shape[0]

    def payload_of(source):
        chosen = received[0][...].astype(jnp.float32)
        for offset in range(1, sections):
            chosen = jnp.where(
                lax.rem(section - offset + sections, sections) == source,
                received[offset][...].astype(jnp.float32),
                chosen,
            )
        return chosen

    real, fake, adverse = [payload_of(source) for source in (1, 2, 3)]
    spread = (real[rows : rows + 16] + real[rows + 16 :])[:1, :1]
    sample_grad = (real[:rows] - fake[:rows]) / spread + ADV_WEIGHT * adverse[:rows]
    grad_ref[0] = sample_grad

    @pl.when(section == 0)
    def _():
        student_step, _ = steps_of(times)
        target = (-noise_level(student_step) * sample_grad).astype(jnp.bfloat16)
        term_ref[...] = dot32_first(student_in[...], target).astype(jnp.bfloat16)

    @pl.when(section == 1)
    def _():
        term_ref[...] = jnp.zeros_like(term_ref)

    @pl.when(section >= 2)
    def _():
        term_ref[...] = dot32_first(critic_in[...], target_in[...].astype(jnp.bfloat16)).astype(
            jnp.bfloat16
        )


def reduce_everywhere(term, seq_devices, seq_place):
    rows = term.shape[0]
    held = term
    trail = []
    bit = 1
    while bit < seq_devices:
        half = held.shape[0] // 2
        upper = (seq_place & bit) != 0
        away = jnp.where(upper, held[:half], held[half:])
        kept = jnp.where(upper, held[half:], held[:half])
        moved = lax.ppermute(away, "seq", swaps(seq_devices, bit))
        held = (kept.astype(jnp.float32) + moved.astype(jnp.float32)).astype(jnp.bfloat16)
        trail.append((bit, upper))
        bit *= 2
    batch_devices = lax.axis_size("dp")
    bit = 1
    while bit < batch_devices:
        moved = lax.ppermute(held, "dp", swaps(batch_devices, bit))
        held = (held.astype(jnp.float32) + moved.astype(jnp.float32)).astype(jnp.bfloat16)
        bit *= 2
    for bit, upper in reversed(trail):
        moved = lax.ppermute(held, "seq", swaps(seq_devices, bit))
        held = jnp.concatenate(
            [jnp.where(upper, moved, held), jnp.where(upper, held, moved)], axis=0
        )
    return held


def shards(
    clean, noise, timesteps, text_vec, w_embed, w_time, w_mod, w_qkv, w_out, qk_gain, w_final
):
    section = lax.axis_index("segment")
    sections = lax.axis_size("segment")
    batch_idx = lax.axis_index("dp")
    seq_place = lax.axis_index("seq")
    tok_rows = clean.shape[1]
    latent_width = clean.shape[2]
    model_width = w_embed.shape[2]
    mod_width = w_mod.shape[2]
    count = lax.axis_size("seq")
    full_rows = tok_rows * count
    head_width = w_qkv.shape[4]
    flat_head_w = w_qkv[0, :, 0].reshape(model_width, 3 * head_width)
    step_pair = lax.dynamic_index_in_dim(timesteps, batch_idx, 0, keepdims=False)
    fraction = step_pair[0].astype(jnp.float32) / 1000.0
    sigma_student = SHIFT * fraction / (1.0 + (SHIFT - 1.0) * fraction)
    noisy_student = (
        (1.0 - sigma_student) * clean[0].astype(jnp.float32)
        + sigma_student * noise[0, :, :latent_width].astype(jnp.float32)
    ).astype(jnp.bfloat16)
    with jax.named_scope("heads"):
        heads_w = gather_doubling(w_out[0, 0], "seq", count)
    with jax.named_scope("student_rows"):
        student_rows = gather_near(noisy_student, "seq", count)
    bf16, f32 = jnp.bfloat16, jnp.float32

    (mod_piece,) = run(
        condition_kernel,
        [array((1, mod_width), f32)],
        (timesteps, text_vec, w_time, w_mod),
        [SMEM, VMEM, VMEM, ANY],
        2 * model_width * mod_width,
        scratch=(
            pltpu.VMEM((model_width, mod_width), bf16),
            pltpu.SemaphoreType.DMA((STREAMS,)),
        ),
    )
    with jax.named_scope("modulation"):
        mod_parts = gather_near(mod_piece, "seq", count)
    mod = jnp.concatenate(in_order(mod_parts, seq_place), axis=1)

    head_blocks = [array((tok_rows, head_width), bf16)] * count
    stored = [
        array((full_rows, 3 * head_width), f32),
        array((full_rows, 128), f32),
        array((full_rows, head_width), bf16),
        array((full_rows, head_width), bf16),
    ]
    *head_outs, short, _, _, _, _ = run(
        functools.partial(student_front_kernel, count),
        head_blocks + [array((latent_width + 16, 3 * head_width), f32)] + stored,
        (mod, w_embed, flat_head_w, qk_gain, *student_rows),
        [VMEM] * (4 + count),
        4 * latent_width * model_width * 3 * head_width,
    )
    mixed = scatter_near(head_outs, "seq", count)
    work = pltpu.VMEM((tok_rows, model_width), f32)
    pair, student_in = run(
        functools.partial(student_tail_kernel, count),
        [array((tok_rows, 2 * latent_width), bf16), array((tok_rows, model_width), bf16)],
        (timesteps, mod, noisy_student, noise, w_embed, w_final, *mixed, *heads_w),
        [SMEM] + [VMEM] * (5 + 2 * count),
        2 * tok_rows * model_width * head_width * count,
        scratch=(work,),
    )
    arrived = [
        lax.ppermute(pair, "segment", [(0, place)]) for place in range(sections - 1, 0, -1)
    ]
    pair = jnp.where(section == 0, pair, sum(arrived[1:], arrived[0]))
    critic_rows = gather_near(pair[:, :latent_width], "seq", count)
    *head_outs, proj, inverse, keys, values = run(
        functools.partial(critic_front_kernel, count),
        head_blocks + stored,
        (short, w_embed, qk_gain, *critic_rows),
        [VMEM] * (3 + count),
        4 * latent_width * model_width * full_rows,
    )
    mixed = scatter_near(head_outs, "seq", count)
    small = array((tok_rows, latent_width), f32)
    *grad_heads, critic_in, term_rows, target, error, direct = run(
        functools.partial(critic_tail_kernel, count),
        head_blocks
        + [array((tok_rows, model_width), bf16), small, small, array((32, latent_width), bf16), small],
        (timesteps, mod, pair, noise, w_embed, w_final, *mixed, *heads_w),
        [SMEM] + [VMEM] * (5 + 2 * count),
        4 * tok_rows * model_width * head_width * count,
        scratch=(pltpu.VMEM((tok_rows, latent_width), bf16), work, work),
    )
    grad_blocks = scatter_near(grad_heads, "seq", count)
    parts = run(
        functools.partial(judge_back_kernel, count),
        [array((tok_rows + 32, latent_width), bf16)] * count,
        (short, w_embed, qk_gain, proj, inverse, keys, values, error, *critic_rows, *grad_blocks),
        [VMEM] * (8 + 2 * count),
        10 * full_rows * full_rows * head_width,
        scratch=(pltpu.VMEM((full_rows, head_width), f32),) * 3,
    )
    parts = scatter_near(parts, "seq", count)
    (payload,) = run(
        functools.partial(merge_kernel, count),
        [array((tok_rows + 32, latent_width), bf16)],
        (timesteps, direct, term_rows, *parts),
        [SMEM] + [VMEM] * (2 + count),
        1000,
    )
    received = [payload] + [
        lax.ppermute(
            payload, "segment", [(place, (place + offset) % sections) for place in range(sections)]
        )
        for offset in range(1, sections)
    ]
    sample_grad, term = run(
        functools.partial(finish_kernel, sections),
        [array((1, tok_rows, latent_width), f32), array((model_width, latent_width), bf16)],
        (timesteps, target, student_in, critic_in, *received),
        [SMEM] + [VMEM] * (3 + sections),
        2 * tok_rows * model_width * latent_width,
    )
    total = reduce_everywhere(term, count, seq_place)
    final_grads = total.astype(f32) / full_rows
    return (sample_grad, final_grads[None])


def solution(mesh):
    placed = (
        P("dp", "seq", None),
        P("dp", "seq", None),
        P(),
        P("dp", None),
        P("segment", None, None),
        P("segment", None, None),
        P("segment", None, "seq"),
        P("segment", None, "seq", None, None),
        P("segment", "seq", None, None),
        P("segment", None, None),
        P("segment", None, None),
    )
    return jax.shard_map(
        shards,
        mesh=mesh,
        in_specs=placed,
        out_specs=(P("dp", "seq", None), P("segment", None, None)),
        check_vma=False,
    )
```

time: 150 us -> 147 us (0.980)
  matrix products: 36.4 us -> 0 us
  Pallas kernels: 0 us -> 34.2 us
  waiting for transfers between devices: 26.3 us -> 56 us
  blocking collectives: 21 us -> 0 us
  between operations: 11.1 us -> 1.04 us
  starting transfers between devices: 29.8 us -> 35.1 us
  other arithmetic: 7.27 us -> 4.98 us
  local copies, waits for them, and re-layouts: 16.7 us -> 15 us
    dot_general x32 -> x0, matrix products: 36.4 us -> none  [the longest x19 15.2 us: dot32(): return jnp.dot(left, right, preferred_element_type=jnp.float32)]
    pallas_call x0 -> x8, Pallas kernels: none -> 34.2 us  [run(): pl.pallas_call(kernel, out_shape=outputs, in_specs=specs, out_specs=[VMEM...]
    all_to_all x2 -> x0, blocking collectives: 21 us -> none  [the longest x1 10.7 us: shards(): lax.all_to_all(term.reshape(share_count, share, latent_width), ('seq', 'd...]
    ppermute x0 -> x5, waiting for transfers between devices: none -> 18 us  [the longest x2 7.69 us: reduce_everywhere(): moved = lax.ppermute(away, 'seq', swaps(seq_devices, bit))]
    ppermute x2, waiting for transfers between devices: 10.1 us -> 18.2 us  [gather_doubling(): moved = lax.ppermute(joined, axis, swaps(count, bit))]
    ppermute x3, starting transfers between devices: 5.29 us -> 11.2 us  [shards(): lax.ppermute(payload, 'segment', [(place, (place + offset) % sections) fo...]
    slice x10 -> x0, local copies, waits for them, and re-layouts: 3.8 us -> none  [the longest x1 0.7 us: shards(): second_noise = noise[0, :, latent_width:].astype(jnp.float32)]
    ppermute x3, starting transfers between devices: 7.64 us -> 3.86 us  [shards(): lax.ppermute(pair, 'segment', [(0, place)])]
  transfers between devices with their start and end apart: 29 -> 34, of which waited for: 13 -> 21; matrix products, arithmetic and copies ran while one was open for 14% -> 7% of each run, Pallas kernels for 0% -> 4%
where the time goes in v2:
time: 147 us; the launch traced here: 146 us
  waiting for transfers between devices  56 us (38%)
  starting transfers between devices  35.1 us (24%)
  Pallas kernels  34.2 us (23%)
  local copies, waits for them, and re-layouts  15 us (10%)
  other arithmetic  4.98 us (3%)
    pallas_call x8, Pallas kernels, run(): pl.pallas_call(kernel, out_shape=outputs, in_specs=specs, out_specs=[VMEM...  34.2 us
    ppermute x2, waiting for transfers between devices, gather_doubling(): moved = lax.ppermute(joined, axis, swaps(count, bit))  18.2 us
    unnamed x63, local copies, waits for them, and re-layouts  11.2 us
    ppermute x3, starting transfers between devices, shards(): lax.ppermute(payload, 'segment', [(place, (place + offset) % sections) fo...  11.2 us
    ppermute x12, waiting for transfers between devices, scatter_near(): lax.ppermute(blocks[offset], axis, swaps(count, offset))  11 us
    ppermute x2, waiting for transfers between devices, reduce_everywhere(): moved = lax.ppermute(away, 'seq', swaps(seq_devices, bit))  7.69 us
    ppermute x12, starting transfers between devices, scatter_near(): lax.ppermute(blocks[offset], axis, swaps(count, offset))  7.6 us
    ppermute x9, starting transfers between devices, gather_near(): lax.ppermute(value, axis, swaps(count, offset))  6.96 us
  transfers between devices with their start and end apart: 34, of which 21 were waited for; matrix products, arithmetic and copies ran while one was open for 7% of the time, Pallas kernels for 4%

profile of v2, /device:TPU:0, one launch (start us, length us, event | category | flops | bytes accessed | tf_op | source)
XLA Modules:
  0.0 146.2 jit_solution(12857054536009722155)
XLA Ops:
  0.7 10.5 %shard_map.122 = f32[1,3840]{1,0:T(1,128)} custom-call(s32[2,2]{1,0:T(2,128)} %times.9, f32[1,256]{1,0:T(1,128)} %text.1, bf16[1,256,3072]{2,1,0:T(8,128)(2,1)} %time_w.1, bf16[1,3072,3840]{2,1,0:T(8,128)(2,1)} %mod_w.1), custom_call_target="tpu_custom_call" | custom-call | flops 23592960 | bytes 25182224 | tf_op jit(solution)/shard_map/pallas_call | solution.py:114
  11.2 2.5 %collective-permute-start = (f32[1,3840]{1,0:T(1,128)}, f32[1,3840]{1,0:T(1,128)}, u32[]{:S(2)}, u32[]{:S(2)}) collective-permute-start(f32[1,3840]{1,0:T(1,128)} %shard_map.122), channel_id=1, source_target_pairs={{0,6},{2,4},{4,2},{6,0},{1,7},{3,5},{5,3},{7,1},{8,14},{10,12},{12... | collective-permute-start | bytes 46088 | tf_op jit(solution)/shard_map/modulation/ppermute | solution.py:37
  13.7 0.6 collective-permute-start.1
  14.7 0.6 fusion.refs_0_.latent
  15.8 1.4 collective-permute-start.4
  17.1 2.8 %copy.20 = bf16[1,3072,1,3,128]{1,4,3,2,0:T(8,128)(2,1)S(1)} copy(bf16[1,3072,1,3,128]{4,1,3,2,0:T(8,128)(2,1)} %param.18) | data formatting | bytes 4718592 | tf_op args[7]
  20.0 2.5 %copy.21.head_w = bf16[3072,384]{1,0:T(8,128)(2,1)} copy(bf16[3072,384]{0,1:T(8,128)(2,1)S(1)} %bitcast.11) | data formatting | bytes 4718592 | tf_op jit(solution)/shard_map/reshape;squeeze | solution.py:559
  22.5 1.2 copy.22.final_w
  23.7 1.7 %collective-permute-start.9 = (bf16[128,3072]{1,0:T(8,128)(2,1)S(1)}, bf16[128,3072]{1,0:T(8,128)(2,1)S(1)}, u32[]{:S(2)}, u32[]{:S(2)}) collective-permute-start(bf16[128,3072]{1,0:T(8,128)(2,1)S(1)} %bitcast.14), channel_id=1, source_target_pairs={{0,4},{2,6},{4,0},{6,2},{1,5},{3,7},{5,1},{7,3},{8,12},{10,14},{12... | collective-permute-start | bytes 2359304 | tf_op jit(solution)/shard_map/heads/ppermute | solution.py:53
  25.4 0.8 broadcast_select_fusion.11
  26.2 18.2 %collective-permute-done.9.refs_6_ = bf16[128,3072]{1,0:T(8,128)(2,1)S(1)} collective-permute-done((bf16[128,3072]{1,0:T(8,128)(2,1)S(1)}, bf16[128,3072]{1,0:T(8,128)(2,1)S(1)}, u32[]{:S(2)}, u32[]{:S(2)}) %collective-permute-start.9) | collective-permute-done | bytes 786464 | tf_op jit(solution)/shard_map/heads/ppermute | solution.py:53
  44.5 0.8 copy-done.1
  45.3 0.7 pad_maximum_fusion.2.mod
  46.0 0.6 copy-done.14
  46.6 6.3 %shard_map.123 = (bf16[128,128]{1,0:T(8,128)(2,1)}, bf16[128,128]{1,0:T(8,128)(2,1)}, bf16[128,128]{1,0:T(8,128)(2,1)}, bf16[128,128]{1,0:T(8,128)(2,1)}, f32[80...) custom-call(f32[1,15360]{1,0:T(1,128)} %pad_maximum_fusion.2.mod, ...), custom_call_target="tpu_custom_call" | custom-call | flops 301989888 | bytes 4445184 | tf_op jit(solution)/shard_map/pallas_call | solution.py:114
  53.5 0.8 collective-permute-start.7
  54.9 1.3 fusion.1
  56.1 1.5 %collective-permute-done.7.refs_2_ = bf16[128,128]{1,0:T(8,128)(2,1)S(1)} collective-permute-done((bf16[128,128]{1,0:T(8,128)(2,1)}, bf16[128,128]{1,0:T(8,128)(2,1)S(1)}, u32[]{:S(2)}, u32[]{:S(2)}) %collective-permute-start.7) | collective-permute-done | bytes 32800 | tf_op jit(solution)/shard_map/ppermute | solution.py:43
  58.8 5.2 %shard_map.124 = (bf16[128,128]{1,0:T(8,128)(2,1)}, bf16[128,3072]{1,0:T(8,128)(2,1)}) custom-call(s32[2,2]{1,0:T(2,128)} %times.9, f32[1,15360]{1,0:T(1,128)} %pad_maximum_fusion.2.mod, bf16[128,64]{1,0:T(8,128)(2,1)} %fusion.refs_0_.latent, bf16[1,128,128]{2,1,0:T(8,128)(2,1)} %noise.3, bf16[1,64,3072]{2,1,0:T(8,128)(2,1)} %embed_w.9, ...), custom_call_target="tpu_custom_call" | custom-call | flops 402653184 | bytes 4993040 | tf_op jit(solution)/shard_map/pallas_call | solution.py:114
  64.0 1.3 collective-permute-start.11
  65.3 1.3 collective-permute-start.12
  66.6 1.3 collective-permute-start.13
  67.9 0.6 collective-permute-done.12
  68.5 1.3 collective-permute-done.13
  69.8 0.8 add_select_fusion.pair
  70.6 1.2 collective-permute-start.15
  71.9 0.6 collective-permute-start.16
  72.5 2.1 %collective-permute-done.15.refs_2_ = bf16[128,64]{1,0:T(8,128)(2,1)S(1)} collective-permute-done((bf16[128,64]{1,0:T(8,128)(2,1)S(1)}, bf16[128,64]{1,0:T(8,128)(2,1)S(1)}, u32[]{:S(2)}, u32[]{:S(2)}) %collective-permute-start.15) | collective-permute-done | bytes 16416 | tf_op jit(solution)/shard_map/ppermute | solution.py:37
  74.6 0.6 collective-permute-done.16.refs_3_
  75.2 0.6 copy-done.23
  75.8 2.2 %shard_map.125 = (bf16[128,128]{1,0:T(8,128)(2,1)}, bf16[128,128]{1,0:T(8,128)(2,1)}, bf16[128,128]{1,0:T(8,128)(2,1)}, bf16[128,128]{1,0:T(8,128)(2,1)}, f32[51...) custom-call(f32[80,384]{1,0:T(8,128)} %get-tuple-element.37.short_in, ...), custom_call_target="tpu_custom_call" | custom-call | flops 402653184 | bytes 2024448 | tf_op jit(solution)/shard_map/pallas_call | solution.py:114
  78.2 0.9 collective-permute-start.18
  79.1 0.8 collective-permute-start.19
  79.9 2.4 %collective-permute-done.18.refs_2_ = bf16[128,128]{1,0:T(8,128)(2,1)S(1)} collective-permute-done((bf16[128,128]{1,0:T(8,128)(2,1)}, bf16[128,128]{1,0:T(8,128)(2,1)S(1)}, u32[]{:S(2)}, u32[]{:S(2)}) %collective-permute-start.18) | collective-permute-done | bytes 32800 | tf_op jit(solution)/shard_map/ppermute | solution.py:43
  83.3 3.3 %shard_map.126 = (bf16[128,128]{1,0:T(8,128)(2,1)}, bf16[128,128]{1,0:T(8,128)(2,1)}, bf16[128,128]{1,0:T(8,128)(2,1)}, bf16[128,128]{1,0:T(8,128)(2,1)}, bf16[1...) custom-call(s32[2,2]{1,0:T(2,128)} %times.9, ...), custom_call_target="tpu_custom_call" | custom-call | flops 805306368 | bytes 5210128 | tf_op jit(solution)/shard_map/pallas_call | solution.py:114
  86.8 1.1 collective-permute-start.21
  88.0 0.6 collective-permute-start.22
  88.6 2.4 %collective-permute-done.21.refs_6_ = bf16[128,128]{1,0:T(8,128)(2,1)S(1)} collective-permute-done((bf16[128,128]{1,0:T(8,128)(2,1)}, bf16[128,128]{1,0:T(8,128)(2,1)S(1)}, u32[]{:S(2)}, u32[]{:S(2)}) %collective-permute-start.21) | collective-permute-done | bytes 32800 | tf_op jit(solution)/shard_map/ppermute | solution.py:43
  91.0 0.6 collective-permute-done.22.refs_7_
  91.6 0.6 copy-done.26
  92.2 2.2 %shard_map.127 = (bf16[160,64]{1,0:T(8,128)(2,1)}, bf16[160,64]{1,0:T(8,128)(2,1)}, bf16[160,64]{1,0:T(8,128)(2,1)}, bf16[160,64]{1,0:T(8,128)(2,1)}) custom-call(f32[80,384]{1,0:T(8,128)} %get-tuple-element.37.short_in, bf16[1,64,3072]{2,1,0:T(8,128)(2,1)} %embed_w.9, f32[1,2,128]{2,1,0:T(2,128)} %gains.5, f32[512,384]{1,0:T(8,128)} %get-tuple-element.47.proj_ref, ...), custom_call_target="tpu_custom_call" | custom-call | flops 335544320 | bytes 2110464 | tf_op jit(solution)/shard_map/pallas_call | solution.py:114
  94.5 1.0 collective-permute-start.24
  95.5 0.8 collective-permute-start.25
  96.3 2.5 %collective-permute-done.24.refs_2_ = bf16[160,64]{1,0:T(8,128)(2,1)S(1)} collective-permute-done((bf16[160,64]{1,0:T(8,128)(2,1)}, bf16[160,64]{1,0:T(8,128)(2,1)S(1)}, u32[]{:S(2)}, u32[]{:S(2)}) %collective-permute-start.24) | collective-permute-done | bytes 20512 | tf_op jit(solution)/shard_map/ppermute | solution.py:43
  99.4 0.6 copy-done.10
  100.0 1.6 %shard_map.128.refs_0_ = bf16[160,64]{1,0:T(8,128)(2,1)} custom-call(s32[2,2]{1,0:T(2,128)} %times.9, f32[128,64]{1,0:T(8,128)} %get-tuple-element.45.direct, f32[128,64]{1,0:T(8,128)} %get-tuple-element.46.term, bf16[160,64]{1,0:T(8,128)(2,1)} %get-tuple-element.56.refs_0_, bf16[160,64]{1,0:T(8,128)(2,1)} %copy-done.8, bf16[160,64]{1,0:T(8,128)(2,1)} %copy-done.9, ...), custom_call_target="tpu_custom_call" | custom-call | flops 1000 | bytes 167952 | tf_op jit(solution)/shard_map/pallas_call | solution.py:114
  101.6 6.2 %collective-permute-start.26 = (bf16[160,64]{1,0:T(8,128)(2,1)}, bf16[160,64]{1,0:T(8,128)(2,1)S(1)}, u32[]{:S(2)}, u32[]{:S(2)}) collective-permute-start(bf16[160,64]{1,0:T(8,128)(2,1)} %shard_map.128.refs_0_), channel_id=1, source_target_pairs={{0,8},{8,16},{16,24},{24,0},{1,9},{9,17},{17,25},{25,1},{2,10},{10... | collective-permute-start | bytes 61448 | tf_op jit(solution)/shard_map/ppermute | solution.py:653
  107.8 5.0 %collective-permute-start.27 = (bf16[160,64]{1,0:T(8,128)(2,1)}, bf16[160,64]{1,0:T(8,128)(2,1)S(1)}, u32[]{:S(2)}, u32[]{:S(2)}) collective-permute-start(bf16[160,64]{1,0:T(8,128)(2,1)} %shard_map.128.refs_0_), channel_id=1, source_target_pairs={{0,16},{8,24},{16,0},{24,8},{1,17},{9,25},{17,1},{25,9},{2,18},{10... | collective-permute-start | bytes 61448 | tf_op jit(solution)/shard_map/ppermute | solution.py:653
  112.8 2.0 %collective-permute-done.26.refs_1_ = bf16[160,64]{1,0:T(8,128)(2,1)S(1)} collective-permute-done((bf16[160,64]{1,0:T(8,128)(2,1)}, bf16[160,64]{1,0:T(8,128)(2,1)S(1)}, u32[]{:S(2)}, u32[]{:S(2)}) %collective-permute-start.26) | collective-permute-done | bytes 20512 | tf_op jit(solution)/shard_map/ppermute | solution.py:653
  114.8 1.3 collective-permute-done.27.refs_2_
  116.1 0.9 collective-permute-done.28.refs_3_
  117.0 0.6 copy-done.13
  117.6 2.8 %shard_map.129 = (f32[1,128,64]{2,1,0:T(8,128)}, bf16[3072,64]{1,0:T(8,128)(2,1)}) custom-call(s32[2,2]{1,0:T(2,128)} %times.9, f32[128,64]{1,0:T(8,128)} %get-tuple-element.42.target_in, bf16[128,3072]{1,0:T(8,128)(2,1)} %get-tuple-element.43.student_in, bf16[128,3072]{1,0:T(8,128)(2,1)} %get-tuple-element.44.critic_in, ...), custom_call_target="tpu_custom_call" | custom-call | flops 50331648 | bytes 2113552 | tf_op jit(solution)/shard_map/pallas_call | solution.py:114
  120.4 1.2 broadcast_select_fusion
  121.7 1.7 %collective-permute-done.29 = bf16[1536,64]{1,0:T(8,128)(2,1)S(1)} collective-permute-done((bf16[1536,64]{1,0:T(8,128)(2,1)S(1)}, bf16[1536,64]{1,0:T(8,128)(2,1)S(1)}, u32[]{:S(2)}, u32[]{:S(2)}) %collective-permute-start.29) | collective-permute-done | bytes 196640 | tf_op jit(solution)/shard_map/ppermute | solution.py:527
  123.6 1.0 collective-permute-start.30
  124.6 6.0 %collective-permute-done.30 = bf16[768,64]{1,0:T(8,128)(2,1)S(1)} collective-permute-done((bf16[768,64]{1,0:T(8,128)(2,1)S(1)}, bf16[768,64]{1,0:T(8,128)(2,1)S(1)}, u32[]{:S(2)}, u32[]{:S(2)}) %collective-permute-start.30) | collective-permute-done | bytes 98336 | tf_op jit(solution)/shard_map/ppermute | solution.py:527
  130.7 1.6 %collective-permute-start.31 = (bf16[768,64]{1,0:T(8,128)(2,1)S(1)}, bf16[768,64]{1,0:T(8,128)(2,1)S(1)}, u32[]{:S(2)}, u32[]{:S(2)}) collective-permute-start(bf16[768,64]{1,0:T(8,128)(2,1)S(1)} %add_convert_fusion.2), channel_id=1, source_target_pairs={{0,1},{1,0},{2,3},{3,2},{4,5},{5,4},{6,7},{7,6},{8,9},{9,8},{10,11... | collective-permute-start | bytes 294920 | tf_op jit(solution)/shard_map/ppermute | solution.py:534
  132.3 4.6 %collective-permute-done.31 = bf16[768,64]{1,0:T(8,128)(2,1)S(1)} collective-permute-done((bf16[768,64]{1,0:T(8,128)(2,1)S(1)}, bf16[768,64]{1,0:T(8,128)(2,1)S(1)}, u32[]{:S(2)}, u32[]{:S(2)}) %collective-permute-start.31) | collective-permute-done | bytes 98336 | tf_op jit(solution)/shard_map/ppermute | solution.py:534
  136.9 1.0 collective-permute-start.32
  137.9 4.7 %collective-permute-done.32 = bf16[768,64]{1,0:T(8,128)(2,1)S(1)} collective-permute-done((bf16[768,64]{1,0:T(8,128)(2,1)S(1)}, bf16[768,64]{1,0:T(8,128)(2,1)S(1)}, u32[]{:S(2)}, u32[]{:S(2)}) %collective-permute-start.32) | collective-permute-done | bytes 98336 | tf_op jit(solution)/shard_map/ppermute | solution.py:538
  142.9 0.7 copy.24
  143.6 1.0 collective-permute-done.33
  144.9 1.3 copy.25
  (92 shorter events, 6.2 us)
Async XLA Ops:
  0.6 13.8 %copy-start.27 = (s32[2,2]{1,0:T(2,128)S(1)}, s32[2,2]{1,0:T(2,128)}, u32[]{:S(2)}) copy-start(s32[2,2]{1,0:T(2,128)} %times.9) | copy-start | bytes 52
  0.6 13.8 %copy-start.28 = (bf16[1,128,64]{1,2,0:T(8,128)(2,1)S(1)}, bf16[1,128,64]{1,2,0:T(8,128)(2,1)}, u32[]{:S(2)}) copy-start(bf16[1,128,64]{1,2,0:T(8,128)(2,1)} %param.11) | copy-start | bytes 49156
  0.7 14.0 %copy-start.4 = (bf16[1,128,128]{2,1,0:T(8,128)(2,1)S(1)}, bf16[1,128,128]{2,1,0:T(8,128)(2,1)}, u32[]{:S(2)}) copy-start(bf16[1,128,128]{2,1,0:T(8,128)(2,1)} %noise.3) | copy-start | bytes 98308
  11.2 12.5 %collective-permute-start = (f32[1,3840]{1,0:T(1,128)}, f32[1,3840]{1,0:T(1,128)}, u32[]{:S(2)}, u32[]{:S(2)}) collective-permute-start(f32[1,3840]{1,0:T(1,128)} %shard_map.122), channel_id=1, source_target_pairs={{0,6},{2,4},{4,2},{6,0},{1,7},{3,5},{5,3},{7,1},{8,14},{10,12},{12... | collective-permute-start | bytes 46088 | tf_op jit(solution)/shard_map/modulation/ppermute | solution.py:37
  13.7 10.0 %collective-permute-start.1 = (f32[1,3840]{1,0:T(1,128)}, f32[1,3840]{1,0:T(1,128)}, u32[]{:S(2)}, u32[]{:S(2)}) collective-permute-start(f32[1,3840]{1,0:T(1,128)} %shard_map.122), channel_id=1, source_target_pairs={{0,4},{2,6},{4,0},{6,2},{1,5},{3,7},{5,1},{7,3},{8,12},{10,14},{12... | collective-permute-start | bytes 46088 | tf_op jit(solution)/shard_map/modulation/ppermute | solution.py:37
  14.4 11.1 %collective-permute-start.2 = (f32[1,3840]{1,0:T(1,128)}, f32[1,3840]{1,0:T(1,128)}, u32[]{:S(2)}, u32[]{:S(2)}) collective-permute-start(f32[1,3840]{1,0:T(1,128)} %shard_map.122), channel_id=1, source_target_pairs={{0,2},{2,0},{4,6},{6,4},{1,3},{3,1},{5,7},{7,5},{8,10},{10,8},{12,... | collective-permute-start | bytes 46088 | tf_op jit(solution)/shard_map/modulation/ppermute | solution.py:37
  15.3 30.7 %collective-permute-start.3 = (bf16[128,64]{1,0:T(8,128)(2,1)}, bf16[128,64]{1,0:T(8,128)(2,1)}, u32[]{:S(2)}, u32[]{:S(2)}) collective-permute-start(bf16[128,64]{1,0:T(8,128)(2,1)} %fusion.refs_0_.latent), channel_id=1, source_target_pairs={{0,2},{2,0},{4,6},{6,4},{1,3},{3,1},{5,7},{7,5},{8,10},{10,8},{12,... | collective-permute-start | bytes 49160 | tf_op jit(solution)/shard_map/student_rows/ppermute | solution.py:37
  15.8 30.3 %collective-permute-start.4 = (bf16[128,64]{1,0:T(8,128)(2,1)}, bf16[128,64]{1,0:T(8,128)(2,1)}, u32[]{:S(2)}, u32[]{:S(2)}) collective-permute-start(bf16[128,64]{1,0:T(8,128)(2,1)} %fusion.refs_0_.latent), channel_id=1, source_target_pairs={{0,4},{2,6},{4,0},{6,2},{1,5},{3,7},{5,1},{7,3},{8,12},{10,14},{12... | collective-permute-start | bytes 49160 | tf_op jit(solution)/shard_map/student_rows/ppermute | solution.py:37
  20.0 2.5 %copy-start.3 = (bf16[1,3072,64]{1,2,0:T(8,128)(2,1)S(1)}, bf16[1,3072,64]{1,2,0:T(8,128)(2,1)}, u32[]{:S(2)}) copy-start(bf16[1,3072,64]{1,2,0:T(8,128)(2,1)} %param.21) | copy-start | bytes 1179652
  20.0 3.7 %copy-start = (bf16[1,1,128,3072]{3,2,1,0:T(8,128)(2,1)S(1)}, bf16[1,1,128,3072]{3,2,1,0:T(8,128)(2,1)}, u32[]{:S(2)}) copy-start(bf16[1,1,128,3072]{3,2,1,0:T(8,128)(2,1)} %param.19) | copy-start | bytes 2359300
  20.0 5.4 %copy-start.7 = (f32[1,3840]{1,0:T(1,128)S(1)}, f32[1,3840]{1,0:T(1,128)}, u32[]{:S(2)}) copy-start(f32[1,3840]{1,0:T(1,128)} %shard_map.122) | copy-start | bytes 46084
  23.7 22.3 %collective-permute-start.5 = (bf16[128,64]{1,0:T(8,128)(2,1)}, bf16[128,64]{1,0:T(8,128)(2,1)S(1)}, u32[]{:S(2)}, u32[]{:S(2)}) collective-permute-start(bf16[128,64]{1,0:T(8,128)(2,1)} %fusion.refs_0_.latent), channel_id=1, source_target_pairs={{0,6},{2,4},{4,2},{6,0},{1,7},{3,5},{5,3},{7,1},{8,14},{10,12},{12... | collective-permute-start | bytes 49160 | tf_op jit(solution)/shard_map/student_rows/ppermute | solution.py:37
  23.7 20.7 %collective-permute-start.9 = (bf16[128,3072]{1,0:T(8,128)(2,1)S(1)}, bf16[128,3072]{1,0:T(8,128)(2,1)S(1)}, u32[]{:S(2)}, u32[]{:S(2)}) collective-permute-start(bf16[128,3072]{1,0:T(8,128)(2,1)S(1)} %bitcast.14), channel_id=1, source_target_pairs={{0,4},{2,6},{4,0},{6,2},{1,5},{3,7},{5,1},{7,3},{8,12},{10,14},{12... | collective-permute-start | bytes 2359304 | tf_op jit(solution)/shard_map/heads/ppermute | solution.py:53
  44.4 0.9 copy-start.1
  45.3 9.6 %collective-permute-start.10 = (bf16[256,3072]{1,0:T(8,128)(2,1)S(1)}, bf16[256,3072]{1,0:T(8,128)(2,1)S(1)}, u32[]{:S(2)}, u32[]{:S(2)}) collective-permute-start(bf16[256,3072]{1,0:T(8,128)(2,1)S(1)} %pad_maximum_fusion), channel_id=1, source_target_pairs={{0,2},{2,0},{4,6},{6,4},{1,3},{3,1},{5,7},{7,5},{8,10},{10,8},{12,... | collective-permute-start | bytes 4718600 | tf_op jit(solution)/shard_map/heads/ppermute | solution.py:53
  46.0 0.6 copy-start.14
  53.0 3.2 %collective-permute-start.6 = (bf16[128,128]{1,0:T(8,128)(2,1)}, bf16[128,128]{1,0:T(8,128)(2,1)S(1)}, u32[]{:S(2)}, u32[]{:S(2)}) collective-permute-start(bf16[128,128]{1,0:T(8,128)(2,1)} %get-tuple-element.33), channel_id=1, source_target_pairs={{0,2},{2,0},{4,6},{6,4},{1,3},{3,1},{5,7},{7,5},{8,10},{10,8},{12,... | collective-permute-start | bytes 98312 | tf_op jit(solution)/shard_map/ppermute | solution.py:43
  53.5 4.2 %collective-permute-start.7 = (bf16[128,128]{1,0:T(8,128)(2,1)}, bf16[128,128]{1,0:T(8,128)(2,1)S(1)}, u32[]{:S(2)}, u32[]{:S(2)}) collective-permute-start(bf16[128,128]{1,0:T(8,128)(2,1)} %get-tuple-element.34), channel_id=1, source_target_pairs={{0,4},{2,6},{4,0},{6,2},{1,5},{3,7},{5,1},{7,3},{8,12},{10,14},{12... | collective-permute-start | bytes 98312 | tf_op jit(solution)/shard_map/ppermute | solution.py:43
  54.3 3.9 %collective-permute-start.8 = (bf16[128,128]{1,0:T(8,128)(2,1)}, bf16[128,128]{1,0:T(8,128)(2,1)S(1)}, u32[]{:S(2)}, u32[]{:S(2)}) collective-permute-start(bf16[128,128]{1,0:T(8,128)(2,1)} %get-tuple-element.35), channel_id=1, source_target_pairs={{0,6},{2,4},{4,2},{6,0},{1,7},{3,5},{5,3},{7,1},{8,14},{10,12},{12... | collective-permute-start | bytes 98312 | tf_op jit(solution)/shard_map/ppermute | solution.py:43
  56.1 2.1 %copy-start.16 = (bf16[128,128]{1,0:T(8,128)(2,1)}, bf16[128,128]{1,0:T(8,128)(2,1)S(1)}, u32[]{:S(2)}) copy-start(bf16[128,128]{1,0:T(8,128)(2,1)S(1)} %collective-permute-done.6.refs_1_) | copy-start | bytes 98308
  57.7 0.6 copy-start.18
  58.2 0.6 copy-start.20
  64.0 3.9 %collective-permute-start.11 = (bf16[128,128]{1,0:T(8,128)(2,1)}, bf16[128,128]{1,0:T(8,128)(2,1)S(1)}, u32[]{:S(2)}, u32[]{:S(2)}) collective-permute-start(bf16[128,128]{1,0:T(8,128)(2,1)} %get-tuple-element.36), channel_id=1, source_target_pairs={{0,24},{1,25},{2,26},{3,27},{4,28},{5,29},{6,30},{7,31}} | collective-permute-start | bytes 98312 | tf_op jit(solution)/shard_map/ppermute | solution.py:613
  65.3 3.2 %collective-permute-start.12 = (bf16[128,128]{1,0:T(8,128)(2,1)}, bf16[128,128]{1,0:T(8,128)(2,1)S(1)}, u32[]{:S(2)}, u32[]{:S(2)}) collective-permute-start(bf16[128,128]{1,0:T(8,128)(2,1)} %get-tuple-element.36), channel_id=1, source_target_pairs={{0,16},{1,17},{2,18},{3,19},{4,20},{5,21},{6,22},{7,23}} | collective-permute-start | bytes 98312 | tf_op jit(solution)/shard_map/ppermute | solution.py:613
  66.6 3.2 %collective-permute-start.13 = (bf16[128,128]{1,0:T(8,128)(2,1)}, bf16[128,128]{1,0:T(8,128)(2,1)S(1)}, u32[]{:S(2)}, u32[]{:S(2)}) collective-permute-start(bf16[128,128]{1,0:T(8,128)(2,1)} %get-tuple-element.36), channel_id=1, source_target_pairs={{0,8},{1,9},{2,10},{3,11},{4,12},{5,13},{6,14},{7,15}} | collective-permute-start | bytes 98312 | tf_op jit(solution)/shard_map/ppermute | solution.py:613
  70.6 4.7 %copy-start.5 = (bf16[128,128]{1,0:T(8,128)(2,1)}, bf16[128,128]{1,0:T(8,128)(2,1)S(1)}, u32[]{:S(2)}) copy-start(bf16[128,128]{1,0:T(8,128)(2,1)S(1)} %add_select_fusion.pair) | copy-start | bytes 98308
  70.6 1.9 %collective-permute-start.14 = (bf16[128,64]{1,0:T(8,128)(2,1)S(1)}, bf16[128,64]{1,0:T(8,128)(2,1)S(1)}, u32[]{:S(2)}, u32[]{:S(2)}) collective-permute-start(bf16[128,64]{1,0:T(8,128)(2,1)S(1)} %bitcast.16), channel_id=1, source_target_pairs={{0,2},{2,0},{4,6},{6,4},{1,3},{3,1},{5,7},{7,5},{8,10},{10,8},{12,... | collective-permute-start | bytes 49160 | tf_op jit(solution)/shard_map/ppermute | solution.py:37
  70.6 4.0 %collective-permute-start.15 = (bf16[128,64]{1,0:T(8,128)(2,1)S(1)}, bf16[128,64]{1,0:T(8,128)(2,1)S(1)}, u32[]{:S(2)}, u32[]{:S(2)}) collective-permute-start(bf16[128,64]{1,0:T(8,128)(2,1)S(1)} %bitcast.17), channel_id=1, source_target_pairs={{0,4},{2,6},{4,0},{6,2},{1,5},{3,7},{5,1},{7,3},{8,12},{10,14},{12... | collective-permute-start | bytes 49160 | tf_op jit(solution)/shard_map/ppermute | solution.py:37
  71.9 3.4 %collective-permute-start.16 = (bf16[128,64]{1,0:T(8,128)(2,1)S(1)}, bf16[128,64]{1,0:T(8,128)(2,1)S(1)}, u32[]{:S(2)}, u32[]{:S(2)}) collective-permute-start(bf16[128,64]{1,0:T(8,128)(2,1)S(1)} %bitcast.18), channel_id=1, source_target_pairs={{0,6},{2,4},{4,2},{6,0},{1,7},{3,5},{5,3},{7,1},{8,14},{10,12},{12... | collective-permute-start | bytes 49160 | tf_op jit(solution)/shard_map/ppermute | solution.py:37
  72.5 2.7 %copy-start.21 = (bf16[128,64]{1,0:T(8,128)(2,1)}, bf16[128,64]{1,0:T(8,128)(2,1)S(1)}, u32[]{:S(2)}) copy-start(bf16[128,64]{1,0:T(8,128)(2,1)S(1)} %collective-permute-done.14.refs_1_) | copy-start | bytes 49156
  74.6 0.6 copy-start.22
  75.2 0.6 copy-start.23
  78.0 1.9 %collective-permute-start.17 = (bf16[128,128]{1,0:T(8,128)(2,1)}, bf16[128,128]{1,0:T(8,128)(2,1)S(1)}, u32[]{:S(2)}, u32[]{:S(2)}) collective-permute-start(bf16[128,128]{1,0:T(8,128)(2,1)} %get-tuple-element.39), channel_id=1, source_target_pairs={{0,2},{2,0},{4,6},{6,4},{1,3},{3,1},{5,7},{7,5},{8,10},{10,8},{12,... | collective-permute-start | bytes 98312 | tf_op jit(solution)/shard_map/ppermute | solution.py:43
  78.2 4.1 %collective-permute-start.18 = (bf16[128,128]{1,0:T(8,128)(2,1)}, bf16[128,128]{1,0:T(8,128)(2,1)S(1)}, u32[]{:S(2)}, u32[]{:S(2)}) collective-permute-start(bf16[128,128]{1,0:T(8,128)(2,1)} %get-tuple-element.40), channel_id=1, source_target_pairs={{0,4},{2,6},{4,0},{6,2},{1,5},{3,7},{5,1},{7,3},{8,12},{10,14},{12... | collective-permute-start | bytes 98312 | tf_op jit(solution)/shard_map/ppermute | solution.py:43
  79.1 3.6 %collective-permute-start.19 = (bf16[128,128]{1,0:T(8,128)(2,1)}, bf16[128,128]{1,0:T(8,128)(2,1)S(1)}, u32[]{:S(2)}, u32[]{:S(2)}) collective-permute-start(bf16[128,128]{1,0:T(8,128)(2,1)} %get-tuple-element.41), channel_id=1, source_target_pairs={{0,6},{2,4},{4,2},{6,0},{1,7},{3,5},{5,3},{7,1},{8,14},{10,12},{12... | collective-permute-start | bytes 98312 | tf_op jit(solution)/shard_map/ppermute | solution.py:43
  79.9 2.8 %copy-start.15 = (bf16[128,128]{1,0:T(8,128)(2,1)}, bf16[128,128]{1,0:T(8,128)(2,1)S(1)}, u32[]{:S(2)}) copy-start(bf16[128,128]{1,0:T(8,128)(2,1)S(1)} %collective-permute-done.17.refs_1_) | copy-start | bytes 98308
  82.3 0.6 copy-start.17
  82.7 0.6 copy-start.19
  86.7 1.9 %collective-permute-start.20 = (bf16[128,128]{1,0:T(8,128)(2,1)}, bf16[128,128]{1,0:T(8,128)(2,1)S(1)}, u32[]{:S(2)}, u32[]{:S(2)}) collective-permute-start(bf16[128,128]{1,0:T(8,128)(2,1)} %get-tuple-element.53), channel_id=1, source_target_pairs={{0,2},{2,0},{4,6},{6,4},{1,3},{3,1},{5,7},{7,5},{8,10},{10,8},{12,... | collective-permute-start | bytes 98312 | tf_op jit(solution)/shard_map/ppermute | solution.py:43
  86.8 4.1 %collective-permute-start.21 = (bf16[128,128]{1,0:T(8,128)(2,1)}, bf16[128,128]{1,0:T(8,128)(2,1)S(1)}, u32[]{:S(2)}, u32[]{:S(2)}) collective-permute-start(bf16[128,128]{1,0:T(8,128)(2,1)} %get-tuple-element.54), channel_id=1, source_target_pairs={{0,4},{2,6},{4,0},{6,2},{1,5},{3,7},{5,1},{7,3},{8,12},{10,14},{12... | collective-permute-start | bytes 98312 | tf_op jit(solution)/shard_map/ppermute | solution.py:43
  88.0 3.6 %collective-permute-start.22 = (bf16[128,128]{1,0:T(8,128)(2,1)}, bf16[128,128]{1,0:T(8,128)(2,1)S(1)}, u32[]{:S(2)}, u32[]{:S(2)}) collective-permute-start(bf16[128,128]{1,0:T(8,128)(2,1)} %get-tuple-element.55), channel_id=1, source_target_pairs={{0,6},{2,4},{4,2},{6,0},{1,7},{3,5},{5,3},{7,1},{8,14},{10,12},{12... | collective-permute-start | bytes 98312 | tf_op jit(solution)/shard_map/ppermute | solution.py:43
  88.6 3.0 %copy-start.24 = (bf16[128,128]{1,0:T(8,128)(2,1)}, bf16[128,128]{1,0:T(8,128)(2,1)S(1)}, u32[]{:S(2)}) copy-start(bf16[128,128]{1,0:T(8,128)(2,1)S(1)} %collective-permute-done.20.refs_5_) | copy-start | bytes 98308
  91.0 0.6 copy-start.25
  91.6 0.6 copy-start.26
  94.4 1.9 %collective-permute-start.23 = (bf16[160,64]{1,0:T(8,128)(2,1)}, bf16[160,64]{1,0:T(8,128)(2,1)S(1)}, u32[]{:S(2)}, u32[]{:S(2)}) collective-permute-start(bf16[160,64]{1,0:T(8,128)(2,1)} %get-tuple-element.57), channel_id=1, source_target_pairs={{0,2},{2,0},{4,6},{6,4},{1,3},{3,1},{5,7},{7,5},{8,10},{10,8},{12,... | collective-permute-start | bytes 61448 | tf_op jit(solution)/shard_map/ppermute | solution.py:43
  94.5 4.3 %collective-permute-start.24 = (bf16[160,64]{1,0:T(8,128)(2,1)}, bf16[160,64]{1,0:T(8,128)(2,1)S(1)}, u32[]{:S(2)}, u32[]{:S(2)}) collective-permute-start(bf16[160,64]{1,0:T(8,128)(2,1)} %get-tuple-element.58), channel_id=1, source_target_pairs={{0,4},{2,6},{4,0},{6,2},{1,5},{3,7},{5,1},{7,3},{8,12},{10,14},{12... | collective-permute-start | bytes 61448 | tf_op jit(solution)/shard_map/ppermute | solution.py:43
  95.5 3.9 %collective-permute-start.25 = (bf16[160,64]{1,0:T(8,128)(2,1)}, bf16[160,64]{1,0:T(8,128)(2,1)S(1)}, u32[]{:S(2)}, u32[]{:S(2)}) collective-permute-start(bf16[160,64]{1,0:T(8,128)(2,1)} %get-tuple-element.59), channel_id=1, source_target_pairs={{0,6},{2,4},{4,2},{6,0},{1,7},{3,5},{5,3},{7,1},{8,14},{10,12},{12... | collective-permute-start | bytes 61448 | tf_op jit(solution)/shard_map/ppermute | solution.py:43
  96.3 3.1 %copy-start.8 = (bf16[160,64]{1,0:T(8,128)(2,1)}, bf16[160,64]{1,0:T(8,128)(2,1)S(1)}, u32[]{:S(2)}) copy-start(bf16[160,64]{1,0:T(8,128)(2,1)S(1)} %collective-permute-done.23.refs_1_) | copy-start | bytes 61444
  98.8 0.6 copy-start.9
  99.4 0.6 copy-start.10
  101.6 13.2 %collective-permute-start.26 = (bf16[160,64]{1,0:T(8,128)(2,1)}, bf16[160,64]{1,0:T(8,128)(2,1)S(1)}, u32[]{:S(2)}, u32[]{:S(2)}) collective-permute-start(bf16[160,64]{1,0:T(8,128)(2,1)} %shard_map.128.refs_0_), channel_id=1, source_target_pairs={{0,8},{8,16},{16,24},{24,0},{1,9},{9,17},{17,25},{25,1},{2,10},{10... | collective-permute-start | bytes 61448 | tf_op jit(solution)/shard_map/ppermute | solution.py:653
  107.8 8.3 %collective-permute-start.27 = (bf16[160,64]{1,0:T(8,128)(2,1)}, bf16[160,64]{1,0:T(8,128)(2,1)S(1)}, u32[]{:S(2)}, u32[]{:S(2)}) collective-permute-start(bf16[160,64]{1,0:T(8,128)(2,1)} %shard_map.128.refs_0_), channel_id=1, source_target_pairs={{0,16},{8,24},{16,0},{24,8},{1,17},{9,25},{17,1},{25,9},{2,18},{10... | collective-permute-start | bytes 61448 | tf_op jit(solution)/shard_map/ppermute | solution.py:653
  112.8 4.2 %collective-permute-start.28 = (bf16[160,64]{1,0:T(8,128)(2,1)}, bf16[160,64]{1,0:T(8,128)(2,1)S(1)}, u32[]{:S(2)}, u32[]{:S(2)}) collective-permute-start(bf16[160,64]{1,0:T(8,128)(2,1)} %shard_map.128.refs_0_), channel_id=1, source_target_pairs={{0,24},{8,0},{16,8},{24,16},{1,25},{9,1},{17,9},{25,17},{2,26},{10... | collective-permute-start | bytes 61448 | tf_op jit(solution)/shard_map/ppermute | solution.py:653
  114.8 2.2 %copy-start.11 = (bf16[160,64]{1,0:T(8,128)(2,1)}, bf16[160,64]{1,0:T(8,128)(2,1)S(1)}, u32[]{:S(2)}) copy-start(bf16[160,64]{1,0:T(8,128)(2,1)S(1)} %collective-permute-done.26.refs_1_) | copy-start | bytes 61444
  116.1 0.9 copy-start.12
  117.0 0.6 copy-start.13
  120.4 3.0 %copy-start.2 = (bf16[3072,64]{1,0:T(8,128)(2,1)S(1)}, bf16[3072,64]{1,0:T(8,128)(2,1)}, u32[]{:S(2)}) copy-start(bf16[3072,64]{1,0:T(8,128)(2,1)} %get-tuple-element.61) | copy-start | bytes 1179652
  121.6 1.8 %collective-permute-start.29 = (bf16[1536,64]{1,0:T(8,128)(2,1)S(1)}, bf16[1536,64]{1,0:T(8,128)(2,1)S(1)}, u32[]{:S(2)}, u32[]{:S(2)}) collective-permute-start(bf16[1536,64]{1,0:T(8,128)(2,1)S(1)} %broadcast_select_fusion), channel_id=1, source_target_pairs={{0,2},{2,0},{4,6},{6,4},{1,3},{3,1},{5,7},{7,5},{8,10},{10,8},{12,... | collective-permute-start | bytes 589832 | tf_op jit(solution)/shard_map/ppermute | solution.py:527
  123.6 19.3 %copy-start.6 = (f32[1,128,64]{2,1,0:T(8,128)S(1)}, f32[1,128,64]{2,1,0:T(8,128)}, u32[]{:S(2)}) copy-start(f32[1,128,64]{2,1,0:T(8,128)} %get-tuple-element.64) | copy-start | bytes 98308
  123.6 7.0 %collective-permute-start.30 = (bf16[768,64]{1,0:T(8,128)(2,1)S(1)}, bf16[768,64]{1,0:T(8,128)(2,1)S(1)}, u32[]{:S(2)}, u32[]{:S(2)}) collective-permute-start(bf16[768,64]{1,0:T(8,128)(2,1)S(1)} %broadcast_select_fusion.3), channel_id=1, source_target_pairs={{0,4},{2,6},{4,0},{6,2},{1,5},{3,7},{5,1},{7,3},{8,12},{10,14},{12... | collective-permute-start | bytes 294920 | tf_op jit(solution)/shard_map/ppermute | solution.py:527
  130.7 6.2 %collective-permute-start.31 = (bf16[768,64]{1,0:T(8,128)(2,1)S(1)}, bf16[768,64]{1,0:T(8,128)(2,1)S(1)}, u32[]{:S(2)}, u32[]{:S(2)}) collective-permute-start(bf16[768,64]{1,0:T(8,128)(2,1)S(1)} %add_convert_fusion.2), channel_id=1, source_target_pairs={{0,1},{1,0},{2,3},{3,2},{4,5},{5,4},{6,7},{7,6},{8,9},{9,8},{10,11... | collective-permute-start | bytes 294920 | tf_op jit(solution)/shard_map/ppermute | solution.py:534
  136.9 5.7 %collective-permute-start.32 = (bf16[768,64]{1,0:T(8,128)(2,1)S(1)}, bf16[768,64]{1,0:T(8,128)(2,1)S(1)}, u32[]{:S(2)}, u32[]{:S(2)}) collective-permute-start(bf16[768,64]{1,0:T(8,128)(2,1)S(1)} %add_convert_fusion.1), channel_id=1, source_target_pairs={{0,4},{2,6},{4,0},{6,2},{1,5},{3,7},{5,1},{7,3},{8,12},{10,14},{12... | collective-permute-start | bytes 294920 | tf_op jit(solution)/shard_map/ppermute | solution.py:538
  142.8 1.8 %collective-permute-start.33 = (bf16[1536,64]{1,0:T(8,128)(2,1)S(1)}, bf16[1536,64]{1,0:T(8,128)(2,1)S(1)}, u32[]{:S(2)}, u32[]{:S(2)}) collective-permute-start(bf16[1536,64]{1,0:T(8,128)(2,1)S(1)} %pad_maximum_fusion.1), channel_id=1, source_target_pairs={{0,2},{2,0},{4,6},{6,4},{1,3},{3,1},{5,7},{7,5},{8,10},{10,8},{12,... | collective-permute-start | bytes 589832 | tf_op jit(solution)/shard_map/ppermute | solution.py:538

commit v3 on v2

--- a/solution.py
+++ b/solution.py
@@ -13,6 +13,7 @@
 ADV_WEIGHT = 3.0
 TILE = 512
 STREAMS = 6
+SPARE = 8 << 20
 VMEM = pl.BlockSpec(memory_space=pltpu.VMEM)
 SMEM = pl.BlockSpec(memory_space=pltpu.SMEM)
 ANY = pl.BlockSpec(memory_space=pl.ANY)
@@ -108,16 +109,27 @@
     return total
 
 
-def run(kernel, outputs, operands, specs, flops, scratch=(), **params):
+def run(kernel, outputs, operands, specs, flops, scratch=()):
     in_bytes = sum(operand.size * operand.dtype.itemsize for operand in operands)
     out_bytes = sum(output.size * output.dtype.itemsize for output in outputs)
+    held = sum(
+        math.prod(ref.shape) * jnp.dtype(ref.dtype).itemsize
+        for ref in scratch
+        if ref.memory_space == pltpu.VMEM
+    )
+    small = sum(
+        operand.size * operand.dtype.itemsize
+        for operand, spec in zip(operands, specs)
+        if spec is VMEM
+    )
+    limit = min(60 << 20, SPARE + held + small + 2 * out_bytes)
     return pl.pallas_call(
         kernel,
         out_shape=outputs,
         in_specs=specs,
         out_specs=[VMEM] * len(outputs),
         scratch_shapes=list(scratch),
-        compiler_params=pltpu.CompilerParams(**params),
+        compiler_params=pltpu.CompilerParams(vmem_limit_bytes=limit),
         cost_estimate=pl.CostEstimate(
             flops=flops, bytes_accessed=in_bytes + out_bytes, transcendentals=0
         ),
@@ -128,7 +140,7 @@
     return jax.ShapeDtypeStruct(shape, dtype)
 
 
-def condition_kernel(times, text, time_w, mod_w, mod_out, held, arrivals):
+def condition_kernel(times, text, time_w, clean_t, noise, mod_w, mod_out, noisy_out, held, arrivals):
     model_width = mod_w.shape[1]
     rows = model_width // STREAMS
     copies = [
@@ -140,6 +152,11 @@
     for copy in copies:
         copy.start()
     student_step, critic_step = steps_of(times)
+    sigma_student = noise_level(student_step)
+    noisy_out[...] = (
+        (1.0 - sigma_student) * clean_t[...].astype(jnp.float32).T
+        + sigma_student * noise[0, :, : clean_t.shape[0]].astype(jnp.float32)
+    ).astype(jnp.bfloat16)
     step = jnp.where(lax.axis_index("segment") == 0, student_step, critic_step)
     half = text.shape[1] // 2
     places = lax.broadcasted_iota(jnp.int32, (1, half), 1).astype(jnp.float32)
@@ -210,11 +227,17 @@
         )
 
 
-def student_front_kernel(count, mod, embed_w, head_w, gains, *refs):
-    rows = refs[:count]
-    head_outs = refs[count : 2 * count]
-    short_ref, proj_ref, inverse_ref, key_ref, value_ref = refs[2 * count :]
+def student_front_kernel(count, embed_w, head_w, gains, *refs):
+    mod_parts = refs[:count]
+    rows = refs[count : 2 * count]
+    head_outs = refs[2 * count : 3 * count]
+    short_ref, late_ref, mod, proj_ref, inverse_ref, key_ref, value_ref = refs[3 * count :]
     model_width = embed_w.shape[2]
+    width = mod_parts[0].shape[1]
+    for place in range(count):
+        first = pl.multiple_of((lax.axis_index("seq") ^ place) * width, 128)
+        mod[:, pl.ds(first, width)] = mod_parts[place][...]
+    late_ref[...] = mod[:, 2 * model_width :]
     central = centred(embed_w)
     scale_in = slot_of(mod, 1, model_width, 0, model_width)
     shift_in = slot_of(mod, 0, model_width, 0, model_width)
@@ -222,7 +245,8 @@
         [central * (1.0 + scale_in), jnp.broadcast_to(shift_in, (16, model_width))], axis=0
     )
     in_top, in_low = halves(in_rows)
-    both = dot32(jnp.concatenate([in_top, in_low], axis=0), head_w[...])
+    in_both = jnp.concatenate([in_top, in_low], axis=0)
+    both = jnp.concatenate([dot32(in_both, head_w[kind]) for kind in range(3)], axis=1)
     short = both[: in_rows.shape[0]] + both[in_rows.shape[0] :]
     short_ref[...] = short
 
@@ -261,7 +285,7 @@
         )
 
 
-def tail(mod, latent, embed_w, final_w, mixed, heads_w, final_in_ref, work):
+def tail(mod, latent, embed_w, final_w, mixed, heads_w, work):
     model_width = embed_w.shape[2]
     block = latent[...]
     sums = None
@@ -272,7 +296,7 @@
             product = dot32(piece[...], rows_w[:, span])
             attended = product if attended is None else attended + product
         residual = (
-            dot32(block, embed_w[0, :, span]) + slot_of(mod, 2, model_width, first, TILE) * attended
+            dot32(block, embed_w[0, :, span]) + slot_of(mod, 0, model_width, first, TILE) * attended
         )
         work[:, span] = residual
         part = lane_sum(residual)
@@ -292,11 +316,10 @@
         normed = work[:, span] * inverse
         work[:, span] = normed
         final_in = (
-            normed * (1.0 + slot_of(mod, 4, model_width, first, TILE))
-            + slot_of(mod, 3, model_width, first, TILE)
+            normed * (1.0 + slot_of(mod, 2, model_width, first, TILE))
+            + slot_of(mod, 1, model_width, first, TILE)
         ).astype(jnp.bfloat16)
-        final_in_ref[:, span] = final_in
-        product = dot32(final_in, final_w[0, span])
+        product = dot32_t(final_in, final_w[:, span])
         result = product if result is None else result + product
     return (result, inverse)
 
@@ -304,14 +327,15 @@
 def student_tail_kernel(count, times, mod, latent, noise, embed_w, final_w, *refs):
     mixed = refs[:count]
     heads_w = refs[count : 2 * count]
-    pair_ref, final_in_ref, work = refs[2 * count :]
+    pair_ref, inverse_ref, work = refs[2 * count :]
     latent_width = latent.shape[1]
 
     @pl.when(lax.axis_index("segment") == 0)
     def _():
         student_step, critic_step = steps_of(times)
         sigma_student, sigma_critic = noise_level(student_step), noise_level(critic_step)
-        velocity, _ = tail(mod, latent, embed_w, final_w, mixed, heads_w, final_in_ref, work)
+        velocity, inverse = tail(mod, latent, embed_w, final_w, mixed, heads_w, work)
+        inverse_ref[...] = jnp.broadcast_to(inverse, inverse_ref.shape)
         sample = latent[...].astype(jnp.float32) - sigma_student * velocity
         second = noise[0, :, latent_width:].astype(jnp.float32)
         critic = (1.0 - sigma_critic) * sample + sigma_critic * second
@@ -322,9 +346,7 @@
     mixed = refs[:count]
     heads_w = refs[count : 2 * count]
     grads = refs[2 * count : 3 * count]
-    final_in_ref, term_ref, target_ref, error_ref, direct_ref, latent, work, other = refs[
-        3 * count :
-    ]
+    inverse_ref, term_ref, target_ref, direct_ref, latent, work, other = refs[3 * count :]
     model_width = embed_w.shape[2]
     latent_width = latent.shape[1]
     section = lax.axis_index("segment")
@@ -336,30 +358,23 @@
         both = pair[...].astype(jnp.float32)
         sample = both[:, latent_width:]
         latent[...] = pair[:, :latent_width]
-        result, inverse = tail(mod, latent, embed_w, final_w, mixed, heads_w, final_in_ref, work)
-        scaled = sigma_critic * result
-        term_ref[...] = scaled
+        result, inverse = tail(mod, latent, embed_w, final_w, mixed, heads_w, work)
+        inverse_ref[...] = jnp.broadcast_to(inverse, inverse_ref.shape)
+        term_ref[...] = (sigma_critic * result).astype(jnp.bfloat16)
         second = noise[0, :, latent_width:].astype(jnp.float32)
         target_ref[...] = jnp.where(
             section == 2,
             2.0 * (result - (second - sample)),
             jnp.where(section == 3, 1.0 / (1.0 + jnp.exp(-result)), 0.0),
         )
-        gaps = jnp.abs(sample - both[:, :latent_width] + scaled)
-        error = jnp.sum(jnp.sum(gaps, axis=1, keepdims=True), axis=0, keepdims=True)
-        error = error / (gaps.shape[0] * latent_width)
-        error_top, error_low = halves(jnp.broadcast_to(error, (16, latent_width)))
-        error_ref[:16] = error_top
-        error_ref[16:] = error_low
-
         @pl.when(section == 3)
         def _():
             grad_logit = (-1.0 / (1.0 + jnp.exp(result))).astype(jnp.bfloat16)
             plain, along = None, None
             for first in range(0, model_width, TILE):
                 span = slice(first, first + TILE)
-                gradient = dot32_t(grad_logit, final_w[0, span]) * (
-                    1.0 + slot_of(mod, 4, model_width, first, TILE)
+                gradient = dot32(grad_logit, final_w[:, span]) * (
+                    1.0 + slot_of(mod, 2, model_width, first, TILE)
                 )
                 other[:, span] = gradient
                 part = lane_sum(gradient)
@@ -376,7 +391,7 @@
                 top, low = halves(grad_residual)
                 product = dot32_t(top, embed_w[0, :, span]) + dot32_t(low, embed_w[0, :, span])
                 direct = product if direct is None else direct + product
-                grad_attended = (slot_of(mod, 2, model_width, first, TILE) * grad_residual).astype(
+                grad_attended = (slot_of(mod, 0, model_width, first, TILE) * grad_residual).astype(
                     jnp.bfloat16
                 )
                 for place in range(count):
@@ -388,7 +403,7 @@
                 grads[place][...] = totals[place].astype(jnp.bfloat16)
 
 
-def judge_back_kernel(count, short_in, embed_w, gains, proj_ref, inverse_ref, key_ref, value_ref, error, *refs):
+def judge_back_kernel(count, short_in, embed_w, gains, proj_ref, inverse_ref, key_ref, value_ref, pair, real, *refs):
     rows = refs[:count]
     grads = refs[count : 2 * count]
     outs = refs[2 * count : 3 * count]
@@ -399,12 +414,19 @@
     head_width = gains.shape[2]
     scale = 1.0 / math.sqrt(head_width)
     size = rows[0].shape[0]
-    for place in range(count):
-        outs[place][size:] = error[...]
 
     @pl.when(section == 3)
     def _():
+        both = pair[...].astype(jnp.float32)
+        gaps = jnp.abs(
+            both[:, latent_width:] - both[:, :latent_width] + real[...].astype(jnp.float32)
+        )
+        error = jnp.sum(jnp.sum(gaps, axis=1, keepdims=True), axis=0, keepdims=True)
+        error = error / (size * latent_width)
+        error_top, error_low = halves(jnp.broadcast_to(error, (16, latent_width)))
         for place in range(count):
+            outs[place][size : size + 16] = error_top
+            outs[place][size + 16 :] = error_low
             low = place * size
             span = slice(low, low + size)
             queries, _, _ = rms_scale(proj_ref[span, :head_width], gains[0, :1])
@@ -458,88 +480,126 @@
             ).astype(jnp.bfloat16)
 
 
-def merge_kernel(count, times, direct, term, *refs):
+def merge_kernel(count, times, direct, real, fake, *refs):
     parts = refs[:count]
     payload_ref = refs[count]
+    rows = direct.shape[0]
+
+    @pl.when(lax.axis_index("segment") == 3)
+    def _():
+        total = parts[0][...].astype(jnp.float32)
+        for part in parts[1:]:
+            total = total + part[...].astype(jnp.float32)
+        _, critic_step = steps_of(times)
+        adverse = (1.0 - noise_level(critic_step)) * (total[:rows] + direct[...])
+        spread = (total[rows : rows + 16] + total[rows + 16 :])[:1, :1] / count + EPS
+        gap = real[...].astype(jnp.float32) - fake[...].astype(jnp.float32)
+        payload_ref[...] = (gap / spread + ADV_WEIGHT * adverse).astype(jnp.bfloat16)
+
+
+def outer_kernel(
+    count, times, arrived, target_in, student_rows, pair, student_inverse, critic_inverse, *refs
+):
+    student_mixed = refs[:count]
+    critic_mixed = refs[count : 2 * count]
+    sums_ref = refs[2 * count]
     section = lax.axis_index("segment")
-    rows = direct.shape[0]
-    total = parts[0][...].astype(jnp.float32)
-    for part in parts[1:]:
-        total = total + part[...].astype(jnp.float32)
-    _, critic_step = steps_of(times)
-    sigma_critic = noise_level(critic_step)
-    adverse = (1.0 - sigma_critic) * (total[:rows] + direct[...])
-    spread = (total[rows : rows + 16] + total[rows + 16 :]) / count + EPS
-    spread_top, spread_low = halves(spread)
-    payload_ref[:rows] = jnp.where(section == 3, adverse, term[...]).astype(jnp.bfloat16)
-    payload_ref[rows : rows + 16] = spread_top
-    payload_ref[rows + 16 :] = spread_low
-
-
-def finish_kernel(sections, times, target_in, student_in, critic_in, *refs):
-    received = refs[:sections]
-    grad_ref, term_ref = refs[sections:]
+    place = lax.axis_index("seq")
+    latent_width = student_rows.shape[1]
+
+    def collect(target, inverse, latent, mixed):
+        target = target.astype(jnp.bfloat16)
+        weighted = inverse[:, :latent_width] * target.astype(jnp.float32)
+        top, low = halves(weighted)
+        for offset in range(count):
+            piece = mixed[offset][...]
+            sums_ref[place ^ offset] = (dot32_first(top, piece) + dot32_first(low, piece)).astype(
+                jnp.bfloat16
+            )
+        near = dot32_first(top, latent) + dot32_first(low, latent)
+        ones = jnp.ones((target.shape[0], sums_ref.shape[2] - latent_width), jnp.bfloat16)
+        sums_ref[count] = jnp.concatenate([near, dot32_first(target, ones)], axis=1).astype(
+            jnp.bfloat16
+        )
+
+    @pl.when(section == 0)
+    def _():
+        student_step, _ = steps_of(times)
+        target = -noise_level(student_step) * arrived[...].astype(jnp.float32)
+        collect(target, student_inverse, student_rows[...], student_mixed)
+
+    @pl.when(section == 1)
+    def _():
+        sums_ref[...] = jnp.zeros_like(sums_ref)
+
+    @pl.when(section >= 2)
+    def _():
+        collect(target_in[...], critic_inverse, pair[:, :latent_width], critic_mixed)
+
+
+def expand_kernel(count, groups, full_rows, own, from_first, from_second, from_third, embed_w, *refs):
+    heads_w = refs[:count]
+    mods = refs[count : count + groups]
+    sums = refs[count + groups : count + 3 * groups]
+    grad_ref, total_ref, work, joined = refs[count + 3 * groups :]
     section = lax.axis_index("segment")
-    rows = target_in.shape[0]
-
-    def payload_of(source):
-        chosen = received[0][...].astype(jnp.float32)
-        for offset in range(1, sections):
-            chosen = jnp.where(
-                lax.rem(section - offset + sections, sections) == source,
-                received[offset][...].astype(jnp.float32),
-                chosen,
+    place = lax.axis_index("seq")
+    latent_width = embed_w.shape[1]
+    model_width = embed_w.shape[2]
+    picked = own[...].astype(jnp.float32)
+    for source, value in ((0, from_first), (2, from_second), (1, from_third)):
+        picked = jnp.where(section == source, value[...].astype(jnp.float32), picked)
+    grad_ref[...] = picked.T
+
+    @pl.when(section == 1)
+    def _():
+        total_ref[...] = jnp.zeros_like(total_ref)
+
+    @pl.when(section != 1)
+    def _():
+        for group in range(groups):
+            low = group * latent_width
+            joined[:, low : low + latent_width] = sums[2 * group][...].astype(jnp.float32) + sums[
+                2 * group + 1
+            ][...].astype(jnp.float32)
+        near_top, near_low = halves(joined[count])
+        heads = [halves(joined[place ^ offset]) for offset in range(count)]
+        averages = None
+        for first in range(0, model_width, TILE):
+            span = slice(first, first + TILE)
+            spread = None
+            for (top, low), rows_w in zip(heads, heads_w):
+                product = dot32(top, rows_w[:, span]) + dot32(low, rows_w[:, span])
+                spread = product if spread is None else spread + product
+            near = dot32(near_top[:, :latent_width], embed_w[0, :, span]) + dot32(
+                near_low[:, :latent_width], embed_w[0, :, span]
             )
-        return chosen
-
-    real, fake, adverse = [payload_of(source) for source in (1, 2, 3)]
-    spread = (real[rows : rows + 16] + real[rows + 16 :])[:1, :1]
-    sample_grad = (real[:rows] - fake[:rows]) / spread + ADV_WEIGHT * adverse[:rows]
-    grad_ref[0] = sample_grad
-
-    @pl.when(section == 0)
-    def _():
-        student_step, _ = steps_of(times)
-        target = (-noise_level(student_step) * sample_grad).astype(jnp.bfloat16)
-        term_ref[...] = dot32_first(student_in[...], target).astype(jnp.bfloat16)
-
-    @pl.when(section == 1)
-    def _():
-        term_ref[...] = jnp.zeros_like(term_ref)
-
-    @pl.when(section >= 2)
-    def _():
-        term_ref[...] = dot32_first(critic_in[...], target_in[...].astype(jnp.bfloat16)).astype(
-            jnp.bfloat16
-        )
-
-
-def reduce_everywhere(term, seq_devices, seq_place):
-    rows = term.shape[0]
-    held = term
-    trail = []
-    bit = 1
-    while bit < seq_devices:
-        half = held.shape[0] // 2
-        upper = (seq_place & bit) != 0
-        away = jnp.where(upper, held[:half], held[half:])
-        kept = jnp.where(upper, held[half:], held[:half])
-        moved = lax.ppermute(away, "seq", swaps(seq_devices, bit))
-        held = (kept.astype(jnp.float32) + moved.astype(jnp.float32)).astype(jnp.bfloat16)
-        trail.append((bit, upper))
-        bit *= 2
-    batch_devices = lax.axis_size("dp")
-    bit = 1
-    while bit < batch_devices:
-        moved = lax.ppermute(held, "dp", swaps(batch_devices, bit))
-        held = (held.astype(jnp.float32) + moved.astype(jnp.float32)).astype(jnp.bfloat16)
-        bit *= 2
-    for bit, upper in reversed(trail):
-        moved = lax.ppermute(held, "seq", swaps(seq_devices, bit))
-        held = jnp.concatenate(
-            [jnp.where(upper, moved, held), jnp.where(upper, held, moved)], axis=0
-        )
-    return held
+            gates = jnp.concatenate(
+                [
+                    jnp.broadcast_to(
+                        slot_of(mod, 0, model_width, first, TILE), (latent_width, TILE)
+                    )
+                    for mod in mods
+                ],
+                axis=0,
+            )
+            value = near + gates * spread
+            work[:, span] = value
+            part = lane_sum(value)
+            averages = part if averages is None else averages + part
+        averages = jnp.sum(averages, axis=1, keepdims=True) / model_width
+        counts = joined[count][:, latent_width : latent_width + 1]
+        for first in range(0, model_width, TILE):
+            span = slice(first, first + TILE)
+            value = work[:, span] - averages
+            total = None
+            for group in range(groups):
+                mine = slice(group * latent_width, (group + 1) * latent_width)
+                product = value[mine] * (
+                    1.0 + slot_of(mods[group], 2, model_width, first, TILE)
+                ) + counts[mine] * slot_of(mods[group], 1, model_width, first, TILE)
+                total = product if total is None else total + product
+            total_ref[:, span] = total / full_rows
 
 
 def shards(
@@ -556,115 +616,204 @@
     count = lax.axis_size("seq")
     full_rows = tok_rows * count
     head_width = w_qkv.shape[4]
-    flat_head_w = w_qkv[0, :, 0].reshape(model_width, 3 * head_width)
-    step_pair = lax.dynamic_index_in_dim(timesteps, batch_idx, 0, keepdims=False)
-    fraction = step_pair[0].astype(jnp.float32) / 1000.0
-    sigma_student = SHIFT * fraction / (1.0 + (SHIFT - 1.0) * fraction)
-    noisy_student = (
-        (1.0 - sigma_student) * clean[0].astype(jnp.float32)
-        + sigma_student * noise[0, :, :latent_width].astype(jnp.float32)
-    ).astype(jnp.bfloat16)
+    kind_w = jnp.transpose(w_qkv[0, :, 0], (1, 0, 2))
+    final_w = jnp.transpose(w_final[0])
     with jax.named_scope("heads"):
         heads_w = gather_doubling(w_out[0, 0], "seq", count)
+    bf16, f32 = jnp.bfloat16, jnp.float32
+
+    with jax.named_scope("conditioning"):
+        mod_piece, noisy_student = run(
+            condition_kernel,
+            [array((1, mod_width), f32), array((tok_rows, latent_width), bf16)],
+            (timesteps, text_vec, w_time, jnp.transpose(clean[0]), noise, w_mod),
+            [SMEM, VMEM, VMEM, VMEM, VMEM, ANY],
+            2 * model_width * mod_width,
+            scratch=(
+                pltpu.VMEM((model_width, mod_width), bf16),
+                pltpu.SemaphoreType.DMA((STREAMS,)),
+            ),
+        )
+    with jax.named_scope("modulation"):
+        mod_parts = gather_near(mod_piece, "seq", count)
     with jax.named_scope("student_rows"):
         student_rows = gather_near(noisy_student, "seq", count)
-    bf16, f32 = jnp.bfloat16, jnp.float32
-
-    (mod_piece,) = run(
-        condition_kernel,
-        [array((1, mod_width), f32)],
-        (timesteps, text_vec, w_time, w_mod),
-        [SMEM, VMEM, VMEM, ANY],
-        2 * model_width * mod_width,
-        scratch=(
-            pltpu.VMEM((model_width, mod_width), bf16),
-            pltpu.SemaphoreType.DMA((STREAMS,)),
-        ),
-    )
-    with jax.named_scope("modulation"):
-        mod_parts = gather_near(mod_piece, "seq", count)
-    mod = jnp.concatenate(in_order(mod_parts, seq_place), axis=1)
 
     head_blocks = [array((tok_rows, head_width), bf16)] * count
     stored = [
-        array((full_rows, 3 * head_width), f32),
-        array((full_rows, 128), f32),
-        array((full_rows, head_width), bf16),
-        array((full_rows, head_width), bf16),
+        ((full_rows, 3 * head_width), f32),
+        ((full_rows, 128), f32),
+        ((full_rows, head_width), bf16),
+        ((full_rows, head_width), bf16),
     ]
-    *head_outs, short, _, _, _, _ = run(
-        functools.partial(student_front_kernel, count),
-        head_blocks + [array((latent_width + 16, 3 * head_width), f32)] + stored,
-        (mod, w_embed, flat_head_w, qk_gain, *student_rows),
-        [VMEM] * (4 + count),
-        4 * latent_width * model_width * 3 * head_width,
-    )
-    mixed = scatter_near(head_outs, "seq", count)
+    with jax.named_scope("student_front"):
+        *head_outs, short, late_mod = run(
+            functools.partial(student_front_kernel, count),
+            head_blocks
+            + [
+                array((latent_width + 16, 3 * head_width), f32),
+                array((1, 3 * model_width), f32),
+            ],
+            (w_embed, kind_w, qk_gain, *mod_parts, *student_rows),
+            [VMEM] * (3 + 2 * count),
+            4 * latent_width * model_width * 3 * head_width,
+            scratch=[pltpu.VMEM((1, 5 * model_width), f32)]
+            + [pltpu.VMEM(shape, kind) for shape, kind in stored],
+        )
+    with jax.named_scope("student_heads"):
+        student_mixed = scatter_near(head_outs, "seq", count)
+    with jax.named_scope("other_mod"):
+        groups = lax.axis_size("dp")
+        late_mods = gather_near(late_mod, "dp", groups)
     work = pltpu.VMEM((tok_rows, model_width), f32)
-    pair, student_in = run(
-        functools.partial(student_tail_kernel, count),
-        [array((tok_rows, 2 * latent_width), bf16), array((tok_rows, model_width), bf16)],
-        (timesteps, mod, noisy_student, noise, w_embed, w_final, *mixed, *heads_w),
-        [SMEM] + [VMEM] * (5 + 2 * count),
-        2 * tok_rows * model_width * head_width * count,
-        scratch=(work,),
-    )
-    arrived = [
-        lax.ppermute(pair, "segment", [(0, place)]) for place in range(sections - 1, 0, -1)
-    ]
-    pair = jnp.where(section == 0, pair, sum(arrived[1:], arrived[0]))
-    critic_rows = gather_near(pair[:, :latent_width], "seq", count)
-    *head_outs, proj, inverse, keys, values = run(
-        functools.partial(critic_front_kernel, count),
-        head_blocks + stored,
-        (short, w_embed, qk_gain, *critic_rows),
-        [VMEM] * (3 + count),
-        4 * latent_width * model_width * full_rows,
-    )
-    mixed = scatter_near(head_outs, "seq", count)
+    inverse_shape = array((tok_rows, 128), f32)
+    with jax.named_scope("student_tail"):
+        pair, student_inverse = run(
+            functools.partial(student_tail_kernel, count),
+            [array((tok_rows, 2 * latent_width), bf16), inverse_shape],
+            (timesteps, late_mod, noisy_student, noise, w_embed, final_w, *student_mixed, *heads_w),
+            [SMEM] + [VMEM] * (5 + 2 * count),
+            2 * tok_rows * model_width * head_width * count,
+            scratch=(work,),
+        )
+    with jax.named_scope("sample"):
+        for offset in range(sections - 1, 0, -1):
+            moved = lax.ppermute(
+                pair,
+                "segment",
+                [(place, (place + offset) % sections) for place in range(sections)],
+            )
+            held = moved if offset == sections - 1 else jnp.where(section == offset, moved, held)
+        pair = jnp.where(section == 0, pair, held)
+    with jax.named_scope("critic_rows"):
+        critic_rows = gather_near(pair[:, :latent_width], "seq", count)
+    with jax.named_scope("critic_front"):
+        *head_outs, proj, inverse, keys, values = run(
+            functools.partial(critic_front_kernel, count),
+            head_blocks + [array(shape, kind) for shape, kind in stored],
+            (short, w_embed, qk_gain, *critic_rows),
+            [VMEM] * (3 + count),
+            4 * latent_width * model_width * full_rows,
+        )
+    with jax.named_scope("critic_heads"):
+        critic_mixed = scatter_near(head_outs, "seq", count)
     small = array((tok_rows, latent_width), f32)
-    *grad_heads, critic_in, term_rows, target, error, direct = run(
-        functools.partial(critic_tail_kernel, count),
-        head_blocks
-        + [array((tok_rows, model_width), bf16), small, small, array((32, latent_width), bf16), small],
-        (timesteps, mod, pair, noise, w_embed, w_final, *mixed, *heads_w),
-        [SMEM] + [VMEM] * (5 + 2 * count),
-        4 * tok_rows * model_width * head_width * count,
-        scratch=(pltpu.VMEM((tok_rows, latent_width), bf16), work, work),
-    )
-    grad_blocks = scatter_near(grad_heads, "seq", count)
-    parts = run(
-        functools.partial(judge_back_kernel, count),
-        [array((tok_rows + 32, latent_width), bf16)] * count,
-        (short, w_embed, qk_gain, proj, inverse, keys, values, error, *critic_rows, *grad_blocks),
-        [VMEM] * (8 + 2 * count),
-        10 * full_rows * full_rows * head_width,
-        scratch=(pltpu.VMEM((full_rows, head_width), f32),) * 3,
-    )
-    parts = scatter_near(parts, "seq", count)
-    (payload,) = run(
-        functools.partial(merge_kernel, count),
-        [array((tok_rows + 32, latent_width), bf16)],
-        (timesteps, direct, term_rows, *parts),
-        [SMEM] + [VMEM] * (2 + count),
-        1000,
-    )
-    received = [payload] + [
-        lax.ppermute(
-            payload, "segment", [(place, (place + offset) % sections) for place in range(sections)]
-        )
-        for offset in range(1, sections)
-    ]
-    sample_grad, term = run(
-        functools.partial(finish_kernel, sections),
-        [array((1, tok_rows, latent_width), f32), array((model_width, latent_width), bf16)],
-        (timesteps, target, student_in, critic_in, *received),
-        [SMEM] + [VMEM] * (3 + sections),
-        2 * tok_rows * model_width * latent_width,
-    )
-    total = reduce_everywhere(term, count, seq_place)
-    final_grads = total.astype(f32) / full_rows
-    return (sample_grad, final_grads[None])
+    thin = array((tok_rows, latent_width), bf16)
+    with jax.named_scope("critic_tail"):
+        *grad_heads, critic_inverse, term_rows, target, direct = run(
+            functools.partial(critic_tail_kernel, count),
+            head_blocks + [inverse_shape, thin, small, small],
+            (timesteps, late_mod, pair, noise, w_embed, final_w, *critic_mixed, *heads_w),
+            [SMEM] + [VMEM] * (5 + 2 * count),
+            4 * tok_rows * model_width * head_width * count,
+            scratch=(pltpu.VMEM((tok_rows, latent_width), bf16), work, work),
+        )
+    with jax.named_scope("grad_heads"):
+        grad_blocks = scatter_near(grad_heads, "seq", count)
+    with jax.named_scope("fake"):
+        fake = lax.ppermute(term_rows, "segment", swaps(sections, 1))
+    with jax.named_scope("real"):
+        real = lax.ppermute(term_rows, "segment", swaps(sections, 2))
+    with jax.named_scope("judge_back"):
+        parts = run(
+            functools.partial(judge_back_kernel, count),
+            [array((tok_rows + 32, latent_width), bf16)] * count,
+            (
+                short,
+                w_embed,
+                qk_gain,
+                proj,
+                inverse,
+                keys,
+                values,
+                pair,
+                real,
+                *critic_rows,
+                *grad_blocks,
+            ),
+            [VMEM] * (9 + 2 * count),
+            10 * full_rows * full_rows * head_width,
+            scratch=(pltpu.VMEM((full_rows, head_width), f32),) * 3,
+        )
+    with jax.named_scope("grad_rows"):
+        parts = scatter_near(parts, "seq", count)
+    with jax.named_scope("merge"):
+        (payload,) = run(
+            functools.partial(merge_kernel, count),
+            [thin],
+            (timesteps, direct, real, fake, *parts),
+            [SMEM] + [VMEM] * (3 + count),
+            1000,
+        )
+    with jax.named_scope("to_student"):
+        to_student = lax.ppermute(
+            payload, "segment", [(place, sections - 1 - place) for place in range(sections)]
+        )
+    with jax.named_scope("outer"):
+        (sums,) = run(
+            functools.partial(outer_kernel, count),
+            [array((count + 1, latent_width, 128), bf16)],
+            (
+                timesteps,
+                to_student,
+                target,
+                noisy_student,
+                pair,
+                student_inverse,
+                critic_inverse,
+                *student_mixed,
+                *critic_mixed,
+            ),
+            [SMEM] + [VMEM] * (6 + 2 * count),
+            2 * tok_rows * latent_width * head_width * (count + 1),
+        )
+    last = count // 2
+    bit = 1
+    while bit < last:
+        with jax.named_scope("sums_near"):
+            moved = lax.ppermute(sums, "seq", swaps(count, bit))
+        sums = (sums.astype(f32) + moved.astype(f32)).astype(bf16)
+        bit *= 2
+    sums_all = []
+    for group in range(groups):
+        for offset in (0, last):
+            moves = [
+                (place * groups + batch, (place ^ offset) * groups + (batch ^ group))
+                for place in range(count)
+                for batch in range(groups)
+            ]
+            with jax.named_scope("sums_far"):
+                sums_all.append(
+                    sums
+                    if offset == group == 0
+                    else lax.ppermute(sums, ("seq", "dp"), moves)
+                )
+    with jax.named_scope("to_second"):
+        to_second = lax.ppermute(payload, "segment", swaps(sections, 1))
+    with jax.named_scope("to_third"):
+        to_third = lax.ppermute(payload, "segment", swaps(sections, 2))
+    with jax.named_scope("expand"):
+        grad_t, total_t = run(
+            functools.partial(expand_kernel, count, groups, full_rows),
+            [array((latent_width, tok_rows), f32), array((latent_width, model_width), f32)],
+            (
+                payload,
+                to_student,
+                to_second,
+                to_third,
+                w_embed,
+                *heads_w,
+                *late_mods,
+                *sums_all,
+            ),
+            [VMEM] * (5 + count + 3 * groups),
+            4 * groups * latent_width * model_width * head_width * count,
+            scratch=(
+                pltpu.VMEM((groups * latent_width, model_width), f32),
+                pltpu.VMEM((count + 1, groups * latent_width, 128), f32),
+            ),
+        )
+    return (jnp.transpose(grad_t)[None], jnp.transpose(total_t)[None])
 
 
 def solution(mesh):

time: 147 us -> 119 us (0.81)
  local copies, waits for them, and re-layouts: 15 us -> 2.38 us
  Pallas kernels: 34.2 us -> 22.2 us
  starting transfers between devices: 35.1 us -> 46 us
  waiting for transfers between devices: 56 us -> 45.5 us
  other arithmetic: 4.98 us -> 2.05 us
    pallas_call x8 -> x9, Pallas kernels: 34.2 us -> 22.2 us  [run(): pl.pallas_call(kernel, out_shape=outputs, in_specs=specs, out_specs=[VMEM...]
    ppermute x11 -> x12, waiting for transfers between devices: 24.1 us -> 13.3 us  [the longest x1 3.43 us: shards(): to_third = lax.ppermute(payload, 'segment', swaps(sections, 2))]
    unnamed x63 -> x58, local copies, waits for them, and re-layouts: 11.2 us -> 2.28 us
    ppermute x11 -> x12, starting transfers between devices: 18.8 us -> 27.3 us  [the longest x1 7.78 us: shards(): lax.ppermute(payload, 'segment', [(place, sections - 1 - place) for place...]
    ppermute x9 -> x10, waiting for transfers between devices: 2.73 us -> 8.66 us  [gather_near(): lax.ppermute(value, axis, swaps(count, offset))]
    ppermute x12, waiting for transfers between devices: 11 us -> 5.78 us  [scatter_near(): lax.ppermute(blocks[offset], axis, swaps(count, offset))]
    another operation x1 -> x0, local copies, waits for them, and re-layouts: 2.5 us -> none  [shards(): flat_head_w = w_qkv[0, :, 0].reshape(model_width, 3 * head_width)]
    select_n x5 -> x1, other arithmetic: 2.85 us -> 0.79 us  [shards(): pair = jnp.where(section == 0, pair, held)]
  transfers between devices with their start and end apart: 34 -> 36, of which waited for: 21 -> 17; matrix products, arithmetic and copies ran while one was open for 7% -> 0% of each run, Pallas kernels for 4% -> 11%
where the time goes in v3:
time: 119 us
  starting transfers between devices  46 us (39%)
  waiting for transfers between devices  45.5 us (38%)
  Pallas kernels  22.2 us (19%)
  local copies, waits for them, and re-layouts  2.38 us (2%)
  other arithmetic  2.05 us (2%)
    pallas_call x9, Pallas kernels, run(): pl.pallas_call(kernel, out_shape=outputs, in_specs=specs, out_specs=[VMEM...  22.2 us
    ppermute x2, waiting for transfers between devices, gather_doubling(): moved = lax.ppermute(joined, axis, swaps(count, bit))  17.8 us
    ppermute x10, waiting for transfers between devices, gather_near(): lax.ppermute(value, axis, swaps(count, offset))  8.66 us
    ppermute x1, starting transfers between devices, shards(): lax.ppermute(payload, 'segment', [(place, sections - 1 - place) for place...  7.78 us
    ppermute x10, starting transfers between devices, gather_near(): lax.ppermute(value, axis, swaps(count, offset))  7.76 us
    ppermute x12, starting transfers between devices, scatter_near(): lax.ppermute(blocks[offset], axis, swaps(count, offset))  7.73 us
    ppermute x1, starting transfers between devices, shards(): real = lax.ppermute(term_rows, 'segment', swaps(sections, 2))  6.19 us
    ppermute x12, waiting for transfers between devices, scatter_near(): lax.ppermute(blocks[offset], axis, swaps(count, offset))  5.78 us
  transfers between devices with their start and end apart: 36, of which 17 were waited for; matrix products, arithmetic and copies ran while one was open for 0% of the time, Pallas kernels for 11%

profile of v3, /device:TPU:0, one launch (start us, length us, event | category | flops | bytes accessed | tf_op | source)
XLA Modules:
  0.0 119.2 jit_solution(16416171140487617011)
XLA Ops:
  0.6 0.0 copy-start.8
  0.7 3.1 %collective-permute-start.9 = (bf16[128,3072]{1,0:T(8,128)(2,1)}, bf16[128,3072]{1,0:T(8,128)(2,1)S(1)}, u32[]{:S(2)}, u32[]{:S(2)}) collective-permute-start(bf16[128,3072]{1,0:T(8,128)(2,1)} %bitcast.17), channel_id=1, source_target_pairs={{0,4},{2,6},{4,0},{6,2},{1,5},{3,7},{5,1},{7,3},{8,12},{10,14},{12... | collective-permute-start | bytes 2359304 | tf_op jit(solution)/shard_map/heads/ppermute | solution.py:54
  3.7 17.8 %collective-permute-done.9.refs_6_.refs_2_ = bf16[128,3072]{1,0:T(8,128)(2,1)S(1)} collective-permute-done((bf16[128,3072]{1,0:T(8,128)(2,1)}, bf16[128,3072]{1,0:T(8,128)(2,1)S(1)}, u32[]{:S(2)}, u32[]{:S(2)}) %collective-permute-start.9) | collective-permute-done | bytes 786464 | tf_op jit(solution)/shard_map/heads/ppermute | solution.py:54
  21.5 1.2 %pad_maximum_fusion = bf16[256,3072]{1,0:T(8,128)(2,1)S(1)} fusion(bf16[128,3072]{1,0:T(8,128)(2,1)S(1)} %collective-permute-done.9.refs_6_.refs_2_, bf16[128,3072]{1,0:T(8,128)(2,1)} %bitcast.18), kind=kLoop, calls=%fused_computation | loop fusion | flops 3145728 | bytes 3145728 | tf_op jit(solution)/shard_map/heads/concatenate | solution.py:53
  22.7 0.1 collective-permute-start.10
  22.9 0.0 copy-start.1
  22.9 9.5 %conditioning.1 = (f32[1,3840]{1,0:T(1,128)S(1)}, bf16[128,64]{1,0:T(8,128)(2,1)S(1)}) custom-call(s32[2,2]{1,0:T(2,128)S(1)} %copy-done.25, f32[1,256]{1,0:T(1,128)S(1)} %copy-done.28, bf16[1,256,3072]{2,1,0:T(8,128)(2,1)S(1)} %copy-done.3, bf16[64,128]{1,0:T(8,128)(2,1)S(1)} %bitcast.30, bf16[1,128,128]{2,1,0:T(8,128)(2,1)S(1)} %copy-done.8, ...), custom_call_target="tpu_custom_call" | custom-call | flops 23592960 | bytes 25247760 | tf_op jit(solution)/shard_map/conditioning/pallas_call | solution.py:126
  32.4 0.5 collective-permute-start
  33.0 1.7 %collective-permute-start.1 = (f32[1,3840]{1,0:T(1,128)S(1)}, f32[1,3840]{1,0:T(1,128)S(1)}, u32[]{:S(2)}, u32[]{:S(2)}) collective-permute-start(f32[1,3840]{1,0:T(1,128)S(1)} %get-tuple-element.34.refs_0_), channel_id=1, source_target_pairs={{0,4},{2,6},{4,0},{6,2},{1,5},{3,7},{5,1},{7,3},{8,12},{10,14},{12... | collective-permute-start | bytes 46088 | tf_op jit(solution)/shard_map/modulation/ppermute | solution.py:38
  34.7 0.3 collective-permute-start.4
  35.0 1.6 %collective-permute-start.5 = (bf16[128,64]{1,0:T(8,128)(2,1)S(1)}, bf16[128,64]{1,0:T(8,128)(2,1)S(1)}, u32[]{:S(2)}, u32[]{:S(2)}) collective-permute-start(bf16[128,64]{1,0:T(8,128)(2,1)S(1)} %get-tuple-element.35.refs_4_.latent.student_rows), channel_id=1, source_target_pairs={{0,6},{2,4},{4,2},{6,0},{1,7},{3,5},{5,3},{7,1},{8,14},{10,12},{12... | collective-permute-start | bytes 49160 | tf_op jit(solution)/shard_map/student_rows/ppermute | solution.py:38
  36.6 0.1 collective-permute-done.1.refs_2_
  36.7 0.3 collective-permute-start.2
  37.0 2.9 %collective-permute-done.2.refs_3_ = f32[1,3840]{1,0:T(1,128)S(1)} collective-permute-done((f32[1,3840]{1,0:T(1,128)S(1)}, f32[1,3840]{1,0:T(1,128)S(1)}, u32[]{:S(2)}, u32[]{:S(2)}) %collective-permute-start.2) | collective-permute-done | bytes 15392 | tf_op jit(solution)/shard_map/modulation/ppermute | solution.py:38
  39.9 3.6 %student_front.1 = (bf16[128,128]{1,0:T(8,128)(2,1)S(1)}, bf16[128,128]{1,0:T(8,128)(2,1)S(1)}, bf16[128,128]{1,0:T(8,128)(2,1)S(1)}, bf16[128,128]{1,0:T(8,128)...) custom-call(bf16[1,64,3072]{2,1,0:T(8,128)(2,1)S(1)} %copy-done.1, bf16[3,3072,128]{2,1,0:T(8,128)(2,1)S(1)} %bitcast.22, ...), custom_call_target="tpu_custom_call" | custom-call | flops 301989888 | bytes 3171328 | tf_op jit(solution)/shard_map/student_front/pallas_call | solution.py:126
  43.5 0.6 copy-done.20
  44.2 0.3 collective-permute-start.6
  44.4 1.6 %collective-permute-start.7 = (bf16[128,128]{1,0:T(8,128)(2,1)S(1)}, bf16[128,128]{1,0:T(8,128)(2,1)S(1)}, u32[]{:S(2)}, u32[]{:S(2)}) collective-permute-start(bf16[128,128]{1,0:T(8,128)(2,1)S(1)} %get-tuple-element.39), channel_id=1, source_target_pairs={{0,4},{2,6},{4,0},{6,2},{1,5},{3,7},{5,1},{7,3},{8,12},{10,14},{12... | collective-permute-start | bytes 98312 | tf_op jit(solution)/shard_map/student_heads/ppermute | solution.py:44
  46.1 0.1 collective-permute-start.8
  46.2 0.1 fusion
  46.3 2.0 %collective-permute-done.7.refs_2_ = bf16[128,128]{1,0:T(8,128)(2,1)S(1)} collective-permute-done((bf16[128,128]{1,0:T(8,128)(2,1)S(1)}, bf16[128,128]{1,0:T(8,128)(2,1)S(1)}, u32[]{:S(2)}, u32[]{:S(2)}) %collective-permute-start.7) | collective-permute-done | bytes 32800 | tf_op jit(solution)/shard_map/student_heads/ppermute | solution.py:44
  48.3 1.1 collective-permute-done.8.refs_3_
  49.4 3.4 %student_tail.1 = (bf16[128,128]{1,0:T(8,128)(2,1)}, f32[128,128]{1,0:T(8,128)S(1)}) custom-call(s32[2,2]{1,0:T(2,128)S(1)} %copy-done.25, f32[1,9216]{1,0:T(1,128)S(1)} %get-tuple-element.36.mod.refs_4_, bf16[128,64]{1,0:T(8,128)(2,1)S(1)} %get-tuple-element.35.refs_4_.latent.student_rows, bf16[1,128,128]{2,1,0:T(8,128)(2,1)S(1)} %copy-done.8, ...), custom_call_target="tpu_custom_call" | custom-call | flops 402653184 | bytes 4247568 | tf_op jit(solution)/shard_map/student_tail/pallas_call | solution.py:126
  52.9 0.6 copy-done.23
  53.5 3.8 %collective-permute-start.13 = (bf16[128,128]{1,0:T(8,128)(2,1)}, bf16[128,128]{1,0:T(8,128)(2,1)}, u32[]{:S(2)}, u32[]{:S(2)}) collective-permute-start(bf16[128,128]{1,0:T(8,128)(2,1)} %get-tuple-element.41), channel_id=1, source_target_pairs={{0,24},{8,0},{16,8},{24,16},{1,25},{9,1},{17,9},{25,17},{2,26},{10... | collective-permute-start | bytes 98312 | tf_op jit(solution)/shard_map/sample/ppermute | solution.py:681
  57.3 2.5 %collective-permute-done.11 = bf16[128,128]{1,0:T(8,128)(2,1)} collective-permute-done((bf16[128,128]{1,0:T(8,128)(2,1)}, bf16[128,128]{1,0:T(8,128)(2,1)}, u32[]{:S(2)}, u32[]{:S(2)}) %collective-permute-start.11) | collective-permute-done | bytes 32800 | tf_op jit(solution)/shard_map/sample/ppermute | solution.py:681
  59.8 0.3 collective-permute-done.13
  60.2 0.8 select_select_fusion.pair
  61.0 0.1 collective-permute-start.14
  61.1 0.8 collective-permute-start.15
  61.9 1.0 collective-permute-start.16
  62.9 2.3 %collective-permute-done.15.refs_2_ = bf16[128,64]{1,0:T(8,128)(2,1)S(1)} collective-permute-done((bf16[128,64]{1,0:T(8,128)(2,1)S(1)}, bf16[128,64]{1,0:T(8,128)(2,1)S(1)}, u32[]{:S(2)}, u32[]{:S(2)}) %collective-permute-start.15) | collective-permute-done | bytes 16416 | tf_op jit(solution)/shard_map/critic_rows/ppermute | solution.py:38
  65.2 0.4 collective-permute-done.16.refs_3_
  65.6 0.9 copy-done.21
  66.5 0.1 collective-permute-start.17
  66.6 1.0 collective-permute-start.18
  67.6 0.8 collective-permute-start.19
  68.3 2.2 %collective-permute-done.18.refs_2_.refs_6_ = bf16[128,128]{1,0:T(8,128)(2,1)S(1)} collective-permute-done((bf16[128,128]{1,0:T(8,128)(2,1)S(1)}, bf16[128,128]{1,0:T(8,128)(2,1)S(1)}, u32[]{:S(2)}, u32[]{:S(2)}) %collective-permute-start.18) | collective-permute-done | bytes 32800 | tf_op jit(solution)/shard_map/critic_heads/ppermute | solution.py:44
  70.5 0.5 collective-permute-done.19.refs_3_.refs_7_
  71.0 0.6 critic_tail.1
  71.7 0.2 collective-permute-start.22
  71.8 1.0 collective-permute-start.23
  72.8 0.7 collective-permute-start.24
  73.6 6.2 %collective-permute-start.20 = (bf16[128,64]{1,0:T(8,128)(2,1)S(1)}, bf16[128,64]{1,0:T(8,128)(2,1)S(1)}, u32[]{:S(2)}, u32[]{:S(2)}) collective-permute-start(bf16[128,64]{1,0:T(8,128)(2,1)S(1)} %get-tuple-element.48), channel_id=1, source_target_pairs={{0,16},{8,24},{16,0},{24,8},{1,17},{9,25},{17,1},{25,9},{2,18},{10... | collective-permute-start | bytes 49160 | tf_op jit(solution)/shard_map/real/ppermute | solution.py:716
  79.8 1.9 %collective-permute-done.20.real = bf16[128,64]{1,0:T(8,128)(2,1)S(1)} collective-permute-done((bf16[128,64]{1,0:T(8,128)(2,1)S(1)}, bf16[128,64]{1,0:T(8,128)(2,1)S(1)}, u32[]{:S(2)}, u32[]{:S(2)}) %collective-permute-start.20) | collective-permute-done | bytes 16416 | tf_op jit(solution)/shard_map/real/ppermute | solution.py:716
  81.8 0.1 collective-permute-start.25
  81.9 1.0 collective-permute-start.26
  82.9 0.8 collective-permute-start.27
  83.7 4.5 %collective-permute-start.21 = (bf16[128,64]{1,0:T(8,128)(2,1)S(1)}, bf16[128,64]{1,0:T(8,128)(2,1)S(1)}, u32[]{:S(2)}, u32[]{:S(2)}) collective-permute-start(bf16[128,64]{1,0:T(8,128)(2,1)S(1)} %get-tuple-element.48), channel_id=1, source_target_pairs={{0,8},{8,0},{16,24},{24,16},{1,9},{9,1},{17,25},{25,17},{2,10},{10... | collective-permute-start | bytes 49160 | tf_op jit(solution)/shard_map/fake/ppermute | solution.py:714
  88.2 1.9 %collective-permute-done.21.fake = bf16[128,64]{1,0:T(8,128)(2,1)S(1)} collective-permute-done((bf16[128,64]{1,0:T(8,128)(2,1)S(1)}, bf16[128,64]{1,0:T(8,128)(2,1)S(1)}, u32[]{:S(2)}, u32[]{:S(2)}) %collective-permute-start.21) | collective-permute-done | bytes 16416 | tf_op jit(solution)/shard_map/fake/ppermute | solution.py:714
  90.2 0.6 merge.1.own
  90.7 7.8 %collective-permute-start.28 = (bf16[128,64]{1,0:T(8,128)(2,1)S(1)}, bf16[128,64]{1,0:T(8,128)(2,1)S(1)}, u32[]{:S(2)}, u32[]{:S(2)}) collective-permute-start(bf16[128,64]{1,0:T(8,128)(2,1)S(1)} %merge.1.own), channel_id=1, source_target_pairs={{0,24},{8,16},{16,8},{24,0},{1,25},{9,17},{17,9},{25,1},{2,26},{10... | collective-permute-start | bytes 49160 | tf_op jit(solution)/shard_map/to_student/ppermute | solution.py:749
  98.5 1.9 %collective-permute-done.28.arrived.from_first = bf16[128,64]{1,0:T(8,128)(2,1)S(1)} collective-permute-done((bf16[128,64]{1,0:T(8,128)(2,1)S(1)}, bf16[128,64]{1,0:T(8,128)(2,1)S(1)}, u32[]{:S(2)}, u32[]{:S(2)}) %collective-permute-start.28) | collective-permute-done | bytes 16416 | tf_op jit(solution)/shard_map/to_student/ppermute | solution.py:749
  100.5 0.9 outer.1
  101.4 0.1 collective-permute-start.32
  101.5 1.3 %collective-permute-done.32 = bf16[5,64,128]{2,1,0:T(8,128)(2,1)S(1)} collective-permute-done((bf16[5,64,128]{2,1,0:T(8,128)(2,1)S(1)}, bf16[5,64,128]{2,1,0:T(8,128)(2,1)S(1)}, u32[]{:S(2)}, u32[]{:S(2)}) %collective-permute-start.32) | collective-permute-done | bytes 81952 | tf_op jit(solution)/shard_map/sums_near/ppermute | solution.py:774
  102.7 1.0 collective-permute-start.33
  103.8 1.4 %collective-permute-start.34 = (bf16[5,64,128]{2,1,0:T(8,128)(2,1)S(1)}, bf16[5,64,128]{2,1,0:T(8,128)(2,1)S(1)}, u32[]{:S(2)}, u32[]{:S(2)}) collective-permute-start(bf16[5,64,128]{2,1,0:T(8,128)(2,1)S(1)} %add_convert_fusion.refs_6_), channel_id=1, source_target_pairs={{0,1},{1,0},{2,3},{3,2},{4,5},{5,4},{6,7},{7,6},{8,9},{9,8},{10,11... | collective-permute-start | bytes 245768 | tf_op jit(solution)/shard_map/sums_far/ppermute | solution.py:789
  105.2 1.1 collective-permute-start.35
  106.3 1.4 %collective-permute-start.31 = (f32[1,9216]{1,0:T(1,128)S(1)}, f32[1,9216]{1,0:T(1,128)S(1)}, u32[]{:S(2)}, u32[]{:S(2)}) collective-permute-start(f32[1,9216]{1,0:T(1,128)S(1)} %copy-done.7), channel_id=1, source_target_pairs={{0,1},{1,0},{2,3},{3,2},{4,5},{5,4},{6,7},{7,6},{8,9},{9,8},{10,11... | collective-permute-start | bytes 110600 | tf_op jit(solution)/shard_map/other_mod/ppermute | solution.py:38
  107.7 3.0 %collective-permute-done.31.refs_5_ = f32[1,9216]{1,0:T(1,128)S(1)} collective-permute-done((f32[1,9216]{1,0:T(1,128)S(1)}, f32[1,9216]{1,0:T(1,128)S(1)}, u32[]{:S(2)}, u32[]{:S(2)}) %collective-permute-start.31) | collective-permute-done | bytes 36896 | tf_op jit(solution)/shard_map/other_mod/ppermute | solution.py:38
  110.7 1.4 %collective-permute-start.30 = (bf16[128,64]{1,0:T(8,128)(2,1)S(1)}, bf16[128,64]{1,0:T(8,128)(2,1)S(1)}, u32[]{:S(2)}, u32[]{:S(2)}) collective-permute-start(bf16[128,64]{1,0:T(8,128)(2,1)S(1)} %merge.1.own), channel_id=1, source_target_pairs={{0,16},{8,24},{16,0},{24,8},{1,17},{9,25},{17,1},{25,9},{2,18},{10... | collective-permute-start | bytes 49160 | tf_op jit(solution)/shard_map/to_third/ppermute | solution.py:794
  112.1 3.4 %collective-permute-done.30.from_third = bf16[128,64]{1,0:T(8,128)(2,1)S(1)} collective-permute-done((bf16[128,64]{1,0:T(8,128)(2,1)S(1)}, bf16[128,64]{1,0:T(8,128)(2,1)S(1)}, u32[]{:S(2)}, u32[]{:S(2)}) %collective-permute-start.30) | collective-permute-done | bytes 16416 | tf_op jit(solution)/shard_map/to_third/ppermute | solution.py:794
  115.6 3.6 %expand.1 = (f32[64,128]{1,0:T(8,128)}, f32[64,3072]{1,0:T(8,128)}) custom-call(bf16[128,64]{1,0:T(8,128)(2,1)S(1)} %merge.1.own, bf16[128,64]{1,0:T(8,128)(2,1)S(1)} %collective-permute-done.28.arrived.from_first, bf16[128,64]{1,0:T(8,128)(2,1)S(1)} %collective-permute-done.29.from_second, bf16[128,64]{1,0:T(8,128)(2,1)S(1)} %collective-permute-done.30.from_third, ...), custom_call_target="tpu_custom_call" | custom-call | flops 805306368 | bytes 4825088 | tf_op jit(solution)/shard_map/expand/pallas_call | solution.py:126
  (79 shorter events, 0.2 us)
Async XLA Ops:
  0.6 22.2 %copy-start.3 = (bf16[1,256,3072]{2,1,0:T(8,128)(2,1)S(1)}, bf16[1,256,3072]{2,1,0:T(8,128)(2,1)}, u32[]{:S(2)}) copy-start(bf16[1,256,3072]{2,1,0:T(8,128)(2,1)} %time_w.1) | copy-start | bytes 4718596
  0.6 22.2 %copy-start.8 = (bf16[1,128,128]{2,1,0:T(8,128)(2,1)S(1)}, bf16[1,128,128]{2,1,0:T(8,128)(2,1)}, u32[]{:S(2)}) copy-start(bf16[1,128,128]{2,1,0:T(8,128)(2,1)} %noise.5) | copy-start | bytes 98308
  0.7 22.2 %copy-start.25 = (s32[2,2]{1,0:T(2,128)S(1)}, s32[2,2]{1,0:T(2,128)}, u32[]{:S(2)}) copy-start(s32[2,2]{1,0:T(2,128)} %times.9) | copy-start | bytes 52
  0.7 22.2 %copy-start.26 = (bf16[1,128,64]{1,2,0:T(8,128)(2,1)S(1)}, bf16[1,128,64]{1,2,0:T(8,128)(2,1)}, u32[]{:S(2)}) copy-start(bf16[1,128,64]{1,2,0:T(8,128)(2,1)} %param.11) | copy-start | bytes 49156
  0.7 22.2 %copy-start.28 = (f32[1,256]{1,0:T(1,128)S(1)}, f32[1,256]{1,0:T(1,128)}, u32[]{:S(2)}) copy-start(f32[1,256]{1,0:T(1,128)} %text.1) | copy-start | bytes 3076
  0.7 20.8 %collective-permute-start.9 = (bf16[128,3072]{1,0:T(8,128)(2,1)}, bf16[128,3072]{1,0:T(8,128)(2,1)S(1)}, u32[]{:S(2)}, u32[]{:S(2)}) collective-permute-start(bf16[128,3072]{1,0:T(8,128)(2,1)} %bitcast.17), channel_id=1, source_target_pairs={{0,4},{2,6},{4,0},{6,2},{1,5},{3,7},{5,1},{7,3},{8,12},{10,14},{12... | collective-permute-start | bytes 2359304 | tf_op jit(solution)/shard_map/heads/ppermute | solution.py:54
  22.7 23.5 %collective-permute-start.10 = (bf16[256,3072]{1,0:T(8,128)(2,1)S(1)}, bf16[256,3072]{1,0:T(8,128)(2,1)S(1)}, u32[]{:S(2)}, u32[]{:S(2)}) collective-permute-start(bf16[256,3072]{1,0:T(8,128)(2,1)S(1)} %pad_maximum_fusion), channel_id=1, source_target_pairs={{0,2},{2,0},{4,6},{6,4},{1,3},{3,1},{5,7},{7,5},{8,10},{10,8},{12,... | collective-permute-start | bytes 4718600 | tf_op jit(solution)/shard_map/heads/ppermute | solution.py:54
  22.9 17.0 %copy-start.1 = (bf16[1,64,3072]{2,1,0:T(8,128)(2,1)S(1)}, bf16[1,64,3072]{2,1,0:T(8,128)(2,1)}, u32[]{:S(2)}) copy-start(bf16[1,64,3072]{2,1,0:T(8,128)(2,1)} %embed_w.11) | copy-start | bytes 1179652
  22.9 17.0 %copy-start.2 = (bf16[1,3072,1,3,128]{4,1,3,2,0:T(8,128)(2,1)S(1)}, bf16[1,3072,1,3,128]{4,1,3,2,0:T(8,128)(2,1)}, u32[]{:S(2)}) copy-start(bf16[1,3072,1,3,128]{4,1,3,2,0:T(8,128)(2,1)} %param.18) | copy-start | bytes 7077892
  22.9 17.0 %copy-start.27 = (f32[1,2,128]{2,1,0:T(2,128)S(1)}, f32[1,2,128]{2,1,0:T(2,128)}, u32[]{:S(2)}) copy-start(f32[1,2,128]{2,1,0:T(2,128)} %gains.5) | copy-start | bytes 3076
  32.4 17.0 %copy-start.10 = (bf16[128,64]{1,0:T(8,128)(2,1)}, bf16[128,64]{1,0:T(8,128)(2,1)S(1)}, u32[]{:S(2)}) copy-start(bf16[128,64]{1,0:T(8,128)(2,1)S(1)} %get-tuple-element.35.refs_4_.latent.student_rows) | copy-start | bytes 49156
  32.4 2.6 %collective-permute-start = (f32[1,3840]{1,0:T(1,128)S(1)}, f32[1,3840]{1,0:T(1,128)S(1)}, u32[]{:S(2)}, u32[]{:S(2)}) collective-permute-start(f32[1,3840]{1,0:T(1,128)S(1)} %get-tuple-element.34.refs_0_), channel_id=1, source_target_pairs={{0,2},{2,0},{4,6},{6,4},{1,3},{3,1},{5,7},{7,5},{8,10},{10,8},{12,... | collective-permute-start | bytes 46088 | tf_op jit(solution)/shard_map/modulation/ppermute | solution.py:38
  33.0 3.7 %collective-permute-start.1 = (f32[1,3840]{1,0:T(1,128)S(1)}, f32[1,3840]{1,0:T(1,128)S(1)}, u32[]{:S(2)}, u32[]{:S(2)}) collective-permute-start(f32[1,3840]{1,0:T(1,128)S(1)} %get-tuple-element.34.refs_0_), channel_id=1, source_target_pairs={{0,4},{2,6},{4,0},{6,2},{1,5},{3,7},{5,1},{7,3},{8,12},{10,14},{12... | collective-permute-start | bytes 46088 | tf_op jit(solution)/shard_map/modulation/ppermute | solution.py:38
  34.7 5.1 %collective-permute-start.3 = (bf16[128,64]{1,0:T(8,128)(2,1)S(1)}, bf16[128,64]{1,0:T(8,128)(2,1)S(1)}, u32[]{:S(2)}, u32[]{:S(2)}) collective-permute-start(bf16[128,64]{1,0:T(8,128)(2,1)S(1)} %get-tuple-element.35.refs_4_.latent.student_rows), channel_id=1, source_target_pairs={{0,2},{2,0},{4,6},{6,4},{1,3},{3,1},{5,7},{7,5},{8,10},{10,8},{12,... | collective-permute-start | bytes 49160 | tf_op jit(solution)/shard_map/student_rows/ppermute | solution.py:38
  34.7 5.1 %collective-permute-start.4 = (bf16[128,64]{1,0:T(8,128)(2,1)S(1)}, bf16[128,64]{1,0:T(8,128)(2,1)S(1)}, u32[]{:S(2)}, u32[]{:S(2)}) collective-permute-start(bf16[128,64]{1,0:T(8,128)(2,1)S(1)} %get-tuple-element.35.refs_4_.latent.student_rows), channel_id=1, source_target_pairs={{0,4},{2,6},{4,0},{6,2},{1,5},{3,7},{5,1},{7,3},{8,12},{10,14},{12... | collective-permute-start | bytes 49160 | tf_op jit(solution)/shard_map/student_rows/ppermute | solution.py:38
  35.0 4.9 %collective-permute-start.5 = (bf16[128,64]{1,0:T(8,128)(2,1)S(1)}, bf16[128,64]{1,0:T(8,128)(2,1)S(1)}, u32[]{:S(2)}, u32[]{:S(2)}) collective-permute-start(bf16[128,64]{1,0:T(8,128)(2,1)S(1)} %get-tuple-element.35.refs_4_.latent.student_rows), channel_id=1, source_target_pairs={{0,6},{2,4},{4,2},{6,0},{1,7},{3,5},{5,3},{7,1},{8,14},{10,12},{12... | collective-permute-start | bytes 49160 | tf_op jit(solution)/shard_map/student_rows/ppermute | solution.py:38
  36.7 3.2 %collective-permute-start.2 = (f32[1,3840]{1,0:T(1,128)S(1)}, f32[1,3840]{1,0:T(1,128)S(1)}, u32[]{:S(2)}, u32[]{:S(2)}) collective-permute-start(f32[1,3840]{1,0:T(1,128)S(1)} %get-tuple-element.34.refs_0_), channel_id=1, source_target_pairs={{0,6},{2,4},{4,2},{6,0},{1,7},{3,5},{5,3},{7,1},{8,14},{10,12},{12... | collective-permute-start | bytes 46088 | tf_op jit(solution)/shard_map/modulation/ppermute | solution.py:38
  43.5 0.7 copy-start.20
  44.2 5.3 %copy-start.6 = (f32[1,9216]{1,0:T(1,128)}, f32[1,9216]{1,0:T(1,128)S(1)}, u32[]{:S(2)}) copy-start(f32[1,9216]{1,0:T(1,128)S(1)} %get-tuple-element.36.mod.refs_4_) | copy-start | bytes 110596
  44.2 5.3 %copy-start.12 = (bf16[128,128]{1,0:T(8,128)(2,1)}, bf16[128,128]{1,0:T(8,128)(2,1)S(1)}, u32[]{:S(2)}) copy-start(bf16[128,128]{1,0:T(8,128)(2,1)S(1)} %get-tuple-element.37.refs_0_) | copy-start | bytes 98308
  44.2 2.1 %collective-permute-start.6 = (bf16[128,128]{1,0:T(8,128)(2,1)S(1)}, bf16[128,128]{1,0:T(8,128)(2,1)S(1)}, u32[]{:S(2)}, u32[]{:S(2)}) collective-permute-start(bf16[128,128]{1,0:T(8,128)(2,1)S(1)} %get-tuple-element.38), channel_id=1, source_target_pairs={{0,2},{2,0},{4,6},{6,4},{1,3},{3,1},{5,7},{7,5},{8,10},{10,8},{12,... | collective-permute-start | bytes 98312 | tf_op jit(solution)/shard_map/student_heads/ppermute | solution.py:44
  44.4 3.9 %collective-permute-start.7 = (bf16[128,128]{1,0:T(8,128)(2,1)S(1)}, bf16[128,128]{1,0:T(8,128)(2,1)S(1)}, u32[]{:S(2)}, u32[]{:S(2)}) collective-permute-start(bf16[128,128]{1,0:T(8,128)(2,1)S(1)} %get-tuple-element.39), channel_id=1, source_target_pairs={{0,4},{2,6},{4,0},{6,2},{1,5},{3,7},{5,1},{7,3},{8,12},{10,14},{12... | collective-permute-start | bytes 98312 | tf_op jit(solution)/shard_map/student_heads/ppermute | solution.py:44
  46.1 3.4 %copy-start = (bf16[1,1,128,3072]{3,2,1,0:T(8,128)(2,1)S(1)}, bf16[1,1,128,3072]{3,2,1,0:T(8,128)(2,1)}, u32[]{:S(2)}) copy-start(bf16[1,1,128,3072]{3,2,1,0:T(8,128)(2,1)} %param.19) | copy-start | bytes 2359300
  46.1 3.4 %copy-start.4 = (bf16[1,3072,64]{1,2,0:T(8,128)(2,1)S(1)}, bf16[1,3072,64]{1,2,0:T(8,128)(2,1)}, u32[]{:S(2)}) copy-start(bf16[1,3072,64]{1,2,0:T(8,128)(2,1)} %param.21) | copy-start | bytes 1179652
  46.1 3.3 %collective-permute-start.8 = (bf16[128,128]{1,0:T(8,128)(2,1)S(1)}, bf16[128,128]{1,0:T(8,128)(2,1)S(1)}, u32[]{:S(2)}, u32[]{:S(2)}) collective-permute-start(bf16[128,128]{1,0:T(8,128)(2,1)S(1)} %get-tuple-element.40), channel_id=1, source_target_pairs={{0,6},{2,4},{4,2},{6,0},{1,7},{3,5},{5,3},{7,1},{8,14},{10,12},{12... | collective-permute-start | bytes 98312 | tf_op jit(solution)/shard_map/student_heads/ppermute | solution.py:44
  46.3 6.6 %copy-start.14 = (bf16[128,128]{1,0:T(8,128)(2,1)}, bf16[128,128]{1,0:T(8,128)(2,1)S(1)}, u32[]{:S(2)}) copy-start(bf16[128,128]{1,0:T(8,128)(2,1)S(1)} %collective-permute-done.6.refs_1_) | copy-start | bytes 98308
  48.3 4.5 %copy-start.16 = (bf16[128,128]{1,0:T(8,128)(2,1)}, bf16[128,128]{1,0:T(8,128)(2,1)S(1)}, u32[]{:S(2)}) copy-start(bf16[128,128]{1,0:T(8,128)(2,1)S(1)} %collective-permute-done.7.refs_2_) | copy-start | bytes 98308
  49.4 3.5 %copy-start.18 = (bf16[128,128]{1,0:T(8,128)(2,1)}, bf16[128,128]{1,0:T(8,128)(2,1)S(1)}, u32[]{:S(2)}) copy-start(bf16[128,128]{1,0:T(8,128)(2,1)S(1)} %collective-permute-done.8.refs_3_) | copy-start | bytes 98308
  53.5 6.3 %collective-permute-start.11 = (bf16[128,128]{1,0:T(8,128)(2,1)}, bf16[128,128]{1,0:T(8,128)(2,1)}, u32[]{:S(2)}, u32[]{:S(2)}) collective-permute-start(bf16[128,128]{1,0:T(8,128)(2,1)} %get-tuple-element.41), channel_id=1, source_target_pairs={{0,8},{8,16},{16,24},{24,0},{1,9},{9,17},{17,25},{25,1},{2,10},{10... | collective-permute-start | bytes 98312 | tf_op jit(solution)/shard_map/sample/ppermute | solution.py:681
  53.5 6.3 %collective-permute-start.12 = (bf16[128,128]{1,0:T(8,128)(2,1)}, bf16[128,128]{1,0:T(8,128)(2,1)}, u32[]{:S(2)}, u32[]{:S(2)}) collective-permute-start(bf16[128,128]{1,0:T(8,128)(2,1)} %get-tuple-element.41), channel_id=1, source_target_pairs={{0,16},{8,24},{16,0},{24,8},{1,17},{9,25},{17,1},{25,9},{2,18},{10... | collective-permute-start | bytes 98312 | tf_op jit(solution)/shard_map/sample/ppermute | solution.py:681
  53.5 6.7 %collective-permute-start.13 = (bf16[128,128]{1,0:T(8,128)(2,1)}, bf16[128,128]{1,0:T(8,128)(2,1)}, u32[]{:S(2)}, u32[]{:S(2)}) collective-permute-start(bf16[128,128]{1,0:T(8,128)(2,1)} %get-tuple-element.41), channel_id=1, source_target_pairs={{0,24},{8,0},{16,8},{24,16},{1,25},{9,1},{17,9},{25,17},{2,26},{10... | collective-permute-start | bytes 98312 | tf_op jit(solution)/shard_map/sample/ppermute | solution.py:681
  57.3 13.7 %copy-start.5 = (bf16[1,3072,64]{1,2,0:T(8,128)(2,1)S(1)}, bf16[1,3072,64]{1,2,0:T(8,128)(2,1)}, u32[]{:S(2)}) copy-start(bf16[1,3072,64]{1,2,0:T(8,128)(2,1)} %param.21) | copy-start | bytes 1179652
  57.3 13.7 %copy-start.7 = (f32[1,9216]{1,0:T(1,128)S(1)}, f32[1,9216]{1,0:T(1,128)}, u32[]{:S(2)}) copy-start(f32[1,9216]{1,0:T(1,128)} %copy-done.6) | copy-start | bytes 110596
  57.3 13.7 %copy-start.9 = (bf16[1,128,128]{2,1,0:T(8,128)(2,1)S(1)}, bf16[1,128,128]{2,1,0:T(8,128)(2,1)}, u32[]{:S(2)}) copy-start(bf16[1,128,128]{2,1,0:T(8,128)(2,1)} %noise.5) | copy-start | bytes 98308
  61.0 1.9 %collective-permute-start.14 = (bf16[128,64]{1,0:T(8,128)(2,1)S(1)}, bf16[128,64]{1,0:T(8,128)(2,1)S(1)}, u32[]{:S(2)}, u32[]{:S(2)}) collective-permute-start(bf16[128,64]{1,0:T(8,128)(2,1)S(1)} %bitcast.25), channel_id=1, source_target_pairs={{0,2},{2,0},{4,6},{6,4},{1,3},{3,1},{5,7},{7,5},{8,10},{10,8},{12,... | collective-permute-start | bytes 49160 | tf_op jit(solution)/shard_map/critic_rows/ppermute | solution.py:38
  61.1 4.1 %collective-permute-start.15 = (bf16[128,64]{1,0:T(8,128)(2,1)S(1)}, bf16[128,64]{1,0:T(8,128)(2,1)S(1)}, u32[]{:S(2)}, u32[]{:S(2)}) collective-permute-start(bf16[128,64]{1,0:T(8,128)(2,1)S(1)} %bitcast.26), channel_id=1, source_target_pairs={{0,4},{2,6},{4,0},{6,2},{1,5},{3,7},{5,1},{7,3},{8,12},{10,14},{12... | collective-permute-start | bytes 49160 | tf_op jit(solution)/shard_map/critic_rows/ppermute | solution.py:38
  61.9 3.7 %collective-permute-start.16 = (bf16[128,64]{1,0:T(8,128)(2,1)S(1)}, bf16[128,64]{1,0:T(8,128)(2,1)S(1)}, u32[]{:S(2)}, u32[]{:S(2)}) collective-permute-start(bf16[128,64]{1,0:T(8,128)(2,1)S(1)} %bitcast.27), channel_id=1, source_target_pairs={{0,6},{2,4},{4,2},{6,0},{1,7},{3,5},{5,3},{7,1},{8,14},{10,12},{12... | collective-permute-start | bytes 49160 | tf_op jit(solution)/shard_map/critic_rows/ppermute | solution.py:38
  65.6 0.9 copy-start.21
  66.5 1.9 %collective-permute-start.17 = (bf16[128,128]{1,0:T(8,128)(2,1)S(1)}, bf16[128,128]{1,0:T(8,128)(2,1)S(1)}, u32[]{:S(2)}, u32[]{:S(2)}) collective-permute-start(bf16[128,128]{1,0:T(8,128)(2,1)S(1)} %get-tuple-element.44), channel_id=1, source_target_pairs={{0,2},{2,0},{4,6},{6,4},{1,3},{3,1},{5,7},{7,5},{8,10},{10,8},{12,... | collective-permute-start | bytes 98312 | tf_op jit(solution)/shard_map/critic_heads/ppermute | solution.py:44
  66.6 3.9 %collective-permute-start.18 = (bf16[128,128]{1,0:T(8,128)(2,1)S(1)}, bf16[128,128]{1,0:T(8,128)(2,1)S(1)}, u32[]{:S(2)}, u32[]{:S(2)}) collective-permute-start(bf16[128,128]{1,0:T(8,128)(2,1)S(1)} %get-tuple-element.45), channel_id=1, source_target_pairs={{0,4},{2,6},{4,0},{6,2},{1,5},{3,7},{5,1},{7,3},{8,12},{10,14},{12... | collective-permute-start | bytes 98312 | tf_op jit(solution)/shard_map/critic_heads/ppermute | solution.py:44
  67.6 3.4 %collective-permute-start.19 = (bf16[128,128]{1,0:T(8,128)(2,1)S(1)}, bf16[128,128]{1,0:T(8,128)(2,1)S(1)}, u32[]{:S(2)}, u32[]{:S(2)}) collective-permute-start(bf16[128,128]{1,0:T(8,128)(2,1)S(1)} %get-tuple-element.46), channel_id=1, source_target_pairs={{0,6},{2,4},{4,2},{6,0},{1,7},{3,5},{5,3},{7,1},{8,14},{10,12},{12... | collective-permute-start | bytes 98312 | tf_op jit(solution)/shard_map/critic_heads/ppermute | solution.py:44
  71.0 10.7 %copy-start.22 = (f32[80,384]{1,0:T(8,128)S(1)}, f32[80,384]{1,0:T(8,128)}, u32[]{:S(2)}) copy-start(f32[80,384]{1,0:T(8,128)} %copy-done.20) | copy-start | bytes 368644
  71.6 28.8 %copy-start.11 = (bf16[128,64]{1,0:T(8,128)(2,1)S(1)}, bf16[128,64]{1,0:T(8,128)(2,1)}, u32[]{:S(2)}) copy-start(bf16[128,64]{1,0:T(8,128)(2,1)} %copy-done.10) | copy-start | bytes 49156
  71.6 28.8 %copy-start.13 = (bf16[128,128]{1,0:T(8,128)(2,1)S(1)}, bf16[128,128]{1,0:T(8,128)(2,1)}, u32[]{:S(2)}) copy-start(bf16[128,128]{1,0:T(8,128)(2,1)} %copy-done.12) | copy-start | bytes 98308
  71.6 28.8 %copy-start.15 = (bf16[128,128]{1,0:T(8,128)(2,1)S(1)}, bf16[128,128]{1,0:T(8,128)(2,1)}, u32[]{:S(2)}) copy-start(bf16[128,128]{1,0:T(8,128)(2,1)} %copy-done.14) | copy-start | bytes 98308
  71.6 28.8 %copy-start.17 = (bf16[128,128]{1,0:T(8,128)(2,1)S(1)}, bf16[128,128]{1,0:T(8,128)(2,1)}, u32[]{:S(2)}) copy-start(bf16[128,128]{1,0:T(8,128)(2,1)} %copy-done.16) | copy-start | bytes 98308
  71.6 28.8 %copy-start.19 = (bf16[128,128]{1,0:T(8,128)(2,1)S(1)}, bf16[128,128]{1,0:T(8,128)(2,1)}, u32[]{:S(2)}) copy-start(bf16[128,128]{1,0:T(8,128)(2,1)} %copy-done.18) | copy-start | bytes 98308
  71.6 28.8 %copy-start.24 = (f32[128,128]{1,0:T(8,128)S(1)}, f32[128,128]{1,0:T(8,128)}, u32[]{:S(2)}) copy-start(f32[128,128]{1,0:T(8,128)} %copy-done.23) | copy-start | bytes 196612
  71.7 10.1 %collective-permute-start.22 = (bf16[128,128]{1,0:T(8,128)(2,1)S(1)}, bf16[128,128]{1,0:T(8,128)(2,1)S(1)}, u32[]{:S(2)}, u32[]{:S(2)}) collective-permute-start(bf16[128,128]{1,0:T(8,128)(2,1)S(1)} %get-tuple-element.54), channel_id=1, source_target_pairs={{0,2},{2,0},{4,6},{6,4},{1,3},{3,1},{5,7},{7,5},{8,10},{10,8},{12,... | collective-permute-start | bytes 98312 | tf_op jit(solution)/shard_map/grad_heads/ppermute | solution.py:44
  71.8 9.9 %collective-permute-start.23 = (bf16[128,128]{1,0:T(8,128)(2,1)S(1)}, bf16[128,128]{1,0:T(8,128)(2,1)S(1)}, u32[]{:S(2)}, u32[]{:S(2)}) collective-permute-start(bf16[128,128]{1,0:T(8,128)(2,1)S(1)} %get-tuple-element.55), channel_id=1, source_target_pairs={{0,4},{2,6},{4,0},{6,2},{1,5},{3,7},{5,1},{7,3},{8,12},{10,14},{12... | collective-permute-start | bytes 98312 | tf_op jit(solution)/shard_map/grad_heads/ppermute | solution.py:44
  72.8 8.9 %collective-permute-start.24 = (bf16[128,128]{1,0:T(8,128)(2,1)S(1)}, bf16[128,128]{1,0:T(8,128)(2,1)S(1)}, u32[]{:S(2)}, u32[]{:S(2)}) collective-permute-start(bf16[128,128]{1,0:T(8,128)(2,1)S(1)} %get-tuple-element.56), channel_id=1, source_target_pairs={{0,6},{2,4},{4,2},{6,0},{1,7},{3,5},{5,3},{7,1},{8,14},{10,12},{12... | collective-permute-start | bytes 98312 | tf_op jit(solution)/shard_map/grad_heads/ppermute | solution.py:44
  73.6 8.1 %collective-permute-start.20 = (bf16[128,64]{1,0:T(8,128)(2,1)S(1)}, bf16[128,64]{1,0:T(8,128)(2,1)S(1)}, u32[]{:S(2)}, u32[]{:S(2)}) collective-permute-start(bf16[128,64]{1,0:T(8,128)(2,1)S(1)} %get-tuple-element.48), channel_id=1, source_target_pairs={{0,16},{8,24},{16,0},{24,8},{1,17},{9,25},{17,1},{25,9},{2,18},{10... | collective-permute-start | bytes 49160 | tf_op jit(solution)/shard_map/real/ppermute | solution.py:716
  81.8 8.4 %collective-permute-start.25 = (bf16[160,64]{1,0:T(8,128)(2,1)S(1)}, bf16[160,64]{1,0:T(8,128)(2,1)S(1)}, u32[]{:S(2)}, u32[]{:S(2)}) collective-permute-start(bf16[160,64]{1,0:T(8,128)(2,1)S(1)} %get-tuple-element.58), channel_id=1, source_target_pairs={{0,2},{2,0},{4,6},{6,4},{1,3},{3,1},{5,7},{7,5},{8,10},{10,8},{12,... | collective-permute-start | bytes 61448 | tf_op jit(solution)/shard_map/grad_rows/ppermute | solution.py:44
  81.9 8.3 %collective-permute-start.26 = (bf16[160,64]{1,0:T(8,128)(2,1)S(1)}, bf16[160,64]{1,0:T(8,128)(2,1)S(1)}, u32[]{:S(2)}, u32[]{:S(2)}) collective-permute-start(bf16[160,64]{1,0:T(8,128)(2,1)S(1)} %get-tuple-element.59), channel_id=1, source_target_pairs={{0,4},{2,6},{4,0},{6,2},{1,5},{3,7},{5,1},{7,3},{8,12},{10,14},{12... | collective-permute-start | bytes 61448 | tf_op jit(solution)/shard_map/grad_rows/ppermute | solution.py:44
  82.9 7.3 %collective-permute-start.27 = (bf16[160,64]{1,0:T(8,128)(2,1)S(1)}, bf16[160,64]{1,0:T(8,128)(2,1)S(1)}, u32[]{:S(2)}, u32[]{:S(2)}) collective-permute-start(bf16[160,64]{1,0:T(8,128)(2,1)S(1)} %get-tuple-element.60), channel_id=1, source_target_pairs={{0,6},{2,4},{4,2},{6,0},{1,7},{3,5},{5,3},{7,1},{8,14},{10,12},{12... | collective-permute-start | bytes 61448 | tf_op jit(solution)/shard_map/grad_rows/ppermute | solution.py:44
  83.7 6.4 %collective-permute-start.21 = (bf16[128,64]{1,0:T(8,128)(2,1)S(1)}, bf16[128,64]{1,0:T(8,128)(2,1)S(1)}, u32[]{:S(2)}, u32[]{:S(2)}) collective-permute-start(bf16[128,64]{1,0:T(8,128)(2,1)S(1)} %get-tuple-element.48), channel_id=1, source_target_pairs={{0,8},{8,0},{16,24},{24,16},{1,9},{9,1},{17,25},{25,17},{2,10},{10... | collective-permute-start | bytes 49160 | tf_op jit(solution)/shard_map/fake/ppermute | solution.py:714
  90.7 9.7 %collective-permute-start.28 = (bf16[128,64]{1,0:T(8,128)(2,1)S(1)}, bf16[128,64]{1,0:T(8,128)(2,1)S(1)}, u32[]{:S(2)}, u32[]{:S(2)}) collective-permute-start(bf16[128,64]{1,0:T(8,128)(2,1)S(1)} %merge.1.own), channel_id=1, source_target_pairs={{0,24},{8,16},{16,8},{24,0},{1,25},{9,17},{17,9},{25,1},{2,26},{10... | collective-permute-start | bytes 49160 | tf_op jit(solution)/shard_map/to_student/ppermute | solution.py:749
  101.4 1.3 %collective-permute-start.32 = (bf16[5,64,128]{2,1,0:T(8,128)(2,1)S(1)}, bf16[5,64,128]{2,1,0:T(8,128)(2,1)S(1)}, u32[]{:S(2)}, u32[]{:S(2)}) collective-permute-start(bf16[5,64,128]{2,1,0:T(8,128)(2,1)S(1)} %outer.1), channel_id=1, source_target_pairs={{0,2},{2,0},{4,6},{6,4},{1,3},{3,1},{5,7},{7,5},{8,10},{10,8},{12,... | collective-permute-start | bytes 245768 | tf_op jit(solution)/shard_map/sums_near/ppermute | solution.py:774
  102.7 12.8 %collective-permute-start.33 = (bf16[5,64,128]{2,1,0:T(8,128)(2,1)S(1)}, bf16[5,64,128]{2,1,0:T(8,128)(2,1)S(1)}, u32[]{:S(2)}, u32[]{:S(2)}) collective-permute-start(bf16[5,64,128]{2,1,0:T(8,128)(2,1)S(1)} %add_convert_fusion.refs_6_), channel_id=1, source_target_pairs={{0,4},{1,5},{2,6},{3,7},{4,0},{5,1},{6,2},{7,3},{8,12},{9,13},{10,... | collective-permute-start | bytes 245768 | tf_op jit(solution)/shard_map/sums_far/ppermute | solution.py:789
  103.8 11.8 %collective-permute-start.34 = (bf16[5,64,128]{2,1,0:T(8,128)(2,1)S(1)}, bf16[5,64,128]{2,1,0:T(8,128)(2,1)S(1)}, u32[]{:S(2)}, u32[]{:S(2)}) collective-permute-start(bf16[5,64,128]{2,1,0:T(8,128)(2,1)S(1)} %add_convert_fusion.refs_6_), channel_id=1, source_target_pairs={{0,1},{1,0},{2,3},{3,2},{4,5},{5,4},{6,7},{7,6},{8,9},{9,8},{10,11... | collective-permute-start | bytes 245768 | tf_op jit(solution)/shard_map/sums_far/ppermute | solution.py:789
  105.2 10.4 %collective-permute-start.35 = (bf16[5,64,128]{2,1,0:T(8,128)(2,1)S(1)}, bf16[5,64,128]{2,1,0:T(8,128)(2,1)S(1)}, u32[]{:S(2)}, u32[]{:S(2)}) collective-permute-start(bf16[5,64,128]{2,1,0:T(8,128)(2,1)S(1)} %add_convert_fusion.refs_6_), channel_id=1, source_target_pairs={{0,5},{1,4},{2,7},{3,6},{4,1},{5,0},{6,3},{7,2},{8,13},{9,12},{10,... | collective-permute-start | bytes 245768 | tf_op jit(solution)/shard_map/sums_far/ppermute | solution.py:789
  106.3 4.4 %collective-permute-start.31 = (f32[1,9216]{1,0:T(1,128)S(1)}, f32[1,9216]{1,0:T(1,128)S(1)}, u32[]{:S(2)}, u32[]{:S(2)}) collective-permute-start(f32[1,9216]{1,0:T(1,128)S(1)} %copy-done.7), channel_id=1, source_target_pairs={{0,1},{1,0},{2,3},{3,2},{4,5},{5,4},{6,7},{7,6},{8,9},{9,8},{10,11... | collective-permute-start | bytes 110600 | tf_op jit(solution)/shard_map/other_mod/ppermute | solution.py:38
  107.7 4.4 %collective-permute-start.29 = (bf16[128,64]{1,0:T(8,128)(2,1)S(1)}, bf16[128,64]{1,0:T(8,128)(2,1)S(1)}, u32[]{:S(2)}, u32[]{:S(2)}) collective-permute-start(bf16[128,64]{1,0:T(8,128)(2,1)S(1)} %merge.1.own), channel_id=1, source_target_pairs={{0,8},{8,0},{16,24},{24,16},{1,9},{9,1},{17,25},{25,17},{2,10},{10... | collective-permute-start | bytes 49160 | tf_op jit(solution)/shard_map/to_second/ppermute | solution.py:792
  110.7 4.8 %collective-permute-start.30 = (bf16[128,64]{1,0:T(8,128)(2,1)S(1)}, bf16[128,64]{1,0:T(8,128)(2,1)S(1)}, u32[]{:S(2)}, u32[]{:S(2)}) collective-permute-start(bf16[128,64]{1,0:T(8,128)(2,1)S(1)} %merge.1.own), channel_id=1, source_target_pairs={{0,16},{8,24},{16,0},{24,8},{1,17},{9,25},{17,1},{25,9},{2,18},{10... | collective-permute-start | bytes 49160 | tf_op jit(solution)/shard_map/to_third/ppermute | solution.py:794
  (1 other events, 0.6 us)

commit v4 on v3

--- a/solution.py
+++ b/solution.py
@@ -7,6 +7,7 @@
 from jax.experimental import pallas as pl
 from jax.experimental.pallas import tpu as pltpu
 from jax.sharding import PartitionSpec as P
+
 
 SHIFT = 7.0
 EPS = 1e-06
@@ -24,24 +25,18 @@
     return (top, (values - top.astype(jnp.float32)).astype(jnp.bfloat16))
 
 
-def split_halves(values):
-    top = lax.reduce_precision(values, 8, 7)
-    return (top.astype(jnp.bfloat16), (values - top).astype(jnp.bfloat16))
-
-
 def swaps(count, offset):
     return [(place, place ^ offset) for place in range(count)]
 
 
 def gather_near(value, axis, count):
-    return [value] + [
-        lax.ppermute(value, axis, swaps(count, offset)) for offset in range(1, count)
-    ]
+    return [value] + [lax.ppermute(value, axis, swaps(count, offset)) for offset in range(1, count)]
 
 
 def scatter_near(blocks, axis, count):
     return [blocks[0]] + [
-        lax.ppermute(blocks[offset], axis, swaps(count, offset)) for offset in range(1, count)
+        lax.ppermute(blocks[offset], axis, swaps(count, offset))
+        for offset in range(1, count)
     ]
 
 
@@ -49,27 +44,10 @@
     held = {0: value}
     bit = count // 2
     while bit:
-        offsets = sorted(held)
-        joined = jnp.concatenate([held[offset] for offset in offsets], axis=0)
-        moved = lax.ppermute(joined, axis, swaps(count, bit))
-        rows = value.shape[0]
-        for place, offset in enumerate(offsets):
-            held[offset | bit] = moved[place * rows : (place + 1) * rows]
+        for offset in sorted(held):
+            held[offset | bit] = lax.ppermute(held[offset], axis, swaps(count, bit))
         bit //= 2
     return [held[offset] for offset in range(count)]
-
-
-def in_order(pieces, own_place):
-    ordered = list(pieces)
-    bit = 1
-    while bit < len(ordered):
-        flipped = (own_place & bit) != 0
-        ordered = [
-            jnp.where(flipped, ordered[place ^ bit], ordered[place])
-            for place in range(len(ordered))
-        ]
-        bit *= 2
-    return ordered
 
 
 def dot32(left, right):
@@ -367,6 +345,7 @@
             2.0 * (result - (second - sample)),
             jnp.where(section == 3, 1.0 / (1.0 + jnp.exp(-result)), 0.0),
         )
+
         @pl.when(section == 3)
         def _():
             grad_logit = (-1.0 / (1.0 + jnp.exp(result))).astype(jnp.bfloat16)
@@ -403,14 +382,23 @@
                 grads[place][...] = totals[place].astype(jnp.bfloat16)
 
 
-def judge_back_kernel(count, short_in, embed_w, gains, proj_ref, inverse_ref, key_ref, value_ref, pair, real, *refs):
+def gram_kernel(embed_w, gram_ref):
+    central_top, central_low = halves(centred(embed_w))
+    gram = (
+        dot32_t(central_top, central_top)
+        + dot32_t(central_top, central_low)
+        + dot32_t(central_low, central_top)
+    )
+    gram_ref[0], gram_ref[1] = halves(gram)
+
+
+def judge_back_kernel(count, model_width, short_in, gram, gains, proj_ref, inverse_ref, key_ref, value_ref, pair, real, *refs):
     rows = refs[:count]
     grads = refs[count : 2 * count]
     outs = refs[2 * count : 3 * count]
     grad_key_ref, grad_value_ref, grad_query_ref = refs[3 * count :]
     section = lax.axis_index("segment")
     latent_width = rows[0].shape[1]
-    model_width = embed_w.shape[2]
     head_width = gains.shape[2]
     scale = 1.0 / math.sqrt(head_width)
     size = rows[0].shape[0]
@@ -448,14 +436,7 @@
             else:
                 grad_value_ref[...] += grad_value
                 grad_key_ref[...] += grad_key
-        central = centred(embed_w)
-        central_top, central_low = halves(central)
-        gram = (
-            dot32_t(central_top, central_top)
-            + dot32_t(central_top, central_low)
-            + dot32_t(central_low, central_top)
-        )
-        gram_top, gram_low = halves(gram)
+        gram_top, gram_low = gram[0], gram[1]
         short_top, short_low = halves(short_in[:latent_width])
         for place in range(count):
             low = place * size
@@ -602,13 +583,11 @@
             total_ref[:, span] = total / full_rows
 
 
-def shards(
+def step(
     clean, noise, timesteps, text_vec, w_embed, w_time, w_mod, w_qkv, w_out, qk_gain, w_final
 ):
     section = lax.axis_index("segment")
     sections = lax.axis_size("segment")
-    batch_idx = lax.axis_index("dp")
-    seq_place = lax.axis_index("seq")
     tok_rows = clean.shape[1]
     latent_width = clean.shape[2]
     model_width = w_embed.shape[2]
@@ -618,26 +597,19 @@
     head_width = w_qkv.shape[4]
     kind_w = jnp.transpose(w_qkv[0, :, 0], (1, 0, 2))
     final_w = jnp.transpose(w_final[0])
-    with jax.named_scope("heads"):
-        heads_w = gather_doubling(w_out[0, 0], "seq", count)
+    heads_w = gather_doubling(w_out[0, 0], "seq", count)
     bf16, f32 = jnp.bfloat16, jnp.float32
 
-    with jax.named_scope("conditioning"):
-        mod_piece, noisy_student = run(
-            condition_kernel,
-            [array((1, mod_width), f32), array((tok_rows, latent_width), bf16)],
-            (timesteps, text_vec, w_time, jnp.transpose(clean[0]), noise, w_mod),
-            [SMEM, VMEM, VMEM, VMEM, VMEM, ANY],
-            2 * model_width * mod_width,
-            scratch=(
-                pltpu.VMEM((model_width, mod_width), bf16),
-                pltpu.SemaphoreType.DMA((STREAMS,)),
-            ),
-        )
-    with jax.named_scope("modulation"):
-        mod_parts = gather_near(mod_piece, "seq", count)
-    with jax.named_scope("student_rows"):
-        student_rows = gather_near(noisy_student, "seq", count)
+    mod_piece, noisy_student = run(
+        condition_kernel,
+        [array((1, mod_width), f32), array((tok_rows, latent_width), bf16)],
+        (timesteps, text_vec, w_time, jnp.transpose(clean[0]), noise, w_mod),
+        [SMEM, VMEM, VMEM, VMEM, VMEM, ANY],
+        2 * model_width * mod_width,
+        scratch=(pltpu.VMEM((model_width, mod_width), bf16), pltpu.SemaphoreType.DMA((STREAMS,))),
+    )
+    mod_parts = gather_near(mod_piece, "seq", count)
+    student_rows = gather_near(noisy_student, "seq", count)
 
     head_blocks = [array((tok_rows, head_width), bf16)] * count
     stored = [
@@ -646,132 +618,110 @@
         ((full_rows, head_width), bf16),
         ((full_rows, head_width), bf16),
     ]
-    with jax.named_scope("student_front"):
-        *head_outs, short, late_mod = run(
-            functools.partial(student_front_kernel, count),
-            head_blocks
-            + [
-                array((latent_width + 16, 3 * head_width), f32),
-                array((1, 3 * model_width), f32),
-            ],
-            (w_embed, kind_w, qk_gain, *mod_parts, *student_rows),
-            [VMEM] * (3 + 2 * count),
-            4 * latent_width * model_width * 3 * head_width,
-            scratch=[pltpu.VMEM((1, 5 * model_width), f32)]
-            + [pltpu.VMEM(shape, kind) for shape, kind in stored],
-        )
-    with jax.named_scope("student_heads"):
-        student_mixed = scatter_near(head_outs, "seq", count)
-    with jax.named_scope("other_mod"):
-        groups = lax.axis_size("dp")
-        late_mods = gather_near(late_mod, "dp", groups)
+    *head_outs, short, late_mod = run(
+        functools.partial(student_front_kernel, count),
+        head_blocks
+        + [
+            array((latent_width + 16, 3 * head_width), f32),
+            array((1, 3 * model_width), f32),
+        ],
+        (w_embed, kind_w, qk_gain, *mod_parts, *student_rows),
+        [VMEM] * (3 + 2 * count),
+        4 * latent_width * model_width * 3 * head_width,
+        scratch=[pltpu.VMEM((1, 5 * model_width), f32)]
+        + [pltpu.VMEM(shape, kind) for shape, kind in stored],
+    )
+    student_mixed = scatter_near(head_outs, "seq", count)
+    groups = lax.axis_size("dp")
+    late_mods = gather_near(late_mod, "dp", groups)
     work = pltpu.VMEM((tok_rows, model_width), f32)
     inverse_shape = array((tok_rows, 128), f32)
-    with jax.named_scope("student_tail"):
-        pair, student_inverse = run(
-            functools.partial(student_tail_kernel, count),
-            [array((tok_rows, 2 * latent_width), bf16), inverse_shape],
-            (timesteps, late_mod, noisy_student, noise, w_embed, final_w, *student_mixed, *heads_w),
-            [SMEM] + [VMEM] * (5 + 2 * count),
-            2 * tok_rows * model_width * head_width * count,
-            scratch=(work,),
-        )
-    with jax.named_scope("sample"):
-        for offset in range(sections - 1, 0, -1):
-            moved = lax.ppermute(
-                pair,
-                "segment",
-                [(place, (place + offset) % sections) for place in range(sections)],
-            )
-            held = moved if offset == sections - 1 else jnp.where(section == offset, moved, held)
-        pair = jnp.where(section == 0, pair, held)
-    with jax.named_scope("critic_rows"):
-        critic_rows = gather_near(pair[:, :latent_width], "seq", count)
-    with jax.named_scope("critic_front"):
-        *head_outs, proj, inverse, keys, values = run(
-            functools.partial(critic_front_kernel, count),
-            head_blocks + [array(shape, kind) for shape, kind in stored],
-            (short, w_embed, qk_gain, *critic_rows),
-            [VMEM] * (3 + count),
-            4 * latent_width * model_width * full_rows,
-        )
-    with jax.named_scope("critic_heads"):
-        critic_mixed = scatter_near(head_outs, "seq", count)
+    pair, student_inverse = run(
+        functools.partial(student_tail_kernel, count),
+        [array((tok_rows, 2 * latent_width), bf16), inverse_shape],
+        (timesteps, late_mod, noisy_student, noise, w_embed, final_w, *student_mixed, *heads_w),
+        [SMEM] + [VMEM] * (5 + 2 * count),
+        2 * tok_rows * model_width * head_width * count,
+        scratch=(work,),
+    )
+    moved = [
+        lax.ppermute(pair, "segment", [(0, place), (place, 0)])
+        for place in range(1, sections)
+    ]
+    held = moved[0]
+    for place in range(2, sections):
+        held = jnp.where(section == place, moved[place - 1], held)
+    pair = jnp.where(section == 0, pair, held)
+    critic_rows = gather_near(pair[:, :latent_width], "seq", count)
+    *head_outs, proj, inverse, keys, values = run(
+        functools.partial(critic_front_kernel, count),
+        head_blocks + [array(shape, kind) for shape, kind in stored],
+        (short, w_embed, qk_gain, *critic_rows),
+        [VMEM] * (3 + count),
+        4 * latent_width * model_width * full_rows,
+    )
+    critic_mixed = scatter_near(head_outs, "seq", count)
     small = array((tok_rows, latent_width), f32)
     thin = array((tok_rows, latent_width), bf16)
-    with jax.named_scope("critic_tail"):
-        *grad_heads, critic_inverse, term_rows, target, direct = run(
-            functools.partial(critic_tail_kernel, count),
-            head_blocks + [inverse_shape, thin, small, small],
-            (timesteps, late_mod, pair, noise, w_embed, final_w, *critic_mixed, *heads_w),
-            [SMEM] + [VMEM] * (5 + 2 * count),
-            4 * tok_rows * model_width * head_width * count,
-            scratch=(pltpu.VMEM((tok_rows, latent_width), bf16), work, work),
-        )
-    with jax.named_scope("grad_heads"):
-        grad_blocks = scatter_near(grad_heads, "seq", count)
-    with jax.named_scope("fake"):
-        fake = lax.ppermute(term_rows, "segment", swaps(sections, 1))
-    with jax.named_scope("real"):
-        real = lax.ppermute(term_rows, "segment", swaps(sections, 2))
-    with jax.named_scope("judge_back"):
-        parts = run(
-            functools.partial(judge_back_kernel, count),
-            [array((tok_rows + 32, latent_width), bf16)] * count,
-            (
-                short,
-                w_embed,
-                qk_gain,
-                proj,
-                inverse,
-                keys,
-                values,
-                pair,
-                real,
-                *critic_rows,
-                *grad_blocks,
-            ),
-            [VMEM] * (9 + 2 * count),
-            10 * full_rows * full_rows * head_width,
-            scratch=(pltpu.VMEM((full_rows, head_width), f32),) * 3,
-        )
-    with jax.named_scope("grad_rows"):
-        parts = scatter_near(parts, "seq", count)
-    with jax.named_scope("merge"):
-        (payload,) = run(
-            functools.partial(merge_kernel, count),
-            [thin],
-            (timesteps, direct, real, fake, *parts),
-            [SMEM] + [VMEM] * (3 + count),
-            1000,
-        )
-    with jax.named_scope("to_student"):
-        to_student = lax.ppermute(
-            payload, "segment", [(place, sections - 1 - place) for place in range(sections)]
-        )
-    with jax.named_scope("outer"):
-        (sums,) = run(
-            functools.partial(outer_kernel, count),
-            [array((count + 1, latent_width, 128), bf16)],
-            (
-                timesteps,
-                to_student,
-                target,
-                noisy_student,
-                pair,
-                student_inverse,
-                critic_inverse,
-                *student_mixed,
-                *critic_mixed,
-            ),
-            [SMEM] + [VMEM] * (6 + 2 * count),
-            2 * tok_rows * latent_width * head_width * (count + 1),
-        )
+    *grad_heads, critic_inverse, term_rows, target, direct = run(
+        functools.partial(critic_tail_kernel, count),
+        head_blocks + [inverse_shape, thin, small, small],
+        (timesteps, late_mod, pair, noise, w_embed, final_w, *critic_mixed, *heads_w),
+        [SMEM] + [VMEM] * (5 + 2 * count),
+        4 * tok_rows * model_width * head_width * count,
+        scratch=(pltpu.VMEM((tok_rows, latent_width), bf16), work, work),
+    )
+    grad_blocks = scatter_near(grad_heads, "seq", count)
+    fake = lax.ppermute(term_rows, "segment", swaps(sections, 1))
+    real = lax.ppermute(term_rows, "segment", swaps(sections, 2))
+    (gram,) = run(
+        gram_kernel,
+        [array((2, latent_width, latent_width), bf16)],
+        (w_embed,),
+        [VMEM],
+        6 * latent_width * latent_width * model_width,
+    )
+    parts = run(
+        functools.partial(judge_back_kernel, count, model_width),
+        [array((tok_rows + 32, latent_width), bf16)] * count,
+        (short, gram, qk_gain, proj, inverse, keys, values, pair, real, *critic_rows, *grad_blocks),
+        [VMEM] * (9 + 2 * count),
+        10 * full_rows * full_rows * head_width,
+        scratch=(pltpu.VMEM((full_rows, head_width), f32),) * 3,
+    )
+    parts = scatter_near(parts, "seq", count)
+    (payload,) = run(
+        functools.partial(merge_kernel, count),
+        [thin],
+        (timesteps, direct, real, fake, *parts),
+        [SMEM] + [VMEM] * (3 + count),
+        1000,
+    )
+    ends = [(place, sections - 1 - place) for place in range(sections)]
+    to_student = lax.ppermute(payload, "segment", ends)
+    to_second = lax.ppermute(payload, "segment", swaps(sections, 1))
+    to_third = lax.ppermute(payload, "segment", swaps(sections, 2))
+    (sums,) = run(
+        functools.partial(outer_kernel, count),
+        [array((count + 1, latent_width, 128), bf16)],
+        (
+            timesteps,
+            to_student,
+            target,
+            noisy_student,
+            pair,
+            student_inverse,
+            critic_inverse,
+            *student_mixed,
+            *critic_mixed,
+        ),
+        [SMEM] + [VMEM] * (6 + 2 * count),
+        2 * tok_rows * latent_width * head_width * (count + 1),
+    )
     last = count // 2
     bit = 1
     while bit < last:
-        with jax.named_scope("sums_near"):
-            moved = lax.ppermute(sums, "seq", swaps(count, bit))
+        moved = lax.ppermute(sums, "seq", swaps(count, bit))
         sums = (sums.astype(f32) + moved.astype(f32)).astype(bf16)
         bit *= 2
     sums_all = []
@@ -782,37 +732,29 @@
                 for place in range(count)
                 for batch in range(groups)
             ]
-            with jax.named_scope("sums_far"):
-                sums_all.append(
-                    sums
-                    if offset == group == 0
-                    else lax.ppermute(sums, ("seq", "dp"), moves)
-                )
-    with jax.named_scope("to_second"):
-        to_second = lax.ppermute(payload, "segment", swaps(sections, 1))
-    with jax.named_scope("to_third"):
-        to_third = lax.ppermute(payload, "segment", swaps(sections, 2))
-    with jax.named_scope("expand"):
-        grad_t, total_t = run(
-            functools.partial(expand_kernel, count, groups, full_rows),
-            [array((latent_width, tok_rows), f32), array((latent_width, model_width), f32)],
-            (
-                payload,
-                to_student,
-                to_second,
-                to_third,
-                w_embed,
-                *heads_w,
-                *late_mods,
-                *sums_all,
-            ),
-            [VMEM] * (5 + count + 3 * groups),
-            4 * groups * latent_width * model_width * head_width * count,
-            scratch=(
-                pltpu.VMEM((groups * latent_width, model_width), f32),
-                pltpu.VMEM((count + 1, groups * latent_width, 128), f32),
-            ),
-        )
+            sums_all.append(
+                sums if offset == group == 0 else lax.ppermute(sums, ("seq", "dp"), moves)
+            )
+    grad_t, total_t = run(
+        functools.partial(expand_kernel, count, groups, full_rows),
+        [array((latent_width, tok_rows), f32), array((latent_width, model_width), f32)],
+        (
+            payload,
+            to_student,
+            to_second,
+            to_third,
+            w_embed,
+            *heads_w,
+            *late_mods,
+            *sums_all,
+        ),
+        [VMEM] * (5 + count + 3 * groups),
+        4 * groups * latent_width * model_width * head_width * count,
+        scratch=(
+            pltpu.VMEM((groups * latent_width, model_width), f32),
+            pltpu.VMEM((count + 1, groups * latent_width, 128), f32),
+        ),
+    )
     return (jnp.transpose(grad_t)[None], jnp.transpose(total_t)[None])
 
 
@@ -831,7 +773,7 @@
         P("segment", None, None),
     )
     return jax.shard_map(
-        shards,
+        step,
         mesh=mesh,
         in_specs=placed,
         out_specs=(P("dp", "seq", None), P("segment", None, None)),

time: 119 us -> 125 us (1.050)
  local copies, waits for them, and re-layouts: 2.38 us -> 9 us
  starting transfers between devices: 46 us -> 43.3 us
  waiting for transfers between devices: 45.5 us -> 47.5 us
    unnamed x58 -> x60, local copies, waits for them, and re-layouts: 2.28 us -> 9 us
    ppermute x14 -> x15, starting transfers between devices: 30.5 us -> 27.7 us  [the longest x1 5.85 us: step(): to_student = lax.ppermute(payload, 'segment', ends)]
    ppermute x10, waiting for transfers between devices: 8.66 us -> 10.7 us  [gather_near(): lax.ppermute(value, axis, swaps(count, offset))]
    ppermute x14 -> x15, waiting for transfers between devices: 31.1 us -> 31.7 us  [the longest x3 17.8 us: gather_doubling(): held[offset | bit] = lax.ppermute(held[offset], axis, swaps(count, bit))]
    pallas_call x9 -> x10, Pallas kernels: 22.2 us -> 22.9 us  [run(): pl.pallas_call(kernel, out_shape=outputs, in_specs=specs, out_specs=[VMEM...]
  transfers between devices with their start and end apart: 36 -> 37, of which waited for: 17 -> 19; matrix products, arithmetic and copies ran while one was open for 0% -> 0% of each run, Pallas kernels for 11% -> 11%
where the time goes in v4:
time: 125 us; the launch traced here: 124 us
  waiting for transfers between devices  47.5 us (38%)
  starting transfers between devices  43.3 us (35%)
  Pallas kernels  22.9 us (18%)
  local copies, waits for them, and re-layouts  9 us (7%)
    pallas_call x10, Pallas kernels, run(): pl.pallas_call(kernel, out_shape=outputs, in_specs=specs, out_specs=[VMEM...  22.9 us
    ppermute x3, waiting for transfers between devices, gather_doubling(): held[offset | bit] = lax.ppermute(held[offset], axis, swaps(count, bit))  17.8 us
    ppermute x10, waiting for transfers between devices, gather_near(): lax.ppermute(value, axis, swaps(count, offset))  10.7 us
    unnamed x60, local copies, waits for them, and re-layouts  9 us
    ppermute x10, starting transfers between devices, gather_near(): lax.ppermute(value, axis, swaps(count, offset))  8 us
    ppermute x12, starting transfers between devices, scatter_near(): lax.ppermute(blocks[offset], axis, swaps(count, offset))  7.57 us
    ppermute x1, starting transfers between devices, step(): to_student = lax.ppermute(payload, 'segment', ends)  5.85 us
    ppermute x3, starting transfers between devices, step(): lax.ppermute(pair, 'segment', [(0, place), (place, 0)])  5.75 us
  transfers between devices with their start and end apart: 37, of which 19 were waited for; matrix products, arithmetic and copies ran while one was open for 0% of the time, Pallas kernels for 11%

profile of v4, /device:TPU:0, one launch (start us, length us, event | category | flops | bytes accessed | tf_op | source)
XLA Modules:
  0.0 124.4 jit_solution(3084682186471189846)
XLA Ops:
  0.6 3.1 %collective-permute-start.10 = (bf16[128,3072]{1,0:T(8,128)(2,1)}, bf16[128,3072]{1,0:T(8,128)(2,1)S(1)}, u32[]{:S(2)}, u32[]{:S(2)}) collective-permute-start(bf16[128,3072]{1,0:T(8,128)(2,1)} %bitcast.17), channel_id=1, source_target_pairs={{0,4},{2,6},{4,0},{6,2},{1,5},{3,7},{5,1},{7,3},{8,12},{10,14},{12... | collective-permute-start | bytes 2359304 | tf_op jit(solution)/shard_map/ppermute | solution.py:48
  3.7 17.8 %collective-permute-done.10.refs_6_.refs_2_ = bf16[128,3072]{1,0:T(8,128)(2,1)S(1)} collective-permute-done((bf16[128,3072]{1,0:T(8,128)(2,1)}, bf16[128,3072]{1,0:T(8,128)(2,1)S(1)}, u32[]{:S(2)}, u32[]{:S(2)}) %collective-permute-start.10) | collective-permute-done | bytes 786464 | tf_op jit(solution)/shard_map/ppermute | solution.py:48
  21.5 1.4 %copy-done.3 = bf16[1,256,3072]{2,1,0:T(8,128)(2,1)S(1)} copy-done((bf16[1,256,3072]{2,1,0:T(8,128)(2,1)S(1)}, bf16[1,256,3072]{2,1,0:T(8,128)(2,1)}, u32[]{:S(2)}) %copy-start.3) | copy-done | bytes 1572888
  22.9 0.8 copy-done.8
  23.6 0.7 copy-done.25
  24.3 0.7 copy-done.27
  25.0 0.7 copy-done.29
  25.7 9.5 %shard_map.122 = (f32[1,3840]{1,0:T(1,128)S(1)}, bf16[128,64]{1,0:T(8,128)(2,1)S(1)}) custom-call(s32[2,2]{1,0:T(2,128)S(1)} %copy-done.25, f32[1,256]{1,0:T(1,128)S(1)} %copy-done.29, bf16[1,256,3072]{2,1,0:T(8,128)(2,1)S(1)} %copy-done.3, bf16[64,128]{1,0:T(8,128)(2,1)S(1)} %bitcast.30, bf16[1,128,128]{2,1,0:T(8,128)(2,1)S(1)} %copy-done.8, ...), custom_call_target="tpu_custom_call" | custom-call | flops 23592960 | bytes 25247760 | tf_op jit(solution)/shard_map/pallas_call | solution.py:104
  35.3 0.6 collective-permute-start
  35.8 1.7 %collective-permute-start.1 = (f32[1,3840]{1,0:T(1,128)S(1)}, f32[1,3840]{1,0:T(1,128)S(1)}, u32[]{:S(2)}, u32[]{:S(2)}) collective-permute-start(f32[1,3840]{1,0:T(1,128)S(1)} %get-tuple-element.34.refs_0_), channel_id=1, source_target_pairs={{0,4},{2,6},{4,0},{6,2},{1,5},{3,7},{5,1},{7,3},{8,12},{10,14},{12... | collective-permute-start | bytes 46088 | tf_op jit(solution)/shard_map/ppermute | solution.py:33
  37.6 0.4 collective-permute-start.3
  38.0 1.6 %collective-permute-done.1.refs_2_ = f32[1,3840]{1,0:T(1,128)S(1)} collective-permute-done((f32[1,3840]{1,0:T(1,128)S(1)}, f32[1,3840]{1,0:T(1,128)S(1)}, u32[]{:S(2)}, u32[]{:S(2)}) %collective-permute-start.1) | collective-permute-done | bytes 15392 | tf_op jit(solution)/shard_map/ppermute | solution.py:33
  39.6 1.7 %collective-permute-start.4 = (bf16[128,64]{1,0:T(8,128)(2,1)S(1)}, bf16[128,64]{1,0:T(8,128)(2,1)S(1)}, u32[]{:S(2)}, u32[]{:S(2)}) collective-permute-start(bf16[128,64]{1,0:T(8,128)(2,1)S(1)} %get-tuple-element.35.refs_4_.latent.student_rows), channel_id=1, source_target_pairs={{0,4},{2,6},{4,0},{6,2},{1,5},{3,7},{5,1},{7,3},{8,12},{10,14},{12... | collective-permute-start | bytes 49160 | tf_op jit(solution)/shard_map/ppermute | solution.py:33
  41.3 2.2 %collective-permute-done.4.refs_6_ = bf16[128,64]{1,0:T(8,128)(2,1)S(1)} collective-permute-done((bf16[128,64]{1,0:T(8,128)(2,1)S(1)}, bf16[128,64]{1,0:T(8,128)(2,1)S(1)}, u32[]{:S(2)}, u32[]{:S(2)}) %collective-permute-start.4) | collective-permute-done | bytes 16416 | tf_op jit(solution)/shard_map/ppermute | solution.py:33
  43.5 1.3 %collective-permute-done.5.refs_7_ = bf16[128,64]{1,0:T(8,128)(2,1)S(1)} collective-permute-done((bf16[128,64]{1,0:T(8,128)(2,1)S(1)}, bf16[128,64]{1,0:T(8,128)(2,1)S(1)}, u32[]{:S(2)}, u32[]{:S(2)}) %collective-permute-start.5) | collective-permute-done | bytes 16416 | tf_op jit(solution)/shard_map/ppermute | solution.py:33
  44.8 3.6 %shard_map.123 = (bf16[128,128]{1,0:T(8,128)(2,1)S(1)}, bf16[128,128]{1,0:T(8,128)(2,1)S(1)}, bf16[128,128]{1,0:T(8,128)(2,1)S(1)}, bf16[128,128]{1,0:T(8,128)(2...) custom-call(bf16[1,64,3072]{2,1,0:T(8,128)(2,1)S(1)} %copy-done, bf16[3,3072,128]{2,1,0:T(8,128)(2,1)S(1)} %bitcast.22, ...), custom_call_target="tpu_custom_call" | custom-call | flops 301989888 | bytes 3171328 | tf_op jit(solution)/shard_map/pallas_call | solution.py:104
  48.5 0.6 copy-done.20
  49.1 0.6 collective-permute-start.7
  49.7 1.2 collective-permute-start.8
  51.0 2.4 %collective-permute-done.7.refs_2_ = bf16[128,128]{1,0:T(8,128)(2,1)S(1)} collective-permute-done((bf16[128,128]{1,0:T(8,128)(2,1)S(1)}, bf16[128,128]{1,0:T(8,128)(2,1)S(1)}, u32[]{:S(2)}, u32[]{:S(2)}) %collective-permute-start.7) | collective-permute-done | bytes 32800 | tf_op jit(solution)/shard_map/ppermute | solution.py:38
  53.5 3.4 %shard_map.124 = (bf16[128,128]{1,0:T(8,128)(2,1)}, f32[128,128]{1,0:T(8,128)S(1)}) custom-call(s32[2,2]{1,0:T(2,128)S(1)} %copy-done.25, f32[1,9216]{1,0:T(1,128)S(1)} %get-tuple-element.36.mod.refs_4_, bf16[128,64]{1,0:T(8,128)(2,1)S(1)} %get-tuple-element.35.refs_4_.latent.student_rows, bf16[1,128,128]{2,1,0:T(8,128)(2,1)S(1)} %copy-done.8, ...), custom_call_target="tpu_custom_call" | custom-call | flops 402653184 | bytes 4247568 | tf_op jit(solution)/shard_map/pallas_call | solution.py:104
  56.9 0.6 copy-done.23
  57.5 1.9 %collective-permute-start.12 = (bf16[128,128]{1,0:T(8,128)(2,1)}, bf16[128,128]{1,0:T(8,128)(2,1)}, u32[]{:S(2)}, u32[]{:S(2)}) collective-permute-start(bf16[128,128]{1,0:T(8,128)(2,1)} %get-tuple-element.41), channel_id=1, source_target_pairs={{0,24},{24,0},{1,25},{25,1},{2,26},{26,2},{3,27},{27,3},{4,28},{28... | collective-permute-start | bytes 98312 | tf_op jit(solution)/shard_map/ppermute | solution.py:648
  59.4 1.9 %collective-permute-start.13 = (bf16[128,128]{1,0:T(8,128)(2,1)}, bf16[128,128]{1,0:T(8,128)(2,1)}, u32[]{:S(2)}, u32[]{:S(2)}) collective-permute-start(bf16[128,128]{1,0:T(8,128)(2,1)} %get-tuple-element.41), channel_id=1, source_target_pairs={{0,16},{16,0},{1,17},{17,1},{2,18},{18,2},{3,19},{19,3},{4,20},{20... | collective-permute-start | bytes 98312 | tf_op jit(solution)/shard_map/ppermute | solution.py:648
  61.4 1.9 %collective-permute-start.14 = (bf16[128,128]{1,0:T(8,128)(2,1)}, bf16[128,128]{1,0:T(8,128)(2,1)}, u32[]{:S(2)}, u32[]{:S(2)}) collective-permute-start(bf16[128,128]{1,0:T(8,128)(2,1)} %get-tuple-element.41), channel_id=1, source_target_pairs={{0,8},{8,0},{1,9},{9,1},{2,10},{10,2},{3,11},{11,3},{4,12},{12,4},... | collective-permute-start | bytes 98312 | tf_op jit(solution)/shard_map/ppermute | solution.py:648
  63.3 2.1 %collective-permute-done.12 = bf16[128,128]{1,0:T(8,128)(2,1)} collective-permute-done((bf16[128,128]{1,0:T(8,128)(2,1)}, bf16[128,128]{1,0:T(8,128)(2,1)}, u32[]{:S(2)}, u32[]{:S(2)}) %collective-permute-start.12) | collective-permute-done | bytes 32800 | tf_op jit(solution)/shard_map/ppermute | solution.py:648
  65.4 1.0 collective-permute-done.13
  66.5 1.0 collective-permute-done.14
  67.5 0.8 select_select_fusion.pair
  68.4 1.1 collective-permute-start.16
  69.5 0.7 collective-permute-start.17
  70.2 2.1 %collective-permute-done.16.refs_2_ = bf16[128,64]{1,0:T(8,128)(2,1)S(1)} collective-permute-done((bf16[128,64]{1,0:T(8,128)(2,1)S(1)}, bf16[128,64]{1,0:T(8,128)(2,1)S(1)}, u32[]{:S(2)}, u32[]{:S(2)}) %collective-permute-start.16) | collective-permute-done | bytes 16416 | tf_op jit(solution)/shard_map/ppermute | solution.py:33
  72.4 0.5 collective-permute-done.17.refs_3_
  72.9 0.9 copy-done.21
  73.9 1.0 collective-permute-start.19
  74.9 0.7 collective-permute-start.20
  75.6 2.2 %collective-permute-done.19.refs_2_.refs_6_ = bf16[128,128]{1,0:T(8,128)(2,1)S(1)} collective-permute-done((bf16[128,128]{1,0:T(8,128)(2,1)S(1)}, bf16[128,128]{1,0:T(8,128)(2,1)S(1)}, u32[]{:S(2)}, u32[]{:S(2)}) %collective-permute-start.19) | collective-permute-done | bytes 32800 | tf_op jit(solution)/shard_map/ppermute | solution.py:38
  77.8 0.5 collective-permute-done.20.refs_3_.refs_7_
  78.3 1.0 copy-done.5
  79.3 0.8 copy-done.7
  80.1 0.8 copy-done.9
  80.9 0.6 shard_map.126
  81.6 1.1 collective-permute-start.24
  82.7 0.7 collective-permute-start.25
  83.4 4.1 %collective-permute-start.21 = (bf16[128,64]{1,0:T(8,128)(2,1)S(1)}, bf16[128,64]{1,0:T(8,128)(2,1)S(1)}, u32[]{:S(2)}, u32[]{:S(2)}) collective-permute-start(bf16[128,64]{1,0:T(8,128)(2,1)S(1)} %get-tuple-element.48), channel_id=1, source_target_pairs={{0,16},{8,24},{16,0},{24,8},{1,17},{9,25},{17,1},{25,9},{2,18},{10... | collective-permute-start | bytes 49160 | tf_op jit(solution)/shard_map/ppermute | solution.py:676
  87.5 0.6 shard_map.127.gram
  88.1 1.3 %collective-permute-done.21.real = bf16[128,64]{1,0:T(8,128)(2,1)S(1)} collective-permute-done((bf16[128,64]{1,0:T(8,128)(2,1)S(1)}, bf16[128,64]{1,0:T(8,128)(2,1)S(1)}, u32[]{:S(2)}, u32[]{:S(2)}) %collective-permute-start.21) | collective-permute-done | bytes 16416 | tf_op jit(solution)/shard_map/ppermute | solution.py:676
  89.6 1.1 collective-permute-start.27
  90.7 0.7 collective-permute-start.28
  91.4 3.9 %collective-permute-start.22 = (bf16[128,64]{1,0:T(8,128)(2,1)S(1)}, bf16[128,64]{1,0:T(8,128)(2,1)S(1)}, u32[]{:S(2)}, u32[]{:S(2)}) collective-permute-start(bf16[128,64]{1,0:T(8,128)(2,1)S(1)} %get-tuple-element.48), channel_id=1, source_target_pairs={{0,8},{8,0},{16,24},{24,16},{1,9},{9,1},{17,25},{25,17},{2,10},{10... | collective-permute-start | bytes 49160 | tf_op jit(solution)/shard_map/ppermute | solution.py:675
  95.3 1.9 %collective-permute-done.22.fake = bf16[128,64]{1,0:T(8,128)(2,1)S(1)} collective-permute-done((bf16[128,64]{1,0:T(8,128)(2,1)S(1)}, bf16[128,64]{1,0:T(8,128)(2,1)S(1)}, u32[]{:S(2)}, u32[]{:S(2)}) %collective-permute-start.22) | collective-permute-done | bytes 16416 | tf_op jit(solution)/shard_map/ppermute | solution.py:675
  97.2 0.6 shard_map.129.own
  97.8 5.8 %collective-permute-start.29 = (bf16[128,64]{1,0:T(8,128)(2,1)S(1)}, bf16[128,64]{1,0:T(8,128)(2,1)S(1)}, u32[]{:S(2)}, u32[]{:S(2)}) collective-permute-start(bf16[128,64]{1,0:T(8,128)(2,1)S(1)} %shard_map.129.own), channel_id=1, source_target_pairs={{0,24},{8,16},{16,8},{24,0},{1,25},{9,17},{17,9},{25,1},{2,26},{10... | collective-permute-start | bytes 49160 | tf_op jit(solution)/shard_map/ppermute | solution.py:701
  103.6 1.9 %collective-permute-done.29.arrived.from_first = bf16[128,64]{1,0:T(8,128)(2,1)S(1)} collective-permute-done((bf16[128,64]{1,0:T(8,128)(2,1)S(1)}, bf16[128,64]{1,0:T(8,128)(2,1)S(1)}, u32[]{:S(2)}, u32[]{:S(2)}) %collective-permute-start.29) | collective-permute-done | bytes 16416 | tf_op jit(solution)/shard_map/ppermute | solution.py:701
  105.6 0.9 shard_map.130
  106.6 1.3 %collective-permute-done.33 = bf16[5,64,128]{2,1,0:T(8,128)(2,1)S(1)} collective-permute-done((bf16[5,64,128]{2,1,0:T(8,128)(2,1)S(1)}, bf16[5,64,128]{2,1,0:T(8,128)(2,1)S(1)}, u32[]{:S(2)}, u32[]{:S(2)}) %collective-permute-start.33) | collective-permute-done | bytes 81952 | tf_op jit(solution)/shard_map/ppermute | solution.py:724
  107.9 1.1 collective-permute-start.34
  109.0 1.5 %collective-permute-start.35 = (bf16[5,64,128]{2,1,0:T(8,128)(2,1)S(1)}, bf16[5,64,128]{2,1,0:T(8,128)(2,1)S(1)}, u32[]{:S(2)}, u32[]{:S(2)}) collective-permute-start(bf16[5,64,128]{2,1,0:T(8,128)(2,1)S(1)} %add_convert_fusion.refs_6_), channel_id=1, source_target_pairs={{0,1},{1,0},{2,3},{3,2},{4,5},{5,4},{6,7},{7,6},{8,9},{9,8},{10,11... | collective-permute-start | bytes 245768 | tf_op jit(solution)/shard_map/ppermute | solution.py:736
  110.5 0.9 collective-permute-start.36
  111.4 1.6 %collective-permute-start.32 = (f32[1,9216]{1,0:T(1,128)S(1)}, f32[1,9216]{1,0:T(1,128)S(1)}, u32[]{:S(2)}, u32[]{:S(2)}) collective-permute-start(f32[1,9216]{1,0:T(1,128)S(1)} %copy-done.7), channel_id=1, source_target_pairs={{0,1},{1,0},{2,3},{3,2},{4,5},{5,4},{6,7},{7,6},{8,9},{9,8},{10,11... | collective-permute-start | bytes 110600 | tf_op jit(solution)/shard_map/ppermute | solution.py:33
  113.1 2.9 %collective-permute-done.32.refs_5_ = f32[1,9216]{1,0:T(1,128)S(1)} collective-permute-done((f32[1,9216]{1,0:T(1,128)S(1)}, f32[1,9216]{1,0:T(1,128)S(1)}, u32[]{:S(2)}, u32[]{:S(2)}) %collective-permute-start.32) | collective-permute-done | bytes 36896 | tf_op jit(solution)/shard_map/ppermute | solution.py:33
  116.0 1.4 %collective-permute-start.31 = (bf16[128,64]{1,0:T(8,128)(2,1)S(1)}, bf16[128,64]{1,0:T(8,128)(2,1)S(1)}, u32[]{:S(2)}, u32[]{:S(2)}) collective-permute-start(bf16[128,64]{1,0:T(8,128)(2,1)S(1)} %shard_map.129.own), channel_id=1, source_target_pairs={{0,16},{8,24},{16,0},{24,8},{1,17},{9,25},{17,1},{25,9},{2,18},{10... | collective-permute-start | bytes 49160 | tf_op jit(solution)/shard_map/ppermute | solution.py:703
  117.4 3.4 %collective-permute-done.31.from_third = bf16[128,64]{1,0:T(8,128)(2,1)S(1)} collective-permute-done((bf16[128,64]{1,0:T(8,128)(2,1)S(1)}, bf16[128,64]{1,0:T(8,128)(2,1)S(1)}, u32[]{:S(2)}, u32[]{:S(2)}) %collective-permute-start.31) | collective-permute-done | bytes 16416 | tf_op jit(solution)/shard_map/ppermute | solution.py:703
  120.8 3.6 %shard_map.131 = (f32[64,128]{1,0:T(8,128)}, f32[64,3072]{1,0:T(8,128)}) custom-call(bf16[128,64]{1,0:T(8,128)(2,1)S(1)} %shard_map.129.own, bf16[128,64]{1,0:T(8,128)(2,1)S(1)} %collective-permute-done.29.arrived.from_first, bf16[128,64]{1,0:T(8,128)(2,1)S(1)} %collective-permute-done.30.from_second, ...), custom_call_target="tpu_custom_call" | custom-call | flops 805306368 | bytes 4825088 | tf_op jit(solution)/shard_map/pallas_call | solution.py:104
  (82 shorter events, 0.8 us)
Async XLA Ops:
  0.6 20.8 %collective-permute-start.10 = (bf16[128,3072]{1,0:T(8,128)(2,1)}, bf16[128,3072]{1,0:T(8,128)(2,1)S(1)}, u32[]{:S(2)}, u32[]{:S(2)}) collective-permute-start(bf16[128,3072]{1,0:T(8,128)(2,1)} %bitcast.17), channel_id=1, source_target_pairs={{0,4},{2,6},{4,0},{6,2},{1,5},{3,7},{5,1},{7,3},{8,12},{10,14},{12... | collective-permute-start | bytes 2359304 | tf_op jit(solution)/shard_map/ppermute | solution.py:48
  3.7 49.7 %collective-permute-start.9 = (bf16[128,3072]{1,0:T(8,128)(2,1)}, bf16[128,3072]{1,0:T(8,128)(2,1)S(1)}, u32[]{:S(2)}, u32[]{:S(2)}) collective-permute-start(bf16[128,3072]{1,0:T(8,128)(2,1)} %bitcast.18), channel_id=1, source_target_pairs={{0,2},{2,0},{4,6},{6,4},{1,3},{3,1},{5,7},{7,5},{8,10},{10,8},{12,... | collective-permute-start | bytes 2359304 | tf_op jit(solution)/shard_map/ppermute | solution.py:48
  21.4 32.0 %collective-permute-start.11 = (bf16[128,3072]{1,0:T(8,128)(2,1)S(1)}, bf16[128,3072]{1,0:T(8,128)(2,1)S(1)}, u32[]{:S(2)}, u32[]{:S(2)}) collective-permute-start(bf16[128,3072]{1,0:T(8,128)(2,1)S(1)} %collective-permute-done.10.refs_6_.refs_2_), channel_id=1, source_target_pairs={{0,2},{2,0},{4,6},{6,4},{1,3},{3,1},{5,7},{7,5},{8,10},{10,8},{12,... | collective-permute-start | bytes 2359304 | tf_op jit(solution)/shard_map/ppermute | solution.py:48
  21.4 1.4 %copy-start.3 = (bf16[1,256,3072]{2,1,0:T(8,128)(2,1)S(1)}, bf16[1,256,3072]{2,1,0:T(8,128)(2,1)}, u32[]{:S(2)}) copy-start(bf16[1,256,3072]{2,1,0:T(8,128)(2,1)} %time_w.1) | copy-start | bytes 4718596
  22.9 0.8 copy-start.8
  23.6 0.7 copy-start.25
  24.3 0.7 copy-start.27
  25.7 19.1 %copy-start = (bf16[1,64,3072]{2,1,0:T(8,128)(2,1)S(1)}, bf16[1,64,3072]{2,1,0:T(8,128)(2,1)}, u32[]{:S(2)}) copy-start(bf16[1,64,3072]{2,1,0:T(8,128)(2,1)} %embed_w.11) | copy-start | bytes 1179652
  25.7 19.1 %copy-start.2 = (bf16[1,3072,1,3,128]{4,1,3,2,0:T(8,128)(2,1)S(1)}, bf16[1,3072,1,3,128]{4,1,3,2,0:T(8,128)(2,1)}, u32[]{:S(2)}) copy-start(bf16[1,3072,1,3,128]{4,1,3,2,0:T(8,128)(2,1)} %param.18) | copy-start | bytes 7077892
  25.7 19.1 %copy-start.28 = (f32[1,2,128]{2,1,0:T(2,128)S(1)}, f32[1,2,128]{2,1,0:T(2,128)}, u32[]{:S(2)}) copy-start(f32[1,2,128]{2,1,0:T(2,128)} %gains.5) | copy-start | bytes 3076
  35.2 21.7 %copy-start.10 = (bf16[128,64]{1,0:T(8,128)(2,1)}, bf16[128,64]{1,0:T(8,128)(2,1)S(1)}, u32[]{:S(2)}) copy-start(bf16[128,64]{1,0:T(8,128)(2,1)S(1)} %get-tuple-element.35.refs_4_.latent.student_rows) | copy-start | bytes 49156
  35.2 18.2 %copy-start.1 = (bf16[1,1,128,3072]{3,2,1,0:T(8,128)(2,1)S(1)}, bf16[1,1,128,3072]{3,2,1,0:T(8,128)(2,1)}, u32[]{:S(2)}) copy-start(bf16[1,1,128,3072]{3,2,1,0:T(8,128)(2,1)} %param.19) | copy-start | bytes 2359300
  35.3 18.2 %copy-start.4 = (bf16[1,3072,64]{1,2,0:T(8,128)(2,1)S(1)}, bf16[1,3072,64]{1,2,0:T(8,128)(2,1)}, u32[]{:S(2)}) copy-start(bf16[1,3072,64]{1,2,0:T(8,128)(2,1)} %param.21) | copy-start | bytes 1179652
  35.3 2.3 %collective-permute-start = (f32[1,3840]{1,0:T(1,128)S(1)}, f32[1,3840]{1,0:T(1,128)S(1)}, u32[]{:S(2)}, u32[]{:S(2)}) collective-permute-start(f32[1,3840]{1,0:T(1,128)S(1)} %get-tuple-element.34.refs_0_), channel_id=1, source_target_pairs={{0,2},{2,0},{4,6},{6,4},{1,3},{3,1},{5,7},{7,5},{8,10},{10,8},{12,... | collective-permute-start | bytes 46088 | tf_op jit(solution)/shard_map/ppermute | solution.py:33
  35.8 3.7 %collective-permute-start.1 = (f32[1,3840]{1,0:T(1,128)S(1)}, f32[1,3840]{1,0:T(1,128)S(1)}, u32[]{:S(2)}, u32[]{:S(2)}) collective-permute-start(f32[1,3840]{1,0:T(1,128)S(1)} %get-tuple-element.34.refs_0_), channel_id=1, source_target_pairs={{0,4},{2,6},{4,0},{6,2},{1,5},{3,7},{5,1},{7,3},{8,12},{10,14},{12... | collective-permute-start | bytes 46088 | tf_op jit(solution)/shard_map/ppermute | solution.py:33
  37.6 3.7 %collective-permute-start.2 = (f32[1,3840]{1,0:T(1,128)S(1)}, f32[1,3840]{1,0:T(1,128)S(1)}, u32[]{:S(2)}, u32[]{:S(2)}) collective-permute-start(f32[1,3840]{1,0:T(1,128)S(1)} %get-tuple-element.34.refs_0_), channel_id=1, source_target_pairs={{0,6},{2,4},{4,2},{6,0},{1,7},{3,5},{5,3},{7,1},{8,14},{10,12},{12... | collective-permute-start | bytes 46088 | tf_op jit(solution)/shard_map/ppermute | solution.py:33
  37.6 3.7 %collective-permute-start.3 = (bf16[128,64]{1,0:T(8,128)(2,1)S(1)}, bf16[128,64]{1,0:T(8,128)(2,1)S(1)}, u32[]{:S(2)}, u32[]{:S(2)}) collective-permute-start(bf16[128,64]{1,0:T(8,128)(2,1)S(1)} %get-tuple-element.35.refs_4_.latent.student_rows), channel_id=1, source_target_pairs={{0,2},{2,0},{4,6},{6,4},{1,3},{3,1},{5,7},{7,5},{8,10},{10,8},{12,... | collective-permute-start | bytes 49160 | tf_op jit(solution)/shard_map/ppermute | solution.py:33
  39.6 3.9 %collective-permute-start.4 = (bf16[128,64]{1,0:T(8,128)(2,1)S(1)}, bf16[128,64]{1,0:T(8,128)(2,1)S(1)}, u32[]{:S(2)}, u32[]{:S(2)}) collective-permute-start(bf16[128,64]{1,0:T(8,128)(2,1)S(1)} %get-tuple-element.35.refs_4_.latent.student_rows), channel_id=1, source_target_pairs={{0,4},{2,6},{4,0},{6,2},{1,5},{3,7},{5,1},{7,3},{8,12},{10,14},{12... | collective-permute-start | bytes 49160 | tf_op jit(solution)/shard_map/ppermute | solution.py:33
  41.3 3.5 %collective-permute-start.5 = (bf16[128,64]{1,0:T(8,128)(2,1)S(1)}, bf16[128,64]{1,0:T(8,128)(2,1)S(1)}, u32[]{:S(2)}, u32[]{:S(2)}) collective-permute-start(bf16[128,64]{1,0:T(8,128)(2,1)S(1)} %get-tuple-element.35.refs_4_.latent.student_rows), channel_id=1, source_target_pairs={{0,6},{2,4},{4,2},{6,0},{1,7},{3,5},{5,3},{7,1},{8,14},{10,12},{12... | collective-permute-start | bytes 49160 | tf_op jit(solution)/shard_map/ppermute | solution.py:33
  49.1 7.8 %copy-start.6 = (f32[1,9216]{1,0:T(1,128)}, f32[1,9216]{1,0:T(1,128)S(1)}, u32[]{:S(2)}) copy-start(f32[1,9216]{1,0:T(1,128)S(1)} %get-tuple-element.36.mod.refs_4_) | copy-start | bytes 110596
  49.1 8.4 %copy-start.12 = (bf16[128,128]{1,0:T(8,128)(2,1)}, bf16[128,128]{1,0:T(8,128)(2,1)S(1)}, u32[]{:S(2)}) copy-start(bf16[128,128]{1,0:T(8,128)(2,1)S(1)} %get-tuple-element.37.refs_0_) | copy-start | bytes 98308
  49.1 1.9 %collective-permute-start.6 = (bf16[128,128]{1,0:T(8,128)(2,1)S(1)}, bf16[128,128]{1,0:T(8,128)(2,1)S(1)}, u32[]{:S(2)}, u32[]{:S(2)}) collective-permute-start(bf16[128,128]{1,0:T(8,128)(2,1)S(1)} %get-tuple-element.38), channel_id=1, source_target_pairs={{0,2},{2,0},{4,6},{6,4},{1,3},{3,1},{5,7},{7,5},{8,10},{10,8},{12,... | collective-permute-start | bytes 98312 | tf_op jit(solution)/shard_map/ppermute | solution.py:38
  49.1 4.2 %collective-permute-start.7 = (bf16[128,128]{1,0:T(8,128)(2,1)S(1)}, bf16[128,128]{1,0:T(8,128)(2,1)S(1)}, u32[]{:S(2)}, u32[]{:S(2)}) collective-permute-start(bf16[128,128]{1,0:T(8,128)(2,1)S(1)} %get-tuple-element.39), channel_id=1, source_target_pairs={{0,4},{2,6},{4,0},{6,2},{1,5},{3,7},{5,1},{7,3},{8,12},{10,14},{12... | collective-permute-start | bytes 98312 | tf_op jit(solution)/shard_map/ppermute | solution.py:38
  49.7 3.7 %collective-permute-start.8 = (bf16[128,128]{1,0:T(8,128)(2,1)S(1)}, bf16[128,128]{1,0:T(8,128)(2,1)S(1)}, u32[]{:S(2)}, u32[]{:S(2)}) collective-permute-start(bf16[128,128]{1,0:T(8,128)(2,1)S(1)} %get-tuple-element.40), channel_id=1, source_target_pairs={{0,6},{2,4},{4,2},{6,0},{1,7},{3,5},{5,3},{7,1},{8,14},{10,12},{12... | collective-permute-start | bytes 98312 | tf_op jit(solution)/shard_map/ppermute | solution.py:38
  51.0 8.5 %copy-start.14 = (bf16[128,128]{1,0:T(8,128)(2,1)}, bf16[128,128]{1,0:T(8,128)(2,1)S(1)}, u32[]{:S(2)}) copy-start(bf16[128,128]{1,0:T(8,128)(2,1)S(1)} %collective-permute-done.6.refs_1_) | copy-start | bytes 98308
  53.3 8.0 %copy-start.16 = (bf16[128,128]{1,0:T(8,128)(2,1)}, bf16[128,128]{1,0:T(8,128)(2,1)S(1)}, u32[]{:S(2)}) copy-start(bf16[128,128]{1,0:T(8,128)(2,1)S(1)} %collective-permute-done.7.refs_2_) | copy-start | bytes 98308
  53.4 9.9 %copy-start.18 = (bf16[128,128]{1,0:T(8,128)(2,1)}, bf16[128,128]{1,0:T(8,128)(2,1)S(1)}, u32[]{:S(2)}) copy-start(bf16[128,128]{1,0:T(8,128)(2,1)S(1)} %collective-permute-done.8.refs_3_) | copy-start | bytes 98308
  53.4 24.9 %copy-start.26 = (s32[2,2]{1,0:T(2,128)S(1)}, s32[2,2]{1,0:T(2,128)}, u32[]{:S(2)}) copy-start(s32[2,2]{1,0:T(2,128)} %times.9) | copy-start | bytes 52
  57.5 7.9 %collective-permute-start.12 = (bf16[128,128]{1,0:T(8,128)(2,1)}, bf16[128,128]{1,0:T(8,128)(2,1)}, u32[]{:S(2)}, u32[]{:S(2)}) collective-permute-start(bf16[128,128]{1,0:T(8,128)(2,1)} %get-tuple-element.41), channel_id=1, source_target_pairs={{0,24},{24,0},{1,25},{25,1},{2,26},{26,2},{3,27},{27,3},{4,28},{28... | collective-permute-start | bytes 98312 | tf_op jit(solution)/shard_map/ppermute | solution.py:648
  59.4 7.0 %collective-permute-start.13 = (bf16[128,128]{1,0:T(8,128)(2,1)}, bf16[128,128]{1,0:T(8,128)(2,1)}, u32[]{:S(2)}, u32[]{:S(2)}) collective-permute-start(bf16[128,128]{1,0:T(8,128)(2,1)} %get-tuple-element.41), channel_id=1, source_target_pairs={{0,16},{16,0},{1,17},{17,1},{2,18},{18,2},{3,19},{19,3},{4,20},{20... | collective-permute-start | bytes 98312 | tf_op jit(solution)/shard_map/ppermute | solution.py:648
  61.4 6.1 %collective-permute-start.14 = (bf16[128,128]{1,0:T(8,128)(2,1)}, bf16[128,128]{1,0:T(8,128)(2,1)}, u32[]{:S(2)}, u32[]{:S(2)}) collective-permute-start(bf16[128,128]{1,0:T(8,128)(2,1)} %get-tuple-element.41), channel_id=1, source_target_pairs={{0,8},{8,0},{1,9},{9,1},{2,10},{10,2},{3,11},{11,3},{4,12},{12,4},... | collective-permute-start | bytes 98312 | tf_op jit(solution)/shard_map/ppermute | solution.py:648
  68.3 1.9 %collective-permute-start.15 = (bf16[128,64]{1,0:T(8,128)(2,1)S(1)}, bf16[128,64]{1,0:T(8,128)(2,1)S(1)}, u32[]{:S(2)}, u32[]{:S(2)}) collective-permute-start(bf16[128,64]{1,0:T(8,128)(2,1)S(1)} %bitcast.25), channel_id=1, source_target_pairs={{0,2},{2,0},{4,6},{6,4},{1,3},{3,1},{5,7},{7,5},{8,10},{10,8},{12,... | collective-permute-start | bytes 49160 | tf_op jit(solution)/shard_map/ppermute | solution.py:33
  68.4 4.0 %collective-permute-start.16 = (bf16[128,64]{1,0:T(8,128)(2,1)S(1)}, bf16[128,64]{1,0:T(8,128)(2,1)S(1)}, u32[]{:S(2)}, u32[]{:S(2)}) collective-permute-start(bf16[128,64]{1,0:T(8,128)(2,1)S(1)} %bitcast.26), channel_id=1, source_target_pairs={{0,4},{2,6},{4,0},{6,2},{1,5},{3,7},{5,1},{7,3},{8,12},{10,14},{12... | collective-permute-start | bytes 49160 | tf_op jit(solution)/shard_map/ppermute | solution.py:33
  69.5 3.4 %collective-permute-start.17 = (bf16[128,64]{1,0:T(8,128)(2,1)S(1)}, bf16[128,64]{1,0:T(8,128)(2,1)S(1)}, u32[]{:S(2)}, u32[]{:S(2)}) collective-permute-start(bf16[128,64]{1,0:T(8,128)(2,1)S(1)} %bitcast.27), channel_id=1, source_target_pairs={{0,6},{2,4},{4,2},{6,0},{1,7},{3,5},{5,3},{7,1},{8,14},{10,12},{12... | collective-permute-start | bytes 49160 | tf_op jit(solution)/shard_map/ppermute | solution.py:33
  72.9 0.9 copy-start.21
  73.8 15.7 %copy-start.22 = (f32[80,384]{1,0:T(8,128)S(1)}, f32[80,384]{1,0:T(8,128)}, u32[]{:S(2)}) copy-start(f32[80,384]{1,0:T(8,128)} %copy-done.20) | copy-start | bytes 368644
  73.8 1.9 %collective-permute-start.18 = (bf16[128,128]{1,0:T(8,128)(2,1)S(1)}, bf16[128,128]{1,0:T(8,128)(2,1)S(1)}, u32[]{:S(2)}, u32[]{:S(2)}) collective-permute-start(bf16[128,128]{1,0:T(8,128)(2,1)S(1)} %get-tuple-element.44), channel_id=1, source_target_pairs={{0,2},{2,0},{4,6},{6,4},{1,3},{3,1},{5,7},{7,5},{8,10},{10,8},{12,... | collective-permute-start | bytes 98312 | tf_op jit(solution)/shard_map/ppermute | solution.py:38
  73.9 3.9 %collective-permute-start.19 = (bf16[128,128]{1,0:T(8,128)(2,1)S(1)}, bf16[128,128]{1,0:T(8,128)(2,1)S(1)}, u32[]{:S(2)}, u32[]{:S(2)}) collective-permute-start(bf16[128,128]{1,0:T(8,128)(2,1)S(1)} %get-tuple-element.45), channel_id=1, source_target_pairs={{0,4},{2,6},{4,0},{6,2},{1,5},{3,7},{5,1},{7,3},{8,12},{10,14},{12... | collective-permute-start | bytes 98312 | tf_op jit(solution)/shard_map/ppermute | solution.py:38
  74.9 3.4 %collective-permute-start.20 = (bf16[128,128]{1,0:T(8,128)(2,1)S(1)}, bf16[128,128]{1,0:T(8,128)(2,1)S(1)}, u32[]{:S(2)}, u32[]{:S(2)}) collective-permute-start(bf16[128,128]{1,0:T(8,128)(2,1)S(1)} %get-tuple-element.46), channel_id=1, source_target_pairs={{0,6},{2,4},{4,2},{6,0},{1,7},{3,5},{5,3},{7,1},{8,14},{10,12},{12... | collective-permute-start | bytes 98312 | tf_op jit(solution)/shard_map/ppermute | solution.py:38
  78.3 1.0 copy-start.5
  79.3 0.8 copy-start.7
  80.1 0.8 copy-start.9
  80.8 24.7 %copy-start.11 = (bf16[128,64]{1,0:T(8,128)(2,1)S(1)}, bf16[128,64]{1,0:T(8,128)(2,1)}, u32[]{:S(2)}) copy-start(bf16[128,64]{1,0:T(8,128)(2,1)} %copy-done.10) | copy-start | bytes 49156
  80.9 24.7 %copy-start.13 = (bf16[128,128]{1,0:T(8,128)(2,1)S(1)}, bf16[128,128]{1,0:T(8,128)(2,1)}, u32[]{:S(2)}) copy-start(bf16[128,128]{1,0:T(8,128)(2,1)} %copy-done.12) | copy-start | bytes 98308
  80.9 24.7 %copy-start.15 = (bf16[128,128]{1,0:T(8,128)(2,1)S(1)}, bf16[128,128]{1,0:T(8,128)(2,1)}, u32[]{:S(2)}) copy-start(bf16[128,128]{1,0:T(8,128)(2,1)} %copy-done.14) | copy-start | bytes 98308
  80.9 24.7 %copy-start.17 = (bf16[128,128]{1,0:T(8,128)(2,1)S(1)}, bf16[128,128]{1,0:T(8,128)(2,1)}, u32[]{:S(2)}) copy-start(bf16[128,128]{1,0:T(8,128)(2,1)} %copy-done.16) | copy-start | bytes 98308
  80.9 24.7 %copy-start.19 = (bf16[128,128]{1,0:T(8,128)(2,1)S(1)}, bf16[128,128]{1,0:T(8,128)(2,1)}, u32[]{:S(2)}) copy-start(bf16[128,128]{1,0:T(8,128)(2,1)} %copy-done.18) | copy-start | bytes 98308
  80.9 24.7 %copy-start.24 = (f32[128,128]{1,0:T(8,128)S(1)}, f32[128,128]{1,0:T(8,128)}, u32[]{:S(2)}) copy-start(f32[128,128]{1,0:T(8,128)} %copy-done.23) | copy-start | bytes 196612
  81.5 8.0 %collective-permute-start.23 = (bf16[128,128]{1,0:T(8,128)(2,1)S(1)}, bf16[128,128]{1,0:T(8,128)(2,1)S(1)}, u32[]{:S(2)}, u32[]{:S(2)}) collective-permute-start(bf16[128,128]{1,0:T(8,128)(2,1)S(1)} %get-tuple-element.54), channel_id=1, source_target_pairs={{0,2},{2,0},{4,6},{6,4},{1,3},{3,1},{5,7},{7,5},{8,10},{10,8},{12,... | collective-permute-start | bytes 98312 | tf_op jit(solution)/shard_map/ppermute | solution.py:38
  81.6 7.8 %collective-permute-start.24 = (bf16[128,128]{1,0:T(8,128)(2,1)S(1)}, bf16[128,128]{1,0:T(8,128)(2,1)S(1)}, u32[]{:S(2)}, u32[]{:S(2)}) collective-permute-start(bf16[128,128]{1,0:T(8,128)(2,1)S(1)} %get-tuple-element.55), channel_id=1, source_target_pairs={{0,4},{2,6},{4,0},{6,2},{1,5},{3,7},{5,1},{7,3},{8,12},{10,14},{12... | collective-permute-start | bytes 98312 | tf_op jit(solution)/shard_map/ppermute | solution.py:38
  82.7 6.7 %collective-permute-start.25 = (bf16[128,128]{1,0:T(8,128)(2,1)S(1)}, bf16[128,128]{1,0:T(8,128)(2,1)S(1)}, u32[]{:S(2)}, u32[]{:S(2)}) collective-permute-start(bf16[128,128]{1,0:T(8,128)(2,1)S(1)} %get-tuple-element.56), channel_id=1, source_target_pairs={{0,6},{2,4},{4,2},{6,0},{1,7},{3,5},{5,3},{7,1},{8,14},{10,12},{12... | collective-permute-start | bytes 98312 | tf_op jit(solution)/shard_map/ppermute | solution.py:38
  83.4 6.0 %collective-permute-start.21 = (bf16[128,64]{1,0:T(8,128)(2,1)S(1)}, bf16[128,64]{1,0:T(8,128)(2,1)S(1)}, u32[]{:S(2)}, u32[]{:S(2)}) collective-permute-start(bf16[128,64]{1,0:T(8,128)(2,1)S(1)} %get-tuple-element.48), channel_id=1, source_target_pairs={{0,16},{8,24},{16,0},{24,8},{1,17},{9,25},{17,1},{25,9},{2,18},{10... | collective-permute-start | bytes 49160 | tf_op jit(solution)/shard_map/ppermute | solution.py:676
  89.5 7.7 %collective-permute-start.26 = (bf16[160,64]{1,0:T(8,128)(2,1)S(1)}, bf16[160,64]{1,0:T(8,128)(2,1)S(1)}, u32[]{:S(2)}, u32[]{:S(2)}) collective-permute-start(bf16[160,64]{1,0:T(8,128)(2,1)S(1)} %get-tuple-element.58), channel_id=1, source_target_pairs={{0,2},{2,0},{4,6},{6,4},{1,3},{3,1},{5,7},{7,5},{8,10},{10,8},{12,... | collective-permute-start | bytes 61448 | tf_op jit(solution)/shard_map/ppermute | solution.py:38
  89.6 7.7 %collective-permute-start.27 = (bf16[160,64]{1,0:T(8,128)(2,1)S(1)}, bf16[160,64]{1,0:T(8,128)(2,1)S(1)}, u32[]{:S(2)}, u32[]{:S(2)}) collective-permute-start(bf16[160,64]{1,0:T(8,128)(2,1)S(1)} %get-tuple-element.59), channel_id=1, source_target_pairs={{0,4},{2,6},{4,0},{6,2},{1,5},{3,7},{5,1},{7,3},{8,12},{10,14},{12... | collective-permute-start | bytes 61448 | tf_op jit(solution)/shard_map/ppermute | solution.py:38
  90.7 6.5 %collective-permute-start.28 = (bf16[160,64]{1,0:T(8,128)(2,1)S(1)}, bf16[160,64]{1,0:T(8,128)(2,1)S(1)}, u32[]{:S(2)}, u32[]{:S(2)}) collective-permute-start(bf16[160,64]{1,0:T(8,128)(2,1)S(1)} %get-tuple-element.60), channel_id=1, source_target_pairs={{0,6},{2,4},{4,2},{6,0},{1,7},{3,5},{5,3},{7,1},{8,14},{10,12},{12... | collective-permute-start | bytes 61448 | tf_op jit(solution)/shard_map/ppermute | solution.py:38
  91.4 5.8 %collective-permute-start.22 = (bf16[128,64]{1,0:T(8,128)(2,1)S(1)}, bf16[128,64]{1,0:T(8,128)(2,1)S(1)}, u32[]{:S(2)}, u32[]{:S(2)}) collective-permute-start(bf16[128,64]{1,0:T(8,128)(2,1)S(1)} %get-tuple-element.48), channel_id=1, source_target_pairs={{0,8},{8,0},{16,24},{24,16},{1,9},{9,1},{17,25},{25,17},{2,10},{10... | collective-permute-start | bytes 49160 | tf_op jit(solution)/shard_map/ppermute | solution.py:675
  97.8 7.7 %collective-permute-start.29 = (bf16[128,64]{1,0:T(8,128)(2,1)S(1)}, bf16[128,64]{1,0:T(8,128)(2,1)S(1)}, u32[]{:S(2)}, u32[]{:S(2)}) collective-permute-start(bf16[128,64]{1,0:T(8,128)(2,1)S(1)} %shard_map.129.own), channel_id=1, source_target_pairs={{0,24},{8,16},{16,8},{24,0},{1,25},{9,17},{17,9},{25,1},{2,26},{10... | collective-permute-start | bytes 49160 | tf_op jit(solution)/shard_map/ppermute | solution.py:701
  106.5 1.3 %collective-permute-start.33 = (bf16[5,64,128]{2,1,0:T(8,128)(2,1)S(1)}, bf16[5,64,128]{2,1,0:T(8,128)(2,1)S(1)}, u32[]{:S(2)}, u32[]{:S(2)}) collective-permute-start(bf16[5,64,128]{2,1,0:T(8,128)(2,1)S(1)} %shard_map.130), channel_id=1, source_target_pairs={{0,2},{2,0},{4,6},{6,4},{1,3},{3,1},{5,7},{7,5},{8,10},{10,8},{12,... | collective-permute-start | bytes 245768 | tf_op jit(solution)/shard_map/ppermute | solution.py:724
  107.9 12.9 %collective-permute-start.34 = (bf16[5,64,128]{2,1,0:T(8,128)(2,1)S(1)}, bf16[5,64,128]{2,1,0:T(8,128)(2,1)S(1)}, u32[]{:S(2)}, u32[]{:S(2)}) collective-permute-start(bf16[5,64,128]{2,1,0:T(8,128)(2,1)S(1)} %add_convert_fusion.refs_6_), channel_id=1, source_target_pairs={{0,4},{1,5},{2,6},{3,7},{4,0},{5,1},{6,2},{7,3},{8,12},{9,13},{10,... | collective-permute-start | bytes 245768 | tf_op jit(solution)/shard_map/ppermute | solution.py:736
  109.0 11.8 %collective-permute-start.35 = (bf16[5,64,128]{2,1,0:T(8,128)(2,1)S(1)}, bf16[5,64,128]{2,1,0:T(8,128)(2,1)S(1)}, u32[]{:S(2)}, u32[]{:S(2)}) collective-permute-start(bf16[5,64,128]{2,1,0:T(8,128)(2,1)S(1)} %add_convert_fusion.refs_6_), channel_id=1, source_target_pairs={{0,1},{1,0},{2,3},{3,2},{4,5},{5,4},{6,7},{7,6},{8,9},{9,8},{10,11... | collective-permute-start | bytes 245768 | tf_op jit(solution)/shard_map/ppermute | solution.py:736
  110.5 10.3 %collective-permute-start.36 = (bf16[5,64,128]{2,1,0:T(8,128)(2,1)S(1)}, bf16[5,64,128]{2,1,0:T(8,128)(2,1)S(1)}, u32[]{:S(2)}, u32[]{:S(2)}) collective-permute-start(bf16[5,64,128]{2,1,0:T(8,128)(2,1)S(1)} %add_convert_fusion.refs_6_), channel_id=1, source_target_pairs={{0,5},{1,4},{2,7},{3,6},{4,1},{5,0},{6,3},{7,2},{8,13},{9,12},{10,... | collective-permute-start | bytes 245768 | tf_op jit(solution)/shard_map/ppermute | solution.py:736
  111.4 4.6 %collective-permute-start.32 = (f32[1,9216]{1,0:T(1,128)S(1)}, f32[1,9216]{1,0:T(1,128)S(1)}, u32[]{:S(2)}, u32[]{:S(2)}) collective-permute-start(f32[1,9216]{1,0:T(1,128)S(1)} %copy-done.7), channel_id=1, source_target_pairs={{0,1},{1,0},{2,3},{3,2},{4,5},{5,4},{6,7},{7,6},{8,9},{9,8},{10,11... | collective-permute-start | bytes 110600 | tf_op jit(solution)/shard_map/ppermute | solution.py:33
  113.1 4.4 %collective-permute-start.30 = (bf16[128,64]{1,0:T(8,128)(2,1)S(1)}, bf16[128,64]{1,0:T(8,128)(2,1)S(1)}, u32[]{:S(2)}, u32[]{:S(2)}) collective-permute-start(bf16[128,64]{1,0:T(8,128)(2,1)S(1)} %shard_map.129.own), channel_id=1, source_target_pairs={{0,8},{8,0},{16,24},{24,16},{1,9},{9,1},{17,25},{25,17},{2,10},{10... | collective-permute-start | bytes 49160 | tf_op jit(solution)/shard_map/ppermute | solution.py:702
  116.0 4.8 %collective-permute-start.31 = (bf16[128,64]{1,0:T(8,128)(2,1)S(1)}, bf16[128,64]{1,0:T(8,128)(2,1)S(1)}, u32[]{:S(2)}, u32[]{:S(2)}) collective-permute-start(bf16[128,64]{1,0:T(8,128)(2,1)S(1)} %shard_map.129.own), channel_id=1, source_target_pairs={{0,16},{8,24},{16,0},{24,8},{1,17},{9,25},{17,1},{25,9},{2,18},{10... | collective-permute-start | bytes 49160 | tf_op jit(solution)/shard_map/ppermute | solution.py:703
  (3 other events, 1.9 us)

commit v5 on v4

--- a/solution.py
+++ b/solution.py
@@ -16,8 +16,7 @@
 STREAMS = 6
 SPARE = 8 << 20
 VMEM = pl.BlockSpec(memory_space=pltpu.VMEM)
-SMEM = pl.BlockSpec(memory_space=pltpu.SMEM)
-ANY = pl.BlockSpec(memory_space=pl.ANY)
+HBM = pl.BlockSpec(memory_space=pltpu.HBM)
 
 
 def halves(values):
@@ -50,6 +49,19 @@
     return [held[offset] for offset in range(count)]
 
 
+def in_order(pieces, own_place):
+    ordered = list(pieces)
+    bit = 1
+    while bit < len(ordered):
+        flipped = (own_place & bit) != 0
+        ordered = [
+            jnp.where(flipped, ordered[place ^ bit], ordered[place])
+            for place in range(len(ordered))
+        ]
+        bit *= 2
+    return ordered
+
+
 def dot32(left, right):
     return jnp.dot(left, right, preferred_element_type=jnp.float32)
 
@@ -66,7 +78,8 @@
     )
 
 
-def steps_of(times_ref):
+def steps_of(times):
+    times_ref = times.ready()
     place = lax.axis_index("dp")
     return (times_ref[place, 0], times_ref[place, 1])
 
@@ -87,63 +100,111 @@
     return total
 
 
-def run(kernel, outputs, operands, specs, flops, scratch=()):
-    in_bytes = sum(operand.size * operand.dtype.itemsize for operand in operands)
-    out_bytes = sum(output.size * output.dtype.itemsize for output in outputs)
-    held = sum(
-        math.prod(ref.shape) * jnp.dtype(ref.dtype).itemsize
-        for ref in scratch
-        if ref.memory_space == pltpu.VMEM
-    )
-    small = sum(
-        operand.size * operand.dtype.itemsize
-        for operand, spec in zip(operands, specs)
-        if spec is VMEM
-    )
-    limit = min(60 << 20, SPARE + held + small + 2 * out_bytes)
+class Fetch:
+    def __init__(self, source, target, arrival):
+        self.copy = pltpu.make_async_copy(source, target, arrival)
+        self.target = target
+        self.waiting = True
+
+    def start(self):
+        self.copy.start()
+
+    def ready(self):
+        if self.waiting:
+            self.copy.wait()
+            self.waiting = False
+        return self.target
+
+
+def bytes_of(items):
+    return sum(math.prod(item.shape) * jnp.dtype(item.dtype).itemsize for item in items)
+
+
+def run(kernel, outputs, operands, flops, scratch=(), fetched=(), streamed=(), sent=()):
+    inputs = len(operands)
+    total = inputs + len(fetched) + len(streamed)
+    results = len(outputs) + len(sent)
+
+    def body(*refs):
+        sources = refs[inputs:total]
+        outs = refs[total : total + results]
+        own = refs[total + results : total + results + len(scratch)]
+        rest = refs[total + results + len(scratch) :]
+        fetches = [
+            Fetch(source, target, rest[-1].at[place])
+            for place, (source, target) in enumerate(zip(sources, rest[:-1]))
+        ]
+        fetches += sources[len(fetched) :]
+        kernel(fetches, *refs[:inputs], *outs, *own)
+
+    places = [
+        (pltpu.SMEM if item.dtype == jnp.int32 else pltpu.VMEM)(item.shape, item.dtype)
+        for item in fetched
+    ]
+    held = bytes_of(
+        [ref for ref in list(scratch) + places if ref.memory_space == pltpu.VMEM]
+    )
+    limit = min(60 << 20, SPARE + held + bytes_of(operands) + 2 * bytes_of(outputs))
     return pl.pallas_call(
-        kernel,
-        out_shape=outputs,
-        in_specs=specs,
-        out_specs=[VMEM] * len(outputs),
-        scratch_shapes=list(scratch),
+        body,
+        out_shape=list(outputs) + list(sent),
+        in_specs=[VMEM] * inputs + [HBM] * (total - inputs),
+        out_specs=[VMEM] * len(outputs) + [HBM] * len(sent),
+        scratch_shapes=list(scratch)
+        + places
+        + [pltpu.SemaphoreType.DMA((max(1, len(fetched)),))],
         compiler_params=pltpu.CompilerParams(vmem_limit_bytes=limit),
         cost_estimate=pl.CostEstimate(
-            flops=flops, bytes_accessed=in_bytes + out_bytes, transcendentals=0
+            flops=flops,
+            bytes_accessed=bytes_of(list(operands) + list(fetched) + list(outputs)),
+            transcendentals=0,
         ),
-    )(*operands)
+    )(*operands, *fetched, *streamed)
 
 
 def array(shape, dtype):
     return jax.ShapeDtypeStruct(shape, dtype)
 
 
-def condition_kernel(times, text, time_w, clean_t, noise, mod_w, mod_out, noisy_out, held, arrivals):
-    model_width = mod_w.shape[1]
+def packed_rows(width):
+    return -(-width // 2048) * 16
+
+
+def condition_kernel(fetches, packed_out, noisy_out, held, mod_rows, arrivals):
+    times, text, time_w, clean_t, noise, mod_w = fetches
+    model_width = held.shape[0]
     rows = model_width // STREAMS
+    for fetch in fetches[:-1]:
+        fetch.start()
     copies = [
         pltpu.make_async_copy(
-            mod_w.at[0, pl.ds(part * rows, rows)], held.at[pl.ds(part * rows, rows)], arrivals.at[part]
+            mod_w.at[pl.ds(part * rows, rows)], held.at[pl.ds(part * rows, rows)], arrivals.at[part]
         )
         for part in range(STREAMS)
     ]
     for copy in copies:
         copy.start()
     student_step, critic_step = steps_of(times)
-    sigma_student = noise_level(student_step)
-    noisy_out[...] = (
-        (1.0 - sigma_student) * clean_t[...].astype(jnp.float32).T
-        + sigma_student * noise[0, :, : clean_t.shape[0]].astype(jnp.float32)
-    ).astype(jnp.bfloat16)
     step = jnp.where(lax.axis_index("segment") == 0, student_step, critic_step)
-    half = text.shape[1] // 2
+    text_ref = text.ready()
+    half = text_ref.shape[1] // 2
     places = lax.broadcasted_iota(jnp.int32, (1, half), 1).astype(jnp.float32)
     frequency = jnp.exp(-math.log(10000.0) * places / half)
     angles = jnp.full((1, half), step, jnp.int32).astype(jnp.float32) * frequency
-    features = jnp.concatenate([jnp.cos(angles), jnp.sin(angles)], axis=1) + text[...]
+    features = jnp.concatenate([jnp.cos(angles), jnp.sin(angles)], axis=1) + text_ref[...]
     features = jnp.broadcast_to(features, (8, 2 * half)).astype(jnp.bfloat16)
-    hidden = dot32(features, time_w[0])
+    hidden = dot32(features, time_w.ready()[...])
     hidden = (hidden / (1.0 + jnp.exp(-hidden))).astype(jnp.bfloat16)
+    sigma_student = noise_level(student_step)
+    clean_ref, noise_ref = clean_t.ready(), noise.ready()
+    noisy = (1.0 - sigma_student) * clean_ref[...].astype(jnp.float32).T + sigma_student * noise_ref[
+        :, : clean_ref.shape[0]
+    ].astype(jnp.float32)
+    noisy = noisy.astype(jnp.bfloat16)
+    noisy_out[...] = noisy
+    top = noisy.shape[0] // 2
+    packed_out[:top] = jnp.concatenate([noisy[:top], noisy[top:]], axis=1)
+    mod_rows[...] = jnp.zeros_like(mod_rows)
     total = None
     for part in range(STREAMS):
         copies[part].wait()
@@ -151,7 +212,12 @@
             hidden[:, part * rows : (part + 1) * rows], held[part * rows : (part + 1) * rows]
         )
         total = piece if total is None else total + piece
-    mod_out[...] = total[:1]
+    width = total.shape[1]
+    for row, first in enumerate(range(0, width, 128)):
+        size = min(128, width - first)
+        mod_rows[row : row + 1, :size] = total[:1, first : first + size]
+    depth = mod_rows.shape[0]
+    packed_out[top : top + depth], packed_out[top + depth :] = halves(mod_rows[...])
 
 
 def rms_scale(values, gain_vec):
@@ -175,10 +241,9 @@
     model_width = central.shape[1]
     count = len(rows)
     head_width = gains.shape[2]
-    short_top, short_low = halves(short[:latent_width])
-    short_shift = short[latent_width : latent_width + 1]
     scale = 1.0 / math.sqrt(head_width)
     size = rows[0].shape[0]
+    short_top = None
     for place in range(count):
         block = rows[place][...]
         squares = None
@@ -187,6 +252,10 @@
             piece = lane_sum(piece * piece)
             squares = piece if squares is None else squares + piece
         inverse = lax.rsqrt(jnp.sum(squares, axis=1, keepdims=True) / model_width + EPS)
+        if short_top is None:
+            values = short()
+            short_top, short_low = halves(values[:latent_width])
+            short_shift = values[latent_width : latent_width + 1]
         projected = inverse * (dot32(block, short_top) + dot32(block, short_low)) + short_shift
         low = place * size
         proj_ref[low : low + size] = projected
@@ -205,17 +274,31 @@
         )
 
 
-def student_front_kernel(count, embed_w, head_w, gains, *refs):
-    mod_parts = refs[:count]
-    rows = refs[count : 2 * count]
-    head_outs = refs[2 * count : 3 * count]
-    short_ref, late_ref, mod, proj_ref, inverse_ref, key_ref, value_ref = refs[3 * count :]
+def student_front_kernel(count, width, fetches, embed_w, head_w, gains, *refs):
+    packed = refs[:count]
+    head_outs = refs[count : 2 * count]
+    short_out, late_out, mod, short_ref, rows_ref, sends, *kept = refs[2 * count :]
     model_width = embed_w.shape[2]
-    width = mod_parts[0].shape[1]
+    latent_width = embed_w.shape[1]
+    size = rows_ref.shape[1]
+    half = size // 2
+    depth = packed_rows(width)
+    parts = [
+        piece[half : half + depth].astype(jnp.float32) + piece[half + depth :].astype(jnp.float32)
+        for piece in packed
+    ]
+    for place, part in enumerate(in_order(parts, lax.axis_index("seq"))):
+        for row, first in enumerate(range(0, width, 128)):
+            lanes = min(128, width - first)
+            low = place * width + first
+            mod[:, low : low + lanes] = part[row : row + 1, :lanes]
+    late = pltpu.make_async_copy(
+        mod.at[:, pl.ds(2 * model_width, 3 * model_width)], late_out, sends.at[0]
+    )
+    late.start()
     for place in range(count):
-        first = pl.multiple_of((lax.axis_index("seq") ^ place) * width, 128)
-        mod[:, pl.ds(first, width)] = mod_parts[place][...]
-    late_ref[...] = mod[:, 2 * model_width :]
+        rows_ref[place, :half] = packed[place][:half, :latent_width]
+        rows_ref[place, half:] = packed[place][:half, latent_width:]
     central = centred(embed_w)
     scale_in = slot_of(mod, 1, model_width, 0, model_width)
     shift_in = slot_of(mod, 0, model_width, 0, model_width)
@@ -227,43 +310,44 @@
     both = jnp.concatenate([dot32(in_both, head_w[kind]) for kind in range(3)], axis=1)
     short = both[: in_rows.shape[0]] + both[in_rows.shape[0] :]
     short_ref[...] = short
+    send = pltpu.make_async_copy(short_ref, short_out, sends.at[1])
+    send.start()
 
     @pl.when(lax.axis_index("segment") == 0)
     def _():
         front(
-            rows,
+            [rows_ref.at[place] for place in range(count)],
             central.astype(jnp.bfloat16),
-            short,
+            lambda: short,
             gains,
             head_outs,
-            proj_ref,
-            inverse_ref,
-            key_ref,
-            value_ref,
+            *kept,
         )
 
-
-def critic_front_kernel(count, short_in, embed_w, gains, *refs):
+    late.wait()
+    send.wait()
+
+
+def critic_front_kernel(count, fetches, embed_w, gains, *refs):
     rows = refs[:count]
     head_outs = refs[count : 2 * count]
-    proj_ref, inverse_ref, key_ref, value_ref = refs[2 * count :]
+    kept = refs[2 * count :]
+    (short,) = fetches
 
     @pl.when(lax.axis_index("segment") != 0)
     def _():
+        short.start()
         front(
             rows,
             centred(embed_w).astype(jnp.bfloat16),
-            short_in[...],
+            lambda: short.ready()[...],
             gains,
             head_outs,
-            proj_ref,
-            inverse_ref,
-            key_ref,
-            value_ref,
+            *kept,
         )
 
 
-def tail(mod, latent, embed_w, final_w, mixed, heads_w, work):
+def tail(late, latent, embed_w, final_t, mixed, heads_w, work):
     model_width = embed_w.shape[2]
     block = latent[...]
     sums = None
@@ -273,6 +357,7 @@
         for piece, rows_w in zip(mixed, heads_w):
             product = dot32(piece[...], rows_w[:, span])
             attended = product if attended is None else attended + product
+        mod = late.ready()
         residual = (
             dot32(block, embed_w[0, :, span]) + slot_of(mod, 0, model_width, first, TILE) * attended
         )
@@ -289,6 +374,7 @@
         sums = part if sums is None else sums + part
     inverse = lax.rsqrt(jnp.sum(sums, axis=1, keepdims=True) / model_width + EPS)
     result = None
+    final_w = final_t.ready()
     for first in range(0, model_width, TILE):
         span = slice(first, first + TILE)
         normed = work[:, span] * inverse
@@ -302,44 +388,61 @@
     return (result, inverse)
 
 
-def student_tail_kernel(count, times, mod, latent, noise, embed_w, final_w, *refs):
+def student_tail_kernel(count, fetches, latent, embed_w, *refs):
     mixed = refs[:count]
     heads_w = refs[count : 2 * count]
-    pair_ref, inverse_ref, work = refs[2 * count :]
+    pair_ref, saved_out, inverse_out, work, inverse_ref, sends = refs[2 * count :]
+    late, final_t, noise, times = fetches
     latent_width = latent.shape[1]
 
     @pl.when(lax.axis_index("segment") == 0)
     def _():
+        for fetch in fetches:
+            fetch.start()
+        copies = [
+            pltpu.make_async_copy(mixed[place], saved_out.at[place], sends.at[place])
+            for place in range(count)
+        ]
+        for copy in copies:
+            copy.start()
+        velocity, inverse = tail(late, latent, embed_w, final_t, mixed, heads_w, work)
+        inverse_ref[...] = jnp.broadcast_to(inverse, inverse_ref.shape)
+        copies.append(pltpu.make_async_copy(inverse_ref, inverse_out, sends.at[count]))
+        copies[-1].start()
         student_step, critic_step = steps_of(times)
         sigma_student, sigma_critic = noise_level(student_step), noise_level(critic_step)
-        velocity, inverse = tail(mod, latent, embed_w, final_w, mixed, heads_w, work)
-        inverse_ref[...] = jnp.broadcast_to(inverse, inverse_ref.shape)
         sample = latent[...].astype(jnp.float32) - sigma_student * velocity
-        second = noise[0, :, latent_width:].astype(jnp.float32)
+        second = noise.ready()[:, latent_width:].astype(jnp.float32)
         critic = (1.0 - sigma_critic) * sample + sigma_critic * second
         pair_ref[...] = jnp.concatenate([critic, sample], axis=1).astype(jnp.bfloat16)
-
-
-def critic_tail_kernel(count, times, mod, pair, noise, embed_w, final_w, *refs):
+        for copy in copies:
+            copy.wait()
+
+
+def critic_tail_kernel(count, fetches, pair, embed_w, *refs):
     mixed = refs[:count]
     heads_w = refs[count : 2 * count]
     grads = refs[2 * count : 3 * count]
     inverse_ref, term_ref, target_ref, direct_ref, latent, work, other = refs[3 * count :]
+    late, final_t, noise, times = fetches
     model_width = embed_w.shape[2]
     latent_width = latent.shape[1]
     section = lax.axis_index("segment")
 
     @pl.when(section != 0)
     def _():
-        _, critic_step = steps_of(times)
-        sigma_critic = noise_level(critic_step)
+        for fetch in fetches:
+            fetch.start()
         both = pair[...].astype(jnp.float32)
         sample = both[:, latent_width:]
         latent[...] = pair[:, :latent_width]
-        result, inverse = tail(mod, latent, embed_w, final_w, mixed, heads_w, work)
+        result, inverse = tail(late, latent, embed_w, final_t, mixed, heads_w, work)
+        mod, final_w = late.ready(), final_t.ready()
+        _, critic_step = steps_of(times)
+        sigma_critic = noise_level(critic_step)
         inverse_ref[...] = jnp.broadcast_to(inverse, inverse_ref.shape)
         term_ref[...] = (sigma_critic * result).astype(jnp.bfloat16)
-        second = noise[0, :, latent_width:].astype(jnp.float32)
+        second = noise.ready()[:, latent_width:].astype(jnp.float32)
         target_ref[...] = jnp.where(
             section == 2,
             2.0 * (result - (second - sample)),
@@ -382,7 +485,7 @@
                 grads[place][...] = totals[place].astype(jnp.bfloat16)
 
 
-def gram_kernel(embed_w, gram_ref):
+def gram_kernel(fetches, embed_w, gram_ref):
     central_top, central_low = halves(centred(embed_w))
     gram = (
         dot32_t(central_top, central_top)
@@ -392,7 +495,7 @@
     gram_ref[0], gram_ref[1] = halves(gram)
 
 
-def judge_back_kernel(count, model_width, short_in, gram, gains, proj_ref, inverse_ref, key_ref, value_ref, pair, real, *refs):
+def judge_back_kernel(count, model_width, fetches, short_in, gram, gains, proj_ref, inverse_ref, key_ref, value_ref, pair, real, *refs):
     rows = refs[:count]
     grads = refs[count : 2 * count]
     outs = refs[2 * count : 3 * count]
@@ -461,13 +564,15 @@
             ).astype(jnp.bfloat16)
 
 
-def merge_kernel(count, times, direct, real, fake, *refs):
+def merge_kernel(count, fetches, direct, real, fake, *refs):
     parts = refs[:count]
     payload_ref = refs[count]
     rows = direct.shape[0]
 
     @pl.when(lax.axis_index("segment") == 3)
     def _():
+        (times,) = fetches
+        times.start()
         total = parts[0][...].astype(jnp.float32)
         for part in parts[1:]:
             total = total + part[...].astype(jnp.float32)
@@ -479,11 +584,19 @@
 
 
 def outer_kernel(
-    count, times, arrived, target_in, student_rows, pair, student_inverse, critic_inverse, *refs
+    count,
+    fetches,
+    arrived,
+    target_in,
+    student_rows,
+    pair,
+    student_mixed,
+    student_inverse,
+    critic_inverse,
+    *refs,
 ):
-    student_mixed = refs[:count]
-    critic_mixed = refs[count : 2 * count]
-    sums_ref = refs[2 * count]
+    critic_mixed = refs[:count]
+    sums_ref = refs[count]
     section = lax.axis_index("segment")
     place = lax.axis_index("seq")
     latent_width = student_rows.shape[1]
@@ -505,9 +618,12 @@
 
     @pl.when(section == 0)
     def _():
+        (times,) = fetches
+        times.start()
         student_step, _ = steps_of(times)
         target = -noise_level(student_step) * arrived[...].astype(jnp.float32)
-        collect(target, student_inverse, student_rows[...], student_mixed)
+        mixed = [student_mixed.at[offset] for offset in range(count)]
+        collect(target, student_inverse, student_rows[...], mixed)
 
     @pl.when(section == 1)
     def _():
@@ -518,11 +634,13 @@
         collect(target_in[...], critic_inverse, pair[:, :latent_width], critic_mixed)
 
 
-def expand_kernel(count, groups, full_rows, own, from_first, from_second, from_third, embed_w, *refs):
+def expand_kernel(
+    count, groups, full_rows, fetches, own, from_first, from_second, from_third, embed_w, *refs
+):
     heads_w = refs[:count]
-    mods = refs[count : count + groups]
-    sums = refs[count + groups : count + 3 * groups]
-    grad_ref, total_ref, work, joined = refs[count + 3 * groups :]
+    other_mods = refs[count : count + groups - 1]
+    sums = refs[count + groups - 1 : count + 3 * groups - 1]
+    grad_ref, total_ref, work, joined = refs[count + 3 * groups - 1 :]
     section = lax.axis_index("segment")
     place = lax.axis_index("seq")
     latent_width = embed_w.shape[1]
@@ -538,23 +656,24 @@
 
     @pl.when(section != 1)
     def _():
+        (late,) = fetches
+        late.start()
         for group in range(groups):
             low = group * latent_width
             joined[:, low : low + latent_width] = sums[2 * group][...].astype(jnp.float32) + sums[
                 2 * group + 1
             ][...].astype(jnp.float32)
-        near_top, near_low = halves(joined[count])
-        heads = [halves(joined[place ^ offset]) for offset in range(count)]
+        near_top = joined[count].astype(jnp.bfloat16)
+        heads = [joined[place ^ offset].astype(jnp.bfloat16) for offset in range(count)]
         averages = None
         for first in range(0, model_width, TILE):
             span = slice(first, first + TILE)
             spread = None
-            for (top, low), rows_w in zip(heads, heads_w):
-                product = dot32(top, rows_w[:, span]) + dot32(low, rows_w[:, span])
+            for head, rows_w in zip(heads, heads_w):
+                product = dot32(head, rows_w[:, span])
                 spread = product if spread is None else spread + product
-            near = dot32(near_top[:, :latent_width], embed_w[0, :, span]) + dot32(
-                near_low[:, :latent_width], embed_w[0, :, span]
-            )
+            near = dot32(near_top[:, :latent_width], embed_w[0, :, span])
+            mods = [late.ready(), *other_mods]
             gates = jnp.concatenate(
                 [
                     jnp.broadcast_to(
@@ -600,16 +719,24 @@
     heads_w = gather_doubling(w_out[0, 0], "seq", count)
     bf16, f32 = jnp.bfloat16, jnp.float32
 
-    mod_piece, noisy_student = run(
+    depth = packed_rows(mod_width)
+    packed, noisy_student = run(
         condition_kernel,
-        [array((1, mod_width), f32), array((tok_rows, latent_width), bf16)],
-        (timesteps, text_vec, w_time, jnp.transpose(clean[0]), noise, w_mod),
-        [SMEM, VMEM, VMEM, VMEM, VMEM, ANY],
+        [
+            array((tok_rows // 2 + 2 * depth, 2 * latent_width), bf16),
+            array((tok_rows, latent_width), bf16),
+        ],
+        (),
         2 * model_width * mod_width,
-        scratch=(pltpu.VMEM((model_width, mod_width), bf16), pltpu.SemaphoreType.DMA((STREAMS,))),
-    )
-    mod_parts = gather_near(mod_piece, "seq", count)
-    student_rows = gather_near(noisy_student, "seq", count)
+        scratch=(
+            pltpu.VMEM((model_width, mod_width), bf16),
+            pltpu.VMEM((depth, 128), f32),
+            pltpu.SemaphoreType.DMA((STREAMS,)),
+        ),
+        fetched=(timesteps, text_vec, w_time[0], jnp.transpose(clean[0]), noise[0]),
+        streamed=(w_mod[0],),
+    )
+    packed_all = gather_near(packed, "seq", count)
 
     head_blocks = [array((tok_rows, head_width), bf16)] * count
     stored = [
@@ -618,36 +745,40 @@
         ((full_rows, head_width), bf16),
         ((full_rows, head_width), bf16),
     ]
+    short_shape = ((latent_width + 16, 3 * head_width), f32)
     *head_outs, short, late_mod = run(
-        functools.partial(student_front_kernel, count),
-        head_blocks
-        + [
-            array((latent_width + 16, 3 * head_width), f32),
-            array((1, 3 * model_width), f32),
-        ],
-        (w_embed, kind_w, qk_gain, *mod_parts, *student_rows),
-        [VMEM] * (3 + 2 * count),
+        functools.partial(student_front_kernel, count, mod_width),
+        head_blocks,
+        (w_embed, kind_w, qk_gain, *packed_all),
         4 * latent_width * model_width * 3 * head_width,
-        scratch=[pltpu.VMEM((1, 5 * model_width), f32)]
+        scratch=[
+            pltpu.VMEM((1, 5 * model_width), f32),
+            pltpu.VMEM(*short_shape),
+            pltpu.VMEM((count, tok_rows, latent_width), bf16),
+            pltpu.SemaphoreType.DMA((2,)),
+        ]
         + [pltpu.VMEM(shape, kind) for shape, kind in stored],
+        sent=[array(*short_shape), array((1, 3 * model_width), f32)],
     )
     student_mixed = scatter_near(head_outs, "seq", count)
     groups = lax.axis_size("dp")
     late_mods = gather_near(late_mod, "dp", groups)
     work = pltpu.VMEM((tok_rows, model_width), f32)
     inverse_shape = array((tok_rows, 128), f32)
-    pair, student_inverse = run(
+    pair, saved, student_inverse = run(
         functools.partial(student_tail_kernel, count),
-        [array((tok_rows, 2 * latent_width), bf16), inverse_shape],
-        (timesteps, late_mod, noisy_student, noise, w_embed, final_w, *student_mixed, *heads_w),
-        [SMEM] + [VMEM] * (5 + 2 * count),
+        [array((tok_rows, 2 * latent_width), bf16)],
+        (noisy_student, w_embed, *student_mixed, *heads_w),
         2 * tok_rows * model_width * head_width * count,
-        scratch=(work,),
-    )
-    moved = [
-        lax.ppermute(pair, "segment", [(0, place), (place, 0)])
-        for place in range(1, sections)
-    ]
+        scratch=(
+            work,
+            pltpu.VMEM((tok_rows, 128), f32),
+            pltpu.SemaphoreType.DMA((count + 1,)),
+        ),
+        fetched=(late_mod, final_w, noise[0], timesteps),
+        sent=[array((count, tok_rows, head_width), bf16), inverse_shape],
+    )
+    moved = [lax.ppermute(pair, "segment", [(0, place)]) for place in range(1, sections)]
     held = moved[0]
     for place in range(2, sections):
         held = jnp.where(section == place, moved[place - 1], held)
@@ -656,9 +787,9 @@
     *head_outs, proj, inverse, keys, values = run(
         functools.partial(critic_front_kernel, count),
         head_blocks + [array(shape, kind) for shape, kind in stored],
-        (short, w_embed, qk_gain, *critic_rows),
-        [VMEM] * (3 + count),
+        (w_embed, qk_gain, *critic_rows),
         4 * latent_width * model_width * full_rows,
+        fetched=(short,),
     )
     critic_mixed = scatter_near(head_outs, "seq", count)
     small = array((tok_rows, latent_width), f32)
@@ -666,10 +797,10 @@
     *grad_heads, critic_inverse, term_rows, target, direct = run(
         functools.partial(critic_tail_kernel, count),
         head_blocks + [inverse_shape, thin, small, small],
-        (timesteps, late_mod, pair, noise, w_embed, final_w, *critic_mixed, *heads_w),
-        [SMEM] + [VMEM] * (5 + 2 * count),
+        (pair, w_embed, *critic_mixed, *heads_w),
         4 * tok_rows * model_width * head_width * count,
         scratch=(pltpu.VMEM((tok_rows, latent_width), bf16), work, work),
+        fetched=(late_mod, final_w, noise[0], timesteps),
     )
     grad_blocks = scatter_near(grad_heads, "seq", count)
     fake = lax.ppermute(term_rows, "segment", swaps(sections, 1))
@@ -678,14 +809,12 @@
         gram_kernel,
         [array((2, latent_width, latent_width), bf16)],
         (w_embed,),
-        [VMEM],
         6 * latent_width * latent_width * model_width,
     )
     parts = run(
         functools.partial(judge_back_kernel, count, model_width),
         [array((tok_rows + 32, latent_width), bf16)] * count,
         (short, gram, qk_gain, proj, inverse, keys, values, pair, real, *critic_rows, *grad_blocks),
-        [VMEM] * (9 + 2 * count),
         10 * full_rows * full_rows * head_width,
         scratch=(pltpu.VMEM((full_rows, head_width), f32),) * 3,
     )
@@ -693,9 +822,9 @@
     (payload,) = run(
         functools.partial(merge_kernel, count),
         [thin],
-        (timesteps, direct, real, fake, *parts),
-        [SMEM] + [VMEM] * (3 + count),
+        (direct, real, fake, *parts),
         1000,
+        fetched=(timesteps,),
     )
     ends = [(place, sections - 1 - place) for place in range(sections)]
     to_student = lax.ppermute(payload, "segment", ends)
@@ -705,18 +834,17 @@
         functools.partial(outer_kernel, count),
         [array((count + 1, latent_width, 128), bf16)],
         (
-            timesteps,
             to_student,
             target,
             noisy_student,
             pair,
+            saved,
             student_inverse,
             critic_inverse,
-            *student_mixed,
             *critic_mixed,
         ),
-        [SMEM] + [VMEM] * (6 + 2 * count),
         2 * tok_rows * latent_width * head_width * (count + 1),
+        fetched=(timesteps,),
     )
     last = count // 2
     bit = 1
@@ -738,22 +866,13 @@
     grad_t, total_t = run(
         functools.partial(expand_kernel, count, groups, full_rows),
         [array((latent_width, tok_rows), f32), array((latent_width, model_width), f32)],
-        (
-            payload,
-            to_student,
-            to_second,
-            to_third,
-            w_embed,
-            *heads_w,
-            *late_mods,
-            *sums_all,
-        ),
-        [VMEM] * (5 + count + 3 * groups),
+        (payload, to_student, to_second, to_third, w_embed, *heads_w, *late_mods[1:], *sums_all),
         4 * groups * latent_width * model_width * head_width * count,
         scratch=(
             pltpu.VMEM((groups * latent_width, model_width), f32),
             pltpu.VMEM((count + 1, groups * latent_width, 128), f32),
         ),
+        fetched=(late_mod,),
     )
     return (jnp.transpose(grad_t)[None], jnp.transpose(total_t)[None])
 

time: 125 us -> 124 us (level)
  starting transfers between devices: 43.3 us -> 47.2 us
  waiting for transfers between devices: 47.5 us -> 44.3 us
  Pallas kernels: 22.9 us -> 20.9 us
    ppermute x1, starting transfers between devices: 3.89 us -> 7.13 us  [step(): fake = lax.ppermute(term_rows, 'segment', swaps(sections, 1))]
    ppermute x3, waiting for transfers between devices: 4.18 us -> 1.3 us  [step(): lax.ppermute(pair, 'segment', [(0, place)])]
    ppermute x1, starting transfers between devices: 5.85 us -> 8.34 us  [step(): to_student = lax.ppermute(payload, 'segment', ends)]
    ppermute x10 -> x7, starting transfers between devices: 8 us -> 5.69 us  [gather_near(): lax.ppermute(value, axis, swaps(count, offset))]
    pallas_call x10, Pallas kernels: 22.9 us -> 20.9 us  [run(): pl.pallas_call(body, out_shape=list(outputs) + list(sent), in_specs=[VMEM...]
    ppermute x1, starting transfers between devices: 4.09 us -> 5.35 us  [step(): real = lax.ppermute(term_rows, 'segment', swaps(sections, 2))]
    ppermute x10 -> x7, waiting for transfers between devices: 10.7 us -> 9.68 us  [gather_near(): lax.ppermute(value, axis, swaps(count, offset))]
    unnamed x60 -> x48, local copies, waits for them, and re-layouts: 9 us -> 9.63 us
  transfers between devices with their start and end apart: 37 -> 34, of which waited for: 19 -> 16; matrix products, arithmetic and copies ran while one was open for 0% -> 0% of each run, Pallas kernels for 11% -> 11%
where the time goes in v5:
time: 124 us
  starting transfers between devices  47.2 us (38%)
  waiting for transfers between devices  44.3 us (36%)
  Pallas kernels  20.9 us (17%)
  local copies, waits for them, and re-layouts  9.63 us (8%)
    pallas_call x10, Pallas kernels, run(): pl.pallas_call(body, out_shape=list(outputs) + list(sent), in_specs=[VMEM...  20.9 us
    ppermute x3, waiting for transfers between devices, gather_doubling(): held[offset | bit] = lax.ppermute(held[offset], axis, swaps(count, bit))  17.8 us
    ppermute x7, waiting for transfers between devices, gather_near(): lax.ppermute(value, axis, swaps(count, offset))  9.68 us
    unnamed x48, local copies, waits for them, and re-layouts  9.63 us
    ppermute x1, starting transfers between devices, step(): to_student = lax.ppermute(payload, 'segment', ends)  8.34 us
    ppermute x12, starting transfers between devices, scatter_near(): lax.ppermute(blocks[offset], axis, swaps(count, offset))  7.63 us
    ppermute x1, starting transfers between devices, step(): fake = lax.ppermute(term_rows, 'segment', swaps(sections, 1))  7.13 us
    ppermute x7, starting transfers between devices, gather_near(): lax.ppermute(value, axis, swaps(count, offset))  5.69 us
  transfers between devices with their start and end apart: 34, of which 16 were waited for; matrix products, arithmetic and copies ran while one was open for 0% of the time, Pallas kernels for 11%

profile of v5, /device:TPU:0, one launch (start us, length us, event | category | flops | bytes accessed | tf_op | source)
XLA Modules:
  0.0 123.8 jit_solution(1429736176922985988)
XLA Ops:
  0.6 3.1 %collective-permute-start.7 = (bf16[128,3072]{1,0:T(8,128)(2,1)}, bf16[128,3072]{1,0:T(8,128)(2,1)S(1)}, u32[]{:S(2)}, u32[]{:S(2)}) collective-permute-start(bf16[128,3072]{1,0:T(8,128)(2,1)} %bitcast.20), channel_id=1, source_target_pairs={{0,4},{2,6},{4,0},{6,2},{1,5},{3,7},{5,1},{7,3},{8,12},{10,14},{12... | collective-permute-start | bytes 2359304 | tf_op jit(solution)/shard_map/ppermute | solution.py:47
  3.7 17.8 %collective-permute-done.7.refs_8_.refs_7_ = bf16[128,3072]{1,0:T(8,128)(2,1)S(1)} collective-permute-done((bf16[128,3072]{1,0:T(8,128)(2,1)}, bf16[128,3072]{1,0:T(8,128)(2,1)S(1)}, u32[]{:S(2)}, u32[]{:S(2)}) %collective-permute-start.7) | collective-permute-done | bytes 786464 | tf_op jit(solution)/shard_map/ppermute | solution.py:47
  21.5 1.4 %copy-done.3 = bf16[1,256,3072]{2,1,0:T(8,128)(2,1)S(1)} copy-done((bf16[1,256,3072]{2,1,0:T(8,128)(2,1)S(1)}, bf16[1,256,3072]{2,1,0:T(8,128)(2,1)}, u32[]{:S(2)}) %copy-start.3) | copy-done | bytes 1572888
  22.9 0.8 copy-done.8
  23.6 0.7 copy-done.19
  24.3 0.7 copy-done.21
  25.0 0.7 copy-done.23
  25.7 8.9 %shard_map.122 = (bf16[128,128]{1,0:T(8,128)(2,1)S(1)}, bf16[128,64]{1,0:T(8,128)(2,1)S(1)}) custom-call(s32[2,2]{1,0:T(2,128)S(1)} %copy-done.19, f32[1,256]{1,0:T(1,128)S(1)} %copy-done.23, bf16[256,3072]{1,0:T(8,128)(2,1)S(1)} %bitcast.26, bf16[64,128]{1,0:T(8,128)(2,1)S(1)} %bitcast.37, bf16[128,128]{1,0:T(8,128)(2,1)S(1)} %bitcast.34, ...), custom_call_target="tpu_custom_call" | custom-call | flops 23592960 | bytes 1672208 | tf_op jit(solution)/shard_map/pallas_call | solution.py:148
  34.6 0.6 collective-permute-start
  35.2 1.7 %collective-permute-start.1 = (bf16[128,128]{1,0:T(8,128)(2,1)S(1)}, bf16[128,128]{1,0:T(8,128)(2,1)S(1)}, u32[]{:S(2)}, u32[]{:S(2)}) collective-permute-start(bf16[128,128]{1,0:T(8,128)(2,1)S(1)} %get-tuple-element.36.refs_3_), channel_id=1, source_target_pairs={{0,4},{2,6},{4,0},{6,2},{1,5},{3,7},{5,1},{7,3},{8,12},{10,14},{12... | collective-permute-start | bytes 98312 | tf_op jit(solution)/shard_map/ppermute | solution.py:32
  36.9 2.2 %collective-permute-done.1.refs_5_ = bf16[128,128]{1,0:T(8,128)(2,1)S(1)} collective-permute-done((bf16[128,128]{1,0:T(8,128)(2,1)S(1)}, bf16[128,128]{1,0:T(8,128)(2,1)S(1)}, u32[]{:S(2)}, u32[]{:S(2)}) %collective-permute-start.1) | collective-permute-done | bytes 32800 | tf_op jit(solution)/shard_map/ppermute | solution.py:32
  39.1 1.5 %collective-permute-done.2.refs_6_ = bf16[128,128]{1,0:T(8,128)(2,1)S(1)} collective-permute-done((bf16[128,128]{1,0:T(8,128)(2,1)S(1)}, bf16[128,128]{1,0:T(8,128)(2,1)S(1)}, u32[]{:S(2)}, u32[]{:S(2)}) %collective-permute-start.2) | collective-permute-done | bytes 32800 | tf_op jit(solution)/shard_map/ppermute | solution.py:32
  40.6 3.9 %shard_map.123 = (bf16[128,128]{1,0:T(8,128)(2,1)S(1)}, bf16[128,128]{1,0:T(8,128)(2,1)S(1)}, bf16[128,128]{1,0:T(8,128)(2,1)S(1)}, bf16[128,128]{1,0:T(8,128)(2...) custom-call(bf16[1,64,3072]{2,1,0:T(8,128)(2,1)S(1)} %copy-done, bf16[3,3072,128]{2,1,0:T(8,128)(2,1)S(1)} %bitcast.25, ...), custom_call_target="tpu_custom_call" | custom-call | flops 301989888 | bytes 3015680 | tf_op jit(solution)/shard_map/pallas_call | solution.py:148
  44.5 0.6 copy-done.14
  45.1 0.1 collective-permute-start.3
  45.2 0.4 collective-permute-start.4
  45.6 1.4 %collective-permute-start.5 = (bf16[128,128]{1,0:T(8,128)(2,1)S(1)}, bf16[128,128]{1,0:T(8,128)(2,1)S(1)}, u32[]{:S(2)}, u32[]{:S(2)}) collective-permute-start(bf16[128,128]{1,0:T(8,128)(2,1)S(1)} %get-tuple-element.40), channel_id=1, source_target_pairs={{0,6},{2,4},{4,2},{6,0},{1,7},{3,5},{5,3},{7,1},{8,14},{10,12},{12... | collective-permute-start | bytes 98312 | tf_op jit(solution)/shard_map/ppermute | solution.py:37
  47.0 2.3 %collective-permute-done.4.refs_4_ = bf16[128,128]{1,0:T(8,128)(2,1)S(1)} collective-permute-done((bf16[128,128]{1,0:T(8,128)(2,1)S(1)}, bf16[128,128]{1,0:T(8,128)(2,1)S(1)}, u32[]{:S(2)}, u32[]{:S(2)}) %collective-permute-start.4) | collective-permute-done | bytes 32800 | tf_op jit(solution)/shard_map/ppermute | solution.py:37
  49.3 3.7 %shard_map.124 = (bf16[128,128]{1,0:T(8,128)(2,1)}, bf16[4,128,128]{2,1,0:T(8,128)(2,1)S(1)}, f32[128,128]{1,0:T(8,128)S(1)}) custom-call(bf16[128,64]{1,0:T(8,128)(2,1)S(1)} %get-tuple-element.35.refs_0_.refs_2_, bf16[1,64,3072]{2,1,0:T(8,128)(2,1)S(1)} %copy-done, bf16[128,128]{1,0:T(8,128)(2,1)S(1)} %get-tuple-element.37.refs_2_, ...), custom_call_target="tpu_custom_call" | custom-call | flops 402653184 | bytes 4182032 | tf_op jit(solution)/shard_map/pallas_call | solution.py:148
  53.1 0.6 copy-done.12
  53.7 0.6 copy-done.17
  54.3 1.9 %collective-permute-start.10 = (bf16[128,128]{1,0:T(8,128)(2,1)}, bf16[128,128]{1,0:T(8,128)(2,1)}, u32[]{:S(2)}, u32[]{:S(2)}) collective-permute-start(bf16[128,128]{1,0:T(8,128)(2,1)} %get-tuple-element.42), channel_id=1, source_target_pairs={{0,16},{1,17},{2,18},{3,19},{4,20},{5,21},{6,22},{7,23}} | collective-permute-start | bytes 98312 | tf_op jit(solution)/shard_map/ppermute | solution.py:781
  56.2 1.9 %collective-permute-start.11 = (bf16[128,128]{1,0:T(8,128)(2,1)}, bf16[128,128]{1,0:T(8,128)(2,1)}, u32[]{:S(2)}, u32[]{:S(2)}) collective-permute-start(bf16[128,128]{1,0:T(8,128)(2,1)} %get-tuple-element.42), channel_id=1, source_target_pairs={{0,8},{1,9},{2,10},{3,11},{4,12},{5,13},{6,14},{7,15}} | collective-permute-start | bytes 98312 | tf_op jit(solution)/shard_map/ppermute | solution.py:781
  58.1 1.9 %collective-permute-start.9 = (bf16[128,128]{1,0:T(8,128)(2,1)}, bf16[128,128]{1,0:T(8,128)(2,1)}, u32[]{:S(2)}, u32[]{:S(2)}) collective-permute-start(bf16[128,128]{1,0:T(8,128)(2,1)} %get-tuple-element.42), channel_id=1, source_target_pairs={{0,24},{1,25},{2,26},{3,27},{4,28},{5,29},{6,30},{7,31}} | collective-permute-start | bytes 98312 | tf_op jit(solution)/shard_map/ppermute | solution.py:781
  60.0 1.3 %collective-permute-done.9 = bf16[128,128]{1,0:T(8,128)(2,1)} collective-permute-done((bf16[128,128]{1,0:T(8,128)(2,1)}, bf16[128,128]{1,0:T(8,128)(2,1)}, u32[]{:S(2)}, u32[]{:S(2)}) %collective-permute-start.9) | collective-permute-done | bytes 32800 | tf_op jit(solution)/shard_map/ppermute | solution.py:781
  61.3 0.8 select_select_fusion.refs_0_.refs_7_.refs_3_
  62.1 0.1 collective-permute-start.12
  62.2 1.4 %collective-permute-start.13 = (bf16[128,64]{1,0:T(8,128)(2,1)S(1)}, bf16[128,64]{1,0:T(8,128)(2,1)S(1)}, u32[]{:S(2)}, u32[]{:S(2)}) collective-permute-start(bf16[128,64]{1,0:T(8,128)(2,1)S(1)} %bitcast.30), channel_id=1, source_target_pairs={{0,4},{2,6},{4,0},{6,2},{1,5},{3,7},{5,1},{7,3},{8,12},{10,14},{12... | collective-permute-start | bytes 49160 | tf_op jit(solution)/shard_map/ppermute | solution.py:32
  63.5 0.5 collective-permute-start.14
  64.0 2.1 %collective-permute-done.13.refs_4_.refs_11_ = bf16[128,64]{1,0:T(8,128)(2,1)S(1)} collective-permute-done((bf16[128,64]{1,0:T(8,128)(2,1)S(1)}, bf16[128,64]{1,0:T(8,128)(2,1)S(1)}, u32[]{:S(2)}, u32[]{:S(2)}) %collective-permute-start.13) | collective-permute-done | bytes 16416 | tf_op jit(solution)/shard_map/ppermute | solution.py:32
  66.1 0.8 collective-permute-done.14.refs_5_.refs_12_
  66.9 0.9 copy-done.15
  67.8 0.2 collective-permute-start.15
  68.0 1.0 collective-permute-start.16
  69.0 0.7 collective-permute-start.17
  69.7 2.2 %collective-permute-done.16.refs_4_.refs_9_ = bf16[128,128]{1,0:T(8,128)(2,1)S(1)} collective-permute-done((bf16[128,128]{1,0:T(8,128)(2,1)S(1)}, bf16[128,128]{1,0:T(8,128)(2,1)S(1)}, u32[]{:S(2)}, u32[]{:S(2)}) %collective-permute-start.16) | collective-permute-done | bytes 32800 | tf_op jit(solution)/shard_map/ppermute | solution.py:37
  72.0 0.5 collective-permute-done.17.refs_5_.refs_10_
  72.4 1.0 copy-done.5
  73.4 0.8 copy-done.7
  74.2 0.8 copy-done.9
  75.0 0.2 collective-permute-start.20
  75.2 1.1 collective-permute-start.21
  76.3 0.7 collective-permute-start.22
  76.9 5.4 %collective-permute-start.18 = (bf16[128,64]{1,0:T(8,128)(2,1)S(1)}, bf16[128,64]{1,0:T(8,128)(2,1)S(1)}, u32[]{:S(2)}, u32[]{:S(2)}) collective-permute-start(bf16[128,64]{1,0:T(8,128)(2,1)S(1)} %get-tuple-element.49), channel_id=1, source_target_pairs={{0,16},{8,24},{16,0},{24,8},{1,17},{9,25},{17,1},{25,9},{2,18},{10... | collective-permute-start | bytes 49160 | tf_op jit(solution)/shard_map/ppermute | solution.py:807
  82.3 0.6 shard_map.127.refs_1_
  82.9 1.3 %collective-permute-done.18.refs_8_.refs_1_ = bf16[128,64]{1,0:T(8,128)(2,1)S(1)} collective-permute-done((bf16[128,64]{1,0:T(8,128)(2,1)S(1)}, bf16[128,64]{1,0:T(8,128)(2,1)S(1)}, u32[]{:S(2)}, u32[]{:S(2)}) %collective-permute-start.18) | collective-permute-done | bytes 16416 | tf_op jit(solution)/shard_map/ppermute | solution.py:807
  84.3 0.1 collective-permute-start.23
  84.4 1.1 collective-permute-start.24
  85.5 0.7 collective-permute-start.25
  86.2 7.1 %collective-permute-start.19 = (bf16[128,64]{1,0:T(8,128)(2,1)S(1)}, bf16[128,64]{1,0:T(8,128)(2,1)S(1)}, u32[]{:S(2)}, u32[]{:S(2)}) collective-permute-start(bf16[128,64]{1,0:T(8,128)(2,1)S(1)} %get-tuple-element.49), channel_id=1, source_target_pairs={{0,8},{8,0},{16,24},{24,16},{1,9},{9,1},{17,25},{25,17},{2,10},{10... | collective-permute-start | bytes 49160 | tf_op jit(solution)/shard_map/ppermute | solution.py:806
  93.4 1.9 %collective-permute-done.19.refs_2_ = bf16[128,64]{1,0:T(8,128)(2,1)S(1)} collective-permute-done((bf16[128,64]{1,0:T(8,128)(2,1)S(1)}, bf16[128,64]{1,0:T(8,128)(2,1)S(1)}, u32[]{:S(2)}, u32[]{:S(2)}) %collective-permute-start.19) | collective-permute-done | bytes 16416 | tf_op jit(solution)/shard_map/ppermute | solution.py:806
  95.3 8.3 %collective-permute-start.26 = (bf16[128,64]{1,0:T(8,128)(2,1)S(1)}, bf16[128,64]{1,0:T(8,128)(2,1)S(1)}, u32[]{:S(2)}, u32[]{:S(2)}) collective-permute-start(bf16[128,64]{1,0:T(8,128)(2,1)S(1)} %shard_map.129.refs_0_), channel_id=1, source_target_pairs={{0,24},{8,16},{16,8},{24,0},{1,25},{9,17},{17,9},{25,1},{2,26},{10... | collective-permute-start | bytes 49160 | tf_op jit(solution)/shard_map/ppermute | solution.py:830
  103.7 1.9 %collective-permute-done.26.refs_0_.refs_1_ = bf16[128,64]{1,0:T(8,128)(2,1)S(1)} collective-permute-done((bf16[128,64]{1,0:T(8,128)(2,1)S(1)}, bf16[128,64]{1,0:T(8,128)(2,1)S(1)}, u32[]{:S(2)}, u32[]{:S(2)}) %collective-permute-start.26) | collective-permute-done | bytes 16416 | tf_op jit(solution)/shard_map/ppermute | solution.py:830
  105.6 0.9 shard_map.130
  106.6 1.3 %collective-permute-done.30 = bf16[5,64,128]{2,1,0:T(8,128)(2,1)S(1)} collective-permute-done((bf16[5,64,128]{2,1,0:T(8,128)(2,1)S(1)}, bf16[5,64,128]{2,1,0:T(8,128)(2,1)S(1)}, u32[]{:S(2)}, u32[]{:S(2)}) %collective-permute-start.30) | collective-permute-done | bytes 81952 | tf_op jit(solution)/shard_map/ppermute | solution.py:852
  107.9 1.2 collective-permute-start.31
  109.1 1.5 %collective-permute-start.32 = (bf16[5,64,128]{2,1,0:T(8,128)(2,1)S(1)}, bf16[5,64,128]{2,1,0:T(8,128)(2,1)S(1)}, u32[]{:S(2)}, u32[]{:S(2)}) collective-permute-start(bf16[5,64,128]{2,1,0:T(8,128)(2,1)S(1)} %add_convert_fusion.refs_10_), channel_id=1, source_target_pairs={{0,1},{1,0},{2,3},{3,2},{4,5},{5,4},{6,7},{7,6},{8,9},{9,8},{10,11... | collective-permute-start | bytes 245768 | tf_op jit(solution)/shard_map/ppermute | solution.py:864
  110.5 0.9 collective-permute-start.33
  111.4 1.5 %collective-permute-start.29 = (f32[1,9216]{1,0:T(1,128)S(1)}, f32[1,9216]{1,0:T(1,128)S(1)}, u32[]{:S(2)}, u32[]{:S(2)}) collective-permute-start(f32[1,9216]{1,0:T(1,128)S(1)} %copy-done.7), channel_id=1, source_target_pairs={{0,1},{1,0},{2,3},{3,2},{4,5},{5,4},{6,7},{7,6},{8,9},{9,8},{10,11... | collective-permute-start | bytes 110600 | tf_op jit(solution)/shard_map/ppermute | solution.py:32
  112.9 3.1 %collective-permute-done.29.refs_9_ = f32[1,9216]{1,0:T(1,128)S(1)} collective-permute-done((f32[1,9216]{1,0:T(1,128)S(1)}, f32[1,9216]{1,0:T(1,128)S(1)}, u32[]{:S(2)}, u32[]{:S(2)}) %collective-permute-start.29) | collective-permute-done | bytes 36896 | tf_op jit(solution)/shard_map/ppermute | solution.py:32
  116.0 0.7 collective-permute-start.28
  116.7 0.1 collective-permute-done.27.refs_2_
  116.8 4.0 %collective-permute-done.28.refs_3_ = bf16[128,64]{1,0:T(8,128)(2,1)S(1)} collective-permute-done((bf16[128,64]{1,0:T(8,128)(2,1)S(1)}, bf16[128,64]{1,0:T(8,128)(2,1)S(1)}, u32[]{:S(2)}, u32[]{:S(2)}) %collective-permute-start.28) | collective-permute-done | bytes 16416 | tf_op jit(solution)/shard_map/ppermute | solution.py:832
  120.9 2.8 %shard_map.131 = (f32[64,128]{1,0:T(8,128)}, f32[64,3072]{1,0:T(8,128)}) custom-call(bf16[128,64]{1,0:T(8,128)(2,1)S(1)} %shard_map.129.refs_0_, bf16[128,64]{1,0:T(8,128)(2,1)S(1)} %collective-permute-done.26.refs_0_.refs_1_, bf16[128,64]{1,0:T(8,128)(2,1)S(1)} %collective-permute-done.27.refs_2_, bf16[128,64]{1,0:T(8,128)(2,1)S(1)} %collective-permute-done.28.refs_3_, ...), custom_call_target="tpu_custom_call" | custom-call | flops 805306368 | bytes 4825088 | tf_op jit(solution)/shard_map/pallas_call | solution.py:148
  (64 shorter events, 0.3 us)
Async XLA Ops:
  0.6 20.8 %collective-permute-start.7 = (bf16[128,3072]{1,0:T(8,128)(2,1)}, bf16[128,3072]{1,0:T(8,128)(2,1)S(1)}, u32[]{:S(2)}, u32[]{:S(2)}) collective-permute-start(bf16[128,3072]{1,0:T(8,128)(2,1)} %bitcast.20), channel_id=1, source_target_pairs={{0,4},{2,6},{4,0},{6,2},{1,5},{3,7},{5,1},{7,3},{8,12},{10,14},{12... | collective-permute-start | bytes 2359304 | tf_op jit(solution)/shard_map/ppermute | solution.py:47
  3.7 45.6 %collective-permute-start.6 = (bf16[128,3072]{1,0:T(8,128)(2,1)}, bf16[128,3072]{1,0:T(8,128)(2,1)S(1)}, u32[]{:S(2)}, u32[]{:S(2)}) collective-permute-start(bf16[128,3072]{1,0:T(8,128)(2,1)} %bitcast.21), channel_id=1, source_target_pairs={{0,2},{2,0},{4,6},{6,4},{1,3},{3,1},{5,7},{7,5},{8,10},{10,8},{12,... | collective-permute-start | bytes 2359304 | tf_op jit(solution)/shard_map/ppermute | solution.py:47
  21.4 27.9 %collective-permute-start.8 = (bf16[128,3072]{1,0:T(8,128)(2,1)S(1)}, bf16[128,3072]{1,0:T(8,128)(2,1)S(1)}, u32[]{:S(2)}, u32[]{:S(2)}) collective-permute-start(bf16[128,3072]{1,0:T(8,128)(2,1)S(1)} %collective-permute-done.7.refs_8_.refs_7_), channel_id=1, source_target_pairs={{0,2},{2,0},{4,6},{6,4},{1,3},{3,1},{5,7},{7,5},{8,10},{10,8},{12,... | collective-permute-start | bytes 2359304 | tf_op jit(solution)/shard_map/ppermute | solution.py:47
  21.4 1.4 %copy-start.3 = (bf16[1,256,3072]{2,1,0:T(8,128)(2,1)S(1)}, bf16[1,256,3072]{2,1,0:T(8,128)(2,1)}, u32[]{:S(2)}) copy-start(bf16[1,256,3072]{2,1,0:T(8,128)(2,1)} %param.16) | copy-start | bytes 4718596
  22.9 0.8 copy-start.8
  23.6 0.7 copy-start.19
  24.3 0.7 copy-start.21
  25.0 0.7 copy-start.23
  25.7 14.9 %copy-start = (bf16[1,64,3072]{2,1,0:T(8,128)(2,1)S(1)}, bf16[1,64,3072]{2,1,0:T(8,128)(2,1)}, u32[]{:S(2)}) copy-start(bf16[1,64,3072]{2,1,0:T(8,128)(2,1)} %refs_4_.1) | copy-start | bytes 1179652
  25.7 14.9 %copy-start.2 = (bf16[1,3072,1,3,128]{4,1,3,2,0:T(8,128)(2,1)S(1)}, bf16[1,3072,1,3,128]{4,1,3,2,0:T(8,128)(2,1)}, u32[]{:S(2)}) copy-start(bf16[1,3072,1,3,128]{4,1,3,2,0:T(8,128)(2,1)} %param.18) | copy-start | bytes 7077892
  25.7 14.9 %copy-start.22 = (f32[1,2,128]{2,1,0:T(2,128)S(1)}, f32[1,2,128]{2,1,0:T(2,128)}, u32[]{:S(2)}) copy-start(f32[1,2,128]{2,1,0:T(2,128)} %refs_2_.3) | copy-start | bytes 3076
  34.6 18.5 %copy-start.10 = (bf16[128,64]{1,0:T(8,128)(2,1)}, bf16[128,64]{1,0:T(8,128)(2,1)S(1)}, u32[]{:S(2)}) copy-start(bf16[128,64]{1,0:T(8,128)(2,1)S(1)} %get-tuple-element.35.refs_0_.refs_2_) | copy-start | bytes 49156
  34.6 14.7 %copy-start.1 = (bf16[1,1,128,3072]{3,2,1,0:T(8,128)(2,1)S(1)}, bf16[1,1,128,3072]{3,2,1,0:T(8,128)(2,1)}, u32[]{:S(2)}) copy-start(bf16[1,1,128,3072]{3,2,1,0:T(8,128)(2,1)} %param.19) | copy-start | bytes 2359300
  34.6 14.7 %copy-start.4 = (bf16[1,3072,64]{1,2,0:T(8,128)(2,1)S(1)}, bf16[1,3072,64]{1,2,0:T(8,128)(2,1)}, u32[]{:S(2)}) copy-start(bf16[1,3072,64]{1,2,0:T(8,128)(2,1)} %param.21) | copy-start | bytes 1179652
  34.6 2.3 %collective-permute-start = (bf16[128,128]{1,0:T(8,128)(2,1)S(1)}, bf16[128,128]{1,0:T(8,128)(2,1)S(1)}, u32[]{:S(2)}, u32[]{:S(2)}) collective-permute-start(bf16[128,128]{1,0:T(8,128)(2,1)S(1)} %get-tuple-element.36.refs_3_), channel_id=1, source_target_pairs={{0,2},{2,0},{4,6},{6,4},{1,3},{3,1},{5,7},{7,5},{8,10},{10,8},{12,... | collective-permute-start | bytes 98312 | tf_op jit(solution)/shard_map/ppermute | solution.py:32
  35.2 3.9 %collective-permute-start.1 = (bf16[128,128]{1,0:T(8,128)(2,1)S(1)}, bf16[128,128]{1,0:T(8,128)(2,1)S(1)}, u32[]{:S(2)}, u32[]{:S(2)}) collective-permute-start(bf16[128,128]{1,0:T(8,128)(2,1)S(1)} %get-tuple-element.36.refs_3_), channel_id=1, source_target_pairs={{0,4},{2,6},{4,0},{6,2},{1,5},{3,7},{5,1},{7,3},{8,12},{10,14},{12... | collective-permute-start | bytes 98312 | tf_op jit(solution)/shard_map/ppermute | solution.py:32
  36.9 3.7 %collective-permute-start.2 = (bf16[128,128]{1,0:T(8,128)(2,1)S(1)}, bf16[128,128]{1,0:T(8,128)(2,1)S(1)}, u32[]{:S(2)}, u32[]{:S(2)}) collective-permute-start(bf16[128,128]{1,0:T(8,128)(2,1)S(1)} %get-tuple-element.36.refs_3_), channel_id=1, source_target_pairs={{0,6},{2,4},{4,2},{6,0},{1,7},{3,5},{5,3},{7,1},{8,14},{10,12},{12... | collective-permute-start | bytes 98312 | tf_op jit(solution)/shard_map/ppermute | solution.py:32
  44.5 0.6 copy-start.14
  45.1 7.9 %copy-start.6 = (f32[1,9216]{1,0:T(1,128)}, f32[1,9216]{1,0:T(1,128)S(1)}, u32[]{:S(2)}) copy-start(f32[1,9216]{1,0:T(1,128)S(1)} %get-tuple-element.41.refs_10_.refs_14_) | copy-start | bytes 110596
  45.1 1.9 %collective-permute-start.3 = (bf16[128,128]{1,0:T(8,128)(2,1)S(1)}, bf16[128,128]{1,0:T(8,128)(2,1)S(1)}, u32[]{:S(2)}, u32[]{:S(2)}) collective-permute-start(bf16[128,128]{1,0:T(8,128)(2,1)S(1)} %get-tuple-element.38), channel_id=1, source_target_pairs={{0,2},{2,0},{4,6},{6,4},{1,3},{3,1},{5,7},{7,5},{8,10},{10,8},{12,... | collective-permute-start | bytes 98312 | tf_op jit(solution)/shard_map/ppermute | solution.py:37
  45.2 4.1 %collective-permute-start.4 = (bf16[128,128]{1,0:T(8,128)(2,1)S(1)}, bf16[128,128]{1,0:T(8,128)(2,1)S(1)}, u32[]{:S(2)}, u32[]{:S(2)}) collective-permute-start(bf16[128,128]{1,0:T(8,128)(2,1)S(1)} %get-tuple-element.39), channel_id=1, source_target_pairs={{0,4},{2,6},{4,0},{6,2},{1,5},{3,7},{5,1},{7,3},{8,12},{10,14},{12... | collective-permute-start | bytes 98312 | tf_op jit(solution)/shard_map/ppermute | solution.py:37
  45.6 3.7 %collective-permute-start.5 = (bf16[128,128]{1,0:T(8,128)(2,1)S(1)}, bf16[128,128]{1,0:T(8,128)(2,1)S(1)}, u32[]{:S(2)}, u32[]{:S(2)}) collective-permute-start(bf16[128,128]{1,0:T(8,128)(2,1)S(1)} %get-tuple-element.40), channel_id=1, source_target_pairs={{0,6},{2,4},{4,2},{6,0},{1,7},{3,5},{5,3},{7,1},{8,14},{10,12},{12... | collective-permute-start | bytes 98312 | tf_op jit(solution)/shard_map/ppermute | solution.py:37
  49.3 23.1 %copy-start.20 = (s32[2,2]{1,0:T(2,128)S(1)}, s32[2,2]{1,0:T(2,128)}, u32[]{:S(2)}) copy-start(s32[2,2]{1,0:T(2,128)} %refs_11_.1) | copy-start | bytes 52
  53.1 0.7 copy-start.12
  53.7 0.6 copy-start.17
  54.3 5.7 %collective-permute-start.10 = (bf16[128,128]{1,0:T(8,128)(2,1)}, bf16[128,128]{1,0:T(8,128)(2,1)}, u32[]{:S(2)}, u32[]{:S(2)}) collective-permute-start(bf16[128,128]{1,0:T(8,128)(2,1)} %get-tuple-element.42), channel_id=1, source_target_pairs={{0,16},{1,17},{2,18},{3,19},{4,20},{5,21},{6,22},{7,23}} | collective-permute-start | bytes 98312 | tf_op jit(solution)/shard_map/ppermute | solution.py:781
  56.2 3.8 %collective-permute-start.11 = (bf16[128,128]{1,0:T(8,128)(2,1)}, bf16[128,128]{1,0:T(8,128)(2,1)}, u32[]{:S(2)}, u32[]{:S(2)}) collective-permute-start(bf16[128,128]{1,0:T(8,128)(2,1)} %get-tuple-element.42), channel_id=1, source_target_pairs={{0,8},{1,9},{2,10},{3,11},{4,12},{5,13},{6,14},{7,15}} | collective-permute-start | bytes 98312 | tf_op jit(solution)/shard_map/ppermute | solution.py:781
  58.1 3.2 %collective-permute-start.9 = (bf16[128,128]{1,0:T(8,128)(2,1)}, bf16[128,128]{1,0:T(8,128)(2,1)}, u32[]{:S(2)}, u32[]{:S(2)}) collective-permute-start(bf16[128,128]{1,0:T(8,128)(2,1)} %get-tuple-element.42), channel_id=1, source_target_pairs={{0,24},{1,25},{2,26},{3,27},{4,28},{5,29},{6,30},{7,31}} | collective-permute-start | bytes 98312 | tf_op jit(solution)/shard_map/ppermute | solution.py:781
  62.1 1.9 %collective-permute-start.12 = (bf16[128,64]{1,0:T(8,128)(2,1)S(1)}, bf16[128,64]{1,0:T(8,128)(2,1)S(1)}, u32[]{:S(2)}, u32[]{:S(2)}) collective-permute-start(bf16[128,64]{1,0:T(8,128)(2,1)S(1)} %bitcast.29), channel_id=1, source_target_pairs={{0,2},{2,0},{4,6},{6,4},{1,3},{3,1},{5,7},{7,5},{8,10},{10,8},{12,... | collective-permute-start | bytes 49160 | tf_op jit(solution)/shard_map/ppermute | solution.py:32
  62.2 4.0 %collective-permute-start.13 = (bf16[128,64]{1,0:T(8,128)(2,1)S(1)}, bf16[128,64]{1,0:T(8,128)(2,1)S(1)}, u32[]{:S(2)}, u32[]{:S(2)}) collective-permute-start(bf16[128,64]{1,0:T(8,128)(2,1)S(1)} %bitcast.30), channel_id=1, source_target_pairs={{0,4},{2,6},{4,0},{6,2},{1,5},{3,7},{5,1},{7,3},{8,12},{10,14},{12... | collective-permute-start | bytes 49160 | tf_op jit(solution)/shard_map/ppermute | solution.py:32
  63.5 3.4 %collective-permute-start.14 = (bf16[128,64]{1,0:T(8,128)(2,1)S(1)}, bf16[128,64]{1,0:T(8,128)(2,1)S(1)}, u32[]{:S(2)}, u32[]{:S(2)}) collective-permute-start(bf16[128,64]{1,0:T(8,128)(2,1)S(1)} %bitcast.31), channel_id=1, source_target_pairs={{0,6},{2,4},{4,2},{6,0},{1,7},{3,5},{5,3},{7,1},{8,14},{10,12},{12... | collective-permute-start | bytes 49160 | tf_op jit(solution)/shard_map/ppermute | solution.py:32
  66.9 0.9 copy-start.15
  67.8 16.5 %copy-start.16 = (f32[80,384]{1,0:T(8,128)S(1)}, f32[80,384]{1,0:T(8,128)}, u32[]{:S(2)}) copy-start(f32[80,384]{1,0:T(8,128)} %copy-done.14) | copy-start | bytes 368644
  67.8 1.9 %collective-permute-start.15 = (bf16[128,128]{1,0:T(8,128)(2,1)S(1)}, bf16[128,128]{1,0:T(8,128)(2,1)S(1)}, u32[]{:S(2)}, u32[]{:S(2)}) collective-permute-start(bf16[128,128]{1,0:T(8,128)(2,1)S(1)} %get-tuple-element.45), channel_id=1, source_target_pairs={{0,2},{2,0},{4,6},{6,4},{1,3},{3,1},{5,7},{7,5},{8,10},{10,8},{12,... | collective-permute-start | bytes 98312 | tf_op jit(solution)/shard_map/ppermute | solution.py:37
  68.0 3.9 %collective-permute-start.16 = (bf16[128,128]{1,0:T(8,128)(2,1)S(1)}, bf16[128,128]{1,0:T(8,128)(2,1)S(1)}, u32[]{:S(2)}, u32[]{:S(2)}) collective-permute-start(bf16[128,128]{1,0:T(8,128)(2,1)S(1)} %get-tuple-element.46), channel_id=1, source_target_pairs={{0,4},{2,6},{4,0},{6,2},{1,5},{3,7},{5,1},{7,3},{8,12},{10,14},{12... | collective-permute-start | bytes 98312 | tf_op jit(solution)/shard_map/ppermute | solution.py:37
  69.0 3.4 %collective-permute-start.17 = (bf16[128,128]{1,0:T(8,128)(2,1)S(1)}, bf16[128,128]{1,0:T(8,128)(2,1)S(1)}, u32[]{:S(2)}, u32[]{:S(2)}) collective-permute-start(bf16[128,128]{1,0:T(8,128)(2,1)S(1)} %get-tuple-element.47), channel_id=1, source_target_pairs={{0,6},{2,4},{4,2},{6,0},{1,7},{3,5},{5,3},{7,1},{8,14},{10,12},{12... | collective-permute-start | bytes 98312 | tf_op jit(solution)/shard_map/ppermute | solution.py:37
  72.4 1.0 copy-start.5
  73.4 0.8 copy-start.7
  74.2 0.8 copy-start.9
  75.0 30.6 %copy-start.11 = (bf16[128,64]{1,0:T(8,128)(2,1)S(1)}, bf16[128,64]{1,0:T(8,128)(2,1)}, u32[]{:S(2)}) copy-start(bf16[128,64]{1,0:T(8,128)(2,1)} %copy-done.10) | copy-start | bytes 49156
  75.0 30.6 %copy-start.13 = (bf16[4,128,128]{2,1,0:T(8,128)(2,1)S(1)}, bf16[4,128,128]{2,1,0:T(8,128)(2,1)}, u32[]{:S(2)}) copy-start(bf16[4,128,128]{2,1,0:T(8,128)(2,1)} %copy-done.12) | copy-start | bytes 393220
  75.0 30.6 %copy-start.18 = (f32[128,128]{1,0:T(8,128)S(1)}, f32[128,128]{1,0:T(8,128)}, u32[]{:S(2)}) copy-start(f32[128,128]{1,0:T(8,128)} %copy-done.17) | copy-start | bytes 196612
  75.0 9.2 %collective-permute-start.20 = (bf16[128,128]{1,0:T(8,128)(2,1)S(1)}, bf16[128,128]{1,0:T(8,128)(2,1)S(1)}, u32[]{:S(2)}, u32[]{:S(2)}) collective-permute-start(bf16[128,128]{1,0:T(8,128)(2,1)S(1)} %get-tuple-element.55), channel_id=1, source_target_pairs={{0,2},{2,0},{4,6},{6,4},{1,3},{3,1},{5,7},{7,5},{8,10},{10,8},{12,... | collective-permute-start | bytes 98312 | tf_op jit(solution)/shard_map/ppermute | solution.py:37
  75.2 9.1 %collective-permute-start.21 = (bf16[128,128]{1,0:T(8,128)(2,1)S(1)}, bf16[128,128]{1,0:T(8,128)(2,1)S(1)}, u32[]{:S(2)}, u32[]{:S(2)}) collective-permute-start(bf16[128,128]{1,0:T(8,128)(2,1)S(1)} %get-tuple-element.56), channel_id=1, source_target_pairs={{0,4},{2,6},{4,0},{6,2},{1,5},{3,7},{5,1},{7,3},{8,12},{10,14},{12... | collective-permute-start | bytes 98312 | tf_op jit(solution)/shard_map/ppermute | solution.py:37
  76.3 8.0 %collective-permute-start.22 = (bf16[128,128]{1,0:T(8,128)(2,1)S(1)}, bf16[128,128]{1,0:T(8,128)(2,1)S(1)}, u32[]{:S(2)}, u32[]{:S(2)}) collective-permute-start(bf16[128,128]{1,0:T(8,128)(2,1)S(1)} %get-tuple-element.57), channel_id=1, source_target_pairs={{0,6},{2,4},{4,2},{6,0},{1,7},{3,5},{5,3},{7,1},{8,14},{10,12},{12... | collective-permute-start | bytes 98312 | tf_op jit(solution)/shard_map/ppermute | solution.py:37
  76.9 7.3 %collective-permute-start.18 = (bf16[128,64]{1,0:T(8,128)(2,1)S(1)}, bf16[128,64]{1,0:T(8,128)(2,1)S(1)}, u32[]{:S(2)}, u32[]{:S(2)}) collective-permute-start(bf16[128,64]{1,0:T(8,128)(2,1)S(1)} %get-tuple-element.49), channel_id=1, source_target_pairs={{0,16},{8,24},{16,0},{24,8},{1,17},{9,25},{17,1},{25,9},{2,18},{10... | collective-permute-start | bytes 49160 | tf_op jit(solution)/shard_map/ppermute | solution.py:807
  84.3 11.0 %collective-permute-start.23 = (bf16[160,64]{1,0:T(8,128)(2,1)S(1)}, bf16[160,64]{1,0:T(8,128)(2,1)S(1)}, u32[]{:S(2)}, u32[]{:S(2)}) collective-permute-start(bf16[160,64]{1,0:T(8,128)(2,1)S(1)} %get-tuple-element.59), channel_id=1, source_target_pairs={{0,2},{2,0},{4,6},{6,4},{1,3},{3,1},{5,7},{7,5},{8,10},{10,8},{12,... | collective-permute-start | bytes 61448 | tf_op jit(solution)/shard_map/ppermute | solution.py:37
  84.4 10.9 %collective-permute-start.24 = (bf16[160,64]{1,0:T(8,128)(2,1)S(1)}, bf16[160,64]{1,0:T(8,128)(2,1)S(1)}, u32[]{:S(2)}, u32[]{:S(2)}) collective-permute-start(bf16[160,64]{1,0:T(8,128)(2,1)S(1)} %get-tuple-element.60), channel_id=1, source_target_pairs={{0,4},{2,6},{4,0},{6,2},{1,5},{3,7},{5,1},{7,3},{8,12},{10,14},{12... | collective-permute-start | bytes 61448 | tf_op jit(solution)/shard_map/ppermute | solution.py:37
  85.5 9.8 %collective-permute-start.25 = (bf16[160,64]{1,0:T(8,128)(2,1)S(1)}, bf16[160,64]{1,0:T(8,128)(2,1)S(1)}, u32[]{:S(2)}, u32[]{:S(2)}) collective-permute-start(bf16[160,64]{1,0:T(8,128)(2,1)S(1)} %get-tuple-element.61), channel_id=1, source_target_pairs={{0,6},{2,4},{4,2},{6,0},{1,7},{3,5},{5,3},{7,1},{8,14},{10,12},{12... | collective-permute-start | bytes 61448 | tf_op jit(solution)/shard_map/ppermute | solution.py:37
  86.2 9.0 %collective-permute-start.19 = (bf16[128,64]{1,0:T(8,128)(2,1)S(1)}, bf16[128,64]{1,0:T(8,128)(2,1)S(1)}, u32[]{:S(2)}, u32[]{:S(2)}) collective-permute-start(bf16[128,64]{1,0:T(8,128)(2,1)S(1)} %get-tuple-element.49), channel_id=1, source_target_pairs={{0,8},{8,0},{16,24},{24,16},{1,9},{9,1},{17,25},{25,17},{2,10},{10... | collective-permute-start | bytes 49160 | tf_op jit(solution)/shard_map/ppermute | solution.py:806
  95.3 10.2 %collective-permute-start.26 = (bf16[128,64]{1,0:T(8,128)(2,1)S(1)}, bf16[128,64]{1,0:T(8,128)(2,1)S(1)}, u32[]{:S(2)}, u32[]{:S(2)}) collective-permute-start(bf16[128,64]{1,0:T(8,128)(2,1)S(1)} %shard_map.129.refs_0_), channel_id=1, source_target_pairs={{0,24},{8,16},{16,8},{24,0},{1,25},{9,17},{17,9},{25,1},{2,26},{10... | collective-permute-start | bytes 49160 | tf_op jit(solution)/shard_map/ppermute | solution.py:830
  106.5 1.3 %collective-permute-start.30 = (bf16[5,64,128]{2,1,0:T(8,128)(2,1)S(1)}, bf16[5,64,128]{2,1,0:T(8,128)(2,1)S(1)}, u32[]{:S(2)}, u32[]{:S(2)}) collective-permute-start(bf16[5,64,128]{2,1,0:T(8,128)(2,1)S(1)} %shard_map.130), channel_id=1, source_target_pairs={{0,2},{2,0},{4,6},{6,4},{1,3},{3,1},{5,7},{7,5},{8,10},{10,8},{12,... | collective-permute-start | bytes 245768 | tf_op jit(solution)/shard_map/ppermute | solution.py:852
  107.9 13.0 %collective-permute-start.31 = (bf16[5,64,128]{2,1,0:T(8,128)(2,1)S(1)}, bf16[5,64,128]{2,1,0:T(8,128)(2,1)S(1)}, u32[]{:S(2)}, u32[]{:S(2)}) collective-permute-start(bf16[5,64,128]{2,1,0:T(8,128)(2,1)S(1)} %add_convert_fusion.refs_10_), channel_id=1, source_target_pairs={{0,4},{1,5},{2,6},{3,7},{4,0},{5,1},{6,2},{7,3},{8,12},{9,13},{10,... | collective-permute-start | bytes 245768 | tf_op jit(solution)/shard_map/ppermute | solution.py:864
  109.1 11.8 %collective-permute-start.32 = (bf16[5,64,128]{2,1,0:T(8,128)(2,1)S(1)}, bf16[5,64,128]{2,1,0:T(8,128)(2,1)S(1)}, u32[]{:S(2)}, u32[]{:S(2)}) collective-permute-start(bf16[5,64,128]{2,1,0:T(8,128)(2,1)S(1)} %add_convert_fusion.refs_10_), channel_id=1, source_target_pairs={{0,1},{1,0},{2,3},{3,2},{4,5},{5,4},{6,7},{7,6},{8,9},{9,8},{10,11... | collective-permute-start | bytes 245768 | tf_op jit(solution)/shard_map/ppermute | solution.py:864
  110.5 10.4 %collective-permute-start.33 = (bf16[5,64,128]{2,1,0:T(8,128)(2,1)S(1)}, bf16[5,64,128]{2,1,0:T(8,128)(2,1)S(1)}, u32[]{:S(2)}, u32[]{:S(2)}) collective-permute-start(bf16[5,64,128]{2,1,0:T(8,128)(2,1)S(1)} %add_convert_fusion.refs_10_), channel_id=1, source_target_pairs={{0,5},{1,4},{2,7},{3,6},{4,1},{5,0},{6,3},{7,2},{8,13},{9,12},{10,... | collective-permute-start | bytes 245768 | tf_op jit(solution)/shard_map/ppermute | solution.py:864
  111.4 4.6 %collective-permute-start.29 = (f32[1,9216]{1,0:T(1,128)S(1)}, f32[1,9216]{1,0:T(1,128)S(1)}, u32[]{:S(2)}, u32[]{:S(2)}) collective-permute-start(f32[1,9216]{1,0:T(1,128)S(1)} %copy-done.7), channel_id=1, source_target_pairs={{0,1},{1,0},{2,3},{3,2},{4,5},{5,4},{6,7},{7,6},{8,9},{9,8},{10,11... | collective-permute-start | bytes 110600 | tf_op jit(solution)/shard_map/ppermute | solution.py:32
  112.9 3.9 %collective-permute-start.27 = (bf16[128,64]{1,0:T(8,128)(2,1)S(1)}, bf16[128,64]{1,0:T(8,128)(2,1)S(1)}, u32[]{:S(2)}, u32[]{:S(2)}) collective-permute-start(bf16[128,64]{1,0:T(8,128)(2,1)S(1)} %shard_map.129.refs_0_), channel_id=1, source_target_pairs={{0,8},{8,0},{16,24},{24,16},{1,9},{9,1},{17,25},{25,17},{2,10},{10... | collective-permute-start | bytes 49160 | tf_op jit(solution)/shard_map/ppermute | solution.py:831
  116.0 4.8 %collective-permute-start.28 = (bf16[128,64]{1,0:T(8,128)(2,1)S(1)}, bf16[128,64]{1,0:T(8,128)(2,1)S(1)}, u32[]{:S(2)}, u32[]{:S(2)}) collective-permute-start(bf16[128,64]{1,0:T(8,128)(2,1)S(1)} %shard_map.129.refs_0_), channel_id=1, source_target_pairs={{0,16},{8,24},{16,0},{24,8},{1,17},{9,25},{17,1},{25,9},{2,18},{10... | collective-permute-start | bytes 49160 | tf_op jit(solution)/shard_map/ppermute | solution.py:832

commit v6 on v5

--- a/solution.py
+++ b/solution.py
@@ -120,6 +120,10 @@
     return sum(math.prod(item.shape) * jnp.dtype(item.dtype).itemsize for item in items)
 
 
+def in_hbm(item):
+    return pltpu.with_memory_space_constraint(item, pltpu.HBM)
+
+
 def run(kernel, outputs, operands, flops, scratch=(), fetched=(), streamed=(), sent=()):
     inputs = len(operands)
     total = inputs + len(fetched) + len(streamed)
@@ -147,7 +151,7 @@
     limit = min(60 << 20, SPARE + held + bytes_of(operands) + 2 * bytes_of(outputs))
     return pl.pallas_call(
         body,
-        out_shape=list(outputs) + list(sent),
+        out_shape=list(outputs) + [pltpu.HBM(item.shape, item.dtype) for item in sent],
         in_specs=[VMEM] * inputs + [HBM] * (total - inputs),
         out_specs=[VMEM] * len(outputs) + [HBM] * len(sent),
         scratch_shapes=list(scratch)
@@ -159,7 +163,7 @@
             bytes_accessed=bytes_of(list(operands) + list(fetched) + list(outputs)),
             transcendentals=0,
         ),
-    )(*operands, *fetched, *streamed)
+    )(*operands, *[in_hbm(item) for item in (*fetched, *streamed)])
 
 
 def array(shape, dtype):
@@ -417,6 +421,19 @@
         pair_ref[...] = jnp.concatenate([critic, sample], axis=1).astype(jnp.bfloat16)
         for copy in copies:
             copy.wait()
+
+
+def pick_kernel(sections, fetches, own, *refs):
+    moved = refs[: sections - 1]
+    pair_ref, rows_ref = refs[sections - 1 :]
+    section = lax.axis_index("segment")
+    for place in range(sections):
+
+        @pl.when(section == place)
+        def _():
+            chosen = own if place == 0 else moved[place - 1]
+            pair_ref[...] = chosen[...]
+            rows_ref[...] = chosen[:, : rows_ref.shape[1]]
 
 
 def critic_tail_kernel(count, fetches, pair, embed_w, *refs):
@@ -705,7 +722,6 @@
 def step(
     clean, noise, timesteps, text_vec, w_embed, w_time, w_mod, w_qkv, w_out, qk_gain, w_final
 ):
-    section = lax.axis_index("segment")
     sections = lax.axis_size("segment")
     tok_rows = clean.shape[1]
     latent_width = clean.shape[2]
@@ -779,11 +795,16 @@
         sent=[array((count, tok_rows, head_width), bf16), inverse_shape],
     )
     moved = [lax.ppermute(pair, "segment", [(0, place)]) for place in range(1, sections)]
-    held = moved[0]
-    for place in range(2, sections):
-        held = jnp.where(section == place, moved[place - 1], held)
-    pair = jnp.where(section == 0, pair, held)
-    critic_rows = gather_near(pair[:, :latent_width], "seq", count)
+    pair, own_rows = run(
+        functools.partial(pick_kernel, sections),
+        [
+            array((tok_rows, 2 * latent_width), bf16),
+            array((tok_rows, latent_width), bf16),
+        ],
+        (pair, *moved),
+        1000,
+    )
+    critic_rows = gather_near(own_rows, "seq", count)
     *head_outs, proj, inverse, keys, values = run(
         functools.partial(critic_front_kernel, count),
         head_blocks + [array(shape, kind) for shape, kind in stored],

time: 124 us -> 114 us (0.919)
  local copies, waits for them, and re-layouts: 9.63 us -> 0.03 us
  starting transfers between devices: 47.2 us -> 44.9 us
  Pallas kernels: 20.9 us -> 22.7 us
    unnamed x48 -> x16, local copies, waits for them, and re-layouts: 9.63 us -> 0.03 us
    ppermute x1, starting transfers between devices: 7.13 us -> 4.68 us  [step(): fake = lax.ppermute(term_rows, 'segment', swaps(sections, 1))]
    ppermute x1, starting transfers between devices: 5.35 us -> 7.21 us  [step(): real = lax.ppermute(term_rows, 'segment', swaps(sections, 2))]
    pallas_call x10 -> x11, Pallas kernels: 20.9 us -> 22.7 us  [run(): pl.pallas_call(body, out_shape=list(outputs) + [pltpu.HBM(item.shape, ite...]
    ppermute x3, starting transfers between devices: 5.65 us -> 3.87 us  [step(): lax.ppermute(pair, 'segment', [(0, place)])]
  transfers between devices with their start and end apart: 34 -> 34, of which waited for: 16 -> 17; matrix products, arithmetic and copies ran while one was open for 0% -> 0% of each run, Pallas kernels for 11% -> 13%
where the time goes in v6:
time: 114 us
  waiting for transfers between devices  45 us (39%)
  starting transfers between devices  44.9 us (39%)
  Pallas kernels  22.7 us (20%)
    pallas_call x11, Pallas kernels, run(): pl.pallas_call(body, out_shape=list(outputs) + [pltpu.HBM(item.shape, ite...  22.7 us
    ppermute x3, waiting for transfers between devices, gather_doubling(): held[offset | bit] = lax.ppermute(held[offset], axis, swaps(count, bit))  17.8 us
    ppermute x7, waiting for transfers between devices, gather_near(): lax.ppermute(value, axis, swaps(count, offset))  9.65 us
    ppermute x1, starting transfers between devices, step(): to_student = lax.ppermute(payload, 'segment', ends)  8.53 us
    ppermute x12, starting transfers between devices, scatter_near(): lax.ppermute(blocks[offset], axis, swaps(count, offset))  7.7 us
    ppermute x1, starting transfers between devices, step(): real = lax.ppermute(term_rows, 'segment', swaps(sections, 2))  7.21 us
    ppermute x7, starting transfers between devices, gather_near(): lax.ppermute(value, axis, swaps(count, offset))  5.66 us
    ppermute x12, waiting for transfers between devices, scatter_near(): lax.ppermute(blocks[offset], axis, swaps(count, offset))  5.03 us
  transfers between devices with their start and end apart: 34, of which 17 were waited for; matrix products, arithmetic and copies ran while one was open for 0% of the time, Pallas kernels for 13%

profile of v6, /device:TPU:0, one launch (start us, length us, event | category | flops | bytes accessed | tf_op | source)
XLA Modules:
  0.0 113.7 jit_solution(8076945828795402451)
XLA Ops:
  0.6 3.1 %collective-permute-start.7 = (bf16[128,3072]{1,0:T(8,128)(2,1)}, bf16[128,3072]{1,0:T(8,128)(2,1)S(1)}, u32[]{:S(2)}, u32[]{:S(2)}) collective-permute-start(bf16[128,3072]{1,0:T(8,128)(2,1)} %bitcast.19), channel_id=1, source_target_pairs={{0,4},{2,6},{4,0},{6,2},{1,5},{3,7},{5,1},{7,3},{8,12},{10,14},{12... | collective-permute-start | bytes 2359304 | tf_op jit(solution)/shard_map/ppermute | solution.py:47
  3.7 17.8 %collective-permute-done.7.refs_8_.refs_7_ = bf16[128,3072]{1,0:T(8,128)(2,1)S(1)} collective-permute-done((bf16[128,3072]{1,0:T(8,128)(2,1)}, bf16[128,3072]{1,0:T(8,128)(2,1)S(1)}, u32[]{:S(2)}, u32[]{:S(2)}) %collective-permute-start.7) | collective-permute-done | bytes 786464 | tf_op jit(solution)/shard_map/ppermute | solution.py:47
  21.5 10.9 %shard_map.122 = (bf16[128,128]{1,0:T(8,128)(2,1)S(1)}, bf16[128,64]{1,0:T(8,128)(2,1)S(1)}) custom-call(s32[2,2]{1,0:T(2,128)} %refs_11_.1, f32[1,256]{1,0:T(1,128)} %refs_1_.4, bf16[256,3072]{1,0:T(8,128)(2,1)} %bitcast.26, bf16[64,128]{1,0:T(8,128)(2,1)} %bitcast.32, bf16[128,128]{1,0:T(8,128)(2,1)} %bitcast.29, bf16[3072,3840]{1,0:T(8,128)(2,1)} %bitcast.25), custom_call_target="tpu_custom_call" | custom-call | flops 23592960 | bytes 1672208 | tf_op jit(solution)/shard_map/pallas_call | solution.py:152
  32.4 0.0 copy-start.1
  32.4 0.6 collective-permute-start
  33.0 1.7 %collective-permute-start.1 = (bf16[128,128]{1,0:T(8,128)(2,1)S(1)}, bf16[128,128]{1,0:T(8,128)(2,1)S(1)}, u32[]{:S(2)}, u32[]{:S(2)}) collective-permute-start(bf16[128,128]{1,0:T(8,128)(2,1)S(1)} %get-tuple-element.38.refs_3_), channel_id=1, source_target_pairs={{0,4},{2,6},{4,0},{6,2},{1,5},{3,7},{5,1},{7,3},{8,12},{10,14},{12... | collective-permute-start | bytes 98312 | tf_op jit(solution)/shard_map/ppermute | solution.py:32
  34.7 0.0 collective-permute-done.refs_4_
  34.7 2.2 %collective-permute-done.1.refs_5_ = bf16[128,128]{1,0:T(8,128)(2,1)S(1)} collective-permute-done((bf16[128,128]{1,0:T(8,128)(2,1)S(1)}, bf16[128,128]{1,0:T(8,128)(2,1)S(1)}, u32[]{:S(2)}, u32[]{:S(2)}) %collective-permute-start.1) | collective-permute-done | bytes 32800 | tf_op jit(solution)/shard_map/ppermute | solution.py:32
  36.9 1.5 %collective-permute-done.2.refs_6_ = bf16[128,128]{1,0:T(8,128)(2,1)S(1)} collective-permute-done((bf16[128,128]{1,0:T(8,128)(2,1)S(1)}, bf16[128,128]{1,0:T(8,128)(2,1)S(1)}, u32[]{:S(2)}, u32[]{:S(2)}) %collective-permute-start.2) | collective-permute-done | bytes 32800 | tf_op jit(solution)/shard_map/ppermute | solution.py:32
  38.4 3.6 %shard_map.123 = (bf16[128,128]{1,0:T(8,128)(2,1)S(1)}, bf16[128,128]{1,0:T(8,128)(2,1)S(1)}, bf16[128,128]{1,0:T(8,128)(2,1)S(1)}, bf16[128,128]{1,0:T(8,128)(2...) custom-call(bf16[1,64,3072]{2,1,0:T(8,128)(2,1)S(1)} %copy-done, bf16[3,3072,128]{2,1,0:T(8,128)(2,1)S(1)} %bitcast.24, ...), custom_call_target="tpu_custom_call" | custom-call | flops 301989888 | bytes 3015680 | tf_op jit(solution)/shard_map/pallas_call | solution.py:152
  42.0 0.2 collective-permute-start.3
  42.2 0.4 collective-permute-start.4
  42.6 1.4 %collective-permute-start.5 = (bf16[128,128]{1,0:T(8,128)(2,1)S(1)}, bf16[128,128]{1,0:T(8,128)(2,1)S(1)}, u32[]{:S(2)}, u32[]{:S(2)}) collective-permute-start(bf16[128,128]{1,0:T(8,128)(2,1)S(1)} %get-tuple-element.42), channel_id=1, source_target_pairs={{0,6},{2,4},{4,2},{6,0},{1,7},{3,5},{5,3},{7,1},{8,14},{10,12},{12... | collective-permute-start | bytes 98312 | tf_op jit(solution)/shard_map/ppermute | solution.py:37
  44.0 2.3 %collective-permute-done.4.refs_4_ = bf16[128,128]{1,0:T(8,128)(2,1)S(1)} collective-permute-done((bf16[128,128]{1,0:T(8,128)(2,1)S(1)}, bf16[128,128]{1,0:T(8,128)(2,1)S(1)}, u32[]{:S(2)}, u32[]{:S(2)}) %collective-permute-start.4) | collective-permute-done | bytes 32800 | tf_op jit(solution)/shard_map/ppermute | solution.py:37
  46.3 2.9 %shard_map.124 = (bf16[128,128]{1,0:T(8,128)(2,1)S(1)}, bf16[4,128,128]{2,1,0:T(8,128)(2,1)}, f32[128,128]{1,0:T(8,128)}) custom-call(bf16[128,64]{1,0:T(8,128)(2,1)S(1)} %get-tuple-element.37.refs_0_.refs_2_, bf16[1,64,3072]{2,1,0:T(8,128)(2,1)S(1)} %copy-done, bf16[128,128]{1,0:T(8,128)(2,1)S(1)} %get-tuple-element.39.refs_2_, ...), custom_call_target="tpu_custom_call" | custom-call | flops 402653184 | bytes 4182032 | tf_op jit(solution)/shard_map/pallas_call | solution.py:152
  49.2 1.3 %collective-permute-start.10 = (bf16[128,128]{1,0:T(8,128)(2,1)S(1)}, bf16[128,128]{1,0:T(8,128)(2,1)S(1)}, u32[]{:S(2)}, u32[]{:S(2)}) collective-permute-start(bf16[128,128]{1,0:T(8,128)(2,1)S(1)} %get-tuple-element.44.refs_0_), channel_id=1, source_target_pairs={{0,16},{1,17},{2,18},{3,19},{4,20},{5,21},{6,22},{7,23}} | collective-permute-start | bytes 98312 | tf_op jit(solution)/shard_map/ppermute | solution.py:797
  50.5 1.3 %collective-permute-start.11 = (bf16[128,128]{1,0:T(8,128)(2,1)S(1)}, bf16[128,128]{1,0:T(8,128)(2,1)S(1)}, u32[]{:S(2)}, u32[]{:S(2)}) collective-permute-start(bf16[128,128]{1,0:T(8,128)(2,1)S(1)} %get-tuple-element.44.refs_0_), channel_id=1, source_target_pairs={{0,24},{1,25},{2,26},{3,27},{4,28},{5,29},{6,30},{7,31}} | collective-permute-start | bytes 98312 | tf_op jit(solution)/shard_map/ppermute | solution.py:797
  51.8 1.3 %collective-permute-start.9 = (bf16[128,128]{1,0:T(8,128)(2,1)S(1)}, bf16[128,128]{1,0:T(8,128)(2,1)S(1)}, u32[]{:S(2)}, u32[]{:S(2)}) collective-permute-start(bf16[128,128]{1,0:T(8,128)(2,1)S(1)} %get-tuple-element.44.refs_0_), channel_id=1, source_target_pairs={{0,8},{1,9},{2,10},{3,11},{4,12},{5,13},{6,14},{7,15}} | collective-permute-start | bytes 98312 | tf_op jit(solution)/shard_map/ppermute | solution.py:797
  53.1 0.0 collective-permute-done.10.refs_2_
  53.2 0.3 collective-permute-done.11.refs_3_
  53.4 1.3 %collective-permute-done.9.refs_1_ = bf16[128,128]{1,0:T(8,128)(2,1)S(1)} collective-permute-done((bf16[128,128]{1,0:T(8,128)(2,1)S(1)}, bf16[128,128]{1,0:T(8,128)(2,1)S(1)}, u32[]{:S(2)}, u32[]{:S(2)}) %collective-permute-start.9) | collective-permute-done | bytes 32800 | tf_op jit(solution)/shard_map/ppermute | solution.py:797
  54.8 0.1 collective-permute-start.12
  54.8 1.4 %collective-permute-start.13 = (bf16[128,64]{1,0:T(8,128)(2,1)S(1)}, bf16[128,64]{1,0:T(8,128)(2,1)S(1)}, u32[]{:S(2)}, u32[]{:S(2)}) collective-permute-start(bf16[128,64]{1,0:T(8,128)(2,1)S(1)} %get-tuple-element.46.refs_2_.refs_9_), channel_id=1, source_target_pairs={{0,4},{2,6},{4,0},{6,2},{1,5},{3,7},{5,1},{7,3},{8,12},{10,14},{12... | collective-permute-start | bytes 49160 | tf_op jit(solution)/shard_map/ppermute | solution.py:32
  56.2 0.5 collective-permute-start.14
  56.7 0.0 collective-permute-done.12.refs_3_.refs_10_
  56.7 2.1 %collective-permute-done.13.refs_4_.refs_11_ = bf16[128,64]{1,0:T(8,128)(2,1)S(1)} collective-permute-done((bf16[128,64]{1,0:T(8,128)(2,1)S(1)}, bf16[128,64]{1,0:T(8,128)(2,1)S(1)}, u32[]{:S(2)}, u32[]{:S(2)}) %collective-permute-start.13) | collective-permute-done | bytes 16416 | tf_op jit(solution)/shard_map/ppermute | solution.py:32
  58.8 0.7 collective-permute-done.14.refs_5_.refs_12_
  59.6 0.2 collective-permute-start.15
  59.8 1.0 collective-permute-start.16
  60.8 0.7 collective-permute-start.17
  61.5 0.0 collective-permute-done.15.refs_3_.refs_8_
  61.5 2.2 %collective-permute-done.16.refs_4_.refs_9_ = bf16[128,128]{1,0:T(8,128)(2,1)S(1)} collective-permute-done((bf16[128,128]{1,0:T(8,128)(2,1)S(1)}, bf16[128,128]{1,0:T(8,128)(2,1)S(1)}, u32[]{:S(2)}, u32[]{:S(2)}) %collective-permute-start.16) | collective-permute-done | bytes 32800 | tf_op jit(solution)/shard_map/ppermute | solution.py:37
  63.7 0.5 collective-permute-done.17.refs_5_.refs_10_
  64.3 0.2 collective-permute-start.20
  64.5 1.0 collective-permute-start.21
  65.5 0.7 collective-permute-start.22
  66.2 7.2 %collective-permute-start.18 = (bf16[128,64]{1,0:T(8,128)(2,1)S(1)}, bf16[128,64]{1,0:T(8,128)(2,1)S(1)}, u32[]{:S(2)}, u32[]{:S(2)}) collective-permute-start(bf16[128,64]{1,0:T(8,128)(2,1)S(1)} %get-tuple-element.53), channel_id=1, source_target_pairs={{0,16},{8,24},{16,0},{24,8},{1,17},{9,25},{17,1},{25,9},{2,18},{10... | collective-permute-start | bytes 49160 | tf_op jit(solution)/shard_map/ppermute | solution.py:828
  73.4 0.6 shard_map.128.refs_1_
  74.1 1.3 %collective-permute-done.18.refs_8_.refs_1_ = bf16[128,64]{1,0:T(8,128)(2,1)S(1)} collective-permute-done((bf16[128,64]{1,0:T(8,128)(2,1)S(1)}, bf16[128,64]{1,0:T(8,128)(2,1)S(1)}, u32[]{:S(2)}, u32[]{:S(2)}) %collective-permute-start.18) | collective-permute-done | bytes 16416 | tf_op jit(solution)/shard_map/ppermute | solution.py:828
  75.4 0.0 collective-permute-done.22.refs_16_
  75.4 0.1 collective-permute-start.23
  75.5 1.1 collective-permute-start.24
  76.6 0.8 collective-permute-start.25
  77.4 4.7 %collective-permute-start.19 = (bf16[128,64]{1,0:T(8,128)(2,1)S(1)}, bf16[128,64]{1,0:T(8,128)(2,1)S(1)}, u32[]{:S(2)}, u32[]{:S(2)}) collective-permute-start(bf16[128,64]{1,0:T(8,128)(2,1)S(1)} %get-tuple-element.53), channel_id=1, source_target_pairs={{0,8},{8,0},{16,24},{24,16},{1,9},{9,1},{17,25},{25,17},{2,10},{10... | collective-permute-start | bytes 49160 | tf_op jit(solution)/shard_map/ppermute | solution.py:827
  82.0 1.9 %collective-permute-done.19.refs_2_ = bf16[128,64]{1,0:T(8,128)(2,1)S(1)} collective-permute-done((bf16[128,64]{1,0:T(8,128)(2,1)S(1)}, bf16[128,64]{1,0:T(8,128)(2,1)S(1)}, u32[]{:S(2)}, u32[]{:S(2)}) %collective-permute-start.19) | collective-permute-done | bytes 16416 | tf_op jit(solution)/shard_map/ppermute | solution.py:827
  84.0 0.0 collective-permute-done.23.refs_4_
  84.0 0.0 collective-permute-done.24.refs_5_
  84.0 0.0 collective-permute-done.25.refs_6_
  84.0 8.5 %collective-permute-start.26 = (bf16[128,64]{1,0:T(8,128)(2,1)S(1)}, bf16[128,64]{1,0:T(8,128)(2,1)S(1)}, u32[]{:S(2)}, u32[]{:S(2)}) collective-permute-start(bf16[128,64]{1,0:T(8,128)(2,1)S(1)} %shard_map.130.refs_0_), channel_id=1, source_target_pairs={{0,24},{8,16},{16,8},{24,0},{1,25},{9,17},{17,9},{25,1},{2,26},{10... | collective-permute-start | bytes 49160 | tf_op jit(solution)/shard_map/ppermute | solution.py:851
  92.5 1.9 %collective-permute-done.26.refs_0_.refs_1_ = bf16[128,64]{1,0:T(8,128)(2,1)S(1)} collective-permute-done((bf16[128,64]{1,0:T(8,128)(2,1)S(1)}, bf16[128,64]{1,0:T(8,128)(2,1)S(1)}, u32[]{:S(2)}, u32[]{:S(2)}) %collective-permute-start.26) | collective-permute-done | bytes 16416 | tf_op jit(solution)/shard_map/ppermute | solution.py:851
  94.4 1.1 shard_map.131
  95.5 0.1 collective-permute-start.30
  95.6 1.3 %collective-permute-done.30 = bf16[5,64,128]{2,1,0:T(8,128)(2,1)S(1)} collective-permute-done((bf16[5,64,128]{2,1,0:T(8,128)(2,1)S(1)}, bf16[5,64,128]{2,1,0:T(8,128)(2,1)S(1)}, u32[]{:S(2)}, u32[]{:S(2)}) %collective-permute-start.30) | collective-permute-done | bytes 81952 | tf_op jit(solution)/shard_map/ppermute | solution.py:873
  96.9 1.1 collective-permute-start.31
  98.0 1.5 %collective-permute-start.32 = (bf16[5,64,128]{2,1,0:T(8,128)(2,1)S(1)}, bf16[5,64,128]{2,1,0:T(8,128)(2,1)S(1)}, u32[]{:S(2)}, u32[]{:S(2)}) collective-permute-start(bf16[5,64,128]{2,1,0:T(8,128)(2,1)S(1)} %add_convert_fusion.refs_10_), channel_id=1, source_target_pairs={{0,1},{1,0},{2,3},{3,2},{4,5},{5,4},{6,7},{7,6},{8,9},{9,8},{10,11... | collective-permute-start | bytes 245768 | tf_op jit(solution)/shard_map/ppermute | solution.py:885
  99.5 1.0 collective-permute-start.33
  100.4 1.4 %collective-permute-start.29 = (f32[1,9216]{1,0:T(1,128)S(1)}, f32[1,9216]{1,0:T(1,128)S(1)}, u32[]{:S(2)}, u32[]{:S(2)}) collective-permute-start(f32[1,9216]{1,0:T(1,128)S(1)} %copy-done.7), channel_id=1, source_target_pairs={{0,1},{1,0},{2,3},{3,2},{4,5},{5,4},{6,7},{7,6},{8,9},{9,8},{10,11... | collective-permute-start | bytes 110600 | tf_op jit(solution)/shard_map/ppermute | solution.py:32
  101.9 3.1 %collective-permute-done.29.refs_9_ = f32[1,9216]{1,0:T(1,128)S(1)} collective-permute-done((f32[1,9216]{1,0:T(1,128)S(1)}, f32[1,9216]{1,0:T(1,128)S(1)}, u32[]{:S(2)}, u32[]{:S(2)}) %collective-permute-start.29) | collective-permute-done | bytes 36896 | tf_op jit(solution)/shard_map/ppermute | solution.py:32
  105.0 0.6 collective-permute-start.28
  105.5 0.2 collective-permute-done.27.refs_2_
  105.8 4.4 %collective-permute-done.28.refs_3_ = bf16[128,64]{1,0:T(8,128)(2,1)S(1)} collective-permute-done((bf16[128,64]{1,0:T(8,128)(2,1)S(1)}, bf16[128,64]{1,0:T(8,128)(2,1)S(1)}, u32[]{:S(2)}, u32[]{:S(2)}) %collective-permute-start.28) | collective-permute-done | bytes 16416 | tf_op jit(solution)/shard_map/ppermute | solution.py:853
  110.1 0.0 collective-permute-done.31.refs_11_
  110.1 0.0 collective-permute-done.32.refs_12_
  110.2 3.3 %shard_map.132 = (f32[64,128]{1,0:T(8,128)}, f32[64,3072]{1,0:T(8,128)}) custom-call(bf16[128,64]{1,0:T(8,128)(2,1)S(1)} %shard_map.130.refs_0_, bf16[128,64]{1,0:T(8,128)(2,1)S(1)} %collective-permute-done.26.refs_0_.refs_1_, bf16[128,64]{1,0:T(8,128)(2,1)S(1)} %collective-permute-done.27.refs_2_, bf16[128,64]{1,0:T(8,128)(2,1)S(1)} %collective-permute-done.28.refs_3_, ...), custom_call_target="tpu_custom_call" | custom-call | flops 805306368 | bytes 4825088 | tf_op jit(solution)/shard_map/pallas_call | solution.py:152
  (32 shorter events, 0.2 us)
Async XLA Ops:
  0.6 20.8 %collective-permute-start.7 = (bf16[128,3072]{1,0:T(8,128)(2,1)}, bf16[128,3072]{1,0:T(8,128)(2,1)S(1)}, u32[]{:S(2)}, u32[]{:S(2)}) collective-permute-start(bf16[128,3072]{1,0:T(8,128)(2,1)} %bitcast.19), channel_id=1, source_target_pairs={{0,4},{2,6},{4,0},{6,2},{1,5},{3,7},{5,1},{7,3},{8,12},{10,14},{12... | collective-permute-start | bytes 2359304 | tf_op jit(solution)/shard_map/ppermute | solution.py:47
  3.7 42.6 %collective-permute-start.6 = (bf16[128,3072]{1,0:T(8,128)(2,1)}, bf16[128,3072]{1,0:T(8,128)(2,1)S(1)}, u32[]{:S(2)}, u32[]{:S(2)}) collective-permute-start(bf16[128,3072]{1,0:T(8,128)(2,1)} %bitcast.20), channel_id=1, source_target_pairs={{0,2},{2,0},{4,6},{6,4},{1,3},{3,1},{5,7},{7,5},{8,10},{10,8},{12,... | collective-permute-start | bytes 2359304 | tf_op jit(solution)/shard_map/ppermute | solution.py:47
  21.4 24.8 %collective-permute-start.8 = (bf16[128,3072]{1,0:T(8,128)(2,1)S(1)}, bf16[128,3072]{1,0:T(8,128)(2,1)S(1)}, u32[]{:S(2)}, u32[]{:S(2)}) collective-permute-start(bf16[128,3072]{1,0:T(8,128)(2,1)S(1)} %collective-permute-done.7.refs_8_.refs_7_), channel_id=1, source_target_pairs={{0,2},{2,0},{4,6},{6,4},{1,3},{3,1},{5,7},{7,5},{8,10},{10,8},{12,... | collective-permute-start | bytes 2359304 | tf_op jit(solution)/shard_map/ppermute | solution.py:47
  21.4 16.9 %copy-start = (bf16[1,64,3072]{2,1,0:T(8,128)(2,1)S(1)}, bf16[1,64,3072]{2,1,0:T(8,128)(2,1)}, u32[]{:S(2)}) copy-start(bf16[1,64,3072]{2,1,0:T(8,128)(2,1)} %refs_4_.1) | copy-start | bytes 1179652
  21.5 16.9 %copy-start.2 = (bf16[1,3072,1,3,128]{4,1,3,2,0:T(8,128)(2,1)S(1)}, bf16[1,3072,1,3,128]{4,1,3,2,0:T(8,128)(2,1)}, u32[]{:S(2)}) copy-start(bf16[1,3072,1,3,128]{4,1,3,2,0:T(8,128)(2,1)} %param.18) | copy-start | bytes 7077892
  21.5 16.9 %copy-start.6 = (f32[1,2,128]{2,1,0:T(2,128)S(1)}, f32[1,2,128]{2,1,0:T(2,128)}, u32[]{:S(2)}) copy-start(f32[1,2,128]{2,1,0:T(2,128)} %refs_2_.3) | copy-start | bytes 3076
  32.4 13.9 %copy-start.1 = (bf16[1,1,128,3072]{3,2,1,0:T(8,128)(2,1)S(1)}, bf16[1,1,128,3072]{3,2,1,0:T(8,128)(2,1)}, u32[]{:S(2)}) copy-start(bf16[1,1,128,3072]{3,2,1,0:T(8,128)(2,1)} %param.19) | copy-start | bytes 2359300
  32.4 2.3 %collective-permute-start = (bf16[128,128]{1,0:T(8,128)(2,1)S(1)}, bf16[128,128]{1,0:T(8,128)(2,1)S(1)}, u32[]{:S(2)}, u32[]{:S(2)}) collective-permute-start(bf16[128,128]{1,0:T(8,128)(2,1)S(1)} %get-tuple-element.38.refs_3_), channel_id=1, source_target_pairs={{0,2},{2,0},{4,6},{6,4},{1,3},{3,1},{5,7},{7,5},{8,10},{10,8},{12,... | collective-permute-start | bytes 98312 | tf_op jit(solution)/shard_map/ppermute | solution.py:32
  33.0 3.9 %collective-permute-start.1 = (bf16[128,128]{1,0:T(8,128)(2,1)S(1)}, bf16[128,128]{1,0:T(8,128)(2,1)S(1)}, u32[]{:S(2)}, u32[]{:S(2)}) collective-permute-start(bf16[128,128]{1,0:T(8,128)(2,1)S(1)} %get-tuple-element.38.refs_3_), channel_id=1, source_target_pairs={{0,4},{2,6},{4,0},{6,2},{1,5},{3,7},{5,1},{7,3},{8,12},{10,14},{12... | collective-permute-start | bytes 98312 | tf_op jit(solution)/shard_map/ppermute | solution.py:32
  34.7 3.7 %collective-permute-start.2 = (bf16[128,128]{1,0:T(8,128)(2,1)S(1)}, bf16[128,128]{1,0:T(8,128)(2,1)S(1)}, u32[]{:S(2)}, u32[]{:S(2)}) collective-permute-start(bf16[128,128]{1,0:T(8,128)(2,1)S(1)} %get-tuple-element.38.refs_3_), channel_id=1, source_target_pairs={{0,6},{2,4},{4,2},{6,0},{1,7},{3,5},{5,3},{7,1},{8,14},{10,12},{12... | collective-permute-start | bytes 98312 | tf_op jit(solution)/shard_map/ppermute | solution.py:32
  42.0 1.9 %collective-permute-start.3 = (bf16[128,128]{1,0:T(8,128)(2,1)S(1)}, bf16[128,128]{1,0:T(8,128)(2,1)S(1)}, u32[]{:S(2)}, u32[]{:S(2)}) collective-permute-start(bf16[128,128]{1,0:T(8,128)(2,1)S(1)} %get-tuple-element.40), channel_id=1, source_target_pairs={{0,2},{2,0},{4,6},{6,4},{1,3},{3,1},{5,7},{7,5},{8,10},{10,8},{12,... | collective-permute-start | bytes 98312 | tf_op jit(solution)/shard_map/ppermute | solution.py:37
  42.2 4.1 %collective-permute-start.4 = (bf16[128,128]{1,0:T(8,128)(2,1)S(1)}, bf16[128,128]{1,0:T(8,128)(2,1)S(1)}, u32[]{:S(2)}, u32[]{:S(2)}) collective-permute-start(bf16[128,128]{1,0:T(8,128)(2,1)S(1)} %get-tuple-element.41), channel_id=1, source_target_pairs={{0,4},{2,6},{4,0},{6,2},{1,5},{3,7},{5,1},{7,3},{8,12},{10,14},{12... | collective-permute-start | bytes 98312 | tf_op jit(solution)/shard_map/ppermute | solution.py:37
  42.6 3.7 %collective-permute-start.5 = (bf16[128,128]{1,0:T(8,128)(2,1)S(1)}, bf16[128,128]{1,0:T(8,128)(2,1)S(1)}, u32[]{:S(2)}, u32[]{:S(2)}) collective-permute-start(bf16[128,128]{1,0:T(8,128)(2,1)S(1)} %get-tuple-element.42), channel_id=1, source_target_pairs={{0,6},{2,4},{4,2},{6,0},{1,7},{3,5},{5,3},{7,1},{8,14},{10,12},{12... | collective-permute-start | bytes 98312 | tf_op jit(solution)/shard_map/ppermute | solution.py:37
  49.2 3.9 %collective-permute-start.10 = (bf16[128,128]{1,0:T(8,128)(2,1)S(1)}, bf16[128,128]{1,0:T(8,128)(2,1)S(1)}, u32[]{:S(2)}, u32[]{:S(2)}) collective-permute-start(bf16[128,128]{1,0:T(8,128)(2,1)S(1)} %get-tuple-element.44.refs_0_), channel_id=1, source_target_pairs={{0,16},{1,17},{2,18},{3,19},{4,20},{5,21},{6,22},{7,23}} | collective-permute-start | bytes 98312 | tf_op jit(solution)/shard_map/ppermute | solution.py:797
  50.5 2.9 %collective-permute-start.11 = (bf16[128,128]{1,0:T(8,128)(2,1)S(1)}, bf16[128,128]{1,0:T(8,128)(2,1)S(1)}, u32[]{:S(2)}, u32[]{:S(2)}) collective-permute-start(bf16[128,128]{1,0:T(8,128)(2,1)S(1)} %get-tuple-element.44.refs_0_), channel_id=1, source_target_pairs={{0,24},{1,25},{2,26},{3,27},{4,28},{5,29},{6,30},{7,31}} | collective-permute-start | bytes 98312 | tf_op jit(solution)/shard_map/ppermute | solution.py:797
  51.8 2.9 %collective-permute-start.9 = (bf16[128,128]{1,0:T(8,128)(2,1)S(1)}, bf16[128,128]{1,0:T(8,128)(2,1)S(1)}, u32[]{:S(2)}, u32[]{:S(2)}) collective-permute-start(bf16[128,128]{1,0:T(8,128)(2,1)S(1)} %get-tuple-element.44.refs_0_), channel_id=1, source_target_pairs={{0,8},{1,9},{2,10},{3,11},{4,12},{5,13},{6,14},{7,15}} | collective-permute-start | bytes 98312 | tf_op jit(solution)/shard_map/ppermute | solution.py:797
  54.8 1.9 %collective-permute-start.12 = (bf16[128,64]{1,0:T(8,128)(2,1)S(1)}, bf16[128,64]{1,0:T(8,128)(2,1)S(1)}, u32[]{:S(2)}, u32[]{:S(2)}) collective-permute-start(bf16[128,64]{1,0:T(8,128)(2,1)S(1)} %get-tuple-element.46.refs_2_.refs_9_), channel_id=1, source_target_pairs={{0,2},{2,0},{4,6},{6,4},{1,3},{3,1},{5,7},{7,5},{8,10},{10,8},{12,... | collective-permute-start | bytes 49160 | tf_op jit(solution)/shard_map/ppermute | solution.py:32
  54.8 4.0 %collective-permute-start.13 = (bf16[128,64]{1,0:T(8,128)(2,1)S(1)}, bf16[128,64]{1,0:T(8,128)(2,1)S(1)}, u32[]{:S(2)}, u32[]{:S(2)}) collective-permute-start(bf16[128,64]{1,0:T(8,128)(2,1)S(1)} %get-tuple-element.46.refs_2_.refs_9_), channel_id=1, source_target_pairs={{0,4},{2,6},{4,0},{6,2},{1,5},{3,7},{5,1},{7,3},{8,12},{10,14},{12... | collective-permute-start | bytes 49160 | tf_op jit(solution)/shard_map/ppermute | solution.py:32
  56.2 3.4 %collective-permute-start.14 = (bf16[128,64]{1,0:T(8,128)(2,1)S(1)}, bf16[128,64]{1,0:T(8,128)(2,1)S(1)}, u32[]{:S(2)}, u32[]{:S(2)}) collective-permute-start(bf16[128,64]{1,0:T(8,128)(2,1)S(1)} %get-tuple-element.46.refs_2_.refs_9_), channel_id=1, source_target_pairs={{0,6},{2,4},{4,2},{6,0},{1,7},{3,5},{5,3},{7,1},{8,14},{10,12},{12... | collective-permute-start | bytes 49160 | tf_op jit(solution)/shard_map/ppermute | solution.py:32
  59.6 15.8 %copy-start.4 = (f32[80,384]{1,0:T(8,128)S(1)}, f32[80,384]{1,0:T(8,128)}, u32[]{:S(2)}) copy-start(f32[80,384]{1,0:T(8,128)} %get-tuple-element.47.refs_6_.refs_0_) | copy-start | bytes 368644
  59.6 1.9 %collective-permute-start.15 = (bf16[128,128]{1,0:T(8,128)(2,1)S(1)}, bf16[128,128]{1,0:T(8,128)(2,1)S(1)}, u32[]{:S(2)}, u32[]{:S(2)}) collective-permute-start(bf16[128,128]{1,0:T(8,128)(2,1)S(1)} %get-tuple-element.49), channel_id=1, source_target_pairs={{0,2},{2,0},{4,6},{6,4},{1,3},{3,1},{5,7},{7,5},{8,10},{10,8},{12,... | collective-permute-start | bytes 98312 | tf_op jit(solution)/shard_map/ppermute | solution.py:37
  59.8 3.9 %collective-permute-start.16 = (bf16[128,128]{1,0:T(8,128)(2,1)S(1)}, bf16[128,128]{1,0:T(8,128)(2,1)S(1)}, u32[]{:S(2)}, u32[]{:S(2)}) collective-permute-start(bf16[128,128]{1,0:T(8,128)(2,1)S(1)} %get-tuple-element.50), channel_id=1, source_target_pairs={{0,4},{2,6},{4,0},{6,2},{1,5},{3,7},{5,1},{7,3},{8,12},{10,14},{12... | collective-permute-start | bytes 98312 | tf_op jit(solution)/shard_map/ppermute | solution.py:37
  60.8 3.4 %collective-permute-start.17 = (bf16[128,128]{1,0:T(8,128)(2,1)S(1)}, bf16[128,128]{1,0:T(8,128)(2,1)S(1)}, u32[]{:S(2)}, u32[]{:S(2)}) collective-permute-start(bf16[128,128]{1,0:T(8,128)(2,1)S(1)} %get-tuple-element.51), channel_id=1, source_target_pairs={{0,6},{2,4},{4,2},{6,0},{1,7},{3,5},{5,3},{7,1},{8,14},{10,12},{12... | collective-permute-start | bytes 98312 | tf_op jit(solution)/shard_map/ppermute | solution.py:37
  64.2 30.2 %copy-start.3 = (bf16[4,128,128]{2,1,0:T(8,128)(2,1)S(1)}, bf16[4,128,128]{2,1,0:T(8,128)(2,1)}, u32[]{:S(2)}) copy-start(bf16[4,128,128]{2,1,0:T(8,128)(2,1)} %get-tuple-element.67.refs_4_) | copy-start | bytes 393220
  64.2 30.2 %copy-start.5 = (f32[128,128]{1,0:T(8,128)S(1)}, f32[128,128]{1,0:T(8,128)}, u32[]{:S(2)}) copy-start(f32[128,128]{1,0:T(8,128)} %get-tuple-element.68.refs_5_) | copy-start | bytes 196612
  64.3 36.2 %copy-start.7 = (f32[1,9216]{1,0:T(1,128)S(1)}, f32[1,9216]{1,0:T(1,128)}, u32[]{:S(2)}) copy-start(f32[1,9216]{1,0:T(1,128)} %get-tuple-element.43.refs_10_.refs_14_) | copy-start | bytes 110596
  64.3 11.1 %collective-permute-start.20 = (bf16[128,128]{1,0:T(8,128)(2,1)S(1)}, bf16[128,128]{1,0:T(8,128)(2,1)S(1)}, u32[]{:S(2)}, u32[]{:S(2)}) collective-permute-start(bf16[128,128]{1,0:T(8,128)(2,1)S(1)} %get-tuple-element.59), channel_id=1, source_target_pairs={{0,2},{2,0},{4,6},{6,4},{1,3},{3,1},{5,7},{7,5},{8,10},{10,8},{12,... | collective-permute-start | bytes 98312 | tf_op jit(solution)/shard_map/ppermute | solution.py:37
  64.5 10.9 %collective-permute-start.21 = (bf16[128,128]{1,0:T(8,128)(2,1)S(1)}, bf16[128,128]{1,0:T(8,128)(2,1)S(1)}, u32[]{:S(2)}, u32[]{:S(2)}) collective-permute-start(bf16[128,128]{1,0:T(8,128)(2,1)S(1)} %get-tuple-element.60), channel_id=1, source_target_pairs={{0,4},{2,6},{4,0},{6,2},{1,5},{3,7},{5,1},{7,3},{8,12},{10,14},{12... | collective-permute-start | bytes 98312 | tf_op jit(solution)/shard_map/ppermute | solution.py:37
  65.5 9.9 %collective-permute-start.22 = (bf16[128,128]{1,0:T(8,128)(2,1)S(1)}, bf16[128,128]{1,0:T(8,128)(2,1)S(1)}, u32[]{:S(2)}, u32[]{:S(2)}) collective-permute-start(bf16[128,128]{1,0:T(8,128)(2,1)S(1)} %get-tuple-element.61), channel_id=1, source_target_pairs={{0,6},{2,4},{4,2},{6,0},{1,7},{3,5},{5,3},{7,1},{8,14},{10,12},{12... | collective-permute-start | bytes 98312 | tf_op jit(solution)/shard_map/ppermute | solution.py:37
  66.2 9.2 %collective-permute-start.18 = (bf16[128,64]{1,0:T(8,128)(2,1)S(1)}, bf16[128,64]{1,0:T(8,128)(2,1)S(1)}, u32[]{:S(2)}, u32[]{:S(2)}) collective-permute-start(bf16[128,64]{1,0:T(8,128)(2,1)S(1)} %get-tuple-element.53), channel_id=1, source_target_pairs={{0,16},{8,24},{16,0},{24,8},{1,17},{9,25},{17,1},{25,9},{2,18},{10... | collective-permute-start | bytes 49160 | tf_op jit(solution)/shard_map/ppermute | solution.py:828
  75.4 8.5 %collective-permute-start.23 = (bf16[160,64]{1,0:T(8,128)(2,1)S(1)}, bf16[160,64]{1,0:T(8,128)(2,1)S(1)}, u32[]{:S(2)}, u32[]{:S(2)}) collective-permute-start(bf16[160,64]{1,0:T(8,128)(2,1)S(1)} %get-tuple-element.63), channel_id=1, source_target_pairs={{0,2},{2,0},{4,6},{6,4},{1,3},{3,1},{5,7},{7,5},{8,10},{10,8},{12,... | collective-permute-start | bytes 61448 | tf_op jit(solution)/shard_map/ppermute | solution.py:37
  75.5 8.5 %collective-permute-start.24 = (bf16[160,64]{1,0:T(8,128)(2,1)S(1)}, bf16[160,64]{1,0:T(8,128)(2,1)S(1)}, u32[]{:S(2)}, u32[]{:S(2)}) collective-permute-start(bf16[160,64]{1,0:T(8,128)(2,1)S(1)} %get-tuple-element.64), channel_id=1, source_target_pairs={{0,4},{2,6},{4,0},{6,2},{1,5},{3,7},{5,1},{7,3},{8,12},{10,14},{12... | collective-permute-start | bytes 61448 | tf_op jit(solution)/shard_map/ppermute | solution.py:37
  76.6 7.4 %collective-permute-start.25 = (bf16[160,64]{1,0:T(8,128)(2,1)S(1)}, bf16[160,64]{1,0:T(8,128)(2,1)S(1)}, u32[]{:S(2)}, u32[]{:S(2)}) collective-permute-start(bf16[160,64]{1,0:T(8,128)(2,1)S(1)} %get-tuple-element.65), channel_id=1, source_target_pairs={{0,6},{2,4},{4,2},{6,0},{1,7},{3,5},{5,3},{7,1},{8,14},{10,12},{12... | collective-permute-start | bytes 61448 | tf_op jit(solution)/shard_map/ppermute | solution.py:37
  77.4 6.6 %collective-permute-start.19 = (bf16[128,64]{1,0:T(8,128)(2,1)S(1)}, bf16[128,64]{1,0:T(8,128)(2,1)S(1)}, u32[]{:S(2)}, u32[]{:S(2)}) collective-permute-start(bf16[128,64]{1,0:T(8,128)(2,1)S(1)} %get-tuple-element.53), channel_id=1, source_target_pairs={{0,8},{8,0},{16,24},{24,16},{1,9},{9,1},{17,25},{25,17},{2,10},{10... | collective-permute-start | bytes 49160 | tf_op jit(solution)/shard_map/ppermute | solution.py:827
  84.0 10.4 %collective-permute-start.26 = (bf16[128,64]{1,0:T(8,128)(2,1)S(1)}, bf16[128,64]{1,0:T(8,128)(2,1)S(1)}, u32[]{:S(2)}, u32[]{:S(2)}) collective-permute-start(bf16[128,64]{1,0:T(8,128)(2,1)S(1)} %shard_map.130.refs_0_), channel_id=1, source_target_pairs={{0,24},{8,16},{16,8},{24,0},{1,25},{9,17},{17,9},{25,1},{2,26},{10... | collective-permute-start | bytes 49160 | tf_op jit(solution)/shard_map/ppermute | solution.py:851
  95.5 1.3 %collective-permute-start.30 = (bf16[5,64,128]{2,1,0:T(8,128)(2,1)S(1)}, bf16[5,64,128]{2,1,0:T(8,128)(2,1)S(1)}, u32[]{:S(2)}, u32[]{:S(2)}) collective-permute-start(bf16[5,64,128]{2,1,0:T(8,128)(2,1)S(1)} %shard_map.131), channel_id=1, source_target_pairs={{0,2},{2,0},{4,6},{6,4},{1,3},{3,1},{5,7},{7,5},{8,10},{10,8},{12,... | collective-permute-start | bytes 245768 | tf_op jit(solution)/shard_map/ppermute | solution.py:873
  96.9 13.3 %collective-permute-start.31 = (bf16[5,64,128]{2,1,0:T(8,128)(2,1)S(1)}, bf16[5,64,128]{2,1,0:T(8,128)(2,1)S(1)}, u32[]{:S(2)}, u32[]{:S(2)}) collective-permute-start(bf16[5,64,128]{2,1,0:T(8,128)(2,1)S(1)} %add_convert_fusion.refs_10_), channel_id=1, source_target_pairs={{0,4},{1,5},{2,6},{3,7},{4,0},{5,1},{6,2},{7,3},{8,12},{9,13},{10,... | collective-permute-start | bytes 245768 | tf_op jit(solution)/shard_map/ppermute | solution.py:885
  98.0 12.2 %collective-permute-start.32 = (bf16[5,64,128]{2,1,0:T(8,128)(2,1)S(1)}, bf16[5,64,128]{2,1,0:T(8,128)(2,1)S(1)}, u32[]{:S(2)}, u32[]{:S(2)}) collective-permute-start(bf16[5,64,128]{2,1,0:T(8,128)(2,1)S(1)} %add_convert_fusion.refs_10_), channel_id=1, source_target_pairs={{0,1},{1,0},{2,3},{3,2},{4,5},{5,4},{6,7},{7,6},{8,9},{9,8},{10,11... | collective-permute-start | bytes 245768 | tf_op jit(solution)/shard_map/ppermute | solution.py:885
  99.5 10.7 %collective-permute-start.33 = (bf16[5,64,128]{2,1,0:T(8,128)(2,1)S(1)}, bf16[5,64,128]{2,1,0:T(8,128)(2,1)S(1)}, u32[]{:S(2)}, u32[]{:S(2)}) collective-permute-start(bf16[5,64,128]{2,1,0:T(8,128)(2,1)S(1)} %add_convert_fusion.refs_10_), channel_id=1, source_target_pairs={{0,5},{1,4},{2,7},{3,6},{4,1},{5,0},{6,3},{7,2},{8,13},{9,12},{10,... | collective-permute-start | bytes 245768 | tf_op jit(solution)/shard_map/ppermute | solution.py:885
  100.4 4.6 %collective-permute-start.29 = (f32[1,9216]{1,0:T(1,128)S(1)}, f32[1,9216]{1,0:T(1,128)S(1)}, u32[]{:S(2)}, u32[]{:S(2)}) collective-permute-start(f32[1,9216]{1,0:T(1,128)S(1)} %copy-done.7), channel_id=1, source_target_pairs={{0,1},{1,0},{2,3},{3,2},{4,5},{5,4},{6,7},{7,6},{8,9},{9,8},{10,11... | collective-permute-start | bytes 110600 | tf_op jit(solution)/shard_map/ppermute | solution.py:32
  101.9 3.9 %collective-permute-start.27 = (bf16[128,64]{1,0:T(8,128)(2,1)S(1)}, bf16[128,64]{1,0:T(8,128)(2,1)S(1)}, u32[]{:S(2)}, u32[]{:S(2)}) collective-permute-start(bf16[128,64]{1,0:T(8,128)(2,1)S(1)} %shard_map.130.refs_0_), channel_id=1, source_target_pairs={{0,8},{8,0},{16,24},{24,16},{1,9},{9,1},{17,25},{25,17},{2,10},{10... | collective-permute-start | bytes 49160 | tf_op jit(solution)/shard_map/ppermute | solution.py:852
  105.0 5.2 %collective-permute-start.28 = (bf16[128,64]{1,0:T(8,128)(2,1)S(1)}, bf16[128,64]{1,0:T(8,128)(2,1)S(1)}, u32[]{:S(2)}, u32[]{:S(2)}) collective-permute-start(bf16[128,64]{1,0:T(8,128)(2,1)S(1)} %shard_map.130.refs_0_), channel_id=1, source_target_pairs={{0,16},{8,24},{16,0},{24,8},{1,17},{9,25},{17,1},{25,9},{2,18},{10... | collective-permute-start | bytes 49160 | tf_op jit(solution)/shard_map/ppermute | solution.py:853

commit v7 on v6

--- a/solution.py
+++ b/solution.py
@@ -39,14 +39,42 @@
     ]
 
 
-def gather_doubling(value, axis, count):
-    held = {0: value}
+def spread_heads(own, count, groups):
+    held = {0: [own]}
     bit = count // 2
+    first = True
     while bit:
         for offset in sorted(held):
-            held[offset | bit] = lax.ppermute(held[offset], axis, swaps(count, bit))
+            if first and groups == 2:
+                width = own.shape[1] // 2
+                part = lax.dynamic_slice_in_dim(own, lax.axis_index("dp") * width, width, axis=1)
+                near = lax.ppermute(part, "seq", swaps(count, bit))
+                held[bit] = [near, lax.ppermute(near, "dp", swaps(groups, 1))]
+            else:
+                held[offset | bit] = [
+                    lax.ppermute(piece, "seq", swaps(count, bit))
+                    for piece in held[offset]
+                ]
+        first = False
         bit //= 2
     return [held[offset] for offset in range(count)]
+
+
+def head_tile(pieces, first, size):
+    if len(pieces) == 1:
+        return pieces[0][:, first : first + size]
+    width = pieces[0].shape[1]
+    inside = slice(first % width, first % width + size)
+    near = lax.axis_index("dp") == first // width
+    return jnp.where(near, pieces[0][:, inside], pieces[1][:, inside])
+
+
+def nested(refs, sizes):
+    groups, first = [], 0
+    for size in sizes:
+        groups.append(refs[first : first + size])
+        first += size
+    return (groups, refs[first:])
 
 
 def in_order(pieces, own_place):
@@ -359,7 +387,7 @@
         span = slice(first, first + TILE)
         attended = None
         for piece, rows_w in zip(mixed, heads_w):
-            product = dot32(piece[...], rows_w[:, span])
+            product = dot32(piece[...], head_tile(rows_w, first, TILE))
             attended = product if attended is None else attended + product
         mod = late.ready()
         residual = (
@@ -392,10 +420,10 @@
     return (result, inverse)
 
 
-def student_tail_kernel(count, fetches, latent, embed_w, *refs):
+def student_tail_kernel(count, sizes, fetches, latent, embed_w, *refs):
     mixed = refs[:count]
-    heads_w = refs[count : 2 * count]
-    pair_ref, saved_out, inverse_out, work, inverse_ref, sends = refs[2 * count :]
+    heads_w, refs = nested(refs[count:], sizes)
+    pair_ref, saved_out, inverse_out, work, inverse_ref, sends = refs
     late, final_t, noise, times = fetches
     latent_width = latent.shape[1]
 
@@ -436,11 +464,11 @@
             rows_ref[...] = chosen[:, : rows_ref.shape[1]]
 
 
-def critic_tail_kernel(count, fetches, pair, embed_w, *refs):
+def critic_tail_kernel(count, sizes, fetches, pair, embed_w, *refs):
     mixed = refs[:count]
-    heads_w = refs[count : 2 * count]
-    grads = refs[2 * count : 3 * count]
-    inverse_ref, term_ref, target_ref, direct_ref, latent, work, other = refs[3 * count :]
+    heads_w, refs = nested(refs[count:], sizes)
+    grads = refs[:count]
+    inverse_ref, term_ref, target_ref, direct_ref, latent, work, other = refs[count:]
     late, final_t, noise, times = fetches
     model_width = embed_w.shape[2]
     latent_width = latent.shape[1]
@@ -465,6 +493,16 @@
             2.0 * (result - (second - sample)),
             jnp.where(section == 3, 1.0 / (1.0 + jnp.exp(-result)), 0.0),
         )
+
+        @pl.when(section == 1)
+        def _():
+            gaps = jnp.abs(sample - both[:, :latent_width] + sigma_critic * result)
+            error = jnp.sum(jnp.sum(gaps, axis=1, keepdims=True), axis=0, keepdims=True)
+            error = error / (gaps.shape[0] * latent_width)
+            error_top, error_low = halves(jnp.broadcast_to(error, (16, grads[0].shape[1])))
+            for place in range(count):
+                grads[place][:16] = error_top
+                grads[place][16:32] = error_low
 
         @pl.when(section == 3)
         def _():
@@ -494,7 +532,7 @@
                     jnp.bfloat16
                 )
                 for place in range(count):
-                    product = dot32_t(grad_attended, heads_w[place][:, span])
+                    product = dot32_t(grad_attended, head_tile(heads_w[place], first, TILE))
                     held = totals[place]
                     totals[place] = product if held is None else held + product
             direct_ref[...] = direct
@@ -512,11 +550,10 @@
     gram_ref[0], gram_ref[1] = halves(gram)
 
 
-def judge_back_kernel(count, model_width, fetches, short_in, gram, gains, proj_ref, inverse_ref, key_ref, value_ref, pair, real, *refs):
+def judge_back_kernel(count, model_width, fetches, short_in, gram, gains, proj_ref, inverse_ref, key_ref, value_ref, term, *refs):
     rows = refs[:count]
     grads = refs[count : 2 * count]
-    outs = refs[2 * count : 3 * count]
-    grad_key_ref, grad_value_ref, grad_query_ref = refs[3 * count :]
+    keep_ref, send_ref, real_ref, grad_key_ref, grad_value_ref, grad_query_ref = refs[2 * count :]
     section = lax.axis_index("segment")
     latent_width = rows[0].shape[1]
     head_width = gains.shape[2]
@@ -525,16 +562,7 @@
 
     @pl.when(section == 3)
     def _():
-        both = pair[...].astype(jnp.float32)
-        gaps = jnp.abs(
-            both[:, latent_width:] - both[:, :latent_width] + real[...].astype(jnp.float32)
-        )
-        error = jnp.sum(jnp.sum(gaps, axis=1, keepdims=True), axis=0, keepdims=True)
-        error = error / (size * latent_width)
-        error_top, error_low = halves(jnp.broadcast_to(error, (16, latent_width)))
         for place in range(count):
-            outs[place][size : size + 16] = error_top
-            outs[place][size + 16 :] = error_low
             low = place * size
             span = slice(low, low + size)
             queries, _, _ = rms_scale(proj_ref[span, :head_width], gains[0, :1])
@@ -576,34 +604,38 @@
             along = jnp.sum(through * block.astype(jnp.float32), axis=1, keepdims=True) / model_width
             spanned = dot32(block, gram_top) + dot32(block, gram_low)
             inverse = inverse_ref[span, :1]
-            outs[place][:size] = (
+            target_ref = send_ref if place % 2 else keep_ref
+            target_ref[place // 2] = (
                 inverse * (through - spanned * (inverse * inverse * along))
             ).astype(jnp.bfloat16)
 
-
-def merge_kernel(count, fetches, direct, real, fake, *refs):
-    parts = refs[:count]
-    payload_ref = refs[count]
-    rows = direct.shape[0]
-
+    @pl.when(section == 1)
+    def _():
+        error = None
+        for grad in grads:
+            part = grad[:16, :latent_width].astype(jnp.float32) + grad[
+                16:32, :latent_width
+            ].astype(jnp.float32)
+            error = part if error is None else error + part
+        real_ref[:size] = term[...]
+        real_ref[size : size + 16], real_ref[size + 16 :] = halves(error / count + EPS)
+
+
+def merge_kernel(fetches, direct, keep, moved, *outs):
     @pl.when(lax.axis_index("segment") == 3)
     def _():
-        (times,) = fetches
-        times.start()
-        total = parts[0][...].astype(jnp.float32)
-        for part in parts[1:]:
-            total = total + part[...].astype(jnp.float32)
-        _, critic_step = steps_of(times)
-        adverse = (1.0 - noise_level(critic_step)) * (total[:rows] + direct[...])
-        spread = (total[rows : rows + 16] + total[rows + 16 :])[:1, :1] / count + EPS
-        gap = real[...].astype(jnp.float32) - fake[...].astype(jnp.float32)
-        payload_ref[...] = (gap / spread + ADV_WEIGHT * adverse).astype(jnp.bfloat16)
+        for place, out in enumerate(outs):
+            total = keep[place].astype(jnp.float32) + moved[place].astype(jnp.float32)
+            if place == 0:
+                total = total + direct[...]
+            out[...] = total.astype(jnp.bfloat16)
 
 
 def outer_kernel(
     count,
     fetches,
-    arrived,
+    real,
+    fake,
     target_in,
     student_rows,
     pair,
@@ -613,10 +645,12 @@
     *refs,
 ):
     critic_mixed = refs[:count]
-    sums_ref = refs[count]
+    arrived = refs[count : count + count // 2]
+    sums_ref, sample_ref = refs[count + count // 2 :]
     section = lax.axis_index("segment")
     place = lax.axis_index("seq")
     latent_width = student_rows.shape[1]
+    rows = student_rows.shape[0]
 
     def collect(target, inverse, latent, mixed):
         target = target.astype(jnp.bfloat16)
@@ -637,8 +671,18 @@
     def _():
         (times,) = fetches
         times.start()
-        student_step, _ = steps_of(times)
-        target = -noise_level(student_step) * arrived[...].astype(jnp.float32)
+        student_step, critic_step = steps_of(times)
+        adverse = arrived[0][...].astype(jnp.float32)
+        for part in arrived[1:]:
+            adverse = adverse + part[...].astype(jnp.float32)
+        adverse = (1.0 - noise_level(critic_step)) * adverse
+        spread = (real[rows : rows + 1] .astype(jnp.float32) + real[rows + 16 : rows + 17].astype(jnp.float32))[
+            :, :1
+        ]
+        gap = real[:rows].astype(jnp.float32) - fake[...].astype(jnp.float32)
+        sample_grad = gap / spread + ADV_WEIGHT * adverse
+        sample_ref[...] = sample_grad.astype(jnp.bfloat16)
+        target = -noise_level(student_step) * sample_grad
         mixed = [student_mixed.at[offset] for offset in range(count)]
         collect(target, student_inverse, student_rows[...], mixed)
 
@@ -652,18 +696,18 @@
 
 
 def expand_kernel(
-    count, groups, full_rows, fetches, own, from_first, from_second, from_third, embed_w, *refs
+    count, groups, sizes, full_rows, fetches, own, to_first, to_second, to_third, embed_w, *refs
 ):
-    heads_w = refs[:count]
-    other_mods = refs[count : count + groups - 1]
-    sums = refs[count + groups - 1 : count + 3 * groups - 1]
-    grad_ref, total_ref, work, joined = refs[count + 3 * groups - 1 :]
+    heads_w, refs = nested(refs, sizes)
+    other_mods = refs[: groups - 1]
+    sums = refs[groups - 1 : 3 * groups - 1]
+    grad_ref, total_ref, work, joined = refs[3 * groups - 1 :]
     section = lax.axis_index("segment")
     place = lax.axis_index("seq")
     latent_width = embed_w.shape[1]
     model_width = embed_w.shape[2]
     picked = own[...].astype(jnp.float32)
-    for source, value in ((0, from_first), (2, from_second), (1, from_third)):
+    for source, value in ((1, to_first), (2, to_second), (3, to_third)):
         picked = jnp.where(section == source, value[...].astype(jnp.float32), picked)
     grad_ref[...] = picked.T
 
@@ -687,7 +731,7 @@
             span = slice(first, first + TILE)
             spread = None
             for head, rows_w in zip(heads, heads_w):
-                product = dot32(head, rows_w[:, span])
+                product = dot32(head, head_tile(rows_w, first, TILE))
                 spread = product if spread is None else spread + product
             near = dot32(near_top[:, :latent_width], embed_w[0, :, span])
             mods = [late.ready(), *other_mods]
@@ -732,7 +776,10 @@
     head_width = w_qkv.shape[4]
     kind_w = jnp.transpose(w_qkv[0, :, 0], (1, 0, 2))
     final_w = jnp.transpose(w_final[0])
-    heads_w = gather_doubling(w_out[0, 0], "seq", count)
+    groups = lax.axis_size("dp")
+    heads_w = spread_heads(w_out[0, 0], count, groups)
+    sizes = [len(pieces) for pieces in heads_w]
+    heads_w = sum(heads_w, [])
     bf16, f32 = jnp.bfloat16, jnp.float32
 
     depth = packed_rows(mod_width)
@@ -777,12 +824,11 @@
         sent=[array(*short_shape), array((1, 3 * model_width), f32)],
     )
     student_mixed = scatter_near(head_outs, "seq", count)
-    groups = lax.axis_size("dp")
     late_mods = gather_near(late_mod, "dp", groups)
     work = pltpu.VMEM((tok_rows, model_width), f32)
     inverse_shape = array((tok_rows, 128), f32)
     pair, saved, student_inverse = run(
-        functools.partial(student_tail_kernel, count),
+        functools.partial(student_tail_kernel, count, sizes),
         [array((tok_rows, 2 * latent_width), bf16)],
         (noisy_student, w_embed, *student_mixed, *heads_w),
         2 * tok_rows * model_width * head_width * count,
@@ -816,7 +862,7 @@
     small = array((tok_rows, latent_width), f32)
     thin = array((tok_rows, latent_width), bf16)
     *grad_heads, critic_inverse, term_rows, target, direct = run(
-        functools.partial(critic_tail_kernel, count),
+        functools.partial(critic_tail_kernel, count, sizes),
         head_blocks + [inverse_shape, thin, small, small],
         (pair, w_embed, *critic_mixed, *heads_w),
         4 * tok_rows * model_width * head_width * count,
@@ -824,38 +870,43 @@
         fetched=(late_mod, final_w, noise[0], timesteps),
     )
     grad_blocks = scatter_near(grad_heads, "seq", count)
-    fake = lax.ppermute(term_rows, "segment", swaps(sections, 1))
-    real = lax.ppermute(term_rows, "segment", swaps(sections, 2))
+    fake = lax.ppermute(term_rows, "segment", swaps(sections, 2))
+    half = count // 2
+    rows_shape = array((half, tok_rows, latent_width), bf16)
     (gram,) = run(
         gram_kernel,
         [array((2, latent_width, latent_width), bf16)],
         (w_embed,),
         6 * latent_width * latent_width * model_width,
     )
-    parts = run(
+    keep, away, real = run(
         functools.partial(judge_back_kernel, count, model_width),
-        [array((tok_rows + 32, latent_width), bf16)] * count,
-        (short, gram, qk_gain, proj, inverse, keys, values, pair, real, *critic_rows, *grad_blocks),
+        [rows_shape, rows_shape, array((tok_rows + 32, latent_width), bf16)],
+        (short, gram, qk_gain, proj, inverse, keys, values, term_rows, *critic_rows, *grad_blocks),
         10 * full_rows * full_rows * head_width,
         scratch=(pltpu.VMEM((full_rows, head_width), f32),) * 3,
     )
-    parts = scatter_near(parts, "seq", count)
-    (payload,) = run(
-        functools.partial(merge_kernel, count),
-        [thin],
-        (direct, real, fake, *parts),
-        1000,
-        fetched=(timesteps,),
-    )
-    ends = [(place, sections - 1 - place) for place in range(sections)]
-    to_student = lax.ppermute(payload, "segment", ends)
-    to_second = lax.ppermute(payload, "segment", swaps(sections, 1))
-    to_third = lax.ppermute(payload, "segment", swaps(sections, 2))
-    (sums,) = run(
+    moved = lax.ppermute(away, "seq", swaps(count, 1))
+    real = lax.ppermute(real, "segment", swaps(sections, 1))
+    parts = run(merge_kernel, [thin] * half, (direct, keep, moved), 1000)
+    to_student = [
+        lax.ppermute(
+            part,
+            ("segment", "seq"),
+            [
+                (place * count + row, (place + 1) % sections * count + (row ^ (2 * index)))
+                for place in range(sections)
+                for row in range(count)
+            ],
+        )
+        for index, part in enumerate(parts)
+    ]
+    sums, sample_grad = run(
         functools.partial(outer_kernel, count),
-        [array((count + 1, latent_width, 128), bf16)],
+        [array((count + 1, latent_width, 128), bf16), thin],
         (
-            to_student,
+            real,
+            fake,
             target,
             noisy_student,
             pair,
@@ -863,10 +914,15 @@
             student_inverse,
             critic_inverse,
             *critic_mixed,
+            *to_student,
         ),
         2 * tok_rows * latent_width * head_width * (count + 1),
         fetched=(timesteps,),
     )
+    ends = [(place, sections - 1 - place) for place in range(sections)]
+    to_third = lax.ppermute(sample_grad, "segment", ends)
+    to_second = lax.ppermute(sample_grad, "segment", swaps(sections, 2))
+    to_first = lax.ppermute(sample_grad, "segment", swaps(sections, 1))
     last = count // 2
     bit = 1
     while bit < last:
@@ -885,9 +941,9 @@
                 sums if offset == group == 0 else lax.ppermute(sums, ("seq", "dp"), moves)
             )
     grad_t, total_t = run(
-        functools.partial(expand_kernel, count, groups, full_rows),
+        functools.partial(expand_kernel, count, groups, sizes, full_rows),
         [array((latent_width, tok_rows), f32), array((latent_width, model_width), f32)],
-        (payload, to_student, to_second, to_third, w_embed, *heads_w, *late_mods[1:], *sums_all),
+        (sample_grad, to_first, to_second, to_third, w_embed, *heads_w, *late_mods[1:], *sums_all),
         4 * groups * latent_width * model_width * head_width * count,
         scratch=(
             pltpu.VMEM((groups * latent_width, model_width), f32),

time: 114 us -> 116 us (1.018)
  waiting for transfers between devices: 45 us -> 47.6 us
  starting transfers between devices: 44.9 us -> 43.2 us
    ppermute x12 -> x9, waiting for transfers between devices: 5.03 us -> 7.77 us  [scatter_near(): lax.ppermute(blocks[offset], axis, swaps(count, offset))]
    ppermute x12 -> x9, starting transfers between devices: 7.7 us -> 5.45 us  [scatter_near(): lax.ppermute(blocks[offset], axis, swaps(count, offset))]
    ppermute x7, waiting for transfers between devices: 9.65 us -> 8.47 us  [gather_near(): lax.ppermute(value, axis, swaps(count, offset))]
    ppermute x8 -> x13, waiting for transfers between devices: 27.5 us -> 28.6 us  [the longest x1 9.11 us: spread_heads(): near = lax.ppermute(part, 'seq', swaps(count, bit))]
    ppermute x8 -> x13, starting transfers between devices: 24.1 us -> 24 us  [the longest x1 10.1 us: step(): fake = lax.ppermute(term_rows, 'segment', swaps(sections, 2))]
  transfers between devices with their start and end apart: 34 -> 36, of which waited for: 17 -> 23; matrix products, arithmetic and copies ran while one was open for 0% -> 0% of each run, Pallas kernels for 13% -> 13%
where the time goes in v7:
time: 116 us
  waiting for transfers between devices  47.6 us (41%)
  starting transfers between devices  43.2 us (37%)
  Pallas kernels  22.7 us (20%)
    pallas_call x11, Pallas kernels, run(): pl.pallas_call(body, out_shape=list(outputs) + [pltpu.HBM(item.shape, ite...  22.7 us
    ppermute x1, starting transfers between devices, step(): fake = lax.ppermute(term_rows, 'segment', swaps(sections, 2))  10.1 us
    ppermute x1, waiting for transfers between devices, spread_heads(): near = lax.ppermute(part, 'seq', swaps(count, bit))  9.11 us
    ppermute x1, waiting for transfers between devices, spread_heads(): held[bit] = [near, lax.ppermute(near, 'dp', swaps(groups, 1))]  8.56 us
    ppermute x7, waiting for transfers between devices, gather_near(): lax.ppermute(value, axis, swaps(count, offset))  8.47 us
    ppermute x9, waiting for transfers between devices, scatter_near(): lax.ppermute(blocks[offset], axis, swaps(count, offset))  7.77 us
    ppermute x1, starting transfers between devices, step(): real = lax.ppermute(real, 'segment', swaps(sections, 1))  6.58 us
    ppermute x7, starting transfers between devices, gather_near(): lax.ppermute(value, axis, swaps(count, offset))  6.24 us
  transfers between devices with their start and end apart: 36, of which 23 were waited for; matrix products, arithmetic and copies ran while one was open for 0% of the time, Pallas kernels for 13%

profile of v7, /device:TPU:0, one launch (start us, length us, event | category | flops | bytes accessed | tf_op | source)
XLA Modules:
  0.0 115.6 jit_solution(13682407872857612757)
XLA Ops:
  0.6 1.0 dynamic-slice_bitcast_fusion
  1.7 3.1 %collective-permute-start.7 = (bf16[128,1536]{1,0:T(8,128)(2,1)S(1)}, bf16[128,1536]{1,0:T(8,128)(2,1)S(1)}, u32[]{:S(2)}, u32[]{:S(2)}) collective-permute-start(bf16[128,1536]{1,0:T(8,128)(2,1)S(1)} %dynamic-slice_bitcast_fusion), channel_id=1, source_target_pairs={{0,4},{2,6},{4,0},{6,2},{1,5},{3,7},{5,1},{7,3},{8,12},{10,14},{12... | collective-permute-start | bytes 1179656 | tf_op jit(solution)/shard_map/ppermute | solution.py:51
  4.7 9.1 %collective-permute-done.7.refs_8_.refs_7_ = bf16[128,1536]{1,0:T(8,128)(2,1)S(1)} collective-permute-done((bf16[128,1536]{1,0:T(8,128)(2,1)S(1)}, bf16[128,1536]{1,0:T(8,128)(2,1)S(1)}, u32[]{:S(2)}, u32[]{:S(2)}) %collective-permute-start.7) | collective-permute-done | bytes 393248 | tf_op jit(solution)/shard_map/ppermute | solution.py:51
  13.8 1.7 %collective-permute-start.8 = (bf16[128,1536]{1,0:T(8,128)(2,1)S(1)}, bf16[128,1536]{1,0:T(8,128)(2,1)S(1)}, u32[]{:S(2)}, u32[]{:S(2)}) collective-permute-start(bf16[128,1536]{1,0:T(8,128)(2,1)S(1)} %collective-permute-done.7.refs_8_.refs_7_), channel_id=1, source_target_pairs={{0,1},{1,0},{2,3},{3,2},{4,5},{5,4},{6,7},{7,6},{8,9},{9,8},{10,11... | collective-permute-start | bytes 1179656 | tf_op jit(solution)/shard_map/ppermute | solution.py:52
  15.6 8.6 %collective-permute-done.8.refs_9_.refs_8_ = bf16[128,1536]{1,0:T(8,128)(2,1)S(1)} collective-permute-done((bf16[128,1536]{1,0:T(8,128)(2,1)S(1)}, bf16[128,1536]{1,0:T(8,128)(2,1)S(1)}, u32[]{:S(2)}, u32[]{:S(2)}) %collective-permute-start.8) | collective-permute-done | bytes 393248 | tf_op jit(solution)/shard_map/ppermute | solution.py:52
  24.1 0.0 collective-permute-start.10
  24.1 10.9 %shard_map.122 = (bf16[128,128]{1,0:T(8,128)(2,1)S(1)}, bf16[128,64]{1,0:T(8,128)(2,1)S(1)}) custom-call(s32[2,2]{1,0:T(2,128)} %refs_14_.1, f32[1,256]{1,0:T(1,128)} %refs_1_.4, bf16[256,3072]{1,0:T(8,128)(2,1)} %bitcast.27, bf16[64,128]{1,0:T(8,128)(2,1)} %bitcast.33, bf16[128,128]{1,0:T(8,128)(2,1)} %bitcast.30, bf16[3072,3840]{1,0:T(8,128)(2,1)} %bitcast.26), custom_call_target="tpu_custom_call" | custom-call | flops 23592960 | bytes 1672208 | tf_op jit(solution)/shard_map/pallas_call | solution.py:180
  35.1 0.0 copy-start.1
  35.1 0.6 collective-permute-start
  35.6 1.5 %collective-permute-start.1 = (bf16[128,128]{1,0:T(8,128)(2,1)S(1)}, bf16[128,128]{1,0:T(8,128)(2,1)S(1)}, u32[]{:S(2)}, u32[]{:S(2)}) collective-permute-start(bf16[128,128]{1,0:T(8,128)(2,1)S(1)} %get-tuple-element.40.refs_3_), channel_id=1, source_target_pairs={{0,4},{2,6},{4,0},{6,2},{1,5},{3,7},{5,1},{7,3},{8,12},{10,14},{12... | collective-permute-start | bytes 98312 | tf_op jit(solution)/shard_map/ppermute | solution.py:32
  37.1 0.0 collective-permute-done.refs_4_
  37.1 0.8 collective-permute-start.2
  37.9 1.6 %collective-permute-done.1.refs_5_ = bf16[128,128]{1,0:T(8,128)(2,1)S(1)} collective-permute-done((bf16[128,128]{1,0:T(8,128)(2,1)S(1)}, bf16[128,128]{1,0:T(8,128)(2,1)S(1)}, u32[]{:S(2)}, u32[]{:S(2)}) %collective-permute-start.1) | collective-permute-done | bytes 32800 | tf_op jit(solution)/shard_map/ppermute | solution.py:32
  39.6 1.2 %collective-permute-done.2.refs_6_ = bf16[128,128]{1,0:T(8,128)(2,1)S(1)} collective-permute-done((bf16[128,128]{1,0:T(8,128)(2,1)S(1)}, bf16[128,128]{1,0:T(8,128)(2,1)S(1)}, u32[]{:S(2)}, u32[]{:S(2)}) %collective-permute-start.2) | collective-permute-done | bytes 32800 | tf_op jit(solution)/shard_map/ppermute | solution.py:32
  40.8 3.6 %shard_map.123 = (bf16[128,128]{1,0:T(8,128)(2,1)S(1)}, bf16[128,128]{1,0:T(8,128)(2,1)S(1)}, bf16[128,128]{1,0:T(8,128)(2,1)S(1)}, bf16[128,128]{1,0:T(8,128)(2...) custom-call(bf16[1,64,3072]{2,1,0:T(8,128)(2,1)S(1)} %copy-done, bf16[3,3072,128]{2,1,0:T(8,128)(2,1)S(1)} %bitcast.25, ...), custom_call_target="tpu_custom_call" | custom-call | flops 301989888 | bytes 3015680 | tf_op jit(solution)/shard_map/pallas_call | solution.py:180
  44.4 0.2 collective-permute-start.3
  44.6 0.8 collective-permute-start.4
  45.4 0.3 collective-permute-done.3.refs_3_
  45.7 0.7 collective-permute-start.5
  46.4 2.1 %collective-permute-done.4.refs_4_ = bf16[128,128]{1,0:T(8,128)(2,1)S(1)} collective-permute-done((bf16[128,128]{1,0:T(8,128)(2,1)S(1)}, bf16[128,128]{1,0:T(8,128)(2,1)S(1)}, u32[]{:S(2)}, u32[]{:S(2)}) %collective-permute-start.4) | collective-permute-done | bytes 32800 | tf_op jit(solution)/shard_map/ppermute | solution.py:37
  48.5 0.5 collective-permute-done.5.refs_5_
  49.1 2.9 %shard_map.125 = (bf16[128,128]{1,0:T(8,128)(2,1)S(1)}, bf16[4,128,128]{2,1,0:T(8,128)(2,1)}, f32[128,128]{1,0:T(8,128)}) custom-call(bf16[128,64]{1,0:T(8,128)(2,1)S(1)} %get-tuple-element.42.refs_0_.refs_3_, bf16[1,64,3072]{2,1,0:T(8,128)(2,1)S(1)} %copy-done, bf16[128,128]{1,0:T(8,128)(2,1)S(1)} %get-tuple-element.43.refs_2_, ...), custom_call_target="tpu_custom_call" | custom-call | flops 402653184 | bytes 4182032 | tf_op jit(solution)/shard_map/pallas_call | solution.py:180
  52.0 1.3 %collective-permute-start.11 = (bf16[128,128]{1,0:T(8,128)(2,1)S(1)}, bf16[128,128]{1,0:T(8,128)(2,1)S(1)}, u32[]{:S(2)}, u32[]{:S(2)}) collective-permute-start(bf16[128,128]{1,0:T(8,128)(2,1)S(1)} %get-tuple-element.48.refs_0_), channel_id=1, source_target_pairs={{0,8},{1,9},{2,10},{3,11},{4,12},{5,13},{6,14},{7,15}} | collective-permute-start | bytes 98312 | tf_op jit(solution)/shard_map/ppermute | solution.py:843
  53.3 1.3 %collective-permute-start.12 = (bf16[128,128]{1,0:T(8,128)(2,1)S(1)}, bf16[128,128]{1,0:T(8,128)(2,1)S(1)}, u32[]{:S(2)}, u32[]{:S(2)}) collective-permute-start(bf16[128,128]{1,0:T(8,128)(2,1)S(1)} %get-tuple-element.48.refs_0_), channel_id=1, source_target_pairs={{0,16},{1,17},{2,18},{3,19},{4,20},{5,21},{6,22},{7,23}} | collective-permute-start | bytes 98312 | tf_op jit(solution)/shard_map/ppermute | solution.py:843
  54.6 1.3 %collective-permute-start.13 = (bf16[128,128]{1,0:T(8,128)(2,1)S(1)}, bf16[128,128]{1,0:T(8,128)(2,1)S(1)}, u32[]{:S(2)}, u32[]{:S(2)}) collective-permute-start(bf16[128,128]{1,0:T(8,128)(2,1)S(1)} %get-tuple-element.48.refs_0_), channel_id=1, source_target_pairs={{0,24},{1,25},{2,26},{3,27},{4,28},{5,29},{6,30},{7,31}} | collective-permute-start | bytes 98312 | tf_op jit(solution)/shard_map/ppermute | solution.py:843
  55.9 0.3 collective-permute-done.12.refs_2_
  56.2 1.3 %collective-permute-done.13.refs_3_ = bf16[128,128]{1,0:T(8,128)(2,1)S(1)} collective-permute-done((bf16[128,128]{1,0:T(8,128)(2,1)S(1)}, bf16[128,128]{1,0:T(8,128)(2,1)S(1)}, u32[]{:S(2)}, u32[]{:S(2)}) %collective-permute-start.13) | collective-permute-done | bytes 32800 | tf_op jit(solution)/shard_map/ppermute | solution.py:843
  57.5 0.1 collective-permute-start.14
  57.6 1.0 collective-permute-start.15
  58.6 0.8 collective-permute-start.16
  59.5 2.1 %collective-permute-done.15.refs_4_.refs_10_ = bf16[128,64]{1,0:T(8,128)(2,1)S(1)} collective-permute-done((bf16[128,64]{1,0:T(8,128)(2,1)S(1)}, bf16[128,64]{1,0:T(8,128)(2,1)S(1)}, u32[]{:S(2)}, u32[]{:S(2)}) %collective-permute-start.15) | collective-permute-done | bytes 16416 | tf_op jit(solution)/shard_map/ppermute | solution.py:32
  61.6 0.4 collective-permute-done.16.refs_5_.refs_11_
  62.0 0.2 collective-permute-start.17
  62.2 1.1 collective-permute-start.18
  63.3 0.6 collective-permute-start.19
  63.9 2.2 %collective-permute-done.18.refs_4_.refs_10_ = bf16[128,128]{1,0:T(8,128)(2,1)S(1)} collective-permute-done((bf16[128,128]{1,0:T(8,128)(2,1)S(1)}, bf16[128,128]{1,0:T(8,128)(2,1)S(1)}, u32[]{:S(2)}, u32[]{:S(2)}) %collective-permute-start.18) | collective-permute-done | bytes 32800 | tf_op jit(solution)/shard_map/ppermute | solution.py:37
  66.1 0.6 collective-permute-done.19.refs_5_.refs_11_
  66.8 0.2 collective-permute-start.20
  67.0 0.9 collective-permute-start.21
  67.9 0.8 collective-permute-start.22
  68.7 0.6 shard_map.124.refs_1_
  69.4 1.5 %collective-permute-done.21.refs_14_ = bf16[128,128]{1,0:T(8,128)(2,1)S(1)} collective-permute-done((bf16[128,128]{1,0:T(8,128)(2,1)S(1)}, bf16[128,128]{1,0:T(8,128)(2,1)S(1)}, u32[]{:S(2)}, u32[]{:S(2)}) %collective-permute-start.21) | collective-permute-done | bytes 32800 | tf_op jit(solution)/shard_map/ppermute | solution.py:37
  70.9 0.4 collective-permute-done.22.refs_15_
  71.3 0.2 collective-permute-start.25
  71.5 6.6 %collective-permute-start.23 = (bf16[160,64]{1,0:T(8,128)(2,1)S(1)}, bf16[160,64]{1,0:T(8,128)(2,1)S(1)}, u32[]{:S(2)}, u32[]{:S(2)}) collective-permute-start(bf16[160,64]{1,0:T(8,128)(2,1)S(1)} %get-tuple-element.64), channel_id=1, source_target_pairs={{0,8},{8,0},{16,24},{24,16},{1,9},{9,1},{17,25},{25,17},{2,10},{10... | collective-permute-start | bytes 61448 | tf_op jit(solution)/shard_map/ppermute | solution.py:890
  78.1 10.1 %collective-permute-start.24 = (bf16[128,64]{1,0:T(8,128)(2,1)S(1)}, bf16[128,64]{1,0:T(8,128)(2,1)S(1)}, u32[]{:S(2)}, u32[]{:S(2)}) collective-permute-start(bf16[128,64]{1,0:T(8,128)(2,1)S(1)} %get-tuple-element.59.refs_7_), channel_id=1, source_target_pairs={{0,16},{8,24},{16,0},{24,8},{1,17},{9,25},{17,1},{25,9},{2,18},{10... | collective-permute-start | bytes 49160 | tf_op jit(solution)/shard_map/ppermute | solution.py:873
  88.2 0.1 collective-permute-start.26
  88.3 1.1 collective-permute-start.27
  89.4 1.3 %collective-permute-done.24.refs_1_ = bf16[128,64]{1,0:T(8,128)(2,1)S(1)} collective-permute-done((bf16[128,64]{1,0:T(8,128)(2,1)S(1)}, bf16[128,64]{1,0:T(8,128)(2,1)S(1)}, u32[]{:S(2)}, u32[]{:S(2)}) %collective-permute-start.24) | collective-permute-done | bytes 16416 | tf_op jit(solution)/shard_map/ppermute | solution.py:873
  90.7 3.3 %collective-permute-done.26.refs_12_ = bf16[128,64]{1,0:T(8,128)(2,1)S(1)} collective-permute-done((bf16[128,64]{1,0:T(8,128)(2,1)S(1)}, bf16[128,64]{1,0:T(8,128)(2,1)S(1)}, u32[]{:S(2)}, u32[]{:S(2)}) %collective-permute-start.26) | collective-permute-done | bytes 16416 | tf_op jit(solution)/shard_map/ppermute | solution.py:893
  94.0 1.0 collective-permute-done.27.refs_13_
  95.0 1.1 shard_map.131
  96.0 0.1 collective-permute-start.32
  96.1 1.3 %collective-permute-done.32 = bf16[5,64,128]{2,1,0:T(8,128)(2,1)S(1)} collective-permute-done((bf16[5,64,128]{2,1,0:T(8,128)(2,1)S(1)}, bf16[5,64,128]{2,1,0:T(8,128)(2,1)S(1)}, u32[]{:S(2)}, u32[]{:S(2)}) %collective-permute-start.32) | collective-permute-done | bytes 81952 | tf_op jit(solution)/shard_map/ppermute | solution.py:929
  97.4 1.2 %collective-permute-start.33 = (bf16[5,64,128]{2,1,0:T(8,128)(2,1)S(1)}, bf16[5,64,128]{2,1,0:T(8,128)(2,1)S(1)}, u32[]{:S(2)}, u32[]{:S(2)}) collective-permute-start(bf16[5,64,128]{2,1,0:T(8,128)(2,1)S(1)} %add_convert_fusion.refs_12_), channel_id=1, source_target_pairs={{0,4},{1,5},{2,6},{3,7},{4,0},{5,1},{6,2},{7,3},{8,12},{9,13},{10,... | collective-permute-start | bytes 245768 | tf_op jit(solution)/shard_map/ppermute | solution.py:941
  98.6 1.5 %collective-permute-start.34 = (bf16[5,64,128]{2,1,0:T(8,128)(2,1)S(1)}, bf16[5,64,128]{2,1,0:T(8,128)(2,1)S(1)}, u32[]{:S(2)}, u32[]{:S(2)}) collective-permute-start(bf16[5,64,128]{2,1,0:T(8,128)(2,1)S(1)} %add_convert_fusion.refs_12_), channel_id=1, source_target_pairs={{0,1},{1,0},{2,3},{3,2},{4,5},{5,4},{6,7},{7,6},{8,9},{9,8},{10,11... | collective-permute-start | bytes 245768 | tf_op jit(solution)/shard_map/ppermute | solution.py:941
  100.1 0.9 collective-permute-start.35
  101.0 1.5 %collective-permute-start.31 = (f32[1,9216]{1,0:T(1,128)S(1)}, f32[1,9216]{1,0:T(1,128)S(1)}, u32[]{:S(2)}, u32[]{:S(2)}) collective-permute-start(f32[1,9216]{1,0:T(1,128)S(1)} %copy-done.7), channel_id=1, source_target_pairs={{0,1},{1,0},{2,3},{3,2},{4,5},{5,4},{6,7},{7,6},{8,9},{9,8},{10,11... | collective-permute-start | bytes 110600 | tf_op jit(solution)/shard_map/ppermute | solution.py:32
  102.5 3.1 %collective-permute-done.31.refs_11_ = f32[1,9216]{1,0:T(1,128)S(1)} collective-permute-done((f32[1,9216]{1,0:T(1,128)S(1)}, f32[1,9216]{1,0:T(1,128)S(1)}, u32[]{:S(2)}, u32[]{:S(2)}) %collective-permute-start.31) | collective-permute-done | bytes 36896 | tf_op jit(solution)/shard_map/ppermute | solution.py:32
  105.6 0.8 collective-permute-done.28.refs_1_
  106.4 1.2 %collective-permute-start.30 = (bf16[128,64]{1,0:T(8,128)(2,1)S(1)}, bf16[128,64]{1,0:T(8,128)(2,1)S(1)}, u32[]{:S(2)}, u32[]{:S(2)}) collective-permute-start(bf16[128,64]{1,0:T(8,128)(2,1)S(1)} %get-tuple-element.74.refs_0_), channel_id=1, source_target_pairs={{0,24},{8,16},{16,8},{24,0},{1,25},{9,17},{17,9},{25,1},{2,26},{10... | collective-permute-start | bytes 49160 | tf_op jit(solution)/shard_map/ppermute | solution.py:923
  107.6 2.8 %collective-permute-done.29.refs_2_ = bf16[128,64]{1,0:T(8,128)(2,1)S(1)} collective-permute-done((bf16[128,64]{1,0:T(8,128)(2,1)S(1)}, bf16[128,64]{1,0:T(8,128)(2,1)S(1)}, u32[]{:S(2)}, u32[]{:S(2)}) %collective-permute-start.29) | collective-permute-done | bytes 16416 | tf_op jit(solution)/shard_map/ppermute | solution.py:924
  110.4 1.7 %collective-permute-done.30.refs_3_ = bf16[128,64]{1,0:T(8,128)(2,1)S(1)} collective-permute-done((bf16[128,64]{1,0:T(8,128)(2,1)S(1)}, bf16[128,64]{1,0:T(8,128)(2,1)S(1)}, u32[]{:S(2)}, u32[]{:S(2)}) %collective-permute-start.30) | collective-permute-done | bytes 16416 | tf_op jit(solution)/shard_map/ppermute | solution.py:923
  112.1 3.4 %shard_map.132 = (f32[64,128]{1,0:T(8,128)}, f32[64,3072]{1,0:T(8,128)}) custom-call(bf16[128,64]{1,0:T(8,128)(2,1)S(1)} %get-tuple-element.74.refs_0_, bf16[128,64]{1,0:T(8,128)(2,1)S(1)} %collective-permute-done.28.refs_1_, bf16[128,64]{1,0:T(8,128)(2,1)S(1)} %collective-permute-done.29.refs_2_, bf16[128,64]{1,0:T(8,128)(2,1)S(1)} %collective-permute-done.30.refs_3_, ...), custom_call_target="tpu_custom_call" | custom-call | flops 805306368 | bytes 4825088 | tf_op jit(solution)/shard_map/pallas_call | solution.py:180
  (37 shorter events, 0.2 us)
Async XLA Ops:
  1.7 12.2 %collective-permute-start.7 = (bf16[128,1536]{1,0:T(8,128)(2,1)S(1)}, bf16[128,1536]{1,0:T(8,128)(2,1)S(1)}, u32[]{:S(2)}, u32[]{:S(2)}) collective-permute-start(bf16[128,1536]{1,0:T(8,128)(2,1)S(1)} %dynamic-slice_bitcast_fusion), channel_id=1, source_target_pairs={{0,4},{2,6},{4,0},{6,2},{1,5},{3,7},{5,1},{7,3},{8,12},{10,14},{12... | collective-permute-start | bytes 1179656 | tf_op jit(solution)/shard_map/ppermute | solution.py:51
  4.7 44.3 %collective-permute-start.6 = (bf16[128,3072]{1,0:T(8,128)(2,1)}, bf16[128,3072]{1,0:T(8,128)(2,1)S(1)}, u32[]{:S(2)}, u32[]{:S(2)}) collective-permute-start(bf16[128,3072]{1,0:T(8,128)(2,1)} %bitcast.21), channel_id=1, source_target_pairs={{0,2},{2,0},{4,6},{6,4},{1,3},{3,1},{5,7},{7,5},{8,10},{10,8},{12,... | collective-permute-start | bytes 2359304 | tf_op jit(solution)/shard_map/ppermute | solution.py:55
  13.8 10.3 %collective-permute-start.8 = (bf16[128,1536]{1,0:T(8,128)(2,1)S(1)}, bf16[128,1536]{1,0:T(8,128)(2,1)S(1)}, u32[]{:S(2)}, u32[]{:S(2)}) collective-permute-start(bf16[128,1536]{1,0:T(8,128)(2,1)S(1)} %collective-permute-done.7.refs_8_.refs_7_), channel_id=1, source_target_pairs={{0,1},{1,0},{2,3},{3,2},{4,5},{5,4},{6,7},{7,6},{8,9},{9,8},{10,11... | collective-permute-start | bytes 1179656 | tf_op jit(solution)/shard_map/ppermute | solution.py:52
  15.6 33.5 %collective-permute-start.9 = (bf16[128,1536]{1,0:T(8,128)(2,1)S(1)}, bf16[128,1536]{1,0:T(8,128)(2,1)S(1)}, u32[]{:S(2)}, u32[]{:S(2)}) collective-permute-start(bf16[128,1536]{1,0:T(8,128)(2,1)S(1)} %collective-permute-done.7.refs_8_.refs_7_), channel_id=1, source_target_pairs={{0,2},{2,0},{4,6},{6,4},{1,3},{3,1},{5,7},{7,5},{8,10},{10,8},{12,... | collective-permute-start | bytes 1179656 | tf_op jit(solution)/shard_map/ppermute | solution.py:55
  24.1 24.9 %collective-permute-start.10 = (bf16[128,1536]{1,0:T(8,128)(2,1)S(1)}, bf16[128,1536]{1,0:T(8,128)(2,1)S(1)}, u32[]{:S(2)}, u32[]{:S(2)}) collective-permute-start(bf16[128,1536]{1,0:T(8,128)(2,1)S(1)} %collective-permute-done.8.refs_9_.refs_8_), channel_id=1, source_target_pairs={{0,2},{2,0},{4,6},{6,4},{1,3},{3,1},{5,7},{7,5},{8,10},{10,8},{12,... | collective-permute-start | bytes 1179656 | tf_op jit(solution)/shard_map/ppermute | solution.py:55
  24.1 16.7 %copy-start = (bf16[1,64,3072]{2,1,0:T(8,128)(2,1)S(1)}, bf16[1,64,3072]{2,1,0:T(8,128)(2,1)}, u32[]{:S(2)}) copy-start(bf16[1,64,3072]{2,1,0:T(8,128)(2,1)} %refs_4_.1) | copy-start | bytes 1179652
  24.1 16.7 %copy-start.2 = (bf16[1,3072,1,3,128]{4,1,3,2,0:T(8,128)(2,1)S(1)}, bf16[1,3072,1,3,128]{4,1,3,2,0:T(8,128)(2,1)}, u32[]{:S(2)}) copy-start(bf16[1,3072,1,3,128]{4,1,3,2,0:T(8,128)(2,1)} %param.18) | copy-start | bytes 7077892
  24.1 16.7 %copy-start.6 = (f32[1,2,128]{2,1,0:T(2,128)S(1)}, f32[1,2,128]{2,1,0:T(2,128)}, u32[]{:S(2)}) copy-start(f32[1,2,128]{2,1,0:T(2,128)} %refs_2_.3) | copy-start | bytes 3076
  35.1 14.0 %copy-start.1 = (bf16[1,1,128,3072]{3,2,1,0:T(8,128)(2,1)S(1)}, bf16[1,1,128,3072]{3,2,1,0:T(8,128)(2,1)}, u32[]{:S(2)}) copy-start(bf16[1,1,128,3072]{3,2,1,0:T(8,128)(2,1)} %param.19) | copy-start | bytes 2359300
  35.1 2.0 %collective-permute-start = (bf16[128,128]{1,0:T(8,128)(2,1)S(1)}, bf16[128,128]{1,0:T(8,128)(2,1)S(1)}, u32[]{:S(2)}, u32[]{:S(2)}) collective-permute-start(bf16[128,128]{1,0:T(8,128)(2,1)S(1)} %get-tuple-element.40.refs_3_), channel_id=1, source_target_pairs={{0,2},{2,0},{4,6},{6,4},{1,3},{3,1},{5,7},{7,5},{8,10},{10,8},{12,... | collective-permute-start | bytes 98312 | tf_op jit(solution)/shard_map/ppermute | solution.py:32
  35.6 3.9 %collective-permute-start.1 = (bf16[128,128]{1,0:T(8,128)(2,1)S(1)}, bf16[128,128]{1,0:T(8,128)(2,1)S(1)}, u32[]{:S(2)}, u32[]{:S(2)}) collective-permute-start(bf16[128,128]{1,0:T(8,128)(2,1)S(1)} %get-tuple-element.40.refs_3_), channel_id=1, source_target_pairs={{0,4},{2,6},{4,0},{6,2},{1,5},{3,7},{5,1},{7,3},{8,12},{10,14},{12... | collective-permute-start | bytes 98312 | tf_op jit(solution)/shard_map/ppermute | solution.py:32
  37.1 3.7 %collective-permute-start.2 = (bf16[128,128]{1,0:T(8,128)(2,1)S(1)}, bf16[128,128]{1,0:T(8,128)(2,1)S(1)}, u32[]{:S(2)}, u32[]{:S(2)}) collective-permute-start(bf16[128,128]{1,0:T(8,128)(2,1)S(1)} %get-tuple-element.40.refs_3_), channel_id=1, source_target_pairs={{0,6},{2,4},{4,2},{6,0},{1,7},{3,5},{5,3},{7,1},{8,14},{10,12},{12... | collective-permute-start | bytes 98312 | tf_op jit(solution)/shard_map/ppermute | solution.py:32
  44.4 1.3 %collective-permute-start.3 = (bf16[128,128]{1,0:T(8,128)(2,1)S(1)}, bf16[128,128]{1,0:T(8,128)(2,1)S(1)}, u32[]{:S(2)}, u32[]{:S(2)}) collective-permute-start(bf16[128,128]{1,0:T(8,128)(2,1)S(1)} %get-tuple-element.44), channel_id=1, source_target_pairs={{0,2},{2,0},{4,6},{6,4},{1,3},{3,1},{5,7},{7,5},{8,10},{10,8},{12,... | collective-permute-start | bytes 98312 | tf_op jit(solution)/shard_map/ppermute | solution.py:37
  44.6 3.9 %collective-permute-start.4 = (bf16[128,128]{1,0:T(8,128)(2,1)S(1)}, bf16[128,128]{1,0:T(8,128)(2,1)S(1)}, u32[]{:S(2)}, u32[]{:S(2)}) collective-permute-start(bf16[128,128]{1,0:T(8,128)(2,1)S(1)} %get-tuple-element.45), channel_id=1, source_target_pairs={{0,4},{2,6},{4,0},{6,2},{1,5},{3,7},{5,1},{7,3},{8,12},{10,14},{12... | collective-permute-start | bytes 98312 | tf_op jit(solution)/shard_map/ppermute | solution.py:37
  45.7 3.3 %collective-permute-start.5 = (bf16[128,128]{1,0:T(8,128)(2,1)S(1)}, bf16[128,128]{1,0:T(8,128)(2,1)S(1)}, u32[]{:S(2)}, u32[]{:S(2)}) collective-permute-start(bf16[128,128]{1,0:T(8,128)(2,1)S(1)} %get-tuple-element.46), channel_id=1, source_target_pairs={{0,6},{2,4},{4,2},{6,0},{1,7},{3,5},{5,3},{7,1},{8,14},{10,12},{12... | collective-permute-start | bytes 98312 | tf_op jit(solution)/shard_map/ppermute | solution.py:37
  52.0 3.9 %collective-permute-start.11 = (bf16[128,128]{1,0:T(8,128)(2,1)S(1)}, bf16[128,128]{1,0:T(8,128)(2,1)S(1)}, u32[]{:S(2)}, u32[]{:S(2)}) collective-permute-start(bf16[128,128]{1,0:T(8,128)(2,1)S(1)} %get-tuple-element.48.refs_0_), channel_id=1, source_target_pairs={{0,8},{1,9},{2,10},{3,11},{4,12},{5,13},{6,14},{7,15}} | collective-permute-start | bytes 98312 | tf_op jit(solution)/shard_map/ppermute | solution.py:843
  53.3 2.9 %collective-permute-start.12 = (bf16[128,128]{1,0:T(8,128)(2,1)S(1)}, bf16[128,128]{1,0:T(8,128)(2,1)S(1)}, u32[]{:S(2)}, u32[]{:S(2)}) collective-permute-start(bf16[128,128]{1,0:T(8,128)(2,1)S(1)} %get-tuple-element.48.refs_0_), channel_id=1, source_target_pairs={{0,16},{1,17},{2,18},{3,19},{4,20},{5,21},{6,22},{7,23}} | collective-permute-start | bytes 98312 | tf_op jit(solution)/shard_map/ppermute | solution.py:843
  54.6 2.9 %collective-permute-start.13 = (bf16[128,128]{1,0:T(8,128)(2,1)S(1)}, bf16[128,128]{1,0:T(8,128)(2,1)S(1)}, u32[]{:S(2)}, u32[]{:S(2)}) collective-permute-start(bf16[128,128]{1,0:T(8,128)(2,1)S(1)} %get-tuple-element.48.refs_0_), channel_id=1, source_target_pairs={{0,24},{1,25},{2,26},{3,27},{4,28},{5,29},{6,30},{7,31}} | collective-permute-start | bytes 98312 | tf_op jit(solution)/shard_map/ppermute | solution.py:843
  57.5 1.9 %collective-permute-start.14 = (bf16[128,64]{1,0:T(8,128)(2,1)S(1)}, bf16[128,64]{1,0:T(8,128)(2,1)S(1)}, u32[]{:S(2)}, u32[]{:S(2)}) collective-permute-start(bf16[128,64]{1,0:T(8,128)(2,1)S(1)} %get-tuple-element.49.refs_2_.refs_8_), channel_id=1, source_target_pairs={{0,2},{2,0},{4,6},{6,4},{1,3},{3,1},{5,7},{7,5},{8,10},{10,8},{12,... | collective-permute-start | bytes 49160 | tf_op jit(solution)/shard_map/ppermute | solution.py:32
  57.6 4.0 %collective-permute-start.15 = (bf16[128,64]{1,0:T(8,128)(2,1)S(1)}, bf16[128,64]{1,0:T(8,128)(2,1)S(1)}, u32[]{:S(2)}, u32[]{:S(2)}) collective-permute-start(bf16[128,64]{1,0:T(8,128)(2,1)S(1)} %get-tuple-element.49.refs_2_.refs_8_), channel_id=1, source_target_pairs={{0,4},{2,6},{4,0},{6,2},{1,5},{3,7},{5,1},{7,3},{8,12},{10,14},{12... | collective-permute-start | bytes 49160 | tf_op jit(solution)/shard_map/ppermute | solution.py:32
  58.6 3.4 %collective-permute-start.16 = (bf16[128,64]{1,0:T(8,128)(2,1)S(1)}, bf16[128,64]{1,0:T(8,128)(2,1)S(1)}, u32[]{:S(2)}, u32[]{:S(2)}) collective-permute-start(bf16[128,64]{1,0:T(8,128)(2,1)S(1)} %get-tuple-element.49.refs_2_.refs_8_), channel_id=1, source_target_pairs={{0,6},{2,4},{4,2},{6,0},{1,7},{3,5},{5,3},{7,1},{8,14},{10,12},{12... | collective-permute-start | bytes 49160 | tf_op jit(solution)/shard_map/ppermute | solution.py:32
  62.0 9.3 %copy-start.4 = (f32[80,384]{1,0:T(8,128)S(1)}, f32[80,384]{1,0:T(8,128)}, u32[]{:S(2)}) copy-start(f32[80,384]{1,0:T(8,128)} %get-tuple-element.41.refs_6_.refs_0_) | copy-start | bytes 368644
  62.0 1.9 %collective-permute-start.17 = (bf16[128,128]{1,0:T(8,128)(2,1)S(1)}, bf16[128,128]{1,0:T(8,128)(2,1)S(1)}, u32[]{:S(2)}, u32[]{:S(2)}) collective-permute-start(bf16[128,128]{1,0:T(8,128)(2,1)S(1)} %get-tuple-element.56), channel_id=1, source_target_pairs={{0,2},{2,0},{4,6},{6,4},{1,3},{3,1},{5,7},{7,5},{8,10},{10,8},{12,... | collective-permute-start | bytes 98312 | tf_op jit(solution)/shard_map/ppermute | solution.py:37
  62.2 3.9 %collective-permute-start.18 = (bf16[128,128]{1,0:T(8,128)(2,1)S(1)}, bf16[128,128]{1,0:T(8,128)(2,1)S(1)}, u32[]{:S(2)}, u32[]{:S(2)}) collective-permute-start(bf16[128,128]{1,0:T(8,128)(2,1)S(1)} %get-tuple-element.57), channel_id=1, source_target_pairs={{0,4},{2,6},{4,0},{6,2},{1,5},{3,7},{5,1},{7,3},{8,12},{10,14},{12... | collective-permute-start | bytes 98312 | tf_op jit(solution)/shard_map/ppermute | solution.py:37
  63.3 3.4 %collective-permute-start.19 = (bf16[128,128]{1,0:T(8,128)(2,1)S(1)}, bf16[128,128]{1,0:T(8,128)(2,1)S(1)}, u32[]{:S(2)}, u32[]{:S(2)}) collective-permute-start(bf16[128,128]{1,0:T(8,128)(2,1)S(1)} %get-tuple-element.58), channel_id=1, source_target_pairs={{0,6},{2,4},{4,2},{6,0},{1,7},{3,5},{5,3},{7,1},{8,14},{10,12},{12... | collective-permute-start | bytes 98312 | tf_op jit(solution)/shard_map/ppermute | solution.py:37
  66.8 28.2 %copy-start.3 = (bf16[4,128,128]{2,1,0:T(8,128)(2,1)S(1)}, bf16[4,128,128]{2,1,0:T(8,128)(2,1)}, u32[]{:S(2)}) copy-start(bf16[4,128,128]{2,1,0:T(8,128)(2,1)} %get-tuple-element.66.refs_5_) | copy-start | bytes 393220
  66.8 28.2 %copy-start.5 = (f32[128,128]{1,0:T(8,128)S(1)}, f32[128,128]{1,0:T(8,128)}, u32[]{:S(2)}) copy-start(f32[128,128]{1,0:T(8,128)} %get-tuple-element.67.refs_6_) | copy-start | bytes 196612
  66.8 34.2 %copy-start.7 = (f32[1,9216]{1,0:T(1,128)S(1)}, f32[1,9216]{1,0:T(1,128)}, u32[]{:S(2)}) copy-start(f32[1,9216]{1,0:T(1,128)} %get-tuple-element.47.refs_12_.refs_16_) | copy-start | bytes 110596
  66.8 2.6 %collective-permute-start.20 = (bf16[128,128]{1,0:T(8,128)(2,1)S(1)}, bf16[128,128]{1,0:T(8,128)(2,1)S(1)}, u32[]{:S(2)}, u32[]{:S(2)}) collective-permute-start(bf16[128,128]{1,0:T(8,128)(2,1)S(1)} %get-tuple-element.61), channel_id=1, source_target_pairs={{0,2},{2,0},{4,6},{6,4},{1,3},{3,1},{5,7},{7,5},{8,10},{10,8},{12,... | collective-permute-start | bytes 98312 | tf_op jit(solution)/shard_map/ppermute | solution.py:37
  67.0 3.9 %collective-permute-start.21 = (bf16[128,128]{1,0:T(8,128)(2,1)S(1)}, bf16[128,128]{1,0:T(8,128)(2,1)S(1)}, u32[]{:S(2)}, u32[]{:S(2)}) collective-permute-start(bf16[128,128]{1,0:T(8,128)(2,1)S(1)} %get-tuple-element.62), channel_id=1, source_target_pairs={{0,4},{2,6},{4,0},{6,2},{1,5},{3,7},{5,1},{7,3},{8,12},{10,14},{12... | collective-permute-start | bytes 98312 | tf_op jit(solution)/shard_map/ppermute | solution.py:37
  67.9 3.4 %collective-permute-start.22 = (bf16[128,128]{1,0:T(8,128)(2,1)S(1)}, bf16[128,128]{1,0:T(8,128)(2,1)S(1)}, u32[]{:S(2)}, u32[]{:S(2)}) collective-permute-start(bf16[128,128]{1,0:T(8,128)(2,1)S(1)} %get-tuple-element.63), channel_id=1, source_target_pairs={{0,6},{2,4},{4,2},{6,0},{1,7},{3,5},{5,3},{7,1},{8,14},{10,12},{12... | collective-permute-start | bytes 98312 | tf_op jit(solution)/shard_map/ppermute | solution.py:37
  71.3 16.9 %collective-permute-start.25 = (bf16[2,128,64]{2,1,0:T(8,128)(2,1)S(1)}, bf16[2,128,64]{2,1,0:T(8,128)(2,1)S(1)}, u32[]{:S(2)}, u32[]{:S(2)}) collective-permute-start(bf16[2,128,64]{2,1,0:T(8,128)(2,1)S(1)} %get-tuple-element.71), channel_id=1, source_target_pairs={{0,2},{2,0},{4,6},{6,4},{1,3},{3,1},{5,7},{7,5},{8,10},{10,8},{12,... | collective-permute-start | bytes 98312 | tf_op jit(solution)/shard_map/ppermute | solution.py:889
  71.5 19.1 %collective-permute-start.23 = (bf16[160,64]{1,0:T(8,128)(2,1)S(1)}, bf16[160,64]{1,0:T(8,128)(2,1)S(1)}, u32[]{:S(2)}, u32[]{:S(2)}) collective-permute-start(bf16[160,64]{1,0:T(8,128)(2,1)S(1)} %get-tuple-element.64), channel_id=1, source_target_pairs={{0,8},{8,0},{16,24},{24,16},{1,9},{9,1},{17,25},{25,17},{2,10},{10... | collective-permute-start | bytes 61448 | tf_op jit(solution)/shard_map/ppermute | solution.py:890
  78.1 12.5 %collective-permute-start.24 = (bf16[128,64]{1,0:T(8,128)(2,1)S(1)}, bf16[128,64]{1,0:T(8,128)(2,1)S(1)}, u32[]{:S(2)}, u32[]{:S(2)}) collective-permute-start(bf16[128,64]{1,0:T(8,128)(2,1)S(1)} %get-tuple-element.59.refs_7_), channel_id=1, source_target_pairs={{0,16},{8,24},{16,0},{24,8},{1,17},{9,25},{17,1},{25,9},{2,18},{10... | collective-permute-start | bytes 49160 | tf_op jit(solution)/shard_map/ppermute | solution.py:873
  88.2 5.8 %collective-permute-start.26 = (bf16[128,64]{1,0:T(8,128)(2,1)S(1)}, bf16[128,64]{1,0:T(8,128)(2,1)S(1)}, u32[]{:S(2)}, u32[]{:S(2)}) collective-permute-start(bf16[128,64]{1,0:T(8,128)(2,1)S(1)} %get-tuple-element.72), channel_id=1, source_target_pairs={{0,8},{2,10},{4,12},{6,14},{8,16},{10,18},{12,20},{14,22},{16,24},... | collective-permute-start | bytes 49160 | tf_op jit(solution)/shard_map/ppermute | solution.py:893
  88.3 6.6 %collective-permute-start.27 = (bf16[128,64]{1,0:T(8,128)(2,1)S(1)}, bf16[128,64]{1,0:T(8,128)(2,1)S(1)}, u32[]{:S(2)}, u32[]{:S(2)}) collective-permute-start(bf16[128,64]{1,0:T(8,128)(2,1)S(1)} %get-tuple-element.73), channel_id=1, source_target_pairs={{0,12},{2,14},{4,8},{6,10},{8,20},{10,22},{12,16},{14,18},{16,28},... | collective-permute-start | bytes 49160 | tf_op jit(solution)/shard_map/ppermute | solution.py:893
  96.0 1.3 %collective-permute-start.32 = (bf16[5,64,128]{2,1,0:T(8,128)(2,1)S(1)}, bf16[5,64,128]{2,1,0:T(8,128)(2,1)S(1)}, u32[]{:S(2)}, u32[]{:S(2)}) collective-permute-start(bf16[5,64,128]{2,1,0:T(8,128)(2,1)S(1)} %get-tuple-element.75), channel_id=1, source_target_pairs={{0,2},{2,0},{4,6},{6,4},{1,3},{3,1},{5,7},{7,5},{8,10},{10,8},{12,... | collective-permute-start | bytes 245768 | tf_op jit(solution)/shard_map/ppermute | solution.py:929
  97.4 14.7 %collective-permute-start.33 = (bf16[5,64,128]{2,1,0:T(8,128)(2,1)S(1)}, bf16[5,64,128]{2,1,0:T(8,128)(2,1)S(1)}, u32[]{:S(2)}, u32[]{:S(2)}) collective-permute-start(bf16[5,64,128]{2,1,0:T(8,128)(2,1)S(1)} %add_convert_fusion.refs_12_), channel_id=1, source_target_pairs={{0,4},{1,5},{2,6},{3,7},{4,0},{5,1},{6,2},{7,3},{8,12},{9,13},{10,... | collective-permute-start | bytes 245768 | tf_op jit(solution)/shard_map/ppermute | solution.py:941
  98.6 13.5 %collective-permute-start.34 = (bf16[5,64,128]{2,1,0:T(8,128)(2,1)S(1)}, bf16[5,64,128]{2,1,0:T(8,128)(2,1)S(1)}, u32[]{:S(2)}, u32[]{:S(2)}) collective-permute-start(bf16[5,64,128]{2,1,0:T(8,128)(2,1)S(1)} %add_convert_fusion.refs_12_), channel_id=1, source_target_pairs={{0,1},{1,0},{2,3},{3,2},{4,5},{5,4},{6,7},{7,6},{8,9},{9,8},{10,11... | collective-permute-start | bytes 245768 | tf_op jit(solution)/shard_map/ppermute | solution.py:941
  100.1 12.0 %collective-permute-start.35 = (bf16[5,64,128]{2,1,0:T(8,128)(2,1)S(1)}, bf16[5,64,128]{2,1,0:T(8,128)(2,1)S(1)}, u32[]{:S(2)}, u32[]{:S(2)}) collective-permute-start(bf16[5,64,128]{2,1,0:T(8,128)(2,1)S(1)} %add_convert_fusion.refs_12_), channel_id=1, source_target_pairs={{0,5},{1,4},{2,7},{3,6},{4,1},{5,0},{6,3},{7,2},{8,13},{9,12},{10,... | collective-permute-start | bytes 245768 | tf_op jit(solution)/shard_map/ppermute | solution.py:941
  101.0 4.6 %collective-permute-start.31 = (f32[1,9216]{1,0:T(1,128)S(1)}, f32[1,9216]{1,0:T(1,128)S(1)}, u32[]{:S(2)}, u32[]{:S(2)}) collective-permute-start(f32[1,9216]{1,0:T(1,128)S(1)} %copy-done.7), channel_id=1, source_target_pairs={{0,1},{1,0},{2,3},{3,2},{4,5},{5,4},{6,7},{7,6},{8,9},{9,8},{10,11... | collective-permute-start | bytes 110600 | tf_op jit(solution)/shard_map/ppermute | solution.py:32
  102.5 3.9 %collective-permute-start.28 = (bf16[128,64]{1,0:T(8,128)(2,1)S(1)}, bf16[128,64]{1,0:T(8,128)(2,1)S(1)}, u32[]{:S(2)}, u32[]{:S(2)}) collective-permute-start(bf16[128,64]{1,0:T(8,128)(2,1)S(1)} %get-tuple-element.74.refs_0_), channel_id=1, source_target_pairs={{0,8},{8,0},{16,24},{24,16},{1,9},{9,1},{17,25},{25,17},{2,10},{10... | collective-permute-start | bytes 49160 | tf_op jit(solution)/shard_map/ppermute | solution.py:925
  105.6 4.8 %collective-permute-start.29 = (bf16[128,64]{1,0:T(8,128)(2,1)S(1)}, bf16[128,64]{1,0:T(8,128)(2,1)S(1)}, u32[]{:S(2)}, u32[]{:S(2)}) collective-permute-start(bf16[128,64]{1,0:T(8,128)(2,1)S(1)} %get-tuple-element.74.refs_0_), channel_id=1, source_target_pairs={{0,16},{8,24},{16,0},{24,8},{1,17},{9,25},{17,1},{25,9},{2,18},{10... | collective-permute-start | bytes 49160 | tf_op jit(solution)/shard_map/ppermute | solution.py:924
  106.4 5.7 %collective-permute-start.30 = (bf16[128,64]{1,0:T(8,128)(2,1)S(1)}, bf16[128,64]{1,0:T(8,128)(2,1)S(1)}, u32[]{:S(2)}, u32[]{:S(2)}) collective-permute-start(bf16[128,64]{1,0:T(8,128)(2,1)S(1)} %get-tuple-element.74.refs_0_), channel_id=1, source_target_pairs={{0,24},{8,16},{16,8},{24,0},{1,25},{9,17},{17,9},{25,1},{2,26},{10... | collective-permute-start | bytes 49160 | tf_op jit(solution)/shard_map/ppermute | solution.py:923

commit v8 on v7

--- a/solution.py
+++ b/solution.py
@@ -13,7 +13,7 @@
 EPS = 1e-06
 ADV_WEIGHT = 3.0
 TILE = 512
-STREAMS = 6
+STREAMS = 12
 SPARE = 8 << 20
 VMEM = pl.BlockSpec(memory_space=pltpu.VMEM)
 HBM = pl.BlockSpec(memory_space=pltpu.HBM)
@@ -39,17 +39,18 @@
     ]
 
 
-def spread_heads(own, count, groups):
+def spread_heads(own, count, groups, stage):
     held = {0: [own]}
     bit = count // 2
     first = True
     while bit:
         for offset in sorted(held):
             if first and groups == 2:
-                width = own.shape[1] // 2
-                part = lax.dynamic_slice_in_dim(own, lax.axis_index("dp") * width, width, axis=1)
+                width = own.shape[1] // 3
+                shift = lax.axis_index("dp") * width
+                part = lax.dynamic_slice_in_dim(own, shift, 2 * width, axis=1)
                 near = lax.ppermute(part, "seq", swaps(count, bit))
-                held[bit] = [near, lax.ppermute(near, "dp", swaps(groups, 1))]
+                held[bit] = [near, lax.ppermute(stage(near), "dp", swaps(groups, 1))]
             else:
                 held[offset | bit] = [
                     lax.ppermute(piece, "seq", swaps(count, bit))
@@ -63,10 +64,16 @@
 def head_tile(pieces, first, size):
     if len(pieces) == 1:
         return pieces[0][:, first : first + size]
-    width = pieces[0].shape[1]
-    inside = slice(first % width, first % width + size)
-    near = lax.axis_index("dp") == first // width
-    return jnp.where(near, pieces[0][:, inside], pieces[1][:, inside])
+    near, far = pieces
+    width = far.shape[1]
+    low = slice(first % width, first % width + size)
+    high = slice(width + first % width, width + first % width + size)
+    choices = (
+        (near[:, low], far[:, low]),
+        (near[:, high], near[:, low]),
+        (far[:, low], near[:, high]),
+    )[first // width]
+    return jnp.where(lax.axis_index("dp") == 0, *choices)
 
 
 def nested(refs, sizes):
@@ -306,10 +313,23 @@
         )
 
 
+def stage_kernel(fetches, near, kind_out, part_out, arrival):
+    copy = pltpu.make_async_copy(fetches[0], kind_out, arrival.at[0])
+    copy.start()
+    width = part_out.shape[1]
+    for place in range(2):
+
+        @pl.when(lax.axis_index("dp") == place)
+        def _():
+            part_out[...] = near[:, place * width : (place + 1) * width]
+
+    copy.wait()
+
+
 def student_front_kernel(count, width, fetches, embed_w, head_w, gains, *refs):
     packed = refs[:count]
     head_outs = refs[count : 2 * count]
-    short_out, late_out, mod, short_ref, rows_ref, sends, *kept = refs[2 * count :]
+    short_out, late_out, mod, rows_ref, sends, *kept = refs[2 * count :]
     model_width = embed_w.shape[2]
     latent_width = embed_w.shape[1]
     size = rows_ref.shape[1]
@@ -341,9 +361,7 @@
     in_both = jnp.concatenate([in_top, in_low], axis=0)
     both = jnp.concatenate([dot32(in_both, head_w[kind]) for kind in range(3)], axis=1)
     short = both[: in_rows.shape[0]] + both[in_rows.shape[0] :]
-    short_ref[...] = short
-    send = pltpu.make_async_copy(short_ref, short_out, sends.at[1])
-    send.start()
+    short_out[...] = short
 
     @pl.when(lax.axis_index("segment") == 0)
     def _():
@@ -357,22 +375,19 @@
         )
 
     late.wait()
-    send.wait()
-
-
-def critic_front_kernel(count, fetches, embed_w, gains, *refs):
+
+
+def critic_front_kernel(count, fetches, short, embed_w, gains, *refs):
     rows = refs[:count]
     head_outs = refs[count : 2 * count]
     kept = refs[2 * count :]
-    (short,) = fetches
 
     @pl.when(lax.axis_index("segment") != 0)
     def _():
-        short.start()
         front(
             rows,
             centred(embed_w).astype(jnp.bfloat16),
-            lambda: short.ready()[...],
+            lambda: short[...],
             gains,
             head_outs,
             *kept,
@@ -695,21 +710,24 @@
         collect(target_in[...], critic_inverse, pair[:, :latent_width], critic_mixed)
 
 
-def expand_kernel(
-    count, groups, sizes, full_rows, fetches, own, to_first, to_second, to_third, embed_w, *refs
-):
+def emit_kernel(fetches, own, to_first, to_second, to_third, grad_ref):
+    section = lax.axis_index("segment")
+    for place, value in enumerate((own, to_first, to_second, to_third)):
+
+        @pl.when(section == place)
+        def _():
+            grad_ref[...] = value[...].astype(jnp.float32).T
+
+
+def expand_kernel(count, groups, sizes, full_rows, fetches, embed_w, *refs):
     heads_w, refs = nested(refs, sizes)
     other_mods = refs[: groups - 1]
     sums = refs[groups - 1 : 3 * groups - 1]
-    grad_ref, total_ref, work, joined = refs[3 * groups - 1 :]
+    total_ref, work, joined = refs[3 * groups - 1 :]
     section = lax.axis_index("segment")
     place = lax.axis_index("seq")
     latent_width = embed_w.shape[1]
     model_width = embed_w.shape[2]
-    picked = own[...].astype(jnp.float32)
-    for source, value in ((1, to_first), (2, to_second), (3, to_third)):
-        picked = jnp.where(section == source, value[...].astype(jnp.float32), picked)
-    grad_ref[...] = picked.T
 
     @pl.when(section == 1)
     def _():
@@ -774,13 +792,30 @@
     count = lax.axis_size("seq")
     full_rows = tok_rows * count
     head_width = w_qkv.shape[4]
+    bf16, f32 = jnp.bfloat16, jnp.float32
     kind_w = jnp.transpose(w_qkv[0, :, 0], (1, 0, 2))
     final_w = jnp.transpose(w_final[0])
     groups = lax.axis_size("dp")
-    heads_w = spread_heads(w_out[0, 0], count, groups)
+    staged = []
+
+    def stage(near):
+        rows, width = near.shape
+        kinds, part = run(
+            stage_kernel,
+            [pltpu.VMEM(kind_w.shape, bf16), array((rows, width // 2), bf16)],
+            (near,),
+            1000,
+            scratch=(pltpu.SemaphoreType.DMA((1,)),),
+            streamed=(kind_w,),
+        )
+        staged.append(kinds)
+        return part
+
+    heads_w = spread_heads(w_out[0, 0], count, groups, stage)
+    if staged:
+        kind_w = pltpu.with_memory_space_constraint(staged[0], pltpu.VMEM)
     sizes = [len(pieces) for pieces in heads_w]
     heads_w = sum(heads_w, [])
-    bf16, f32 = jnp.bfloat16, jnp.float32
 
     depth = packed_rows(mod_width)
     packed, noisy_student = run(
@@ -811,17 +846,16 @@
     short_shape = ((latent_width + 16, 3 * head_width), f32)
     *head_outs, short, late_mod = run(
         functools.partial(student_front_kernel, count, mod_width),
-        head_blocks,
+        head_blocks + [pltpu.VMEM(*short_shape)],
         (w_embed, kind_w, qk_gain, *packed_all),
         4 * latent_width * model_width * 3 * head_width,
         scratch=[
             pltpu.VMEM((1, 5 * model_width), f32),
-            pltpu.VMEM(*short_shape),
             pltpu.VMEM((count, tok_rows, latent_width), bf16),
-            pltpu.SemaphoreType.DMA((2,)),
+            pltpu.SemaphoreType.DMA((1,)),
         ]
         + [pltpu.VMEM(shape, kind) for shape, kind in stored],
-        sent=[array(*short_shape), array((1, 3 * model_width), f32)],
+        sent=[array((1, 3 * model_width), f32)],
     )
     student_mixed = scatter_near(head_outs, "seq", count)
     late_mods = gather_near(late_mod, "dp", groups)
@@ -854,9 +888,13 @@
     *head_outs, proj, inverse, keys, values = run(
         functools.partial(critic_front_kernel, count),
         head_blocks + [array(shape, kind) for shape, kind in stored],
-        (w_embed, qk_gain, *critic_rows),
+        (
+            pltpu.with_memory_space_constraint(short, pltpu.VMEM),
+            w_embed,
+            qk_gain,
+            *critic_rows,
+        ),
         4 * latent_width * model_width * full_rows,
-        fetched=(short,),
     )
     critic_mixed = scatter_near(head_outs, "seq", count)
     small = array((tok_rows, latent_width), f32)
@@ -940,16 +978,27 @@
             sums_all.append(
                 sums if offset == group == 0 else lax.ppermute(sums, ("seq", "dp"), moves)
             )
-    grad_t, total_t = run(
+    (total_t,) = run(
         functools.partial(expand_kernel, count, groups, sizes, full_rows),
-        [array((latent_width, tok_rows), f32), array((latent_width, model_width), f32)],
-        (sample_grad, to_first, to_second, to_third, w_embed, *heads_w, *late_mods[1:], *sums_all),
+        [array((latent_width, model_width), f32)],
+        (
+            w_embed,
+            *heads_w,
+            *late_mods[1:],
+            *sums_all,
+        ),
         4 * groups * latent_width * model_width * head_width * count,
         scratch=(
             pltpu.VMEM((groups * latent_width, model_width), f32),
             pltpu.VMEM((count + 1, groups * latent_width, 128), f32),
         ),
         fetched=(late_mod,),
+    )
+    (grad_t,) = run(
+        emit_kernel,
+        [array((latent_width, tok_rows), f32)],
+        (sample_grad, to_first, to_second, to_third),
+        1000,
     )
     return (jnp.transpose(grad_t)[None], jnp.transpose(total_t)[None])
 

time: 116 us -> 121 us (1.043)
  waiting for transfers between devices: 47.6 us -> 51.1 us
  Pallas kernels: 22.7 us -> 25.4 us
    ppermute x7, waiting for transfers between devices: 8.47 us -> 5.38 us  [gather_near(): lax.ppermute(value, axis, swaps(count, offset))]
    ppermute x1, waiting for transfers between devices: 9.11 us -> 11.9 us  [spread_heads(): near = lax.ppermute(part, 'seq', swaps(count, bit))]
    ppermute x1, waiting for transfers between devices: 8.56 us -> 5.76 us  [spread_heads(): held[bit] = [near, lax.ppermute(stage(near), 'dp', swaps(groups, 1))]]
    ppermute x1, waiting for transfers between devices: 1.71 us -> 4.47 us  [step(): to_third = lax.ppermute(sample_grad, 'segment', ends)]
    pallas_call x11 -> x13, Pallas kernels: 22.7 us -> 25.4 us  [run(): pl.pallas_call(body, out_shape=list(outputs) + [pltpu.HBM(item.shape, ite...]
    ppermute x1, waiting for transfers between devices: 2.77 us -> 4.95 us  [step(): to_second = lax.ppermute(sample_grad, 'segment', swaps(sections, 2))]
    ppermute x1, waiting for transfers between devices: 0.81 us -> 2.42 us  [step(): to_first = lax.ppermute(sample_grad, 'segment', swaps(sections, 1))]
  transfers between devices with their start and end apart: 36 -> 36, of which waited for: 23 -> 22; matrix products, arithmetic and copies ran while one was open for 0% -> 0% of each run, Pallas kernels for 13% -> 15%
where the time goes in v8:
time: 121 us
  waiting for transfers between devices  51.1 us (42%)
  starting transfers between devices  42.4 us (35%)
  Pallas kernels  25.4 us (21%)
    pallas_call x13, Pallas kernels, run(): pl.pallas_call(body, out_shape=list(outputs) + [pltpu.HBM(item.shape, ite...  25.4 us
    ppermute x1, waiting for transfers between devices, spread_heads(): near = lax.ppermute(part, 'seq', swaps(count, bit))  11.9 us
    ppermute x1, starting transfers between devices, step(): fake = lax.ppermute(term_rows, 'segment', swaps(sections, 2))  10.1 us
    ppermute x9, waiting for transfers between devices, scatter_near(): lax.ppermute(blocks[offset], axis, swaps(count, offset))  7.77 us
    ppermute x7, starting transfers between devices, gather_near(): lax.ppermute(value, axis, swaps(count, offset))  6.25 us
    ppermute x1, waiting for transfers between devices, spread_heads(): held[bit] = [near, lax.ppermute(stage(near), 'dp', swaps(groups, 1))]  5.76 us
    ppermute x1, starting transfers between devices, step(): real = lax.ppermute(real, 'segment', swaps(sections, 1))  5.67 us
    ppermute x9, starting transfers between devices, scatter_near(): lax.ppermute(blocks[offset], axis, swaps(count, offset))  5.45 us
  transfers between devices with their start and end apart: 36, of which 22 were waited for; matrix products, arithmetic and copies ran while one was open for 0% of the time, Pallas kernels for 15%

profile of v8, /device:TPU:0, one launch (start us, length us, event | category | flops | bytes accessed | tf_op | source)
XLA Modules:
  0.0 121.0 jit_solution(1110818613070970424)
XLA Ops:
  0.6 1.1 dynamic-slice_bitcast_fusion
  1.7 3.1 %collective-permute-start = (bf16[128,2048]{1,0:T(8,128)(2,1)S(1)}, bf16[128,2048]{1,0:T(8,128)(2,1)S(1)}, u32[]{:S(2)}, u32[]{:S(2)}) collective-permute-start(bf16[128,2048]{1,0:T(8,128)(2,1)S(1)} %dynamic-slice_bitcast_fusion), channel_id=1, source_target_pairs={{0,4},{2,6},{4,0},{6,2},{1,5},{3,7},{5,1},{7,3},{8,12},{10,14},{12... | collective-permute-start | bytes 1572872 | tf_op jit(solution)/shard_map/ppermute | solution.py:52
  4.8 0.0 collective-permute-start.7
  4.8 11.9 %collective-permute-done.refs_0_.refs_8_.refs_3_ = bf16[128,2048]{1,0:T(8,128)(2,1)S(1)} collective-permute-done((bf16[128,2048]{1,0:T(8,128)(2,1)S(1)}, bf16[128,2048]{1,0:T(8,128)(2,1)S(1)}, u32[]{:S(2)}, u32[]{:S(2)}) %collective-permute-start) | collective-permute-done | bytes 524320 | tf_op jit(solution)/shard_map/ppermute | solution.py:52
  16.7 1.7 %shard_map.122 = (bf16[3,3072,128]{2,1,0:T(8,128)(2,1)S(1)}, bf16[128,1024]{1,0:T(8,128)(2,1)S(1)}) custom-call(bf16[128,2048]{1,0:T(8,128)(2,1)S(1)} %collective-permute-done.refs_0_.refs_8_.refs_3_, bf16[3,3072,128]{2,1,0:T(8,128)(2,1)} %bitcast.26), custom_call_target="tpu_custom_call" | custom-call | flops 1000 | bytes 3145728 | tf_op jit(solution)/shard_map/pallas_call | solution.py:187
  18.4 1.8 %collective-permute-start.8 = (bf16[128,1024]{1,0:T(8,128)(2,1)S(1)}, bf16[128,1024]{1,0:T(8,128)(2,1)S(1)}, u32[]{:S(2)}, u32[]{:S(2)}) collective-permute-start(bf16[128,1024]{1,0:T(8,128)(2,1)S(1)} %get-tuple-element.48), channel_id=1, source_target_pairs={{0,1},{1,0},{2,3},{3,2},{4,5},{5,4},{6,7},{7,6},{8,9},{9,8},{10,11... | collective-permute-start | bytes 786440 | tf_op jit(solution)/shard_map/ppermute | solution.py:53
  20.2 5.8 %collective-permute-done.8.refs_9_.refs_4_ = bf16[128,1024]{1,0:T(8,128)(2,1)S(1)} collective-permute-done((bf16[128,1024]{1,0:T(8,128)(2,1)S(1)}, bf16[128,1024]{1,0:T(8,128)(2,1)S(1)}, u32[]{:S(2)}, u32[]{:S(2)}) %collective-permute-start.8) | collective-permute-done | bytes 262176 | tf_op jit(solution)/shard_map/ppermute | solution.py:53
  25.9 11.3 %shard_map.123 = (bf16[128,128]{1,0:T(8,128)(2,1)S(1)}, bf16[128,64]{1,0:T(8,128)(2,1)S(1)}) custom-call(s32[2,2]{1,0:T(2,128)} %refs_14_.1, f32[1,256]{1,0:T(1,128)} %refs_1_.4, bf16[256,3072]{1,0:T(8,128)(2,1)} %bitcast.27, bf16[64,128]{1,0:T(8,128)(2,1)} %bitcast.35, bf16[128,128]{1,0:T(8,128)(2,1)} %bitcast.31, bf16[3072,3840]{1,0:T(8,128)(2,1)} %bitcast.25), custom_call_target="tpu_custom_call" | custom-call | flops 23592960 | bytes 1672208 | tf_op jit(solution)/shard_map/pallas_call | solution.py:187
  37.3 0.0 copy-start
  37.3 0.6 collective-permute-start.1
  37.9 1.5 %collective-permute-start.2 = (bf16[128,128]{1,0:T(8,128)(2,1)S(1)}, bf16[128,128]{1,0:T(8,128)(2,1)S(1)}, u32[]{:S(2)}, u32[]{:S(2)}) collective-permute-start(bf16[128,128]{1,0:T(8,128)(2,1)S(1)} %get-tuple-element.41.refs_3_), channel_id=1, source_target_pairs={{0,4},{2,6},{4,0},{6,2},{1,5},{3,7},{5,1},{7,3},{8,12},{10,14},{12... | collective-permute-start | bytes 98312 | tf_op jit(solution)/shard_map/ppermute | solution.py:32
  39.3 0.8 collective-permute-start.3
  40.1 1.6 %collective-permute-done.2.refs_5_ = bf16[128,128]{1,0:T(8,128)(2,1)S(1)} collective-permute-done((bf16[128,128]{1,0:T(8,128)(2,1)S(1)}, bf16[128,128]{1,0:T(8,128)(2,1)S(1)}, u32[]{:S(2)}, u32[]{:S(2)}) %collective-permute-start.2) | collective-permute-done | bytes 32800 | tf_op jit(solution)/shard_map/ppermute | solution.py:32
  41.8 1.2 %collective-permute-done.3.refs_6_ = bf16[128,128]{1,0:T(8,128)(2,1)S(1)} collective-permute-done((bf16[128,128]{1,0:T(8,128)(2,1)S(1)}, bf16[128,128]{1,0:T(8,128)(2,1)S(1)}, u32[]{:S(2)}, u32[]{:S(2)}) %collective-permute-start.3) | collective-permute-done | bytes 32800 | tf_op jit(solution)/shard_map/ppermute | solution.py:32
  43.0 3.6 %shard_map.124 = (bf16[128,128]{1,0:T(8,128)(2,1)S(1)}, bf16[128,128]{1,0:T(8,128)(2,1)S(1)}, bf16[128,128]{1,0:T(8,128)(2,1)S(1)}, bf16[128,128]{1,0:T(8,128)(2...) custom-call(bf16[1,64,3072]{2,1,0:T(8,128)(2,1)S(1)} %copy-done.1, ...), custom_call_target="tpu_custom_call" | custom-call | flops 301989888 | bytes 3138560 | tf_op jit(solution)/shard_map/pallas_call | solution.py:187
  46.6 0.1 collective-permute-start.4
  46.8 0.8 collective-permute-start.5
  47.6 0.3 collective-permute-done.4.refs_3_
  47.9 0.7 collective-permute-start.6
  48.6 2.1 %collective-permute-done.5.refs_4_ = bf16[128,128]{1,0:T(8,128)(2,1)S(1)} collective-permute-done((bf16[128,128]{1,0:T(8,128)(2,1)S(1)}, bf16[128,128]{1,0:T(8,128)(2,1)S(1)}, u32[]{:S(2)}, u32[]{:S(2)}) %collective-permute-start.5) | collective-permute-done | bytes 32800 | tf_op jit(solution)/shard_map/ppermute | solution.py:37
  50.7 0.6 collective-permute-done.6.refs_5_
  51.3 2.9 %shard_map.126 = (bf16[128,128]{1,0:T(8,128)(2,1)S(1)}, bf16[4,128,128]{2,1,0:T(8,128)(2,1)}, f32[128,128]{1,0:T(8,128)}) custom-call(bf16[128,64]{1,0:T(8,128)(2,1)S(1)} %get-tuple-element.43.refs_0_.refs_3_, bf16[1,64,3072]{2,1,0:T(8,128)(2,1)S(1)} %copy-done.1, bf16[128,128]{1,0:T(8,128)(2,1)S(1)} %get-tuple-element.44.refs_2_, ...), custom_call_target="tpu_custom_call" | custom-call | flops 402653184 | bytes 4182032 | tf_op jit(solution)/shard_map/pallas_call | solution.py:187
  54.2 1.3 %collective-permute-start.11 = (bf16[128,128]{1,0:T(8,128)(2,1)S(1)}, bf16[128,128]{1,0:T(8,128)(2,1)S(1)}, u32[]{:S(2)}, u32[]{:S(2)}) collective-permute-start(bf16[128,128]{1,0:T(8,128)(2,1)S(1)} %get-tuple-element.50.refs_0_), channel_id=1, source_target_pairs={{0,8},{1,9},{2,10},{3,11},{4,12},{5,13},{6,14},{7,15}} | collective-permute-start | bytes 98312 | tf_op jit(solution)/shard_map/ppermute | solution.py:877
  55.5 1.3 %collective-permute-start.12 = (bf16[128,128]{1,0:T(8,128)(2,1)S(1)}, bf16[128,128]{1,0:T(8,128)(2,1)S(1)}, u32[]{:S(2)}, u32[]{:S(2)}) collective-permute-start(bf16[128,128]{1,0:T(8,128)(2,1)S(1)} %get-tuple-element.50.refs_0_), channel_id=1, source_target_pairs={{0,16},{1,17},{2,18},{3,19},{4,20},{5,21},{6,22},{7,23}} | collective-permute-start | bytes 98312 | tf_op jit(solution)/shard_map/ppermute | solution.py:877
  56.8 1.3 %collective-permute-start.13 = (bf16[128,128]{1,0:T(8,128)(2,1)S(1)}, bf16[128,128]{1,0:T(8,128)(2,1)S(1)}, u32[]{:S(2)}, u32[]{:S(2)}) collective-permute-start(bf16[128,128]{1,0:T(8,128)(2,1)S(1)} %get-tuple-element.50.refs_0_), channel_id=1, source_target_pairs={{0,24},{1,25},{2,26},{3,27},{4,28},{5,29},{6,30},{7,31}} | collective-permute-start | bytes 98312 | tf_op jit(solution)/shard_map/ppermute | solution.py:877
  58.1 0.3 collective-permute-done.12.refs_2_
  58.4 1.3 %collective-permute-done.13.refs_3_ = bf16[128,128]{1,0:T(8,128)(2,1)S(1)} collective-permute-done((bf16[128,128]{1,0:T(8,128)(2,1)S(1)}, bf16[128,128]{1,0:T(8,128)(2,1)S(1)}, u32[]{:S(2)}, u32[]{:S(2)}) %collective-permute-start.13) | collective-permute-done | bytes 32800 | tf_op jit(solution)/shard_map/ppermute | solution.py:877
  59.7 0.1 collective-permute-start.14
  59.8 1.0 collective-permute-start.15
  60.8 0.9 collective-permute-start.16
  61.7 2.1 %collective-permute-done.15.refs_5_.refs_10_ = bf16[128,64]{1,0:T(8,128)(2,1)S(1)} collective-permute-done((bf16[128,64]{1,0:T(8,128)(2,1)S(1)}, bf16[128,64]{1,0:T(8,128)(2,1)S(1)}, u32[]{:S(2)}, u32[]{:S(2)}) %collective-permute-start.15) | collective-permute-done | bytes 16416 | tf_op jit(solution)/shard_map/ppermute | solution.py:32
  63.8 0.4 collective-permute-done.16.refs_6_.refs_11_
  64.2 0.2 collective-permute-start.17
  64.4 1.1 collective-permute-start.18
  65.5 0.6 collective-permute-start.19
  66.1 2.2 %collective-permute-done.18.refs_4_.refs_10_ = bf16[128,128]{1,0:T(8,128)(2,1)S(1)} collective-permute-done((bf16[128,128]{1,0:T(8,128)(2,1)S(1)}, bf16[128,128]{1,0:T(8,128)(2,1)S(1)}, u32[]{:S(2)}, u32[]{:S(2)}) %collective-permute-start.18) | collective-permute-done | bytes 32800 | tf_op jit(solution)/shard_map/ppermute | solution.py:37
  68.3 0.6 collective-permute-done.19.refs_5_.refs_11_
  69.0 0.2 collective-permute-start.20
  69.2 0.9 collective-permute-start.21
  70.1 0.8 collective-permute-start.22
  70.9 0.6 shard_map.125.refs_1_
  71.6 1.5 %collective-permute-done.21.refs_14_ = bf16[128,128]{1,0:T(8,128)(2,1)S(1)} collective-permute-done((bf16[128,128]{1,0:T(8,128)(2,1)S(1)}, bf16[128,128]{1,0:T(8,128)(2,1)S(1)}, u32[]{:S(2)}, u32[]{:S(2)}) %collective-permute-start.21) | collective-permute-done | bytes 32800 | tf_op jit(solution)/shard_map/ppermute | solution.py:37
  73.1 0.4 collective-permute-done.22.refs_15_
  73.5 0.2 collective-permute-start.25
  73.7 5.7 %collective-permute-start.23 = (bf16[160,64]{1,0:T(8,128)(2,1)S(1)}, bf16[160,64]{1,0:T(8,128)(2,1)S(1)}, u32[]{:S(2)}, u32[]{:S(2)}) collective-permute-start(bf16[160,64]{1,0:T(8,128)(2,1)S(1)} %get-tuple-element.66), channel_id=1, source_target_pairs={{0,8},{8,0},{16,24},{24,16},{1,9},{9,1},{17,25},{25,17},{2,10},{10... | collective-permute-start | bytes 61448 | tf_op jit(solution)/shard_map/ppermute | solution.py:928
  79.4 10.1 %collective-permute-start.24 = (bf16[128,64]{1,0:T(8,128)(2,1)S(1)}, bf16[128,64]{1,0:T(8,128)(2,1)S(1)}, u32[]{:S(2)}, u32[]{:S(2)}) collective-permute-start(bf16[128,64]{1,0:T(8,128)(2,1)S(1)} %get-tuple-element.61.refs_7_), channel_id=1, source_target_pairs={{0,16},{8,24},{16,0},{24,8},{1,17},{9,25},{17,1},{25,9},{2,18},{10... | collective-permute-start | bytes 49160 | tf_op jit(solution)/shard_map/ppermute | solution.py:911
  89.5 0.1 collective-permute-start.26
  89.6 1.0 collective-permute-start.27
  90.6 1.3 %collective-permute-done.24.refs_1_ = bf16[128,64]{1,0:T(8,128)(2,1)S(1)} collective-permute-done((bf16[128,64]{1,0:T(8,128)(2,1)S(1)}, bf16[128,64]{1,0:T(8,128)(2,1)S(1)}, u32[]{:S(2)}, u32[]{:S(2)}) %collective-permute-start.24) | collective-permute-done | bytes 16416 | tf_op jit(solution)/shard_map/ppermute | solution.py:911
  91.9 3.3 %collective-permute-done.26.refs_12_ = bf16[128,64]{1,0:T(8,128)(2,1)S(1)} collective-permute-done((bf16[128,64]{1,0:T(8,128)(2,1)S(1)}, bf16[128,64]{1,0:T(8,128)(2,1)S(1)}, u32[]{:S(2)}, u32[]{:S(2)}) %collective-permute-start.26) | collective-permute-done | bytes 16416 | tf_op jit(solution)/shard_map/ppermute | solution.py:931
  95.2 1.0 collective-permute-done.27.refs_13_
  96.2 1.1 shard_map.132
  97.3 0.1 collective-permute-start.32
  97.4 1.3 %collective-permute-done.32 = bf16[5,64,128]{2,1,0:T(8,128)(2,1)S(1)} collective-permute-done((bf16[5,64,128]{2,1,0:T(8,128)(2,1)S(1)}, bf16[5,64,128]{2,1,0:T(8,128)(2,1)S(1)}, u32[]{:S(2)}, u32[]{:S(2)}) %collective-permute-start.32) | collective-permute-done | bytes 81952 | tf_op jit(solution)/shard_map/ppermute | solution.py:967
  98.7 1.2 collective-permute-start.33
  99.8 1.5 %collective-permute-start.34 = (bf16[5,64,128]{2,1,0:T(8,128)(2,1)S(1)}, bf16[5,64,128]{2,1,0:T(8,128)(2,1)S(1)}, u32[]{:S(2)}, u32[]{:S(2)}) collective-permute-start(bf16[5,64,128]{2,1,0:T(8,128)(2,1)S(1)} %add_convert_fusion.refs_8_), channel_id=1, source_target_pairs={{0,1},{1,0},{2,3},{3,2},{4,5},{5,4},{6,7},{7,6},{8,9},{9,8},{10,11... | collective-permute-start | bytes 245768 | tf_op jit(solution)/shard_map/ppermute | solution.py:979
  101.3 0.9 collective-permute-start.35
  102.2 1.5 %collective-permute-start.31 = (f32[1,9216]{1,0:T(1,128)S(1)}, f32[1,9216]{1,0:T(1,128)S(1)}, u32[]{:S(2)}, u32[]{:S(2)}) collective-permute-start(f32[1,9216]{1,0:T(1,128)S(1)} %copy-done.5), channel_id=1, source_target_pairs={{0,1},{1,0},{2,3},{3,2},{4,5},{5,4},{6,7},{7,6},{8,9},{9,8},{10,11... | collective-permute-start | bytes 110600 | tf_op jit(solution)/shard_map/ppermute | solution.py:32
  103.7 2.4 %collective-permute-done.28.refs_1_ = bf16[128,64]{1,0:T(8,128)(2,1)S(1)} collective-permute-done((bf16[128,64]{1,0:T(8,128)(2,1)S(1)}, bf16[128,64]{1,0:T(8,128)(2,1)S(1)}, u32[]{:S(2)}, u32[]{:S(2)}) %collective-permute-start.28) | collective-permute-done | bytes 16416 | tf_op jit(solution)/shard_map/ppermute | solution.py:963
  106.2 5.0 %collective-permute-done.29.refs_2_ = bf16[128,64]{1,0:T(8,128)(2,1)S(1)} collective-permute-done((bf16[128,64]{1,0:T(8,128)(2,1)S(1)}, bf16[128,64]{1,0:T(8,128)(2,1)S(1)}, u32[]{:S(2)}, u32[]{:S(2)}) %collective-permute-start.29) | collective-permute-done | bytes 16416 | tf_op jit(solution)/shard_map/ppermute | solution.py:962
  111.1 1.2 %collective-permute-start.30 = (bf16[128,64]{1,0:T(8,128)(2,1)S(1)}, bf16[128,64]{1,0:T(8,128)(2,1)S(1)}, u32[]{:S(2)}, u32[]{:S(2)}) collective-permute-start(bf16[128,64]{1,0:T(8,128)(2,1)S(1)} %get-tuple-element.76.refs_0_), channel_id=1, source_target_pairs={{0,24},{8,16},{16,8},{24,0},{1,25},{9,17},{17,9},{25,1},{2,26},{10... | collective-permute-start | bytes 49160 | tf_op jit(solution)/shard_map/ppermute | solution.py:961
  112.3 4.5 %collective-permute-done.30.refs_3_ = bf16[128,64]{1,0:T(8,128)(2,1)S(1)} collective-permute-done((bf16[128,64]{1,0:T(8,128)(2,1)S(1)}, bf16[128,64]{1,0:T(8,128)(2,1)S(1)}, u32[]{:S(2)}, u32[]{:S(2)}) %collective-permute-start.30) | collective-permute-done | bytes 16416 | tf_op jit(solution)/shard_map/ppermute | solution.py:961
  116.8 0.7 shard_map.133
  117.6 3.3 %shard_map.134 = f32[64,3072]{1,0:T(8,128)} custom-call(bf16[1,64,3072]{2,1,0:T(8,128)(2,1)S(1)} %copy-done.1, bf16[128,3072]{1,0:T(8,128)(2,1)S(1)} %bitcast.24, bf16[128,3072]{1,0:T(8,128)(2,1)S(1)} %collective-permute-done.7.refs_7_.refs_2_, bf16[128,2048]{1,0:T(8,128)(2,1)S(1)} %collective-permute-done.refs_0_.refs_8_.refs_3_, ...), custom_call_target="tpu_custom_call" | custom-call | flops 805306368 | bytes 4726784 | tf_op jit(solution)/shard_map/pallas_call | solution.py:187
  (35 shorter events, 0.2 us)
Async XLA Ops:
  1.7 15.0 %collective-permute-start = (bf16[128,2048]{1,0:T(8,128)(2,1)S(1)}, bf16[128,2048]{1,0:T(8,128)(2,1)S(1)}, u32[]{:S(2)}, u32[]{:S(2)}) collective-permute-start(bf16[128,2048]{1,0:T(8,128)(2,1)S(1)} %dynamic-slice_bitcast_fusion), channel_id=1, source_target_pairs={{0,4},{2,6},{4,0},{6,2},{1,5},{3,7},{5,1},{7,3},{8,12},{10,14},{12... | collective-permute-start | bytes 1572872 | tf_op jit(solution)/shard_map/ppermute | solution.py:52
  4.8 46.5 %collective-permute-start.7 = (bf16[128,3072]{1,0:T(8,128)(2,1)}, bf16[128,3072]{1,0:T(8,128)(2,1)S(1)}, u32[]{:S(2)}, u32[]{:S(2)}) collective-permute-start(bf16[128,3072]{1,0:T(8,128)(2,1)} %bitcast.21), channel_id=1, source_target_pairs={{0,2},{2,0},{4,6},{6,4},{1,3},{3,1},{5,7},{7,5},{8,10},{10,8},{12,... | collective-permute-start | bytes 2359304 | tf_op jit(solution)/shard_map/ppermute | solution.py:56
  18.4 7.5 %collective-permute-start.8 = (bf16[128,1024]{1,0:T(8,128)(2,1)S(1)}, bf16[128,1024]{1,0:T(8,128)(2,1)S(1)}, u32[]{:S(2)}, u32[]{:S(2)}) collective-permute-start(bf16[128,1024]{1,0:T(8,128)(2,1)S(1)} %get-tuple-element.48), channel_id=1, source_target_pairs={{0,1},{1,0},{2,3},{3,2},{4,5},{5,4},{6,7},{7,6},{8,9},{9,8},{10,11... | collective-permute-start | bytes 786440 | tf_op jit(solution)/shard_map/ppermute | solution.py:53
  20.2 31.1 %collective-permute-start.9 = (bf16[128,2048]{1,0:T(8,128)(2,1)S(1)}, bf16[128,2048]{1,0:T(8,128)(2,1)S(1)}, u32[]{:S(2)}, u32[]{:S(2)}) collective-permute-start(bf16[128,2048]{1,0:T(8,128)(2,1)S(1)} %collective-permute-done.refs_0_.refs_8_.refs_3_), channel_id=1, source_target_pairs={{0,2},{2,0},{4,6},{6,4},{1,3},{3,1},{5,7},{7,5},{8,10},{10,8},{12,... | collective-permute-start | bytes 1572872 | tf_op jit(solution)/shard_map/ppermute | solution.py:56
  25.9 25.3 %collective-permute-start.10 = (bf16[128,1024]{1,0:T(8,128)(2,1)S(1)}, bf16[128,1024]{1,0:T(8,128)(2,1)S(1)}, u32[]{:S(2)}, u32[]{:S(2)}) collective-permute-start(bf16[128,1024]{1,0:T(8,128)(2,1)S(1)} %collective-permute-done.8.refs_9_.refs_4_), channel_id=1, source_target_pairs={{0,2},{2,0},{4,6},{6,4},{1,3},{3,1},{5,7},{7,5},{8,10},{10,8},{12,... | collective-permute-start | bytes 786440 | tf_op jit(solution)/shard_map/ppermute | solution.py:56
  25.9 17.1 %copy-start.1 = (bf16[1,64,3072]{2,1,0:T(8,128)(2,1)S(1)}, bf16[1,64,3072]{2,1,0:T(8,128)(2,1)}, u32[]{:S(2)}) copy-start(bf16[1,64,3072]{2,1,0:T(8,128)(2,1)} %refs_0_.7) | copy-start | bytes 1179652
  25.9 17.1 %copy-start.4 = (f32[1,2,128]{2,1,0:T(2,128)S(1)}, f32[1,2,128]{2,1,0:T(2,128)}, u32[]{:S(2)}) copy-start(f32[1,2,128]{2,1,0:T(2,128)} %refs_2_.5) | copy-start | bytes 3076
  37.3 14.0 %copy-start = (bf16[1,1,128,3072]{3,2,1,0:T(8,128)(2,1)S(1)}, bf16[1,1,128,3072]{3,2,1,0:T(8,128)(2,1)}, u32[]{:S(2)}) copy-start(bf16[1,1,128,3072]{3,2,1,0:T(8,128)(2,1)} %param.19) | copy-start | bytes 2359300
  37.3 2.0 %collective-permute-start.1 = (bf16[128,128]{1,0:T(8,128)(2,1)S(1)}, bf16[128,128]{1,0:T(8,128)(2,1)S(1)}, u32[]{:S(2)}, u32[]{:S(2)}) collective-permute-start(bf16[128,128]{1,0:T(8,128)(2,1)S(1)} %get-tuple-element.41.refs_3_), channel_id=1, source_target_pairs={{0,2},{2,0},{4,6},{6,4},{1,3},{3,1},{5,7},{7,5},{8,10},{10,8},{12,... | collective-permute-start | bytes 98312 | tf_op jit(solution)/shard_map/ppermute | solution.py:32
  37.9 3.9 %collective-permute-start.2 = (bf16[128,128]{1,0:T(8,128)(2,1)S(1)}, bf16[128,128]{1,0:T(8,128)(2,1)S(1)}, u32[]{:S(2)}, u32[]{:S(2)}) collective-permute-start(bf16[128,128]{1,0:T(8,128)(2,1)S(1)} %get-tuple-element.41.refs_3_), channel_id=1, source_target_pairs={{0,4},{2,6},{4,0},{6,2},{1,5},{3,7},{5,1},{7,3},{8,12},{10,14},{12... | collective-permute-start | bytes 98312 | tf_op jit(solution)/shard_map/ppermute | solution.py:32
  39.3 3.7 %collective-permute-start.3 = (bf16[128,128]{1,0:T(8,128)(2,1)S(1)}, bf16[128,128]{1,0:T(8,128)(2,1)S(1)}, u32[]{:S(2)}, u32[]{:S(2)}) collective-permute-start(bf16[128,128]{1,0:T(8,128)(2,1)S(1)} %get-tuple-element.41.refs_3_), channel_id=1, source_target_pairs={{0,6},{2,4},{4,2},{6,0},{1,7},{3,5},{5,3},{7,1},{8,14},{10,12},{12... | collective-permute-start | bytes 98312 | tf_op jit(solution)/shard_map/ppermute | solution.py:32
  46.6 1.3 %collective-permute-start.4 = (bf16[128,128]{1,0:T(8,128)(2,1)S(1)}, bf16[128,128]{1,0:T(8,128)(2,1)S(1)}, u32[]{:S(2)}, u32[]{:S(2)}) collective-permute-start(bf16[128,128]{1,0:T(8,128)(2,1)S(1)} %get-tuple-element.45), channel_id=1, source_target_pairs={{0,2},{2,0},{4,6},{6,4},{1,3},{3,1},{5,7},{7,5},{8,10},{10,8},{12,... | collective-permute-start | bytes 98312 | tf_op jit(solution)/shard_map/ppermute | solution.py:37
  46.8 3.9 %collective-permute-start.5 = (bf16[128,128]{1,0:T(8,128)(2,1)S(1)}, bf16[128,128]{1,0:T(8,128)(2,1)S(1)}, u32[]{:S(2)}, u32[]{:S(2)}) collective-permute-start(bf16[128,128]{1,0:T(8,128)(2,1)S(1)} %get-tuple-element.46), channel_id=1, source_target_pairs={{0,4},{2,6},{4,0},{6,2},{1,5},{3,7},{5,1},{7,3},{8,12},{10,14},{12... | collective-permute-start | bytes 98312 | tf_op jit(solution)/shard_map/ppermute | solution.py:37
  47.9 3.3 %collective-permute-start.6 = (bf16[128,128]{1,0:T(8,128)(2,1)S(1)}, bf16[128,128]{1,0:T(8,128)(2,1)S(1)}, u32[]{:S(2)}, u32[]{:S(2)}) collective-permute-start(bf16[128,128]{1,0:T(8,128)(2,1)S(1)} %get-tuple-element.47), channel_id=1, source_target_pairs={{0,6},{2,4},{4,2},{6,0},{1,7},{3,5},{5,3},{7,1},{8,14},{10,12},{12... | collective-permute-start | bytes 98312 | tf_op jit(solution)/shard_map/ppermute | solution.py:37
  54.2 3.9 %collective-permute-start.11 = (bf16[128,128]{1,0:T(8,128)(2,1)S(1)}, bf16[128,128]{1,0:T(8,128)(2,1)S(1)}, u32[]{:S(2)}, u32[]{:S(2)}) collective-permute-start(bf16[128,128]{1,0:T(8,128)(2,1)S(1)} %get-tuple-element.50.refs_0_), channel_id=1, source_target_pairs={{0,8},{1,9},{2,10},{3,11},{4,12},{5,13},{6,14},{7,15}} | collective-permute-start | bytes 98312 | tf_op jit(solution)/shard_map/ppermute | solution.py:877
  55.5 2.9 %collective-permute-start.12 = (bf16[128,128]{1,0:T(8,128)(2,1)S(1)}, bf16[128,128]{1,0:T(8,128)(2,1)S(1)}, u32[]{:S(2)}, u32[]{:S(2)}) collective-permute-start(bf16[128,128]{1,0:T(8,128)(2,1)S(1)} %get-tuple-element.50.refs_0_), channel_id=1, source_target_pairs={{0,16},{1,17},{2,18},{3,19},{4,20},{5,21},{6,22},{7,23}} | collective-permute-start | bytes 98312 | tf_op jit(solution)/shard_map/ppermute | solution.py:877
  56.8 2.9 %collective-permute-start.13 = (bf16[128,128]{1,0:T(8,128)(2,1)S(1)}, bf16[128,128]{1,0:T(8,128)(2,1)S(1)}, u32[]{:S(2)}, u32[]{:S(2)}) collective-permute-start(bf16[128,128]{1,0:T(8,128)(2,1)S(1)} %get-tuple-element.50.refs_0_), channel_id=1, source_target_pairs={{0,24},{1,25},{2,26},{3,27},{4,28},{5,29},{6,30},{7,31}} | collective-permute-start | bytes 98312 | tf_op jit(solution)/shard_map/ppermute | solution.py:877
  59.7 1.9 %collective-permute-start.14 = (bf16[128,64]{1,0:T(8,128)(2,1)S(1)}, bf16[128,64]{1,0:T(8,128)(2,1)S(1)}, u32[]{:S(2)}, u32[]{:S(2)}) collective-permute-start(bf16[128,64]{1,0:T(8,128)(2,1)S(1)} %get-tuple-element.51.refs_3_.refs_8_), channel_id=1, source_target_pairs={{0,2},{2,0},{4,6},{6,4},{1,3},{3,1},{5,7},{7,5},{8,10},{10,8},{12,... | collective-permute-start | bytes 49160 | tf_op jit(solution)/shard_map/ppermute | solution.py:32
  59.8 4.0 %collective-permute-start.15 = (bf16[128,64]{1,0:T(8,128)(2,1)S(1)}, bf16[128,64]{1,0:T(8,128)(2,1)S(1)}, u32[]{:S(2)}, u32[]{:S(2)}) collective-permute-start(bf16[128,64]{1,0:T(8,128)(2,1)S(1)} %get-tuple-element.51.refs_3_.refs_8_), channel_id=1, source_target_pairs={{0,4},{2,6},{4,0},{6,2},{1,5},{3,7},{5,1},{7,3},{8,12},{10,14},{12... | collective-permute-start | bytes 49160 | tf_op jit(solution)/shard_map/ppermute | solution.py:32
  60.8 3.4 %collective-permute-start.16 = (bf16[128,64]{1,0:T(8,128)(2,1)S(1)}, bf16[128,64]{1,0:T(8,128)(2,1)S(1)}, u32[]{:S(2)}, u32[]{:S(2)}) collective-permute-start(bf16[128,64]{1,0:T(8,128)(2,1)S(1)} %get-tuple-element.51.refs_3_.refs_8_), channel_id=1, source_target_pairs={{0,6},{2,4},{4,2},{6,0},{1,7},{3,5},{5,3},{7,1},{8,14},{10,12},{12... | collective-permute-start | bytes 49160 | tf_op jit(solution)/shard_map/ppermute | solution.py:32
  64.2 1.9 %collective-permute-start.17 = (bf16[128,128]{1,0:T(8,128)(2,1)S(1)}, bf16[128,128]{1,0:T(8,128)(2,1)S(1)}, u32[]{:S(2)}, u32[]{:S(2)}) collective-permute-start(bf16[128,128]{1,0:T(8,128)(2,1)S(1)} %get-tuple-element.58), channel_id=1, source_target_pairs={{0,2},{2,0},{4,6},{6,4},{1,3},{3,1},{5,7},{7,5},{8,10},{10,8},{12,... | collective-permute-start | bytes 98312 | tf_op jit(solution)/shard_map/ppermute | solution.py:37
  64.4 3.9 %collective-permute-start.18 = (bf16[128,128]{1,0:T(8,128)(2,1)S(1)}, bf16[128,128]{1,0:T(8,128)(2,1)S(1)}, u32[]{:S(2)}, u32[]{:S(2)}) collective-permute-start(bf16[128,128]{1,0:T(8,128)(2,1)S(1)} %get-tuple-element.59), channel_id=1, source_target_pairs={{0,4},{2,6},{4,0},{6,2},{1,5},{3,7},{5,1},{7,3},{8,12},{10,14},{12... | collective-permute-start | bytes 98312 | tf_op jit(solution)/shard_map/ppermute | solution.py:37
  65.5 3.4 %collective-permute-start.19 = (bf16[128,128]{1,0:T(8,128)(2,1)S(1)}, bf16[128,128]{1,0:T(8,128)(2,1)S(1)}, u32[]{:S(2)}, u32[]{:S(2)}) collective-permute-start(bf16[128,128]{1,0:T(8,128)(2,1)S(1)} %get-tuple-element.60), channel_id=1, source_target_pairs={{0,6},{2,4},{4,2},{6,0},{1,7},{3,5},{5,3},{7,1},{8,14},{10,12},{12... | collective-permute-start | bytes 98312 | tf_op jit(solution)/shard_map/ppermute | solution.py:37
  68.9 27.3 %copy-start.2 = (bf16[4,128,128]{2,1,0:T(8,128)(2,1)S(1)}, bf16[4,128,128]{2,1,0:T(8,128)(2,1)}, u32[]{:S(2)}) copy-start(bf16[4,128,128]{2,1,0:T(8,128)(2,1)} %get-tuple-element.68.refs_5_) | copy-start | bytes 393220
  68.9 27.3 %copy-start.3 = (f32[128,128]{1,0:T(8,128)S(1)}, f32[128,128]{1,0:T(8,128)}, u32[]{:S(2)}) copy-start(f32[128,128]{1,0:T(8,128)} %get-tuple-element.69.refs_6_) | copy-start | bytes 196612
  69.0 33.3 %copy-start.5 = (f32[1,9216]{1,0:T(1,128)S(1)}, f32[1,9216]{1,0:T(1,128)}, u32[]{:S(2)}) copy-start(f32[1,9216]{1,0:T(1,128)} %get-tuple-element.49.refs_12_) | copy-start | bytes 110596
  69.0 2.6 %collective-permute-start.20 = (bf16[128,128]{1,0:T(8,128)(2,1)S(1)}, bf16[128,128]{1,0:T(8,128)(2,1)S(1)}, u32[]{:S(2)}, u32[]{:S(2)}) collective-permute-start(bf16[128,128]{1,0:T(8,128)(2,1)S(1)} %get-tuple-element.63), channel_id=1, source_target_pairs={{0,2},{2,0},{4,6},{6,4},{1,3},{3,1},{5,7},{7,5},{8,10},{10,8},{12,... | collective-permute-start | bytes 98312 | tf_op jit(solution)/shard_map/ppermute | solution.py:37
  69.2 3.9 %collective-permute-start.21 = (bf16[128,128]{1,0:T(8,128)(2,1)S(1)}, bf16[128,128]{1,0:T(8,128)(2,1)S(1)}, u32[]{:S(2)}, u32[]{:S(2)}) collective-permute-start(bf16[128,128]{1,0:T(8,128)(2,1)S(1)} %get-tuple-element.64), channel_id=1, source_target_pairs={{0,4},{2,6},{4,0},{6,2},{1,5},{3,7},{5,1},{7,3},{8,12},{10,14},{12... | collective-permute-start | bytes 98312 | tf_op jit(solution)/shard_map/ppermute | solution.py:37
  70.1 3.4 %collective-permute-start.22 = (bf16[128,128]{1,0:T(8,128)(2,1)S(1)}, bf16[128,128]{1,0:T(8,128)(2,1)S(1)}, u32[]{:S(2)}, u32[]{:S(2)}) collective-permute-start(bf16[128,128]{1,0:T(8,128)(2,1)S(1)} %get-tuple-element.65), channel_id=1, source_target_pairs={{0,6},{2,4},{4,2},{6,0},{1,7},{3,5},{5,3},{7,1},{8,14},{10,12},{12... | collective-permute-start | bytes 98312 | tf_op jit(solution)/shard_map/ppermute | solution.py:37
  73.5 15.9 %collective-permute-start.25 = (bf16[2,128,64]{2,1,0:T(8,128)(2,1)S(1)}, bf16[2,128,64]{2,1,0:T(8,128)(2,1)S(1)}, u32[]{:S(2)}, u32[]{:S(2)}) collective-permute-start(bf16[2,128,64]{2,1,0:T(8,128)(2,1)S(1)} %get-tuple-element.73), channel_id=1, source_target_pairs={{0,2},{2,0},{4,6},{6,4},{1,3},{3,1},{5,7},{7,5},{8,10},{10,8},{12,... | collective-permute-start | bytes 98312 | tf_op jit(solution)/shard_map/ppermute | solution.py:927
  73.7 18.2 %collective-permute-start.23 = (bf16[160,64]{1,0:T(8,128)(2,1)S(1)}, bf16[160,64]{1,0:T(8,128)(2,1)S(1)}, u32[]{:S(2)}, u32[]{:S(2)}) collective-permute-start(bf16[160,64]{1,0:T(8,128)(2,1)S(1)} %get-tuple-element.66), channel_id=1, source_target_pairs={{0,8},{8,0},{16,24},{24,16},{1,9},{9,1},{17,25},{25,17},{2,10},{10... | collective-permute-start | bytes 61448 | tf_op jit(solution)/shard_map/ppermute | solution.py:928
  79.4 12.5 %collective-permute-start.24 = (bf16[128,64]{1,0:T(8,128)(2,1)S(1)}, bf16[128,64]{1,0:T(8,128)(2,1)S(1)}, u32[]{:S(2)}, u32[]{:S(2)}) collective-permute-start(bf16[128,64]{1,0:T(8,128)(2,1)S(1)} %get-tuple-element.61.refs_7_), channel_id=1, source_target_pairs={{0,16},{8,24},{16,0},{24,8},{1,17},{9,25},{17,1},{25,9},{2,18},{10... | collective-permute-start | bytes 49160 | tf_op jit(solution)/shard_map/ppermute | solution.py:911
  89.5 5.8 %collective-permute-start.26 = (bf16[128,64]{1,0:T(8,128)(2,1)S(1)}, bf16[128,64]{1,0:T(8,128)(2,1)S(1)}, u32[]{:S(2)}, u32[]{:S(2)}) collective-permute-start(bf16[128,64]{1,0:T(8,128)(2,1)S(1)} %get-tuple-element.74), channel_id=1, source_target_pairs={{0,8},{2,10},{4,12},{6,14},{8,16},{10,18},{12,20},{14,22},{16,24},... | collective-permute-start | bytes 49160 | tf_op jit(solution)/shard_map/ppermute | solution.py:931
  89.6 6.6 %collective-permute-start.27 = (bf16[128,64]{1,0:T(8,128)(2,1)S(1)}, bf16[128,64]{1,0:T(8,128)(2,1)S(1)}, u32[]{:S(2)}, u32[]{:S(2)}) collective-permute-start(bf16[128,64]{1,0:T(8,128)(2,1)S(1)} %get-tuple-element.75), channel_id=1, source_target_pairs={{0,12},{2,14},{4,8},{6,10},{8,20},{10,22},{12,16},{14,18},{16,28},... | collective-permute-start | bytes 49160 | tf_op jit(solution)/shard_map/ppermute | solution.py:931
  97.3 1.3 %collective-permute-start.32 = (bf16[5,64,128]{2,1,0:T(8,128)(2,1)S(1)}, bf16[5,64,128]{2,1,0:T(8,128)(2,1)S(1)}, u32[]{:S(2)}, u32[]{:S(2)}) collective-permute-start(bf16[5,64,128]{2,1,0:T(8,128)(2,1)S(1)} %get-tuple-element.77), channel_id=1, source_target_pairs={{0,2},{2,0},{4,6},{6,4},{1,3},{3,1},{5,7},{7,5},{8,10},{10,8},{12,... | collective-permute-start | bytes 245768 | tf_op jit(solution)/shard_map/ppermute | solution.py:967
  98.7 18.9 %collective-permute-start.33 = (bf16[5,64,128]{2,1,0:T(8,128)(2,1)S(1)}, bf16[5,64,128]{2,1,0:T(8,128)(2,1)S(1)}, u32[]{:S(2)}, u32[]{:S(2)}) collective-permute-start(bf16[5,64,128]{2,1,0:T(8,128)(2,1)S(1)} %add_convert_fusion.refs_8_), channel_id=1, source_target_pairs={{0,4},{1,5},{2,6},{3,7},{4,0},{5,1},{6,2},{7,3},{8,12},{9,13},{10,... | collective-permute-start | bytes 245768 | tf_op jit(solution)/shard_map/ppermute | solution.py:979
  99.8 17.7 %collective-permute-start.34 = (bf16[5,64,128]{2,1,0:T(8,128)(2,1)S(1)}, bf16[5,64,128]{2,1,0:T(8,128)(2,1)S(1)}, u32[]{:S(2)}, u32[]{:S(2)}) collective-permute-start(bf16[5,64,128]{2,1,0:T(8,128)(2,1)S(1)} %add_convert_fusion.refs_8_), channel_id=1, source_target_pairs={{0,1},{1,0},{2,3},{3,2},{4,5},{5,4},{6,7},{7,6},{8,9},{9,8},{10,11... | collective-permute-start | bytes 245768 | tf_op jit(solution)/shard_map/ppermute | solution.py:979
  101.3 16.2 %collective-permute-start.35 = (bf16[5,64,128]{2,1,0:T(8,128)(2,1)S(1)}, bf16[5,64,128]{2,1,0:T(8,128)(2,1)S(1)}, u32[]{:S(2)}, u32[]{:S(2)}) collective-permute-start(bf16[5,64,128]{2,1,0:T(8,128)(2,1)S(1)} %add_convert_fusion.refs_8_), channel_id=1, source_target_pairs={{0,5},{1,4},{2,7},{3,6},{4,1},{5,0},{6,3},{7,2},{8,13},{9,12},{10,... | collective-permute-start | bytes 245768 | tf_op jit(solution)/shard_map/ppermute | solution.py:979
  102.2 3.9 %collective-permute-start.28 = (bf16[128,64]{1,0:T(8,128)(2,1)S(1)}, bf16[128,64]{1,0:T(8,128)(2,1)S(1)}, u32[]{:S(2)}, u32[]{:S(2)}) collective-permute-start(bf16[128,64]{1,0:T(8,128)(2,1)S(1)} %get-tuple-element.76.refs_0_), channel_id=1, source_target_pairs={{0,8},{8,0},{16,24},{24,16},{1,9},{9,1},{17,25},{25,17},{2,10},{10... | collective-permute-start | bytes 49160 | tf_op jit(solution)/shard_map/ppermute | solution.py:963
  102.2 15.3 %collective-permute-start.31 = (f32[1,9216]{1,0:T(1,128)S(1)}, f32[1,9216]{1,0:T(1,128)S(1)}, u32[]{:S(2)}, u32[]{:S(2)}) collective-permute-start(f32[1,9216]{1,0:T(1,128)S(1)} %copy-done.5), channel_id=1, source_target_pairs={{0,1},{1,0},{2,3},{3,2},{4,5},{5,4},{6,7},{7,6},{8,9},{9,8},{10,11... | collective-permute-start | bytes 110600 | tf_op jit(solution)/shard_map/ppermute | solution.py:32
  106.1 5.0 %collective-permute-start.29 = (bf16[128,64]{1,0:T(8,128)(2,1)S(1)}, bf16[128,64]{1,0:T(8,128)(2,1)S(1)}, u32[]{:S(2)}, u32[]{:S(2)}) collective-permute-start(bf16[128,64]{1,0:T(8,128)(2,1)S(1)} %get-tuple-element.76.refs_0_), channel_id=1, source_target_pairs={{0,16},{8,24},{16,0},{24,8},{1,17},{9,25},{17,1},{25,9},{2,18},{10... | collective-permute-start | bytes 49160 | tf_op jit(solution)/shard_map/ppermute | solution.py:962
  111.1 5.7 %collective-permute-start.30 = (bf16[128,64]{1,0:T(8,128)(2,1)S(1)}, bf16[128,64]{1,0:T(8,128)(2,1)S(1)}, u32[]{:S(2)}, u32[]{:S(2)}) collective-permute-start(bf16[128,64]{1,0:T(8,128)(2,1)S(1)} %get-tuple-element.76.refs_0_), channel_id=1, source_target_pairs={{0,24},{8,16},{16,8},{24,0},{1,25},{9,17},{17,9},{25,1},{2,26},{10... | collective-permute-start | bytes 49160 | tf_op jit(solution)/shard_map/ppermute | solution.py:961

commit v9 on v8

--- a/solution.py
+++ b/solution.py
@@ -13,7 +13,7 @@
 EPS = 1e-06
 ADV_WEIGHT = 3.0
 TILE = 512
-STREAMS = 12
+STREAMS = 6
 SPARE = 8 << 20
 VMEM = pl.BlockSpec(memory_space=pltpu.VMEM)
 HBM = pl.BlockSpec(memory_space=pltpu.HBM)
@@ -209,11 +209,11 @@
     return -(-width // 2048) * 16
 
 
-def condition_kernel(fetches, packed_out, noisy_out, held, mod_rows, arrivals):
-    times, text, time_w, clean_t, noise, mod_w = fetches
+def condition_kernel(fetches, packed_out, noisy_out, kind_out, held, mod_rows, arrivals):
+    times, text, time_w, clean_t, noise, mod_w, kind_w = fetches
     model_width = held.shape[0]
     rows = model_width // STREAMS
-    for fetch in fetches[:-1]:
+    for fetch in fetches[:-2]:
         fetch.start()
     copies = [
         pltpu.make_async_copy(
@@ -221,6 +221,7 @@
         )
         for part in range(STREAMS)
     ]
+    copies.append(pltpu.make_async_copy(kind_w, kind_out, arrivals.at[STREAMS]))
     for copy in copies:
         copy.start()
     student_step, critic_step = steps_of(times)
@@ -234,6 +235,14 @@
     features = jnp.broadcast_to(features, (8, 2 * half)).astype(jnp.bfloat16)
     hidden = dot32(features, time_w.ready()[...])
     hidden = (hidden / (1.0 + jnp.exp(-hidden))).astype(jnp.bfloat16)
+    mod_rows[...] = jnp.zeros_like(mod_rows)
+    total = None
+    for part in range(STREAMS):
+        copies[part].wait()
+        piece = dot32(
+            hidden[:, part * rows : (part + 1) * rows], held[part * rows : (part + 1) * rows]
+        )
+        total = piece if total is None else total + piece
     sigma_student = noise_level(student_step)
     clean_ref, noise_ref = clean_t.ready(), noise.ready()
     noisy = (1.0 - sigma_student) * clean_ref[...].astype(jnp.float32).T + sigma_student * noise_ref[
@@ -243,20 +252,13 @@
     noisy_out[...] = noisy
     top = noisy.shape[0] // 2
     packed_out[:top] = jnp.concatenate([noisy[:top], noisy[top:]], axis=1)
-    mod_rows[...] = jnp.zeros_like(mod_rows)
-    total = None
-    for part in range(STREAMS):
-        copies[part].wait()
-        piece = dot32(
-            hidden[:, part * rows : (part + 1) * rows], held[part * rows : (part + 1) * rows]
-        )
-        total = piece if total is None else total + piece
     width = total.shape[1]
     for row, first in enumerate(range(0, width, 128)):
         size = min(128, width - first)
         mod_rows[row : row + 1, :size] = total[:1, first : first + size]
     depth = mod_rows.shape[0]
     packed_out[top : top + depth], packed_out[top + depth :] = halves(mod_rows[...])
+    copies[STREAMS].wait()
 
 
 def rms_scale(values, gain_vec):
@@ -313,17 +315,13 @@
         )
 
 
-def stage_kernel(fetches, near, kind_out, part_out, arrival):
-    copy = pltpu.make_async_copy(fetches[0], kind_out, arrival.at[0])
-    copy.start()
+def stage_kernel(fetches, near, part_out):
     width = part_out.shape[1]
     for place in range(2):
 
         @pl.when(lax.axis_index("dp") == place)
         def _():
             part_out[...] = near[:, place * width : (place + 1) * width]
-
-    copy.wait()
 
 
 def student_front_kernel(count, width, fetches, embed_w, head_w, gains, *refs):
@@ -796,44 +794,35 @@
     kind_w = jnp.transpose(w_qkv[0, :, 0], (1, 0, 2))
     final_w = jnp.transpose(w_final[0])
     groups = lax.axis_size("dp")
-    staged = []
 
     def stage(near):
         rows, width = near.shape
-        kinds, part = run(
-            stage_kernel,
-            [pltpu.VMEM(kind_w.shape, bf16), array((rows, width // 2), bf16)],
-            (near,),
-            1000,
-            scratch=(pltpu.SemaphoreType.DMA((1,)),),
-            streamed=(kind_w,),
-        )
-        staged.append(kinds)
+        (part,) = run(stage_kernel, [array((rows, width // 2), bf16)], (near,), 1000)
         return part
 
     heads_w = spread_heads(w_out[0, 0], count, groups, stage)
-    if staged:
-        kind_w = pltpu.with_memory_space_constraint(staged[0], pltpu.VMEM)
     sizes = [len(pieces) for pieces in heads_w]
     heads_w = sum(heads_w, [])
 
     depth = packed_rows(mod_width)
-    packed, noisy_student = run(
+    packed, noisy_student, kind_w = run(
         condition_kernel,
         [
             array((tok_rows // 2 + 2 * depth, 2 * latent_width), bf16),
             array((tok_rows, latent_width), bf16),
+            pltpu.VMEM(kind_w.shape, bf16),
         ],
         (),
         2 * model_width * mod_width,
         scratch=(
             pltpu.VMEM((model_width, mod_width), bf16),
             pltpu.VMEM((depth, 128), f32),
-            pltpu.SemaphoreType.DMA((STREAMS,)),
+            pltpu.SemaphoreType.DMA((STREAMS + 1,)),
         ),
         fetched=(timesteps, text_vec, w_time[0], jnp.transpose(clean[0]), noise[0]),
-        streamed=(w_mod[0],),
-    )
+        streamed=(w_mod[0], kind_w),
+    )
+    kind_w = pltpu.with_memory_space_constraint(kind_w, pltpu.VMEM)
     packed_all = gather_near(packed, "seq", count)
 
     head_blocks = [array((tok_rows, head_width), bf16)] * count

time: 121 us -> 119 us (0.983)
  Pallas kernels: 25.4 us -> 22.8 us
    pallas_call x13, Pallas kernels: 25.4 us -> 22.8 us  [run(): pl.pallas_call(body, out_shape=list(outputs) + [pltpu.HBM(item.shape, ite...]
  transfers between devices with their start and end apart: 36 -> 36, of which waited for: 22 -> 22; matrix products, arithmetic and copies ran while one was open for 0% -> 0% of each run, Pallas kernels for 15% -> 13%
where the time goes in v9:
time: 119 us; the launch traced here: 118 us
  waiting for transfers between devices  51.1 us (43%)
  starting transfers between devices  42.4 us (36%)
  Pallas kernels  22.8 us (19%)
    pallas_call x13, Pallas kernels, run(): pl.pallas_call(body, out_shape=list(outputs) + [pltpu.HBM(item.shape, ite...  22.8 us
    ppermute x1, waiting for transfers between devices, spread_heads(): near = lax.ppermute(part, 'seq', swaps(count, bit))  11.9 us
    ppermute x1, starting transfers between devices, step(): fake = lax.ppermute(term_rows, 'segment', swaps(sections, 2))  10.1 us
    ppermute x9, waiting for transfers between devices, scatter_near(): lax.ppermute(blocks[offset], axis, swaps(count, offset))  7.77 us
    ppermute x7, starting transfers between devices, gather_near(): lax.ppermute(value, axis, swaps(count, offset))  6.25 us
    ppermute x1, waiting for transfers between devices, spread_heads(): held[bit] = [near, lax.ppermute(stage(near), 'dp', swaps(groups, 1))]  5.76 us
    ppermute x1, starting transfers between devices, step(): real = lax.ppermute(real, 'segment', swaps(sections, 1))  5.68 us
    ppermute x9, starting transfers between devices, scatter_near(): lax.ppermute(blocks[offset], axis, swaps(count, offset))  5.45 us
  transfers between devices with their start and end apart: 36, of which 22 were waited for; matrix products, arithmetic and copies ran while one was open for 0% of the time, Pallas kernels for 13%

profile of v9, /device:TPU:0, one launch (start us, length us, event | category | flops | bytes accessed | tf_op | source)
XLA Modules:
  0.0 118.5 jit_solution(10417516412454899602)
XLA Ops:
  0.6 1.1 dynamic-slice_bitcast_fusion
  1.7 3.1 %collective-permute-start.7 = (bf16[128,2048]{1,0:T(8,128)(2,1)S(1)}, bf16[128,2048]{1,0:T(8,128)(2,1)S(1)}, u32[]{:S(2)}, u32[]{:S(2)}) collective-permute-start(bf16[128,2048]{1,0:T(8,128)(2,1)S(1)} %dynamic-slice_bitcast_fusion), channel_id=1, source_target_pairs={{0,4},{2,6},{4,0},{6,2},{1,5},{3,7},{5,1},{7,3},{8,12},{10,14},{12... | collective-permute-start | bytes 1572872 | tf_op jit(solution)/shard_map/ppermute | solution.py:52
  4.8 0.0 collective-permute-start.6
  4.8 11.9 %collective-permute-done.7.refs_0_.refs_8_.refs_3_ = bf16[128,2048]{1,0:T(8,128)(2,1)S(1)} collective-permute-done((bf16[128,2048]{1,0:T(8,128)(2,1)S(1)}, bf16[128,2048]{1,0:T(8,128)(2,1)S(1)}, u32[]{:S(2)}, u32[]{:S(2)}) %collective-permute-start.7) | collective-permute-done | bytes 524320 | tf_op jit(solution)/shard_map/ppermute | solution.py:52
  16.7 1.8 %collective-permute-start.8 = (bf16[128,1024]{1,0:T(8,128)(2,1)S(1)}, bf16[128,1024]{1,0:T(8,128)(2,1)S(1)}, u32[]{:S(2)}, u32[]{:S(2)}) collective-permute-start(bf16[128,1024]{1,0:T(8,128)(2,1)S(1)} %shard_map.125), channel_id=1, source_target_pairs={{0,1},{1,0},{2,3},{3,2},{4,5},{5,4},{6,7},{7,6},{8,9},{9,8},{10,11... | collective-permute-start | bytes 786440 | tf_op jit(solution)/shard_map/ppermute | solution.py:53
  18.5 5.8 %collective-permute-done.8.refs_9_.refs_4_ = bf16[128,1024]{1,0:T(8,128)(2,1)S(1)} collective-permute-done((bf16[128,1024]{1,0:T(8,128)(2,1)S(1)}, bf16[128,1024]{1,0:T(8,128)(2,1)S(1)}, u32[]{:S(2)}, u32[]{:S(2)}) %collective-permute-start.8) | collective-permute-done | bytes 262176 | tf_op jit(solution)/shard_map/ppermute | solution.py:53
  24.3 0.0 collective-permute-start.10
  24.3 10.5 %shard_map.122 = (bf16[128,128]{1,0:T(8,128)(2,1)S(1)}, bf16[128,64]{1,0:T(8,128)(2,1)S(1)}, bf16[3,3072,128]{2,1,0:T(8,128)(2,1)S(1)}) custom-call(s32[2,2]{1,0:T(2,128)} %refs_14_.1, f32[1,256]{1,0:T(1,128)} %refs_1_.4, bf16[256,3072]{1,0:T(8,128)(2,1)} %bitcast.27, bf16[64,128]{1,0:T(8,128)(2,1)} %bitcast.35, bf16[128,128]{1,0:T(8,128)(2,1)} %bitcast.31, ...), custom_call_target="tpu_custom_call" | custom-call | flops 23592960 | bytes 4031504 | tf_op jit(solution)/shard_map/pallas_call | solution.py:187
  34.7 0.0 copy-start
  34.8 0.6 collective-permute-start
  35.3 1.5 %collective-permute-start.1 = (bf16[128,128]{1,0:T(8,128)(2,1)S(1)}, bf16[128,128]{1,0:T(8,128)(2,1)S(1)}, u32[]{:S(2)}, u32[]{:S(2)}) collective-permute-start(bf16[128,128]{1,0:T(8,128)(2,1)S(1)} %get-tuple-element.40.refs_3_), channel_id=1, source_target_pairs={{0,4},{2,6},{4,0},{6,2},{1,5},{3,7},{5,1},{7,3},{8,12},{10,14},{12... | collective-permute-start | bytes 98312 | tf_op jit(solution)/shard_map/ppermute | solution.py:32
  36.8 0.8 collective-permute-start.2
  37.6 1.6 %collective-permute-done.1.refs_5_ = bf16[128,128]{1,0:T(8,128)(2,1)S(1)} collective-permute-done((bf16[128,128]{1,0:T(8,128)(2,1)S(1)}, bf16[128,128]{1,0:T(8,128)(2,1)S(1)}, u32[]{:S(2)}, u32[]{:S(2)}) %collective-permute-start.1) | collective-permute-done | bytes 32800 | tf_op jit(solution)/shard_map/ppermute | solution.py:32
  39.2 1.2 %collective-permute-done.2.refs_6_ = bf16[128,128]{1,0:T(8,128)(2,1)S(1)} collective-permute-done((bf16[128,128]{1,0:T(8,128)(2,1)S(1)}, bf16[128,128]{1,0:T(8,128)(2,1)S(1)}, u32[]{:S(2)}, u32[]{:S(2)}) %collective-permute-start.2) | collective-permute-done | bytes 32800 | tf_op jit(solution)/shard_map/ppermute | solution.py:32
  40.5 3.6 %shard_map.123 = (bf16[128,128]{1,0:T(8,128)(2,1)S(1)}, bf16[128,128]{1,0:T(8,128)(2,1)S(1)}, bf16[128,128]{1,0:T(8,128)(2,1)S(1)}, bf16[128,128]{1,0:T(8,128)(2...) custom-call(bf16[1,64,3072]{2,1,0:T(8,128)(2,1)S(1)} %copy-done.1, ...), custom_call_target="tpu_custom_call" | custom-call | flops 301989888 | bytes 3138560 | tf_op jit(solution)/shard_map/pallas_call | solution.py:187
  44.1 0.2 collective-permute-start.3
  44.2 0.8 collective-permute-start.4
  45.0 0.3 collective-permute-done.3.refs_3_
  45.4 0.7 collective-permute-start.5
  46.0 2.1 %collective-permute-done.4.refs_4_ = bf16[128,128]{1,0:T(8,128)(2,1)S(1)} collective-permute-done((bf16[128,128]{1,0:T(8,128)(2,1)S(1)}, bf16[128,128]{1,0:T(8,128)(2,1)S(1)}, u32[]{:S(2)}, u32[]{:S(2)}) %collective-permute-start.4) | collective-permute-done | bytes 32800 | tf_op jit(solution)/shard_map/ppermute | solution.py:37
  48.2 0.5 collective-permute-done.5.refs_5_
  48.7 3.0 %shard_map.126 = (bf16[128,128]{1,0:T(8,128)(2,1)S(1)}, bf16[4,128,128]{2,1,0:T(8,128)(2,1)}, f32[128,128]{1,0:T(8,128)}) custom-call(bf16[128,64]{1,0:T(8,128)(2,1)S(1)} %get-tuple-element.42.refs_0_.refs_3_, bf16[1,64,3072]{2,1,0:T(8,128)(2,1)S(1)} %copy-done.1, bf16[128,128]{1,0:T(8,128)(2,1)S(1)} %get-tuple-element.43.refs_2_, ...), custom_call_target="tpu_custom_call" | custom-call | flops 402653184 | bytes 4182032 | tf_op jit(solution)/shard_map/pallas_call | solution.py:187
  51.7 1.3 %collective-permute-start.11 = (bf16[128,128]{1,0:T(8,128)(2,1)S(1)}, bf16[128,128]{1,0:T(8,128)(2,1)S(1)}, u32[]{:S(2)}, u32[]{:S(2)}) collective-permute-start(bf16[128,128]{1,0:T(8,128)(2,1)S(1)} %get-tuple-element.48.refs_0_), channel_id=1, source_target_pairs={{0,8},{1,9},{2,10},{3,11},{4,12},{5,13},{6,14},{7,15}} | collective-permute-start | bytes 98312 | tf_op jit(solution)/shard_map/ppermute | solution.py:866
  53.0 1.3 %collective-permute-start.12 = (bf16[128,128]{1,0:T(8,128)(2,1)S(1)}, bf16[128,128]{1,0:T(8,128)(2,1)S(1)}, u32[]{:S(2)}, u32[]{:S(2)}) collective-permute-start(bf16[128,128]{1,0:T(8,128)(2,1)S(1)} %get-tuple-element.48.refs_0_), channel_id=1, source_target_pairs={{0,16},{1,17},{2,18},{3,19},{4,20},{5,21},{6,22},{7,23}} | collective-permute-start | bytes 98312 | tf_op jit(solution)/shard_map/ppermute | solution.py:866
  54.3 1.3 %collective-permute-start.13 = (bf16[128,128]{1,0:T(8,128)(2,1)S(1)}, bf16[128,128]{1,0:T(8,128)(2,1)S(1)}, u32[]{:S(2)}, u32[]{:S(2)}) collective-permute-start(bf16[128,128]{1,0:T(8,128)(2,1)S(1)} %get-tuple-element.48.refs_0_), channel_id=1, source_target_pairs={{0,24},{1,25},{2,26},{3,27},{4,28},{5,29},{6,30},{7,31}} | collective-permute-start | bytes 98312 | tf_op jit(solution)/shard_map/ppermute | solution.py:866
  55.6 0.3 collective-permute-done.12.refs_2_
  55.9 1.3 %collective-permute-done.13.refs_3_ = bf16[128,128]{1,0:T(8,128)(2,1)S(1)} collective-permute-done((bf16[128,128]{1,0:T(8,128)(2,1)S(1)}, bf16[128,128]{1,0:T(8,128)(2,1)S(1)}, u32[]{:S(2)}, u32[]{:S(2)}) %collective-permute-start.13) | collective-permute-done | bytes 32800 | tf_op jit(solution)/shard_map/ppermute | solution.py:866
  57.2 0.1 collective-permute-start.14
  57.3 1.0 collective-permute-start.15
  58.3 0.8 collective-permute-start.16
  59.1 2.1 %collective-permute-done.15.refs_5_.refs_10_ = bf16[128,64]{1,0:T(8,128)(2,1)S(1)} collective-permute-done((bf16[128,64]{1,0:T(8,128)(2,1)S(1)}, bf16[128,64]{1,0:T(8,128)(2,1)S(1)}, u32[]{:S(2)}, u32[]{:S(2)}) %collective-permute-start.15) | collective-permute-done | bytes 16416 | tf_op jit(solution)/shard_map/ppermute | solution.py:32
  61.3 0.4 collective-permute-done.16.refs_6_.refs_11_
  61.7 0.2 collective-permute-start.17
  61.9 1.1 collective-permute-start.18
  63.0 0.6 collective-permute-start.19
  63.6 2.2 %collective-permute-done.18.refs_4_.refs_10_ = bf16[128,128]{1,0:T(8,128)(2,1)S(1)} collective-permute-done((bf16[128,128]{1,0:T(8,128)(2,1)S(1)}, bf16[128,128]{1,0:T(8,128)(2,1)S(1)}, u32[]{:S(2)}, u32[]{:S(2)}) %collective-permute-start.18) | collective-permute-done | bytes 32800 | tf_op jit(solution)/shard_map/ppermute | solution.py:37
  65.8 0.6 collective-permute-done.19.refs_5_.refs_11_
  66.5 0.2 collective-permute-start.20
  66.6 0.9 collective-permute-start.21
  67.6 0.8 collective-permute-start.22
  68.4 0.6 shard_map.124.refs_1_
  69.0 1.5 %collective-permute-done.21.refs_14_ = bf16[128,128]{1,0:T(8,128)(2,1)S(1)} collective-permute-done((bf16[128,128]{1,0:T(8,128)(2,1)S(1)}, bf16[128,128]{1,0:T(8,128)(2,1)S(1)}, u32[]{:S(2)}, u32[]{:S(2)}) %collective-permute-start.21) | collective-permute-done | bytes 32800 | tf_op jit(solution)/shard_map/ppermute | solution.py:37
  70.6 0.4 collective-permute-done.22.refs_15_
  71.0 0.2 collective-permute-start.25
  71.2 5.7 %collective-permute-start.23 = (bf16[160,64]{1,0:T(8,128)(2,1)S(1)}, bf16[160,64]{1,0:T(8,128)(2,1)S(1)}, u32[]{:S(2)}, u32[]{:S(2)}) collective-permute-start(bf16[160,64]{1,0:T(8,128)(2,1)S(1)} %get-tuple-element.64), channel_id=1, source_target_pairs={{0,8},{8,0},{16,24},{24,16},{1,9},{9,1},{17,25},{25,17},{2,10},{10... | collective-permute-start | bytes 61448 | tf_op jit(solution)/shard_map/ppermute | solution.py:917
  76.9 10.1 %collective-permute-start.24 = (bf16[128,64]{1,0:T(8,128)(2,1)S(1)}, bf16[128,64]{1,0:T(8,128)(2,1)S(1)}, u32[]{:S(2)}, u32[]{:S(2)}) collective-permute-start(bf16[128,64]{1,0:T(8,128)(2,1)S(1)} %get-tuple-element.59.refs_7_), channel_id=1, source_target_pairs={{0,16},{8,24},{16,0},{24,8},{1,17},{9,25},{17,1},{25,9},{2,18},{10... | collective-permute-start | bytes 49160 | tf_op jit(solution)/shard_map/ppermute | solution.py:900
  87.0 0.1 collective-permute-start.26
  87.0 1.1 collective-permute-start.27
  88.1 1.3 %collective-permute-done.24.refs_1_ = bf16[128,64]{1,0:T(8,128)(2,1)S(1)} collective-permute-done((bf16[128,64]{1,0:T(8,128)(2,1)S(1)}, bf16[128,64]{1,0:T(8,128)(2,1)S(1)}, u32[]{:S(2)}, u32[]{:S(2)}) %collective-permute-start.24) | collective-permute-done | bytes 16416 | tf_op jit(solution)/shard_map/ppermute | solution.py:900
  89.4 3.3 %collective-permute-done.26.refs_12_ = bf16[128,64]{1,0:T(8,128)(2,1)S(1)} collective-permute-done((bf16[128,64]{1,0:T(8,128)(2,1)S(1)}, bf16[128,64]{1,0:T(8,128)(2,1)S(1)}, u32[]{:S(2)}, u32[]{:S(2)}) %collective-permute-start.26) | collective-permute-done | bytes 16416 | tf_op jit(solution)/shard_map/ppermute | solution.py:920
  92.7 1.0 collective-permute-done.27.refs_13_
  93.7 1.1 shard_map.132
  94.8 0.1 collective-permute-start.32
  94.9 1.3 %collective-permute-done.32 = bf16[5,64,128]{2,1,0:T(8,128)(2,1)S(1)} collective-permute-done((bf16[5,64,128]{2,1,0:T(8,128)(2,1)S(1)}, bf16[5,64,128]{2,1,0:T(8,128)(2,1)S(1)}, u32[]{:S(2)}, u32[]{:S(2)}) %collective-permute-start.32) | collective-permute-done | bytes 81952 | tf_op jit(solution)/shard_map/ppermute | solution.py:956
  96.2 1.1 collective-permute-start.33
  97.3 1.5 %collective-permute-start.34 = (bf16[5,64,128]{2,1,0:T(8,128)(2,1)S(1)}, bf16[5,64,128]{2,1,0:T(8,128)(2,1)S(1)}, u32[]{:S(2)}, u32[]{:S(2)}) collective-permute-start(bf16[5,64,128]{2,1,0:T(8,128)(2,1)S(1)} %add_convert_fusion.refs_8_), channel_id=1, source_target_pairs={{0,1},{1,0},{2,3},{3,2},{4,5},{5,4},{6,7},{7,6},{8,9},{9,8},{10,11... | collective-permute-start | bytes 245768 | tf_op jit(solution)/shard_map/ppermute | solution.py:968
  98.8 0.9 collective-permute-start.35
  99.7 1.5 %collective-permute-start.31 = (f32[1,9216]{1,0:T(1,128)S(1)}, f32[1,9216]{1,0:T(1,128)S(1)}, u32[]{:S(2)}, u32[]{:S(2)}) collective-permute-start(f32[1,9216]{1,0:T(1,128)S(1)} %copy-done.5), channel_id=1, source_target_pairs={{0,1},{1,0},{2,3},{3,2},{4,5},{5,4},{6,7},{7,6},{8,9},{9,8},{10,11... | collective-permute-start | bytes 110600 | tf_op jit(solution)/shard_map/ppermute | solution.py:32
  101.2 2.4 %collective-permute-done.28.refs_1_ = bf16[128,64]{1,0:T(8,128)(2,1)S(1)} collective-permute-done((bf16[128,64]{1,0:T(8,128)(2,1)S(1)}, bf16[128,64]{1,0:T(8,128)(2,1)S(1)}, u32[]{:S(2)}, u32[]{:S(2)}) %collective-permute-start.28) | collective-permute-done | bytes 16416 | tf_op jit(solution)/shard_map/ppermute | solution.py:952
  103.6 5.0 %collective-permute-done.29.refs_2_ = bf16[128,64]{1,0:T(8,128)(2,1)S(1)} collective-permute-done((bf16[128,64]{1,0:T(8,128)(2,1)S(1)}, bf16[128,64]{1,0:T(8,128)(2,1)S(1)}, u32[]{:S(2)}, u32[]{:S(2)}) %collective-permute-start.29) | collective-permute-done | bytes 16416 | tf_op jit(solution)/shard_map/ppermute | solution.py:951
  108.6 1.2 %collective-permute-start.30 = (bf16[128,64]{1,0:T(8,128)(2,1)S(1)}, bf16[128,64]{1,0:T(8,128)(2,1)S(1)}, u32[]{:S(2)}, u32[]{:S(2)}) collective-permute-start(bf16[128,64]{1,0:T(8,128)(2,1)S(1)} %get-tuple-element.74.refs_0_), channel_id=1, source_target_pairs={{0,24},{8,16},{16,8},{24,0},{1,25},{9,17},{17,9},{25,1},{2,26},{10... | collective-permute-start | bytes 49160 | tf_op jit(solution)/shard_map/ppermute | solution.py:950
  109.8 4.5 %collective-permute-done.30.refs_3_ = bf16[128,64]{1,0:T(8,128)(2,1)S(1)} collective-permute-done((bf16[128,64]{1,0:T(8,128)(2,1)S(1)}, bf16[128,64]{1,0:T(8,128)(2,1)S(1)}, u32[]{:S(2)}, u32[]{:S(2)}) %collective-permute-start.30) | collective-permute-done | bytes 16416 | tf_op jit(solution)/shard_map/ppermute | solution.py:950
  114.3 0.7 shard_map.133
  115.1 3.3 %shard_map.134 = f32[64,3072]{1,0:T(8,128)} custom-call(bf16[1,64,3072]{2,1,0:T(8,128)(2,1)S(1)} %copy-done.1, bf16[128,3072]{1,0:T(8,128)(2,1)S(1)} %bitcast.24, bf16[128,3072]{1,0:T(8,128)(2,1)S(1)} %collective-permute-done.6.refs_7_.refs_2_, bf16[128,2048]{1,0:T(8,128)(2,1)S(1)} %collective-permute-done.7.refs_0_.refs_8_.refs_3_, ...), custom_call_target="tpu_custom_call" | custom-call | flops 805306368 | bytes 4726784 | tf_op jit(solution)/shard_map/pallas_call | solution.py:187
  (35 shorter events, 0.2 us)
Async XLA Ops:
  1.7 15.0 %collective-permute-start.7 = (bf16[128,2048]{1,0:T(8,128)(2,1)S(1)}, bf16[128,2048]{1,0:T(8,128)(2,1)S(1)}, u32[]{:S(2)}, u32[]{:S(2)}) collective-permute-start(bf16[128,2048]{1,0:T(8,128)(2,1)S(1)} %dynamic-slice_bitcast_fusion), channel_id=1, source_target_pairs={{0,4},{2,6},{4,0},{6,2},{1,5},{3,7},{5,1},{7,3},{8,12},{10,14},{12... | collective-permute-start | bytes 1572872 | tf_op jit(solution)/shard_map/ppermute | solution.py:52
  4.8 43.9 %collective-permute-start.6 = (bf16[128,3072]{1,0:T(8,128)(2,1)}, bf16[128,3072]{1,0:T(8,128)(2,1)S(1)}, u32[]{:S(2)}, u32[]{:S(2)}) collective-permute-start(bf16[128,3072]{1,0:T(8,128)(2,1)} %bitcast.21), channel_id=1, source_target_pairs={{0,2},{2,0},{4,6},{6,4},{1,3},{3,1},{5,7},{7,5},{8,10},{10,8},{12,... | collective-permute-start | bytes 2359304 | tf_op jit(solution)/shard_map/ppermute | solution.py:56
  16.7 7.5 %collective-permute-start.8 = (bf16[128,1024]{1,0:T(8,128)(2,1)S(1)}, bf16[128,1024]{1,0:T(8,128)(2,1)S(1)}, u32[]{:S(2)}, u32[]{:S(2)}) collective-permute-start(bf16[128,1024]{1,0:T(8,128)(2,1)S(1)} %shard_map.125), channel_id=1, source_target_pairs={{0,1},{1,0},{2,3},{3,2},{4,5},{5,4},{6,7},{7,6},{8,9},{9,8},{10,11... | collective-permute-start | bytes 786440 | tf_op jit(solution)/shard_map/ppermute | solution.py:53
  18.5 30.2 %collective-permute-start.9 = (bf16[128,2048]{1,0:T(8,128)(2,1)S(1)}, bf16[128,2048]{1,0:T(8,128)(2,1)S(1)}, u32[]{:S(2)}, u32[]{:S(2)}) collective-permute-start(bf16[128,2048]{1,0:T(8,128)(2,1)S(1)} %collective-permute-done.7.refs_0_.refs_8_.refs_3_), channel_id=1, source_target_pairs={{0,2},{2,0},{4,6},{6,4},{1,3},{3,1},{5,7},{7,5},{8,10},{10,8},{12,... | collective-permute-start | bytes 1572872 | tf_op jit(solution)/shard_map/ppermute | solution.py:56
  24.3 24.4 %collective-permute-start.10 = (bf16[128,1024]{1,0:T(8,128)(2,1)S(1)}, bf16[128,1024]{1,0:T(8,128)(2,1)S(1)}, u32[]{:S(2)}, u32[]{:S(2)}) collective-permute-start(bf16[128,1024]{1,0:T(8,128)(2,1)S(1)} %collective-permute-done.8.refs_9_.refs_4_), channel_id=1, source_target_pairs={{0,2},{2,0},{4,6},{6,4},{1,3},{3,1},{5,7},{7,5},{8,10},{10,8},{12,... | collective-permute-start | bytes 786440 | tf_op jit(solution)/shard_map/ppermute | solution.py:56
  24.3 16.2 %copy-start.1 = (bf16[1,64,3072]{2,1,0:T(8,128)(2,1)S(1)}, bf16[1,64,3072]{2,1,0:T(8,128)(2,1)}, u32[]{:S(2)}) copy-start(bf16[1,64,3072]{2,1,0:T(8,128)(2,1)} %refs_0_.7) | copy-start | bytes 1179652
  24.3 16.2 %copy-start.4 = (f32[1,2,128]{2,1,0:T(2,128)S(1)}, f32[1,2,128]{2,1,0:T(2,128)}, u32[]{:S(2)}) copy-start(f32[1,2,128]{2,1,0:T(2,128)} %refs_2_.5) | copy-start | bytes 3076
  34.7 14.0 %copy-start = (bf16[1,1,128,3072]{3,2,1,0:T(8,128)(2,1)S(1)}, bf16[1,1,128,3072]{3,2,1,0:T(8,128)(2,1)}, u32[]{:S(2)}) copy-start(bf16[1,1,128,3072]{3,2,1,0:T(8,128)(2,1)} %param.19) | copy-start | bytes 2359300
  34.8 2.0 %collective-permute-start = (bf16[128,128]{1,0:T(8,128)(2,1)S(1)}, bf16[128,128]{1,0:T(8,128)(2,1)S(1)}, u32[]{:S(2)}, u32[]{:S(2)}) collective-permute-start(bf16[128,128]{1,0:T(8,128)(2,1)S(1)} %get-tuple-element.40.refs_3_), channel_id=1, source_target_pairs={{0,2},{2,0},{4,6},{6,4},{1,3},{3,1},{5,7},{7,5},{8,10},{10,8},{12,... | collective-permute-start | bytes 98312 | tf_op jit(solution)/shard_map/ppermute | solution.py:32
  35.3 3.9 %collective-permute-start.1 = (bf16[128,128]{1,0:T(8,128)(2,1)S(1)}, bf16[128,128]{1,0:T(8,128)(2,1)S(1)}, u32[]{:S(2)}, u32[]{:S(2)}) collective-permute-start(bf16[128,128]{1,0:T(8,128)(2,1)S(1)} %get-tuple-element.40.refs_3_), channel_id=1, source_target_pairs={{0,4},{2,6},{4,0},{6,2},{1,5},{3,7},{5,1},{7,3},{8,12},{10,14},{12... | collective-permute-start | bytes 98312 | tf_op jit(solution)/shard_map/ppermute | solution.py:32
  36.8 3.7 %collective-permute-start.2 = (bf16[128,128]{1,0:T(8,128)(2,1)S(1)}, bf16[128,128]{1,0:T(8,128)(2,1)S(1)}, u32[]{:S(2)}, u32[]{:S(2)}) collective-permute-start(bf16[128,128]{1,0:T(8,128)(2,1)S(1)} %get-tuple-element.40.refs_3_), channel_id=1, source_target_pairs={{0,6},{2,4},{4,2},{6,0},{1,7},{3,5},{5,3},{7,1},{8,14},{10,12},{12... | collective-permute-start | bytes 98312 | tf_op jit(solution)/shard_map/ppermute | solution.py:32
  44.1 1.3 %collective-permute-start.3 = (bf16[128,128]{1,0:T(8,128)(2,1)S(1)}, bf16[128,128]{1,0:T(8,128)(2,1)S(1)}, u32[]{:S(2)}, u32[]{:S(2)}) collective-permute-start(bf16[128,128]{1,0:T(8,128)(2,1)S(1)} %get-tuple-element.44), channel_id=1, source_target_pairs={{0,2},{2,0},{4,6},{6,4},{1,3},{3,1},{5,7},{7,5},{8,10},{10,8},{12,... | collective-permute-start | bytes 98312 | tf_op jit(solution)/shard_map/ppermute | solution.py:37
  44.2 3.9 %collective-permute-start.4 = (bf16[128,128]{1,0:T(8,128)(2,1)S(1)}, bf16[128,128]{1,0:T(8,128)(2,1)S(1)}, u32[]{:S(2)}, u32[]{:S(2)}) collective-permute-start(bf16[128,128]{1,0:T(8,128)(2,1)S(1)} %get-tuple-element.45), channel_id=1, source_target_pairs={{0,4},{2,6},{4,0},{6,2},{1,5},{3,7},{5,1},{7,3},{8,12},{10,14},{12... | collective-permute-start | bytes 98312 | tf_op jit(solution)/shard_map/ppermute | solution.py:37
  45.4 3.3 %collective-permute-start.5 = (bf16[128,128]{1,0:T(8,128)(2,1)S(1)}, bf16[128,128]{1,0:T(8,128)(2,1)S(1)}, u32[]{:S(2)}, u32[]{:S(2)}) collective-permute-start(bf16[128,128]{1,0:T(8,128)(2,1)S(1)} %get-tuple-element.46), channel_id=1, source_target_pairs={{0,6},{2,4},{4,2},{6,0},{1,7},{3,5},{5,3},{7,1},{8,14},{10,12},{12... | collective-permute-start | bytes 98312 | tf_op jit(solution)/shard_map/ppermute | solution.py:37
  51.7 3.9 %collective-permute-start.11 = (bf16[128,128]{1,0:T(8,128)(2,1)S(1)}, bf16[128,128]{1,0:T(8,128)(2,1)S(1)}, u32[]{:S(2)}, u32[]{:S(2)}) collective-permute-start(bf16[128,128]{1,0:T(8,128)(2,1)S(1)} %get-tuple-element.48.refs_0_), channel_id=1, source_target_pairs={{0,8},{1,9},{2,10},{3,11},{4,12},{5,13},{6,14},{7,15}} | collective-permute-start | bytes 98312 | tf_op jit(solution)/shard_map/ppermute | solution.py:866
  53.0 2.9 %collective-permute-start.12 = (bf16[128,128]{1,0:T(8,128)(2,1)S(1)}, bf16[128,128]{1,0:T(8,128)(2,1)S(1)}, u32[]{:S(2)}, u32[]{:S(2)}) collective-permute-start(bf16[128,128]{1,0:T(8,128)(2,1)S(1)} %get-tuple-element.48.refs_0_), channel_id=1, source_target_pairs={{0,16},{1,17},{2,18},{3,19},{4,20},{5,21},{6,22},{7,23}} | collective-permute-start | bytes 98312 | tf_op jit(solution)/shard_map/ppermute | solution.py:866
  54.3 2.9 %collective-permute-start.13 = (bf16[128,128]{1,0:T(8,128)(2,1)S(1)}, bf16[128,128]{1,0:T(8,128)(2,1)S(1)}, u32[]{:S(2)}, u32[]{:S(2)}) collective-permute-start(bf16[128,128]{1,0:T(8,128)(2,1)S(1)} %get-tuple-element.48.refs_0_), channel_id=1, source_target_pairs={{0,24},{1,25},{2,26},{3,27},{4,28},{5,29},{6,30},{7,31}} | collective-permute-start | bytes 98312 | tf_op jit(solution)/shard_map/ppermute | solution.py:866
  57.2 1.9 %collective-permute-start.14 = (bf16[128,64]{1,0:T(8,128)(2,1)S(1)}, bf16[128,64]{1,0:T(8,128)(2,1)S(1)}, u32[]{:S(2)}, u32[]{:S(2)}) collective-permute-start(bf16[128,64]{1,0:T(8,128)(2,1)S(1)} %get-tuple-element.49.refs_3_.refs_8_), channel_id=1, source_target_pairs={{0,2},{2,0},{4,6},{6,4},{1,3},{3,1},{5,7},{7,5},{8,10},{10,8},{12,... | collective-permute-start | bytes 49160 | tf_op jit(solution)/shard_map/ppermute | solution.py:32
  57.3 4.0 %collective-permute-start.15 = (bf16[128,64]{1,0:T(8,128)(2,1)S(1)}, bf16[128,64]{1,0:T(8,128)(2,1)S(1)}, u32[]{:S(2)}, u32[]{:S(2)}) collective-permute-start(bf16[128,64]{1,0:T(8,128)(2,1)S(1)} %get-tuple-element.49.refs_3_.refs_8_), channel_id=1, source_target_pairs={{0,4},{2,6},{4,0},{6,2},{1,5},{3,7},{5,1},{7,3},{8,12},{10,14},{12... | collective-permute-start | bytes 49160 | tf_op jit(solution)/shard_map/ppermute | solution.py:32
  58.3 3.4 %collective-permute-start.16 = (bf16[128,64]{1,0:T(8,128)(2,1)S(1)}, bf16[128,64]{1,0:T(8,128)(2,1)S(1)}, u32[]{:S(2)}, u32[]{:S(2)}) collective-permute-start(bf16[128,64]{1,0:T(8,128)(2,1)S(1)} %get-tuple-element.49.refs_3_.refs_8_), channel_id=1, source_target_pairs={{0,6},{2,4},{4,2},{6,0},{1,7},{3,5},{5,3},{7,1},{8,14},{10,12},{12... | collective-permute-start | bytes 49160 | tf_op jit(solution)/shard_map/ppermute | solution.py:32
  61.7 1.9 %collective-permute-start.17 = (bf16[128,128]{1,0:T(8,128)(2,1)S(1)}, bf16[128,128]{1,0:T(8,128)(2,1)S(1)}, u32[]{:S(2)}, u32[]{:S(2)}) collective-permute-start(bf16[128,128]{1,0:T(8,128)(2,1)S(1)} %get-tuple-element.56), channel_id=1, source_target_pairs={{0,2},{2,0},{4,6},{6,4},{1,3},{3,1},{5,7},{7,5},{8,10},{10,8},{12,... | collective-permute-start | bytes 98312 | tf_op jit(solution)/shard_map/ppermute | solution.py:37
  61.9 3.9 %collective-permute-start.18 = (bf16[128,128]{1,0:T(8,128)(2,1)S(1)}, bf16[128,128]{1,0:T(8,128)(2,1)S(1)}, u32[]{:S(2)}, u32[]{:S(2)}) collective-permute-start(bf16[128,128]{1,0:T(8,128)(2,1)S(1)} %get-tuple-element.57), channel_id=1, source_target_pairs={{0,4},{2,6},{4,0},{6,2},{1,5},{3,7},{5,1},{7,3},{8,12},{10,14},{12... | collective-permute-start | bytes 98312 | tf_op jit(solution)/shard_map/ppermute | solution.py:37
  63.0 3.4 %collective-permute-start.19 = (bf16[128,128]{1,0:T(8,128)(2,1)S(1)}, bf16[128,128]{1,0:T(8,128)(2,1)S(1)}, u32[]{:S(2)}, u32[]{:S(2)}) collective-permute-start(bf16[128,128]{1,0:T(8,128)(2,1)S(1)} %get-tuple-element.58), channel_id=1, source_target_pairs={{0,6},{2,4},{4,2},{6,0},{1,7},{3,5},{5,3},{7,1},{8,14},{10,12},{12... | collective-permute-start | bytes 98312 | tf_op jit(solution)/shard_map/ppermute | solution.py:37
  66.4 27.3 %copy-start.2 = (bf16[4,128,128]{2,1,0:T(8,128)(2,1)S(1)}, bf16[4,128,128]{2,1,0:T(8,128)(2,1)}, u32[]{:S(2)}) copy-start(bf16[4,128,128]{2,1,0:T(8,128)(2,1)} %get-tuple-element.66.refs_5_) | copy-start | bytes 393220
  66.4 27.3 %copy-start.3 = (f32[128,128]{1,0:T(8,128)S(1)}, f32[128,128]{1,0:T(8,128)}, u32[]{:S(2)}) copy-start(f32[128,128]{1,0:T(8,128)} %get-tuple-element.67.refs_6_) | copy-start | bytes 196612
  66.5 33.3 %copy-start.5 = (f32[1,9216]{1,0:T(1,128)S(1)}, f32[1,9216]{1,0:T(1,128)}, u32[]{:S(2)}) copy-start(f32[1,9216]{1,0:T(1,128)} %get-tuple-element.47.refs_12_) | copy-start | bytes 110596
  66.5 2.6 %collective-permute-start.20 = (bf16[128,128]{1,0:T(8,128)(2,1)S(1)}, bf16[128,128]{1,0:T(8,128)(2,1)S(1)}, u32[]{:S(2)}, u32[]{:S(2)}) collective-permute-start(bf16[128,128]{1,0:T(8,128)(2,1)S(1)} %get-tuple-element.61), channel_id=1, source_target_pairs={{0,2},{2,0},{4,6},{6,4},{1,3},{3,1},{5,7},{7,5},{8,10},{10,8},{12,... | collective-permute-start | bytes 98312 | tf_op jit(solution)/shard_map/ppermute | solution.py:37
  66.6 3.9 %collective-permute-start.21 = (bf16[128,128]{1,0:T(8,128)(2,1)S(1)}, bf16[128,128]{1,0:T(8,128)(2,1)S(1)}, u32[]{:S(2)}, u32[]{:S(2)}) collective-permute-start(bf16[128,128]{1,0:T(8,128)(2,1)S(1)} %get-tuple-element.62), channel_id=1, source_target_pairs={{0,4},{2,6},{4,0},{6,2},{1,5},{3,7},{5,1},{7,3},{8,12},{10,14},{12... | collective-permute-start | bytes 98312 | tf_op jit(solution)/shard_map/ppermute | solution.py:37
  67.6 3.4 %collective-permute-start.22 = (bf16[128,128]{1,0:T(8,128)(2,1)S(1)}, bf16[128,128]{1,0:T(8,128)(2,1)S(1)}, u32[]{:S(2)}, u32[]{:S(2)}) collective-permute-start(bf16[128,128]{1,0:T(8,128)(2,1)S(1)} %get-tuple-element.63), channel_id=1, source_target_pairs={{0,6},{2,4},{4,2},{6,0},{1,7},{3,5},{5,3},{7,1},{8,14},{10,12},{12... | collective-permute-start | bytes 98312 | tf_op jit(solution)/shard_map/ppermute | solution.py:37
  71.0 15.9 %collective-permute-start.25 = (bf16[2,128,64]{2,1,0:T(8,128)(2,1)S(1)}, bf16[2,128,64]{2,1,0:T(8,128)(2,1)S(1)}, u32[]{:S(2)}, u32[]{:S(2)}) collective-permute-start(bf16[2,128,64]{2,1,0:T(8,128)(2,1)S(1)} %get-tuple-element.71), channel_id=1, source_target_pairs={{0,2},{2,0},{4,6},{6,4},{1,3},{3,1},{5,7},{7,5},{8,10},{10,8},{12,... | collective-permute-start | bytes 98312 | tf_op jit(solution)/shard_map/ppermute | solution.py:916
  71.2 18.2 %collective-permute-start.23 = (bf16[160,64]{1,0:T(8,128)(2,1)S(1)}, bf16[160,64]{1,0:T(8,128)(2,1)S(1)}, u32[]{:S(2)}, u32[]{:S(2)}) collective-permute-start(bf16[160,64]{1,0:T(8,128)(2,1)S(1)} %get-tuple-element.64), channel_id=1, source_target_pairs={{0,8},{8,0},{16,24},{24,16},{1,9},{9,1},{17,25},{25,17},{2,10},{10... | collective-permute-start | bytes 61448 | tf_op jit(solution)/shard_map/ppermute | solution.py:917
  76.9 12.5 %collective-permute-start.24 = (bf16[128,64]{1,0:T(8,128)(2,1)S(1)}, bf16[128,64]{1,0:T(8,128)(2,1)S(1)}, u32[]{:S(2)}, u32[]{:S(2)}) collective-permute-start(bf16[128,64]{1,0:T(8,128)(2,1)S(1)} %get-tuple-element.59.refs_7_), channel_id=1, source_target_pairs={{0,16},{8,24},{16,0},{24,8},{1,17},{9,25},{17,1},{25,9},{2,18},{10... | collective-permute-start | bytes 49160 | tf_op jit(solution)/shard_map/ppermute | solution.py:900
  87.0 5.8 %collective-permute-start.26 = (bf16[128,64]{1,0:T(8,128)(2,1)S(1)}, bf16[128,64]{1,0:T(8,128)(2,1)S(1)}, u32[]{:S(2)}, u32[]{:S(2)}) collective-permute-start(bf16[128,64]{1,0:T(8,128)(2,1)S(1)} %get-tuple-element.72), channel_id=1, source_target_pairs={{0,8},{2,10},{4,12},{6,14},{8,16},{10,18},{12,20},{14,22},{16,24},... | collective-permute-start | bytes 49160 | tf_op jit(solution)/shard_map/ppermute | solution.py:920
  87.0 6.6 %collective-permute-start.27 = (bf16[128,64]{1,0:T(8,128)(2,1)S(1)}, bf16[128,64]{1,0:T(8,128)(2,1)S(1)}, u32[]{:S(2)}, u32[]{:S(2)}) collective-permute-start(bf16[128,64]{1,0:T(8,128)(2,1)S(1)} %get-tuple-element.73), channel_id=1, source_target_pairs={{0,12},{2,14},{4,8},{6,10},{8,20},{10,22},{12,16},{14,18},{16,28},... | collective-permute-start | bytes 49160 | tf_op jit(solution)/shard_map/ppermute | solution.py:920
  94.8 1.3 %collective-permute-start.32 = (bf16[5,64,128]{2,1,0:T(8,128)(2,1)S(1)}, bf16[5,64,128]{2,1,0:T(8,128)(2,1)S(1)}, u32[]{:S(2)}, u32[]{:S(2)}) collective-permute-start(bf16[5,64,128]{2,1,0:T(8,128)(2,1)S(1)} %get-tuple-element.75), channel_id=1, source_target_pairs={{0,2},{2,0},{4,6},{6,4},{1,3},{3,1},{5,7},{7,5},{8,10},{10,8},{12,... | collective-permute-start | bytes 245768 | tf_op jit(solution)/shard_map/ppermute | solution.py:956
  96.2 18.9 %collective-permute-start.33 = (bf16[5,64,128]{2,1,0:T(8,128)(2,1)S(1)}, bf16[5,64,128]{2,1,0:T(8,128)(2,1)S(1)}, u32[]{:S(2)}, u32[]{:S(2)}) collective-permute-start(bf16[5,64,128]{2,1,0:T(8,128)(2,1)S(1)} %add_convert_fusion.refs_8_), channel_id=1, source_target_pairs={{0,4},{1,5},{2,6},{3,7},{4,0},{5,1},{6,2},{7,3},{8,12},{9,13},{10,... | collective-permute-start | bytes 245768 | tf_op jit(solution)/shard_map/ppermute | solution.py:968
  97.3 17.7 %collective-permute-start.34 = (bf16[5,64,128]{2,1,0:T(8,128)(2,1)S(1)}, bf16[5,64,128]{2,1,0:T(8,128)(2,1)S(1)}, u32[]{:S(2)}, u32[]{:S(2)}) collective-permute-start(bf16[5,64,128]{2,1,0:T(8,128)(2,1)S(1)} %add_convert_fusion.refs_8_), channel_id=1, source_target_pairs={{0,1},{1,0},{2,3},{3,2},{4,5},{5,4},{6,7},{7,6},{8,9},{9,8},{10,11... | collective-permute-start | bytes 245768 | tf_op jit(solution)/shard_map/ppermute | solution.py:968
  98.8 16.3 %collective-permute-start.35 = (bf16[5,64,128]{2,1,0:T(8,128)(2,1)S(1)}, bf16[5,64,128]{2,1,0:T(8,128)(2,1)S(1)}, u32[]{:S(2)}, u32[]{:S(2)}) collective-permute-start(bf16[5,64,128]{2,1,0:T(8,128)(2,1)S(1)} %add_convert_fusion.refs_8_), channel_id=1, source_target_pairs={{0,5},{1,4},{2,7},{3,6},{4,1},{5,0},{6,3},{7,2},{8,13},{9,12},{10,... | collective-permute-start | bytes 245768 | tf_op jit(solution)/shard_map/ppermute | solution.py:968
  99.7 3.9 %collective-permute-start.28 = (bf16[128,64]{1,0:T(8,128)(2,1)S(1)}, bf16[128,64]{1,0:T(8,128)(2,1)S(1)}, u32[]{:S(2)}, u32[]{:S(2)}) collective-permute-start(bf16[128,64]{1,0:T(8,128)(2,1)S(1)} %get-tuple-element.74.refs_0_), channel_id=1, source_target_pairs={{0,8},{8,0},{16,24},{24,16},{1,9},{9,1},{17,25},{25,17},{2,10},{10... | collective-permute-start | bytes 49160 | tf_op jit(solution)/shard_map/ppermute | solution.py:952
  99.7 15.3 %collective-permute-start.31 = (f32[1,9216]{1,0:T(1,128)S(1)}, f32[1,9216]{1,0:T(1,128)S(1)}, u32[]{:S(2)}, u32[]{:S(2)}) collective-permute-start(f32[1,9216]{1,0:T(1,128)S(1)} %copy-done.5), channel_id=1, source_target_pairs={{0,1},{1,0},{2,3},{3,2},{4,5},{5,4},{6,7},{7,6},{8,9},{9,8},{10,11... | collective-permute-start | bytes 110600 | tf_op jit(solution)/shard_map/ppermute | solution.py:32
  103.6 5.0 %collective-permute-start.29 = (bf16[128,64]{1,0:T(8,128)(2,1)S(1)}, bf16[128,64]{1,0:T(8,128)(2,1)S(1)}, u32[]{:S(2)}, u32[]{:S(2)}) collective-permute-start(bf16[128,64]{1,0:T(8,128)(2,1)S(1)} %get-tuple-element.74.refs_0_), channel_id=1, source_target_pairs={{0,16},{8,24},{16,0},{24,8},{1,17},{9,25},{17,1},{25,9},{2,18},{10... | collective-permute-start | bytes 49160 | tf_op jit(solution)/shard_map/ppermute | solution.py:951
  108.6 5.7 %collective-permute-start.30 = (bf16[128,64]{1,0:T(8,128)(2,1)S(1)}, bf16[128,64]{1,0:T(8,128)(2,1)S(1)}, u32[]{:S(2)}, u32[]{:S(2)}) collective-permute-start(bf16[128,64]{1,0:T(8,128)(2,1)S(1)} %get-tuple-element.74.refs_0_), channel_id=1, source_target_pairs={{0,24},{8,16},{16,8},{24,0},{1,25},{9,17},{17,9},{25,1},{2,26},{10... | collective-permute-start | bytes 49160 | tf_op jit(solution)/shard_map/ppermute | solution.py:950

commit v10 on v9

--- a/solution.py
+++ b/solution.py
@@ -76,6 +76,10 @@
     return jnp.where(lax.axis_index("dp") == 0, *choices)
 
 
+def stacked_tile(heads_w, first):
+    return jnp.concatenate([head_tile(pieces, first, TILE) for pieces in heads_w], axis=0)
+
+
 def nested(refs, sizes):
     groups, first = [], 0
     for size in sizes:
@@ -209,8 +213,8 @@
     return -(-width // 2048) * 16
 
 
-def condition_kernel(fetches, packed_out, noisy_out, kind_out, held, mod_rows, arrivals):
-    times, text, time_w, clean_t, noise, mod_w, kind_w = fetches
+def condition_kernel(fetches, packed_out, noisy_out, kind_out, gram_out, held, mod_rows, arrivals):
+    times, text, time_w, clean_t, noise, embed_w, mod_w, kind_w = fetches
     model_width = held.shape[0]
     rows = model_width // STREAMS
     for fetch in fetches[:-2]:
@@ -243,20 +247,29 @@
             hidden[:, part * rows : (part + 1) * rows], held[part * rows : (part + 1) * rows]
         )
         total = piece if total is None else total + piece
-    sigma_student = noise_level(student_step)
-    clean_ref, noise_ref = clean_t.ready(), noise.ready()
-    noisy = (1.0 - sigma_student) * clean_ref[...].astype(jnp.float32).T + sigma_student * noise_ref[
-        :, : clean_ref.shape[0]
-    ].astype(jnp.float32)
-    noisy = noisy.astype(jnp.bfloat16)
-    noisy_out[...] = noisy
-    top = noisy.shape[0] // 2
-    packed_out[:top] = jnp.concatenate([noisy[:top], noisy[top:]], axis=1)
+        if part == STREAMS // 2:
+            sigma_student = noise_level(student_step)
+            clean_ref, noise_ref = clean_t.ready(), noise.ready()
+            noisy = (1.0 - sigma_student) * clean_ref[...].astype(jnp.float32).T + sigma_student * noise_ref[
+                :, : clean_ref.shape[0]
+            ].astype(jnp.float32)
+            noisy = noisy.astype(jnp.bfloat16)
+            noisy_out[...] = noisy
+            top = noisy.shape[0] // 2
+            packed_out[:top] = jnp.concatenate([noisy[:top], noisy[top:]], axis=1)
+            central_top, central_low = halves(centred(embed_w.ready()))
+            gram = (
+                dot32_t(central_top, central_top)
+                + dot32_t(central_top, central_low)
+                + dot32_t(central_low, central_top)
+            )
+            gram_out[0], gram_out[1] = halves(gram)
     width = total.shape[1]
     for row, first in enumerate(range(0, width, 128)):
         size = min(128, width - first)
         mod_rows[row : row + 1, :size] = total[:1, first : first + size]
     depth = mod_rows.shape[0]
+    top = noisy_out.shape[0] // 2
     packed_out[top : top + depth], packed_out[top + depth :] = halves(mod_rows[...])
     copies[STREAMS].wait()
 
@@ -277,9 +290,8 @@
     return values - jnp.mean(values, axis=1, keepdims=True)
 
 
-def front(rows, central, short, gains, head_outs, proj_ref, inverse_ref, key_ref, value_ref):
-    latent_width = central.shape[0]
-    model_width = central.shape[1]
+def front(rows, gram, model_width, short, gains, head_outs, proj_ref, inverse_ref, key_ref, value_ref):
+    latent_width = gram.shape[1]
     count = len(rows)
     head_width = gains.shape[2]
     scale = 1.0 / math.sqrt(head_width)
@@ -287,12 +299,9 @@
     short_top = None
     for place in range(count):
         block = rows[place][...]
-        squares = None
-        for first in range(0, model_width, TILE):
-            piece = dot32(block, central[:, first : first + TILE])
-            piece = lane_sum(piece * piece)
-            squares = piece if squares is None else squares + piece
-        inverse = lax.rsqrt(jnp.sum(squares, axis=1, keepdims=True) / model_width + EPS)
+        spanned = dot32(block, gram[0]) + dot32(block, gram[1])
+        squares = jnp.sum(spanned * block.astype(jnp.float32), axis=1, keepdims=True)
+        inverse = lax.rsqrt(jnp.maximum(squares, 0.0) / model_width + EPS)
         if short_top is None:
             values = short()
             short_top, short_low = halves(values[:latent_width])
@@ -324,7 +333,7 @@
             part_out[...] = near[:, place * width : (place + 1) * width]
 
 
-def student_front_kernel(count, width, fetches, embed_w, head_w, gains, *refs):
+def student_front_kernel(count, width, fetches, embed_w, head_w, gram, gains, *refs):
     packed = refs[:count]
     head_outs = refs[count : 2 * count]
     short_out, late_out, mod, rows_ref, sends, *kept = refs[2 * count :]
@@ -365,7 +374,8 @@
     def _():
         front(
             [rows_ref.at[place] for place in range(count)],
-            central.astype(jnp.bfloat16),
+            gram,
+            model_width,
             lambda: short,
             gains,
             head_outs,
@@ -375,7 +385,7 @@
     late.wait()
 
 
-def critic_front_kernel(count, fetches, short, embed_w, gains, *refs):
+def critic_front_kernel(count, model_width, fetches, short, gram, gains, *refs):
     rows = refs[:count]
     head_outs = refs[count : 2 * count]
     kept = refs[2 * count :]
@@ -384,7 +394,8 @@
     def _():
         front(
             rows,
-            centred(embed_w).astype(jnp.bfloat16),
+            gram,
+            model_width,
             lambda: short[...],
             gains,
             head_outs,
@@ -395,13 +406,11 @@
 def tail(late, latent, embed_w, final_t, mixed, heads_w, work):
     model_width = embed_w.shape[2]
     block = latent[...]
+    joined_heads = jnp.concatenate([piece[...] for piece in mixed], axis=1)
     sums = None
     for first in range(0, model_width, TILE):
         span = slice(first, first + TILE)
-        attended = None
-        for piece, rows_w in zip(mixed, heads_w):
-            product = dot32(piece[...], head_tile(rows_w, first, TILE))
-            attended = product if attended is None else attended + product
+        attended = dot32(joined_heads, stacked_tile(heads_w, first))
         mod = late.ready()
         residual = (
             dot32(block, embed_w[0, :, span]) + slot_of(mod, 0, model_width, first, TILE) * attended
@@ -534,7 +543,7 @@
             plain = jnp.sum(plain, axis=1, keepdims=True) / model_width
             along = jnp.sum(along, axis=1, keepdims=True) / model_width
             direct = None
-            totals = [None] * count
+            totals = None
             for first in range(0, model_width, TILE):
                 span = slice(first, first + TILE)
                 grad_residual = inverse * (other[:, span] - plain - work[:, span] * along)
@@ -544,23 +553,14 @@
                 grad_attended = (slot_of(mod, 0, model_width, first, TILE) * grad_residual).astype(
                     jnp.bfloat16
                 )
-                for place in range(count):
-                    product = dot32_t(grad_attended, head_tile(heads_w[place], first, TILE))
-                    held = totals[place]
-                    totals[place] = product if held is None else held + product
+                product = dot32_t(grad_attended, stacked_tile(heads_w, first))
+                totals = product if totals is None else totals + product
             direct_ref[...] = direct
+            width = totals.shape[1] // count
             for place in range(count):
-                grads[place][...] = totals[place].astype(jnp.bfloat16)
-
-
-def gram_kernel(fetches, embed_w, gram_ref):
-    central_top, central_low = halves(centred(embed_w))
-    gram = (
-        dot32_t(central_top, central_top)
-        + dot32_t(central_top, central_low)
-        + dot32_t(central_low, central_top)
-    )
-    gram_ref[0], gram_ref[1] = halves(gram)
+                grads[place][...] = totals[:, place * width : (place + 1) * width].astype(
+                    jnp.bfloat16
+                )
 
 
 def judge_back_kernel(count, model_width, fetches, short_in, gram, gains, proj_ref, inverse_ref, key_ref, value_ref, term, *refs):
@@ -741,14 +741,13 @@
                 2 * group + 1
             ][...].astype(jnp.float32)
         near_top = joined[count].astype(jnp.bfloat16)
-        heads = [joined[place ^ offset].astype(jnp.bfloat16) for offset in range(count)]
+        heads = jnp.concatenate(
+            [joined[place ^ offset].astype(jnp.bfloat16) for offset in range(count)], axis=1
+        )
         averages = None
         for first in range(0, model_width, TILE):
             span = slice(first, first + TILE)
-            spread = None
-            for head, rows_w in zip(heads, heads_w):
-                product = dot32(head, head_tile(rows_w, first, TILE))
-                spread = product if spread is None else spread + product
+            spread = dot32(heads, stacked_tile(heads_w, first))
             near = dot32(near_top[:, :latent_width], embed_w[0, :, span])
             mods = [late.ready(), *other_mods]
             gates = jnp.concatenate(
@@ -805,12 +804,13 @@
     heads_w = sum(heads_w, [])
 
     depth = packed_rows(mod_width)
-    packed, noisy_student, kind_w = run(
+    packed, noisy_student, kind_w, gram = run(
         condition_kernel,
         [
             array((tok_rows // 2 + 2 * depth, 2 * latent_width), bf16),
             array((tok_rows, latent_width), bf16),
             pltpu.VMEM(kind_w.shape, bf16),
+            array((2, latent_width, latent_width), bf16),
         ],
         (),
         2 * model_width * mod_width,
@@ -819,7 +819,7 @@
             pltpu.VMEM((depth, 128), f32),
             pltpu.SemaphoreType.DMA((STREAMS + 1,)),
         ),
-        fetched=(timesteps, text_vec, w_time[0], jnp.transpose(clean[0]), noise[0]),
+        fetched=(timesteps, text_vec, w_time[0], jnp.transpose(clean[0]), noise[0], w_embed),
         streamed=(w_mod[0], kind_w),
     )
     kind_w = pltpu.with_memory_space_constraint(kind_w, pltpu.VMEM)
@@ -836,7 +836,7 @@
     *head_outs, short, late_mod = run(
         functools.partial(student_front_kernel, count, mod_width),
         head_blocks + [pltpu.VMEM(*short_shape)],
-        (w_embed, kind_w, qk_gain, *packed_all),
+        (w_embed, kind_w, gram, qk_gain, *packed_all),
         4 * latent_width * model_width * 3 * head_width,
         scratch=[
             pltpu.VMEM((1, 5 * model_width), f32),
@@ -875,11 +875,11 @@
     )
     critic_rows = gather_near(own_rows, "seq", count)
     *head_outs, proj, inverse, keys, values = run(
-        functools.partial(critic_front_kernel, count),
+        functools.partial(critic_front_kernel, count, model_width),
         head_blocks + [array(shape, kind) for shape, kind in stored],
         (
             pltpu.with_memory_space_constraint(short, pltpu.VMEM),
-            w_embed,
+            gram,
             qk_gain,
             *critic_rows,
         ),
@@ -900,12 +900,6 @@
     fake = lax.ppermute(term_rows, "segment", swaps(sections, 2))
     half = count // 2
     rows_shape = array((half, tok_rows, latent_width), bf16)
-    (gram,) = run(
-        gram_kernel,
-        [array((2, latent_width, latent_width), bf16)],
-        (w_embed,),
-        6 * latent_width * latent_width * model_width,
-    )
     keep, away, real = run(
         functools.partial(judge_back_kernel, count, model_width),
         [rows_shape, rows_shape, array((tok_rows + 32, latent_width), bf16)],

time: 119 us -> 116 us (0.975)
  Pallas kernels: 22.8 us -> 20.8 us
    pallas_call x13 -> x12, Pallas kernels: 22.8 us -> 20.8 us  [run(): pl.pallas_call(body, out_shape=list(outputs) + [pltpu.HBM(item.shape, ite...]
  transfers between devices with their start and end apart: 36 -> 36, of which waited for: 22 -> 22; matrix products, arithmetic and copies ran while one was open for 0% -> 0% of each run, Pallas kernels for 13% -> 12%
where the time goes in v10:
time: 116 us
  waiting for transfers between devices  51.7 us (45%)
  starting transfers between devices  41.4 us (36%)
  Pallas kernels  20.8 us (18%)
    pallas_call x12, Pallas kernels, run(): pl.pallas_call(body, out_shape=list(outputs) + [pltpu.HBM(item.shape, ite...  20.8 us
    ppermute x1, waiting for transfers between devices, spread_heads(): near = lax.ppermute(part, 'seq', swaps(count, bit))  11.9 us
    ppermute x1, starting transfers between devices, step(): fake = lax.ppermute(term_rows, 'segment', swaps(sections, 2))  10.1 us
    ppermute x9, waiting for transfers between devices, scatter_near(): lax.ppermute(blocks[offset], axis, swaps(count, offset))  8.42 us
    ppermute x7, starting transfers between devices, gather_near(): lax.ppermute(value, axis, swaps(count, offset))  6.25 us
    ppermute x1, waiting for transfers between devices, spread_heads(): held[bit] = [near, lax.ppermute(stage(near), 'dp', swaps(groups, 1))]  5.76 us
    ppermute x9, starting transfers between devices, scatter_near(): lax.ppermute(blocks[offset], axis, swaps(count, offset))  5.45 us
    ppermute x7, waiting for transfers between devices, gather_near(): lax.ppermute(value, axis, swaps(count, offset))  5.37 us
  transfers between devices with their start and end apart: 36, of which 22 were waited for; matrix products, arithmetic and copies ran while one was open for 0% of the time, Pallas kernels for 12%

profile of v10, /device:TPU:0, one launch (start us, length us, event | category | flops | bytes accessed | tf_op | source)
XLA Modules:
  0.0 116.1 jit_solution(11007642870390723375)
XLA Ops:
  0.6 1.1 dynamic-slice_bitcast_fusion
  1.7 3.1 %collective-permute-start.7 = (bf16[128,2048]{1,0:T(8,128)(2,1)S(1)}, bf16[128,2048]{1,0:T(8,128)(2,1)S(1)}, u32[]{:S(2)}, u32[]{:S(2)}) collective-permute-start(bf16[128,2048]{1,0:T(8,128)(2,1)S(1)} %dynamic-slice_bitcast_fusion), channel_id=1, source_target_pairs={{0,4},{2,6},{4,0},{6,2},{1,5},{3,7},{5,1},{7,3},{8,12},{10,14},{12... | collective-permute-start | bytes 1572872 | tf_op jit(solution)/shard_map/ppermute | solution.py:52
  4.8 0.0 collective-permute-start.6
  4.8 11.9 %collective-permute-done.7.refs_0_.refs_8_.refs_3_ = bf16[128,2048]{1,0:T(8,128)(2,1)S(1)} collective-permute-done((bf16[128,2048]{1,0:T(8,128)(2,1)S(1)}, bf16[128,2048]{1,0:T(8,128)(2,1)S(1)}, u32[]{:S(2)}, u32[]{:S(2)}) %collective-permute-start.7) | collective-permute-done | bytes 524320 | tf_op jit(solution)/shard_map/ppermute | solution.py:52
  16.7 1.8 %collective-permute-start.8 = (bf16[128,1024]{1,0:T(8,128)(2,1)S(1)}, bf16[128,1024]{1,0:T(8,128)(2,1)S(1)}, u32[]{:S(2)}, u32[]{:S(2)}) collective-permute-start(bf16[128,1024]{1,0:T(8,128)(2,1)S(1)} %shard_map.124), channel_id=1, source_target_pairs={{0,1},{1,0},{2,3},{3,2},{4,5},{5,4},{6,7},{7,6},{8,9},{9,8},{10,11... | collective-permute-start | bytes 786440 | tf_op jit(solution)/shard_map/ppermute | solution.py:53
  18.5 5.8 %collective-permute-done.8.refs_9_.refs_4_ = bf16[128,1024]{1,0:T(8,128)(2,1)S(1)} collective-permute-done((bf16[128,1024]{1,0:T(8,128)(2,1)S(1)}, bf16[128,1024]{1,0:T(8,128)(2,1)S(1)}, u32[]{:S(2)}, u32[]{:S(2)}) %collective-permute-start.8) | collective-permute-done | bytes 262176 | tf_op jit(solution)/shard_map/ppermute | solution.py:53
  24.3 0.0 collective-permute-start.10
  24.3 10.5 %shard_map.122 = (bf16[128,128]{1,0:T(8,128)(2,1)S(1)}, bf16[128,64]{1,0:T(8,128)(2,1)S(1)}, bf16[3,3072,128]{2,1,0:T(8,128)(2,1)S(1)}, bf16[2,64,64]{2,1,0:T(8,128)(2,1)S(1)}) custom-call(s32[2,2]{1,0:T(2,128)} %refs_14_.1, f32[1,256]{1,0:T(1,128)} %refs_1_.3, bf16[256,3072]{1,0:T(8,128)(2,1)} %bitcast.27, bf16[64,128]{1,0:T(8,128)(2,1)} %bitcast.35, ...), custom_call_target="tpu_custom_call" | custom-call | flops 23592960 | bytes 4441104 | tf_op jit(solution)/shard_map/pallas_call | solution.py:191
  34.8 0.0 copy-start
  34.8 0.6 collective-permute-start
  35.4 1.5 %collective-permute-start.1 = (bf16[128,128]{1,0:T(8,128)(2,1)S(1)}, bf16[128,128]{1,0:T(8,128)(2,1)S(1)}, u32[]{:S(2)}, u32[]{:S(2)}) collective-permute-start(bf16[128,128]{1,0:T(8,128)(2,1)S(1)} %get-tuple-element.42.refs_4_), channel_id=1, source_target_pairs={{0,4},{2,6},{4,0},{6,2},{1,5},{3,7},{5,1},{7,3},{8,12},{10,14},{12... | collective-permute-start | bytes 98312 | tf_op jit(solution)/shard_map/ppermute | solution.py:32
  36.8 0.8 collective-permute-start.2
  37.6 1.6 %collective-permute-done.1.refs_6_ = bf16[128,128]{1,0:T(8,128)(2,1)S(1)} collective-permute-done((bf16[128,128]{1,0:T(8,128)(2,1)S(1)}, bf16[128,128]{1,0:T(8,128)(2,1)S(1)}, u32[]{:S(2)}, u32[]{:S(2)}) %collective-permute-start.1) | collective-permute-done | bytes 32800 | tf_op jit(solution)/shard_map/ppermute | solution.py:32
  39.3 1.2 %collective-permute-done.2.refs_7_ = bf16[128,128]{1,0:T(8,128)(2,1)S(1)} collective-permute-done((bf16[128,128]{1,0:T(8,128)(2,1)S(1)}, bf16[128,128]{1,0:T(8,128)(2,1)S(1)}, u32[]{:S(2)}, u32[]{:S(2)}) %collective-permute-start.2) | collective-permute-done | bytes 32800 | tf_op jit(solution)/shard_map/ppermute | solution.py:32
  40.5 2.9 %shard_map.123 = (bf16[128,128]{1,0:T(8,128)(2,1)S(1)}, bf16[128,128]{1,0:T(8,128)(2,1)S(1)}, bf16[128,128]{1,0:T(8,128)(2,1)S(1)}, bf16[128,128]{1,0:T(8,128)(2...) custom-call(bf16[1,64,3072]{2,1,0:T(8,128)(2,1)S(1)} %copy-done.1, ...), custom_call_target="tpu_custom_call" | custom-call | flops 301989888 | bytes 3154944 | tf_op jit(solution)/shard_map/pallas_call | solution.py:191
  43.4 0.2 collective-permute-start.3
  43.6 0.8 collective-permute-start.4
  44.3 0.3 collective-permute-done.3.refs_3_
  44.7 0.7 collective-permute-start.5
  45.3 2.1 %collective-permute-done.4.refs_4_ = bf16[128,128]{1,0:T(8,128)(2,1)S(1)} collective-permute-done((bf16[128,128]{1,0:T(8,128)(2,1)S(1)}, bf16[128,128]{1,0:T(8,128)(2,1)S(1)}, u32[]{:S(2)}, u32[]{:S(2)}) %collective-permute-start.4) | collective-permute-done | bytes 32800 | tf_op jit(solution)/shard_map/ppermute | solution.py:37
  47.5 0.5 collective-permute-done.5.refs_5_
  48.0 0.0 collective-permute-done.6.refs_7_.refs_2_
  48.0 2.7 %shard_map.125 = (bf16[128,128]{1,0:T(8,128)(2,1)S(1)}, bf16[4,128,128]{2,1,0:T(8,128)(2,1)}, f32[128,128]{1,0:T(8,128)}) custom-call(bf16[128,64]{1,0:T(8,128)(2,1)S(1)} %get-tuple-element.44.refs_0_.refs_3_, bf16[1,64,3072]{2,1,0:T(8,128)(2,1)S(1)} %copy-done.1, bf16[128,128]{1,0:T(8,128)(2,1)S(1)} %get-tuple-element.45.refs_2_, ...), custom_call_target="tpu_custom_call" | custom-call | flops 402653184 | bytes 4182032 | tf_op jit(solution)/shard_map/pallas_call | solution.py:191
  50.8 1.3 %collective-permute-start.11 = (bf16[128,128]{1,0:T(8,128)(2,1)S(1)}, bf16[128,128]{1,0:T(8,128)(2,1)S(1)}, u32[]{:S(2)}, u32[]{:S(2)}) collective-permute-start(bf16[128,128]{1,0:T(8,128)(2,1)S(1)} %get-tuple-element.50.refs_0_), channel_id=1, source_target_pairs={{0,8},{1,9},{2,10},{3,11},{4,12},{5,13},{6,14},{7,15}} | collective-permute-start | bytes 98312 | tf_op jit(solution)/shard_map/ppermute | solution.py:866
  52.1 1.3 %collective-permute-start.12 = (bf16[128,128]{1,0:T(8,128)(2,1)S(1)}, bf16[128,128]{1,0:T(8,128)(2,1)S(1)}, u32[]{:S(2)}, u32[]{:S(2)}) collective-permute-start(bf16[128,128]{1,0:T(8,128)(2,1)S(1)} %get-tuple-element.50.refs_0_), channel_id=1, source_target_pairs={{0,16},{1,17},{2,18},{3,19},{4,20},{5,21},{6,22},{7,23}} | collective-permute-start | bytes 98312 | tf_op jit(solution)/shard_map/ppermute | solution.py:866
  53.4 1.3 %collective-permute-start.13 = (bf16[128,128]{1,0:T(8,128)(2,1)S(1)}, bf16[128,128]{1,0:T(8,128)(2,1)S(1)}, u32[]{:S(2)}, u32[]{:S(2)}) collective-permute-start(bf16[128,128]{1,0:T(8,128)(2,1)S(1)} %get-tuple-element.50.refs_0_), channel_id=1, source_target_pairs={{0,24},{1,25},{2,26},{3,27},{4,28},{5,29},{6,30},{7,31}} | collective-permute-start | bytes 98312 | tf_op jit(solution)/shard_map/ppermute | solution.py:866
  54.7 0.3 collective-permute-done.12.refs_2_
  54.9 1.3 %collective-permute-done.13.refs_3_ = bf16[128,128]{1,0:T(8,128)(2,1)S(1)} collective-permute-done((bf16[128,128]{1,0:T(8,128)(2,1)S(1)}, bf16[128,128]{1,0:T(8,128)(2,1)S(1)}, u32[]{:S(2)}, u32[]{:S(2)}) %collective-permute-start.13) | collective-permute-done | bytes 32800 | tf_op jit(solution)/shard_map/ppermute | solution.py:866
  56.3 0.1 collective-permute-start.14
  56.4 1.0 collective-permute-start.15
  57.3 0.9 collective-permute-start.16
  58.2 2.1 %collective-permute-done.15.refs_5_.refs_10_ = bf16[128,64]{1,0:T(8,128)(2,1)S(1)} collective-permute-done((bf16[128,64]{1,0:T(8,128)(2,1)S(1)}, bf16[128,64]{1,0:T(8,128)(2,1)S(1)}, u32[]{:S(2)}, u32[]{:S(2)}) %collective-permute-start.15) | collective-permute-done | bytes 16416 | tf_op jit(solution)/shard_map/ppermute | solution.py:32
  60.3 0.4 collective-permute-done.16.refs_6_.refs_11_
  60.7 0.2 collective-permute-start.17
  60.9 1.1 collective-permute-start.18
  62.0 0.6 collective-permute-start.19
  62.7 2.2 %collective-permute-done.18.refs_4_.refs_10_ = bf16[128,128]{1,0:T(8,128)(2,1)S(1)} collective-permute-done((bf16[128,128]{1,0:T(8,128)(2,1)S(1)}, bf16[128,128]{1,0:T(8,128)(2,1)S(1)}, u32[]{:S(2)}, u32[]{:S(2)}) %collective-permute-start.18) | collective-permute-done | bytes 32800 | tf_op jit(solution)/shard_map/ppermute | solution.py:37
  64.9 0.6 collective-permute-done.19.refs_5_.refs_11_
  65.5 0.2 collective-permute-start.20
  65.7 0.9 collective-permute-start.21
  66.6 0.8 collective-permute-start.22
  67.5 2.2 %collective-permute-done.21.refs_14_ = bf16[128,128]{1,0:T(8,128)(2,1)S(1)} collective-permute-done((bf16[128,128]{1,0:T(8,128)(2,1)S(1)}, bf16[128,128]{1,0:T(8,128)(2,1)S(1)}, u32[]{:S(2)}, u32[]{:S(2)}) %collective-permute-start.21) | collective-permute-done | bytes 32800 | tf_op jit(solution)/shard_map/ppermute | solution.py:37
  69.6 0.4 collective-permute-done.22.refs_15_
  70.1 0.2 collective-permute-start.25
  70.2 4.7 %collective-permute-start.23 = (bf16[160,64]{1,0:T(8,128)(2,1)S(1)}, bf16[160,64]{1,0:T(8,128)(2,1)S(1)}, u32[]{:S(2)}, u32[]{:S(2)}) collective-permute-start(bf16[160,64]{1,0:T(8,128)(2,1)S(1)} %get-tuple-element.66), channel_id=1, source_target_pairs={{0,8},{8,0},{16,24},{24,16},{1,9},{9,1},{17,25},{25,17},{2,10},{10... | collective-permute-start | bytes 61448 | tf_op jit(solution)/shard_map/ppermute | solution.py:911
  74.9 10.1 %collective-permute-start.24 = (bf16[128,64]{1,0:T(8,128)(2,1)S(1)}, bf16[128,64]{1,0:T(8,128)(2,1)S(1)}, u32[]{:S(2)}, u32[]{:S(2)}) collective-permute-start(bf16[128,64]{1,0:T(8,128)(2,1)S(1)} %get-tuple-element.61.refs_7_), channel_id=1, source_target_pairs={{0,16},{8,24},{16,0},{24,8},{1,17},{9,25},{17,1},{25,9},{2,18},{10... | collective-permute-start | bytes 49160 | tf_op jit(solution)/shard_map/ppermute | solution.py:900
  85.0 0.1 collective-permute-start.26
  85.1 1.1 collective-permute-start.27
  86.2 1.3 %collective-permute-done.24.refs_1_ = bf16[128,64]{1,0:T(8,128)(2,1)S(1)} collective-permute-done((bf16[128,64]{1,0:T(8,128)(2,1)S(1)}, bf16[128,64]{1,0:T(8,128)(2,1)S(1)}, u32[]{:S(2)}, u32[]{:S(2)}) %collective-permute-start.24) | collective-permute-done | bytes 16416 | tf_op jit(solution)/shard_map/ppermute | solution.py:900
  87.5 3.3 %collective-permute-done.26.refs_12_ = bf16[128,64]{1,0:T(8,128)(2,1)S(1)} collective-permute-done((bf16[128,64]{1,0:T(8,128)(2,1)S(1)}, bf16[128,64]{1,0:T(8,128)(2,1)S(1)}, u32[]{:S(2)}, u32[]{:S(2)}) %collective-permute-start.26) | collective-permute-done | bytes 16416 | tf_op jit(solution)/shard_map/ppermute | solution.py:914
  90.8 1.0 collective-permute-done.27.refs_13_
  91.8 1.1 shard_map.131
  92.9 0.1 collective-permute-start.32
  93.0 1.3 %collective-permute-done.32 = bf16[5,64,128]{2,1,0:T(8,128)(2,1)S(1)} collective-permute-done((bf16[5,64,128]{2,1,0:T(8,128)(2,1)S(1)}, bf16[5,64,128]{2,1,0:T(8,128)(2,1)S(1)}, u32[]{:S(2)}, u32[]{:S(2)}) %collective-permute-start.32) | collective-permute-done | bytes 81952 | tf_op jit(solution)/shard_map/ppermute | solution.py:950
  94.3 1.2 %collective-permute-start.33 = (bf16[5,64,128]{2,1,0:T(8,128)(2,1)S(1)}, bf16[5,64,128]{2,1,0:T(8,128)(2,1)S(1)}, u32[]{:S(2)}, u32[]{:S(2)}) collective-permute-start(bf16[5,64,128]{2,1,0:T(8,128)(2,1)S(1)} %add_convert_fusion.refs_8_), channel_id=1, source_target_pairs={{0,4},{1,5},{2,6},{3,7},{4,0},{5,1},{6,2},{7,3},{8,12},{9,13},{10,... | collective-permute-start | bytes 245768 | tf_op jit(solution)/shard_map/ppermute | solution.py:962
  95.4 1.5 %collective-permute-start.34 = (bf16[5,64,128]{2,1,0:T(8,128)(2,1)S(1)}, bf16[5,64,128]{2,1,0:T(8,128)(2,1)S(1)}, u32[]{:S(2)}, u32[]{:S(2)}) collective-permute-start(bf16[5,64,128]{2,1,0:T(8,128)(2,1)S(1)} %add_convert_fusion.refs_8_), channel_id=1, source_target_pairs={{0,1},{1,0},{2,3},{3,2},{4,5},{5,4},{6,7},{7,6},{8,9},{9,8},{10,11... | collective-permute-start | bytes 245768 | tf_op jit(solution)/shard_map/ppermute | solution.py:962
  96.9 0.9 collective-permute-start.35
  97.8 1.5 %collective-permute-start.31 = (f32[1,9216]{1,0:T(1,128)S(1)}, f32[1,9216]{1,0:T(1,128)S(1)}, u32[]{:S(2)}, u32[]{:S(2)}) collective-permute-start(f32[1,9216]{1,0:T(1,128)S(1)} %copy-done.5), channel_id=1, source_target_pairs={{0,1},{1,0},{2,3},{3,2},{4,5},{5,4},{6,7},{7,6},{8,9},{9,8},{10,11... | collective-permute-start | bytes 110600 | tf_op jit(solution)/shard_map/ppermute | solution.py:32
  99.3 2.4 %collective-permute-done.28.refs_1_ = bf16[128,64]{1,0:T(8,128)(2,1)S(1)} collective-permute-done((bf16[128,64]{1,0:T(8,128)(2,1)S(1)}, bf16[128,64]{1,0:T(8,128)(2,1)S(1)}, u32[]{:S(2)}, u32[]{:S(2)}) %collective-permute-start.28) | collective-permute-done | bytes 16416 | tf_op jit(solution)/shard_map/ppermute | solution.py:946
  101.7 5.0 %collective-permute-done.29.refs_2_ = bf16[128,64]{1,0:T(8,128)(2,1)S(1)} collective-permute-done((bf16[128,64]{1,0:T(8,128)(2,1)S(1)}, bf16[128,64]{1,0:T(8,128)(2,1)S(1)}, u32[]{:S(2)}, u32[]{:S(2)}) %collective-permute-start.29) | collective-permute-done | bytes 16416 | tf_op jit(solution)/shard_map/ppermute | solution.py:945
  106.7 1.2 %collective-permute-start.30 = (bf16[128,64]{1,0:T(8,128)(2,1)S(1)}, bf16[128,64]{1,0:T(8,128)(2,1)S(1)}, u32[]{:S(2)}, u32[]{:S(2)}) collective-permute-start(bf16[128,64]{1,0:T(8,128)(2,1)S(1)} %get-tuple-element.76.refs_0_), channel_id=1, source_target_pairs={{0,24},{8,16},{16,8},{24,0},{1,25},{9,17},{17,9},{25,1},{2,26},{10... | collective-permute-start | bytes 49160 | tf_op jit(solution)/shard_map/ppermute | solution.py:944
  107.9 4.5 %collective-permute-done.30.refs_3_ = bf16[128,64]{1,0:T(8,128)(2,1)S(1)} collective-permute-done((bf16[128,64]{1,0:T(8,128)(2,1)S(1)}, bf16[128,64]{1,0:T(8,128)(2,1)S(1)}, u32[]{:S(2)}, u32[]{:S(2)}) %collective-permute-start.30) | collective-permute-done | bytes 16416 | tf_op jit(solution)/shard_map/ppermute | solution.py:944
  112.4 0.7 shard_map.132
  113.2 2.8 %shard_map.133 = f32[64,3072]{1,0:T(8,128)} custom-call(bf16[1,64,3072]{2,1,0:T(8,128)(2,1)S(1)} %copy-done.1, bf16[128,3072]{1,0:T(8,128)(2,1)S(1)} %bitcast.24, bf16[128,3072]{1,0:T(8,128)(2,1)S(1)} %collective-permute-done.6.refs_7_.refs_2_, bf16[128,2048]{1,0:T(8,128)(2,1)S(1)} %collective-permute-done.7.refs_0_.refs_8_.refs_3_, ...), custom_call_target="tpu_custom_call" | custom-call | flops 805306368 | bytes 4726784 | tf_op jit(solution)/shard_map/pallas_call | solution.py:191
  (34 shorter events, 0.2 us)
Async XLA Ops:
  1.7 15.0 %collective-permute-start.7 = (bf16[128,2048]{1,0:T(8,128)(2,1)S(1)}, bf16[128,2048]{1,0:T(8,128)(2,1)S(1)}, u32[]{:S(2)}, u32[]{:S(2)}) collective-permute-start(bf16[128,2048]{1,0:T(8,128)(2,1)S(1)} %dynamic-slice_bitcast_fusion), channel_id=1, source_target_pairs={{0,4},{2,6},{4,0},{6,2},{1,5},{3,7},{5,1},{7,3},{8,12},{10,14},{12... | collective-permute-start | bytes 1572872 | tf_op jit(solution)/shard_map/ppermute | solution.py:52
  4.8 43.2 %collective-permute-start.6 = (bf16[128,3072]{1,0:T(8,128)(2,1)}, bf16[128,3072]{1,0:T(8,128)(2,1)S(1)}, u32[]{:S(2)}, u32[]{:S(2)}) collective-permute-start(bf16[128,3072]{1,0:T(8,128)(2,1)} %bitcast.21), channel_id=1, source_target_pairs={{0,2},{2,0},{4,6},{6,4},{1,3},{3,1},{5,7},{7,5},{8,10},{10,8},{12,... | collective-permute-start | bytes 2359304 | tf_op jit(solution)/shard_map/ppermute | solution.py:56
  16.7 7.5 %collective-permute-start.8 = (bf16[128,1024]{1,0:T(8,128)(2,1)S(1)}, bf16[128,1024]{1,0:T(8,128)(2,1)S(1)}, u32[]{:S(2)}, u32[]{:S(2)}) collective-permute-start(bf16[128,1024]{1,0:T(8,128)(2,1)S(1)} %shard_map.124), channel_id=1, source_target_pairs={{0,1},{1,0},{2,3},{3,2},{4,5},{5,4},{6,7},{7,6},{8,9},{9,8},{10,11... | collective-permute-start | bytes 786440 | tf_op jit(solution)/shard_map/ppermute | solution.py:53
  18.5 29.5 %collective-permute-start.9 = (bf16[128,2048]{1,0:T(8,128)(2,1)S(1)}, bf16[128,2048]{1,0:T(8,128)(2,1)S(1)}, u32[]{:S(2)}, u32[]{:S(2)}) collective-permute-start(bf16[128,2048]{1,0:T(8,128)(2,1)S(1)} %collective-permute-done.7.refs_0_.refs_8_.refs_3_), channel_id=1, source_target_pairs={{0,2},{2,0},{4,6},{6,4},{1,3},{3,1},{5,7},{7,5},{8,10},{10,8},{12,... | collective-permute-start | bytes 1572872 | tf_op jit(solution)/shard_map/ppermute | solution.py:56
  24.3 23.8 %collective-permute-start.10 = (bf16[128,1024]{1,0:T(8,128)(2,1)S(1)}, bf16[128,1024]{1,0:T(8,128)(2,1)S(1)}, u32[]{:S(2)}, u32[]{:S(2)}) collective-permute-start(bf16[128,1024]{1,0:T(8,128)(2,1)S(1)} %collective-permute-done.8.refs_9_.refs_4_), channel_id=1, source_target_pairs={{0,2},{2,0},{4,6},{6,4},{1,3},{3,1},{5,7},{7,5},{8,10},{10,8},{12,... | collective-permute-start | bytes 786440 | tf_op jit(solution)/shard_map/ppermute | solution.py:56
  24.3 16.2 %copy-start.1 = (bf16[1,64,3072]{2,1,0:T(8,128)(2,1)S(1)}, bf16[1,64,3072]{2,1,0:T(8,128)(2,1)}, u32[]{:S(2)}) copy-start(bf16[1,64,3072]{2,1,0:T(8,128)(2,1)} %refs_0_.5) | copy-start | bytes 1179652
  24.3 16.2 %copy-start.4 = (f32[1,2,128]{2,1,0:T(2,128)S(1)}, f32[1,2,128]{2,1,0:T(2,128)}, u32[]{:S(2)}) copy-start(f32[1,2,128]{2,1,0:T(2,128)} %refs_2_.3) | copy-start | bytes 3076
  34.8 13.2 %copy-start = (bf16[1,1,128,3072]{3,2,1,0:T(8,128)(2,1)S(1)}, bf16[1,1,128,3072]{3,2,1,0:T(8,128)(2,1)}, u32[]{:S(2)}) copy-start(bf16[1,1,128,3072]{3,2,1,0:T(8,128)(2,1)} %param.19) | copy-start | bytes 2359300
  34.8 2.0 %collective-permute-start = (bf16[128,128]{1,0:T(8,128)(2,1)S(1)}, bf16[128,128]{1,0:T(8,128)(2,1)S(1)}, u32[]{:S(2)}, u32[]{:S(2)}) collective-permute-start(bf16[128,128]{1,0:T(8,128)(2,1)S(1)} %get-tuple-element.42.refs_4_), channel_id=1, source_target_pairs={{0,2},{2,0},{4,6},{6,4},{1,3},{3,1},{5,7},{7,5},{8,10},{10,8},{12,... | collective-permute-start | bytes 98312 | tf_op jit(solution)/shard_map/ppermute | solution.py:32
  35.4 3.9 %collective-permute-start.1 = (bf16[128,128]{1,0:T(8,128)(2,1)S(1)}, bf16[128,128]{1,0:T(8,128)(2,1)S(1)}, u32[]{:S(2)}, u32[]{:S(2)}) collective-permute-start(bf16[128,128]{1,0:T(8,128)(2,1)S(1)} %get-tuple-element.42.refs_4_), channel_id=1, source_target_pairs={{0,4},{2,6},{4,0},{6,2},{1,5},{3,7},{5,1},{7,3},{8,12},{10,14},{12... | collective-permute-start | bytes 98312 | tf_op jit(solution)/shard_map/ppermute | solution.py:32
  36.8 3.7 %collective-permute-start.2 = (bf16[128,128]{1,0:T(8,128)(2,1)S(1)}, bf16[128,128]{1,0:T(8,128)(2,1)S(1)}, u32[]{:S(2)}, u32[]{:S(2)}) collective-permute-start(bf16[128,128]{1,0:T(8,128)(2,1)S(1)} %get-tuple-element.42.refs_4_), channel_id=1, source_target_pairs={{0,6},{2,4},{4,2},{6,0},{1,7},{3,5},{5,3},{7,1},{8,14},{10,12},{12... | collective-permute-start | bytes 98312 | tf_op jit(solution)/shard_map/ppermute | solution.py:32
  43.4 1.3 %collective-permute-start.3 = (bf16[128,128]{1,0:T(8,128)(2,1)S(1)}, bf16[128,128]{1,0:T(8,128)(2,1)S(1)}, u32[]{:S(2)}, u32[]{:S(2)}) collective-permute-start(bf16[128,128]{1,0:T(8,128)(2,1)S(1)} %get-tuple-element.46), channel_id=1, source_target_pairs={{0,2},{2,0},{4,6},{6,4},{1,3},{3,1},{5,7},{7,5},{8,10},{10,8},{12,... | collective-permute-start | bytes 98312 | tf_op jit(solution)/shard_map/ppermute | solution.py:37
  43.6 3.9 %collective-permute-start.4 = (bf16[128,128]{1,0:T(8,128)(2,1)S(1)}, bf16[128,128]{1,0:T(8,128)(2,1)S(1)}, u32[]{:S(2)}, u32[]{:S(2)}) collective-permute-start(bf16[128,128]{1,0:T(8,128)(2,1)S(1)} %get-tuple-element.47), channel_id=1, source_target_pairs={{0,4},{2,6},{4,0},{6,2},{1,5},{3,7},{5,1},{7,3},{8,12},{10,14},{12... | collective-permute-start | bytes 98312 | tf_op jit(solution)/shard_map/ppermute | solution.py:37
  44.7 3.3 %collective-permute-start.5 = (bf16[128,128]{1,0:T(8,128)(2,1)S(1)}, bf16[128,128]{1,0:T(8,128)(2,1)S(1)}, u32[]{:S(2)}, u32[]{:S(2)}) collective-permute-start(bf16[128,128]{1,0:T(8,128)(2,1)S(1)} %get-tuple-element.48), channel_id=1, source_target_pairs={{0,6},{2,4},{4,2},{6,0},{1,7},{3,5},{5,3},{7,1},{8,14},{10,12},{12... | collective-permute-start | bytes 98312 | tf_op jit(solution)/shard_map/ppermute | solution.py:37
  50.8 3.9 %collective-permute-start.11 = (bf16[128,128]{1,0:T(8,128)(2,1)S(1)}, bf16[128,128]{1,0:T(8,128)(2,1)S(1)}, u32[]{:S(2)}, u32[]{:S(2)}) collective-permute-start(bf16[128,128]{1,0:T(8,128)(2,1)S(1)} %get-tuple-element.50.refs_0_), channel_id=1, source_target_pairs={{0,8},{1,9},{2,10},{3,11},{4,12},{5,13},{6,14},{7,15}} | collective-permute-start | bytes 98312 | tf_op jit(solution)/shard_map/ppermute | solution.py:866
  52.1 2.9 %collective-permute-start.12 = (bf16[128,128]{1,0:T(8,128)(2,1)S(1)}, bf16[128,128]{1,0:T(8,128)(2,1)S(1)}, u32[]{:S(2)}, u32[]{:S(2)}) collective-permute-start(bf16[128,128]{1,0:T(8,128)(2,1)S(1)} %get-tuple-element.50.refs_0_), channel_id=1, source_target_pairs={{0,16},{1,17},{2,18},{3,19},{4,20},{5,21},{6,22},{7,23}} | collective-permute-start | bytes 98312 | tf_op jit(solution)/shard_map/ppermute | solution.py:866
  53.4 2.9 %collective-permute-start.13 = (bf16[128,128]{1,0:T(8,128)(2,1)S(1)}, bf16[128,128]{1,0:T(8,128)(2,1)S(1)}, u32[]{:S(2)}, u32[]{:S(2)}) collective-permute-start(bf16[128,128]{1,0:T(8,128)(2,1)S(1)} %get-tuple-element.50.refs_0_), channel_id=1, source_target_pairs={{0,24},{1,25},{2,26},{3,27},{4,28},{5,29},{6,30},{7,31}} | collective-permute-start | bytes 98312 | tf_op jit(solution)/shard_map/ppermute | solution.py:866
  56.3 1.9 %collective-permute-start.14 = (bf16[128,64]{1,0:T(8,128)(2,1)S(1)}, bf16[128,64]{1,0:T(8,128)(2,1)S(1)}, u32[]{:S(2)}, u32[]{:S(2)}) collective-permute-start(bf16[128,64]{1,0:T(8,128)(2,1)S(1)} %get-tuple-element.51.refs_3_.refs_8_), channel_id=1, source_target_pairs={{0,2},{2,0},{4,6},{6,4},{1,3},{3,1},{5,7},{7,5},{8,10},{10,8},{12,... | collective-permute-start | bytes 49160 | tf_op jit(solution)/shard_map/ppermute | solution.py:32
  56.4 4.0 %collective-permute-start.15 = (bf16[128,64]{1,0:T(8,128)(2,1)S(1)}, bf16[128,64]{1,0:T(8,128)(2,1)S(1)}, u32[]{:S(2)}, u32[]{:S(2)}) collective-permute-start(bf16[128,64]{1,0:T(8,128)(2,1)S(1)} %get-tuple-element.51.refs_3_.refs_8_), channel_id=1, source_target_pairs={{0,4},{2,6},{4,0},{6,2},{1,5},{3,7},{5,1},{7,3},{8,12},{10,14},{12... | collective-permute-start | bytes 49160 | tf_op jit(solution)/shard_map/ppermute | solution.py:32
  57.3 3.4 %collective-permute-start.16 = (bf16[128,64]{1,0:T(8,128)(2,1)S(1)}, bf16[128,64]{1,0:T(8,128)(2,1)S(1)}, u32[]{:S(2)}, u32[]{:S(2)}) collective-permute-start(bf16[128,64]{1,0:T(8,128)(2,1)S(1)} %get-tuple-element.51.refs_3_.refs_8_), channel_id=1, source_target_pairs={{0,6},{2,4},{4,2},{6,0},{1,7},{3,5},{5,3},{7,1},{8,14},{10,12},{12... | collective-permute-start | bytes 49160 | tf_op jit(solution)/shard_map/ppermute | solution.py:32
  60.7 1.9 %collective-permute-start.17 = (bf16[128,128]{1,0:T(8,128)(2,1)S(1)}, bf16[128,128]{1,0:T(8,128)(2,1)S(1)}, u32[]{:S(2)}, u32[]{:S(2)}) collective-permute-start(bf16[128,128]{1,0:T(8,128)(2,1)S(1)} %get-tuple-element.58), channel_id=1, source_target_pairs={{0,2},{2,0},{4,6},{6,4},{1,3},{3,1},{5,7},{7,5},{8,10},{10,8},{12,... | collective-permute-start | bytes 98312 | tf_op jit(solution)/shard_map/ppermute | solution.py:37
  60.9 3.9 %collective-permute-start.18 = (bf16[128,128]{1,0:T(8,128)(2,1)S(1)}, bf16[128,128]{1,0:T(8,128)(2,1)S(1)}, u32[]{:S(2)}, u32[]{:S(2)}) collective-permute-start(bf16[128,128]{1,0:T(8,128)(2,1)S(1)} %get-tuple-element.59), channel_id=1, source_target_pairs={{0,4},{2,6},{4,0},{6,2},{1,5},{3,7},{5,1},{7,3},{8,12},{10,14},{12... | collective-permute-start | bytes 98312 | tf_op jit(solution)/shard_map/ppermute | solution.py:37
  62.0 3.4 %collective-permute-start.19 = (bf16[128,128]{1,0:T(8,128)(2,1)S(1)}, bf16[128,128]{1,0:T(8,128)(2,1)S(1)}, u32[]{:S(2)}, u32[]{:S(2)}) collective-permute-start(bf16[128,128]{1,0:T(8,128)(2,1)S(1)} %get-tuple-element.60), channel_id=1, source_target_pairs={{0,6},{2,4},{4,2},{6,0},{1,7},{3,5},{5,3},{7,1},{8,14},{10,12},{12... | collective-permute-start | bytes 98312 | tf_op jit(solution)/shard_map/ppermute | solution.py:37
  65.5 26.3 %copy-start.2 = (bf16[4,128,128]{2,1,0:T(8,128)(2,1)S(1)}, bf16[4,128,128]{2,1,0:T(8,128)(2,1)}, u32[]{:S(2)}) copy-start(bf16[4,128,128]{2,1,0:T(8,128)(2,1)} %get-tuple-element.68.refs_5_) | copy-start | bytes 393220
  65.5 26.3 %copy-start.3 = (f32[128,128]{1,0:T(8,128)S(1)}, f32[128,128]{1,0:T(8,128)}, u32[]{:S(2)}) copy-start(f32[128,128]{1,0:T(8,128)} %get-tuple-element.69.refs_6_) | copy-start | bytes 196612
  65.5 32.3 %copy-start.5 = (f32[1,9216]{1,0:T(1,128)S(1)}, f32[1,9216]{1,0:T(1,128)}, u32[]{:S(2)}) copy-start(f32[1,9216]{1,0:T(1,128)} %get-tuple-element.49.refs_12_) | copy-start | bytes 110596
  65.5 1.9 %collective-permute-start.20 = (bf16[128,128]{1,0:T(8,128)(2,1)S(1)}, bf16[128,128]{1,0:T(8,128)(2,1)S(1)}, u32[]{:S(2)}, u32[]{:S(2)}) collective-permute-start(bf16[128,128]{1,0:T(8,128)(2,1)S(1)} %get-tuple-element.63), channel_id=1, source_target_pairs={{0,2},{2,0},{4,6},{6,4},{1,3},{3,1},{5,7},{7,5},{8,10},{10,8},{12,... | collective-permute-start | bytes 98312 | tf_op jit(solution)/shard_map/ppermute | solution.py:37
  65.7 3.9 %collective-permute-start.21 = (bf16[128,128]{1,0:T(8,128)(2,1)S(1)}, bf16[128,128]{1,0:T(8,128)(2,1)S(1)}, u32[]{:S(2)}, u32[]{:S(2)}) collective-permute-start(bf16[128,128]{1,0:T(8,128)(2,1)S(1)} %get-tuple-element.64), channel_id=1, source_target_pairs={{0,4},{2,6},{4,0},{6,2},{1,5},{3,7},{5,1},{7,3},{8,12},{10,14},{12... | collective-permute-start | bytes 98312 | tf_op jit(solution)/shard_map/ppermute | solution.py:37
  66.6 3.4 %collective-permute-start.22 = (bf16[128,128]{1,0:T(8,128)(2,1)S(1)}, bf16[128,128]{1,0:T(8,128)(2,1)S(1)}, u32[]{:S(2)}, u32[]{:S(2)}) collective-permute-start(bf16[128,128]{1,0:T(8,128)(2,1)S(1)} %get-tuple-element.65), channel_id=1, source_target_pairs={{0,6},{2,4},{4,2},{6,0},{1,7},{3,5},{5,3},{7,1},{8,14},{10,12},{12... | collective-permute-start | bytes 98312 | tf_op jit(solution)/shard_map/ppermute | solution.py:37
  70.1 15.0 %collective-permute-start.25 = (bf16[2,128,64]{2,1,0:T(8,128)(2,1)S(1)}, bf16[2,128,64]{2,1,0:T(8,128)(2,1)S(1)}, u32[]{:S(2)}, u32[]{:S(2)}) collective-permute-start(bf16[2,128,64]{2,1,0:T(8,128)(2,1)S(1)} %get-tuple-element.73), channel_id=1, source_target_pairs={{0,2},{2,0},{4,6},{6,4},{1,3},{3,1},{5,7},{7,5},{8,10},{10,8},{12,... | collective-permute-start | bytes 98312 | tf_op jit(solution)/shard_map/ppermute | solution.py:910
  70.2 17.2 %collective-permute-start.23 = (bf16[160,64]{1,0:T(8,128)(2,1)S(1)}, bf16[160,64]{1,0:T(8,128)(2,1)S(1)}, u32[]{:S(2)}, u32[]{:S(2)}) collective-permute-start(bf16[160,64]{1,0:T(8,128)(2,1)S(1)} %get-tuple-element.66), channel_id=1, source_target_pairs={{0,8},{8,0},{16,24},{24,16},{1,9},{9,1},{17,25},{25,17},{2,10},{10... | collective-permute-start | bytes 61448 | tf_op jit(solution)/shard_map/ppermute | solution.py:911
  74.9 12.6 %collective-permute-start.24 = (bf16[128,64]{1,0:T(8,128)(2,1)S(1)}, bf16[128,64]{1,0:T(8,128)(2,1)S(1)}, u32[]{:S(2)}, u32[]{:S(2)}) collective-permute-start(bf16[128,64]{1,0:T(8,128)(2,1)S(1)} %get-tuple-element.61.refs_7_), channel_id=1, source_target_pairs={{0,16},{8,24},{16,0},{24,8},{1,17},{9,25},{17,1},{25,9},{2,18},{10... | collective-permute-start | bytes 49160 | tf_op jit(solution)/shard_map/ppermute | solution.py:900
  85.0 5.8 %collective-permute-start.26 = (bf16[128,64]{1,0:T(8,128)(2,1)S(1)}, bf16[128,64]{1,0:T(8,128)(2,1)S(1)}, u32[]{:S(2)}, u32[]{:S(2)}) collective-permute-start(bf16[128,64]{1,0:T(8,128)(2,1)S(1)} %get-tuple-element.74), channel_id=1, source_target_pairs={{0,8},{2,10},{4,12},{6,14},{8,16},{10,18},{12,20},{14,22},{16,24},... | collective-permute-start | bytes 49160 | tf_op jit(solution)/shard_map/ppermute | solution.py:914
  85.1 6.6 %collective-permute-start.27 = (bf16[128,64]{1,0:T(8,128)(2,1)S(1)}, bf16[128,64]{1,0:T(8,128)(2,1)S(1)}, u32[]{:S(2)}, u32[]{:S(2)}) collective-permute-start(bf16[128,64]{1,0:T(8,128)(2,1)S(1)} %get-tuple-element.75), channel_id=1, source_target_pairs={{0,12},{2,14},{4,8},{6,10},{8,20},{10,22},{12,16},{14,18},{16,28},... | collective-permute-start | bytes 49160 | tf_op jit(solution)/shard_map/ppermute | solution.py:914
  92.9 1.3 %collective-permute-start.32 = (bf16[5,64,128]{2,1,0:T(8,128)(2,1)S(1)}, bf16[5,64,128]{2,1,0:T(8,128)(2,1)S(1)}, u32[]{:S(2)}, u32[]{:S(2)}) collective-permute-start(bf16[5,64,128]{2,1,0:T(8,128)(2,1)S(1)} %get-tuple-element.77), channel_id=1, source_target_pairs={{0,2},{2,0},{4,6},{6,4},{1,3},{3,1},{5,7},{7,5},{8,10},{10,8},{12,... | collective-permute-start | bytes 245768 | tf_op jit(solution)/shard_map/ppermute | solution.py:950
  94.3 18.9 %collective-permute-start.33 = (bf16[5,64,128]{2,1,0:T(8,128)(2,1)S(1)}, bf16[5,64,128]{2,1,0:T(8,128)(2,1)S(1)}, u32[]{:S(2)}, u32[]{:S(2)}) collective-permute-start(bf16[5,64,128]{2,1,0:T(8,128)(2,1)S(1)} %add_convert_fusion.refs_8_), channel_id=1, source_target_pairs={{0,4},{1,5},{2,6},{3,7},{4,0},{5,1},{6,2},{7,3},{8,12},{9,13},{10,... | collective-permute-start | bytes 245768 | tf_op jit(solution)/shard_map/ppermute | solution.py:962
  95.4 17.7 %collective-permute-start.34 = (bf16[5,64,128]{2,1,0:T(8,128)(2,1)S(1)}, bf16[5,64,128]{2,1,0:T(8,128)(2,1)S(1)}, u32[]{:S(2)}, u32[]{:S(2)}) collective-permute-start(bf16[5,64,128]{2,1,0:T(8,128)(2,1)S(1)} %add_convert_fusion.refs_8_), channel_id=1, source_target_pairs={{0,1},{1,0},{2,3},{3,2},{4,5},{5,4},{6,7},{7,6},{8,9},{9,8},{10,11... | collective-permute-start | bytes 245768 | tf_op jit(solution)/shard_map/ppermute | solution.py:962
  96.9 16.2 %collective-permute-start.35 = (bf16[5,64,128]{2,1,0:T(8,128)(2,1)S(1)}, bf16[5,64,128]{2,1,0:T(8,128)(2,1)S(1)}, u32[]{:S(2)}, u32[]{:S(2)}) collective-permute-start(bf16[5,64,128]{2,1,0:T(8,128)(2,1)S(1)} %add_convert_fusion.refs_8_), channel_id=1, source_target_pairs={{0,5},{1,4},{2,7},{3,6},{4,1},{5,0},{6,3},{7,2},{8,13},{9,12},{10,... | collective-permute-start | bytes 245768 | tf_op jit(solution)/shard_map/ppermute | solution.py:962
  97.8 3.9 %collective-permute-start.28 = (bf16[128,64]{1,0:T(8,128)(2,1)S(1)}, bf16[128,64]{1,0:T(8,128)(2,1)S(1)}, u32[]{:S(2)}, u32[]{:S(2)}) collective-permute-start(bf16[128,64]{1,0:T(8,128)(2,1)S(1)} %get-tuple-element.76.refs_0_), channel_id=1, source_target_pairs={{0,8},{8,0},{16,24},{24,16},{1,9},{9,1},{17,25},{25,17},{2,10},{10... | collective-permute-start | bytes 49160 | tf_op jit(solution)/shard_map/ppermute | solution.py:946
  97.8 15.3 %collective-permute-start.31 = (f32[1,9216]{1,0:T(1,128)S(1)}, f32[1,9216]{1,0:T(1,128)S(1)}, u32[]{:S(2)}, u32[]{:S(2)}) collective-permute-start(f32[1,9216]{1,0:T(1,128)S(1)} %copy-done.5), channel_id=1, source_target_pairs={{0,1},{1,0},{2,3},{3,2},{4,5},{5,4},{6,7},{7,6},{8,9},{9,8},{10,11... | collective-permute-start | bytes 110600 | tf_op jit(solution)/shard_map/ppermute | solution.py:32
  101.7 5.0 %collective-permute-start.29 = (bf16[128,64]{1,0:T(8,128)(2,1)S(1)}, bf16[128,64]{1,0:T(8,128)(2,1)S(1)}, u32[]{:S(2)}, u32[]{:S(2)}) collective-permute-start(bf16[128,64]{1,0:T(8,128)(2,1)S(1)} %get-tuple-element.76.refs_0_), channel_id=1, source_target_pairs={{0,16},{8,24},{16,0},{24,8},{1,17},{9,25},{17,1},{25,9},{2,18},{10... | collective-permute-start | bytes 49160 | tf_op jit(solution)/shard_map/ppermute | solution.py:945
  106.7 5.7 %collective-permute-start.30 = (bf16[128,64]{1,0:T(8,128)(2,1)S(1)}, bf16[128,64]{1,0:T(8,128)(2,1)S(1)}, u32[]{:S(2)}, u32[]{:S(2)}) collective-permute-start(bf16[128,64]{1,0:T(8,128)(2,1)S(1)} %get-tuple-element.76.refs_0_), channel_id=1, source_target_pairs={{0,24},{8,16},{16,8},{24,0},{1,25},{9,17},{17,9},{25,1},{2,26},{10... | collective-permute-start | bytes 49160 | tf_op jit(solution)/shard_map/ppermute | solution.py:944

commit v11 on v10

--- a/solution.py
+++ b/solution.py
@@ -553,12 +553,12 @@
                 grad_attended = (slot_of(mod, 0, model_width, first, TILE) * grad_residual).astype(
                     jnp.bfloat16
                 )
-                product = dot32_t(grad_attended, stacked_tile(heads_w, first))
+                product = dot32_t(stacked_tile(heads_w, first), grad_attended)
                 totals = product if totals is None else totals + product
             direct_ref[...] = direct
-            width = totals.shape[1] // count
+            width = totals.shape[0] // count
             for place in range(count):
-                grads[place][...] = totals[:, place * width : (place + 1) * width].astype(
+                grads[place][...] = totals[place * width : (place + 1) * width].T.astype(
                     jnp.bfloat16
                 )
 
@@ -721,7 +721,7 @@
     heads_w, refs = nested(refs, sizes)
     other_mods = refs[: groups - 1]
     sums = refs[groups - 1 : 3 * groups - 1]
-    total_ref, work, joined = refs[3 * groups - 1 :]
+    total_out, work, joined, total_ref, sends = refs[3 * groups - 1 :]
     section = lax.axis_index("segment")
     place = lax.axis_index("seq")
     latent_width = embed_w.shape[1]
@@ -730,6 +730,9 @@
     @pl.when(section == 1)
     def _():
         total_ref[...] = jnp.zeros_like(total_ref)
+        copy = pltpu.make_async_copy(total_ref, total_out, sends.at[0])
+        copy.start()
+        copy.wait()
 
     @pl.when(section != 1)
     def _():
@@ -765,7 +768,8 @@
             averages = part if averages is None else averages + part
         averages = jnp.sum(averages, axis=1, keepdims=True) / model_width
         counts = joined[count][:, latent_width : latent_width + 1]
-        for first in range(0, model_width, TILE):
+        copies = []
+        for number, first in enumerate(range(0, model_width, TILE)):
             span = slice(first, first + TILE)
             value = work[:, span] - averages
             total = None
@@ -776,6 +780,13 @@
                 ) + counts[mine] * slot_of(mods[group], 1, model_width, first, TILE)
                 total = product if total is None else total + product
             total_ref[:, span] = total / full_rows
+            area = (slice(None), pl.ds(first, TILE))
+            copies.append(
+                pltpu.make_async_copy(total_ref.at[area], total_out.at[area], sends.at[number])
+            )
+            copies[-1].start()
+        for copy in copies:
+            copy.wait()
 
 
 def step(
@@ -963,7 +974,7 @@
             )
     (total_t,) = run(
         functools.partial(expand_kernel, count, groups, sizes, full_rows),
-        [array((latent_width, model_width), f32)],
+        [],
         (
             w_embed,
             *heads_w,
@@ -974,8 +985,11 @@
         scratch=(
             pltpu.VMEM((groups * latent_width, model_width), f32),
             pltpu.VMEM((count + 1, groups * latent_width, 128), f32),
+            pltpu.VMEM((latent_width, model_width), f32),
+            pltpu.SemaphoreType.DMA((model_width // TILE,)),
         ),
         fetched=(late_mod,),
+        sent=[array((latent_width, model_width), f32)],
     )
     (grad_t,) = run(
         emit_kernel,

time: 116 us -> 117 us (level)
  no operation moved by 1% of the time
where the time goes in v11:
time: 117 us; the launch traced here: 116 us
  waiting for transfers between devices  51.7 us (44%)
  starting transfers between devices  41.5 us (35%)
  Pallas kernels  20.8 us (18%)
    pallas_call x12, Pallas kernels, run(): pl.pallas_call(body, out_shape=list(outputs) + [pltpu.HBM(item.shape, ite...  20.8 us
    ppermute x1, waiting for transfers between devices, spread_heads(): near = lax.ppermute(part, 'seq', swaps(count, bit))  11.9 us
    ppermute x1, starting transfers between devices, step(): fake = lax.ppermute(term_rows, 'segment', swaps(sections, 2))  10.2 us
    ppermute x9, waiting for transfers between devices, scatter_near(): lax.ppermute(blocks[offset], axis, swaps(count, offset))  8.42 us
    ppermute x7, starting transfers between devices, gather_near(): lax.ppermute(value, axis, swaps(count, offset))  6.25 us
    ppermute x1, waiting for transfers between devices, spread_heads(): held[bit] = [near, lax.ppermute(stage(near), 'dp', swaps(groups, 1))]  5.76 us
    ppermute x9, starting transfers between devices, scatter_near(): lax.ppermute(blocks[offset], axis, swaps(count, offset))  5.45 us
    ppermute x7, waiting for transfers between devices, gather_near(): lax.ppermute(value, axis, swaps(count, offset))  5.37 us
  transfers between devices with their start and end apart: 36, of which 22 were waited for; matrix products, arithmetic and copies ran while one was open for 0% of the time, Pallas kernels for 12%

profile of v11, /device:TPU:0, one launch (start us, length us, event | category | flops | bytes accessed | tf_op | source)
XLA Modules:
  0.0 116.2 jit_solution(17437256103358202186)
XLA Ops:
  0.6 1.1 dynamic-slice_bitcast_fusion
  1.7 3.1 %collective-permute-start.7 = (bf16[128,2048]{1,0:T(8,128)(2,1)S(1)}, bf16[128,2048]{1,0:T(8,128)(2,1)S(1)}, u32[]{:S(2)}, u32[]{:S(2)}) collective-permute-start(bf16[128,2048]{1,0:T(8,128)(2,1)S(1)} %dynamic-slice_bitcast_fusion), channel_id=1, source_target_pairs={{0,4},{2,6},{4,0},{6,2},{1,5},{3,7},{5,1},{7,3},{8,12},{10,14},{12... | collective-permute-start | bytes 1572872 | tf_op jit(solution)/shard_map/ppermute | solution.py:52
  4.8 0.0 collective-permute-start.6
  4.8 11.9 %collective-permute-done.7.refs_0_.refs_8_.refs_3_ = bf16[128,2048]{1,0:T(8,128)(2,1)S(1)} collective-permute-done((bf16[128,2048]{1,0:T(8,128)(2,1)S(1)}, bf16[128,2048]{1,0:T(8,128)(2,1)S(1)}, u32[]{:S(2)}, u32[]{:S(2)}) %collective-permute-start.7) | collective-permute-done | bytes 524320 | tf_op jit(solution)/shard_map/ppermute | solution.py:52
  16.7 1.8 %collective-permute-start.8 = (bf16[128,1024]{1,0:T(8,128)(2,1)S(1)}, bf16[128,1024]{1,0:T(8,128)(2,1)S(1)}, u32[]{:S(2)}, u32[]{:S(2)}) collective-permute-start(bf16[128,1024]{1,0:T(8,128)(2,1)S(1)} %shard_map.124), channel_id=1, source_target_pairs={{0,1},{1,0},{2,3},{3,2},{4,5},{5,4},{6,7},{7,6},{8,9},{9,8},{10,11... | collective-permute-start | bytes 786440 | tf_op jit(solution)/shard_map/ppermute | solution.py:53
  18.5 5.8 %collective-permute-done.8.refs_9_.refs_4_ = bf16[128,1024]{1,0:T(8,128)(2,1)S(1)} collective-permute-done((bf16[128,1024]{1,0:T(8,128)(2,1)S(1)}, bf16[128,1024]{1,0:T(8,128)(2,1)S(1)}, u32[]{:S(2)}, u32[]{:S(2)}) %collective-permute-start.8) | collective-permute-done | bytes 262176 | tf_op jit(solution)/shard_map/ppermute | solution.py:53
  24.3 0.0 collective-permute-start.10
  24.3 10.5 %shard_map.122 = (bf16[128,128]{1,0:T(8,128)(2,1)S(1)}, bf16[128,64]{1,0:T(8,128)(2,1)S(1)}, bf16[3,3072,128]{2,1,0:T(8,128)(2,1)S(1)}, bf16[2,64,64]{2,1,0:T(8,128)(2,1)S(1)}) custom-call(s32[2,2]{1,0:T(2,128)} %refs_14_.1, f32[1,256]{1,0:T(1,128)} %refs_1_.3, bf16[256,3072]{1,0:T(8,128)(2,1)} %bitcast.27, bf16[64,128]{1,0:T(8,128)(2,1)} %bitcast.35, ...), custom_call_target="tpu_custom_call" | custom-call | flops 23592960 | bytes 4441104 | tf_op jit(solution)/shard_map/pallas_call | solution.py:191
  34.8 0.0 copy-start
  34.8 0.6 collective-permute-start
  35.4 1.5 %collective-permute-start.1 = (bf16[128,128]{1,0:T(8,128)(2,1)S(1)}, bf16[128,128]{1,0:T(8,128)(2,1)S(1)}, u32[]{:S(2)}, u32[]{:S(2)}) collective-permute-start(bf16[128,128]{1,0:T(8,128)(2,1)S(1)} %get-tuple-element.42.refs_4_), channel_id=1, source_target_pairs={{0,4},{2,6},{4,0},{6,2},{1,5},{3,7},{5,1},{7,3},{8,12},{10,14},{12... | collective-permute-start | bytes 98312 | tf_op jit(solution)/shard_map/ppermute | solution.py:32
  36.8 0.8 collective-permute-start.2
  37.6 1.6 %collective-permute-done.1.refs_6_ = bf16[128,128]{1,0:T(8,128)(2,1)S(1)} collective-permute-done((bf16[128,128]{1,0:T(8,128)(2,1)S(1)}, bf16[128,128]{1,0:T(8,128)(2,1)S(1)}, u32[]{:S(2)}, u32[]{:S(2)}) %collective-permute-start.1) | collective-permute-done | bytes 32800 | tf_op jit(solution)/shard_map/ppermute | solution.py:32
  39.3 1.2 %collective-permute-done.2.refs_7_ = bf16[128,128]{1,0:T(8,128)(2,1)S(1)} collective-permute-done((bf16[128,128]{1,0:T(8,128)(2,1)S(1)}, bf16[128,128]{1,0:T(8,128)(2,1)S(1)}, u32[]{:S(2)}, u32[]{:S(2)}) %collective-permute-start.2) | collective-permute-done | bytes 32800 | tf_op jit(solution)/shard_map/ppermute | solution.py:32
  40.5 2.9 %shard_map.123 = (bf16[128,128]{1,0:T(8,128)(2,1)S(1)}, bf16[128,128]{1,0:T(8,128)(2,1)S(1)}, bf16[128,128]{1,0:T(8,128)(2,1)S(1)}, bf16[128,128]{1,0:T(8,128)(2...) custom-call(bf16[1,64,3072]{2,1,0:T(8,128)(2,1)S(1)} %copy-done.1, ...), custom_call_target="tpu_custom_call" | custom-call | flops 301989888 | bytes 3154944 | tf_op jit(solution)/shard_map/pallas_call | solution.py:191
  43.4 0.2 collective-permute-start.3
  43.6 0.8 collective-permute-start.4
  44.3 0.3 collective-permute-done.3.refs_3_
  44.7 0.7 collective-permute-start.5
  45.3 2.1 %collective-permute-done.4.refs_4_ = bf16[128,128]{1,0:T(8,128)(2,1)S(1)} collective-permute-done((bf16[128,128]{1,0:T(8,128)(2,1)S(1)}, bf16[128,128]{1,0:T(8,128)(2,1)S(1)}, u32[]{:S(2)}, u32[]{:S(2)}) %collective-permute-start.4) | collective-permute-done | bytes 32800 | tf_op jit(solution)/shard_map/ppermute | solution.py:37
  47.5 0.5 collective-permute-done.5.refs_5_
  48.0 0.0 collective-permute-done.6.refs_7_.refs_2_
  48.0 2.7 %shard_map.125 = (bf16[128,128]{1,0:T(8,128)(2,1)S(1)}, bf16[4,128,128]{2,1,0:T(8,128)(2,1)}, f32[128,128]{1,0:T(8,128)}) custom-call(bf16[128,64]{1,0:T(8,128)(2,1)S(1)} %get-tuple-element.44.refs_0_.refs_3_, bf16[1,64,3072]{2,1,0:T(8,128)(2,1)S(1)} %copy-done.1, bf16[128,128]{1,0:T(8,128)(2,1)S(1)} %get-tuple-element.45.refs_2_, ...), custom_call_target="tpu_custom_call" | custom-call | flops 402653184 | bytes 4182032 | tf_op jit(solution)/shard_map/pallas_call | solution.py:191
  50.8 1.3 %collective-permute-start.11 = (bf16[128,128]{1,0:T(8,128)(2,1)S(1)}, bf16[128,128]{1,0:T(8,128)(2,1)S(1)}, u32[]{:S(2)}, u32[]{:S(2)}) collective-permute-start(bf16[128,128]{1,0:T(8,128)(2,1)S(1)} %get-tuple-element.50.refs_0_), channel_id=1, source_target_pairs={{0,8},{1,9},{2,10},{3,11},{4,12},{5,13},{6,14},{7,15}} | collective-permute-start | bytes 98312 | tf_op jit(solution)/shard_map/ppermute | solution.py:877
  52.1 1.3 %collective-permute-start.12 = (bf16[128,128]{1,0:T(8,128)(2,1)S(1)}, bf16[128,128]{1,0:T(8,128)(2,1)S(1)}, u32[]{:S(2)}, u32[]{:S(2)}) collective-permute-start(bf16[128,128]{1,0:T(8,128)(2,1)S(1)} %get-tuple-element.50.refs_0_), channel_id=1, source_target_pairs={{0,16},{1,17},{2,18},{3,19},{4,20},{5,21},{6,22},{7,23}} | collective-permute-start | bytes 98312 | tf_op jit(solution)/shard_map/ppermute | solution.py:877
  53.4 1.3 %collective-permute-start.13 = (bf16[128,128]{1,0:T(8,128)(2,1)S(1)}, bf16[128,128]{1,0:T(8,128)(2,1)S(1)}, u32[]{:S(2)}, u32[]{:S(2)}) collective-permute-start(bf16[128,128]{1,0:T(8,128)(2,1)S(1)} %get-tuple-element.50.refs_0_), channel_id=1, source_target_pairs={{0,24},{1,25},{2,26},{3,27},{4,28},{5,29},{6,30},{7,31}} | collective-permute-start | bytes 98312 | tf_op jit(solution)/shard_map/ppermute | solution.py:877
  54.7 0.3 collective-permute-done.12.refs_2_
  54.9 1.3 %collective-permute-done.13.refs_3_ = bf16[128,128]{1,0:T(8,128)(2,1)S(1)} collective-permute-done((bf16[128,128]{1,0:T(8,128)(2,1)S(1)}, bf16[128,128]{1,0:T(8,128)(2,1)S(1)}, u32[]{:S(2)}, u32[]{:S(2)}) %collective-permute-start.13) | collective-permute-done | bytes 32800 | tf_op jit(solution)/shard_map/ppermute | solution.py:877
  56.3 0.1 collective-permute-start.14
  56.4 1.0 collective-permute-start.15
  57.3 0.9 collective-permute-start.16
  58.2 2.1 %collective-permute-done.15.refs_5_.refs_10_ = bf16[128,64]{1,0:T(8,128)(2,1)S(1)} collective-permute-done((bf16[128,64]{1,0:T(8,128)(2,1)S(1)}, bf16[128,64]{1,0:T(8,128)(2,1)S(1)}, u32[]{:S(2)}, u32[]{:S(2)}) %collective-permute-start.15) | collective-permute-done | bytes 16416 | tf_op jit(solution)/shard_map/ppermute | solution.py:32
  60.3 0.4 collective-permute-done.16.refs_6_.refs_11_
  60.7 0.2 collective-permute-start.17
  60.9 1.1 collective-permute-start.18
  62.0 0.6 collective-permute-start.19
  62.7 2.2 %collective-permute-done.18.refs_4_.refs_10_ = bf16[128,128]{1,0:T(8,128)(2,1)S(1)} collective-permute-done((bf16[128,128]{1,0:T(8,128)(2,1)S(1)}, bf16[128,128]{1,0:T(8,128)(2,1)S(1)}, u32[]{:S(2)}, u32[]{:S(2)}) %collective-permute-start.18) | collective-permute-done | bytes 32800 | tf_op jit(solution)/shard_map/ppermute | solution.py:37
  64.9 0.6 collective-permute-done.19.refs_5_.refs_11_
  65.5 0.2 collective-permute-start.20
  65.7 0.9 collective-permute-start.21
  66.6 0.8 collective-permute-start.22
  67.5 2.2 %collective-permute-done.21.refs_14_ = bf16[128,128]{1,0:T(8,128)(2,1)S(1)} collective-permute-done((bf16[128,128]{1,0:T(8,128)(2,1)S(1)}, bf16[128,128]{1,0:T(8,128)(2,1)S(1)}, u32[]{:S(2)}, u32[]{:S(2)}) %collective-permute-start.21) | collective-permute-done | bytes 32800 | tf_op jit(solution)/shard_map/ppermute | solution.py:37
  69.6 0.4 collective-permute-done.22.refs_15_
  70.1 0.2 collective-permute-start.25
  70.2 4.7 %collective-permute-start.23 = (bf16[160,64]{1,0:T(8,128)(2,1)S(1)}, bf16[160,64]{1,0:T(8,128)(2,1)S(1)}, u32[]{:S(2)}, u32[]{:S(2)}) collective-permute-start(bf16[160,64]{1,0:T(8,128)(2,1)S(1)} %get-tuple-element.66), channel_id=1, source_target_pairs={{0,8},{8,0},{16,24},{24,16},{1,9},{9,1},{17,25},{25,17},{2,10},{10... | collective-permute-start | bytes 61448 | tf_op jit(solution)/shard_map/ppermute | solution.py:922
  74.9 10.2 %collective-permute-start.24 = (bf16[128,64]{1,0:T(8,128)(2,1)S(1)}, bf16[128,64]{1,0:T(8,128)(2,1)S(1)}, u32[]{:S(2)}, u32[]{:S(2)}) collective-permute-start(bf16[128,64]{1,0:T(8,128)(2,1)S(1)} %get-tuple-element.61.refs_7_), channel_id=1, source_target_pairs={{0,16},{8,24},{16,0},{24,8},{1,17},{9,25},{17,1},{25,9},{2,18},{10... | collective-permute-start | bytes 49160 | tf_op jit(solution)/shard_map/ppermute | solution.py:911
  85.1 0.1 collective-permute-start.26
  85.2 1.1 collective-permute-start.27
  86.3 1.3 %collective-permute-done.24.refs_1_ = bf16[128,64]{1,0:T(8,128)(2,1)S(1)} collective-permute-done((bf16[128,64]{1,0:T(8,128)(2,1)S(1)}, bf16[128,64]{1,0:T(8,128)(2,1)S(1)}, u32[]{:S(2)}, u32[]{:S(2)}) %collective-permute-start.24) | collective-permute-done | bytes 16416 | tf_op jit(solution)/shard_map/ppermute | solution.py:911
  87.5 3.3 %collective-permute-done.26.refs_12_ = bf16[128,64]{1,0:T(8,128)(2,1)S(1)} collective-permute-done((bf16[128,64]{1,0:T(8,128)(2,1)S(1)}, bf16[128,64]{1,0:T(8,128)(2,1)S(1)}, u32[]{:S(2)}, u32[]{:S(2)}) %collective-permute-start.26) | collective-permute-done | bytes 16416 | tf_op jit(solution)/shard_map/ppermute | solution.py:925
  90.9 1.0 collective-permute-done.27.refs_13_
  91.8 1.1 shard_map.131
  92.9 0.1 collective-permute-start.32
  93.0 1.3 %collective-permute-done.32 = bf16[5,64,128]{2,1,0:T(8,128)(2,1)S(1)} collective-permute-done((bf16[5,64,128]{2,1,0:T(8,128)(2,1)S(1)}, bf16[5,64,128]{2,1,0:T(8,128)(2,1)S(1)}, u32[]{:S(2)}, u32[]{:S(2)}) %collective-permute-start.32) | collective-permute-done | bytes 81952 | tf_op jit(solution)/shard_map/ppermute | solution.py:961
  94.3 1.2 %collective-permute-start.33 = (bf16[5,64,128]{2,1,0:T(8,128)(2,1)S(1)}, bf16[5,64,128]{2,1,0:T(8,128)(2,1)S(1)}, u32[]{:S(2)}, u32[]{:S(2)}) collective-permute-start(bf16[5,64,128]{2,1,0:T(8,128)(2,1)S(1)} %add_convert_fusion.refs_8_), channel_id=1, source_target_pairs={{0,4},{1,5},{2,6},{3,7},{4,0},{5,1},{6,2},{7,3},{8,12},{9,13},{10,... | collective-permute-start | bytes 245768 | tf_op jit(solution)/shard_map/ppermute | solution.py:973
  95.5 1.5 %collective-permute-start.34 = (bf16[5,64,128]{2,1,0:T(8,128)(2,1)S(1)}, bf16[5,64,128]{2,1,0:T(8,128)(2,1)S(1)}, u32[]{:S(2)}, u32[]{:S(2)}) collective-permute-start(bf16[5,64,128]{2,1,0:T(8,128)(2,1)S(1)} %add_convert_fusion.refs_8_), channel_id=1, source_target_pairs={{0,1},{1,0},{2,3},{3,2},{4,5},{5,4},{6,7},{7,6},{8,9},{9,8},{10,11... | collective-permute-start | bytes 245768 | tf_op jit(solution)/shard_map/ppermute | solution.py:973
  97.0 0.9 collective-permute-start.35
  97.9 1.5 %collective-permute-start.31 = (f32[1,9216]{1,0:T(1,128)S(1)}, f32[1,9216]{1,0:T(1,128)S(1)}, u32[]{:S(2)}, u32[]{:S(2)}) collective-permute-start(f32[1,9216]{1,0:T(1,128)S(1)} %copy-done.5), channel_id=1, source_target_pairs={{0,1},{1,0},{2,3},{3,2},{4,5},{5,4},{6,7},{7,6},{8,9},{9,8},{10,11... | collective-permute-start | bytes 110600 | tf_op jit(solution)/shard_map/ppermute | solution.py:32
  99.4 2.4 %collective-permute-done.28.refs_1_ = bf16[128,64]{1,0:T(8,128)(2,1)S(1)} collective-permute-done((bf16[128,64]{1,0:T(8,128)(2,1)S(1)}, bf16[128,64]{1,0:T(8,128)(2,1)S(1)}, u32[]{:S(2)}, u32[]{:S(2)}) %collective-permute-start.28) | collective-permute-done | bytes 16416 | tf_op jit(solution)/shard_map/ppermute | solution.py:957
  101.8 5.0 %collective-permute-done.29.refs_2_ = bf16[128,64]{1,0:T(8,128)(2,1)S(1)} collective-permute-done((bf16[128,64]{1,0:T(8,128)(2,1)S(1)}, bf16[128,64]{1,0:T(8,128)(2,1)S(1)}, u32[]{:S(2)}, u32[]{:S(2)}) %collective-permute-start.29) | collective-permute-done | bytes 16416 | tf_op jit(solution)/shard_map/ppermute | solution.py:956
  106.7 1.2 %collective-permute-start.30 = (bf16[128,64]{1,0:T(8,128)(2,1)S(1)}, bf16[128,64]{1,0:T(8,128)(2,1)S(1)}, u32[]{:S(2)}, u32[]{:S(2)}) collective-permute-start(bf16[128,64]{1,0:T(8,128)(2,1)S(1)} %get-tuple-element.76.refs_0_), channel_id=1, source_target_pairs={{0,24},{8,16},{16,8},{24,0},{1,25},{9,17},{17,9},{25,1},{2,26},{10... | collective-permute-start | bytes 49160 | tf_op jit(solution)/shard_map/ppermute | solution.py:955
  108.0 4.5 %collective-permute-done.30.refs_3_ = bf16[128,64]{1,0:T(8,128)(2,1)S(1)} collective-permute-done((bf16[128,64]{1,0:T(8,128)(2,1)S(1)}, bf16[128,64]{1,0:T(8,128)(2,1)S(1)}, u32[]{:S(2)}, u32[]{:S(2)}) %collective-permute-start.30) | collective-permute-done | bytes 16416 | tf_op jit(solution)/shard_map/ppermute | solution.py:955
  112.4 0.7 shard_map.132
  113.2 2.8 %shard_map.133 = f32[64,3072]{1,0:T(8,128)} custom-call(bf16[1,64,3072]{2,1,0:T(8,128)(2,1)S(1)} %copy-done.1, bf16[128,3072]{1,0:T(8,128)(2,1)S(1)} %bitcast.24, bf16[128,3072]{1,0:T(8,128)(2,1)S(1)} %collective-permute-done.6.refs_7_.refs_2_, bf16[128,2048]{1,0:T(8,128)(2,1)S(1)} %collective-permute-done.7.refs_0_.refs_8_.refs_3_, ...), custom_call_target="tpu_custom_call" | custom-call | flops 805306368 | bytes 3940352 | tf_op jit(solution)/shard_map/pallas_call | solution.py:191
  (34 shorter events, 0.2 us)
Async XLA Ops:
  1.7 15.0 %collective-permute-start.7 = (bf16[128,2048]{1,0:T(8,128)(2,1)S(1)}, bf16[128,2048]{1,0:T(8,128)(2,1)S(1)}, u32[]{:S(2)}, u32[]{:S(2)}) collective-permute-start(bf16[128,2048]{1,0:T(8,128)(2,1)S(1)} %dynamic-slice_bitcast_fusion), channel_id=1, source_target_pairs={{0,4},{2,6},{4,0},{6,2},{1,5},{3,7},{5,1},{7,3},{8,12},{10,14},{12... | collective-permute-start | bytes 1572872 | tf_op jit(solution)/shard_map/ppermute | solution.py:52
  4.8 43.2 %collective-permute-start.6 = (bf16[128,3072]{1,0:T(8,128)(2,1)}, bf16[128,3072]{1,0:T(8,128)(2,1)S(1)}, u32[]{:S(2)}, u32[]{:S(2)}) collective-permute-start(bf16[128,3072]{1,0:T(8,128)(2,1)} %bitcast.21), channel_id=1, source_target_pairs={{0,2},{2,0},{4,6},{6,4},{1,3},{3,1},{5,7},{7,5},{8,10},{10,8},{12,... | collective-permute-start | bytes 2359304 | tf_op jit(solution)/shard_map/ppermute | solution.py:56
  16.7 7.5 %collective-permute-start.8 = (bf16[128,1024]{1,0:T(8,128)(2,1)S(1)}, bf16[128,1024]{1,0:T(8,128)(2,1)S(1)}, u32[]{:S(2)}, u32[]{:S(2)}) collective-permute-start(bf16[128,1024]{1,0:T(8,128)(2,1)S(1)} %shard_map.124), channel_id=1, source_target_pairs={{0,1},{1,0},{2,3},{3,2},{4,5},{5,4},{6,7},{7,6},{8,9},{9,8},{10,11... | collective-permute-start | bytes 786440 | tf_op jit(solution)/shard_map/ppermute | solution.py:53
  18.5 29.5 %collective-permute-start.9 = (bf16[128,2048]{1,0:T(8,128)(2,1)S(1)}, bf16[128,2048]{1,0:T(8,128)(2,1)S(1)}, u32[]{:S(2)}, u32[]{:S(2)}) collective-permute-start(bf16[128,2048]{1,0:T(8,128)(2,1)S(1)} %collective-permute-done.7.refs_0_.refs_8_.refs_3_), channel_id=1, source_target_pairs={{0,2},{2,0},{4,6},{6,4},{1,3},{3,1},{5,7},{7,5},{8,10},{10,8},{12,... | collective-permute-start | bytes 1572872 | tf_op jit(solution)/shard_map/ppermute | solution.py:56
  24.3 23.8 %collective-permute-start.10 = (bf16[128,1024]{1,0:T(8,128)(2,1)S(1)}, bf16[128,1024]{1,0:T(8,128)(2,1)S(1)}, u32[]{:S(2)}, u32[]{:S(2)}) collective-permute-start(bf16[128,1024]{1,0:T(8,128)(2,1)S(1)} %collective-permute-done.8.refs_9_.refs_4_), channel_id=1, source_target_pairs={{0,2},{2,0},{4,6},{6,4},{1,3},{3,1},{5,7},{7,5},{8,10},{10,8},{12,... | collective-permute-start | bytes 786440 | tf_op jit(solution)/shard_map/ppermute | solution.py:56
  24.3 16.2 %copy-start.1 = (bf16[1,64,3072]{2,1,0:T(8,128)(2,1)S(1)}, bf16[1,64,3072]{2,1,0:T(8,128)(2,1)}, u32[]{:S(2)}) copy-start(bf16[1,64,3072]{2,1,0:T(8,128)(2,1)} %refs_0_.5) | copy-start | bytes 1179652
  24.3 16.2 %copy-start.4 = (f32[1,2,128]{2,1,0:T(2,128)S(1)}, f32[1,2,128]{2,1,0:T(2,128)}, u32[]{:S(2)}) copy-start(f32[1,2,128]{2,1,0:T(2,128)} %refs_2_.3) | copy-start | bytes 3076
  34.8 13.2 %copy-start = (bf16[1,1,128,3072]{3,2,1,0:T(8,128)(2,1)S(1)}, bf16[1,1,128,3072]{3,2,1,0:T(8,128)(2,1)}, u32[]{:S(2)}) copy-start(bf16[1,1,128,3072]{3,2,1,0:T(8,128)(2,1)} %param.19) | copy-start | bytes 2359300
  34.8 2.0 %collective-permute-start = (bf16[128,128]{1,0:T(8,128)(2,1)S(1)}, bf16[128,128]{1,0:T(8,128)(2,1)S(1)}, u32[]{:S(2)}, u32[]{:S(2)}) collective-permute-start(bf16[128,128]{1,0:T(8,128)(2,1)S(1)} %get-tuple-element.42.refs_4_), channel_id=1, source_target_pairs={{0,2},{2,0},{4,6},{6,4},{1,3},{3,1},{5,7},{7,5},{8,10},{10,8},{12,... | collective-permute-start | bytes 98312 | tf_op jit(solution)/shard_map/ppermute | solution.py:32
  35.4 3.9 %collective-permute-start.1 = (bf16[128,128]{1,0:T(8,128)(2,1)S(1)}, bf16[128,128]{1,0:T(8,128)(2,1)S(1)}, u32[]{:S(2)}, u32[]{:S(2)}) collective-permute-start(bf16[128,128]{1,0:T(8,128)(2,1)S(1)} %get-tuple-element.42.refs_4_), channel_id=1, source_target_pairs={{0,4},{2,6},{4,0},{6,2},{1,5},{3,7},{5,1},{7,3},{8,12},{10,14},{12... | collective-permute-start | bytes 98312 | tf_op jit(solution)/shard_map/ppermute | solution.py:32
  36.8 3.7 %collective-permute-start.2 = (bf16[128,128]{1,0:T(8,128)(2,1)S(1)}, bf16[128,128]{1,0:T(8,128)(2,1)S(1)}, u32[]{:S(2)}, u32[]{:S(2)}) collective-permute-start(bf16[128,128]{1,0:T(8,128)(2,1)S(1)} %get-tuple-element.42.refs_4_), channel_id=1, source_target_pairs={{0,6},{2,4},{4,2},{6,0},{1,7},{3,5},{5,3},{7,1},{8,14},{10,12},{12... | collective-permute-start | bytes 98312 | tf_op jit(solution)/shard_map/ppermute | solution.py:32
  43.4 1.3 %collective-permute-start.3 = (bf16[128,128]{1,0:T(8,128)(2,1)S(1)}, bf16[128,128]{1,0:T(8,128)(2,1)S(1)}, u32[]{:S(2)}, u32[]{:S(2)}) collective-permute-start(bf16[128,128]{1,0:T(8,128)(2,1)S(1)} %get-tuple-element.46), channel_id=1, source_target_pairs={{0,2},{2,0},{4,6},{6,4},{1,3},{3,1},{5,7},{7,5},{8,10},{10,8},{12,... | collective-permute-start | bytes 98312 | tf_op jit(solution)/shard_map/ppermute | solution.py:37
  43.6 3.9 %collective-permute-start.4 = (bf16[128,128]{1,0:T(8,128)(2,1)S(1)}, bf16[128,128]{1,0:T(8,128)(2,1)S(1)}, u32[]{:S(2)}, u32[]{:S(2)}) collective-permute-start(bf16[128,128]{1,0:T(8,128)(2,1)S(1)} %get-tuple-element.47), channel_id=1, source_target_pairs={{0,4},{2,6},{4,0},{6,2},{1,5},{3,7},{5,1},{7,3},{8,12},{10,14},{12... | collective-permute-start | bytes 98312 | tf_op jit(solution)/shard_map/ppermute | solution.py:37
  44.7 3.3 %collective-permute-start.5 = (bf16[128,128]{1,0:T(8,128)(2,1)S(1)}, bf16[128,128]{1,0:T(8,128)(2,1)S(1)}, u32[]{:S(2)}, u32[]{:S(2)}) collective-permute-start(bf16[128,128]{1,0:T(8,128)(2,1)S(1)} %get-tuple-element.48), channel_id=1, source_target_pairs={{0,6},{2,4},{4,2},{6,0},{1,7},{3,5},{5,3},{7,1},{8,14},{10,12},{12... | collective-permute-start | bytes 98312 | tf_op jit(solution)/shard_map/ppermute | solution.py:37
  50.8 3.9 %collective-permute-start.11 = (bf16[128,128]{1,0:T(8,128)(2,1)S(1)}, bf16[128,128]{1,0:T(8,128)(2,1)S(1)}, u32[]{:S(2)}, u32[]{:S(2)}) collective-permute-start(bf16[128,128]{1,0:T(8,128)(2,1)S(1)} %get-tuple-element.50.refs_0_), channel_id=1, source_target_pairs={{0,8},{1,9},{2,10},{3,11},{4,12},{5,13},{6,14},{7,15}} | collective-permute-start | bytes 98312 | tf_op jit(solution)/shard_map/ppermute | solution.py:877
  52.1 2.9 %collective-permute-start.12 = (bf16[128,128]{1,0:T(8,128)(2,1)S(1)}, bf16[128,128]{1,0:T(8,128)(2,1)S(1)}, u32[]{:S(2)}, u32[]{:S(2)}) collective-permute-start(bf16[128,128]{1,0:T(8,128)(2,1)S(1)} %get-tuple-element.50.refs_0_), channel_id=1, source_target_pairs={{0,16},{1,17},{2,18},{3,19},{4,20},{5,21},{6,22},{7,23}} | collective-permute-start | bytes 98312 | tf_op jit(solution)/shard_map/ppermute | solution.py:877
  53.4 2.9 %collective-permute-start.13 = (bf16[128,128]{1,0:T(8,128)(2,1)S(1)}, bf16[128,128]{1,0:T(8,128)(2,1)S(1)}, u32[]{:S(2)}, u32[]{:S(2)}) collective-permute-start(bf16[128,128]{1,0:T(8,128)(2,1)S(1)} %get-tuple-element.50.refs_0_), channel_id=1, source_target_pairs={{0,24},{1,25},{2,26},{3,27},{4,28},{5,29},{6,30},{7,31}} | collective-permute-start | bytes 98312 | tf_op jit(solution)/shard_map/ppermute | solution.py:877
  56.3 1.9 %collective-permute-start.14 = (bf16[128,64]{1,0:T(8,128)(2,1)S(1)}, bf16[128,64]{1,0:T(8,128)(2,1)S(1)}, u32[]{:S(2)}, u32[]{:S(2)}) collective-permute-start(bf16[128,64]{1,0:T(8,128)(2,1)S(1)} %get-tuple-element.51.refs_3_.refs_8_), channel_id=1, source_target_pairs={{0,2},{2,0},{4,6},{6,4},{1,3},{3,1},{5,7},{7,5},{8,10},{10,8},{12,... | collective-permute-start | bytes 49160 | tf_op jit(solution)/shard_map/ppermute | solution.py:32
  56.4 4.0 %collective-permute-start.15 = (bf16[128,64]{1,0:T(8,128)(2,1)S(1)}, bf16[128,64]{1,0:T(8,128)(2,1)S(1)}, u32[]{:S(2)}, u32[]{:S(2)}) collective-permute-start(bf16[128,64]{1,0:T(8,128)(2,1)S(1)} %get-tuple-element.51.refs_3_.refs_8_), channel_id=1, source_target_pairs={{0,4},{2,6},{4,0},{6,2},{1,5},{3,7},{5,1},{7,3},{8,12},{10,14},{12... | collective-permute-start | bytes 49160 | tf_op jit(solution)/shard_map/ppermute | solution.py:32
  57.3 3.4 %collective-permute-start.16 = (bf16[128,64]{1,0:T(8,128)(2,1)S(1)}, bf16[128,64]{1,0:T(8,128)(2,1)S(1)}, u32[]{:S(2)}, u32[]{:S(2)}) collective-permute-start(bf16[128,64]{1,0:T(8,128)(2,1)S(1)} %get-tuple-element.51.refs_3_.refs_8_), channel_id=1, source_target_pairs={{0,6},{2,4},{4,2},{6,0},{1,7},{3,5},{5,3},{7,1},{8,14},{10,12},{12... | collective-permute-start | bytes 49160 | tf_op jit(solution)/shard_map/ppermute | solution.py:32
  60.7 1.9 %collective-permute-start.17 = (bf16[128,128]{1,0:T(8,128)(2,1)S(1)}, bf16[128,128]{1,0:T(8,128)(2,1)S(1)}, u32[]{:S(2)}, u32[]{:S(2)}) collective-permute-start(bf16[128,128]{1,0:T(8,128)(2,1)S(1)} %get-tuple-element.58), channel_id=1, source_target_pairs={{0,2},{2,0},{4,6},{6,4},{1,3},{3,1},{5,7},{7,5},{8,10},{10,8},{12,... | collective-permute-start | bytes 98312 | tf_op jit(solution)/shard_map/ppermute | solution.py:37
  60.9 3.9 %collective-permute-start.18 = (bf16[128,128]{1,0:T(8,128)(2,1)S(1)}, bf16[128,128]{1,0:T(8,128)(2,1)S(1)}, u32[]{:S(2)}, u32[]{:S(2)}) collective-permute-start(bf16[128,128]{1,0:T(8,128)(2,1)S(1)} %get-tuple-element.59), channel_id=1, source_target_pairs={{0,4},{2,6},{4,0},{6,2},{1,5},{3,7},{5,1},{7,3},{8,12},{10,14},{12... | collective-permute-start | bytes 98312 | tf_op jit(solution)/shard_map/ppermute | solution.py:37
  62.0 3.4 %collective-permute-start.19 = (bf16[128,128]{1,0:T(8,128)(2,1)S(1)}, bf16[128,128]{1,0:T(8,128)(2,1)S(1)}, u32[]{:S(2)}, u32[]{:S(2)}) collective-permute-start(bf16[128,128]{1,0:T(8,128)(2,1)S(1)} %get-tuple-element.60), channel_id=1, source_target_pairs={{0,6},{2,4},{4,2},{6,0},{1,7},{3,5},{5,3},{7,1},{8,14},{10,12},{12... | collective-permute-start | bytes 98312 | tf_op jit(solution)/shard_map/ppermute | solution.py:37
  65.5 26.4 %copy-start.2 = (bf16[4,128,128]{2,1,0:T(8,128)(2,1)S(1)}, bf16[4,128,128]{2,1,0:T(8,128)(2,1)}, u32[]{:S(2)}) copy-start(bf16[4,128,128]{2,1,0:T(8,128)(2,1)} %get-tuple-element.68.refs_5_) | copy-start | bytes 393220
  65.5 26.4 %copy-start.3 = (f32[128,128]{1,0:T(8,128)S(1)}, f32[128,128]{1,0:T(8,128)}, u32[]{:S(2)}) copy-start(f32[128,128]{1,0:T(8,128)} %get-tuple-element.69.refs_6_) | copy-start | bytes 196612
  65.5 32.3 %copy-start.5 = (f32[1,9216]{1,0:T(1,128)S(1)}, f32[1,9216]{1,0:T(1,128)}, u32[]{:S(2)}) copy-start(f32[1,9216]{1,0:T(1,128)} %get-tuple-element.49.refs_12_) | copy-start | bytes 110596
  65.5 1.9 %collective-permute-start.20 = (bf16[128,128]{1,0:T(8,128)(2,1)S(1)}, bf16[128,128]{1,0:T(8,128)(2,1)S(1)}, u32[]{:S(2)}, u32[]{:S(2)}) collective-permute-start(bf16[128,128]{1,0:T(8,128)(2,1)S(1)} %get-tuple-element.63), channel_id=1, source_target_pairs={{0,2},{2,0},{4,6},{6,4},{1,3},{3,1},{5,7},{7,5},{8,10},{10,8},{12,... | collective-permute-start | bytes 98312 | tf_op jit(solution)/shard_map/ppermute | solution.py:37
  65.7 3.9 %collective-permute-start.21 = (bf16[128,128]{1,0:T(8,128)(2,1)S(1)}, bf16[128,128]{1,0:T(8,128)(2,1)S(1)}, u32[]{:S(2)}, u32[]{:S(2)}) collective-permute-start(bf16[128,128]{1,0:T(8,128)(2,1)S(1)} %get-tuple-element.64), channel_id=1, source_target_pairs={{0,4},{2,6},{4,0},{6,2},{1,5},{3,7},{5,1},{7,3},{8,12},{10,14},{12... | collective-permute-start | bytes 98312 | tf_op jit(solution)/shard_map/ppermute | solution.py:37
  66.6 3.4 %collective-permute-start.22 = (bf16[128,128]{1,0:T(8,128)(2,1)S(1)}, bf16[128,128]{1,0:T(8,128)(2,1)S(1)}, u32[]{:S(2)}, u32[]{:S(2)}) collective-permute-start(bf16[128,128]{1,0:T(8,128)(2,1)S(1)} %get-tuple-element.65), channel_id=1, source_target_pairs={{0,6},{2,4},{4,2},{6,0},{1,7},{3,5},{5,3},{7,1},{8,14},{10,12},{12... | collective-permute-start | bytes 98312 | tf_op jit(solution)/shard_map/ppermute | solution.py:37
  70.1 15.0 %collective-permute-start.25 = (bf16[2,128,64]{2,1,0:T(8,128)(2,1)S(1)}, bf16[2,128,64]{2,1,0:T(8,128)(2,1)S(1)}, u32[]{:S(2)}, u32[]{:S(2)}) collective-permute-start(bf16[2,128,64]{2,1,0:T(8,128)(2,1)S(1)} %get-tuple-element.73), channel_id=1, source_target_pairs={{0,2},{2,0},{4,6},{6,4},{1,3},{3,1},{5,7},{7,5},{8,10},{10,8},{12,... | collective-permute-start | bytes 98312 | tf_op jit(solution)/shard_map/ppermute | solution.py:921
  70.2 17.3 %collective-permute-start.23 = (bf16[160,64]{1,0:T(8,128)(2,1)S(1)}, bf16[160,64]{1,0:T(8,128)(2,1)S(1)}, u32[]{:S(2)}, u32[]{:S(2)}) collective-permute-start(bf16[160,64]{1,0:T(8,128)(2,1)S(1)} %get-tuple-element.66), channel_id=1, source_target_pairs={{0,8},{8,0},{16,24},{24,16},{1,9},{9,1},{17,25},{25,17},{2,10},{10... | collective-permute-start | bytes 61448 | tf_op jit(solution)/shard_map/ppermute | solution.py:922
  74.9 12.6 %collective-permute-start.24 = (bf16[128,64]{1,0:T(8,128)(2,1)S(1)}, bf16[128,64]{1,0:T(8,128)(2,1)S(1)}, u32[]{:S(2)}, u32[]{:S(2)}) collective-permute-start(bf16[128,64]{1,0:T(8,128)(2,1)S(1)} %get-tuple-element.61.refs_7_), channel_id=1, source_target_pairs={{0,16},{8,24},{16,0},{24,8},{1,17},{9,25},{17,1},{25,9},{2,18},{10... | collective-permute-start | bytes 49160 | tf_op jit(solution)/shard_map/ppermute | solution.py:911
  85.1 5.8 %collective-permute-start.26 = (bf16[128,64]{1,0:T(8,128)(2,1)S(1)}, bf16[128,64]{1,0:T(8,128)(2,1)S(1)}, u32[]{:S(2)}, u32[]{:S(2)}) collective-permute-start(bf16[128,64]{1,0:T(8,128)(2,1)S(1)} %get-tuple-element.74), channel_id=1, source_target_pairs={{0,8},{2,10},{4,12},{6,14},{8,16},{10,18},{12,20},{14,22},{16,24},... | collective-permute-start | bytes 49160 | tf_op jit(solution)/shard_map/ppermute | solution.py:925
  85.2 6.6 %collective-permute-start.27 = (bf16[128,64]{1,0:T(8,128)(2,1)S(1)}, bf16[128,64]{1,0:T(8,128)(2,1)S(1)}, u32[]{:S(2)}, u32[]{:S(2)}) collective-permute-start(bf16[128,64]{1,0:T(8,128)(2,1)S(1)} %get-tuple-element.75), channel_id=1, source_target_pairs={{0,12},{2,14},{4,8},{6,10},{8,20},{10,22},{12,16},{14,18},{16,28},... | collective-permute-start | bytes 49160 | tf_op jit(solution)/shard_map/ppermute | solution.py:925
  92.9 1.3 %collective-permute-start.32 = (bf16[5,64,128]{2,1,0:T(8,128)(2,1)S(1)}, bf16[5,64,128]{2,1,0:T(8,128)(2,1)S(1)}, u32[]{:S(2)}, u32[]{:S(2)}) collective-permute-start(bf16[5,64,128]{2,1,0:T(8,128)(2,1)S(1)} %get-tuple-element.77), channel_id=1, source_target_pairs={{0,2},{2,0},{4,6},{6,4},{1,3},{3,1},{5,7},{7,5},{8,10},{10,8},{12,... | collective-permute-start | bytes 245768 | tf_op jit(solution)/shard_map/ppermute | solution.py:961
  94.3 18.9 %collective-permute-start.33 = (bf16[5,64,128]{2,1,0:T(8,128)(2,1)S(1)}, bf16[5,64,128]{2,1,0:T(8,128)(2,1)S(1)}, u32[]{:S(2)}, u32[]{:S(2)}) collective-permute-start(bf16[5,64,128]{2,1,0:T(8,128)(2,1)S(1)} %add_convert_fusion.refs_8_), channel_id=1, source_target_pairs={{0,4},{1,5},{2,6},{3,7},{4,0},{5,1},{6,2},{7,3},{8,12},{9,13},{10,... | collective-permute-start | bytes 245768 | tf_op jit(solution)/shard_map/ppermute | solution.py:973
  95.5 17.7 %collective-permute-start.34 = (bf16[5,64,128]{2,1,0:T(8,128)(2,1)S(1)}, bf16[5,64,128]{2,1,0:T(8,128)(2,1)S(1)}, u32[]{:S(2)}, u32[]{:S(2)}) collective-permute-start(bf16[5,64,128]{2,1,0:T(8,128)(2,1)S(1)} %add_convert_fusion.refs_8_), channel_id=1, source_target_pairs={{0,1},{1,0},{2,3},{3,2},{4,5},{5,4},{6,7},{7,6},{8,9},{9,8},{10,11... | collective-permute-start | bytes 245768 | tf_op jit(solution)/shard_map/ppermute | solution.py:973
  97.0 16.2 %collective-permute-start.35 = (bf16[5,64,128]{2,1,0:T(8,128)(2,1)S(1)}, bf16[5,64,128]{2,1,0:T(8,128)(2,1)S(1)}, u32[]{:S(2)}, u32[]{:S(2)}) collective-permute-start(bf16[5,64,128]{2,1,0:T(8,128)(2,1)S(1)} %add_convert_fusion.refs_8_), channel_id=1, source_target_pairs={{0,5},{1,4},{2,7},{3,6},{4,1},{5,0},{6,3},{7,2},{8,13},{9,12},{10,... | collective-permute-start | bytes 245768 | tf_op jit(solution)/shard_map/ppermute | solution.py:973
  97.9 3.9 %collective-permute-start.28 = (bf16[128,64]{1,0:T(8,128)(2,1)S(1)}, bf16[128,64]{1,0:T(8,128)(2,1)S(1)}, u32[]{:S(2)}, u32[]{:S(2)}) collective-permute-start(bf16[128,64]{1,0:T(8,128)(2,1)S(1)} %get-tuple-element.76.refs_0_), channel_id=1, source_target_pairs={{0,8},{8,0},{16,24},{24,16},{1,9},{9,1},{17,25},{25,17},{2,10},{10... | collective-permute-start | bytes 49160 | tf_op jit(solution)/shard_map/ppermute | solution.py:957
  97.9 15.3 %collective-permute-start.31 = (f32[1,9216]{1,0:T(1,128)S(1)}, f32[1,9216]{1,0:T(1,128)S(1)}, u32[]{:S(2)}, u32[]{:S(2)}) collective-permute-start(f32[1,9216]{1,0:T(1,128)S(1)} %copy-done.5), channel_id=1, source_target_pairs={{0,1},{1,0},{2,3},{3,2},{4,5},{5,4},{6,7},{7,6},{8,9},{9,8},{10,11... | collective-permute-start | bytes 110600 | tf_op jit(solution)/shard_map/ppermute | solution.py:32
  101.8 5.0 %collective-permute-start.29 = (bf16[128,64]{1,0:T(8,128)(2,1)S(1)}, bf16[128,64]{1,0:T(8,128)(2,1)S(1)}, u32[]{:S(2)}, u32[]{:S(2)}) collective-permute-start(bf16[128,64]{1,0:T(8,128)(2,1)S(1)} %get-tuple-element.76.refs_0_), channel_id=1, source_target_pairs={{0,16},{8,24},{16,0},{24,8},{1,17},{9,25},{17,1},{25,9},{2,18},{10... | collective-permute-start | bytes 49160 | tf_op jit(solution)/shard_map/ppermute | solution.py:956
  106.7 5.7 %collective-permute-start.30 = (bf16[128,64]{1,0:T(8,128)(2,1)S(1)}, bf16[128,64]{1,0:T(8,128)(2,1)S(1)}, u32[]{:S(2)}, u32[]{:S(2)}) collective-permute-start(bf16[128,64]{1,0:T(8,128)(2,1)S(1)} %get-tuple-element.76.refs_0_), channel_id=1, source_target_pairs={{0,24},{8,16},{16,8},{24,0},{1,25},{9,17},{17,9},{25,1},{2,26},{10... | collective-permute-start | bytes 49160 | tf_op jit(solution)/shard_map/ppermute | solution.py:955

commit v12 on v11

--- a/solution.py
+++ b/solution.py
@@ -39,6 +39,16 @@
     ]
 
 
+def window_kernel(fetches, part_out, arrival):
+    width = part_out.shape[1] // 2
+    first = pl.multiple_of(lax.axis_index("dp") * width, width)
+    copy = pltpu.make_async_copy(
+        fetches[0].at[:, pl.ds(first, 2 * width)], part_out, arrival.at[0]
+    )
+    copy.start()
+    copy.wait()
+
+
 def spread_heads(own, count, groups, stage):
     held = {0: [own]}
     bit = count // 2
@@ -47,8 +57,14 @@
         for offset in sorted(held):
             if first and groups == 2:
                 width = own.shape[1] // 3
-                shift = lax.axis_index("dp") * width
-                part = lax.dynamic_slice_in_dim(own, shift, 2 * width, axis=1)
+                (part,) = run(
+                    window_kernel,
+                    [array((own.shape[0], 2 * width), own.dtype)],
+                    (),
+                    1000,
+                    scratch=(pltpu.SemaphoreType.DMA((1,)),),
+                    streamed=(own,),
+                )
                 near = lax.ppermute(part, "seq", swaps(count, bit))
                 held[bit] = [near, lax.ppermute(stage(near), "dp", swaps(groups, 1))]
             else:
@@ -460,11 +476,20 @@
         for copy in copies:
             copy.start()
         velocity, inverse = tail(late, latent, embed_w, final_t, mixed, heads_w, work)
-        inverse_ref[...] = jnp.broadcast_to(inverse, inverse_ref.shape)
+        student_step, critic_step = steps_of(times)
+        sigma_student, sigma_critic = noise_level(student_step), noise_level(critic_step)
+        rows, lanes = inverse_ref.shape
+        rest = (lanes - latent_width) // 2
+        inverse_ref[...] = jnp.concatenate(
+            [
+                jnp.broadcast_to(inverse, (rows, latent_width)),
+                jnp.broadcast_to(sigma_student, (rows, rest)),
+                jnp.broadcast_to(sigma_critic, (rows, rest)),
+            ],
+            axis=1,
+        )
         copies.append(pltpu.make_async_copy(inverse_ref, inverse_out, sends.at[count]))
         copies[-1].start()
-        student_step, critic_step = steps_of(times)
-        sigma_student, sigma_critic = noise_level(student_step), noise_level(critic_step)
         sample = latent[...].astype(jnp.float32) - sigma_student * velocity
         second = noise.ready()[:, latent_width:].astype(jnp.float32)
         critic = (1.0 - sigma_critic) * sample + sigma_critic * second
@@ -543,7 +568,7 @@
             plain = jnp.sum(plain, axis=1, keepdims=True) / model_width
             along = jnp.sum(along, axis=1, keepdims=True) / model_width
             direct = None
-            totals = None
+            totals = [None] * count
             for first in range(0, model_width, TILE):
                 span = slice(first, first + TILE)
                 grad_residual = inverse * (other[:, span] - plain - work[:, span] * along)
@@ -553,14 +578,13 @@
                 grad_attended = (slot_of(mod, 0, model_width, first, TILE) * grad_residual).astype(
                     jnp.bfloat16
                 )
-                product = dot32_t(stacked_tile(heads_w, first), grad_attended)
-                totals = product if totals is None else totals + product
+                for place in range(count):
+                    product = dot32_t(grad_attended, head_tile(heads_w[place], first, TILE))
+                    held = totals[place]
+                    totals[place] = product if held is None else held + product
             direct_ref[...] = direct
-            width = totals.shape[0] // count
             for place in range(count):
-                grads[place][...] = totals[place * width : (place + 1) * width].T.astype(
-                    jnp.bfloat16
-                )
+                grads[place][...] = totals[place].astype(jnp.bfloat16)
 
 
 def judge_back_kernel(count, model_width, fetches, short_in, gram, gains, proj_ref, inverse_ref, key_ref, value_ref, term, *refs):
@@ -682,20 +706,21 @@
 
     @pl.when(section == 0)
     def _():
-        (times,) = fetches
-        times.start()
-        student_step, critic_step = steps_of(times)
+        lanes = student_inverse.shape[1]
+        middle = (lanes + latent_width) // 2
+        sigma_student = student_inverse[:1, latent_width : latent_width + 1]
+        sigma_critic = student_inverse[:1, middle : middle + 1]
         adverse = arrived[0][...].astype(jnp.float32)
         for part in arrived[1:]:
             adverse = adverse + part[...].astype(jnp.float32)
-        adverse = (1.0 - noise_level(critic_step)) * adverse
+        adverse = (1.0 - sigma_critic) * adverse
         spread = (real[rows : rows + 1] .astype(jnp.float32) + real[rows + 16 : rows + 17].astype(jnp.float32))[
             :, :1
         ]
         gap = real[:rows].astype(jnp.float32) - fake[...].astype(jnp.float32)
         sample_grad = gap / spread + ADV_WEIGHT * adverse
         sample_ref[...] = sample_grad.astype(jnp.bfloat16)
-        target = -noise_level(student_step) * sample_grad
+        target = -sigma_student * sample_grad
         mixed = [student_mixed.at[offset] for offset in range(count)]
         collect(target, student_inverse, student_rows[...], mixed)
 
@@ -949,7 +974,6 @@
             *to_student,
         ),
         2 * tok_rows * latent_width * head_width * (count + 1),
-        fetched=(timesteps,),
     )
     ends = [(place, sections - 1 - place) for place in range(sections)]
     to_third = lax.ppermute(sample_grad, "segment", ends)

time: 117 us -> 117 us (level)
    pallas_call x12 -> x13, Pallas kernels: 20.8 us -> 21.8 us  [run(): pl.pallas_call(body, out_shape=list(outputs) + [pltpu.HBM(item.shape, ite...]
where the time goes in v12:
time: 117 us; the launch traced here: 116 us
  waiting for transfers between devices  51.1 us (44%)
  starting transfers between devices  42.2 us (36%)
  Pallas kernels  21.8 us (19%)
    pallas_call x13, Pallas kernels, run(): pl.pallas_call(body, out_shape=list(outputs) + [pltpu.HBM(item.shape, ite...  21.8 us
    ppermute x1, waiting for transfers between devices, spread_heads(): near = lax.ppermute(part, 'seq', swaps(count, bit))  11.9 us
    ppermute x1, starting transfers between devices, step(): fake = lax.ppermute(term_rows, 'segment', swaps(sections, 2))  10.1 us
    ppermute x9, waiting for transfers between devices, scatter_near(): lax.ppermute(blocks[offset], axis, swaps(count, offset))  8.42 us
    ppermute x7, starting transfers between devices, gather_near(): lax.ppermute(value, axis, swaps(count, offset))  6.26 us
    ppermute x1, waiting for transfers between devices, spread_heads(): held[bit] = [near, lax.ppermute(stage(near), 'dp', swaps(groups, 1))]  5.76 us
    ppermute x9, starting transfers between devices, scatter_near(): lax.ppermute(blocks[offset], axis, swaps(count, offset))  5.45 us
    ppermute x7, waiting for transfers between devices, gather_near(): lax.ppermute(value, axis, swaps(count, offset))  5.37 us
  transfers between devices with their start and end apart: 36, of which 22 were waited for; matrix products, arithmetic and copies ran while one was open for 0% of the time, Pallas kernels for 12%

profile of v12, /device:TPU:0, one launch (start us, length us, event | category | flops | bytes accessed | tf_op | source)
XLA Modules:
  0.0 116.2 jit_solution(16082377384779732516)
XLA Ops:
  0.6 1.1 shard_map.124
  1.7 3.1 %collective-permute-start.7 = (bf16[128,2048]{1,0:T(8,128)(2,1)S(1)}, bf16[128,2048]{1,0:T(8,128)(2,1)S(1)}, u32[]{:S(2)}, u32[]{:S(2)}) collective-permute-start(bf16[128,2048]{1,0:T(8,128)(2,1)S(1)} %shard_map.124), channel_id=1, source_target_pairs={{0,4},{2,6},{4,0},{6,2},{1,5},{3,7},{5,1},{7,3},{8,12},{10,14},{12... | collective-permute-start | bytes 1572872 | tf_op jit(solution)/shard_map/ppermute | solution.py:68
  4.8 0.0 collective-permute-start.6
  4.8 11.9 %collective-permute-done.7.refs_0_.refs_8_.refs_3_ = bf16[128,2048]{1,0:T(8,128)(2,1)S(1)} collective-permute-done((bf16[128,2048]{1,0:T(8,128)(2,1)S(1)}, bf16[128,2048]{1,0:T(8,128)(2,1)S(1)}, u32[]{:S(2)}, u32[]{:S(2)}) %collective-permute-start.7) | collective-permute-done | bytes 524320 | tf_op jit(solution)/shard_map/ppermute | solution.py:68
  16.7 1.8 %collective-permute-start.8 = (bf16[128,1024]{1,0:T(8,128)(2,1)S(1)}, bf16[128,1024]{1,0:T(8,128)(2,1)S(1)}, u32[]{:S(2)}, u32[]{:S(2)}) collective-permute-start(bf16[128,1024]{1,0:T(8,128)(2,1)S(1)} %shard_map.125), channel_id=1, source_target_pairs={{0,1},{1,0},{2,3},{3,2},{4,5},{5,4},{6,7},{7,6},{8,9},{9,8},{10,11... | collective-permute-start | bytes 786440 | tf_op jit(solution)/shard_map/ppermute | solution.py:69
  18.5 5.8 %collective-permute-done.8.refs_9_.refs_4_ = bf16[128,1024]{1,0:T(8,128)(2,1)S(1)} collective-permute-done((bf16[128,1024]{1,0:T(8,128)(2,1)S(1)}, bf16[128,1024]{1,0:T(8,128)(2,1)S(1)}, u32[]{:S(2)}, u32[]{:S(2)}) %collective-permute-start.8) | collective-permute-done | bytes 262176 | tf_op jit(solution)/shard_map/ppermute | solution.py:69
  24.3 0.0 collective-permute-start.10
  24.3 10.5 %shard_map.122 = (bf16[128,128]{1,0:T(8,128)(2,1)S(1)}, bf16[128,64]{1,0:T(8,128)(2,1)S(1)}, bf16[3,3072,128]{2,1,0:T(8,128)(2,1)S(1)}, bf16[2,64,64]{2,1,0:T(8,128)(2,1)S(1)}) custom-call(s32[2,2]{1,0:T(2,128)} %refs_15_.3, f32[1,256]{1,0:T(1,128)} %refs_1_.3, bf16[256,3072]{1,0:T(8,128)(2,1)} %bitcast.26, bf16[64,128]{1,0:T(8,128)(2,1)} %bitcast.34, ...), custom_call_target="tpu_custom_call" | custom-call | flops 23592960 | bytes 4441104 | tf_op jit(solution)/shard_map/pallas_call | solution.py:207
  34.8 0.0 copy-start
  34.8 0.6 collective-permute-start
  35.4 1.5 %collective-permute-start.1 = (bf16[128,128]{1,0:T(8,128)(2,1)S(1)}, bf16[128,128]{1,0:T(8,128)(2,1)S(1)}, u32[]{:S(2)}, u32[]{:S(2)}) collective-permute-start(bf16[128,128]{1,0:T(8,128)(2,1)S(1)} %get-tuple-element.42.refs_4_), channel_id=1, source_target_pairs={{0,4},{2,6},{4,0},{6,2},{1,5},{3,7},{5,1},{7,3},{8,12},{10,14},{12... | collective-permute-start | bytes 98312 | tf_op jit(solution)/shard_map/ppermute | solution.py:32
  36.8 0.8 collective-permute-start.2
  37.6 1.6 %collective-permute-done.1.refs_6_ = bf16[128,128]{1,0:T(8,128)(2,1)S(1)} collective-permute-done((bf16[128,128]{1,0:T(8,128)(2,1)S(1)}, bf16[128,128]{1,0:T(8,128)(2,1)S(1)}, u32[]{:S(2)}, u32[]{:S(2)}) %collective-permute-start.1) | collective-permute-done | bytes 32800 | tf_op jit(solution)/shard_map/ppermute | solution.py:32
  39.3 1.2 %collective-permute-done.2.refs_7_ = bf16[128,128]{1,0:T(8,128)(2,1)S(1)} collective-permute-done((bf16[128,128]{1,0:T(8,128)(2,1)S(1)}, bf16[128,128]{1,0:T(8,128)(2,1)S(1)}, u32[]{:S(2)}, u32[]{:S(2)}) %collective-permute-start.2) | collective-permute-done | bytes 32800 | tf_op jit(solution)/shard_map/ppermute | solution.py:32
  40.5 2.9 %shard_map.123 = (bf16[128,128]{1,0:T(8,128)(2,1)S(1)}, bf16[128,128]{1,0:T(8,128)(2,1)S(1)}, bf16[128,128]{1,0:T(8,128)(2,1)S(1)}, bf16[128,128]{1,0:T(8,128)(2...) custom-call(bf16[1,64,3072]{2,1,0:T(8,128)(2,1)S(1)} %copy-done.1, ...), custom_call_target="tpu_custom_call" | custom-call | flops 301989888 | bytes 3154944 | tf_op jit(solution)/shard_map/pallas_call | solution.py:207
  43.4 0.2 collective-permute-start.3
  43.5 0.8 collective-permute-start.4
  44.3 0.3 collective-permute-done.3.refs_3_
  44.7 0.7 collective-permute-start.5
  45.3 2.1 %collective-permute-done.4.refs_4_ = bf16[128,128]{1,0:T(8,128)(2,1)S(1)} collective-permute-done((bf16[128,128]{1,0:T(8,128)(2,1)S(1)}, bf16[128,128]{1,0:T(8,128)(2,1)S(1)}, u32[]{:S(2)}, u32[]{:S(2)}) %collective-permute-start.4) | collective-permute-done | bytes 32800 | tf_op jit(solution)/shard_map/ppermute | solution.py:37
  47.5 0.5 collective-permute-done.5.refs_5_
  48.0 3.2 %shard_map.126 = (bf16[128,128]{1,0:T(8,128)(2,1)S(1)}, bf16[4,128,128]{2,1,0:T(8,128)(2,1)}, f32[128,128]{1,0:T(8,128)}) custom-call(bf16[128,64]{1,0:T(8,128)(2,1)S(1)} %get-tuple-element.44.refs_0_.refs_3_, bf16[1,64,3072]{2,1,0:T(8,128)(2,1)S(1)} %copy-done.1, bf16[128,128]{1,0:T(8,128)(2,1)S(1)} %get-tuple-element.45.refs_2_, ...), custom_call_target="tpu_custom_call" | custom-call | flops 402653184 | bytes 4182032 | tf_op jit(solution)/shard_map/pallas_call | solution.py:207
  51.3 1.3 %collective-permute-start.11 = (bf16[128,128]{1,0:T(8,128)(2,1)S(1)}, bf16[128,128]{1,0:T(8,128)(2,1)S(1)}, u32[]{:S(2)}, u32[]{:S(2)}) collective-permute-start(bf16[128,128]{1,0:T(8,128)(2,1)S(1)} %get-tuple-element.50.refs_0_), channel_id=1, source_target_pairs={{0,8},{1,9},{2,10},{3,11},{4,12},{5,13},{6,14},{7,15}} | collective-permute-start | bytes 98312 | tf_op jit(solution)/shard_map/ppermute | solution.py:902
  52.6 1.3 %collective-permute-start.12 = (bf16[128,128]{1,0:T(8,128)(2,1)S(1)}, bf16[128,128]{1,0:T(8,128)(2,1)S(1)}, u32[]{:S(2)}, u32[]{:S(2)}) collective-permute-start(bf16[128,128]{1,0:T(8,128)(2,1)S(1)} %get-tuple-element.50.refs_0_), channel_id=1, source_target_pairs={{0,16},{1,17},{2,18},{3,19},{4,20},{5,21},{6,22},{7,23}} | collective-permute-start | bytes 98312 | tf_op jit(solution)/shard_map/ppermute | solution.py:902
  53.9 1.3 %collective-permute-start.13 = (bf16[128,128]{1,0:T(8,128)(2,1)S(1)}, bf16[128,128]{1,0:T(8,128)(2,1)S(1)}, u32[]{:S(2)}, u32[]{:S(2)}) collective-permute-start(bf16[128,128]{1,0:T(8,128)(2,1)S(1)} %get-tuple-element.50.refs_0_), channel_id=1, source_target_pairs={{0,24},{1,25},{2,26},{3,27},{4,28},{5,29},{6,30},{7,31}} | collective-permute-start | bytes 98312 | tf_op jit(solution)/shard_map/ppermute | solution.py:902
  55.2 0.3 collective-permute-done.12.refs_2_
  55.5 1.3 %collective-permute-done.13.refs_3_ = bf16[128,128]{1,0:T(8,128)(2,1)S(1)} collective-permute-done((bf16[128,128]{1,0:T(8,128)(2,1)S(1)}, bf16[128,128]{1,0:T(8,128)(2,1)S(1)}, u32[]{:S(2)}, u32[]{:S(2)}) %collective-permute-start.13) | collective-permute-done | bytes 32800 | tf_op jit(solution)/shard_map/ppermute | solution.py:902
  56.8 0.1 collective-permute-start.14
  56.9 1.0 collective-permute-start.15
  57.9 0.9 collective-permute-start.16
  58.7 2.1 %collective-permute-done.15.refs_5_.refs_10_ = bf16[128,64]{1,0:T(8,128)(2,1)S(1)} collective-permute-done((bf16[128,64]{1,0:T(8,128)(2,1)S(1)}, bf16[128,64]{1,0:T(8,128)(2,1)S(1)}, u32[]{:S(2)}, u32[]{:S(2)}) %collective-permute-start.15) | collective-permute-done | bytes 16416 | tf_op jit(solution)/shard_map/ppermute | solution.py:32
  60.9 0.4 collective-permute-done.16.refs_6_.refs_11_
  61.2 0.2 collective-permute-start.17
  61.5 1.1 collective-permute-start.18
  62.6 0.6 collective-permute-start.19
  63.2 2.2 %collective-permute-done.18.refs_4_.refs_10_ = bf16[128,128]{1,0:T(8,128)(2,1)S(1)} collective-permute-done((bf16[128,128]{1,0:T(8,128)(2,1)S(1)}, bf16[128,128]{1,0:T(8,128)(2,1)S(1)}, u32[]{:S(2)}, u32[]{:S(2)}) %collective-permute-start.18) | collective-permute-done | bytes 32800 | tf_op jit(solution)/shard_map/ppermute | solution.py:37
  65.4 0.6 collective-permute-done.19.refs_5_.refs_11_
  66.1 0.2 collective-permute-start.20
  66.2 0.9 collective-permute-start.21
  67.2 0.8 collective-permute-start.22
  68.0 2.2 %collective-permute-done.21.refs_14_ = bf16[128,128]{1,0:T(8,128)(2,1)S(1)} collective-permute-done((bf16[128,128]{1,0:T(8,128)(2,1)S(1)}, bf16[128,128]{1,0:T(8,128)(2,1)S(1)}, u32[]{:S(2)}, u32[]{:S(2)}) %collective-permute-start.21) | collective-permute-done | bytes 32800 | tf_op jit(solution)/shard_map/ppermute | solution.py:37
  70.2 0.4 collective-permute-done.22.refs_15_
  70.6 0.2 collective-permute-start.25
  70.8 4.7 %collective-permute-start.23 = (bf16[160,64]{1,0:T(8,128)(2,1)S(1)}, bf16[160,64]{1,0:T(8,128)(2,1)S(1)}, u32[]{:S(2)}, u32[]{:S(2)}) collective-permute-start(bf16[160,64]{1,0:T(8,128)(2,1)S(1)} %get-tuple-element.66), channel_id=1, source_target_pairs={{0,8},{8,0},{16,24},{24,16},{1,9},{9,1},{17,25},{25,17},{2,10},{10... | collective-permute-start | bytes 61448 | tf_op jit(solution)/shard_map/ppermute | solution.py:947
  75.4 10.1 %collective-permute-start.24 = (bf16[128,64]{1,0:T(8,128)(2,1)S(1)}, bf16[128,64]{1,0:T(8,128)(2,1)S(1)}, u32[]{:S(2)}, u32[]{:S(2)}) collective-permute-start(bf16[128,64]{1,0:T(8,128)(2,1)S(1)} %get-tuple-element.61.refs_7_), channel_id=1, source_target_pairs={{0,16},{8,24},{16,0},{24,8},{1,17},{9,25},{17,1},{25,9},{2,18},{10... | collective-permute-start | bytes 49160 | tf_op jit(solution)/shard_map/ppermute | solution.py:936
  85.5 0.1 collective-permute-start.26
  85.6 1.1 collective-permute-start.27
  86.7 1.3 %collective-permute-done.24.refs_1_ = bf16[128,64]{1,0:T(8,128)(2,1)S(1)} collective-permute-done((bf16[128,64]{1,0:T(8,128)(2,1)S(1)}, bf16[128,64]{1,0:T(8,128)(2,1)S(1)}, u32[]{:S(2)}, u32[]{:S(2)}) %collective-permute-start.24) | collective-permute-done | bytes 16416 | tf_op jit(solution)/shard_map/ppermute | solution.py:936
  88.0 3.3 %collective-permute-done.26.refs_12_ = bf16[128,64]{1,0:T(8,128)(2,1)S(1)} collective-permute-done((bf16[128,64]{1,0:T(8,128)(2,1)S(1)}, bf16[128,64]{1,0:T(8,128)(2,1)S(1)}, u32[]{:S(2)}, u32[]{:S(2)}) %collective-permute-start.26) | collective-permute-done | bytes 16416 | tf_op jit(solution)/shard_map/ppermute | solution.py:950
  91.3 1.0 collective-permute-done.27.refs_13_
  92.3 0.5 shard_map.132
  92.7 0.1 collective-permute-start.32
  92.8 1.3 %collective-permute-done.32 = bf16[5,64,128]{2,1,0:T(8,128)(2,1)S(1)} collective-permute-done((bf16[5,64,128]{2,1,0:T(8,128)(2,1)S(1)}, bf16[5,64,128]{2,1,0:T(8,128)(2,1)S(1)}, u32[]{:S(2)}, u32[]{:S(2)}) %collective-permute-start.32) | collective-permute-done | bytes 81952 | tf_op jit(solution)/shard_map/ppermute | solution.py:985
  94.1 1.2 collective-permute-start.33
  95.3 1.5 %collective-permute-start.34 = (bf16[5,64,128]{2,1,0:T(8,128)(2,1)S(1)}, bf16[5,64,128]{2,1,0:T(8,128)(2,1)S(1)}, u32[]{:S(2)}, u32[]{:S(2)}) collective-permute-start(bf16[5,64,128]{2,1,0:T(8,128)(2,1)S(1)} %add_convert_fusion.refs_8_), channel_id=1, source_target_pairs={{0,1},{1,0},{2,3},{3,2},{4,5},{5,4},{6,7},{7,6},{8,9},{9,8},{10,11... | collective-permute-start | bytes 245768 | tf_op jit(solution)/shard_map/ppermute | solution.py:997
  96.8 0.9 collective-permute-start.35
  97.7 1.5 %collective-permute-start.31 = (f32[1,9216]{1,0:T(1,128)S(1)}, f32[1,9216]{1,0:T(1,128)S(1)}, u32[]{:S(2)}, u32[]{:S(2)}) collective-permute-start(f32[1,9216]{1,0:T(1,128)S(1)} %copy-done.5), channel_id=1, source_target_pairs={{0,1},{1,0},{2,3},{3,2},{4,5},{5,4},{6,7},{7,6},{8,9},{9,8},{10,11... | collective-permute-start | bytes 110600 | tf_op jit(solution)/shard_map/ppermute | solution.py:32
  99.2 2.4 %collective-permute-done.28.refs_1_ = bf16[128,64]{1,0:T(8,128)(2,1)S(1)} collective-permute-done((bf16[128,64]{1,0:T(8,128)(2,1)S(1)}, bf16[128,64]{1,0:T(8,128)(2,1)S(1)}, u32[]{:S(2)}, u32[]{:S(2)}) %collective-permute-start.28) | collective-permute-done | bytes 16416 | tf_op jit(solution)/shard_map/ppermute | solution.py:981
  101.6 0.4 collective-permute-start.29
  102.0 4.8 %collective-permute-done.29.refs_2_ = bf16[128,64]{1,0:T(8,128)(2,1)S(1)} collective-permute-done((bf16[128,64]{1,0:T(8,128)(2,1)S(1)}, bf16[128,64]{1,0:T(8,128)(2,1)S(1)}, u32[]{:S(2)}, u32[]{:S(2)}) %collective-permute-start.29) | collective-permute-done | bytes 16416 | tf_op jit(solution)/shard_map/ppermute | solution.py:980
  106.7 1.7 %collective-permute-start.30 = (bf16[128,64]{1,0:T(8,128)(2,1)S(1)}, bf16[128,64]{1,0:T(8,128)(2,1)S(1)}, u32[]{:S(2)}, u32[]{:S(2)}) collective-permute-start(bf16[128,64]{1,0:T(8,128)(2,1)S(1)} %get-tuple-element.76.refs_0_), channel_id=1, source_target_pairs={{0,24},{8,16},{16,8},{24,0},{1,25},{9,17},{17,9},{25,1},{2,26},{10... | collective-permute-start | bytes 49160 | tf_op jit(solution)/shard_map/ppermute | solution.py:979
  108.4 4.1 %collective-permute-done.30.refs_3_ = bf16[128,64]{1,0:T(8,128)(2,1)S(1)} collective-permute-done((bf16[128,64]{1,0:T(8,128)(2,1)S(1)}, bf16[128,64]{1,0:T(8,128)(2,1)S(1)}, u32[]{:S(2)}, u32[]{:S(2)}) %collective-permute-start.30) | collective-permute-done | bytes 16416 | tf_op jit(solution)/shard_map/ppermute | solution.py:979
  112.4 0.7 shard_map.133
  113.2 2.8 %shard_map.134 = f32[64,3072]{1,0:T(8,128)} custom-call(bf16[1,64,3072]{2,1,0:T(8,128)(2,1)S(1)} %copy-done.1, bf16[128,3072]{1,0:T(8,128)(2,1)S(1)} %bitcast.23, bf16[128,3072]{1,0:T(8,128)(2,1)S(1)} %collective-permute-done.6.refs_7_.refs_2_, bf16[128,2048]{1,0:T(8,128)(2,1)S(1)} %collective-permute-done.7.refs_0_.refs_8_.refs_3_, ...), custom_call_target="tpu_custom_call" | custom-call | flops 805306368 | bytes 3940352 | tf_op jit(solution)/shard_map/pallas_call | solution.py:207
  (34 shorter events, 0.2 us)
Async XLA Ops:
  1.7 15.0 %collective-permute-start.7 = (bf16[128,2048]{1,0:T(8,128)(2,1)S(1)}, bf16[128,2048]{1,0:T(8,128)(2,1)S(1)}, u32[]{:S(2)}, u32[]{:S(2)}) collective-permute-start(bf16[128,2048]{1,0:T(8,128)(2,1)S(1)} %shard_map.124), channel_id=1, source_target_pairs={{0,4},{2,6},{4,0},{6,2},{1,5},{3,7},{5,1},{7,3},{8,12},{10,14},{12... | collective-permute-start | bytes 1572872 | tf_op jit(solution)/shard_map/ppermute | solution.py:68
  4.8 43.2 %collective-permute-start.6 = (bf16[128,3072]{1,0:T(8,128)(2,1)}, bf16[128,3072]{1,0:T(8,128)(2,1)S(1)}, u32[]{:S(2)}, u32[]{:S(2)}) collective-permute-start(bf16[128,3072]{1,0:T(8,128)(2,1)} %bitcast.20), channel_id=1, source_target_pairs={{0,2},{2,0},{4,6},{6,4},{1,3},{3,1},{5,7},{7,5},{8,10},{10,8},{12,... | collective-permute-start | bytes 2359304 | tf_op jit(solution)/shard_map/ppermute | solution.py:72
  16.7 7.5 %collective-permute-start.8 = (bf16[128,1024]{1,0:T(8,128)(2,1)S(1)}, bf16[128,1024]{1,0:T(8,128)(2,1)S(1)}, u32[]{:S(2)}, u32[]{:S(2)}) collective-permute-start(bf16[128,1024]{1,0:T(8,128)(2,1)S(1)} %shard_map.125), channel_id=1, source_target_pairs={{0,1},{1,0},{2,3},{3,2},{4,5},{5,4},{6,7},{7,6},{8,9},{9,8},{10,11... | collective-permute-start | bytes 786440 | tf_op jit(solution)/shard_map/ppermute | solution.py:69
  18.5 29.5 %collective-permute-start.9 = (bf16[128,2048]{1,0:T(8,128)(2,1)S(1)}, bf16[128,2048]{1,0:T(8,128)(2,1)S(1)}, u32[]{:S(2)}, u32[]{:S(2)}) collective-permute-start(bf16[128,2048]{1,0:T(8,128)(2,1)S(1)} %collective-permute-done.7.refs_0_.refs_8_.refs_3_), channel_id=1, source_target_pairs={{0,2},{2,0},{4,6},{6,4},{1,3},{3,1},{5,7},{7,5},{8,10},{10,8},{12,... | collective-permute-start | bytes 1572872 | tf_op jit(solution)/shard_map/ppermute | solution.py:72
  24.3 23.8 %collective-permute-start.10 = (bf16[128,1024]{1,0:T(8,128)(2,1)S(1)}, bf16[128,1024]{1,0:T(8,128)(2,1)S(1)}, u32[]{:S(2)}, u32[]{:S(2)}) collective-permute-start(bf16[128,1024]{1,0:T(8,128)(2,1)S(1)} %collective-permute-done.8.refs_9_.refs_4_), channel_id=1, source_target_pairs={{0,2},{2,0},{4,6},{6,4},{1,3},{3,1},{5,7},{7,5},{8,10},{10,8},{12,... | collective-permute-start | bytes 786440 | tf_op jit(solution)/shard_map/ppermute | solution.py:72
  24.3 16.2 %copy-start.1 = (bf16[1,64,3072]{2,1,0:T(8,128)(2,1)S(1)}, bf16[1,64,3072]{2,1,0:T(8,128)(2,1)}, u32[]{:S(2)}) copy-start(bf16[1,64,3072]{2,1,0:T(8,128)(2,1)} %refs_0_.5) | copy-start | bytes 1179652
  24.3 16.2 %copy-start.4 = (f32[1,2,128]{2,1,0:T(2,128)S(1)}, f32[1,2,128]{2,1,0:T(2,128)}, u32[]{:S(2)}) copy-start(f32[1,2,128]{2,1,0:T(2,128)} %refs_2_.3) | copy-start | bytes 3076
  34.8 13.2 %copy-start = (bf16[1,1,128,3072]{3,2,1,0:T(8,128)(2,1)S(1)}, bf16[1,1,128,3072]{3,2,1,0:T(8,128)(2,1)}, u32[]{:S(2)}) copy-start(bf16[1,1,128,3072]{3,2,1,0:T(8,128)(2,1)} %param.19) | copy-start | bytes 2359300
  34.8 2.0 %collective-permute-start = (bf16[128,128]{1,0:T(8,128)(2,1)S(1)}, bf16[128,128]{1,0:T(8,128)(2,1)S(1)}, u32[]{:S(2)}, u32[]{:S(2)}) collective-permute-start(bf16[128,128]{1,0:T(8,128)(2,1)S(1)} %get-tuple-element.42.refs_4_), channel_id=1, source_target_pairs={{0,2},{2,0},{4,6},{6,4},{1,3},{3,1},{5,7},{7,5},{8,10},{10,8},{12,... | collective-permute-start | bytes 98312 | tf_op jit(solution)/shard_map/ppermute | solution.py:32
  35.4 3.9 %collective-permute-start.1 = (bf16[128,128]{1,0:T(8,128)(2,1)S(1)}, bf16[128,128]{1,0:T(8,128)(2,1)S(1)}, u32[]{:S(2)}, u32[]{:S(2)}) collective-permute-start(bf16[128,128]{1,0:T(8,128)(2,1)S(1)} %get-tuple-element.42.refs_4_), channel_id=1, source_target_pairs={{0,4},{2,6},{4,0},{6,2},{1,5},{3,7},{5,1},{7,3},{8,12},{10,14},{12... | collective-permute-start | bytes 98312 | tf_op jit(solution)/shard_map/ppermute | solution.py:32
  36.8 3.7 %collective-permute-start.2 = (bf16[128,128]{1,0:T(8,128)(2,1)S(1)}, bf16[128,128]{1,0:T(8,128)(2,1)S(1)}, u32[]{:S(2)}, u32[]{:S(2)}) collective-permute-start(bf16[128,128]{1,0:T(8,128)(2,1)S(1)} %get-tuple-element.42.refs_4_), channel_id=1, source_target_pairs={{0,6},{2,4},{4,2},{6,0},{1,7},{3,5},{5,3},{7,1},{8,14},{10,12},{12... | collective-permute-start | bytes 98312 | tf_op jit(solution)/shard_map/ppermute | solution.py:32
  43.4 1.3 %collective-permute-start.3 = (bf16[128,128]{1,0:T(8,128)(2,1)S(1)}, bf16[128,128]{1,0:T(8,128)(2,1)S(1)}, u32[]{:S(2)}, u32[]{:S(2)}) collective-permute-start(bf16[128,128]{1,0:T(8,128)(2,1)S(1)} %get-tuple-element.46), channel_id=1, source_target_pairs={{0,2},{2,0},{4,6},{6,4},{1,3},{3,1},{5,7},{7,5},{8,10},{10,8},{12,... | collective-permute-start | bytes 98312 | tf_op jit(solution)/shard_map/ppermute | solution.py:37
  43.5 3.9 %collective-permute-start.4 = (bf16[128,128]{1,0:T(8,128)(2,1)S(1)}, bf16[128,128]{1,0:T(8,128)(2,1)S(1)}, u32[]{:S(2)}, u32[]{:S(2)}) collective-permute-start(bf16[128,128]{1,0:T(8,128)(2,1)S(1)} %get-tuple-element.47), channel_id=1, source_target_pairs={{0,4},{2,6},{4,0},{6,2},{1,5},{3,7},{5,1},{7,3},{8,12},{10,14},{12... | collective-permute-start | bytes 98312 | tf_op jit(solution)/shard_map/ppermute | solution.py:37
  44.7 3.3 %collective-permute-start.5 = (bf16[128,128]{1,0:T(8,128)(2,1)S(1)}, bf16[128,128]{1,0:T(8,128)(2,1)S(1)}, u32[]{:S(2)}, u32[]{:S(2)}) collective-permute-start(bf16[128,128]{1,0:T(8,128)(2,1)S(1)} %get-tuple-element.48), channel_id=1, source_target_pairs={{0,6},{2,4},{4,2},{6,0},{1,7},{3,5},{5,3},{7,1},{8,14},{10,12},{12... | collective-permute-start | bytes 98312 | tf_op jit(solution)/shard_map/ppermute | solution.py:37
  51.3 3.9 %collective-permute-start.11 = (bf16[128,128]{1,0:T(8,128)(2,1)S(1)}, bf16[128,128]{1,0:T(8,128)(2,1)S(1)}, u32[]{:S(2)}, u32[]{:S(2)}) collective-permute-start(bf16[128,128]{1,0:T(8,128)(2,1)S(1)} %get-tuple-element.50.refs_0_), channel_id=1, source_target_pairs={{0,8},{1,9},{2,10},{3,11},{4,12},{5,13},{6,14},{7,15}} | collective-permute-start | bytes 98312 | tf_op jit(solution)/shard_map/ppermute | solution.py:902
  52.6 2.9 %collective-permute-start.12 = (bf16[128,128]{1,0:T(8,128)(2,1)S(1)}, bf16[128,128]{1,0:T(8,128)(2,1)S(1)}, u32[]{:S(2)}, u32[]{:S(2)}) collective-permute-start(bf16[128,128]{1,0:T(8,128)(2,1)S(1)} %get-tuple-element.50.refs_0_), channel_id=1, source_target_pairs={{0,16},{1,17},{2,18},{3,19},{4,20},{5,21},{6,22},{7,23}} | collective-permute-start | bytes 98312 | tf_op jit(solution)/shard_map/ppermute | solution.py:902
  53.9 2.9 %collective-permute-start.13 = (bf16[128,128]{1,0:T(8,128)(2,1)S(1)}, bf16[128,128]{1,0:T(8,128)(2,1)S(1)}, u32[]{:S(2)}, u32[]{:S(2)}) collective-permute-start(bf16[128,128]{1,0:T(8,128)(2,1)S(1)} %get-tuple-element.50.refs_0_), channel_id=1, source_target_pairs={{0,24},{1,25},{2,26},{3,27},{4,28},{5,29},{6,30},{7,31}} | collective-permute-start | bytes 98312 | tf_op jit(solution)/shard_map/ppermute | solution.py:902
  56.8 1.9 %collective-permute-start.14 = (bf16[128,64]{1,0:T(8,128)(2,1)S(1)}, bf16[128,64]{1,0:T(8,128)(2,1)S(1)}, u32[]{:S(2)}, u32[]{:S(2)}) collective-permute-start(bf16[128,64]{1,0:T(8,128)(2,1)S(1)} %get-tuple-element.51.refs_3_.refs_8_), channel_id=1, source_target_pairs={{0,2},{2,0},{4,6},{6,4},{1,3},{3,1},{5,7},{7,5},{8,10},{10,8},{12,... | collective-permute-start | bytes 49160 | tf_op jit(solution)/shard_map/ppermute | solution.py:32
  56.9 4.0 %collective-permute-start.15 = (bf16[128,64]{1,0:T(8,128)(2,1)S(1)}, bf16[128,64]{1,0:T(8,128)(2,1)S(1)}, u32[]{:S(2)}, u32[]{:S(2)}) collective-permute-start(bf16[128,64]{1,0:T(8,128)(2,1)S(1)} %get-tuple-element.51.refs_3_.refs_8_), channel_id=1, source_target_pairs={{0,4},{2,6},{4,0},{6,2},{1,5},{3,7},{5,1},{7,3},{8,12},{10,14},{12... | collective-permute-start | bytes 49160 | tf_op jit(solution)/shard_map/ppermute | solution.py:32
  57.9 3.4 %collective-permute-start.16 = (bf16[128,64]{1,0:T(8,128)(2,1)S(1)}, bf16[128,64]{1,0:T(8,128)(2,1)S(1)}, u32[]{:S(2)}, u32[]{:S(2)}) collective-permute-start(bf16[128,64]{1,0:T(8,128)(2,1)S(1)} %get-tuple-element.51.refs_3_.refs_8_), channel_id=1, source_target_pairs={{0,6},{2,4},{4,2},{6,0},{1,7},{3,5},{5,3},{7,1},{8,14},{10,12},{12... | collective-permute-start | bytes 49160 | tf_op jit(solution)/shard_map/ppermute | solution.py:32
  61.2 1.9 %collective-permute-start.17 = (bf16[128,128]{1,0:T(8,128)(2,1)S(1)}, bf16[128,128]{1,0:T(8,128)(2,1)S(1)}, u32[]{:S(2)}, u32[]{:S(2)}) collective-permute-start(bf16[128,128]{1,0:T(8,128)(2,1)S(1)} %get-tuple-element.58), channel_id=1, source_target_pairs={{0,2},{2,0},{4,6},{6,4},{1,3},{3,1},{5,7},{7,5},{8,10},{10,8},{12,... | collective-permute-start | bytes 98312 | tf_op jit(solution)/shard_map/ppermute | solution.py:37
  61.5 3.9 %collective-permute-start.18 = (bf16[128,128]{1,0:T(8,128)(2,1)S(1)}, bf16[128,128]{1,0:T(8,128)(2,1)S(1)}, u32[]{:S(2)}, u32[]{:S(2)}) collective-permute-start(bf16[128,128]{1,0:T(8,128)(2,1)S(1)} %get-tuple-element.59), channel_id=1, source_target_pairs={{0,4},{2,6},{4,0},{6,2},{1,5},{3,7},{5,1},{7,3},{8,12},{10,14},{12... | collective-permute-start | bytes 98312 | tf_op jit(solution)/shard_map/ppermute | solution.py:37
  62.6 3.4 %collective-permute-start.19 = (bf16[128,128]{1,0:T(8,128)(2,1)S(1)}, bf16[128,128]{1,0:T(8,128)(2,1)S(1)}, u32[]{:S(2)}, u32[]{:S(2)}) collective-permute-start(bf16[128,128]{1,0:T(8,128)(2,1)S(1)} %get-tuple-element.60), channel_id=1, source_target_pairs={{0,6},{2,4},{4,2},{6,0},{1,7},{3,5},{5,3},{7,1},{8,14},{10,12},{12... | collective-permute-start | bytes 98312 | tf_op jit(solution)/shard_map/ppermute | solution.py:37
  66.0 26.3 %copy-start.2 = (bf16[4,128,128]{2,1,0:T(8,128)(2,1)S(1)}, bf16[4,128,128]{2,1,0:T(8,128)(2,1)}, u32[]{:S(2)}) copy-start(bf16[4,128,128]{2,1,0:T(8,128)(2,1)} %get-tuple-element.68.refs_5_) | copy-start | bytes 393220
  66.0 26.3 %copy-start.3 = (f32[128,128]{1,0:T(8,128)S(1)}, f32[128,128]{1,0:T(8,128)}, u32[]{:S(2)}) copy-start(f32[128,128]{1,0:T(8,128)} %get-tuple-element.69.refs_6_) | copy-start | bytes 196612
  66.0 31.6 %copy-start.5 = (f32[1,9216]{1,0:T(1,128)S(1)}, f32[1,9216]{1,0:T(1,128)}, u32[]{:S(2)}) copy-start(f32[1,9216]{1,0:T(1,128)} %get-tuple-element.49.refs_12_) | copy-start | bytes 110596
  66.1 1.9 %collective-permute-start.20 = (bf16[128,128]{1,0:T(8,128)(2,1)S(1)}, bf16[128,128]{1,0:T(8,128)(2,1)S(1)}, u32[]{:S(2)}, u32[]{:S(2)}) collective-permute-start(bf16[128,128]{1,0:T(8,128)(2,1)S(1)} %get-tuple-element.63), channel_id=1, source_target_pairs={{0,2},{2,0},{4,6},{6,4},{1,3},{3,1},{5,7},{7,5},{8,10},{10,8},{12,... | collective-permute-start | bytes 98312 | tf_op jit(solution)/shard_map/ppermute | solution.py:37
  66.2 3.9 %collective-permute-start.21 = (bf16[128,128]{1,0:T(8,128)(2,1)S(1)}, bf16[128,128]{1,0:T(8,128)(2,1)S(1)}, u32[]{:S(2)}, u32[]{:S(2)}) collective-permute-start(bf16[128,128]{1,0:T(8,128)(2,1)S(1)} %get-tuple-element.64), channel_id=1, source_target_pairs={{0,4},{2,6},{4,0},{6,2},{1,5},{3,7},{5,1},{7,3},{8,12},{10,14},{12... | collective-permute-start | bytes 98312 | tf_op jit(solution)/shard_map/ppermute | solution.py:37
  67.2 3.4 %collective-permute-start.22 = (bf16[128,128]{1,0:T(8,128)(2,1)S(1)}, bf16[128,128]{1,0:T(8,128)(2,1)S(1)}, u32[]{:S(2)}, u32[]{:S(2)}) collective-permute-start(bf16[128,128]{1,0:T(8,128)(2,1)S(1)} %get-tuple-element.65), channel_id=1, source_target_pairs={{0,6},{2,4},{4,2},{6,0},{1,7},{3,5},{5,3},{7,1},{8,14},{10,12},{12... | collective-permute-start | bytes 98312 | tf_op jit(solution)/shard_map/ppermute | solution.py:37
  70.6 14.9 %collective-permute-start.25 = (bf16[2,128,64]{2,1,0:T(8,128)(2,1)S(1)}, bf16[2,128,64]{2,1,0:T(8,128)(2,1)S(1)}, u32[]{:S(2)}, u32[]{:S(2)}) collective-permute-start(bf16[2,128,64]{2,1,0:T(8,128)(2,1)S(1)} %get-tuple-element.73), channel_id=1, source_target_pairs={{0,2},{2,0},{4,6},{6,4},{1,3},{3,1},{5,7},{7,5},{8,10},{10,8},{12,... | collective-permute-start | bytes 98312 | tf_op jit(solution)/shard_map/ppermute | solution.py:946
  70.8 17.2 %collective-permute-start.23 = (bf16[160,64]{1,0:T(8,128)(2,1)S(1)}, bf16[160,64]{1,0:T(8,128)(2,1)S(1)}, u32[]{:S(2)}, u32[]{:S(2)}) collective-permute-start(bf16[160,64]{1,0:T(8,128)(2,1)S(1)} %get-tuple-element.66), channel_id=1, source_target_pairs={{0,8},{8,0},{16,24},{24,16},{1,9},{9,1},{17,25},{25,17},{2,10},{10... | collective-permute-start | bytes 61448 | tf_op jit(solution)/shard_map/ppermute | solution.py:947
  75.4 12.5 %collective-permute-start.24 = (bf16[128,64]{1,0:T(8,128)(2,1)S(1)}, bf16[128,64]{1,0:T(8,128)(2,1)S(1)}, u32[]{:S(2)}, u32[]{:S(2)}) collective-permute-start(bf16[128,64]{1,0:T(8,128)(2,1)S(1)} %get-tuple-element.61.refs_7_), channel_id=1, source_target_pairs={{0,16},{8,24},{16,0},{24,8},{1,17},{9,25},{17,1},{25,9},{2,18},{10... | collective-permute-start | bytes 49160 | tf_op jit(solution)/shard_map/ppermute | solution.py:936
  85.5 5.8 %collective-permute-start.26 = (bf16[128,64]{1,0:T(8,128)(2,1)S(1)}, bf16[128,64]{1,0:T(8,128)(2,1)S(1)}, u32[]{:S(2)}, u32[]{:S(2)}) collective-permute-start(bf16[128,64]{1,0:T(8,128)(2,1)S(1)} %get-tuple-element.74), channel_id=1, source_target_pairs={{0,8},{2,10},{4,12},{6,14},{8,16},{10,18},{12,20},{14,22},{16,24},... | collective-permute-start | bytes 49160 | tf_op jit(solution)/shard_map/ppermute | solution.py:950
  85.6 6.6 %collective-permute-start.27 = (bf16[128,64]{1,0:T(8,128)(2,1)S(1)}, bf16[128,64]{1,0:T(8,128)(2,1)S(1)}, u32[]{:S(2)}, u32[]{:S(2)}) collective-permute-start(bf16[128,64]{1,0:T(8,128)(2,1)S(1)} %get-tuple-element.75), channel_id=1, source_target_pairs={{0,12},{2,14},{4,8},{6,10},{8,20},{10,22},{12,16},{14,18},{16,28},... | collective-permute-start | bytes 49160 | tf_op jit(solution)/shard_map/ppermute | solution.py:950
  92.7 1.3 %collective-permute-start.32 = (bf16[5,64,128]{2,1,0:T(8,128)(2,1)S(1)}, bf16[5,64,128]{2,1,0:T(8,128)(2,1)S(1)}, u32[]{:S(2)}, u32[]{:S(2)}) collective-permute-start(bf16[5,64,128]{2,1,0:T(8,128)(2,1)S(1)} %get-tuple-element.77), channel_id=1, source_target_pairs={{0,2},{2,0},{4,6},{6,4},{1,3},{3,1},{5,7},{7,5},{8,10},{10,8},{12,... | collective-permute-start | bytes 245768 | tf_op jit(solution)/shard_map/ppermute | solution.py:985
  94.1 19.1 %collective-permute-start.33 = (bf16[5,64,128]{2,1,0:T(8,128)(2,1)S(1)}, bf16[5,64,128]{2,1,0:T(8,128)(2,1)S(1)}, u32[]{:S(2)}, u32[]{:S(2)}) collective-permute-start(bf16[5,64,128]{2,1,0:T(8,128)(2,1)S(1)} %add_convert_fusion.refs_8_), channel_id=1, source_target_pairs={{0,4},{1,5},{2,6},{3,7},{4,0},{5,1},{6,2},{7,3},{8,12},{9,13},{10,... | collective-permute-start | bytes 245768 | tf_op jit(solution)/shard_map/ppermute | solution.py:997
  95.3 17.9 %collective-permute-start.34 = (bf16[5,64,128]{2,1,0:T(8,128)(2,1)S(1)}, bf16[5,64,128]{2,1,0:T(8,128)(2,1)S(1)}, u32[]{:S(2)}, u32[]{:S(2)}) collective-permute-start(bf16[5,64,128]{2,1,0:T(8,128)(2,1)S(1)} %add_convert_fusion.refs_8_), channel_id=1, source_target_pairs={{0,1},{1,0},{2,3},{3,2},{4,5},{5,4},{6,7},{7,6},{8,9},{9,8},{10,11... | collective-permute-start | bytes 245768 | tf_op jit(solution)/shard_map/ppermute | solution.py:997
  96.8 16.4 %collective-permute-start.35 = (bf16[5,64,128]{2,1,0:T(8,128)(2,1)S(1)}, bf16[5,64,128]{2,1,0:T(8,128)(2,1)S(1)}, u32[]{:S(2)}, u32[]{:S(2)}) collective-permute-start(bf16[5,64,128]{2,1,0:T(8,128)(2,1)S(1)} %add_convert_fusion.refs_8_), channel_id=1, source_target_pairs={{0,5},{1,4},{2,7},{3,6},{4,1},{5,0},{6,3},{7,2},{8,13},{9,12},{10,... | collective-permute-start | bytes 245768 | tf_op jit(solution)/shard_map/ppermute | solution.py:997
  97.7 3.9 %collective-permute-start.28 = (bf16[128,64]{1,0:T(8,128)(2,1)S(1)}, bf16[128,64]{1,0:T(8,128)(2,1)S(1)}, u32[]{:S(2)}, u32[]{:S(2)}) collective-permute-start(bf16[128,64]{1,0:T(8,128)(2,1)S(1)} %get-tuple-element.76.refs_0_), channel_id=1, source_target_pairs={{0,8},{8,0},{16,24},{24,16},{1,9},{9,1},{17,25},{25,17},{2,10},{10... | collective-permute-start | bytes 49160 | tf_op jit(solution)/shard_map/ppermute | solution.py:981
  97.7 15.5 %collective-permute-start.31 = (f32[1,9216]{1,0:T(1,128)S(1)}, f32[1,9216]{1,0:T(1,128)S(1)}, u32[]{:S(2)}, u32[]{:S(2)}) collective-permute-start(f32[1,9216]{1,0:T(1,128)S(1)} %copy-done.5), channel_id=1, source_target_pairs={{0,1},{1,0},{2,3},{3,2},{4,5},{5,4},{6,7},{7,6},{8,9},{9,8},{10,11... | collective-permute-start | bytes 110600 | tf_op jit(solution)/shard_map/ppermute | solution.py:32
  101.6 5.1 %collective-permute-start.29 = (bf16[128,64]{1,0:T(8,128)(2,1)S(1)}, bf16[128,64]{1,0:T(8,128)(2,1)S(1)}, u32[]{:S(2)}, u32[]{:S(2)}) collective-permute-start(bf16[128,64]{1,0:T(8,128)(2,1)S(1)} %get-tuple-element.76.refs_0_), channel_id=1, source_target_pairs={{0,16},{8,24},{16,0},{24,8},{1,17},{9,25},{17,1},{25,9},{2,18},{10... | collective-permute-start | bytes 49160 | tf_op jit(solution)/shard_map/ppermute | solution.py:980
  106.7 5.7 %collective-permute-start.30 = (bf16[128,64]{1,0:T(8,128)(2,1)S(1)}, bf16[128,64]{1,0:T(8,128)(2,1)S(1)}, u32[]{:S(2)}, u32[]{:S(2)}) collective-permute-start(bf16[128,64]{1,0:T(8,128)(2,1)S(1)} %get-tuple-element.76.refs_0_), channel_id=1, source_target_pairs={{0,24},{8,16},{16,8},{24,0},{1,25},{9,17},{17,9},{25,1},{2,26},{10... | collective-permute-start | bytes 49160 | tf_op jit(solution)/shard_map/ppermute | solution.py:979

commit v13 on v12

--- a/solution.py
+++ b/solution.py
@@ -419,14 +419,21 @@
         )
 
 
-def tail(late, latent, embed_w, final_t, mixed, heads_w, work):
+def tail(late, latent, embed_w, final_t, mixed, heads_w, work, stacked, keep):
     model_width = embed_w.shape[2]
     block = latent[...]
-    joined_heads = jnp.concatenate([piece[...] for piece in mixed], axis=1)
+    if stacked:
+        joined_heads = jnp.concatenate([piece[...] for piece in mixed], axis=1)
     sums = None
     for first in range(0, model_width, TILE):
         span = slice(first, first + TILE)
-        attended = dot32(joined_heads, stacked_tile(heads_w, first))
+        if stacked:
+            attended = dot32(joined_heads, stacked_tile(heads_w, first))
+        else:
+            attended = None
+            for piece, pieces in zip(mixed, heads_w):
+                product = dot32(piece[...], head_tile(pieces, first, TILE))
+                attended = product if attended is None else attended + product
         mod = late.ready()
         residual = (
             dot32(block, embed_w[0, :, span]) + slot_of(mod, 0, model_width, first, TILE) * attended
@@ -443,6 +450,7 @@
         part = lane_sum(middle * middle)
         sums = part if sums is None else sums + part
     inverse = lax.rsqrt(jnp.sum(sums, axis=1, keepdims=True) / model_width + EPS)
+    keep(inverse)
     result = None
     final_w = final_t.ready()
     for first in range(0, model_width, TILE):
@@ -475,21 +483,28 @@
         ]
         for copy in copies:
             copy.start()
-        velocity, inverse = tail(late, latent, embed_w, final_t, mixed, heads_w, work)
-        student_step, critic_step = steps_of(times)
-        sigma_student, sigma_critic = noise_level(student_step), noise_level(critic_step)
-        rows, lanes = inverse_ref.shape
-        rest = (lanes - latent_width) // 2
-        inverse_ref[...] = jnp.concatenate(
-            [
-                jnp.broadcast_to(inverse, (rows, latent_width)),
-                jnp.broadcast_to(sigma_student, (rows, rest)),
-                jnp.broadcast_to(sigma_critic, (rows, rest)),
-            ],
-            axis=1,
-        )
-        copies.append(pltpu.make_async_copy(inverse_ref, inverse_out, sends.at[count]))
-        copies[-1].start()
+        levels = []
+
+        def keep(inverse):
+            levels.extend(noise_level(step) for step in steps_of(times))
+            sigma_student, sigma_critic = levels
+            rows, lanes = inverse_ref.shape
+            rest = (lanes - latent_width) // 2
+            inverse_ref[...] = jnp.concatenate(
+                [
+                    jnp.broadcast_to(inverse, (rows, latent_width)),
+                    jnp.broadcast_to(sigma_student, (rows, rest)),
+                    jnp.broadcast_to(sigma_critic, (rows, rest)),
+                ],
+                axis=1,
+            )
+            copies.append(pltpu.make_async_copy(inverse_ref, inverse_out, sends.at[count]))
+            copies[-1].start()
+
+        velocity, _ = tail(
+            late, latent, embed_w, final_t, mixed, heads_w, work, stacked=True, keep=keep
+        )
+        sigma_student, sigma_critic = levels
         sample = latent[...].astype(jnp.float32) - sigma_student * velocity
         second = noise.ready()[:, latent_width:].astype(jnp.float32)
         critic = (1.0 - sigma_critic) * sample + sigma_critic * second
@@ -528,7 +543,17 @@
         both = pair[...].astype(jnp.float32)
         sample = both[:, latent_width:]
         latent[...] = pair[:, :latent_width]
-        result, inverse = tail(late, latent, embed_w, final_t, mixed, heads_w, work)
+        result, inverse = tail(
+            late,
+            latent,
+            embed_w,
+            final_t,
+            mixed,
+            heads_w,
+            work,
+            stacked=False,
+            keep=lambda inverse: None,
+        )
         mod, final_w = late.ready(), final_t.ready()
         _, critic_step = steps_of(times)
         sigma_critic = noise_level(critic_step)

time: 117 us -> 116 us (level)
  no operation moved by 1% of the time
where the time goes in v13:
time: 116 us
  waiting for transfers between devices  51.2 us (44%)
  starting transfers between devices  42.3 us (36%)
  Pallas kernels  21.3 us (18%)
    pallas_call x13, Pallas kernels, run(): pl.pallas_call(body, out_shape=list(outputs) + [pltpu.HBM(item.shape, ite...  21.3 us
    ppermute x1, waiting for transfers between devices, spread_heads(): near = lax.ppermute(part, 'seq', swaps(count, bit))  11.9 us
    ppermute x1, starting transfers between devices, step(): fake = lax.ppermute(term_rows, 'segment', swaps(sections, 2))  10.1 us
    ppermute x9, waiting for transfers between devices, scatter_near(): lax.ppermute(blocks[offset], axis, swaps(count, offset))  8.42 us
    ppermute x7, starting transfers between devices, gather_near(): lax.ppermute(value, axis, swaps(count, offset))  6.23 us
    ppermute x1, waiting for transfers between devices, spread_heads(): held[bit] = [near, lax.ppermute(stage(near), 'dp', swaps(groups, 1))]  5.76 us
    ppermute x9, starting transfers between devices, scatter_near(): lax.ppermute(blocks[offset], axis, swaps(count, offset))  5.45 us
    ppermute x7, waiting for transfers between devices, gather_near(): lax.ppermute(value, axis, swaps(count, offset))  5.36 us
  transfers between devices with their start and end apart: 36, of which 22 were waited for; matrix products, arithmetic and copies ran while one was open for 0% of the time, Pallas kernels for 12%

profile of v13, /device:TPU:0, one launch (start us, length us, event | category | flops | bytes accessed | tf_op | source)
XLA Modules:
  0.0 115.8 jit_solution(11285462895025389108)
XLA Ops:
  0.6 1.1 shard_map.124
  1.7 3.1 %collective-permute-start.7 = (bf16[128,2048]{1,0:T(8,128)(2,1)S(1)}, bf16[128,2048]{1,0:T(8,128)(2,1)S(1)}, u32[]{:S(2)}, u32[]{:S(2)}) collective-permute-start(bf16[128,2048]{1,0:T(8,128)(2,1)S(1)} %shard_map.124), channel_id=1, source_target_pairs={{0,4},{2,6},{4,0},{6,2},{1,5},{3,7},{5,1},{7,3},{8,12},{10,14},{12... | collective-permute-start | bytes 1572872 | tf_op jit(solution)/shard_map/ppermute | solution.py:68
  4.8 0.0 collective-permute-start.6
  4.8 11.9 %collective-permute-done.7.refs_0_.refs_8_.refs_3_ = bf16[128,2048]{1,0:T(8,128)(2,1)S(1)} collective-permute-done((bf16[128,2048]{1,0:T(8,128)(2,1)S(1)}, bf16[128,2048]{1,0:T(8,128)(2,1)S(1)}, u32[]{:S(2)}, u32[]{:S(2)}) %collective-permute-start.7) | collective-permute-done | bytes 524320 | tf_op jit(solution)/shard_map/ppermute | solution.py:68
  16.7 1.8 %collective-permute-start.8 = (bf16[128,1024]{1,0:T(8,128)(2,1)S(1)}, bf16[128,1024]{1,0:T(8,128)(2,1)S(1)}, u32[]{:S(2)}, u32[]{:S(2)}) collective-permute-start(bf16[128,1024]{1,0:T(8,128)(2,1)S(1)} %shard_map.125), channel_id=1, source_target_pairs={{0,1},{1,0},{2,3},{3,2},{4,5},{5,4},{6,7},{7,6},{8,9},{9,8},{10,11... | collective-permute-start | bytes 786440 | tf_op jit(solution)/shard_map/ppermute | solution.py:69
  18.5 5.8 %collective-permute-done.8.refs_9_.refs_4_ = bf16[128,1024]{1,0:T(8,128)(2,1)S(1)} collective-permute-done((bf16[128,1024]{1,0:T(8,128)(2,1)S(1)}, bf16[128,1024]{1,0:T(8,128)(2,1)S(1)}, u32[]{:S(2)}, u32[]{:S(2)}) %collective-permute-start.8) | collective-permute-done | bytes 262176 | tf_op jit(solution)/shard_map/ppermute | solution.py:69
  24.3 0.0 collective-permute-start.10
  24.3 10.5 %shard_map.122 = (bf16[128,128]{1,0:T(8,128)(2,1)S(1)}, bf16[128,64]{1,0:T(8,128)(2,1)S(1)}, bf16[3,3072,128]{2,1,0:T(8,128)(2,1)S(1)}, bf16[2,64,64]{2,1,0:T(8,128)(2,1)S(1)}) custom-call(s32[2,2]{1,0:T(2,128)} %refs_15_.3, f32[1,256]{1,0:T(1,128)} %refs_1_.3, bf16[256,3072]{1,0:T(8,128)(2,1)} %bitcast.26, bf16[64,128]{1,0:T(8,128)(2,1)} %bitcast.34, ...), custom_call_target="tpu_custom_call" | custom-call | flops 23592960 | bytes 4441104 | tf_op jit(solution)/shard_map/pallas_call | solution.py:207
  34.8 0.0 copy-start
  34.8 0.6 collective-permute-start
  35.4 1.5 %collective-permute-start.1 = (bf16[128,128]{1,0:T(8,128)(2,1)S(1)}, bf16[128,128]{1,0:T(8,128)(2,1)S(1)}, u32[]{:S(2)}, u32[]{:S(2)}) collective-permute-start(bf16[128,128]{1,0:T(8,128)(2,1)S(1)} %get-tuple-element.42.refs_4_), channel_id=1, source_target_pairs={{0,4},{2,6},{4,0},{6,2},{1,5},{3,7},{5,1},{7,3},{8,12},{10,14},{12... | collective-permute-start | bytes 98312 | tf_op jit(solution)/shard_map/ppermute | solution.py:32
  36.8 0.8 collective-permute-start.2
  37.6 1.6 %collective-permute-done.1.refs_6_ = bf16[128,128]{1,0:T(8,128)(2,1)S(1)} collective-permute-done((bf16[128,128]{1,0:T(8,128)(2,1)S(1)}, bf16[128,128]{1,0:T(8,128)(2,1)S(1)}, u32[]{:S(2)}, u32[]{:S(2)}) %collective-permute-start.1) | collective-permute-done | bytes 32800 | tf_op jit(solution)/shard_map/ppermute | solution.py:32
  39.3 1.2 %collective-permute-done.2.refs_7_ = bf16[128,128]{1,0:T(8,128)(2,1)S(1)} collective-permute-done((bf16[128,128]{1,0:T(8,128)(2,1)S(1)}, bf16[128,128]{1,0:T(8,128)(2,1)S(1)}, u32[]{:S(2)}, u32[]{:S(2)}) %collective-permute-start.2) | collective-permute-done | bytes 32800 | tf_op jit(solution)/shard_map/ppermute | solution.py:32
  40.5 2.9 %shard_map.123 = (bf16[128,128]{1,0:T(8,128)(2,1)S(1)}, bf16[128,128]{1,0:T(8,128)(2,1)S(1)}, bf16[128,128]{1,0:T(8,128)(2,1)S(1)}, bf16[128,128]{1,0:T(8,128)(2...) custom-call(bf16[1,64,3072]{2,1,0:T(8,128)(2,1)S(1)} %copy-done.1, ...), custom_call_target="tpu_custom_call" | custom-call | flops 301989888 | bytes 3154944 | tf_op jit(solution)/shard_map/pallas_call | solution.py:207
  43.4 0.2 collective-permute-start.3
  43.5 0.8 collective-permute-start.4
  44.3 0.3 collective-permute-done.3.refs_3_
  44.7 0.7 collective-permute-start.5
  45.3 2.1 %collective-permute-done.4.refs_4_ = bf16[128,128]{1,0:T(8,128)(2,1)S(1)} collective-permute-done((bf16[128,128]{1,0:T(8,128)(2,1)S(1)}, bf16[128,128]{1,0:T(8,128)(2,1)S(1)}, u32[]{:S(2)}, u32[]{:S(2)}) %collective-permute-start.4) | collective-permute-done | bytes 32800 | tf_op jit(solution)/shard_map/ppermute | solution.py:37
  47.5 0.5 collective-permute-done.5.refs_5_
  48.0 2.7 %shard_map.126 = (bf16[128,128]{1,0:T(8,128)(2,1)S(1)}, bf16[4,128,128]{2,1,0:T(8,128)(2,1)}, f32[128,128]{1,0:T(8,128)}) custom-call(bf16[128,64]{1,0:T(8,128)(2,1)S(1)} %get-tuple-element.44.refs_0_.refs_3_, bf16[1,64,3072]{2,1,0:T(8,128)(2,1)S(1)} %copy-done.1, bf16[128,128]{1,0:T(8,128)(2,1)S(1)} %get-tuple-element.45.refs_2_, ...), custom_call_target="tpu_custom_call" | custom-call | flops 402653184 | bytes 4182032 | tf_op jit(solution)/shard_map/pallas_call | solution.py:207
  50.8 1.3 %collective-permute-start.11 = (bf16[128,128]{1,0:T(8,128)(2,1)S(1)}, bf16[128,128]{1,0:T(8,128)(2,1)S(1)}, u32[]{:S(2)}, u32[]{:S(2)}) collective-permute-start(bf16[128,128]{1,0:T(8,128)(2,1)S(1)} %get-tuple-element.50.refs_0_), channel_id=1, source_target_pairs={{0,8},{1,9},{2,10},{3,11},{4,12},{5,13},{6,14},{7,15}} | collective-permute-start | bytes 98312 | tf_op jit(solution)/shard_map/ppermute | solution.py:927
  52.1 1.3 %collective-permute-start.12 = (bf16[128,128]{1,0:T(8,128)(2,1)S(1)}, bf16[128,128]{1,0:T(8,128)(2,1)S(1)}, u32[]{:S(2)}, u32[]{:S(2)}) collective-permute-start(bf16[128,128]{1,0:T(8,128)(2,1)S(1)} %get-tuple-element.50.refs_0_), channel_id=1, source_target_pairs={{0,16},{1,17},{2,18},{3,19},{4,20},{5,21},{6,22},{7,23}} | collective-permute-start | bytes 98312 | tf_op jit(solution)/shard_map/ppermute | solution.py:927
  53.4 1.3 %collective-permute-start.13 = (bf16[128,128]{1,0:T(8,128)(2,1)S(1)}, bf16[128,128]{1,0:T(8,128)(2,1)S(1)}, u32[]{:S(2)}, u32[]{:S(2)}) collective-permute-start(bf16[128,128]{1,0:T(8,128)(2,1)S(1)} %get-tuple-element.50.refs_0_), channel_id=1, source_target_pairs={{0,24},{1,25},{2,26},{3,27},{4,28},{5,29},{6,30},{7,31}} | collective-permute-start | bytes 98312 | tf_op jit(solution)/shard_map/ppermute | solution.py:927
  54.7 0.3 collective-permute-done.12.refs_2_
  54.9 1.3 %collective-permute-done.13.refs_3_ = bf16[128,128]{1,0:T(8,128)(2,1)S(1)} collective-permute-done((bf16[128,128]{1,0:T(8,128)(2,1)S(1)}, bf16[128,128]{1,0:T(8,128)(2,1)S(1)}, u32[]{:S(2)}, u32[]{:S(2)}) %collective-permute-start.13) | collective-permute-done | bytes 32800 | tf_op jit(solution)/shard_map/ppermute | solution.py:927
  56.3 0.1 collective-permute-start.14
  56.3 1.0 collective-permute-start.15
  57.3 0.9 collective-permute-start.16
  58.2 2.1 %collective-permute-done.15.refs_5_.refs_10_ = bf16[128,64]{1,0:T(8,128)(2,1)S(1)} collective-permute-done((bf16[128,64]{1,0:T(8,128)(2,1)S(1)}, bf16[128,64]{1,0:T(8,128)(2,1)S(1)}, u32[]{:S(2)}, u32[]{:S(2)}) %collective-permute-start.15) | collective-permute-done | bytes 16416 | tf_op jit(solution)/shard_map/ppermute | solution.py:32
  60.3 0.4 collective-permute-done.16.refs_6_.refs_11_
  60.7 0.2 collective-permute-start.17
  60.9 1.1 collective-permute-start.18
  62.0 0.6 collective-permute-start.19
  62.6 2.2 %collective-permute-done.18.refs_4_.refs_10_ = bf16[128,128]{1,0:T(8,128)(2,1)S(1)} collective-permute-done((bf16[128,128]{1,0:T(8,128)(2,1)S(1)}, bf16[128,128]{1,0:T(8,128)(2,1)S(1)}, u32[]{:S(2)}, u32[]{:S(2)}) %collective-permute-start.18) | collective-permute-done | bytes 32800 | tf_op jit(solution)/shard_map/ppermute | solution.py:37
  64.8 0.6 collective-permute-done.19.refs_5_.refs_11_
  65.5 0.2 collective-permute-start.20
  65.7 0.9 collective-permute-start.21
  66.6 0.8 collective-permute-start.22
  67.5 2.2 %collective-permute-done.21.refs_14_ = bf16[128,128]{1,0:T(8,128)(2,1)S(1)} collective-permute-done((bf16[128,128]{1,0:T(8,128)(2,1)S(1)}, bf16[128,128]{1,0:T(8,128)(2,1)S(1)}, u32[]{:S(2)}, u32[]{:S(2)}) %collective-permute-start.21) | collective-permute-done | bytes 32800 | tf_op jit(solution)/shard_map/ppermute | solution.py:37
  69.6 0.4 collective-permute-done.22.refs_15_
  70.0 0.2 collective-permute-start.25
  70.2 4.8 %collective-permute-start.23 = (bf16[160,64]{1,0:T(8,128)(2,1)S(1)}, bf16[160,64]{1,0:T(8,128)(2,1)S(1)}, u32[]{:S(2)}, u32[]{:S(2)}) collective-permute-start(bf16[160,64]{1,0:T(8,128)(2,1)S(1)} %get-tuple-element.66), channel_id=1, source_target_pairs={{0,8},{8,0},{16,24},{24,16},{1,9},{9,1},{17,25},{25,17},{2,10},{10... | collective-permute-start | bytes 61448 | tf_op jit(solution)/shard_map/ppermute | solution.py:972
  75.0 10.1 %collective-permute-start.24 = (bf16[128,64]{1,0:T(8,128)(2,1)S(1)}, bf16[128,64]{1,0:T(8,128)(2,1)S(1)}, u32[]{:S(2)}, u32[]{:S(2)}) collective-permute-start(bf16[128,64]{1,0:T(8,128)(2,1)S(1)} %get-tuple-element.61.refs_7_), channel_id=1, source_target_pairs={{0,16},{8,24},{16,0},{24,8},{1,17},{9,25},{17,1},{25,9},{2,18},{10... | collective-permute-start | bytes 49160 | tf_op jit(solution)/shard_map/ppermute | solution.py:961
  85.2 0.1 collective-permute-start.26
  85.3 1.0 collective-permute-start.27
  86.3 1.3 %collective-permute-done.24.refs_1_ = bf16[128,64]{1,0:T(8,128)(2,1)S(1)} collective-permute-done((bf16[128,64]{1,0:T(8,128)(2,1)S(1)}, bf16[128,64]{1,0:T(8,128)(2,1)S(1)}, u32[]{:S(2)}, u32[]{:S(2)}) %collective-permute-start.24) | collective-permute-done | bytes 16416 | tf_op jit(solution)/shard_map/ppermute | solution.py:961
  87.6 3.3 %collective-permute-done.26.refs_12_ = bf16[128,64]{1,0:T(8,128)(2,1)S(1)} collective-permute-done((bf16[128,64]{1,0:T(8,128)(2,1)S(1)}, bf16[128,64]{1,0:T(8,128)(2,1)S(1)}, u32[]{:S(2)}, u32[]{:S(2)}) %collective-permute-start.26) | collective-permute-done | bytes 16416 | tf_op jit(solution)/shard_map/ppermute | solution.py:975
  90.9 1.0 collective-permute-done.27.refs_13_
  91.9 0.5 shard_map.132
  92.4 0.1 collective-permute-start.32
  92.5 1.3 %collective-permute-done.32 = bf16[5,64,128]{2,1,0:T(8,128)(2,1)S(1)} collective-permute-done((bf16[5,64,128]{2,1,0:T(8,128)(2,1)S(1)}, bf16[5,64,128]{2,1,0:T(8,128)(2,1)S(1)}, u32[]{:S(2)}, u32[]{:S(2)}) %collective-permute-start.32) | collective-permute-done | bytes 81952 | tf_op jit(solution)/shard_map/ppermute | solution.py:1010
  93.8 1.1 collective-permute-start.33
  94.9 1.5 %collective-permute-start.34 = (bf16[5,64,128]{2,1,0:T(8,128)(2,1)S(1)}, bf16[5,64,128]{2,1,0:T(8,128)(2,1)S(1)}, u32[]{:S(2)}, u32[]{:S(2)}) collective-permute-start(bf16[5,64,128]{2,1,0:T(8,128)(2,1)S(1)} %add_convert_fusion.refs_8_), channel_id=1, source_target_pairs={{0,1},{1,0},{2,3},{3,2},{4,5},{5,4},{6,7},{7,6},{8,9},{9,8},{10,11... | collective-permute-start | bytes 245768 | tf_op jit(solution)/shard_map/ppermute | solution.py:1022
  96.4 0.9 collective-permute-start.35
  97.3 1.5 %collective-permute-start.31 = (f32[1,9216]{1,0:T(1,128)S(1)}, f32[1,9216]{1,0:T(1,128)S(1)}, u32[]{:S(2)}, u32[]{:S(2)}) collective-permute-start(f32[1,9216]{1,0:T(1,128)S(1)} %copy-done.5), channel_id=1, source_target_pairs={{0,1},{1,0},{2,3},{3,2},{4,5},{5,4},{6,7},{7,6},{8,9},{9,8},{10,11... | collective-permute-start | bytes 110600 | tf_op jit(solution)/shard_map/ppermute | solution.py:32
  98.8 2.4 %collective-permute-done.28.refs_1_ = bf16[128,64]{1,0:T(8,128)(2,1)S(1)} collective-permute-done((bf16[128,64]{1,0:T(8,128)(2,1)S(1)}, bf16[128,64]{1,0:T(8,128)(2,1)S(1)}, u32[]{:S(2)}, u32[]{:S(2)}) %collective-permute-start.28) | collective-permute-done | bytes 16416 | tf_op jit(solution)/shard_map/ppermute | solution.py:1006
  101.2 0.4 collective-permute-start.29
  101.6 4.8 %collective-permute-done.29.refs_2_ = bf16[128,64]{1,0:T(8,128)(2,1)S(1)} collective-permute-done((bf16[128,64]{1,0:T(8,128)(2,1)S(1)}, bf16[128,64]{1,0:T(8,128)(2,1)S(1)}, u32[]{:S(2)}, u32[]{:S(2)}) %collective-permute-start.29) | collective-permute-done | bytes 16416 | tf_op jit(solution)/shard_map/ppermute | solution.py:1005
  106.4 1.7 %collective-permute-start.30 = (bf16[128,64]{1,0:T(8,128)(2,1)S(1)}, bf16[128,64]{1,0:T(8,128)(2,1)S(1)}, u32[]{:S(2)}, u32[]{:S(2)}) collective-permute-start(bf16[128,64]{1,0:T(8,128)(2,1)S(1)} %get-tuple-element.76.refs_0_), channel_id=1, source_target_pairs={{0,24},{8,16},{16,8},{24,0},{1,25},{9,17},{17,9},{25,1},{2,26},{10... | collective-permute-start | bytes 49160 | tf_op jit(solution)/shard_map/ppermute | solution.py:1004
  108.0 4.1 %collective-permute-done.30.refs_3_ = bf16[128,64]{1,0:T(8,128)(2,1)S(1)} collective-permute-done((bf16[128,64]{1,0:T(8,128)(2,1)S(1)}, bf16[128,64]{1,0:T(8,128)(2,1)S(1)}, u32[]{:S(2)}, u32[]{:S(2)}) %collective-permute-start.30) | collective-permute-done | bytes 16416 | tf_op jit(solution)/shard_map/ppermute | solution.py:1004
  112.1 0.7 shard_map.133
  112.8 2.8 %shard_map.134 = f32[64,3072]{1,0:T(8,128)} custom-call(bf16[1,64,3072]{2,1,0:T(8,128)(2,1)S(1)} %copy-done.1, bf16[128,3072]{1,0:T(8,128)(2,1)S(1)} %bitcast.23, bf16[128,3072]{1,0:T(8,128)(2,1)S(1)} %collective-permute-done.6.refs_7_.refs_2_, bf16[128,2048]{1,0:T(8,128)(2,1)S(1)} %collective-permute-done.7.refs_0_.refs_8_.refs_3_, ...), custom_call_target="tpu_custom_call" | custom-call | flops 805306368 | bytes 3940352 | tf_op jit(solution)/shard_map/pallas_call | solution.py:207
  (34 shorter events, 0.2 us)
Async XLA Ops:
  1.7 15.0 %collective-permute-start.7 = (bf16[128,2048]{1,0:T(8,128)(2,1)S(1)}, bf16[128,2048]{1,0:T(8,128)(2,1)S(1)}, u32[]{:S(2)}, u32[]{:S(2)}) collective-permute-start(bf16[128,2048]{1,0:T(8,128)(2,1)S(1)} %shard_map.124), channel_id=1, source_target_pairs={{0,4},{2,6},{4,0},{6,2},{1,5},{3,7},{5,1},{7,3},{8,12},{10,14},{12... | collective-permute-start | bytes 1572872 | tf_op jit(solution)/shard_map/ppermute | solution.py:68
  4.8 43.2 %collective-permute-start.6 = (bf16[128,3072]{1,0:T(8,128)(2,1)}, bf16[128,3072]{1,0:T(8,128)(2,1)S(1)}, u32[]{:S(2)}, u32[]{:S(2)}) collective-permute-start(bf16[128,3072]{1,0:T(8,128)(2,1)} %bitcast.20), channel_id=1, source_target_pairs={{0,2},{2,0},{4,6},{6,4},{1,3},{3,1},{5,7},{7,5},{8,10},{10,8},{12,... | collective-permute-start | bytes 2359304 | tf_op jit(solution)/shard_map/ppermute | solution.py:72
  16.7 7.5 %collective-permute-start.8 = (bf16[128,1024]{1,0:T(8,128)(2,1)S(1)}, bf16[128,1024]{1,0:T(8,128)(2,1)S(1)}, u32[]{:S(2)}, u32[]{:S(2)}) collective-permute-start(bf16[128,1024]{1,0:T(8,128)(2,1)S(1)} %shard_map.125), channel_id=1, source_target_pairs={{0,1},{1,0},{2,3},{3,2},{4,5},{5,4},{6,7},{7,6},{8,9},{9,8},{10,11... | collective-permute-start | bytes 786440 | tf_op jit(solution)/shard_map/ppermute | solution.py:69
  18.5 29.5 %collective-permute-start.9 = (bf16[128,2048]{1,0:T(8,128)(2,1)S(1)}, bf16[128,2048]{1,0:T(8,128)(2,1)S(1)}, u32[]{:S(2)}, u32[]{:S(2)}) collective-permute-start(bf16[128,2048]{1,0:T(8,128)(2,1)S(1)} %collective-permute-done.7.refs_0_.refs_8_.refs_3_), channel_id=1, source_target_pairs={{0,2},{2,0},{4,6},{6,4},{1,3},{3,1},{5,7},{7,5},{8,10},{10,8},{12,... | collective-permute-start | bytes 1572872 | tf_op jit(solution)/shard_map/ppermute | solution.py:72
  24.3 23.8 %collective-permute-start.10 = (bf16[128,1024]{1,0:T(8,128)(2,1)S(1)}, bf16[128,1024]{1,0:T(8,128)(2,1)S(1)}, u32[]{:S(2)}, u32[]{:S(2)}) collective-permute-start(bf16[128,1024]{1,0:T(8,128)(2,1)S(1)} %collective-permute-done.8.refs_9_.refs_4_), channel_id=1, source_target_pairs={{0,2},{2,0},{4,6},{6,4},{1,3},{3,1},{5,7},{7,5},{8,10},{10,8},{12,... | collective-permute-start | bytes 786440 | tf_op jit(solution)/shard_map/ppermute | solution.py:72
  24.3 16.2 %copy-start.1 = (bf16[1,64,3072]{2,1,0:T(8,128)(2,1)S(1)}, bf16[1,64,3072]{2,1,0:T(8,128)(2,1)}, u32[]{:S(2)}) copy-start(bf16[1,64,3072]{2,1,0:T(8,128)(2,1)} %refs_0_.5) | copy-start | bytes 1179652
  24.3 16.2 %copy-start.4 = (f32[1,2,128]{2,1,0:T(2,128)S(1)}, f32[1,2,128]{2,1,0:T(2,128)}, u32[]{:S(2)}) copy-start(f32[1,2,128]{2,1,0:T(2,128)} %refs_2_.3) | copy-start | bytes 3076
  34.8 13.2 %copy-start = (bf16[1,1,128,3072]{3,2,1,0:T(8,128)(2,1)S(1)}, bf16[1,1,128,3072]{3,2,1,0:T(8,128)(2,1)}, u32[]{:S(2)}) copy-start(bf16[1,1,128,3072]{3,2,1,0:T(8,128)(2,1)} %param.19) | copy-start | bytes 2359300
  34.8 2.0 %collective-permute-start = (bf16[128,128]{1,0:T(8,128)(2,1)S(1)}, bf16[128,128]{1,0:T(8,128)(2,1)S(1)}, u32[]{:S(2)}, u32[]{:S(2)}) collective-permute-start(bf16[128,128]{1,0:T(8,128)(2,1)S(1)} %get-tuple-element.42.refs_4_), channel_id=1, source_target_pairs={{0,2},{2,0},{4,6},{6,4},{1,3},{3,1},{5,7},{7,5},{8,10},{10,8},{12,... | collective-permute-start | bytes 98312 | tf_op jit(solution)/shard_map/ppermute | solution.py:32
  35.4 3.9 %collective-permute-start.1 = (bf16[128,128]{1,0:T(8,128)(2,1)S(1)}, bf16[128,128]{1,0:T(8,128)(2,1)S(1)}, u32[]{:S(2)}, u32[]{:S(2)}) collective-permute-start(bf16[128,128]{1,0:T(8,128)(2,1)S(1)} %get-tuple-element.42.refs_4_), channel_id=1, source_target_pairs={{0,4},{2,6},{4,0},{6,2},{1,5},{3,7},{5,1},{7,3},{8,12},{10,14},{12... | collective-permute-start | bytes 98312 | tf_op jit(solution)/shard_map/ppermute | solution.py:32
  36.8 3.7 %collective-permute-start.2 = (bf16[128,128]{1,0:T(8,128)(2,1)S(1)}, bf16[128,128]{1,0:T(8,128)(2,1)S(1)}, u32[]{:S(2)}, u32[]{:S(2)}) collective-permute-start(bf16[128,128]{1,0:T(8,128)(2,1)S(1)} %get-tuple-element.42.refs_4_), channel_id=1, source_target_pairs={{0,6},{2,4},{4,2},{6,0},{1,7},{3,5},{5,3},{7,1},{8,14},{10,12},{12... | collective-permute-start | bytes 98312 | tf_op jit(solution)/shard_map/ppermute | solution.py:32
  43.4 1.3 %collective-permute-start.3 = (bf16[128,128]{1,0:T(8,128)(2,1)S(1)}, bf16[128,128]{1,0:T(8,128)(2,1)S(1)}, u32[]{:S(2)}, u32[]{:S(2)}) collective-permute-start(bf16[128,128]{1,0:T(8,128)(2,1)S(1)} %get-tuple-element.46), channel_id=1, source_target_pairs={{0,2},{2,0},{4,6},{6,4},{1,3},{3,1},{5,7},{7,5},{8,10},{10,8},{12,... | collective-permute-start | bytes 98312 | tf_op jit(solution)/shard_map/ppermute | solution.py:37
  43.5 3.9 %collective-permute-start.4 = (bf16[128,128]{1,0:T(8,128)(2,1)S(1)}, bf16[128,128]{1,0:T(8,128)(2,1)S(1)}, u32[]{:S(2)}, u32[]{:S(2)}) collective-permute-start(bf16[128,128]{1,0:T(8,128)(2,1)S(1)} %get-tuple-element.47), channel_id=1, source_target_pairs={{0,4},{2,6},{4,0},{6,2},{1,5},{3,7},{5,1},{7,3},{8,12},{10,14},{12... | collective-permute-start | bytes 98312 | tf_op jit(solution)/shard_map/ppermute | solution.py:37
  44.7 3.3 %collective-permute-start.5 = (bf16[128,128]{1,0:T(8,128)(2,1)S(1)}, bf16[128,128]{1,0:T(8,128)(2,1)S(1)}, u32[]{:S(2)}, u32[]{:S(2)}) collective-permute-start(bf16[128,128]{1,0:T(8,128)(2,1)S(1)} %get-tuple-element.48), channel_id=1, source_target_pairs={{0,6},{2,4},{4,2},{6,0},{1,7},{3,5},{5,3},{7,1},{8,14},{10,12},{12... | collective-permute-start | bytes 98312 | tf_op jit(solution)/shard_map/ppermute | solution.py:37
  50.8 3.9 %collective-permute-start.11 = (bf16[128,128]{1,0:T(8,128)(2,1)S(1)}, bf16[128,128]{1,0:T(8,128)(2,1)S(1)}, u32[]{:S(2)}, u32[]{:S(2)}) collective-permute-start(bf16[128,128]{1,0:T(8,128)(2,1)S(1)} %get-tuple-element.50.refs_0_), channel_id=1, source_target_pairs={{0,8},{1,9},{2,10},{3,11},{4,12},{5,13},{6,14},{7,15}} | collective-permute-start | bytes 98312 | tf_op jit(solution)/shard_map/ppermute | solution.py:927
  52.1 2.9 %collective-permute-start.12 = (bf16[128,128]{1,0:T(8,128)(2,1)S(1)}, bf16[128,128]{1,0:T(8,128)(2,1)S(1)}, u32[]{:S(2)}, u32[]{:S(2)}) collective-permute-start(bf16[128,128]{1,0:T(8,128)(2,1)S(1)} %get-tuple-element.50.refs_0_), channel_id=1, source_target_pairs={{0,16},{1,17},{2,18},{3,19},{4,20},{5,21},{6,22},{7,23}} | collective-permute-start | bytes 98312 | tf_op jit(solution)/shard_map/ppermute | solution.py:927
  53.4 2.9 %collective-permute-start.13 = (bf16[128,128]{1,0:T(8,128)(2,1)S(1)}, bf16[128,128]{1,0:T(8,128)(2,1)S(1)}, u32[]{:S(2)}, u32[]{:S(2)}) collective-permute-start(bf16[128,128]{1,0:T(8,128)(2,1)S(1)} %get-tuple-element.50.refs_0_), channel_id=1, source_target_pairs={{0,24},{1,25},{2,26},{3,27},{4,28},{5,29},{6,30},{7,31}} | collective-permute-start | bytes 98312 | tf_op jit(solution)/shard_map/ppermute | solution.py:927
  56.3 1.9 %collective-permute-start.14 = (bf16[128,64]{1,0:T(8,128)(2,1)S(1)}, bf16[128,64]{1,0:T(8,128)(2,1)S(1)}, u32[]{:S(2)}, u32[]{:S(2)}) collective-permute-start(bf16[128,64]{1,0:T(8,128)(2,1)S(1)} %get-tuple-element.51.refs_3_.refs_8_), channel_id=1, source_target_pairs={{0,2},{2,0},{4,6},{6,4},{1,3},{3,1},{5,7},{7,5},{8,10},{10,8},{12,... | collective-permute-start | bytes 49160 | tf_op jit(solution)/shard_map/ppermute | solution.py:32
  56.3 4.0 %collective-permute-start.15 = (bf16[128,64]{1,0:T(8,128)(2,1)S(1)}, bf16[128,64]{1,0:T(8,128)(2,1)S(1)}, u32[]{:S(2)}, u32[]{:S(2)}) collective-permute-start(bf16[128,64]{1,0:T(8,128)(2,1)S(1)} %get-tuple-element.51.refs_3_.refs_8_), channel_id=1, source_target_pairs={{0,4},{2,6},{4,0},{6,2},{1,5},{3,7},{5,1},{7,3},{8,12},{10,14},{12... | collective-permute-start | bytes 49160 | tf_op jit(solution)/shard_map/ppermute | solution.py:32
  57.3 3.4 %collective-permute-start.16 = (bf16[128,64]{1,0:T(8,128)(2,1)S(1)}, bf16[128,64]{1,0:T(8,128)(2,1)S(1)}, u32[]{:S(2)}, u32[]{:S(2)}) collective-permute-start(bf16[128,64]{1,0:T(8,128)(2,1)S(1)} %get-tuple-element.51.refs_3_.refs_8_), channel_id=1, source_target_pairs={{0,6},{2,4},{4,2},{6,0},{1,7},{3,5},{5,3},{7,1},{8,14},{10,12},{12... | collective-permute-start | bytes 49160 | tf_op jit(solution)/shard_map/ppermute | solution.py:32
  60.7 1.9 %collective-permute-start.17 = (bf16[128,128]{1,0:T(8,128)(2,1)S(1)}, bf16[128,128]{1,0:T(8,128)(2,1)S(1)}, u32[]{:S(2)}, u32[]{:S(2)}) collective-permute-start(bf16[128,128]{1,0:T(8,128)(2,1)S(1)} %get-tuple-element.58), channel_id=1, source_target_pairs={{0,2},{2,0},{4,6},{6,4},{1,3},{3,1},{5,7},{7,5},{8,10},{10,8},{12,... | collective-permute-start | bytes 98312 | tf_op jit(solution)/shard_map/ppermute | solution.py:37
  60.9 3.9 %collective-permute-start.18 = (bf16[128,128]{1,0:T(8,128)(2,1)S(1)}, bf16[128,128]{1,0:T(8,128)(2,1)S(1)}, u32[]{:S(2)}, u32[]{:S(2)}) collective-permute-start(bf16[128,128]{1,0:T(8,128)(2,1)S(1)} %get-tuple-element.59), channel_id=1, source_target_pairs={{0,4},{2,6},{4,0},{6,2},{1,5},{3,7},{5,1},{7,3},{8,12},{10,14},{12... | collective-permute-start | bytes 98312 | tf_op jit(solution)/shard_map/ppermute | solution.py:37
  62.0 3.4 %collective-permute-start.19 = (bf16[128,128]{1,0:T(8,128)(2,1)S(1)}, bf16[128,128]{1,0:T(8,128)(2,1)S(1)}, u32[]{:S(2)}, u32[]{:S(2)}) collective-permute-start(bf16[128,128]{1,0:T(8,128)(2,1)S(1)} %get-tuple-element.60), channel_id=1, source_target_pairs={{0,6},{2,4},{4,2},{6,0},{1,7},{3,5},{5,3},{7,1},{8,14},{10,12},{12... | collective-permute-start | bytes 98312 | tf_op jit(solution)/shard_map/ppermute | solution.py:37
  65.5 26.4 %copy-start.2 = (bf16[4,128,128]{2,1,0:T(8,128)(2,1)S(1)}, bf16[4,128,128]{2,1,0:T(8,128)(2,1)}, u32[]{:S(2)}) copy-start(bf16[4,128,128]{2,1,0:T(8,128)(2,1)} %get-tuple-element.68.refs_5_) | copy-start | bytes 393220
  65.5 26.4 %copy-start.3 = (f32[128,128]{1,0:T(8,128)S(1)}, f32[128,128]{1,0:T(8,128)}, u32[]{:S(2)}) copy-start(f32[128,128]{1,0:T(8,128)} %get-tuple-element.69.refs_6_) | copy-start | bytes 196612
  65.5 31.8 %copy-start.5 = (f32[1,9216]{1,0:T(1,128)S(1)}, f32[1,9216]{1,0:T(1,128)}, u32[]{:S(2)}) copy-start(f32[1,9216]{1,0:T(1,128)} %get-tuple-element.49.refs_12_) | copy-start | bytes 110596
  65.5 1.9 %collective-permute-start.20 = (bf16[128,128]{1,0:T(8,128)(2,1)S(1)}, bf16[128,128]{1,0:T(8,128)(2,1)S(1)}, u32[]{:S(2)}, u32[]{:S(2)}) collective-permute-start(bf16[128,128]{1,0:T(8,128)(2,1)S(1)} %get-tuple-element.63), channel_id=1, source_target_pairs={{0,2},{2,0},{4,6},{6,4},{1,3},{3,1},{5,7},{7,5},{8,10},{10,8},{12,... | collective-permute-start | bytes 98312 | tf_op jit(solution)/shard_map/ppermute | solution.py:37
  65.7 3.9 %collective-permute-start.21 = (bf16[128,128]{1,0:T(8,128)(2,1)S(1)}, bf16[128,128]{1,0:T(8,128)(2,1)S(1)}, u32[]{:S(2)}, u32[]{:S(2)}) collective-permute-start(bf16[128,128]{1,0:T(8,128)(2,1)S(1)} %get-tuple-element.64), channel_id=1, source_target_pairs={{0,4},{2,6},{4,0},{6,2},{1,5},{3,7},{5,1},{7,3},{8,12},{10,14},{12... | collective-permute-start | bytes 98312 | tf_op jit(solution)/shard_map/ppermute | solution.py:37
  66.6 3.4 %collective-permute-start.22 = (bf16[128,128]{1,0:T(8,128)(2,1)S(1)}, bf16[128,128]{1,0:T(8,128)(2,1)S(1)}, u32[]{:S(2)}, u32[]{:S(2)}) collective-permute-start(bf16[128,128]{1,0:T(8,128)(2,1)S(1)} %get-tuple-element.65), channel_id=1, source_target_pairs={{0,6},{2,4},{4,2},{6,0},{1,7},{3,5},{5,3},{7,1},{8,14},{10,12},{12... | collective-permute-start | bytes 98312 | tf_op jit(solution)/shard_map/ppermute | solution.py:37
  70.0 15.1 %collective-permute-start.25 = (bf16[2,128,64]{2,1,0:T(8,128)(2,1)S(1)}, bf16[2,128,64]{2,1,0:T(8,128)(2,1)S(1)}, u32[]{:S(2)}, u32[]{:S(2)}) collective-permute-start(bf16[2,128,64]{2,1,0:T(8,128)(2,1)S(1)} %get-tuple-element.73), channel_id=1, source_target_pairs={{0,2},{2,0},{4,6},{6,4},{1,3},{3,1},{5,7},{7,5},{8,10},{10,8},{12,... | collective-permute-start | bytes 98312 | tf_op jit(solution)/shard_map/ppermute | solution.py:971
  70.2 17.4 %collective-permute-start.23 = (bf16[160,64]{1,0:T(8,128)(2,1)S(1)}, bf16[160,64]{1,0:T(8,128)(2,1)S(1)}, u32[]{:S(2)}, u32[]{:S(2)}) collective-permute-start(bf16[160,64]{1,0:T(8,128)(2,1)S(1)} %get-tuple-element.66), channel_id=1, source_target_pairs={{0,8},{8,0},{16,24},{24,16},{1,9},{9,1},{17,25},{25,17},{2,10},{10... | collective-permute-start | bytes 61448 | tf_op jit(solution)/shard_map/ppermute | solution.py:972
  75.0 12.6 %collective-permute-start.24 = (bf16[128,64]{1,0:T(8,128)(2,1)S(1)}, bf16[128,64]{1,0:T(8,128)(2,1)S(1)}, u32[]{:S(2)}, u32[]{:S(2)}) collective-permute-start(bf16[128,64]{1,0:T(8,128)(2,1)S(1)} %get-tuple-element.61.refs_7_), channel_id=1, source_target_pairs={{0,16},{8,24},{16,0},{24,8},{1,17},{9,25},{17,1},{25,9},{2,18},{10... | collective-permute-start | bytes 49160 | tf_op jit(solution)/shard_map/ppermute | solution.py:961
  85.2 5.8 %collective-permute-start.26 = (bf16[128,64]{1,0:T(8,128)(2,1)S(1)}, bf16[128,64]{1,0:T(8,128)(2,1)S(1)}, u32[]{:S(2)}, u32[]{:S(2)}) collective-permute-start(bf16[128,64]{1,0:T(8,128)(2,1)S(1)} %get-tuple-element.74), channel_id=1, source_target_pairs={{0,8},{2,10},{4,12},{6,14},{8,16},{10,18},{12,20},{14,22},{16,24},... | collective-permute-start | bytes 49160 | tf_op jit(solution)/shard_map/ppermute | solution.py:975
  85.3 6.6 %collective-permute-start.27 = (bf16[128,64]{1,0:T(8,128)(2,1)S(1)}, bf16[128,64]{1,0:T(8,128)(2,1)S(1)}, u32[]{:S(2)}, u32[]{:S(2)}) collective-permute-start(bf16[128,64]{1,0:T(8,128)(2,1)S(1)} %get-tuple-element.75), channel_id=1, source_target_pairs={{0,12},{2,14},{4,8},{6,10},{8,20},{10,22},{12,16},{14,18},{16,28},... | collective-permute-start | bytes 49160 | tf_op jit(solution)/shard_map/ppermute | solution.py:975
  92.4 1.3 %collective-permute-start.32 = (bf16[5,64,128]{2,1,0:T(8,128)(2,1)S(1)}, bf16[5,64,128]{2,1,0:T(8,128)(2,1)S(1)}, u32[]{:S(2)}, u32[]{:S(2)}) collective-permute-start(bf16[5,64,128]{2,1,0:T(8,128)(2,1)S(1)} %get-tuple-element.77), channel_id=1, source_target_pairs={{0,2},{2,0},{4,6},{6,4},{1,3},{3,1},{5,7},{7,5},{8,10},{10,8},{12,... | collective-permute-start | bytes 245768 | tf_op jit(solution)/shard_map/ppermute | solution.py:1010
  93.8 19.1 %collective-permute-start.33 = (bf16[5,64,128]{2,1,0:T(8,128)(2,1)S(1)}, bf16[5,64,128]{2,1,0:T(8,128)(2,1)S(1)}, u32[]{:S(2)}, u32[]{:S(2)}) collective-permute-start(bf16[5,64,128]{2,1,0:T(8,128)(2,1)S(1)} %add_convert_fusion.refs_8_), channel_id=1, source_target_pairs={{0,4},{1,5},{2,6},{3,7},{4,0},{5,1},{6,2},{7,3},{8,12},{9,13},{10,... | collective-permute-start | bytes 245768 | tf_op jit(solution)/shard_map/ppermute | solution.py:1022
  94.9 17.9 %collective-permute-start.34 = (bf16[5,64,128]{2,1,0:T(8,128)(2,1)S(1)}, bf16[5,64,128]{2,1,0:T(8,128)(2,1)S(1)}, u32[]{:S(2)}, u32[]{:S(2)}) collective-permute-start(bf16[5,64,128]{2,1,0:T(8,128)(2,1)S(1)} %add_convert_fusion.refs_8_), channel_id=1, source_target_pairs={{0,1},{1,0},{2,3},{3,2},{4,5},{5,4},{6,7},{7,6},{8,9},{9,8},{10,11... | collective-permute-start | bytes 245768 | tf_op jit(solution)/shard_map/ppermute | solution.py:1022
  96.4 16.4 %collective-permute-start.35 = (bf16[5,64,128]{2,1,0:T(8,128)(2,1)S(1)}, bf16[5,64,128]{2,1,0:T(8,128)(2,1)S(1)}, u32[]{:S(2)}, u32[]{:S(2)}) collective-permute-start(bf16[5,64,128]{2,1,0:T(8,128)(2,1)S(1)} %add_convert_fusion.refs_8_), channel_id=1, source_target_pairs={{0,5},{1,4},{2,7},{3,6},{4,1},{5,0},{6,3},{7,2},{8,13},{9,12},{10,... | collective-permute-start | bytes 245768 | tf_op jit(solution)/shard_map/ppermute | solution.py:1022
  97.3 3.9 %collective-permute-start.28 = (bf16[128,64]{1,0:T(8,128)(2,1)S(1)}, bf16[128,64]{1,0:T(8,128)(2,1)S(1)}, u32[]{:S(2)}, u32[]{:S(2)}) collective-permute-start(bf16[128,64]{1,0:T(8,128)(2,1)S(1)} %get-tuple-element.76.refs_0_), channel_id=1, source_target_pairs={{0,8},{8,0},{16,24},{24,16},{1,9},{9,1},{17,25},{25,17},{2,10},{10... | collective-permute-start | bytes 49160 | tf_op jit(solution)/shard_map/ppermute | solution.py:1006
  97.3 15.5 %collective-permute-start.31 = (f32[1,9216]{1,0:T(1,128)S(1)}, f32[1,9216]{1,0:T(1,128)S(1)}, u32[]{:S(2)}, u32[]{:S(2)}) collective-permute-start(f32[1,9216]{1,0:T(1,128)S(1)} %copy-done.5), channel_id=1, source_target_pairs={{0,1},{1,0},{2,3},{3,2},{4,5},{5,4},{6,7},{7,6},{8,9},{9,8},{10,11... | collective-permute-start | bytes 110600 | tf_op jit(solution)/shard_map/ppermute | solution.py:32
  101.2 5.1 %collective-permute-start.29 = (bf16[128,64]{1,0:T(8,128)(2,1)S(1)}, bf16[128,64]{1,0:T(8,128)(2,1)S(1)}, u32[]{:S(2)}, u32[]{:S(2)}) collective-permute-start(bf16[128,64]{1,0:T(8,128)(2,1)S(1)} %get-tuple-element.76.refs_0_), channel_id=1, source_target_pairs={{0,16},{8,24},{16,0},{24,8},{1,17},{9,25},{17,1},{25,9},{2,18},{10... | collective-permute-start | bytes 49160 | tf_op jit(solution)/shard_map/ppermute | solution.py:1005
  106.4 5.7 %collective-permute-start.30 = (bf16[128,64]{1,0:T(8,128)(2,1)S(1)}, bf16[128,64]{1,0:T(8,128)(2,1)S(1)}, u32[]{:S(2)}, u32[]{:S(2)}) collective-permute-start(bf16[128,64]{1,0:T(8,128)(2,1)S(1)} %get-tuple-element.76.refs_0_), channel_id=1, source_target_pairs={{0,24},{8,16},{16,8},{24,0},{1,25},{9,17},{17,9},{25,1},{2,26},{10... | collective-permute-start | bytes 49160 | tf_op jit(solution)/shard_map/ppermute | solution.py:1004

commit v14 on v13

--- a/solution.py
+++ b/solution.py
@@ -13,7 +13,7 @@
 EPS = 1e-06
 ADV_WEIGHT = 3.0
 TILE = 512
-STREAMS = 6
+STREAMS = 4
 SPARE = 8 << 20
 VMEM = pl.BlockSpec(memory_space=pltpu.VMEM)
 HBM = pl.BlockSpec(memory_space=pltpu.HBM)
@@ -401,7 +401,7 @@
     late.wait()
 
 
-def critic_front_kernel(count, model_width, fetches, short, gram, gains, *refs):
+def critic_front_kernel(count, model_width, fetches, short, embed_w, gram, gains, *refs):
     rows = refs[:count]
     head_outs = refs[count : 2 * count]
     kept = refs[2 * count :]
@@ -940,6 +940,7 @@
         head_blocks + [array(shape, kind) for shape, kind in stored],
         (
             pltpu.with_memory_space_constraint(short, pltpu.VMEM),
+            w_embed,
             gram,
             qk_gain,
             *critic_rows,

time: 116 us -> 116 us (level)
  no operation moved by 1% of the time
where the time goes in v14:
time: 116 us
  waiting for transfers between devices  51.1 us (44%)
  starting transfers between devices  42.3 us (36%)
  Pallas kernels  21 us (18%)
    pallas_call x13, Pallas kernels, run(): pl.pallas_call(body, out_shape=list(outputs) + [pltpu.HBM(item.shape, ite...  21 us
    ppermute x1, waiting for transfers between devices, spread_heads(): near = lax.ppermute(part, 'seq', swaps(count, bit))  11.9 us
    ppermute x1, starting transfers between devices, step(): fake = lax.ppermute(term_rows, 'segment', swaps(sections, 2))  10.1 us
    ppermute x9, waiting for transfers between devices, scatter_near(): lax.ppermute(blocks[offset], axis, swaps(count, offset))  8.42 us
    ppermute x7, starting transfers between devices, gather_near(): lax.ppermute(value, axis, swaps(count, offset))  6.27 us
    ppermute x1, waiting for transfers between devices, spread_heads(): held[bit] = [near, lax.ppermute(stage(near), 'dp', swaps(groups, 1))]  5.76 us
    ppermute x9, starting transfers between devices, scatter_near(): lax.ppermute(blocks[offset], axis, swaps(count, offset))  5.45 us
    ppermute x7, waiting for transfers between devices, gather_near(): lax.ppermute(value, axis, swaps(count, offset))  5.38 us
  transfers between devices with their start and end apart: 36, of which 22 were waited for; matrix products, arithmetic and copies ran while one was open for 0% of the time, Pallas kernels for 12%

profile of v14, /device:TPU:0, one launch (start us, length us, event | category | flops | bytes accessed | tf_op | source)
XLA Modules:
  0.0 115.5 jit_solution(4697943356792453925)
XLA Ops:
  0.6 1.1 shard_map.124
  1.7 3.1 %collective-permute-start.7 = (bf16[128,2048]{1,0:T(8,128)(2,1)S(1)}, bf16[128,2048]{1,0:T(8,128)(2,1)S(1)}, u32[]{:S(2)}, u32[]{:S(2)}) collective-permute-start(bf16[128,2048]{1,0:T(8,128)(2,1)S(1)} %shard_map.124), channel_id=1, source_target_pairs={{0,4},{2,6},{4,0},{6,2},{1,5},{3,7},{5,1},{7,3},{8,12},{10,14},{12... | collective-permute-start | bytes 1572872 | tf_op jit(solution)/shard_map/ppermute | solution.py:68
  4.8 0.0 collective-permute-start.6
  4.8 11.9 %collective-permute-done.7.refs_0_.refs_8_.refs_3_ = bf16[128,2048]{1,0:T(8,128)(2,1)S(1)} collective-permute-done((bf16[128,2048]{1,0:T(8,128)(2,1)S(1)}, bf16[128,2048]{1,0:T(8,128)(2,1)S(1)}, u32[]{:S(2)}, u32[]{:S(2)}) %collective-permute-start.7) | collective-permute-done | bytes 524320 | tf_op jit(solution)/shard_map/ppermute | solution.py:68
  16.7 1.8 %collective-permute-start.8 = (bf16[128,1024]{1,0:T(8,128)(2,1)S(1)}, bf16[128,1024]{1,0:T(8,128)(2,1)S(1)}, u32[]{:S(2)}, u32[]{:S(2)}) collective-permute-start(bf16[128,1024]{1,0:T(8,128)(2,1)S(1)} %shard_map.125), channel_id=1, source_target_pairs={{0,1},{1,0},{2,3},{3,2},{4,5},{5,4},{6,7},{7,6},{8,9},{9,8},{10,11... | collective-permute-start | bytes 786440 | tf_op jit(solution)/shard_map/ppermute | solution.py:69
  18.5 5.8 %collective-permute-done.8.refs_9_.refs_4_ = bf16[128,1024]{1,0:T(8,128)(2,1)S(1)} collective-permute-done((bf16[128,1024]{1,0:T(8,128)(2,1)S(1)}, bf16[128,1024]{1,0:T(8,128)(2,1)S(1)}, u32[]{:S(2)}, u32[]{:S(2)}) %collective-permute-start.8) | collective-permute-done | bytes 262176 | tf_op jit(solution)/shard_map/ppermute | solution.py:69
  24.3 0.0 collective-permute-start.10
  24.3 10.2 %shard_map.122 = (bf16[128,128]{1,0:T(8,128)(2,1)S(1)}, bf16[128,64]{1,0:T(8,128)(2,1)S(1)}, bf16[3,3072,128]{2,1,0:T(8,128)(2,1)S(1)}, bf16[2,64,64]{2,1,0:T(8,128)(2,1)S(1)}) custom-call(s32[2,2]{1,0:T(2,128)} %refs_15_.3, f32[1,256]{1,0:T(1,128)} %refs_1_.4, bf16[256,3072]{1,0:T(8,128)(2,1)} %bitcast.26, bf16[64,128]{1,0:T(8,128)(2,1)} %bitcast.34, ...), custom_call_target="tpu_custom_call" | custom-call | flops 23592960 | bytes 4441104 | tf_op jit(solution)/shard_map/pallas_call | solution.py:207
  34.5 0.0 copy-start
  34.5 0.6 collective-permute-start
  35.1 1.5 %collective-permute-start.1 = (bf16[128,128]{1,0:T(8,128)(2,1)S(1)}, bf16[128,128]{1,0:T(8,128)(2,1)S(1)}, u32[]{:S(2)}, u32[]{:S(2)}) collective-permute-start(bf16[128,128]{1,0:T(8,128)(2,1)S(1)} %get-tuple-element.42.refs_4_), channel_id=1, source_target_pairs={{0,4},{2,6},{4,0},{6,2},{1,5},{3,7},{5,1},{7,3},{8,12},{10,14},{12... | collective-permute-start | bytes 98312 | tf_op jit(solution)/shard_map/ppermute | solution.py:32
  36.5 0.8 collective-permute-start.2
  37.3 1.6 %collective-permute-done.1.refs_6_ = bf16[128,128]{1,0:T(8,128)(2,1)S(1)} collective-permute-done((bf16[128,128]{1,0:T(8,128)(2,1)S(1)}, bf16[128,128]{1,0:T(8,128)(2,1)S(1)}, u32[]{:S(2)}, u32[]{:S(2)}) %collective-permute-start.1) | collective-permute-done | bytes 32800 | tf_op jit(solution)/shard_map/ppermute | solution.py:32
  39.0 1.2 %collective-permute-done.2.refs_7_ = bf16[128,128]{1,0:T(8,128)(2,1)S(1)} collective-permute-done((bf16[128,128]{1,0:T(8,128)(2,1)S(1)}, bf16[128,128]{1,0:T(8,128)(2,1)S(1)}, u32[]{:S(2)}, u32[]{:S(2)}) %collective-permute-start.2) | collective-permute-done | bytes 32800 | tf_op jit(solution)/shard_map/ppermute | solution.py:32
  40.2 2.9 %shard_map.123 = (bf16[128,128]{1,0:T(8,128)(2,1)S(1)}, bf16[128,128]{1,0:T(8,128)(2,1)S(1)}, bf16[128,128]{1,0:T(8,128)(2,1)S(1)}, bf16[128,128]{1,0:T(8,128)(2...) custom-call(bf16[1,64,3072]{2,1,0:T(8,128)(2,1)S(1)} %copy-done.1, ...), custom_call_target="tpu_custom_call" | custom-call | flops 301989888 | bytes 3154944 | tf_op jit(solution)/shard_map/pallas_call | solution.py:207
  43.1 0.1 collective-permute-start.3
  43.2 0.8 collective-permute-start.4
  44.0 0.3 collective-permute-done.3.refs_3_
  44.4 0.7 collective-permute-start.5
  45.0 2.1 %collective-permute-done.4.refs_4_ = bf16[128,128]{1,0:T(8,128)(2,1)S(1)} collective-permute-done((bf16[128,128]{1,0:T(8,128)(2,1)S(1)}, bf16[128,128]{1,0:T(8,128)(2,1)S(1)}, u32[]{:S(2)}, u32[]{:S(2)}) %collective-permute-start.4) | collective-permute-done | bytes 32800 | tf_op jit(solution)/shard_map/ppermute | solution.py:37
  47.2 0.6 collective-permute-done.5.refs_5_
  47.7 2.7 %shard_map.126 = (bf16[128,128]{1,0:T(8,128)(2,1)S(1)}, bf16[4,128,128]{2,1,0:T(8,128)(2,1)}, f32[128,128]{1,0:T(8,128)}) custom-call(bf16[128,64]{1,0:T(8,128)(2,1)S(1)} %get-tuple-element.44.refs_0_.refs_3_, bf16[1,64,3072]{2,1,0:T(8,128)(2,1)S(1)} %copy-done.1, bf16[128,128]{1,0:T(8,128)(2,1)S(1)} %get-tuple-element.45.refs_2_, ...), custom_call_target="tpu_custom_call" | custom-call | flops 402653184 | bytes 4182032 | tf_op jit(solution)/shard_map/pallas_call | solution.py:207
  50.5 1.3 %collective-permute-start.11 = (bf16[128,128]{1,0:T(8,128)(2,1)S(1)}, bf16[128,128]{1,0:T(8,128)(2,1)S(1)}, u32[]{:S(2)}, u32[]{:S(2)}) collective-permute-start(bf16[128,128]{1,0:T(8,128)(2,1)S(1)} %get-tuple-element.50.refs_0_), channel_id=1, source_target_pairs={{0,8},{1,9},{2,10},{3,11},{4,12},{5,13},{6,14},{7,15}} | collective-permute-start | bytes 98312 | tf_op jit(solution)/shard_map/ppermute | solution.py:927
  51.8 1.3 %collective-permute-start.12 = (bf16[128,128]{1,0:T(8,128)(2,1)S(1)}, bf16[128,128]{1,0:T(8,128)(2,1)S(1)}, u32[]{:S(2)}, u32[]{:S(2)}) collective-permute-start(bf16[128,128]{1,0:T(8,128)(2,1)S(1)} %get-tuple-element.50.refs_0_), channel_id=1, source_target_pairs={{0,16},{1,17},{2,18},{3,19},{4,20},{5,21},{6,22},{7,23}} | collective-permute-start | bytes 98312 | tf_op jit(solution)/shard_map/ppermute | solution.py:927
  53.1 1.3 %collective-permute-start.13 = (bf16[128,128]{1,0:T(8,128)(2,1)S(1)}, bf16[128,128]{1,0:T(8,128)(2,1)S(1)}, u32[]{:S(2)}, u32[]{:S(2)}) collective-permute-start(bf16[128,128]{1,0:T(8,128)(2,1)S(1)} %get-tuple-element.50.refs_0_), channel_id=1, source_target_pairs={{0,24},{1,25},{2,26},{3,27},{4,28},{5,29},{6,30},{7,31}} | collective-permute-start | bytes 98312 | tf_op jit(solution)/shard_map/ppermute | solution.py:927
  54.4 0.3 collective-permute-done.12.refs_2_
  54.6 1.3 %collective-permute-done.13.refs_3_ = bf16[128,128]{1,0:T(8,128)(2,1)S(1)} collective-permute-done((bf16[128,128]{1,0:T(8,128)(2,1)S(1)}, bf16[128,128]{1,0:T(8,128)(2,1)S(1)}, u32[]{:S(2)}, u32[]{:S(2)}) %collective-permute-start.13) | collective-permute-done | bytes 32800 | tf_op jit(solution)/shard_map/ppermute | solution.py:927
  56.0 0.1 collective-permute-start.14
  56.1 1.0 collective-permute-start.15
  57.0 0.9 collective-permute-start.16
  57.9 2.1 %collective-permute-done.15.refs_6_.refs_10_ = bf16[128,64]{1,0:T(8,128)(2,1)S(1)} collective-permute-done((bf16[128,64]{1,0:T(8,128)(2,1)S(1)}, bf16[128,64]{1,0:T(8,128)(2,1)S(1)}, u32[]{:S(2)}, u32[]{:S(2)}) %collective-permute-start.15) | collective-permute-done | bytes 16416 | tf_op jit(solution)/shard_map/ppermute | solution.py:32
  60.0 0.4 collective-permute-done.16.refs_7_.refs_11_
  60.4 0.2 collective-permute-start.17
  60.6 1.1 collective-permute-start.18
  61.7 0.6 collective-permute-start.19
  62.4 2.2 %collective-permute-done.18.refs_4_.refs_10_ = bf16[128,128]{1,0:T(8,128)(2,1)S(1)} collective-permute-done((bf16[128,128]{1,0:T(8,128)(2,1)S(1)}, bf16[128,128]{1,0:T(8,128)(2,1)S(1)}, u32[]{:S(2)}, u32[]{:S(2)}) %collective-permute-start.18) | collective-permute-done | bytes 32800 | tf_op jit(solution)/shard_map/ppermute | solution.py:37
  64.6 0.6 collective-permute-done.19.refs_5_.refs_11_
  65.2 0.2 collective-permute-start.20
  65.4 0.9 collective-permute-start.21
  66.3 0.8 collective-permute-start.22
  67.2 2.2 %collective-permute-done.21.refs_14_ = bf16[128,128]{1,0:T(8,128)(2,1)S(1)} collective-permute-done((bf16[128,128]{1,0:T(8,128)(2,1)S(1)}, bf16[128,128]{1,0:T(8,128)(2,1)S(1)}, u32[]{:S(2)}, u32[]{:S(2)}) %collective-permute-start.21) | collective-permute-done | bytes 32800 | tf_op jit(solution)/shard_map/ppermute | solution.py:37
  69.3 0.4 collective-permute-done.22.refs_15_
  69.8 0.2 collective-permute-start.25
  69.9 4.8 %collective-permute-start.23 = (bf16[160,64]{1,0:T(8,128)(2,1)S(1)}, bf16[160,64]{1,0:T(8,128)(2,1)S(1)}, u32[]{:S(2)}, u32[]{:S(2)}) collective-permute-start(bf16[160,64]{1,0:T(8,128)(2,1)S(1)} %get-tuple-element.66), channel_id=1, source_target_pairs={{0,8},{8,0},{16,24},{24,16},{1,9},{9,1},{17,25},{25,17},{2,10},{10... | collective-permute-start | bytes 61448 | tf_op jit(solution)/shard_map/ppermute | solution.py:973
  74.8 10.1 %collective-permute-start.24 = (bf16[128,64]{1,0:T(8,128)(2,1)S(1)}, bf16[128,64]{1,0:T(8,128)(2,1)S(1)}, u32[]{:S(2)}, u32[]{:S(2)}) collective-permute-start(bf16[128,64]{1,0:T(8,128)(2,1)S(1)} %get-tuple-element.61.refs_7_), channel_id=1, source_target_pairs={{0,16},{8,24},{16,0},{24,8},{1,17},{9,25},{17,1},{25,9},{2,18},{10... | collective-permute-start | bytes 49160 | tf_op jit(solution)/shard_map/ppermute | solution.py:962
  84.8 0.1 collective-permute-start.26
  84.9 1.1 collective-permute-start.27
  86.0 1.3 %collective-permute-done.24.refs_1_ = bf16[128,64]{1,0:T(8,128)(2,1)S(1)} collective-permute-done((bf16[128,64]{1,0:T(8,128)(2,1)S(1)}, bf16[128,64]{1,0:T(8,128)(2,1)S(1)}, u32[]{:S(2)}, u32[]{:S(2)}) %collective-permute-start.24) | collective-permute-done | bytes 16416 | tf_op jit(solution)/shard_map/ppermute | solution.py:962
  87.3 3.3 %collective-permute-done.26.refs_12_ = bf16[128,64]{1,0:T(8,128)(2,1)S(1)} collective-permute-done((bf16[128,64]{1,0:T(8,128)(2,1)S(1)}, bf16[128,64]{1,0:T(8,128)(2,1)S(1)}, u32[]{:S(2)}, u32[]{:S(2)}) %collective-permute-start.26) | collective-permute-done | bytes 16416 | tf_op jit(solution)/shard_map/ppermute | solution.py:976
  90.6 1.0 collective-permute-done.27.refs_13_
  91.6 0.5 shard_map.132
  92.1 0.1 collective-permute-start.32
  92.1 1.3 %collective-permute-done.32 = bf16[5,64,128]{2,1,0:T(8,128)(2,1)S(1)} collective-permute-done((bf16[5,64,128]{2,1,0:T(8,128)(2,1)S(1)}, bf16[5,64,128]{2,1,0:T(8,128)(2,1)S(1)}, u32[]{:S(2)}, u32[]{:S(2)}) %collective-permute-start.32) | collective-permute-done | bytes 81952 | tf_op jit(solution)/shard_map/ppermute | solution.py:1011
  93.4 1.2 %collective-permute-start.33 = (bf16[5,64,128]{2,1,0:T(8,128)(2,1)S(1)}, bf16[5,64,128]{2,1,0:T(8,128)(2,1)S(1)}, u32[]{:S(2)}, u32[]{:S(2)}) collective-permute-start(bf16[5,64,128]{2,1,0:T(8,128)(2,1)S(1)} %add_convert_fusion.refs_8_), channel_id=1, source_target_pairs={{0,4},{1,5},{2,6},{3,7},{4,0},{5,1},{6,2},{7,3},{8,12},{9,13},{10,... | collective-permute-start | bytes 245768 | tf_op jit(solution)/shard_map/ppermute | solution.py:1023
  94.6 1.5 %collective-permute-start.34 = (bf16[5,64,128]{2,1,0:T(8,128)(2,1)S(1)}, bf16[5,64,128]{2,1,0:T(8,128)(2,1)S(1)}, u32[]{:S(2)}, u32[]{:S(2)}) collective-permute-start(bf16[5,64,128]{2,1,0:T(8,128)(2,1)S(1)} %add_convert_fusion.refs_8_), channel_id=1, source_target_pairs={{0,1},{1,0},{2,3},{3,2},{4,5},{5,4},{6,7},{7,6},{8,9},{9,8},{10,11... | collective-permute-start | bytes 245768 | tf_op jit(solution)/shard_map/ppermute | solution.py:1023
  96.1 0.9 collective-permute-start.35
  97.0 1.5 %collective-permute-start.31 = (f32[1,9216]{1,0:T(1,128)S(1)}, f32[1,9216]{1,0:T(1,128)S(1)}, u32[]{:S(2)}, u32[]{:S(2)}) collective-permute-start(f32[1,9216]{1,0:T(1,128)S(1)} %copy-done.5), channel_id=1, source_target_pairs={{0,1},{1,0},{2,3},{3,2},{4,5},{5,4},{6,7},{7,6},{8,9},{9,8},{10,11... | collective-permute-start | bytes 110600 | tf_op jit(solution)/shard_map/ppermute | solution.py:32
  98.5 2.4 %collective-permute-done.28.refs_1_ = bf16[128,64]{1,0:T(8,128)(2,1)S(1)} collective-permute-done((bf16[128,64]{1,0:T(8,128)(2,1)S(1)}, bf16[128,64]{1,0:T(8,128)(2,1)S(1)}, u32[]{:S(2)}, u32[]{:S(2)}) %collective-permute-start.28) | collective-permute-done | bytes 16416 | tf_op jit(solution)/shard_map/ppermute | solution.py:1007
  100.9 0.4 collective-permute-start.29
  101.3 4.8 %collective-permute-done.29.refs_2_ = bf16[128,64]{1,0:T(8,128)(2,1)S(1)} collective-permute-done((bf16[128,64]{1,0:T(8,128)(2,1)S(1)}, bf16[128,64]{1,0:T(8,128)(2,1)S(1)}, u32[]{:S(2)}, u32[]{:S(2)}) %collective-permute-start.29) | collective-permute-done | bytes 16416 | tf_op jit(solution)/shard_map/ppermute | solution.py:1006
  106.0 1.7 %collective-permute-start.30 = (bf16[128,64]{1,0:T(8,128)(2,1)S(1)}, bf16[128,64]{1,0:T(8,128)(2,1)S(1)}, u32[]{:S(2)}, u32[]{:S(2)}) collective-permute-start(bf16[128,64]{1,0:T(8,128)(2,1)S(1)} %get-tuple-element.76.refs_0_), channel_id=1, source_target_pairs={{0,24},{8,16},{16,8},{24,0},{1,25},{9,17},{17,9},{25,1},{2,26},{10... | collective-permute-start | bytes 49160 | tf_op jit(solution)/shard_map/ppermute | solution.py:1005
  107.7 4.1 %collective-permute-done.30.refs_3_ = bf16[128,64]{1,0:T(8,128)(2,1)S(1)} collective-permute-done((bf16[128,64]{1,0:T(8,128)(2,1)S(1)}, bf16[128,64]{1,0:T(8,128)(2,1)S(1)}, u32[]{:S(2)}, u32[]{:S(2)}) %collective-permute-start.30) | collective-permute-done | bytes 16416 | tf_op jit(solution)/shard_map/ppermute | solution.py:1005
  111.8 0.7 shard_map.133
  112.5 2.8 %shard_map.134 = f32[64,3072]{1,0:T(8,128)} custom-call(bf16[1,64,3072]{2,1,0:T(8,128)(2,1)S(1)} %copy-done.1, bf16[128,3072]{1,0:T(8,128)(2,1)S(1)} %bitcast.23, bf16[128,3072]{1,0:T(8,128)(2,1)S(1)} %collective-permute-done.6.refs_7_.refs_2_, bf16[128,2048]{1,0:T(8,128)(2,1)S(1)} %collective-permute-done.7.refs_0_.refs_8_.refs_3_, ...), custom_call_target="tpu_custom_call" | custom-call | flops 805306368 | bytes 3940352 | tf_op jit(solution)/shard_map/pallas_call | solution.py:207
  (34 shorter events, 0.2 us)
Async XLA Ops:
  1.7 15.0 %collective-permute-start.7 = (bf16[128,2048]{1,0:T(8,128)(2,1)S(1)}, bf16[128,2048]{1,0:T(8,128)(2,1)S(1)}, u32[]{:S(2)}, u32[]{:S(2)}) collective-permute-start(bf16[128,2048]{1,0:T(8,128)(2,1)S(1)} %shard_map.124), channel_id=1, source_target_pairs={{0,4},{2,6},{4,0},{6,2},{1,5},{3,7},{5,1},{7,3},{8,12},{10,14},{12... | collective-permute-start | bytes 1572872 | tf_op jit(solution)/shard_map/ppermute | solution.py:68
  4.8 42.9 %collective-permute-start.6 = (bf16[128,3072]{1,0:T(8,128)(2,1)}, bf16[128,3072]{1,0:T(8,128)(2,1)S(1)}, u32[]{:S(2)}, u32[]{:S(2)}) collective-permute-start(bf16[128,3072]{1,0:T(8,128)(2,1)} %bitcast.20), channel_id=1, source_target_pairs={{0,2},{2,0},{4,6},{6,4},{1,3},{3,1},{5,7},{7,5},{8,10},{10,8},{12,... | collective-permute-start | bytes 2359304 | tf_op jit(solution)/shard_map/ppermute | solution.py:72
  16.7 7.5 %collective-permute-start.8 = (bf16[128,1024]{1,0:T(8,128)(2,1)S(1)}, bf16[128,1024]{1,0:T(8,128)(2,1)S(1)}, u32[]{:S(2)}, u32[]{:S(2)}) collective-permute-start(bf16[128,1024]{1,0:T(8,128)(2,1)S(1)} %shard_map.125), channel_id=1, source_target_pairs={{0,1},{1,0},{2,3},{3,2},{4,5},{5,4},{6,7},{7,6},{8,9},{9,8},{10,11... | collective-permute-start | bytes 786440 | tf_op jit(solution)/shard_map/ppermute | solution.py:69
  18.5 29.2 %collective-permute-start.9 = (bf16[128,2048]{1,0:T(8,128)(2,1)S(1)}, bf16[128,2048]{1,0:T(8,128)(2,1)S(1)}, u32[]{:S(2)}, u32[]{:S(2)}) collective-permute-start(bf16[128,2048]{1,0:T(8,128)(2,1)S(1)} %collective-permute-done.7.refs_0_.refs_8_.refs_3_), channel_id=1, source_target_pairs={{0,2},{2,0},{4,6},{6,4},{1,3},{3,1},{5,7},{7,5},{8,10},{10,8},{12,... | collective-permute-start | bytes 1572872 | tf_op jit(solution)/shard_map/ppermute | solution.py:72
  24.3 23.5 %collective-permute-start.10 = (bf16[128,1024]{1,0:T(8,128)(2,1)S(1)}, bf16[128,1024]{1,0:T(8,128)(2,1)S(1)}, u32[]{:S(2)}, u32[]{:S(2)}) collective-permute-start(bf16[128,1024]{1,0:T(8,128)(2,1)S(1)} %collective-permute-done.8.refs_9_.refs_4_), channel_id=1, source_target_pairs={{0,2},{2,0},{4,6},{6,4},{1,3},{3,1},{5,7},{7,5},{8,10},{10,8},{12,... | collective-permute-start | bytes 786440 | tf_op jit(solution)/shard_map/ppermute | solution.py:72
  24.3 15.9 %copy-start.1 = (bf16[1,64,3072]{2,1,0:T(8,128)(2,1)S(1)}, bf16[1,64,3072]{2,1,0:T(8,128)(2,1)}, u32[]{:S(2)}) copy-start(bf16[1,64,3072]{2,1,0:T(8,128)(2,1)} %refs_0_.5) | copy-start | bytes 1179652
  24.3 15.9 %copy-start.4 = (f32[1,2,128]{2,1,0:T(2,128)S(1)}, f32[1,2,128]{2,1,0:T(2,128)}, u32[]{:S(2)}) copy-start(f32[1,2,128]{2,1,0:T(2,128)} %refs_2_.1) | copy-start | bytes 3076
  34.5 13.2 %copy-start = (bf16[1,1,128,3072]{3,2,1,0:T(8,128)(2,1)S(1)}, bf16[1,1,128,3072]{3,2,1,0:T(8,128)(2,1)}, u32[]{:S(2)}) copy-start(bf16[1,1,128,3072]{3,2,1,0:T(8,128)(2,1)} %param.19) | copy-start | bytes 2359300
  34.5 2.0 %collective-permute-start = (bf16[128,128]{1,0:T(8,128)(2,1)S(1)}, bf16[128,128]{1,0:T(8,128)(2,1)S(1)}, u32[]{:S(2)}, u32[]{:S(2)}) collective-permute-start(bf16[128,128]{1,0:T(8,128)(2,1)S(1)} %get-tuple-element.42.refs_4_), channel_id=1, source_target_pairs={{0,2},{2,0},{4,6},{6,4},{1,3},{3,1},{5,7},{7,5},{8,10},{10,8},{12,... | collective-permute-start | bytes 98312 | tf_op jit(solution)/shard_map/ppermute | solution.py:32
  35.1 3.9 %collective-permute-start.1 = (bf16[128,128]{1,0:T(8,128)(2,1)S(1)}, bf16[128,128]{1,0:T(8,128)(2,1)S(1)}, u32[]{:S(2)}, u32[]{:S(2)}) collective-permute-start(bf16[128,128]{1,0:T(8,128)(2,1)S(1)} %get-tuple-element.42.refs_4_), channel_id=1, source_target_pairs={{0,4},{2,6},{4,0},{6,2},{1,5},{3,7},{5,1},{7,3},{8,12},{10,14},{12... | collective-permute-start | bytes 98312 | tf_op jit(solution)/shard_map/ppermute | solution.py:32
  36.5 3.7 %collective-permute-start.2 = (bf16[128,128]{1,0:T(8,128)(2,1)S(1)}, bf16[128,128]{1,0:T(8,128)(2,1)S(1)}, u32[]{:S(2)}, u32[]{:S(2)}) collective-permute-start(bf16[128,128]{1,0:T(8,128)(2,1)S(1)} %get-tuple-element.42.refs_4_), channel_id=1, source_target_pairs={{0,6},{2,4},{4,2},{6,0},{1,7},{3,5},{5,3},{7,1},{8,14},{10,12},{12... | collective-permute-start | bytes 98312 | tf_op jit(solution)/shard_map/ppermute | solution.py:32
  43.1 1.3 %collective-permute-start.3 = (bf16[128,128]{1,0:T(8,128)(2,1)S(1)}, bf16[128,128]{1,0:T(8,128)(2,1)S(1)}, u32[]{:S(2)}, u32[]{:S(2)}) collective-permute-start(bf16[128,128]{1,0:T(8,128)(2,1)S(1)} %get-tuple-element.46), channel_id=1, source_target_pairs={{0,2},{2,0},{4,6},{6,4},{1,3},{3,1},{5,7},{7,5},{8,10},{10,8},{12,... | collective-permute-start | bytes 98312 | tf_op jit(solution)/shard_map/ppermute | solution.py:37
  43.2 3.9 %collective-permute-start.4 = (bf16[128,128]{1,0:T(8,128)(2,1)S(1)}, bf16[128,128]{1,0:T(8,128)(2,1)S(1)}, u32[]{:S(2)}, u32[]{:S(2)}) collective-permute-start(bf16[128,128]{1,0:T(8,128)(2,1)S(1)} %get-tuple-element.47), channel_id=1, source_target_pairs={{0,4},{2,6},{4,0},{6,2},{1,5},{3,7},{5,1},{7,3},{8,12},{10,14},{12... | collective-permute-start | bytes 98312 | tf_op jit(solution)/shard_map/ppermute | solution.py:37
  44.4 3.3 %collective-permute-start.5 = (bf16[128,128]{1,0:T(8,128)(2,1)S(1)}, bf16[128,128]{1,0:T(8,128)(2,1)S(1)}, u32[]{:S(2)}, u32[]{:S(2)}) collective-permute-start(bf16[128,128]{1,0:T(8,128)(2,1)S(1)} %get-tuple-element.48), channel_id=1, source_target_pairs={{0,6},{2,4},{4,2},{6,0},{1,7},{3,5},{5,3},{7,1},{8,14},{10,12},{12... | collective-permute-start | bytes 98312 | tf_op jit(solution)/shard_map/ppermute | solution.py:37
  50.5 3.9 %collective-permute-start.11 = (bf16[128,128]{1,0:T(8,128)(2,1)S(1)}, bf16[128,128]{1,0:T(8,128)(2,1)S(1)}, u32[]{:S(2)}, u32[]{:S(2)}) collective-permute-start(bf16[128,128]{1,0:T(8,128)(2,1)S(1)} %get-tuple-element.50.refs_0_), channel_id=1, source_target_pairs={{0,8},{1,9},{2,10},{3,11},{4,12},{5,13},{6,14},{7,15}} | collective-permute-start | bytes 98312 | tf_op jit(solution)/shard_map/ppermute | solution.py:927
  51.8 2.9 %collective-permute-start.12 = (bf16[128,128]{1,0:T(8,128)(2,1)S(1)}, bf16[128,128]{1,0:T(8,128)(2,1)S(1)}, u32[]{:S(2)}, u32[]{:S(2)}) collective-permute-start(bf16[128,128]{1,0:T(8,128)(2,1)S(1)} %get-tuple-element.50.refs_0_), channel_id=1, source_target_pairs={{0,16},{1,17},{2,18},{3,19},{4,20},{5,21},{6,22},{7,23}} | collective-permute-start | bytes 98312 | tf_op jit(solution)/shard_map/ppermute | solution.py:927
  53.1 2.9 %collective-permute-start.13 = (bf16[128,128]{1,0:T(8,128)(2,1)S(1)}, bf16[128,128]{1,0:T(8,128)(2,1)S(1)}, u32[]{:S(2)}, u32[]{:S(2)}) collective-permute-start(bf16[128,128]{1,0:T(8,128)(2,1)S(1)} %get-tuple-element.50.refs_0_), channel_id=1, source_target_pairs={{0,24},{1,25},{2,26},{3,27},{4,28},{5,29},{6,30},{7,31}} | collective-permute-start | bytes 98312 | tf_op jit(solution)/shard_map/ppermute | solution.py:927
  56.0 1.9 %collective-permute-start.14 = (bf16[128,64]{1,0:T(8,128)(2,1)S(1)}, bf16[128,64]{1,0:T(8,128)(2,1)S(1)}, u32[]{:S(2)}, u32[]{:S(2)}) collective-permute-start(bf16[128,64]{1,0:T(8,128)(2,1)S(1)} %get-tuple-element.51.refs_4_.refs_8_), channel_id=1, source_target_pairs={{0,2},{2,0},{4,6},{6,4},{1,3},{3,1},{5,7},{7,5},{8,10},{10,8},{12,... | collective-permute-start | bytes 49160 | tf_op jit(solution)/shard_map/ppermute | solution.py:32
  56.1 4.0 %collective-permute-start.15 = (bf16[128,64]{1,0:T(8,128)(2,1)S(1)}, bf16[128,64]{1,0:T(8,128)(2,1)S(1)}, u32[]{:S(2)}, u32[]{:S(2)}) collective-permute-start(bf16[128,64]{1,0:T(8,128)(2,1)S(1)} %get-tuple-element.51.refs_4_.refs_8_), channel_id=1, source_target_pairs={{0,4},{2,6},{4,0},{6,2},{1,5},{3,7},{5,1},{7,3},{8,12},{10,14},{12... | collective-permute-start | bytes 49160 | tf_op jit(solution)/shard_map/ppermute | solution.py:32
  57.0 3.4 %collective-permute-start.16 = (bf16[128,64]{1,0:T(8,128)(2,1)S(1)}, bf16[128,64]{1,0:T(8,128)(2,1)S(1)}, u32[]{:S(2)}, u32[]{:S(2)}) collective-permute-start(bf16[128,64]{1,0:T(8,128)(2,1)S(1)} %get-tuple-element.51.refs_4_.refs_8_), channel_id=1, source_target_pairs={{0,6},{2,4},{4,2},{6,0},{1,7},{3,5},{5,3},{7,1},{8,14},{10,12},{12... | collective-permute-start | bytes 49160 | tf_op jit(solution)/shard_map/ppermute | solution.py:32
  60.4 1.9 %collective-permute-start.17 = (bf16[128,128]{1,0:T(8,128)(2,1)S(1)}, bf16[128,128]{1,0:T(8,128)(2,1)S(1)}, u32[]{:S(2)}, u32[]{:S(2)}) collective-permute-start(bf16[128,128]{1,0:T(8,128)(2,1)S(1)} %get-tuple-element.58), channel_id=1, source_target_pairs={{0,2},{2,0},{4,6},{6,4},{1,3},{3,1},{5,7},{7,5},{8,10},{10,8},{12,... | collective-permute-start | bytes 98312 | tf_op jit(solution)/shard_map/ppermute | solution.py:37
  60.6 3.9 %collective-permute-start.18 = (bf16[128,128]{1,0:T(8,128)(2,1)S(1)}, bf16[128,128]{1,0:T(8,128)(2,1)S(1)}, u32[]{:S(2)}, u32[]{:S(2)}) collective-permute-start(bf16[128,128]{1,0:T(8,128)(2,1)S(1)} %get-tuple-element.59), channel_id=1, source_target_pairs={{0,4},{2,6},{4,0},{6,2},{1,5},{3,7},{5,1},{7,3},{8,12},{10,14},{12... | collective-permute-start | bytes 98312 | tf_op jit(solution)/shard_map/ppermute | solution.py:37
  61.7 3.4 %collective-permute-start.19 = (bf16[128,128]{1,0:T(8,128)(2,1)S(1)}, bf16[128,128]{1,0:T(8,128)(2,1)S(1)}, u32[]{:S(2)}, u32[]{:S(2)}) collective-permute-start(bf16[128,128]{1,0:T(8,128)(2,1)S(1)} %get-tuple-element.60), channel_id=1, source_target_pairs={{0,6},{2,4},{4,2},{6,0},{1,7},{3,5},{5,3},{7,1},{8,14},{10,12},{12... | collective-permute-start | bytes 98312 | tf_op jit(solution)/shard_map/ppermute | solution.py:37
  65.2 26.4 %copy-start.2 = (bf16[4,128,128]{2,1,0:T(8,128)(2,1)S(1)}, bf16[4,128,128]{2,1,0:T(8,128)(2,1)}, u32[]{:S(2)}) copy-start(bf16[4,128,128]{2,1,0:T(8,128)(2,1)} %get-tuple-element.68.refs_5_) | copy-start | bytes 393220
  65.2 26.4 %copy-start.3 = (f32[128,128]{1,0:T(8,128)S(1)}, f32[128,128]{1,0:T(8,128)}, u32[]{:S(2)}) copy-start(f32[128,128]{1,0:T(8,128)} %get-tuple-element.69.refs_6_) | copy-start | bytes 196612
  65.2 31.8 %copy-start.5 = (f32[1,9216]{1,0:T(1,128)S(1)}, f32[1,9216]{1,0:T(1,128)}, u32[]{:S(2)}) copy-start(f32[1,9216]{1,0:T(1,128)} %get-tuple-element.49.refs_12_) | copy-start | bytes 110596
  65.2 1.9 %collective-permute-start.20 = (bf16[128,128]{1,0:T(8,128)(2,1)S(1)}, bf16[128,128]{1,0:T(8,128)(2,1)S(1)}, u32[]{:S(2)}, u32[]{:S(2)}) collective-permute-start(bf16[128,128]{1,0:T(8,128)(2,1)S(1)} %get-tuple-element.63), channel_id=1, source_target_pairs={{0,2},{2,0},{4,6},{6,4},{1,3},{3,1},{5,7},{7,5},{8,10},{10,8},{12,... | collective-permute-start | bytes 98312 | tf_op jit(solution)/shard_map/ppermute | solution.py:37
  65.4 3.9 %collective-permute-start.21 = (bf16[128,128]{1,0:T(8,128)(2,1)S(1)}, bf16[128,128]{1,0:T(8,128)(2,1)S(1)}, u32[]{:S(2)}, u32[]{:S(2)}) collective-permute-start(bf16[128,128]{1,0:T(8,128)(2,1)S(1)} %get-tuple-element.64), channel_id=1, source_target_pairs={{0,4},{2,6},{4,0},{6,2},{1,5},{3,7},{5,1},{7,3},{8,12},{10,14},{12... | collective-permute-start | bytes 98312 | tf_op jit(solution)/shard_map/ppermute | solution.py:37
  66.3 3.4 %collective-permute-start.22 = (bf16[128,128]{1,0:T(8,128)(2,1)S(1)}, bf16[128,128]{1,0:T(8,128)(2,1)S(1)}, u32[]{:S(2)}, u32[]{:S(2)}) collective-permute-start(bf16[128,128]{1,0:T(8,128)(2,1)S(1)} %get-tuple-element.65), channel_id=1, source_target_pairs={{0,6},{2,4},{4,2},{6,0},{1,7},{3,5},{5,3},{7,1},{8,14},{10,12},{12... | collective-permute-start | bytes 98312 | tf_op jit(solution)/shard_map/ppermute | solution.py:37
  69.8 15.1 %collective-permute-start.25 = (bf16[2,128,64]{2,1,0:T(8,128)(2,1)S(1)}, bf16[2,128,64]{2,1,0:T(8,128)(2,1)S(1)}, u32[]{:S(2)}, u32[]{:S(2)}) collective-permute-start(bf16[2,128,64]{2,1,0:T(8,128)(2,1)S(1)} %get-tuple-element.73), channel_id=1, source_target_pairs={{0,2},{2,0},{4,6},{6,4},{1,3},{3,1},{5,7},{7,5},{8,10},{10,8},{12,... | collective-permute-start | bytes 98312 | tf_op jit(solution)/shard_map/ppermute | solution.py:972
  69.9 17.3 %collective-permute-start.23 = (bf16[160,64]{1,0:T(8,128)(2,1)S(1)}, bf16[160,64]{1,0:T(8,128)(2,1)S(1)}, u32[]{:S(2)}, u32[]{:S(2)}) collective-permute-start(bf16[160,64]{1,0:T(8,128)(2,1)S(1)} %get-tuple-element.66), channel_id=1, source_target_pairs={{0,8},{8,0},{16,24},{24,16},{1,9},{9,1},{17,25},{25,17},{2,10},{10... | collective-permute-start | bytes 61448 | tf_op jit(solution)/shard_map/ppermute | solution.py:973
  74.8 12.5 %collective-permute-start.24 = (bf16[128,64]{1,0:T(8,128)(2,1)S(1)}, bf16[128,64]{1,0:T(8,128)(2,1)S(1)}, u32[]{:S(2)}, u32[]{:S(2)}) collective-permute-start(bf16[128,64]{1,0:T(8,128)(2,1)S(1)} %get-tuple-element.61.refs_7_), channel_id=1, source_target_pairs={{0,16},{8,24},{16,0},{24,8},{1,17},{9,25},{17,1},{25,9},{2,18},{10... | collective-permute-start | bytes 49160 | tf_op jit(solution)/shard_map/ppermute | solution.py:962
  84.8 5.8 %collective-permute-start.26 = (bf16[128,64]{1,0:T(8,128)(2,1)S(1)}, bf16[128,64]{1,0:T(8,128)(2,1)S(1)}, u32[]{:S(2)}, u32[]{:S(2)}) collective-permute-start(bf16[128,64]{1,0:T(8,128)(2,1)S(1)} %get-tuple-element.74), channel_id=1, source_target_pairs={{0,8},{2,10},{4,12},{6,14},{8,16},{10,18},{12,20},{14,22},{16,24},... | collective-permute-start | bytes 49160 | tf_op jit(solution)/shard_map/ppermute | solution.py:976
  84.9 6.6 %collective-permute-start.27 = (bf16[128,64]{1,0:T(8,128)(2,1)S(1)}, bf16[128,64]{1,0:T(8,128)(2,1)S(1)}, u32[]{:S(2)}, u32[]{:S(2)}) collective-permute-start(bf16[128,64]{1,0:T(8,128)(2,1)S(1)} %get-tuple-element.75), channel_id=1, source_target_pairs={{0,12},{2,14},{4,8},{6,10},{8,20},{10,22},{12,16},{14,18},{16,28},... | collective-permute-start | bytes 49160 | tf_op jit(solution)/shard_map/ppermute | solution.py:976
  92.1 1.3 %collective-permute-start.32 = (bf16[5,64,128]{2,1,0:T(8,128)(2,1)S(1)}, bf16[5,64,128]{2,1,0:T(8,128)(2,1)S(1)}, u32[]{:S(2)}, u32[]{:S(2)}) collective-permute-start(bf16[5,64,128]{2,1,0:T(8,128)(2,1)S(1)} %get-tuple-element.77), channel_id=1, source_target_pairs={{0,2},{2,0},{4,6},{6,4},{1,3},{3,1},{5,7},{7,5},{8,10},{10,8},{12,... | collective-permute-start | bytes 245768 | tf_op jit(solution)/shard_map/ppermute | solution.py:1011
  93.4 19.1 %collective-permute-start.33 = (bf16[5,64,128]{2,1,0:T(8,128)(2,1)S(1)}, bf16[5,64,128]{2,1,0:T(8,128)(2,1)S(1)}, u32[]{:S(2)}, u32[]{:S(2)}) collective-permute-start(bf16[5,64,128]{2,1,0:T(8,128)(2,1)S(1)} %add_convert_fusion.refs_8_), channel_id=1, source_target_pairs={{0,4},{1,5},{2,6},{3,7},{4,0},{5,1},{6,2},{7,3},{8,12},{9,13},{10,... | collective-permute-start | bytes 245768 | tf_op jit(solution)/shard_map/ppermute | solution.py:1023
  94.6 17.9 %collective-permute-start.34 = (bf16[5,64,128]{2,1,0:T(8,128)(2,1)S(1)}, bf16[5,64,128]{2,1,0:T(8,128)(2,1)S(1)}, u32[]{:S(2)}, u32[]{:S(2)}) collective-permute-start(bf16[5,64,128]{2,1,0:T(8,128)(2,1)S(1)} %add_convert_fusion.refs_8_), channel_id=1, source_target_pairs={{0,1},{1,0},{2,3},{3,2},{4,5},{5,4},{6,7},{7,6},{8,9},{9,8},{10,11... | collective-permute-start | bytes 245768 | tf_op jit(solution)/shard_map/ppermute | solution.py:1023
  96.1 16.4 %collective-permute-start.35 = (bf16[5,64,128]{2,1,0:T(8,128)(2,1)S(1)}, bf16[5,64,128]{2,1,0:T(8,128)(2,1)S(1)}, u32[]{:S(2)}, u32[]{:S(2)}) collective-permute-start(bf16[5,64,128]{2,1,0:T(8,128)(2,1)S(1)} %add_convert_fusion.refs_8_), channel_id=1, source_target_pairs={{0,5},{1,4},{2,7},{3,6},{4,1},{5,0},{6,3},{7,2},{8,13},{9,12},{10,... | collective-permute-start | bytes 245768 | tf_op jit(solution)/shard_map/ppermute | solution.py:1023
  97.0 3.9 %collective-permute-start.28 = (bf16[128,64]{1,0:T(8,128)(2,1)S(1)}, bf16[128,64]{1,0:T(8,128)(2,1)S(1)}, u32[]{:S(2)}, u32[]{:S(2)}) collective-permute-start(bf16[128,64]{1,0:T(8,128)(2,1)S(1)} %get-tuple-element.76.refs_0_), channel_id=1, source_target_pairs={{0,8},{8,0},{16,24},{24,16},{1,9},{9,1},{17,25},{25,17},{2,10},{10... | collective-permute-start | bytes 49160 | tf_op jit(solution)/shard_map/ppermute | solution.py:1007
  97.0 15.5 %collective-permute-start.31 = (f32[1,9216]{1,0:T(1,128)S(1)}, f32[1,9216]{1,0:T(1,128)S(1)}, u32[]{:S(2)}, u32[]{:S(2)}) collective-permute-start(f32[1,9216]{1,0:T(1,128)S(1)} %copy-done.5), channel_id=1, source_target_pairs={{0,1},{1,0},{2,3},{3,2},{4,5},{5,4},{6,7},{7,6},{8,9},{9,8},{10,11... | collective-permute-start | bytes 110600 | tf_op jit(solution)/shard_map/ppermute | solution.py:32
  100.9 5.1 %collective-permute-start.29 = (bf16[128,64]{1,0:T(8,128)(2,1)S(1)}, bf16[128,64]{1,0:T(8,128)(2,1)S(1)}, u32[]{:S(2)}, u32[]{:S(2)}) collective-permute-start(bf16[128,64]{1,0:T(8,128)(2,1)S(1)} %get-tuple-element.76.refs_0_), channel_id=1, source_target_pairs={{0,16},{8,24},{16,0},{24,8},{1,17},{9,25},{17,1},{25,9},{2,18},{10... | collective-permute-start | bytes 49160 | tf_op jit(solution)/shard_map/ppermute | solution.py:1006
  106.0 5.7 %collective-permute-start.30 = (bf16[128,64]{1,0:T(8,128)(2,1)S(1)}, bf16[128,64]{1,0:T(8,128)(2,1)S(1)}, u32[]{:S(2)}, u32[]{:S(2)}) collective-permute-start(bf16[128,64]{1,0:T(8,128)(2,1)S(1)} %get-tuple-element.76.refs_0_), channel_id=1, source_target_pairs={{0,24},{8,16},{16,8},{24,0},{1,25},{9,17},{17,9},{25,1},{2,26},{10... | collective-permute-start | bytes 49160 | tf_op jit(solution)/shard_map/ppermute | solution.py:1005
